TPU v7x, 256 devices: a whole 4x4x8 slice. The times are simulated.
256 devices in a mesh: wide: 32 (over z, x_lo, core), narrow: 8 (over x_hi, y).
Axes of the slice: x: 4 (x_hi: 2, x_lo: 2; x = x_hi * 2 + x_lo), y: 4, z: 8, core: 2. Of those that a mesh axis runs over, the one named last changes fastest.
Arguments:
- tokens: bfloat16 [4096, 2048], P('wide'), may hold values from -6 to 6
- request_lengths: int32 [32, 3], replicated, may hold values from 1 to 64, 128 in all within a row
- w_qkv: bfloat16 [2048, 3, 2048], P(None, None, 'narrow'), may hold values from -0.19921875 to 0.19921875
- qk_gain: float32 [2, 2048], P(None, 'narrow'), may hold values from 0.5 to 7
- w_out: bfloat16 [2048, 2048], P('narrow'), may hold values from -0.125 to 0.125
- norm_gains: float32 [3, 2048], replicated, may hold values from 0.25 to 1.75
- w_router: bfloat16 [2048, 64], replicated, may hold values from -0.0625 to 0.0625
- routes: int32 [4096, 8], P('wide'), may hold values from 0 to 63, all different within a row; in each aligned block of 128 rows (0 to 127, 128 to 255, ...) at most 20 rows name the same one
- w_gate: bfloat16 [64, 2048, 1024], P('wide', None, 'narrow'), may hold values from -0.125 to 0.125
- w_up: bfloat16 [64, 2048, 1024], P('wide', None, 'narrow'), may hold values from -0.125 to 0.125
- w_down: bfloat16 [64, 1024, 2048], P('wide', 'narrow'), may hold values from -0.1875 to 0.1875
- w_proj: bfloat16 [2048, 128], replicated, may hold values from -0.125 to 0.125
- doc_vectors: bfloat16 [262144, 128], P(('wide', 'narrow')), may hold values from -6 to 6
- doc_segment: int32 [256, 1024], P(('wide', 'narrow')), may hold values from 0 to 15, never falling along the last dimension, each value on 1 to 128 neighbouring positions
- doc_request: int32 [256, 16], P(('wide', 'narrow')), may hold values from 0 to 95
Outputs:
- layer_out: bfloat16 [4096, 2048], P('wide')
- doc_scores: float32 [256, 16], P(('wide', 'narrow'))
Inputs may be any that keep to these rules, and one draw needn't show every extreme that they name: `request_lengths`: each row sums to 128, and its largest entry is exactly 64. `routes`: each row names 8 different experts. In the rows of one index of wide (aligned blocks of 128 rows) no expert is named by more than 20 rows, a bound that some block reaches. `doc_segment`: in each row the numbers never fall, every document has one or more rows, and one document has exactly 128.
All inputs are finite; a program needn't handle non-finite values.
Results may differ from a plain program's by a relative error of at most 0.009.
Values may be sent and summed in bfloat16 or wider, within the bound.
No kernel may reach another device: no remote copies, remote signals or barrier semaphores. Data moves between devices by JAX's collectives and lax.ppermute only.
A program may use at most 128 MiB of HBM per device.

v0:
```python
import jax
import jax.numpy as jnp
from jax import lax
from jax.sharding import PartitionSpec as P

HD = 128
TOPK = 8
TOK_DEV = 128


EPS = 1e-06
THETA = 50000.0
NEG = -1e30


def rms_norm(values, gain):
    return values * lax.rsqrt(jnp.mean(values * values, axis=-1, keepdims=True) + EPS) * gain


def rotary(values, offsets):
    half = values.shape[-1] // 2
    freq = THETA ** (-jnp.arange(half, dtype=jnp.float32) / half)
    angle = offsets.astype(jnp.float32)[:, None] * freq[None, :]
    cosine = jnp.cos(angle)[:, None, :]
    sine = jnp.sin(angle)[:, None, :]
    first = values[..., :half]
    second = values[..., half:]
    return jnp.concatenate(
        [first * cosine - second * sine, second * cosine + first * sine], axis=-1
    )


def request_layout(lengths_row, count):
    bounds = jnp.cumsum(lengths_row)
    places = jnp.arange(count, dtype=jnp.int32)
    member = jnp.sum((places[:, None] >= bounds[None, :-1]).astype(jnp.int32), axis=1)
    starts = bounds - lengths_row
    pick = member[:, None] == jnp.arange(lengths_row.shape[0], dtype=jnp.int32)[None, :]
    offsets = places - jnp.sum(jnp.where(pick, starts[None, :], 0), axis=1)
    return (member, offsets)


def request_of(index, request_lengths):
    shard_count, per_shard = request_lengths.shape
    bounds = jnp.cumsum(request_lengths, axis=1)
    shard = index // TOK_DEV
    place = index - shard * TOK_DEV
    pick = shard[:, None] == jnp.arange(shard_count, dtype=jnp.int32)[None, :]
    row_bounds = jnp.sum(jnp.where(pick[:, :, None], bounds[None, :, :], 0), axis=1)
    member = jnp.sum((place[:, None] >= row_bounds[:, :-1]).astype(jnp.int32), axis=1)
    return shard * per_shard + member


def body(
    tokens,
    request_lengths,
    w_qkv,
    qk_gain,
    w_out,
    norm_gains,
    w_router,
    routes,
    w_gate,
    w_up,
    w_down,
    w_proj,
    doc_vectors,
    doc_segment,
    doc_request,
):
    f32 = jnp.float32
    bf16 = jnp.bfloat16
    count, width = tokens.shape
    experts = w_router.shape[1]
    capacity = max(2, 5 * TOK_DEV * TOPK // (4 * experts))
    heads_here = w_qkv.shape[2] // HD
    lengths_row = lax.dynamic_slice_in_dim(request_lengths, lax.axis_index("wide"), 1, 0)[0]
    member, offsets = request_layout(lengths_row, count)
    xf = tokens.astype(f32)
    normed = rms_norm(xf, norm_gains[0]).astype(bf16)
    proj = jnp.dot(normed, w_qkv.reshape(width, -1), preferred_element_type=f32).reshape(
        count, 3, heads_here, HD
    )
    query = rotary(rms_norm(proj[:, 0], qk_gain[0].reshape(heads_here, HD)), offsets).astype(bf16)
    keys = rotary(rms_norm(proj[:, 1], qk_gain[1].reshape(heads_here, HD)), offsets).astype(bf16)
    values = proj[:, 2].astype(bf16)
    scores = jnp.einsum("qhd,khd->hqk", query, keys, preferred_element_type=f32) * HD ** (-0.5)
    scores = jnp.where((member[:, None] == member[None, :])[None], scores, NEG)
    peak = jnp.max(scores, axis=-1, keepdims=True)
    weights = jnp.exp(scores - peak)
    probs = (weights / jnp.sum(weights, axis=-1, keepdims=True)).astype(bf16)
    mixed = (
        jnp.einsum("hqk,khd->qhd", probs, values, preferred_element_type=f32)
        .astype(bf16)
        .reshape(count, heads_here * HD)
    )
    attn = lax.psum(jnp.dot(mixed, w_out, preferred_element_type=f32), "narrow")
    hidden = (xf + attn).astype(bf16)
    normed_two = rms_norm(hidden.astype(f32), norm_gains[1]).astype(bf16)
    logits = jnp.dot(normed_two, w_router, preferred_element_type=f32)
    onehot = routes[:, :, None] == jnp.arange(experts, dtype=jnp.int32)[None, None, :]
    chosen = jnp.sum(jnp.where(onehot, logits[:, None, :], 0.0), axis=-1)
    lifted = jax.nn.sigmoid(chosen)
    gates = lifted / jnp.sum(lifted, axis=-1, keepdims=True)
    counts = jnp.sum(onehot.astype(bf16), axis=1)
    positions = jnp.arange(count, dtype=jnp.int32)
    lower = (positions[:, None] > positions[None, :]).astype(bf16)
    before = jnp.dot(lower, counts, preferred_element_type=f32)
    slots = jnp.sum(jnp.where(onehot, before[:, None, :], 0.0), axis=-1).astype(jnp.int32)
    places = routes * capacity + slots
    owner = (
        jnp.full((experts * capacity,), count, jnp.int32)
        .at[places.reshape(-1)]
        .set(jnp.repeat(positions, TOPK))
    )
    padded = jnp.concatenate([normed_two, jnp.zeros((1, width), bf16)], axis=0)
    buffer = padded[owner].reshape(experts, 1, capacity, width)
    received = lax.all_to_all(buffer, "wide", split_axis=0, concat_axis=1, tiled=True)
    gate = jnp.einsum("esrd,edf->esrf", received, w_gate, preferred_element_type=f32)
    upward = jnp.einsum("esrd,edf->esrf", received, w_up, preferred_element_type=f32)
    active = (jax.nn.silu(gate) * upward).astype(bf16)
    partial_out = jnp.einsum("esrf,efd->esrd", active, w_down, preferred_element_type=f32).astype(
        bf16
    )
    expert_rows = lax.all_to_all(partial_out, "wide", split_axis=1, concat_axis=0, tiled=True)
    flat_rows = expert_rows.reshape(experts * capacity, expert_rows.shape[3])
    picked = flat_rows[places]
    mixture = jnp.sum(gates[:, :, None] * picked.astype(f32), axis=1)
    moe = lax.psum(mixture.astype(jnp.bfloat16), "narrow").astype(jnp.float32)
    layer_out = (hidden.astype(f32) + moe).astype(bf16)
    normed_three = rms_norm(layer_out.astype(f32), norm_gains[2]).astype(bf16)
    embedded = jnp.dot(normed_three, w_proj, preferred_element_type=f32)
    vectors = (
        embedded * lax.rsqrt(jnp.sum(embedded * embedded, axis=-1, keepdims=True) + EPS)
    ).astype(bf16)
    segment_row = doc_segment[0]
    requests = doc_request[0]
    docs_held = requests.shape[0]
    piece = lax.all_gather(vectors, "wide", axis=0, tiled=True)
    sims = lax.dot_general(piece, doc_vectors, (((1,), (1,)), ((), ())), preferred_element_type=f32)
    owners = request_of(jnp.arange(piece.shape[0], dtype=jnp.int32), request_lengths)
    best = jnp.stack(
        [
            jnp.max(jnp.where(segment_row[None, :] == doc, sims, NEG), axis=1)
            for doc in range(docs_held)
        ],
        axis=1,
    )
    totals = jnp.sum(jnp.where(owners[:, None] == requests[None, :], best, 0.0), axis=0)
    flat_lengths = request_lengths.reshape(-1)
    request_total = flat_lengths.shape[0]
    match = requests[:, None] == jnp.arange(request_total, dtype=jnp.int32)[None, :]
    doc_lengths = jnp.sum(jnp.where(match, flat_lengths[None, :], 0), axis=1).astype(f32)
    doc_scores = (totals / doc_lengths)[None, :]
    return (layer_out, doc_scores)


def solution(mesh):
    placed = (
        P("wide", None),
        P(),
        P(None, None, "narrow"),
        P(None, "narrow"),
        P("narrow", None),
        P(),
        P(),
        P("wide", None),
        P("wide", None, "narrow"),
        P("wide", None, "narrow"),
        P("wide", "narrow", None),
        P(),
        P(("wide", "narrow"), None),
        P(("wide", "narrow"), None),
        P(("wide", "narrow"), None),
    )
    return jax.shard_map(
        body,
        mesh=mesh,
        in_specs=placed,
        out_specs=(P("wide", None), P(("wide", "narrow"), None)),
        check_vma=False,
    )
```

profile of v0, /device:TPU:1, one launch (start us, length us, event | category | flops | bytes accessed | tf_op | source)
XLA Modules:
  0.0 670.0 jit_solution(17985373668858841175)
XLA Ops:
  7.2 0.9 copy.75
  8.1 0.2 reduce-window.4
  8.6 0.9 fusion.85
  9.5 4.7 copy.74
  14.2 0.2 fusion.20
  14.4 3.0 fusion.41
  17.6 0.2 multiply_cosine_fusion
  17.8 0.1 multiply_multiply_fusion
  18.0 0.9 fusion.16
  18.8 0.3 fusion.87
  19.1 1.2 convolution_convert_fusion.1
  20.3 1.4 fusion.92
  21.8 0.1 fusion.61
  22.0 91.5 %all-reduce.4.cloned.1.call-done = f32[128,2048]{1,0:T(8,128)} async-done(((f32[128,2048]{1,0:T(8,128)}), f32[128,2048]{1,0:T(8,128)}) %all-reduce.4.cloned.1.call-update) | async-done | bytes 1048592 | tf_op jit(solution)/shard_map/psum | solution.py:97
  113.5 1.5 fusion.24
  115.0 0.2 fusion.26
  115.2 0.3 fusion.93
  115.6 0.1 copy.80
  115.8 4.3 scatter_custom_fusion
  120.2 6.2 gather_fusion
  126.4 8.9 %reshape.299 = bf16[64,1,20,2048]{3,2,0,1:T(8,128)(2,1)} reshape(bf16[1280,2048]{1,0:T(8,128)(2,1)} %gather_fusion) | data formatting | bytes 10485760 | tf_op jit(solution)/shard_map/reshape | solution.py:117
  135.3 153.4 %all_to_all.33 = bf16[64,1,20,2048]{3,2,1,0:T(8,128)(2,1)S(1)} all-to-all(bf16[64,1,20,2048]{3,2,1,0:T(8,128)(2,1)} %bitcast.113), channel_id=1, replica_groups=mesh['wide'=32,'narrow'=8] {'wide'}, dimensions={0} | all-to-all | bytes 10485760 | tf_op jit(solution)/shard_map/all_to_all | solution.py:118
  288.7 2.7 copy-done.2
  291.4 4.4 fusion.4
  295.8 10.6 %convolution_convert_fusion = bf16[2,32,20,2048]{3,1,2,0:T(8,128)(2,1)} fusion(bf16[2,128,2048]{2,1,0:T(8,128)(2,1)S(1)} %copy-done, bf16[32,2,1,20,2048]{4,3,1,0,2:T(8,128)(2,1)} %bitcast.116, bf16[2,2048,128]{2,1,0:T(8,128)(2,1)} %param.24, f32[2,32,20,128]{3,1,2,0:T(8,128)} %fusion.4), kind=kOutput, calls=%fused_computation.26 | convolution fusion | flops 1345781760 | bytes 13238272 | tf_op jit(solution)/shard_map/esrf,efd->esrd/dot_general | solution.py:122
  306.3 10.4 %copy.84 = bf16[2,32,20,2048]{3,0,2,1:T(2,128)(2,1)} copy(bf16[2,32,20,2048]{3,1,2,0:T(8,128)(2,1)} %convolution_convert_fusion) | data formatting | bytes 10485760 | tf_op jit(solution)/shard_map/convert_element_type | solution.py:122
  316.8 5.7 all-to-all-start.1
  322.5 0.1 copy.86
  322.7 0.1 copy.79
  322.9 118.7 %all-to-all-done.1 = bf16[2,32,20,2048]{3,0,2,1:T(2,128)(2,1)} async-done(((bf16[2,32,20,2048]{3,0,2,1:T(2,128)(2,1)}), bf16[2,32,20,2048]{3,0,2,1:T(2,128)(2,1)}, u32[]{:S(2)}, u32[]{:S(2)}) %all-to-all-start.1) | async-done | bytes 5242912 | tf_op jit(solution)/shard_map/all_to_all | solution.py:125
  441.6 7.8 %copy.85 = bf16[32,2,1,20,2048]{4,3,1,0,2:T(8,128)(2,1)} copy(bf16[32,2,1,20,2048]{4,1,3,0,2:T(2,128)(2,1)} %bitcast.31) | data formatting | bytes 10485760 | tf_op jit(solution)/shard_map/all_to_all | solution.py:125
  449.4 9.0 %reshape.300 = bf16[1280,2048]{1,0:T(8,128)(2,1)} reshape(bf16[32,2,1,20,2048]{4,3,1,0,2:T(8,128)(2,1)} %copy.85) | data formatting | bytes 10485760 | tf_op jit(solution)/shard_map/reshape | solution.py:126
  458.3 12.0 %gather_fusion.1 = bf16[1024,2048]{1,0:T(8,128)(2,1)} fusion(bf16[1280,2048]{1,0:T(8,128)(2,1)} %reshape.300, s32[1024]{0:T(1024)S(1)} %broadcast_clamp_fusion), kind=kCustom, calls=%fused_computation.1 | custom fusion | bytes 8392704 | tf_op jit(solution)/shard_map/gather | solution.py:127
  470.4 7.4 %fusion.1 = bf16[128,2048]{1,0:T(8,128)(2,1)} fusion(bf16[1024,2048]{1,0:T(8,128)(2,1)} %gather_fusion.1, f32[128,8]{1,0:T(8,128)S(1)} %copy.79), kind=kLoop, calls=%fused_computation.21 | loop fusion | flops 6029312 | bytes 4722688 | tf_op jit(solution)/shard_map/reduce_sum | solution.py:128
  477.7 0.3 all-gather.2.cloned.1.call-start
  478.1 78.3 %all-reduce.6.cloned.1.call-done = bf16[128,2048]{1,0:T(8,128)(2,1)} async-done(((bf16[128,2048]{1,0:T(8,128)(2,1)}), bf16[128,2048]{1,0:T(8,128)(2,1)}) %all-reduce.6.cloned.1.call-update) | async-done | bytes 524304 | tf_op jit(solution)/shard_map/psum | solution.py:129
  556.3 1.3 fusion.17
  557.7 0.4 multiply_reduce_fusion.2
  558.1 0.6 multiply_convert_fusion
  558.8 0.1 broadcast_in_dim.319
  558.9 0.2 select_reduce_fusion.20
  559.2 0.3 select_reduce_fusion.16
  559.5 0.2 compare_reduce_fusion
  559.8 65.5 %all-gather.2.cloned.1.call-done = bf16[4096,128]{0,1:T(8,128)(2,1)} async-done(((bf16[128,128]{0,1:T(8,128)(2,1)}), bf16[4096,128]{0,1:T(8,128)(2,1)}) %all-gather.2.cloned.1.call-update) | async-done | bytes 1048592 | tf_op jit(solution)/shard_map/all_gather | solution.py:139
  625.2 37.1 %select_reduce_fusion = (f32[4096]{0:T(1024)S(1)}, f32[4096]{0:T(1024)S(1)}, f32[4096]{0:T(1024)S(1)}, f32[4096]{0:T(1024)S(1)}, f32[4096]{0:T(1024)S(1)}, /*ind...) fusion(pred[1024]{0:T(1024)(128)(4,1)S(1)} %get-tuple-element.2, ...), kind=kOutput, calls=%fused_computation.4 | convolution fusion | flops 1207894016 | bytes 1589248 | tf_op jit(solution)/shard_map/dot_general | solution.py:140
  662.3 0.4 stack.67
  662.7 0.2 select_reduce_fusion.17
  662.9 0.5 fusion.74
  (68 shorter events, 1.3 us)
Async XLA Ops:
  7.2 288.6 %copy-start = (bf16[2,128,2048]{2,1,0:T(8,128)(2,1)S(1)}, bf16[2,128,2048]{2,1,0:T(8,128)(2,1)}, u32[]{:S(2)}) copy-start(bf16[2,128,2048]{2,1,0:T(8,128)(2,1)} %param.25) | copy-start | bytes 3145732
  7.2 7.1 %copy-start.3 = (bf16[128,2048]{1,0:T(8,128)(2,1)S(1)}, bf16[128,2048]{1,0:T(8,128)(2,1)}, u32[]{:S(2)}) copy-start(bf16[128,2048]{1,0:T(8,128)(2,1)} %param.15) | copy-start | bytes 1572868
  7.2 106.3 %all-reduce.4.cloned.1.call-start = ((), (), s32[]{:S(2)}) async-start(), calls=%async_computation.2 | async-start | bytes 2097152 | tf_op jit(solution)/shard_map/psum | solution.py:97
  9.5 8.0 %copy-start.10 = (f32[2,256]{1,0:T(2,128)S(1)}, f32[2,256]{1,0:T(2,128)}, u32[]{:S(2)}) copy-start(f32[2,256]{1,0:T(2,128)} %param.18) | copy-start | bytes 6148
  14.2 6.1 copy-start.4
  14.2 7.6 %copy-start.7 = (s32[128,8]{0,1:T(8,128)S(1)}, s32[128,8]{0,1:T(8,128)}, u32[]{:S(2)}) copy-start(s32[128,8]{0,1:T(8,128)} %param.22) | copy-start | bytes 12292
  17.5 97.7 %copy-start.6 = (bf16[2048,64]{0,1:T(8,128)(2,1)S(1)}, bf16[2048,64]{0,1:T(8,128)(2,1)}, u32[]{:S(2)}) copy-start(bf16[2048,64]{0,1:T(8,128)(2,1)} %param.21) | copy-start | bytes 786436
  135.3 156.0 %copy-start.12 = (bf16[2,2048,128]{2,1,0:T(8,128)(2,1)S(1)}, bf16[2,2048,128]{2,1,0:T(8,128)(2,1)}, u32[]{:S(2)}) copy-start(bf16[2,2048,128]{2,1,0:T(8,128)(2,1)} %param.23) | copy-start | bytes 3145732
  288.7 2.7 copy-start.2
  316.8 124.8 %all-to-all-start.1 = ((bf16[2,32,20,2048]{3,0,2,1:T(2,128)(2,1)}), bf16[2,32,20,2048]{3,0,2,1:T(2,128)(2,1)}, u32[]{:S(2)}, u32[]{:S(2)}) async-start(bf16[2,32,20,2048]{3,0,2,1:T(2,128)(2,1)} %copy.84), calls=%async_computation.1 | async-start | bytes 10485760 | tf_op jit(solution)/shard_map/all_to_all | solution.py:125
  322.4 233.9 %all-reduce.6.cloned.1.call-start = ((), (), s32[]{:S(2)}) async-start(), calls=%async_computation.3 | async-start | bytes 1048576 | tf_op jit(solution)/shard_map/psum | solution.py:129
  470.3 87.3 %copy-start.13 = (bf16[2048,128]{1,0:T(8,128)(2,1)S(1)}, bf16[2048,128]{1,0:T(8,128)(2,1)}, u32[]{:S(2)}) copy-start(bf16[2048,128]{1,0:T(8,128)(2,1)} %param.26) | copy-start | bytes 1572868
  470.3 88.4 %copy-start.8 = (s32[32,3]{0,1:T(4,128)S(1)}, s32[32,3]{0,1:T(4,128)}, u32[]{:S(2)}) copy-start(s32[32,3]{0,1:T(4,128)} %param.16) | copy-start | bytes 1156
  470.3 88.6 %copy-start.11 = (s32[1,16]{1,0:T(1,128)S(1)}, s32[1,16]{1,0:T(1,128)}, u32[]{:S(2)}) copy-start(s32[1,16]{1,0:T(1,128)} %param.29) | copy-start | bytes 196
  470.3 89.2 %copy-start.9 = (s32[1,1024]{1,0:T(1,128)S(1)}, s32[1,1024]{1,0:T(1,128)}, u32[]{:S(2)}) copy-start(s32[1,1024]{1,0:T(1,128)} %param.28) | copy-start | bytes 12292
  477.7 147.5 %all-gather.2.cloned.1.call-start = ((), (), s32[]{:S(2)}) async-start(), calls=%async_computation.4 | async-start | bytes 1081344 | tf_op jit(solution)/shard_map/all_gather | solution.py:139
  557.6 104.7 %copy-start.5 = (bf16[128,2048]{1,0:T(8,128)(2,1)}, bf16[128,2048]{1,0:T(8,128)(2,1)S(1)}, u32[]{:S(2)}) copy-start(bf16[128,2048]{1,0:T(8,128)(2,1)S(1)} %get-tuple-element.39) | copy-start | bytes 1572868
  625.2 38.2 %copy-start.1 = (bf16[2,128,2048]{2,1,0:T(8,128)(2,1)S(1)}, bf16[2,128,2048]{2,1,0:T(8,128)(2,1)}, u32[]{:S(2)}) copy-start(bf16[2,128,2048]{2,1,0:T(8,128)(2,1)} %param.25) | copy-start | bytes 3145732
Sparse Core Ops, SparseCore 0:
  21.8 91.6 all-reduce.3
  477.9 78.4 all-reduce.5
  558.9 66.3 all-gather.1
where the time goes:
time: 671 us; the launch traced here: 670 us
  waiting for transfers between devices  354 us (53%)
  blocking collectives  153 us (23%)
  local copies, waits for them, and re-layouts  69 us (10%)
  matrix products  59.6 us (9%)
  between operations  14.1 us (2%)
  other arithmetic  13.8 us (2%)
    all_to_all x1, blocking collectives, body(): lax.all_to_all(buffer, 'wide', split_axis=0, concat_axis=1, tiled=True)  153 us
    all_to_all x1, waiting for transfers between devices, body(): lax.all_to_all(partial_out, 'wide', split_axis=1, concat_axis=0, tiled=True)  119 us
    psum x1, waiting for transfers between devices, body(): attn = lax.psum(jnp.dot(mixed, w_out, preferred_element_type=f32), 'narrow')  91.5 us
    psum x1, waiting for transfers between devices, body(): moe = lax.psum(mixture.astype(jnp.bfloat16), 'narrow').astype(jnp.float32)  78.3 us
    all_gather x1, waiting for transfers between devices, body(): piece = lax.all_gather(vectors, 'wide', axis=0, tiled=True)  65.5 us
    dot_general x1, matrix products, body(): lax.dot_general(piece, doc_vectors, (((1,), (1,)), ((), ())), preferred_e...  37.1 us
  transfers between devices with their start and end apart: 4, of which 4 were waited for; matrix products, arithmetic and copies ran while one was open for 0% of the time, Pallas kernels for 0%

commit v1 on v0

v1 whole, which is shorter than its diff:
```python
import functools

import jax
import jax.numpy as jnp
from jax import lax
from jax.experimental import pallas as pl
from jax.experimental.pallas import tpu as pltpu
from jax.sharding import Mesh, PartitionSpec as P

HD = 128
TOPK = 8
TOK = 128
CAP = 20
EXPERTS = 64
WIDE = 32
EPS = 1e-06
THETA = 50000.0
NEG = -1e30
W = ("z", "xl", "core")
N = ("xh", "y")
f32 = jnp.float32
bf16 = jnp.bfloat16


def rms_norm(values, gain):
    return values * lax.rsqrt(jnp.mean(values * values, axis=-1, keepdims=True) + EPS) * gain


def rotary(values, offsets):
    half = values.shape[-1] // 2
    freq = THETA ** (-jnp.arange(half, dtype=f32) / half)
    angle = offsets.astype(f32)[:, None] * freq[None, :]
    cosine = jnp.cos(angle)[:, None, :]
    sine = jnp.sin(angle)[:, None, :]
    first = values[..., :half]
    second = values[..., half:]
    return jnp.concatenate(
        [first * cosine - second * sine, second * cosine + first * sine], axis=-1
    )


def request_layout(lengths_row, count):
    bounds = jnp.cumsum(lengths_row)
    places = jnp.arange(count, dtype=jnp.int32)
    member = jnp.sum((places[:, None] >= bounds[None, :-1]).astype(jnp.int32), axis=1)
    starts = bounds - lengths_row
    pick = member[:, None] == jnp.arange(lengths_row.shape[0], dtype=jnp.int32)[None, :]
    offsets = places - jnp.sum(jnp.where(pick, starts[None, :], 0), axis=1)
    return (member, offsets)


def y_shift(x, k):
    return lax.ppermute(x, "y", [(s, (s + k) % 4) for s in range(4)])


def x_swap(x):
    return lax.ppermute(x, "xh", [(0, 1), (1, 0)])


def gate_up_kernel(j_ref, x0, x1, x2, x3, w_own, w_par, gain_ref, out_ref):
    j = j_ref[0]
    xs = (x0, x1, x2, x3)
    total = jnp.zeros((x0.shape[0], 1), f32)
    for x in xs:
        v = x[...].astype(f32)
        total = total + jnp.sum(v * v, axis=1, keepdims=True)
    scale = lax.rsqrt(total / 2048.0 + EPS)
    own = jnp.zeros((x0.shape[0], 256), f32)
    par = jnp.zeros((x0.shape[0], 256), f32)
    for k, x in enumerate(xs):
        part = lax.rem(j - k + 4, 4)
        at = pl.multiple_of(part * 512, 512)
        normed = (x[...].astype(f32) * scale * gain_ref[part]).astype(bf16)
        own = own + jnp.dot(normed, w_own[pl.ds(at, 512), :], preferred_element_type=f32)
        par = par + jnp.dot(normed, w_par[pl.ds(at, 512), :], preferred_element_type=f32)
    for at, both in ((0, own), (128, par)):
        gate, up = both[:, :128], both[:, 128:]
        out_ref[:, at : at + 128] = (gate / (1.0 + jnp.exp(-gate)) * up).astype(bf16)


def down_kernel(a0, a1, a2, a3, w0, w1, w2, w3, out_ref):
    total = jnp.dot(a0[...], w0[...], preferred_element_type=f32)
    for a, w in ((a1, w1), (a2, w2), (a3, w3)):
        total = total + jnp.dot(a[...], w[...], preferred_element_type=f32)
    for s in range(WIDE):
        out_ref[s] = total[s * CAP : (s + 1) * CAP].astype(bf16)


def score_kernel(info_ref, vec_ref, doc_ref, out_ref):
    lane = lax.broadcasted_iota(jnp.int32, (1, 16), 1)
    scores = jnp.zeros((1, 16), f32)
    rows = lax.broadcasted_iota(jnp.int32, (144, 128), 0)
    columns = lax.broadcasted_iota(jnp.int32, (1, 128), 1)
    for d in range(16):
        first, size = info_ref[0, d], info_ref[1, d]
        q_first, q_size = info_ref[2, d], info_ref[3, d]
        at = pl.multiple_of(jnp.minimum((first // 16) * 16, 1024 - 144), 16)
        q_at = pl.multiple_of(jnp.minimum((q_first // 16) * 16, 4096 - 128), 16)
        sims = lax.dot_general(
            doc_ref[pl.ds(at, 144), :],
            vec_ref[pl.ds(q_at, 128), :],
            (((1,), (1,)), ((), ())),
            preferred_element_type=f32,
        )
        keep = (rows >= first - at) & (rows < first - at + size)
        best = jnp.max(jnp.where(keep, sims, NEG), axis=0, keepdims=True)
        used = (columns >= q_first - q_at) & (columns < q_first - q_at + q_size)
        value = jnp.sum(jnp.where(used, best, 0.0), axis=1, keepdims=True) / q_size.astype(f32)
        scores = jnp.where(lane == d, value, scores)
    out_ref[...] = scores


def vmem():
    return pl.BlockSpec(memory_space=pltpu.VMEM)


def smem():
    return pl.BlockSpec(memory_space=pltpu.SMEM)


def body(
    tokens,
    request_lengths,
    w_qkv,
    qk_gain,
    w_out,
    norm_gains,
    w_router,
    routes,
    w_gate,
    w_up,
    w_down,
    w_proj,
    doc_vectors,
    doc_segment,
    doc_request,
):
    i = lax.axis_index("xh")
    j = lax.axis_index("y")
    wide = lax.axis_index(W)

    def pick(array, which):
        return lax.dynamic_index_in_dim(array, which, 0, keepdims=False)

    w_own = jnp.concatenate([pick(w_gate, i), pick(w_up, i)], axis=1)
    w_par = x_swap(jnp.concatenate([pick(w_gate, 1 - i), pick(w_up, 1 - i)], axis=1))
    d_par = x_swap(pick(w_down, 1 - i))
    d_both = jnp.concatenate([pick(w_down, i), d_par], axis=0)

    def d_columns(which):
        return lax.dynamic_slice_in_dim(d_both, lax.rem(which, 4) * 512, 512, 1)

    downs = [d_columns(j)] + [y_shift(d_columns(j + k), k) for k in (1, 2, 3)]

    experts_here = 2 * jnp.arange(WIDE, dtype=jnp.int32) + i
    hit = jnp.sum((routes.T[None, :, :] == experts_here[:, None, None]).astype(f32), axis=1)
    places = jnp.arange(TOK, dtype=jnp.int32)
    earlier = (places[:, None] < places[None, :]).astype(bf16)
    before = jnp.dot(hit.astype(bf16), earlier, preferred_element_type=f32)
    slot = jnp.arange(CAP, dtype=jnp.int32).astype(f32)
    chosen = (before[:, None, :] == slot[None, :, None]) & (hit[:, None, :] > 0)

    heads = w_qkv.shape[2] // HD
    lengths_row = lax.dynamic_slice_in_dim(request_lengths, wide, 1, 0)[0]
    member, offsets = request_layout(lengths_row, TOK)
    xf = tokens.astype(f32)
    normed = rms_norm(xf, norm_gains[0]).astype(bf16)
    proj = jnp.dot(normed, w_qkv.reshape(2048, -1), preferred_element_type=f32).reshape(
        TOK, 3, heads, HD
    )
    query = rotary(rms_norm(proj[:, 0], qk_gain[0].reshape(heads, HD)), offsets).astype(bf16)
    keys = rotary(rms_norm(proj[:, 1], qk_gain[1].reshape(heads, HD)), offsets).astype(bf16)
    values = proj[:, 2].astype(bf16)
    scores = jnp.einsum("qhd,khd->hqk", query, keys, preferred_element_type=f32) * HD ** (-0.5)
    scores = jnp.where((member[:, None] == member[None, :])[None], scores, NEG)
    peak = jnp.max(scores, axis=-1, keepdims=True)
    weights = jnp.exp(scores - peak)
    probs = (weights / jnp.sum(weights, axis=-1, keepdims=True)).astype(bf16)
    mixed = (
        jnp.einsum("hqk,khd->qhd", probs, values, preferred_element_type=f32)
        .astype(bf16)
        .reshape(TOK, heads * HD)
    )
    w_out4 = w_out.reshape(heads * HD, 4, 512)
    attn = jnp.einsum("th,hyd->ytd", mixed, w_out4, preferred_element_type=f32).astype(bf16)
    attn = lax.all_to_all(attn, "y", 0, 0, tiled=True)
    attn = jnp.sum(attn.astype(f32), axis=0).astype(bf16)
    attn_par = x_swap(attn)
    mine = lax.dynamic_slice_in_dim(tokens, j * 512, 512, 1)
    hidden = (mine.astype(f32) + (attn.astype(f32) + attn_par.astype(f32))).astype(bf16)

    rows = lax.dot_general(
        chosen.astype(bf16), hidden, (((2,), (0,)), ((), ())), preferred_element_type=f32
    ).astype(bf16)
    rows = lax.all_to_all(rows, W, 0, 0, tiled=True).reshape(WIDE * CAP, 512)
    gathered = [rows] + [y_shift(rows, k) for k in (1, 2, 3)]

    hf = hidden.astype(f32)
    gain_mine = lax.dynamic_slice_in_dim(norm_gains[1], j * 512, 512, 0)
    router_mine = lax.dynamic_slice_in_dim(w_router, j * 512, 512, 0)
    part = jnp.dot((hf * gain_mine).astype(bf16), router_mine, preferred_element_type=f32)
    square = jnp.sum(hf * hf, axis=1, keepdims=True)
    part = jnp.concatenate([part, jnp.broadcast_to(square, (TOK, EXPERTS))], axis=1)
    whole = part
    for k in (1, 2, 3):
        whole = whole + y_shift(part, k)
    logits = whole[:, :EXPERTS] * lax.rsqrt(whole[:, EXPERTS : EXPERTS + 1] / 2048.0 + EPS)
    lifted = jax.nn.sigmoid(logits)
    onehot = jnp.sum(
        (routes[:, :, None] == jnp.arange(EXPERTS, dtype=jnp.int32)[None, None, :]).astype(f32),
        axis=1,
    )
    lifted = lifted * onehot
    gates = lifted / jnp.sum(lifted, axis=1, keepdims=True)
    gates = lax.dynamic_index_in_dim(gates.reshape(TOK, WIDE, 2), i, 2, keepdims=False).T
    mixing = jnp.where(chosen, gates[:, None, :], 0.0)
    mixing_hi = lax.reduce_precision(mixing, 8, 7)
    mixing_lo = (mixing - mixing_hi).astype(bf16)
    mixing_hi = mixing_hi.astype(bf16)

    act = pl.pallas_call(
        gate_up_kernel,
        out_shape=jax.ShapeDtypeStruct((WIDE * CAP, 256), bf16),
        in_specs=[smem()] + [vmem()] * 7,
        out_specs=vmem(),
        compiler_params=pltpu.CompilerParams(vmem_limit_bytes=40 << 20),
        name="gate_up",
    )(j.reshape(1), *gathered, w_own, w_par, norm_gains[1].reshape(4, 1, 512))
    acts = [act] + [y_shift(act, k) for k in (1, 2, 3)]
    out = pl.pallas_call(
        down_kernel,
        out_shape=jax.ShapeDtypeStruct((WIDE, CAP, 512), bf16),
        in_specs=[vmem()] * 8,
        out_specs=vmem(),
        compiler_params=pltpu.CompilerParams(vmem_limit_bytes=40 << 20),
        name="down",
    )(*acts, *downs)
    out = lax.all_to_all(out, W, 0, 0, tiled=True)

    contract = (((0, 1), (0, 1)), ((), ()))
    moe = lax.dot_general(mixing_hi, out, contract, preferred_element_type=f32)
    moe = moe + lax.dot_general(mixing_lo, out, contract, preferred_element_type=f32)
    moe = moe.astype(bf16)
    moe_par = x_swap(moe)
    layer = (hf + (moe.astype(f32) + moe_par.astype(f32))).astype(bf16)
    layer = lax.all_to_all(jnp.broadcast_to(layer[None], (4, TOK, 512)), "y", 0, 0, tiled=True)
    layer_out = layer.transpose(1, 0, 2).reshape(TOK, 2048)

    normed_three = rms_norm(layer_out.astype(f32), norm_gains[2]).astype(bf16)
    embedded = jnp.dot(normed_three, w_proj, preferred_element_type=f32)
    vectors = (
        embedded * lax.rsqrt(jnp.sum(embedded * embedded, axis=-1, keepdims=True) + EPS)
    ).astype(bf16)
    piece = lax.all_to_all(
        jnp.broadcast_to(vectors[None], (WIDE, TOK, 128)), W, 0, 0, tiled=True
    ).reshape(WIDE * TOK, 128)
    segment = doc_segment[0]
    requests = doc_request[0]
    docs = jnp.arange(16, dtype=jnp.int32)
    first = jnp.sum((segment[None, :] < docs[:, None]).astype(jnp.int32), axis=1)
    size = jnp.sum((segment[None, :] == docs[:, None]).astype(jnp.int32), axis=1)
    starts = jnp.cumsum(request_lengths, axis=1) - request_lengths
    starts = (starts + TOK * jnp.arange(WIDE, dtype=jnp.int32)[:, None]).reshape(-1)
    match = requests[:, None] == jnp.arange(96, dtype=jnp.int32)[None, :]
    q_first = jnp.sum(jnp.where(match, starts[None, :], 0), axis=1)
    q_size = jnp.sum(jnp.where(match, request_lengths.reshape(-1)[None, :], 0), axis=1)
    info = jnp.stack([first, size, q_first, q_size])
    doc_scores = pl.pallas_call(
        score_kernel,
        out_shape=jax.ShapeDtypeStruct((1, 16), f32),
        in_specs=[smem(), vmem(), vmem()],
        out_specs=vmem(),
        name="score",
    )(info, piece, doc_vectors)
    return (layer_out, doc_scores)


def solution(mesh):
    split = Mesh(mesh.devices.reshape(8, 2, 2, 2, 4), ("z", "xl", "core", "xh", "y"))
    placed = (
        P(W, None),
        P(),
        P(None, None, N),
        P(None, N),
        P(N, None),
        P(),
        P(),
        P(W, None),
        P(W, None, N),
        P(W, None, N),
        P(W, N, None),
        P(),
        P(W + N, None),
        P(W + N, None),
        P(W + N, None),
    )
    return jax.shard_map(
        body,
        mesh=split,
        in_specs=placed,
        out_specs=(P(W, None), P(W + N, None)),
        check_vma=False,
    )
```

time: 671 us -> 225 us (0.34)
  waiting for transfers between devices: 354 us -> 119 us
  blocking collectives: 153 us -> 10.3 us
  local copies, waits for them, and re-layouts: 69 us -> 16.2 us
  matrix products: 59.6 us -> 7.85 us
  starting transfers between devices: 6.06 us -> 55.7 us
  between operations: 14.1 us -> 1.1 us
  other arithmetic: 13.8 us -> 6 us
  Pallas kernels: 0 us -> 7.24 us
    psum x2 -> x0, waiting for transfers between devices: 170 us -> none  [the longest x1 91.5 us: body(): attn = lax.psum(jnp.dot(mixed, w_out, preferred_element_type=f32), 'narrow')]
    all_to_all x1, blocking collectives: 153 us -> 10.3 us  [body(): lax.all_to_all(jnp.broadcast_to(layer[None], (4, TOK, 512)), 'y', 0, 0, t...]
    all_gather x1 -> x0, waiting for transfers between devices: 65.5 us -> none  [body(): piece = lax.all_gather(vectors, 'wide', axis=0, tiled=True)]
    ppermute x0 -> x16, waiting for transfers between devices: none -> 58.3 us  [the longest x12 30.6 us: y_shift(): return lax.ppermute(x, 'y', [(s, (s + k) % 4) for s in range(4)])]
    all_to_all x1 -> x4, waiting for transfers between devices: 119 us -> 61.1 us  [the longest x1 25.8 us: body(): lax.all_to_all(jnp.broadcast_to(vectors[None], (WIDE, TOK, 128)), W, 0, 0...]
    dot_general x7, matrix products: 56.9 us -> 6.52 us  [the longest x1 2.94 us: body(): jnp.dot(normed, w_qkv.reshape(2048, -1), preferred_element_type=f32)]
    all_to_all x1 -> x4, starting transfers between devices: 5.67 us -> 31.8 us  [the longest x1 13.1 us: body(): rows = lax.all_to_all(rows, W, 0, 0, tiled=True).reshape(WIDE * CAP, 512)]
    ppermute x0 -> x16, starting transfers between devices: none -> 23.9 us  [the longest x12 14.9 us: y_shift(): return lax.ppermute(x, 'y', [(s, (s + k) % 4) for s in range(4)])]
  transfers between devices with their start and end apart: 4 -> 20, of which waited for: 4 -> 14; matrix products, arithmetic and copies ran while one was open for 0% -> 4% of each run, Pallas kernels for 0% -> 1%
where the time goes in v1:
time: 225 us; the launch traced here: 224 us
  waiting for transfers between devices  119 us (53%)
  starting transfers between devices  55.7 us (25%)
  local copies, waits for them, and re-layouts  16.2 us (7%)
  blocking collectives  10.3 us (5%)
  matrix products  7.85 us (3%)
  Pallas kernels  7.24 us (3%)
  other arithmetic  6 us (3%)
    ppermute x12, waiting for transfers between devices, y_shift(): return lax.ppermute(x, 'y', [(s, (s + k) % 4) for s in range(4)])  30.6 us
    ppermute x4, waiting for transfers between devices, x_swap(): return lax.ppermute(x, 'xh', [(0, 1), (1, 0)])  27.7 us
    all_to_all x1, waiting for transfers between devices, body(): lax.all_to_all(jnp.broadcast_to(vectors[None], (WIDE, TOK, 128)), W, 0, 0...  25.8 us
    all_to_all x1, waiting for transfers between devices, body(): rows = lax.all_to_all(rows, W, 0, 0, tiled=True).reshape(WIDE * CAP, 512)  15.1 us
    ppermute x12, starting transfers between devices, y_shift(): return lax.ppermute(x, 'y', [(s, (s + k) % 4) for s in range(4)])  14.9 us
    all_to_all x1, starting transfers between devices, body(): rows = lax.all_to_all(rows, W, 0, 0, tiled=True).reshape(WIDE * CAP, 512)  13.1 us
    all_to_all x1, waiting for transfers between devices, body(): out = lax.all_to_all(out, W, 0, 0, tiled=True)  12.9 us
    all_to_all x1, blocking collectives, body(): lax.all_to_all(jnp.broadcast_to(layer[None], (4, TOK, 512)), 'y', 0, 0, t...  10.3 us
  transfers between devices with their start and end apart: 20, of which 14 were waited for; matrix products, arithmetic and copies ran while one was open for 4% of the time, Pallas kernels for 1%

profile of v1, /device:TPU:1, one launch (start us, length us, event | category | flops | bytes accessed | tf_op | source)
XLA Modules:
  0.0 223.8 jit_solution(6199422477784024049)
XLA Ops:
  0.7 0.8 copy.75
  2.1 4.8 %copy.74 = bf16[2048,3,256]{0,2,1:T(8,128)(2,1)} copy(bf16[2048,3,256]{2,0,1:T(8,128)(2,1)} %param.17) | data formatting | bytes 6291456 | tf_op args[2]
  7.7 2.9 %fusion.14 = f32[128,3,2,128]{0,3,2,1:T(8,128)S(1)} fusion(bf16[3,2,128,2048]{3,2,1,0:T(8,128)(2,1)} %bitcast.99, bf16[128,2048]{1,0:T(8,128)(2,1)S(1)} %copy-done.2, f32[2048]{0:T(1024)S(1)} %bitcast.106, f32[128]{0:T(128)S(1)} %add_rsqrt_fusion.4), kind=kOutput, calls=%fused_computation.34 | convolution fusion | flops 403701760 | bytes 4071936 | tf_op jit(solution)/shard_map/dot_general | solution.py:168
  12.1 1.1 fusion.1
  13.2 5.0 %all-to-all-start = ((bf16[4,128,512]{2,1,0:T(8,128)(2,1)}), bf16[4,128,512]{2,1,0:T(8,128)(2,1)S(1)}, u32[]{:S(2)}, u32[]{:S(2)}) async-start(bf16[4,128,512]{2,1,0:T(8,128)(2,1)} %fusion.1), calls=%async_computation | async-start | bytes 1048576 | tf_op jit(solution)/shard_map/all_to_all | solution.py:186
  18.5 7.3 %all-to-all-done = bf16[4,128,512]{2,1,0:T(8,128)(2,1)S(1)} async-done(((bf16[4,128,512]{2,1,0:T(8,128)(2,1)}), bf16[4,128,512]{2,1,0:T(8,128)(2,1)S(1)}, u32[]{:S(2)}, u32[]{:S(2)}) %all-to-all-start) | async-done | bytes 524320 | tf_op jit(solution)/shard_map/all_to_all | solution.py:186
  25.8 3.6 %collective-permute-start = (bf16[128,512]{1,0:T(8,128)(2,1)S(1)}, bf16[128,512]{1,0:T(8,128)(2,1)S(1)}, u32[]{:S(2)}, u32[]{:S(2)}) collective-permute-start(bf16[128,512]{1,0:T(8,128)(2,1)S(1)} %reduce_sum.162), channel_id=1, source_target_pairs={{0,4},{4,0},{1,5},{5,1},{2,6},{6,2},{3,7},{7,3},{8,12},{12,8},{9,1... | collective-permute-start | bytes 393224 | tf_op jit(solution)/shard_map/ppermute | solution.py:57
  29.4 2.3 %collective-permute-done = bf16[128,512]{1,0:T(8,128)(2,1)S(1)} collective-permute-done((bf16[128,512]{1,0:T(8,128)(2,1)S(1)}, bf16[128,512]{1,0:T(8,128)(2,1)S(1)}, u32[]{:S(2)}, u32[]{:S(2)}) %collective-permute-start) | collective-permute-done | bytes 131104 | tf_op jit(solution)/shard_map/ppermute | solution.py:57
  31.7 0.7 fusion.24
  32.4 0.6 copy-done.5
  33.5 1.3 copy.81
  34.8 13.1 %all-to-all-start.1 = ((bf16[32,20,512]{2,1,0:T(8,128)(2,1)}), bf16[32,20,512]{2,1,0:T(8,128)(2,1)S(1)}, u32[]{:S(2)}, u32[]{:S(2)}) async-start(bf16[32,20,512]{2,1,0:T(8,128)(2,1)} %copy.81), calls=%async_computation.1 | async-start | bytes 1572864 | tf_op jit(solution)/shard_map/all_to_all | solution.py:195
  47.9 2.4 %dynamic-slice_bitcast_fusion.2 = (bf16[2048,128]{1,0:T(8,128)(2,1)S(1)}, bf16[2048,128]{1,0:T(8,128)(2,1)}, bf16[2048,128]{1,0:T(8,128)(2,1)}, bf16[2048,128]{1,0:T(8,128)(2,1)S(1)}) fusion(bf16[2,2048,128]{2,1,0:T(8,128)(2,1)S(1)} %copy-done.7, s32[]{:T(128)S(6)} %select_n.59, s32[]{:T(128)S(6)} %select_n.57, bf16[2,2048,128]{2,1,0:T(8,128)(2,1)} %param.23), kind=kLoop, calls=%fused_computation.39 | loop fusion | bytes 4194312 | tf_op jit(solution)/shard_map/jit(dynamic_index_in_dim)/squeeze | solution.py:143
  50.3 1.1 pad_maximum_fusion.1
  51.4 2.4 %collective-permute-start.7 = (bf16[2048,256]{1,0:T(8,128)(2,1)}, bf16[2048,256]{1,0:T(8,128)(2,1)S(1)}, u32[]{:S(2)}, u32[]{:S(2)}) collective-permute-start(bf16[2048,256]{1,0:T(8,128)(2,1)} %pad_maximum_fusion.1), channel_id=1, source_target_pairs={{0,4},{4,0},{1,5},{5,1},{2,6},{6,2},{3,7},{7,3},{8,12},{12,8},{9,1... | collective-permute-start | bytes 3145736 | tf_op jit(solution)/shard_map/ppermute | solution.py:57
  53.8 1.0 dynamic-slice_bitcast_fusion
  55.4 15.1 %all-to-all-done.1 = bf16[32,20,512]{2,1,0:T(8,128)(2,1)S(1)} async-done(((bf16[32,20,512]{2,1,0:T(8,128)(2,1)}), bf16[32,20,512]{2,1,0:T(8,128)(2,1)S(1)}, u32[]{:S(2)}, u32[]{:S(2)}) %all-to-all-start.1) | async-done | bytes 655392 | tf_op jit(solution)/shard_map/all_to_all | solution.py:195
  71.0 1.8 collective-permute-start.5
  72.8 0.7 collective-permute-start.6
  73.5 22.4 %collective-permute-done.11 = bf16[128,2048]{1,0:T(8,128)(2,1)} collective-permute-done((bf16[128,2048]{1,0:T(8,128)(2,1)}, bf16[128,2048]{1,0:T(8,128)(2,1)}, u32[]{:S(2)}, u32[]{:S(2)}) %collective-permute-start.11) | collective-permute-done | bytes 524320 | tf_op jit(solution)/shard_map/ppermute | solution.py:57
  95.9 1.4 fusion.26
  97.8 2.7 %collective-permute-done.5.x2 = bf16[640,512]{1,0:T(8,128)(2,1)S(1)} collective-permute-done((bf16[640,512]{1,0:T(8,128)(2,1)S(1)}, bf16[640,512]{1,0:T(8,128)(2,1)S(1)}, u32[]{:S(2)}, u32[]{:S(2)}) %collective-permute-start.5) | collective-permute-done | bytes 655392 | tf_op jit(solution)/shard_map/ppermute | solution.py:53
  100.5 1.3 collective-permute-done.6.x3
  101.8 3.1 %gate_up.1.a0 = bf16[640,256]{1,0:T(8,128)(2,1)S(1)} custom-call(s32[1]{0:T(128)} %bitcast.25.j_ref, bf16[640,512]{1,0:T(8,128)(2,1)S(1)} %reshape.209.x0, bf16[640,512]{1,0:T(8,128)(2,1)S(1)} %collective-permute-done.4.x1, bf16[640,512]{1,0:T(8,128)(2,1)S(1)} %collective-permute-done.5.x2, bf16[640,512]{1,0:T(8,128)(2,1)} %collective-permute-done.6.x3, ...), custom_call_target="tpu_custom_call" | custom-call | tf_op jit(solution)/shard_map/gate_up/pallas_call | solution.py:221
  104.9 1.7 collective-permute-start.8
  106.6 3.1 %collective-permute-start.9 = (bf16[640,256]{1,0:T(8,128)(2,1)S(1)}, bf16[640,256]{1,0:T(8,128)(2,1)S(1)}, u32[]{:S(2)}, u32[]{:S(2)}) collective-permute-start(bf16[640,256]{1,0:T(8,128)(2,1)S(1)} %gate_up.1.a0), channel_id=1, source_target_pairs={{0,2},{1,3},{2,0},{3,1},{4,6},{5,7},{6,4},{7,5},{8,10},{9,11},{10,... | collective-permute-start | bytes 983048 | tf_op jit(solution)/shard_map/ppermute | solution.py:53
  109.7 1.5 collective-permute-start.13
  111.2 2.4 %collective-permute-start.14 = (bf16[256,512]{1,0:T(8,128)(2,1)S(1)}, bf16[256,512]{1,0:T(8,128)(2,1)S(1)}, u32[]{:S(2)}, u32[]{:S(2)}) collective-permute-start(bf16[256,512]{1,0:T(8,128)(2,1)S(1)} %get-tuple-element.14), channel_id=1, source_target_pairs={{0,3},{1,0},{2,1},{3,2},{4,7},{5,4},{6,5},{7,6},{8,11},{9,8},{10,9... | collective-permute-start | bytes 786440 | tf_op jit(solution)/shard_map/ppermute | solution.py:53
  113.6 15.9 %collective-permute-done.13.w2 = bf16[256,512]{1,0:T(8,128)(2,1)S(1)} collective-permute-done((bf16[256,512]{1,0:T(8,128)(2,1)S(1)}, bf16[256,512]{1,0:T(8,128)(2,1)S(1)}, u32[]{:S(2)}, u32[]{:S(2)}) %collective-permute-start.13) | collective-permute-done | bytes 262176 | tf_op jit(solution)/shard_map/ppermute | solution.py:53
  129.4 5.3 %collective-permute-done.14.w3 = bf16[256,512]{1,0:T(8,128)(2,1)S(1)} collective-permute-done((bf16[256,512]{1,0:T(8,128)(2,1)S(1)}, bf16[256,512]{1,0:T(8,128)(2,1)S(1)}, u32[]{:S(2)}, u32[]{:S(2)}) %collective-permute-start.14) | collective-permute-done | bytes 262176 | tf_op jit(solution)/shard_map/ppermute | solution.py:53
  134.8 1.7 down.1
  136.5 5.4 %all-to-all-start.2 = ((bf16[32,20,512]{2,1,0:T(8,128)(2,1)}), bf16[32,20,512]{2,1,0:T(8,128)(2,1)S(1)}, u32[]{:S(2)}, u32[]{:S(2)}) async-start(bf16[32,20,512]{2,1,0:T(8,128)(2,1)} %down.1), calls=%async_computation.2 | async-start | bytes 1572864 | tf_op jit(solution)/shard_map/all_to_all | solution.py:238
  142.0 1.0 fusion.44
  143.0 2.4 %collective-permute-start.3 = (f32[128,128]{0,1:T(8,128)S(1)}, f32[128,128]{0,1:T(8,128)S(1)}, u32[]{:S(2)}, u32[]{:S(2)}) collective-permute-start(f32[128,128]{0,1:T(8,128)S(1)} %pad_maximum_fusion.2), channel_id=1, source_target_pairs={{0,3},{1,0},{2,1},{3,2},{4,7},{5,4},{6,5},{7,6},{8,11},{9,8},{10,9... | collective-permute-start | bytes 196616 | tf_op jit(solution)/shard_map/ppermute | solution.py:53
  145.4 0.7 collective-permute-start.1
  146.8 3.6 %collective-permute-done.2 = f32[128,128]{0,1:T(8,128)S(1)} collective-permute-done((f32[128,128]{0,1:T(8,128)S(1)}, f32[128,128]{0,1:T(8,128)S(1)}, u32[]{:S(2)}, u32[]{:S(2)}) %collective-permute-start.2) | collective-permute-done | bytes 65568 | tf_op jit(solution)/shard_map/ppermute | solution.py:53
  150.3 1.2 collective-permute-done.1
  151.7 12.9 %all-to-all-done.2 = bf16[32,20,512]{2,1,0:T(8,128)(2,1)S(1)} async-done(((bf16[32,20,512]{2,1,0:T(8,128)(2,1)}), bf16[32,20,512]{2,1,0:T(8,128)(2,1)S(1)}, u32[]{:S(2)}, u32[]{:S(2)}) %all-to-all-start.2) | async-done | bytes 655392 | tf_op jit(solution)/shard_map/all_to_all | solution.py:238
  165.5 2.5 %collective-permute-start.15 = (bf16[128,512]{1,0:T(8,128)(2,1)S(1)}, bf16[128,512]{1,0:T(8,128)(2,1)S(1)}, u32[]{:S(2)}, u32[]{:S(2)}) collective-permute-start(bf16[128,512]{1,0:T(8,128)(2,1)S(1)} %fusion.3), channel_id=1, source_target_pairs={{0,4},{4,0},{1,5},{5,1},{2,6},{6,2},{3,7},{7,3},{8,12},{12,8},{9,1... | collective-permute-start | bytes 393224 | tf_op jit(solution)/shard_map/ppermute | solution.py:57
  168.0 3.0 %collective-permute-done.15 = bf16[128,512]{1,0:T(8,128)(2,1)S(1)} collective-permute-done((bf16[128,512]{1,0:T(8,128)(2,1)S(1)}, bf16[128,512]{1,0:T(8,128)(2,1)S(1)}, u32[]{:S(2)}, u32[]{:S(2)}) %collective-permute-start.15) | collective-permute-done | bytes 131104 | tf_op jit(solution)/shard_map/ppermute | solution.py:57
  171.1 10.3 %all_to_all.25 = bf16[4,128,512]{2,1,0:T(8,128)(2,1)S(1)} all-to-all(bf16[4,128,512]{2,1,0:T(8,128)(2,1)S(1)} %broadcast_in_dim.70), channel_id=1, replica_groups=mesh['z'=8,'xl'=2,'core'=2,'xh'=2,'y'=4] {'y'}, dimensions={0} | all-to-all | bytes 1048576 | tf_op jit(solution)/shard_map/all_to_all | solution.py:246
  182.0 0.7 multiply_reduce_fusion.3
  182.8 1.2 broadcast_in_dim.76
  184.1 8.2 %all-to-all-start.4 = ((bf16[32,128,128]{2,1,0:T(8,128)(2,1)}), bf16[32,128,128]{2,1,0:T(8,128)(2,1)S(1)}, u32[]{:S(2)}, u32[]{:S(2)}) async-start(bf16[32,128,128]{2,1,0:T(8,128)(2,1)} %broadcast_in_dim.76), calls=%async_computation.4 | async-start | bytes 2097152 | tf_op jit(solution)/shard_map/all_to_all | solution.py:254
  193.6 1.0 copy.88
  194.6 25.8 %all-to-all-done.4 = bf16[32,128,128]{2,1,0:T(8,128)(2,1)S(1)} async-done(((bf16[32,128,128]{2,1,0:T(8,128)(2,1)}), bf16[32,128,128]{2,1,0:T(8,128)(2,1)S(1)}, u32[]{:S(2)}, u32[]{:S(2)}) %all-to-all-start.4) | async-done | bytes 1048608 | tf_op jit(solution)/shard_map/all_to_all | solution.py:254
  220.4 1.0 copy-done.1
  221.4 2.4 %score.1 = f32[1,16]{1,0:T(1,128)} custom-call(s32[4,16]{1,0:T(4,128)} %pad_add_fusion.info_ref, bf16[4096,128]{1,0:T(8,128)(2,1)} %bitcast.102, bf16[1024,128]{1,0:T(8,128)(2,1)} %doc_ref.1), custom_call_target="tpu_custom_call" | custom-call | tf_op jit(solution)/shard_map/score/pallas_call | solution.py:268
  (116 shorter events, 8.8 us)
Async XLA Ops:
  0.6 181.3 %copy-start = (bf16[2048,128]{1,0:T(8,128)(2,1)S(1)}, bf16[2048,128]{1,0:T(8,128)(2,1)}, u32[]{:S(2)}) copy-start(bf16[2048,128]{1,0:T(8,128)(2,1)} %param.26) | copy-start | bytes 1572868
  1.5 0.6 copy-start.10
  2.1 4.8 %copy-start.14 = (f32[3,2048]{1,0:T(4,128)S(1)}, f32[3,2048]{1,0:T(4,128)}, u32[]{:S(2)}) copy-start(f32[3,2048]{1,0:T(4,128)} %param.20) | copy-start | bytes 73732
  2.1 5.4 %copy-start.2 = (bf16[128,2048]{1,0:T(8,128)(2,1)S(1)}, bf16[128,2048]{1,0:T(8,128)(2,1)}, u32[]{:S(2)}) copy-start(bf16[128,2048]{1,0:T(8,128)(2,1)} %param.15) | copy-start | bytes 1572868
  2.1 5.6 %copy-start.19 = (f32[2,256]{1,0:T(2,128)S(1)}, f32[2,256]{1,0:T(2,128)}, u32[]{:S(2)}) copy-start(f32[2,256]{1,0:T(2,128)} %param.18) | copy-start | bytes 6148
  10.6 1.4 copy-start.8
  11.3 6.9 %copy-start.16 = (s32[128,8]{0,1:T(8,128)S(1)}, s32[128,8]{0,1:T(8,128)}, u32[]{:S(2)}) copy-start(s32[128,8]{0,1:T(8,128)} %param.22) | copy-start | bytes 12292
  13.2 12.6 %all-to-all-start = ((bf16[4,128,512]{2,1,0:T(8,128)(2,1)}), bf16[4,128,512]{2,1,0:T(8,128)(2,1)S(1)}, u32[]{:S(2)}, u32[]{:S(2)}) async-start(bf16[4,128,512]{2,1,0:T(8,128)(2,1)} %fusion.1), calls=%async_computation | async-start | bytes 1048576 | tf_op jit(solution)/shard_map/all_to_all | solution.py:186
  18.5 16.3 %copy-start.12 = (f32[32,128]{1,0:T(8,128)}, f32[32,128]{1,0:T(8,128)S(1)}, u32[]{:S(2)}) copy-start(f32[32,128]{1,0:T(8,128)S(1)} %fusion.58) | copy-start | bytes 49156
  25.8 5.9 %collective-permute-start = (bf16[128,512]{1,0:T(8,128)(2,1)S(1)}, bf16[128,512]{1,0:T(8,128)(2,1)S(1)}, u32[]{:S(2)}, u32[]{:S(2)}) collective-permute-start(bf16[128,512]{1,0:T(8,128)(2,1)S(1)} %reduce_sum.162), channel_id=1, source_target_pairs={{0,4},{4,0},{1,5},{5,1},{2,6},{6,2},{3,7},{7,3},{8,12},{12,8},{9,1... | collective-permute-start | bytes 393224 | tf_op jit(solution)/shard_map/ppermute | solution.py:57
  29.4 5.4 %copy-start.22 = (f32[20]{0:T(128)}, f32[20]{0:T(128)S(1)}, u32[]{:S(2)}) copy-start(f32[20]{0:T(128)S(1)} %iota_convert_fusion) | copy-start | bytes 244
  29.4 18.5 %copy-start.7 = (bf16[2,2048,128]{2,1,0:T(8,128)(2,1)S(1)}, bf16[2,2048,128]{2,1,0:T(8,128)(2,1)}, u32[]{:S(2)}) copy-start(bf16[2,2048,128]{2,1,0:T(8,128)(2,1)} %param.24) | copy-start | bytes 3145732
  32.4 0.6 copy-start.5
  34.8 35.7 %all-to-all-start.1 = ((bf16[32,20,512]{2,1,0:T(8,128)(2,1)}), bf16[32,20,512]{2,1,0:T(8,128)(2,1)S(1)}, u32[]{:S(2)}, u32[]{:S(2)}) async-start(bf16[32,20,512]{2,1,0:T(8,128)(2,1)} %copy.81), calls=%async_computation.1 | async-start | bytes 1572864 | tf_op jit(solution)/shard_map/all_to_all | solution.py:195
  50.3 3.6 %copy-start.9 = (bf16[2,128,2048]{2,1,0:T(8,128)(2,1)S(1)}, bf16[2,128,2048]{2,1,0:T(8,128)(2,1)}, u32[]{:S(2)}) copy-start(bf16[2,128,2048]{2,1,0:T(8,128)(2,1)} %param.25) | copy-start | bytes 3145732
  51.4 46.4 %collective-permute-start.7 = (bf16[2048,256]{1,0:T(8,128)(2,1)}, bf16[2048,256]{1,0:T(8,128)(2,1)S(1)}, u32[]{:S(2)}, u32[]{:S(2)}) collective-permute-start(bf16[2048,256]{1,0:T(8,128)(2,1)} %pad_maximum_fusion.1), channel_id=1, source_target_pairs={{0,4},{4,0},{1,5},{5,1},{2,6},{6,2},{3,7},{7,3},{8,12},{12,8},{9,1... | collective-permute-start | bytes 3145736 | tf_op jit(solution)/shard_map/ppermute | solution.py:57
  54.9 41.0 %collective-permute-start.11 = (bf16[128,2048]{1,0:T(8,128)(2,1)}, bf16[128,2048]{1,0:T(8,128)(2,1)}, u32[]{:S(2)}, u32[]{:S(2)}) collective-permute-start(bf16[128,2048]{1,0:T(8,128)(2,1)} %get-tuple-element.18), channel_id=1, source_target_pairs={{0,4},{4,0},{1,5},{5,1},{2,6},{6,2},{3,7},{7,3},{8,12},{12,8},{9,1... | collective-permute-start | bytes 1572872 | tf_op jit(solution)/shard_map/ppermute | solution.py:57
  70.6 27.2 %collective-permute-start.4 = (bf16[640,512]{1,0:T(8,128)(2,1)S(1)}, bf16[640,512]{1,0:T(8,128)(2,1)S(1)}, u32[]{:S(2)}, u32[]{:S(2)}) collective-permute-start(bf16[640,512]{1,0:T(8,128)(2,1)S(1)} %reshape.209.x0), channel_id=1, source_target_pairs={{0,1},{1,2},{2,3},{3,0},{4,5},{5,6},{6,7},{7,4},{8,9},{9,10},{10,1... | collective-permute-start | bytes 1966088 | tf_op jit(solution)/shard_map/ppermute | solution.py:53
  71.0 29.5 %collective-permute-start.5 = (bf16[640,512]{1,0:T(8,128)(2,1)S(1)}, bf16[640,512]{1,0:T(8,128)(2,1)S(1)}, u32[]{:S(2)}, u32[]{:S(2)}) collective-permute-start(bf16[640,512]{1,0:T(8,128)(2,1)S(1)} %reshape.209.x0), channel_id=1, source_target_pairs={{0,2},{1,3},{2,0},{3,1},{4,6},{5,7},{6,4},{7,5},{8,10},{9,11},{10,... | collective-permute-start | bytes 1966088 | tf_op jit(solution)/shard_map/ppermute | solution.py:53
  72.8 29.0 %collective-permute-start.6 = (bf16[640,512]{1,0:T(8,128)(2,1)S(1)}, bf16[640,512]{1,0:T(8,128)(2,1)}, u32[]{:S(2)}, u32[]{:S(2)}) collective-permute-start(bf16[640,512]{1,0:T(8,128)(2,1)S(1)} %reshape.209.x0), channel_id=1, source_target_pairs={{0,3},{1,0},{2,1},{3,2},{4,7},{5,4},{6,5},{7,6},{8,11},{9,8},{10,9... | collective-permute-start | bytes 1966088 | tf_op jit(solution)/shard_map/ppermute | solution.py:53
  73.5 24.2 %copy-start.3 = (bf16[2048,128]{1,0:T(8,128)(2,1)S(1)}, bf16[2048,128]{1,0:T(8,128)(2,1)}, u32[]{:S(2)}) copy-start(bf16[2048,128]{1,0:T(8,128)(2,1)} %get-tuple-element.23) | copy-start | bytes 1572868
  73.5 24.2 %copy-start.4 = (bf16[2048,128]{1,0:T(8,128)(2,1)S(1)}, bf16[2048,128]{1,0:T(8,128)(2,1)}, u32[]{:S(2)}) copy-start(bf16[2048,128]{1,0:T(8,128)(2,1)} %get-tuple-element.43) | copy-start | bytes 1572868
  97.3 13.9 %collective-permute-start.12 = (bf16[256,512]{1,0:T(8,128)(2,1)S(1)}, bf16[256,512]{1,0:T(8,128)(2,1)S(1)}, u32[]{:S(2)}, u32[]{:S(2)}) collective-permute-start(bf16[256,512]{1,0:T(8,128)(2,1)S(1)} %get-tuple-element.16), channel_id=1, source_target_pairs={{0,1},{1,2},{2,3},{3,0},{4,5},{5,6},{6,7},{7,4},{8,9},{9,10},{10,1... | collective-permute-start | bytes 786440 | tf_op jit(solution)/shard_map/ppermute | solution.py:53
  104.9 29.9 %collective-permute-start.8 = (bf16[640,256]{1,0:T(8,128)(2,1)S(1)}, bf16[640,256]{1,0:T(8,128)(2,1)S(1)}, u32[]{:S(2)}, u32[]{:S(2)}) collective-permute-start(bf16[640,256]{1,0:T(8,128)(2,1)S(1)} %gate_up.1.a0), channel_id=1, source_target_pairs={{0,1},{1,2},{2,3},{3,0},{4,5},{5,6},{6,7},{7,4},{8,9},{9,10},{10,1... | collective-permute-start | bytes 983048 | tf_op jit(solution)/shard_map/ppermute | solution.py:53
  106.6 28.2 %collective-permute-start.9 = (bf16[640,256]{1,0:T(8,128)(2,1)S(1)}, bf16[640,256]{1,0:T(8,128)(2,1)S(1)}, u32[]{:S(2)}, u32[]{:S(2)}) collective-permute-start(bf16[640,256]{1,0:T(8,128)(2,1)S(1)} %gate_up.1.a0), channel_id=1, source_target_pairs={{0,2},{1,3},{2,0},{3,1},{4,6},{5,7},{6,4},{7,5},{8,10},{9,11},{10,... | collective-permute-start | bytes 983048 | tf_op jit(solution)/shard_map/ppermute | solution.py:53
  109.7 25.1 %collective-permute-start.10 = (bf16[640,256]{1,0:T(8,128)(2,1)S(1)}, bf16[640,256]{1,0:T(8,128)(2,1)S(1)}, u32[]{:S(2)}, u32[]{:S(2)}) collective-permute-start(bf16[640,256]{1,0:T(8,128)(2,1)S(1)} %gate_up.1.a0), channel_id=1, source_target_pairs={{0,3},{1,0},{2,1},{3,2},{4,7},{5,4},{6,5},{7,6},{8,11},{9,8},{10,9... | collective-permute-start | bytes 983048 | tf_op jit(solution)/shard_map/ppermute | solution.py:53
  109.7 19.7 %collective-permute-start.13 = (bf16[256,512]{1,0:T(8,128)(2,1)S(1)}, bf16[256,512]{1,0:T(8,128)(2,1)S(1)}, u32[]{:S(2)}, u32[]{:S(2)}) collective-permute-start(bf16[256,512]{1,0:T(8,128)(2,1)S(1)} %get-tuple-element.17), channel_id=1, source_target_pairs={{0,2},{1,3},{2,0},{3,1},{4,6},{5,7},{6,4},{7,5},{8,10},{9,11},{10,... | collective-permute-start | bytes 786440 | tf_op jit(solution)/shard_map/ppermute | solution.py:53
  111.2 23.6 %collective-permute-start.14 = (bf16[256,512]{1,0:T(8,128)(2,1)S(1)}, bf16[256,512]{1,0:T(8,128)(2,1)S(1)}, u32[]{:S(2)}, u32[]{:S(2)}) collective-permute-start(bf16[256,512]{1,0:T(8,128)(2,1)S(1)} %get-tuple-element.14), channel_id=1, source_target_pairs={{0,3},{1,0},{2,1},{3,2},{4,7},{5,4},{6,5},{7,6},{8,11},{9,8},{10,9... | collective-permute-start | bytes 786440 | tf_op jit(solution)/shard_map/ppermute | solution.py:53
  134.8 7.2 %copy-start.6 = (bf16[128,512]{1,0:T(8,128)(2,1)S(1)}, bf16[128,512]{1,0:T(8,128)(2,1)}, u32[]{:S(2)}) copy-start(bf16[128,512]{1,0:T(8,128)(2,1)} %copy-done.5) | copy-start | bytes 393220
  134.8 8.2 %copy-start.20 = (f32[128]{0:T(128)S(1)}, f32[128]{0:T(128)}, u32[]{:S(2)}) copy-start(f32[128]{0:T(128)} %get-tuple-element.12) | copy-start | bytes 1540
  134.8 29.8 %copy-start.13 = (f32[32,128]{1,0:T(8,128)S(1)}, f32[32,128]{1,0:T(8,128)}, u32[]{:S(2)}) copy-start(f32[32,128]{1,0:T(8,128)} %copy-done.12) | copy-start | bytes 49156
  134.8 29.8 %copy-start.23 = (f32[20]{0:T(128)S(1)}, f32[20]{0:T(128)}, u32[]{:S(2)}) copy-start(f32[20]{0:T(128)} %copy-done.22) | copy-start | bytes 244
  136.5 28.0 %all-to-all-start.2 = ((bf16[32,20,512]{2,1,0:T(8,128)(2,1)}), bf16[32,20,512]{2,1,0:T(8,128)(2,1)S(1)}, u32[]{:S(2)}, u32[]{:S(2)}) async-start(bf16[32,20,512]{2,1,0:T(8,128)(2,1)} %down.1), calls=%async_computation.2 | async-start | bytes 1572864 | tf_op jit(solution)/shard_map/all_to_all | solution.py:238
  143.0 3.7 %collective-permute-start.3 = (f32[128,128]{0,1:T(8,128)S(1)}, f32[128,128]{0,1:T(8,128)S(1)}, u32[]{:S(2)}, u32[]{:S(2)}) collective-permute-start(f32[128,128]{0,1:T(8,128)S(1)} %pad_maximum_fusion.2), channel_id=1, source_target_pairs={{0,3},{1,0},{2,1},{3,2},{4,7},{5,4},{6,5},{7,6},{8,11},{9,8},{10,9... | collective-permute-start | bytes 196616 | tf_op jit(solution)/shard_map/ppermute | solution.py:53
  145.4 4.9 %collective-permute-start.2 = (f32[128,128]{0,1:T(8,128)S(1)}, f32[128,128]{0,1:T(8,128)S(1)}, u32[]{:S(2)}, u32[]{:S(2)}) collective-permute-start(f32[128,128]{0,1:T(8,128)S(1)} %pad_maximum_fusion.2), channel_id=1, source_target_pairs={{0,2},{1,3},{2,0},{3,1},{4,6},{5,7},{6,4},{7,5},{8,10},{9,11},{10,... | collective-permute-start | bytes 196616 | tf_op jit(solution)/shard_map/ppermute | solution.py:53
  145.4 6.1 %collective-permute-start.1 = (f32[128,128]{0,1:T(8,128)S(1)}, f32[128,128]{0,1:T(8,128)S(1)}, u32[]{:S(2)}, u32[]{:S(2)}) collective-permute-start(f32[128,128]{0,1:T(8,128)S(1)} %pad_maximum_fusion.2), channel_id=1, source_target_pairs={{0,1},{1,2},{2,3},{3,0},{4,5},{5,6},{6,7},{7,4},{8,9},{9,10},{10,1... | collective-permute-start | bytes 196616 | tf_op jit(solution)/shard_map/ppermute | solution.py:53
  165.5 16.4 %copy-start.17 = (f32[1,2048]{1,0:T(1,128)S(1)}, f32[1,2048]{1,0:T(1,128)}, u32[]{:S(2)}) copy-start(f32[1,2048]{1,0:T(1,128)} %get-tuple-element.32) | copy-start | bytes 24580
  165.5 5.4 %collective-permute-start.15 = (bf16[128,512]{1,0:T(8,128)(2,1)S(1)}, bf16[128,512]{1,0:T(8,128)(2,1)S(1)}, u32[]{:S(2)}, u32[]{:S(2)}) collective-permute-start(bf16[128,512]{1,0:T(8,128)(2,1)S(1)} %fusion.3), channel_id=1, source_target_pairs={{0,4},{4,0},{1,5},{5,1},{2,6},{6,2},{3,7},{7,3},{8,12},{12,8},{9,1... | collective-permute-start | bytes 393224 | tf_op jit(solution)/shard_map/ppermute | solution.py:57
  182.0 10.3 %copy-start.15 = (s32[32,3]{0,1:T(4,128)S(1)}, s32[32,3]{0,1:T(4,128)}, u32[]{:S(2)}) copy-start(s32[32,3]{0,1:T(4,128)} %param.16) | copy-start | bytes 1156
  182.0 10.4 %copy-start.11 = (s32[32,3]{1,0:T(8,128)S(1)}, s32[32,3]{1,0:T(8,128)}, u32[]{:S(2)}) copy-start(s32[32,3]{1,0:T(8,128)} %copy-done.10) | copy-start | bytes 1156
  182.0 10.7 %copy-start.21 = (s32[1,16]{1,0:T(1,128)S(1)}, s32[1,16]{1,0:T(1,128)}, u32[]{:S(2)}) copy-start(s32[1,16]{1,0:T(1,128)} %param.29) | copy-start | bytes 196
  182.0 10.9 %copy-start.18 = (s32[1,1024]{1,0:T(1,128)S(1)}, s32[1,1024]{1,0:T(1,128)}, u32[]{:S(2)}) copy-start(s32[1,1024]{1,0:T(1,128)} %param.28) | copy-start | bytes 12292
  184.1 36.4 %all-to-all-start.4 = ((bf16[32,128,128]{2,1,0:T(8,128)(2,1)}), bf16[32,128,128]{2,1,0:T(8,128)(2,1)S(1)}, u32[]{:S(2)}, u32[]{:S(2)}) async-start(bf16[32,128,128]{2,1,0:T(8,128)(2,1)} %broadcast_in_dim.76), calls=%async_computation.4 | async-start | bytes 2097152 | tf_op jit(solution)/shard_map/all_to_all | solution.py:254
  220.4 1.0 copy-start.1

commit v2 on v1

v2 whole, which is shorter than its diff:
```python
import math

import jax
import jax.numpy as jnp
from jax import lax
from jax.experimental import pallas as pl
from jax.experimental.pallas import tpu as pltpu
from jax.sharding import Mesh, PartitionSpec as P

HD = 128
TOPK = 8
TOK = 128
CAP = 20
EXPERTS = 64
WIDE = 32
EPS = 1e-06
THETA = 50000.0
NEG = -1e30
W = ("z", "xl", "core")
N = ("xh", "y")
f32 = jnp.float32
bf16 = jnp.bfloat16


def y_shift(x, k):
    return lax.ppermute(x, "y", [(s, (s + k) % 4) for s in range(4)])


def x_swap(x):
    return lax.ppermute(x, "xh", [(0, 1), (1, 0)])


def attention_kernel(wide_ref, lengths_ref, x_ref, w_ref, qk_ref, out_w_ref, gain_ref, out_ref):
    wide = wide_ref[0]
    one, two = lengths_ref[wide, 0], lengths_ref[wide, 0] + lengths_ref[wide, 1]

    def member_of(places):
        return (places >= one).astype(jnp.int32) + (places >= two).astype(jnp.int32)

    down_places = lax.broadcasted_iota(jnp.int32, (TOK, HD), 0)
    across_places = lax.broadcasted_iota(jnp.int32, (TOK, HD), 1)
    member = member_of(down_places)
    same = member == member_of(across_places)
    start = jnp.where(member == 0, 0, jnp.where(member == 1, one, two))
    half = lax.rem(across_places, HD // 2).astype(f32)
    freq = jnp.exp(half * (-math.log(THETA) / (HD // 2)))
    angle = (down_places - start).astype(f32) * freq
    cosine = jnp.cos(angle)
    sine = jnp.sin(angle)
    sine = jnp.where(across_places < HD // 2, -sine, sine)

    x = x_ref[...].astype(f32)
    scale = lax.rsqrt(jnp.mean(x * x, axis=1, keepdims=True) + EPS)
    normed = (x * scale * gain_ref[...]).astype(bf16)
    query, keys, values = (
        jnp.dot(normed, w_ref[part], preferred_element_type=f32) for part in range(3)
    )

    def turned(v, gain):
        v = v * lax.rsqrt(jnp.mean(v * v, axis=1, keepdims=True) + EPS) * gain
        return (v * cosine + pltpu.roll(v, HD // 2, 1) * sine).astype(bf16)

    mixed = []
    for head in range(2):
        at = slice(head * HD, (head + 1) * HD)
        q = turned(query[:, at], qk_ref[0:1, at])
        k = turned(keys[:, at], qk_ref[1:2, at])
        scores = lax.dot_general(q, k, (((1,), (1,)), ((), ())), preferred_element_type=f32)
        scores = jnp.where(same, scores * HD ** (-0.5), NEG)
        weights = jnp.exp(scores - jnp.max(scores, axis=1, keepdims=True))
        probs = (weights / jnp.sum(weights, axis=1, keepdims=True)).astype(bf16)
        mixed.append(
            jnp.dot(probs, values[:, at].astype(bf16), preferred_element_type=f32).astype(bf16)
        )
    mixed = jnp.concatenate(mixed, axis=1)
    for part in range(4):
        out_ref[part] = jnp.dot(
            mixed, out_w_ref[:, part * 512 : (part + 1) * 512], preferred_element_type=f32
        ).astype(bf16)


def gate_up_kernel(at_ref, x0, x1, x2, x3, gate_ref, up_ref, gate_par, up_par, gain_ref, out_ref):
    i, j = at_ref[0], at_ref[1]
    xs = (x0, x1, x2, x3)
    total = jnp.zeros((x0.shape[0], 1), f32)
    for x in xs:
        v = x[...].astype(f32)
        total = total + jnp.sum(v * v, axis=1, keepdims=True)
    scale = lax.rsqrt(total / 2048.0 + EPS)
    own = jnp.zeros((x0.shape[0], 256), f32)
    par = jnp.zeros((x0.shape[0], 256), f32)
    for k, x in enumerate(xs):
        part = lax.rem(j - k + 4, 4)
        rows = pl.ds(pl.multiple_of(part * 512, 512), 512)
        normed = (x[...].astype(f32) * scale * gain_ref[part]).astype(bf16)
        w_own = jnp.concatenate([gate_ref[i, rows, :], up_ref[i, rows, :]], axis=1)
        w_par = jnp.concatenate([gate_par[rows, :], up_par[rows, :]], axis=1)
        own = own + jnp.dot(normed, w_own, preferred_element_type=f32)
        par = par + jnp.dot(normed, w_par, preferred_element_type=f32)
    for at, both in ((0, own), (128, par)):
        gate, up = both[:, :128], both[:, 128:]
        out_ref[:, at : at + 128] = (gate / (1.0 + jnp.exp(-gate)) * up).astype(bf16)


def down_kernel(at_ref, a0, a1, a2, a3, w0, w1, w2, w3, par_ref, out_ref):
    i = at_ref[0]
    total = jnp.zeros((a0.shape[0], 512), f32)
    for k, (a, w) in enumerate(((a0, w0), (a1, w1), (a2, w2), (a3, w3))):
        weight = jnp.concatenate([w[i], par_ref[k]], axis=0)
        total = total + jnp.dot(a[...], weight, preferred_element_type=f32)
    for s in range(WIDE):
        out_ref[s] = total[s * CAP : (s + 1) * CAP].astype(bf16)


def embed_kernel(hidden_ref, moe_ref, par_ref, gain_ref, w_ref, layer_ref, part_ref):
    layer = hidden_ref[...].astype(f32) + (moe_ref[...].astype(f32) + par_ref[...].astype(f32))
    layer = layer.astype(bf16)
    layer_ref[...] = layer
    layer = layer.astype(f32)
    scaled = (layer * gain_ref[...]).astype(bf16)
    part_ref[0:TOK, :] = jnp.dot(scaled, w_ref[...], preferred_element_type=f32)
    square = jnp.broadcast_to(jnp.sum(layer * layer, axis=1, keepdims=True), (TOK, TOK))
    part_ref[TOK:, :] = jnp.transpose(square)[0:8]


def vector_kernel(p0, p1, p2, p3, out_ref):
    whole = p0[...] + p1[...] + p2[...] + p3[...]
    square = jnp.transpose(jnp.broadcast_to(whole[TOK : TOK + 1], (TOK, TOK)))
    embedded = whole[0:TOK] * lax.rsqrt(square / 2048.0 + EPS)
    norm = jnp.sum(embedded * embedded, axis=1, keepdims=True)
    vectors = (embedded * lax.rsqrt(norm + EPS)).astype(bf16)
    for copy in range(16):
        out_ref[copy] = vectors


def assemble_kernel(at_ref, p0, p1, p2, p3, out_ref):
    j = at_ref[1]
    for k, piece in enumerate((p0, p1, p2, p3)):
        part = lax.rem(j - k + 4, 4)
        out_ref[:, pl.ds(pl.multiple_of(part * 512, 512), 512)] = piece[...]


def score_kernel(info_ref, own_ref, other_ref, doc_ref, out_ref):
    lane = lax.broadcasted_iota(jnp.int32, (1, 16), 1)
    scores = jnp.zeros((1, 16), f32)
    rows = lax.broadcasted_iota(jnp.int32, (144, 128), 0)
    columns = lax.broadcasted_iota(jnp.int32, (1, 128), 1)
    for d in range(16):
        first, size = info_ref[0, d], info_ref[1, d]
        q_first, q_size = info_ref[2, d], info_ref[3, d]
        at = pl.multiple_of(jnp.minimum((first // 16) * 16, 1024 - 144), 16)
        q_at = pl.multiple_of(jnp.minimum((q_first // 16) * 16, 2048 - 128), 16)
        query = jnp.where(
            info_ref[4, d] == 0, own_ref[pl.ds(q_at, 128), :], other_ref[pl.ds(q_at, 128), :]
        )
        sims = lax.dot_general(
            doc_ref[pl.ds(at, 144), :],
            query,
            (((1,), (1,)), ((), ())),
            preferred_element_type=f32,
        )
        keep = (rows >= first - at) & (rows < first - at + size)
        best = jnp.max(jnp.where(keep, sims, NEG), axis=0, keepdims=True)
        used = (columns >= q_first - q_at) & (columns < q_first - q_at + q_size)
        value = jnp.sum(jnp.where(used, best, 0.0), axis=1, keepdims=True) / q_size.astype(f32)
        scores = jnp.where(lane == d, value, scores)
    out_ref[...] = scores


def vmem():
    return pl.BlockSpec(memory_space=pltpu.VMEM)


def smem():
    return pl.BlockSpec(memory_space=pltpu.SMEM)


def body(
    tokens,
    request_lengths,
    w_qkv,
    qk_gain,
    w_out,
    norm_gains,
    w_router,
    routes,
    w_gate,
    w_up,
    w_down,
    w_proj,
    doc_vectors,
    doc_segment,
    doc_request,
):
    i = lax.axis_index("xh")
    j = lax.axis_index("y")
    core = lax.axis_index("core")
    wide = lax.axis_index(W)
    here = jnp.stack([i, j])

    def pick(array, which):
        return lax.dynamic_index_in_dim(array, which, 0, keepdims=False)

    def cut(array, part, axis):
        return lax.dynamic_slice_in_dim(array, lax.rem(part, 4) * 512, 512, axis)

    gate_par = x_swap(pick(w_gate, 1 - i))
    up_par = x_swap(pick(w_up, 1 - i))
    downs = [cut(w_down, j, 2)] + [y_shift(cut(w_down, j + k, 2), k) for k in (1, 2, 3)]
    down_par = x_swap(jnp.stack([pick(d, 1 - i) for d in downs]))

    experts_here = 2 * jnp.arange(WIDE, dtype=jnp.int32) + i
    hit = jnp.sum((routes.T[None, :, :] == experts_here[:, None, None]).astype(f32), axis=1)
    places = jnp.arange(TOK, dtype=jnp.int32)
    earlier = (places[:, None] < places[None, :]).astype(bf16)
    before = jnp.dot(hit.astype(bf16), earlier, preferred_element_type=f32)
    slot = jnp.arange(CAP, dtype=jnp.int32).astype(f32)
    chosen = (before[:, None, :] == slot[None, :, None]) & (hit[:, None, :] > 0)

    attn = pl.pallas_call(
        attention_kernel,
        out_shape=jax.ShapeDtypeStruct((4, TOK, 512), bf16),
        in_specs=[smem()] * 2 + [vmem()] * 5,
        out_specs=vmem(),
        compiler_params=pltpu.CompilerParams(vmem_limit_bytes=40 << 20),
        name="attention",
    )(
        wide.reshape(1),
        request_lengths,
        tokens,
        w_qkv.transpose(1, 0, 2),
        qk_gain,
        w_out,
        norm_gains[0:1],
    )
    attn = lax.all_to_all(attn, "y", 0, 0, tiled=True)
    attn = jnp.sum(attn.astype(f32), axis=0).astype(bf16)
    attn_par = x_swap(attn)
    mine = lax.dynamic_slice_in_dim(tokens, j * 512, 512, 1)
    hidden = (mine.astype(f32) + (attn.astype(f32) + attn_par.astype(f32))).astype(bf16)

    rows = lax.dot_general(
        chosen.astype(bf16), hidden, (((2,), (0,)), ((), ())), preferred_element_type=f32
    ).astype(bf16)
    rows = lax.all_to_all(rows, W, 0, 0, tiled=True).reshape(WIDE * CAP, 512)
    rows, gate_par, up_par = lax.optimization_barrier((rows, gate_par, up_par))
    gathered = [rows] + [y_shift(rows, k) for k in (1, 2, 3)]

    hf = hidden.astype(f32)
    gain_mine = lax.dynamic_slice_in_dim(norm_gains[1], j * 512, 512, 0)
    router_mine = lax.dynamic_slice_in_dim(w_router, j * 512, 512, 0)
    part = jnp.dot((hf * gain_mine).astype(bf16), router_mine, preferred_element_type=f32)
    square = jnp.sum(hf * hf, axis=1, keepdims=True)
    part = jnp.concatenate([part, jnp.broadcast_to(square, (TOK, EXPERTS))], axis=1)
    whole = part
    for k in (1, 2, 3):
        whole = whole + y_shift(part, k)
    logits = whole[:, :EXPERTS] * lax.rsqrt(whole[:, EXPERTS : EXPERTS + 1] / 2048.0 + EPS)
    lifted = jax.nn.sigmoid(logits)
    onehot = jnp.sum(
        (routes[:, :, None] == jnp.arange(EXPERTS, dtype=jnp.int32)[None, None, :]).astype(f32),
        axis=1,
    )
    lifted = lifted * onehot
    gates = lifted / jnp.sum(lifted, axis=1, keepdims=True)
    gates = lax.dynamic_index_in_dim(gates.reshape(TOK, WIDE, 2), i, 2, keepdims=False).T
    mixing = jnp.where(chosen, gates[:, None, :], 0.0)
    mixing_hi = lax.reduce_precision(mixing, 8, 7)
    mixing_lo = (mixing - mixing_hi).astype(bf16)
    mixing_hi = mixing_hi.astype(bf16)

    act = pl.pallas_call(
        gate_up_kernel,
        out_shape=jax.ShapeDtypeStruct((WIDE * CAP, 256), bf16),
        in_specs=[smem()] + [vmem()] * 9,
        out_specs=vmem(),
        compiler_params=pltpu.CompilerParams(vmem_limit_bytes=40 << 20),
        name="gate_up",
    )(here, *gathered, w_gate, w_up, gate_par, up_par, norm_gains[1].reshape(4, 1, 512))
    act, down_par = lax.optimization_barrier((act, down_par))
    acts = [act] + [y_shift(act, k) for k in (1, 2, 3)]
    out = pl.pallas_call(
        down_kernel,
        out_shape=jax.ShapeDtypeStruct((WIDE, CAP, 512), bf16),
        in_specs=[smem()] + [vmem()] * 9,
        out_specs=vmem(),
        compiler_params=pltpu.CompilerParams(vmem_limit_bytes=40 << 20),
        name="down",
    )(here, *acts, *downs, down_par)
    out = lax.all_to_all(out, W, 0, 0, tiled=True)

    contract = (((0, 1), (0, 1)), ((), ()))
    moe = lax.dot_general(mixing_hi, out, contract, preferred_element_type=f32)
    moe = moe + lax.dot_general(mixing_lo, out, contract, preferred_element_type=f32)
    moe = moe.astype(bf16)
    moe_par = x_swap(moe)
    layer, part = pl.pallas_call(
        embed_kernel,
        out_shape=(
            jax.ShapeDtypeStruct((TOK, 512), bf16),
            jax.ShapeDtypeStruct((TOK + 8, 128), f32),
        ),
        in_specs=[vmem()] * 5,
        out_specs=(vmem(), vmem()),
        name="embed",
    )(hidden, moe, moe_par, cut(norm_gains[2:3], j, 1), cut(w_proj, j, 0))
    parts = [part] + [y_shift(part, k) for k in (1, 2, 3)]
    layers = [layer] + [y_shift(layer, k) for k in (1, 2, 3)]

    vectors = pl.pallas_call(
        vector_kernel,
        out_shape=jax.ShapeDtypeStruct((16, TOK, 128), bf16),
        in_specs=[vmem()] * 4,
        out_specs=vmem(),
        name="vectors",
    )(*parts)
    own = lax.all_to_all(vectors, ("z", "xl"), 0, 0, tiled=True).reshape(16 * TOK, 128)
    other = lax.ppermute(own, "core", [(0, 1), (1, 0)])
    layer_out = pl.pallas_call(
        assemble_kernel,
        out_shape=jax.ShapeDtypeStruct((TOK, 2048), bf16),
        in_specs=[smem()] + [vmem()] * 4,
        out_specs=vmem(),
        name="assemble",
    )(here, *layers)
    segment = doc_segment[0]
    requests = doc_request[0]
    docs = jnp.arange(16, dtype=jnp.int32)
    first = jnp.sum((segment[None, :] < docs[:, None]).astype(jnp.int32), axis=1)
    size = jnp.sum((segment[None, :] == docs[:, None]).astype(jnp.int32), axis=1)
    starts = jnp.cumsum(request_lengths, axis=1) - request_lengths
    starts = (starts + TOK * (jnp.arange(WIDE, dtype=jnp.int32) // 2)[:, None]).reshape(-1)
    match = requests[:, None] == jnp.arange(96, dtype=jnp.int32)[None, :]
    q_first = jnp.sum(jnp.where(match, starts[None, :], 0), axis=1)
    q_size = jnp.sum(jnp.where(match, request_lengths.reshape(-1)[None, :], 0), axis=1)
    away = lax.rem(requests // 3, 2) ^ core
    info = jnp.stack([first, size, q_first, q_size, away])
    doc_scores = pl.pallas_call(
        score_kernel,
        out_shape=jax.ShapeDtypeStruct((1, 16), f32),
        in_specs=[smem(), vmem(), vmem(), vmem()],
        out_specs=vmem(),
        name="score",
    )(info, own, other, doc_vectors)
    return (layer_out, doc_scores)


def solution(mesh):
    split = Mesh(mesh.devices.reshape(8, 2, 2, 2, 4), ("z", "xl", "core", "xh", "y"))
    placed = (
        P(W, None),
        P(),
        P(None, None, N),
        P(None, N),
        P(N, None),
        P(),
        P(),
        P(W, None),
        P(W, None, N),
        P(W, None, N),
        P(W, N, None),
        P(),
        P(W + N, None),
        P(W + N, None),
        P(W + N, None),
    )
    return jax.shard_map(
        body,
        mesh=split,
        in_specs=placed,
        out_specs=(P(W, None), P(W + N, None)),
        check_vma=False,
    )
```

time: 225 us -> 235 us (1.044)
  local copies, waits for them, and re-layouts: 16.2 us -> 29.5 us
  starting transfers between devices: 55.7 us -> 67.4 us
  Pallas kernels: 7.24 us -> 18.7 us
  blocking collectives: 10.3 us -> 0 us
  waiting for transfers between devices: 119 us -> 110 us
  matrix products: 7.85 us -> 3.24 us
  other arithmetic: 6 us -> 3.44 us
    ppermute x12 -> x18, waiting for transfers between devices: 30.6 us -> 55.5 us  [y_shift(): return lax.ppermute(x, 'y', [(s, (s + k) % 4) for s in range(4)])]
    ppermute x4 -> x5, waiting for transfers between devices: 27.7 us -> 14.1 us  [x_swap(): return lax.ppermute(x, 'xh', [(0, 1), (1, 0)])]
    all_to_all x1, waiting for transfers between devices: 25.8 us -> 13.9 us  [body(): lax.all_to_all(vectors, ('z', 'xl'), 0, 0, tiled=True)]
    all_to_all x1 -> x0, blocking collectives: 10.3 us -> none  [body(): lax.all_to_all(jnp.broadcast_to(layer[None], (4, TOK, 512)), 'y', 0, 0, t...]
    pallas_call x0 -> x4, Pallas kernels: none -> 9.43 us  [the longest x1 3.56 us: body(): pl.pallas_call(attention_kernel, out_shape=jax.ShapeDtypeStruct((4, TOK,...]
    all_to_all x1, waiting for transfers between devices: 15.1 us -> 5.66 us  [body(): rows = lax.all_to_all(rows, W, 0, 0, tiled=True).reshape(WIDE * CAP, 512)]
    dynamic_slice x0 -> x7, local copies, waits for them, and re-layouts: none -> 8.04 us  [the longest x3 4.03 us: cut(): return lax.dynamic_slice_in_dim(array, lax.rem(part, 4) * 512, 512, axis)]
    unnamed x51 -> x79, local copies, waits for them, and re-layouts: 8.74 us -> 14.2 us
  transfers between devices with their start and end apart: 20 -> 28, of which waited for: 14 -> 23; matrix products, arithmetic and copies ran while one was open for 4% -> 7% of each run, Pallas kernels for 1% -> 3%
where the time goes in v2:
time: 235 us; the launch traced here: 233 us
  waiting for transfers between devices  110 us (47%)
  starting transfers between devices  67.4 us (29%)
  local copies, waits for them, and re-layouts  29.5 us (13%)
  Pallas kernels  18.7 us (8%)
  other arithmetic  3.44 us (1%)
  matrix products  3.24 us (1%)
    ppermute x18, waiting for transfers between devices, y_shift(): return lax.ppermute(x, 'y', [(s, (s + k) % 4) for s in range(4)])  55.5 us
    ppermute x18, starting transfers between devices, y_shift(): return lax.ppermute(x, 'y', [(s, (s + k) % 4) for s in range(4)])  18.5 us
    unnamed x79, local copies, waits for them, and re-layouts  14.2 us
    ppermute x5, waiting for transfers between devices, x_swap(): return lax.ppermute(x, 'xh', [(0, 1), (1, 0)])  14.1 us
    all_to_all x1, waiting for transfers between devices, body(): lax.all_to_all(vectors, ('z', 'xl'), 0, 0, tiled=True)  13.9 us
    all_to_all x1, waiting for transfers between devices, body(): out = lax.all_to_all(out, W, 0, 0, tiled=True)  13.7 us
    all_to_all x1, starting transfers between devices, body(): rows = lax.all_to_all(rows, W, 0, 0, tiled=True).reshape(WIDE * CAP, 512)  13.1 us
    ppermute x5, starting transfers between devices, x_swap(): return lax.ppermute(x, 'xh', [(0, 1), (1, 0)])  11.4 us
  transfers between devices with their start and end apart: 28, of which 23 were waited for; matrix products, arithmetic and copies ran while one was open for 7% of the time, Pallas kernels for 3%

profile of v2, /device:TPU:1, one launch (start us, length us, event | category | flops | bytes accessed | tf_op | source)
XLA Modules:
  0.0 233.3 jit_solution(3991854770346043987)
XLA Ops:
  1.5 1.5 fusion.43
  3.0 1.9 copy-done.1
  4.8 1.2 copy-done.4
  7.8 3.6 %attention.1 = bf16[4,128,512]{2,1,0:T(8,128)(2,1)} custom-call(s32[1]{0:T(128)} %bitcast.2.wide_ref, s32[32,3]{1,0:T(8,128)S(1)} %copy.38.lengths_ref, bf16[128,2048]{1,0:T(8,128)(2,1)S(1)} %copy-done.5, bf16[3,2048,256]{2,1,0:T(8,128)(2,1)S(1)} %bitcast.35, f32[2,256]{1,0:T(2,128)S(1)} %copy-done.15, bf16[256,2048]{1,0:T(8,128)(2,1)S(1)} %copy-done.4, ...), custom_call_target="tpu_custom_call" | custom-call | tf_op jit(solution)/shard_map/attention/pallas_call | solution.py:220
  11.4 5.1 %all-to-all-start = ((bf16[4,128,512]{2,1,0:T(8,128)(2,1)}), bf16[4,128,512]{2,1,0:T(8,128)(2,1)S(1)}, u32[]{:S(2)}, u32[]{:S(2)}) async-start(bf16[4,128,512]{2,1,0:T(8,128)(2,1)} %attention.1), calls=%async_computation | async-start | bytes 1048576 | tf_op jit(solution)/shard_map/all_to_all | solution.py:236
  16.8 7.3 %all-to-all-done = bf16[4,128,512]{2,1,0:T(8,128)(2,1)S(1)} async-done(((bf16[4,128,512]{2,1,0:T(8,128)(2,1)}), bf16[4,128,512]{2,1,0:T(8,128)(2,1)S(1)}, u32[]{:S(2)}, u32[]{:S(2)}) %all-to-all-start) | async-done | bytes 524320 | tf_op jit(solution)/shard_map/all_to_all | solution.py:236
  24.1 3.6 %collective-permute-start = (bf16[128,512]{1,0:T(8,128)(2,1)S(1)}, bf16[128,512]{1,0:T(8,128)(2,1)S(1)}, u32[]{:S(2)}, u32[]{:S(2)}) collective-permute-start(bf16[128,512]{1,0:T(8,128)(2,1)S(1)} %reduce_sum.84), channel_id=1, source_target_pairs={{0,4},{4,0},{1,5},{5,1},{2,6},{6,2},{3,7},{7,3},{8,12},{12,8},{9,1... | collective-permute-start | bytes 393224 | tf_op jit(solution)/shard_map/ppermute | solution.py:30
  27.7 2.3 collective-permute-done
  30.0 1.6 fusion.6
  32.6 1.3 copy.39
  33.9 13.1 %all-to-all-start.1 = ((bf16[32,20,512]{2,1,0:T(8,128)(2,1)}), bf16[32,20,512]{2,1,0:T(8,128)(2,1)}, u32[]{:S(2)}, u32[]{:S(2)}) async-start(bf16[32,20,512]{2,1,0:T(8,128)(2,1)} %copy.39), calls=%async_computation.1 | async-start | bytes 1572864 | tf_op jit(solution)/shard_map/all_to_all | solution.py:245
  47.9 2.5 %collective-permute-start.4 = (bf16[2048,128]{1,0:T(8,128)(2,1)}, bf16[2048,128]{1,0:T(8,128)(2,1)}, u32[]{:S(2)}, u32[]{:S(2)}) collective-permute-start(bf16[2048,128]{1,0:T(8,128)(2,1)} %dynamic-slice_bitcast_fusion.1), channel_id=1, source_target_pairs={{0,4},{4,0},{1,5},{5,1},{2,6},{6,2},{3,7},{7,3},{8,12},{12,8},{9,1... | collective-permute-start | bytes 1572872 | tf_op jit(solution)/shard_map/ppermute | solution.py:30
  51.8 2.1 constant_dynamic-slice_fusion.2
  55.9 1.7 constant_dynamic-slice_fusion.9
  57.6 3.5 %collective-permute-done.11.w3 = bf16[2,128,512]{2,1,0:T(8,128)(2,1)S(1)} collective-permute-done((bf16[2,128,512]{2,1,0:T(8,128)(2,1)}, bf16[2,128,512]{2,1,0:T(8,128)(2,1)S(1)}, u32[]{:S(2)}, u32[]{:S(2)}) %collective-permute-start.11) | collective-permute-done | bytes 262176 | tf_op jit(solution)/shard_map/ppermute | solution.py:26
  61.8 1.4 collective-permute-done.10.w2
  64.0 5.7 %all-to-all-done.1 = bf16[32,20,512]{2,1,0:T(8,128)(2,1)} async-done(((bf16[32,20,512]{2,1,0:T(8,128)(2,1)}), bf16[32,20,512]{2,1,0:T(8,128)(2,1)}, u32[]{:S(2)}, u32[]{:S(2)}) %all-to-all-start.1) | async-done | bytes 655392 | tf_op jit(solution)/shard_map/all_to_all | solution.py:245
  69.7 1.2 reshape.57.x0
  70.9 10.3 %collective-permute-done.5.up_par = bf16[2048,128]{1,0:T(8,128)(2,1)} collective-permute-done((bf16[2048,128]{1,0:T(8,128)(2,1)}, bf16[2048,128]{1,0:T(8,128)(2,1)}, u32[]{:S(2)}, u32[]{:S(2)}) %collective-permute-start.5) | collective-permute-done | bytes 524320 | tf_op jit(solution)/shard_map/ppermute | solution.py:30
  81.5 1.8 collective-permute-start.7
  86.0 2.8 %collective-permute-start.12 = (bf16[4,128,512]{2,1,0:T(8,128)(2,1)S(1)}, bf16[4,128,512]{2,1,0:T(8,128)(2,1)S(1)}, u32[]{:S(2)}, u32[]{:S(2)}) collective-permute-start(bf16[4,128,512]{2,1,0:T(8,128)(2,1)S(1)} %pad_maximum_fusion), channel_id=1, source_target_pairs={{0,4},{4,0},{1,5},{5,1},{2,6},{6,2},{3,7},{7,3},{8,12},{12,8},{9,1... | collective-permute-start | bytes 1572872 | tf_op jit(solution)/shard_map/ppermute | solution.py:30
  88.8 9.4 %collective-permute-done.6.x1 = bf16[640,512]{1,0:T(8,128)(2,1)S(1)} collective-permute-done((bf16[640,512]{1,0:T(8,128)(2,1)S(1)}, bf16[640,512]{1,0:T(8,128)(2,1)S(1)}, u32[]{:S(2)}, u32[]{:S(2)}) %collective-permute-start.6) | collective-permute-done | bytes 655392 | tf_op jit(solution)/shard_map/ppermute | solution.py:26
  98.2 12.9 %collective-permute-done.7.x2 = bf16[640,512]{1,0:T(8,128)(2,1)S(1)} collective-permute-done((bf16[640,512]{1,0:T(8,128)(2,1)S(1)}, bf16[640,512]{1,0:T(8,128)(2,1)S(1)}, u32[]{:S(2)}, u32[]{:S(2)}) %collective-permute-start.7) | collective-permute-done | bytes 655392 | tf_op jit(solution)/shard_map/ppermute | solution.py:26
  112.8 3.9 %gate_up.1.a0 = bf16[640,256]{1,0:T(8,128)(2,1)} custom-call(s32[2]{0:T(128)S(1)} %pad_add_fusion.at_ref, bf16[640,512]{1,0:T(8,128)(2,1)S(1)} %reshape.57.x0, bf16[640,512]{1,0:T(8,128)(2,1)S(1)} %collective-permute-done.6.x1, bf16[640,512]{1,0:T(8,128)(2,1)S(1)} %collective-permute-done.7.x2, bf16[640,512]{1,0:T(8,128)(2,1)S(1)} %collective-permute-done.8.x3, ...), custom_call_target="tpu_custom_call" | custom-call | tf_op jit(solution)/shard_map/gate_up/pallas_call | solution.py:272
  117.5 1.7 collective-permute-start.13
  119.2 2.9 %collective-permute-start.14 = (bf16[640,256]{1,0:T(8,128)(2,1)}, bf16[640,256]{1,0:T(8,128)(2,1)S(1)}, u32[]{:S(2)}, u32[]{:S(2)}) collective-permute-start(bf16[640,256]{1,0:T(8,128)(2,1)} %gate_up.1.a0), channel_id=1, source_target_pairs={{0,2},{1,3},{2,0},{3,1},{4,6},{5,7},{6,4},{7,5},{8,10},{9,11},{10,... | collective-permute-start | bytes 983048 | tf_op jit(solution)/shard_map/ppermute | solution.py:26
  122.8 4.6 %collective-permute-done.13.a1 = bf16[640,256]{1,0:T(8,128)(2,1)S(1)} collective-permute-done((bf16[640,256]{1,0:T(8,128)(2,1)}, bf16[640,256]{1,0:T(8,128)(2,1)S(1)}, u32[]{:S(2)}, u32[]{:S(2)}) %collective-permute-start.13) | collective-permute-done | bytes 327712 | tf_op jit(solution)/shard_map/ppermute | solution.py:26
  127.4 8.8 %collective-permute-done.14.a2 = bf16[640,256]{1,0:T(8,128)(2,1)S(1)} collective-permute-done((bf16[640,256]{1,0:T(8,128)(2,1)}, bf16[640,256]{1,0:T(8,128)(2,1)S(1)}, u32[]{:S(2)}, u32[]{:S(2)}) %collective-permute-start.14) | collective-permute-done | bytes 327712 | tf_op jit(solution)/shard_map/ppermute | solution.py:26
  139.9 2.8 %down.1 = bf16[32,20,512]{2,1,0:T(8,128)(2,1)} custom-call(s32[2]{0:T(128)S(1)} %copy-done.14, bf16[640,256]{1,0:T(8,128)(2,1)} %gate_up.1.a0, bf16[640,256]{1,0:T(8,128)(2,1)S(1)} %collective-permute-done.13.a1, bf16[640,256]{1,0:T(8,128)(2,1)S(1)} %collective-permute-done.14.a2, bf16[640,256]{1,0:T(8,128)(2,1)S(1)} %collective-permute-done.15.a3, ...), custom_call_target="tpu_custom_call" | custom-call | tf_op jit(solution)/shard_map/down/pallas_call | solution.py:282
  142.7 9.7 %all-to-all-start.2 = ((bf16[32,20,512]{2,1,0:T(8,128)(2,1)}), bf16[32,20,512]{2,1,0:T(8,128)(2,1)S(1)}, u32[]{:S(2)}, u32[]{:S(2)}) async-start(bf16[32,20,512]{2,1,0:T(8,128)(2,1)} %down.1), calls=%async_computation.2 | async-start | bytes 1572864 | tf_op jit(solution)/shard_map/all_to_all | solution.py:290
  153.5 1.9 collective-permute-start.3
  157.1 3.2 %collective-permute-done.2 = f32[128,128]{0,1:T(8,128)S(1)} collective-permute-done((f32[128,128]{0,1:T(8,128)S(1)}, f32[128,128]{0,1:T(8,128)S(1)}, u32[]{:S(2)}, u32[]{:S(2)}) %collective-permute-start.2) | collective-permute-done | bytes 65568 | tf_op jit(solution)/shard_map/ppermute | solution.py:26
  161.3 13.7 %all-to-all-done.2 = bf16[32,20,512]{2,1,0:T(8,128)(2,1)S(1)} async-done(((bf16[32,20,512]{2,1,0:T(8,128)(2,1)}), bf16[32,20,512]{2,1,0:T(8,128)(2,1)S(1)}, u32[]{:S(2)}, u32[]{:S(2)}) %all-to-all-start.2) | async-done | bytes 655392 | tf_op jit(solution)/shard_map/all_to_all | solution.py:290
  176.7 2.0 collective-permute-start.16
  178.7 1.3 constant_dynamic-slice_fusion.1.gain_ref
  180.6 1.4 collective-permute-done.16.par_ref
  182.7 1.9 embed.1
  184.7 2.9 %collective-permute-start.21 = (f32[136,128]{1,0:T(8,128)}, f32[136,128]{1,0:T(8,128)S(1)}, u32[]{:S(2)}, u32[]{:S(2)}) collective-permute-start(f32[136,128]{1,0:T(8,128)} %get-tuple-element.15.p0), channel_id=1, source_target_pairs={{0,2},{1,3},{2,0},{3,1},{4,6},{5,7},{6,4},{7,5},{8,10},{9,11},{10,... | collective-permute-start | bytes 208904 | tf_op jit(solution)/shard_map/ppermute | solution.py:26
  187.6 1.6 collective-permute-done.20.p1
  191.6 2.0 vectors.1
  193.6 5.1 %all-to-all-start.3 = ((bf16[16,128,128]{2,1,0:T(8,128)(2,1)}), bf16[16,128,128]{2,1,0:T(8,128)(2,1)S(1)}, u32[]{:S(2)}, u32[]{:S(2)}) async-start(bf16[16,128,128]{2,1,0:T(8,128)(2,1)} %vectors.1), calls=%async_computation.3 | async-start | bytes 1048576 | tf_op jit(solution)/shard_map/all_to_all | solution.py:317
  198.8 13.9 %all-to-all-done.3 = bf16[16,128,128]{2,1,0:T(8,128)(2,1)S(1)} async-done(((bf16[16,128,128]{2,1,0:T(8,128)(2,1)}), bf16[16,128,128]{2,1,0:T(8,128)(2,1)S(1)}, u32[]{:S(2)}, u32[]{:S(2)}) %all-to-all-start.3) | async-done | bytes 524320 | tf_op jit(solution)/shard_map/all_to_all | solution.py:317
  212.8 4.4 %collective-permute-start.23 = (bf16[2048,128]{1,0:T(8,128)(2,1)S(1)}, bf16[2048,128]{1,0:T(8,128)(2,1)S(1)}, u32[]{:S(2)}, u32[]{:S(2)}) collective-permute-start(bf16[2048,128]{1,0:T(8,128)(2,1)S(1)} %bitcast.37), channel_id=1, source_target_pairs={{0,8},{8,0},{1,9},{9,1},{2,10},{10,2},{3,11},{11,3},{4,12},{12,4},... | collective-permute-start | bytes 1572872 | tf_op jit(solution)/shard_map/ppermute | solution.py:318
  218.1 2.0 collective-permute-start.18
  222.1 2.7 %collective-permute-done.17.p1 = bf16[128,512]{1,0:T(8,128)(2,1)S(1)} collective-permute-done((bf16[128,512]{1,0:T(8,128)(2,1)}, bf16[128,512]{1,0:T(8,128)(2,1)S(1)}, u32[]{:S(2)}, u32[]{:S(2)}) %collective-permute-start.17) | collective-permute-done | bytes 131104 | tf_op jit(solution)/shard_map/ppermute | solution.py:26
  224.7 2.1 collective-permute-done.18.p2
  228.1 1.9 assemble.1
  230.9 2.5 %score.1 = f32[1,16]{1,0:T(1,128)} custom-call(s32[5,16]{1,0:T(8,128)} %stack.40.info_ref, bf16[2048,128]{1,0:T(8,128)(2,1)} %bitcast.38, bf16[2048,128]{1,0:T(8,128)(2,1)} %copy-done.18, bf16[1024,128]{1,0:T(8,128)(2,1)} %doc_ref.1), custom_call_target="tpu_custom_call" | custom-call | tf_op jit(solution)/shard_map/score/pallas_call | solution.py:338
  (138 shorter events, 33.7 us)
Async XLA Ops:
  0.6 179.3 %copy-start = (bf16[2048,128]{1,0:T(8,128)(2,1)S(1)}, bf16[2048,128]{1,0:T(8,128)(2,1)}, u32[]{:S(2)}) copy-start(bf16[2048,128]{1,0:T(8,128)(2,1)} %param.26) | copy-start | bytes 1572868
  7.8 8.7 %copy-start.32 = (s32[128,8]{0,1:T(8,128)S(1)}, s32[128,8]{0,1:T(8,128)}, u32[]{:S(2)}) copy-start(s32[128,8]{0,1:T(8,128)} %param.22) | copy-start | bytes 12292
  11.4 35.7 %copy-start.2 = (bf16[2,2048,128]{2,1,0:T(8,128)(2,1)S(1)}, bf16[2,2048,128]{2,1,0:T(8,128)(2,1)}, u32[]{:S(2)}) copy-start(bf16[2,2048,128]{2,1,0:T(8,128)(2,1)} %gate_ref.1) | copy-start | bytes 3145732
  11.4 12.7 %all-to-all-start = ((bf16[4,128,512]{2,1,0:T(8,128)(2,1)}), bf16[4,128,512]{2,1,0:T(8,128)(2,1)S(1)}, u32[]{:S(2)}, u32[]{:S(2)}) async-start(bf16[4,128,512]{2,1,0:T(8,128)(2,1)} %attention.1), calls=%async_computation | async-start | bytes 1048576 | tf_op jit(solution)/shard_map/all_to_all | solution.py:236
  16.5 33.8 %copy-start.3 = (bf16[2,2048,128]{2,1,0:T(8,128)(2,1)S(1)}, bf16[2,2048,128]{2,1,0:T(8,128)(2,1)}, u32[]{:S(2)}) copy-start(bf16[2,2048,128]{2,1,0:T(8,128)(2,1)} %up_ref.1) | copy-start | bytes 3145732
  16.8 34.4 %copy-start.27 = (f32[32,128]{1,0:T(8,128)}, f32[32,128]{1,0:T(8,128)S(1)}, u32[]{:S(2)}) copy-start(f32[32,128]{1,0:T(8,128)S(1)} %fusion.26) | copy-start | bytes 49156
  24.1 5.9 %collective-permute-start = (bf16[128,512]{1,0:T(8,128)(2,1)S(1)}, bf16[128,512]{1,0:T(8,128)(2,1)S(1)}, u32[]{:S(2)}, u32[]{:S(2)}) collective-permute-start(bf16[128,512]{1,0:T(8,128)(2,1)S(1)} %reduce_sum.84), channel_id=1, source_target_pairs={{0,4},{4,0},{1,5},{5,1},{2,6},{6,2},{3,7},{7,3},{8,12},{12,8},{9,1... | collective-permute-start | bytes 393224 | tf_op jit(solution)/shard_map/ppermute | solution.py:30
  27.7 23.5 %copy-start.30 = (pred[32,128]{1,0:T(8,128)(4,1)}, pred[32,128]{1,0:T(8,128)(4,1)S(1)}, u32[]{:S(2)}) copy-start(pred[32,128]{1,0:T(8,128)(4,1)S(1)} %broadcast_compare_fusion) | copy-start | bytes 12292
  27.7 23.5 %copy-start.37 = (f32[20]{0:T(128)}, f32[20]{0:T(128)S(1)}, u32[]{:S(2)}) copy-start(f32[20]{0:T(128)S(1)} %iota_convert_fusion) | copy-start | bytes 244
  33.9 35.8 %all-to-all-start.1 = ((bf16[32,20,512]{2,1,0:T(8,128)(2,1)}), bf16[32,20,512]{2,1,0:T(8,128)(2,1)}, u32[]{:S(2)}, u32[]{:S(2)}) async-start(bf16[32,20,512]{2,1,0:T(8,128)(2,1)} %copy.39), calls=%async_computation.1 | async-start | bytes 1572864 | tf_op jit(solution)/shard_map/all_to_all | solution.py:245
  47.9 23.1 %collective-permute-start.4 = (bf16[2048,128]{1,0:T(8,128)(2,1)}, bf16[2048,128]{1,0:T(8,128)(2,1)}, u32[]{:S(2)}, u32[]{:S(2)}) collective-permute-start(bf16[2048,128]{1,0:T(8,128)(2,1)} %dynamic-slice_bitcast_fusion.1), channel_id=1, source_target_pairs={{0,4},{4,0},{1,5},{5,1},{2,6},{6,2},{3,7},{7,3},{8,12},{12,8},{9,1... | collective-permute-start | bytes 1572872 | tf_op jit(solution)/shard_map/ppermute | solution.py:30
  51.2 30.1 %collective-permute-start.5 = (bf16[2048,128]{1,0:T(8,128)(2,1)}, bf16[2048,128]{1,0:T(8,128)(2,1)}, u32[]{:S(2)}, u32[]{:S(2)}) collective-permute-start(bf16[2048,128]{1,0:T(8,128)(2,1)} %dynamic-slice_bitcast_fusion), channel_id=1, source_target_pairs={{0,4},{4,0},{1,5},{5,1},{2,6},{6,2},{3,7},{7,3},{8,12},{12,8},{9,1... | collective-permute-start | bytes 1572872 | tf_op jit(solution)/shard_map/ppermute | solution.py:30
  53.9 7.3 %collective-permute-start.11 = (bf16[2,128,512]{2,1,0:T(8,128)(2,1)}, bf16[2,128,512]{2,1,0:T(8,128)(2,1)S(1)}, u32[]{:S(2)}, u32[]{:S(2)}) collective-permute-start(bf16[2,128,512]{2,1,0:T(8,128)(2,1)} %get-tuple-element.25), channel_id=1, source_target_pairs={{0,3},{1,0},{2,1},{3,2},{4,7},{5,4},{6,5},{7,6},{8,11},{9,8},{10,9... | collective-permute-start | bytes 786440 | tf_op jit(solution)/shard_map/ppermute | solution.py:26
  54.8 8.5 %collective-permute-start.10 = (bf16[2,128,512]{2,1,0:T(8,128)(2,1)}, bf16[2,128,512]{2,1,0:T(8,128)(2,1)S(1)}, u32[]{:S(2)}, u32[]{:S(2)}) collective-permute-start(bf16[2,128,512]{2,1,0:T(8,128)(2,1)} %get-tuple-element.23), channel_id=1, source_target_pairs={{0,2},{1,3},{2,0},{3,1},{4,6},{5,7},{6,4},{7,5},{8,10},{9,11},{10,... | collective-permute-start | bytes 786440 | tf_op jit(solution)/shard_map/ppermute | solution.py:26
  55.9 28.0 %collective-permute-start.9 = (bf16[2,128,512]{2,1,0:T(8,128)(2,1)}, bf16[2,128,512]{2,1,0:T(8,128)(2,1)}, u32[]{:S(2)}, u32[]{:S(2)}) collective-permute-start(bf16[2,128,512]{2,1,0:T(8,128)(2,1)} %get-tuple-element.24), channel_id=1, source_target_pairs={{0,1},{1,2},{2,3},{3,0},{4,5},{5,6},{6,7},{7,4},{8,9},{9,10},{10,1... | collective-permute-start | bytes 786440 | tf_op jit(solution)/shard_map/ppermute | solution.py:26
  61.1 2.9 %copy-start.6 = (bf16[2,128,512]{2,1,0:T(8,128)(2,1)}, bf16[2,128,512]{2,1,0:T(8,128)(2,1)S(1)}, u32[]{:S(2)}) copy-start(bf16[2,128,512]{2,1,0:T(8,128)(2,1)S(1)} %collective-permute-done.11.w3) | copy-start | bytes 786436
  81.3 16.9 %collective-permute-start.6 = (bf16[640,512]{1,0:T(8,128)(2,1)S(1)}, bf16[640,512]{1,0:T(8,128)(2,1)S(1)}, u32[]{:S(2)}, u32[]{:S(2)}) collective-permute-start(bf16[640,512]{1,0:T(8,128)(2,1)S(1)} %reshape.57.x0), channel_id=1, source_target_pairs={{0,1},{1,2},{2,3},{3,0},{4,5},{5,6},{6,7},{7,4},{8,9},{9,10},{10,1... | collective-permute-start | bytes 1966088 | tf_op jit(solution)/shard_map/ppermute | solution.py:26
  81.5 29.5 %collective-permute-start.7 = (bf16[640,512]{1,0:T(8,128)(2,1)S(1)}, bf16[640,512]{1,0:T(8,128)(2,1)S(1)}, u32[]{:S(2)}, u32[]{:S(2)}) collective-permute-start(bf16[640,512]{1,0:T(8,128)(2,1)S(1)} %reshape.57.x0), channel_id=1, source_target_pairs={{0,2},{1,3},{2,0},{3,1},{4,6},{5,7},{6,4},{7,5},{8,10},{9,11},{10,... | collective-permute-start | bytes 1966088 | tf_op jit(solution)/shard_map/ppermute | solution.py:26
  83.3 28.8 %collective-permute-start.8 = (bf16[640,512]{1,0:T(8,128)(2,1)S(1)}, bf16[640,512]{1,0:T(8,128)(2,1)S(1)}, u32[]{:S(2)}, u32[]{:S(2)}) collective-permute-start(bf16[640,512]{1,0:T(8,128)(2,1)S(1)} %reshape.57.x0), channel_id=1, source_target_pairs={{0,3},{1,0},{2,1},{3,2},{4,7},{5,4},{6,5},{7,6},{8,11},{9,8},{10,9... | collective-permute-start | bytes 1966088 | tf_op jit(solution)/shard_map/ppermute | solution.py:26
  86.0 30.8 %collective-permute-start.12 = (bf16[4,128,512]{2,1,0:T(8,128)(2,1)S(1)}, bf16[4,128,512]{2,1,0:T(8,128)(2,1)S(1)}, u32[]{:S(2)}, u32[]{:S(2)}) collective-permute-start(bf16[4,128,512]{2,1,0:T(8,128)(2,1)S(1)} %pad_maximum_fusion), channel_id=1, source_target_pairs={{0,4},{4,0},{1,5},{5,1},{2,6},{6,2},{3,7},{7,3},{8,12},{12,8},{9,1... | collective-permute-start | bytes 1572872 | tf_op jit(solution)/shard_map/ppermute | solution.py:30
  88.8 30.4 %copy-start.13 = (s32[2]{0:T(128)}, s32[2]{0:T(128)S(1)}, u32[]{:S(2)}) copy-start(s32[2]{0:T(128)S(1)} %pad_add_fusion.at_ref) | copy-start | bytes 28
  116.7 36.8 %copy-start.35 = (f32[128]{0:T(128)S(1)}, f32[128]{0:T(128)}, u32[]{:S(2)}) copy-start(f32[128]{0:T(128)} %get-tuple-element.20) | copy-start | bytes 1540
  116.7 39.4 %copy-start.33 = (s32[128,8]{0,1:T(8,128)S(1)}, s32[128,8]{0,1:T(8,128)}, u32[]{:S(2)}) copy-start(s32[128,8]{0,1:T(8,128)} %param.22) | copy-start | bytes 12292
  116.7 58.3 %copy-start.31 = (pred[32,128]{1,0:T(8,128)(4,1)S(1)}, pred[32,128]{1,0:T(8,128)(4,1)}, u32[]{:S(2)}) copy-start(pred[32,128]{1,0:T(8,128)(4,1)} %copy-done.30) | copy-start | bytes 12292
  116.7 58.3 %copy-start.38 = (f32[20]{0:T(128)S(1)}, f32[20]{0:T(128)}, u32[]{:S(2)}) copy-start(f32[20]{0:T(128)} %copy-done.37) | copy-start | bytes 244
  117.5 9.9 %collective-permute-start.13 = (bf16[640,256]{1,0:T(8,128)(2,1)}, bf16[640,256]{1,0:T(8,128)(2,1)S(1)}, u32[]{:S(2)}, u32[]{:S(2)}) collective-permute-start(bf16[640,256]{1,0:T(8,128)(2,1)} %gate_up.1.a0), channel_id=1, source_target_pairs={{0,1},{1,2},{2,3},{3,0},{4,5},{5,6},{6,7},{7,4},{8,9},{9,10},{10,1... | collective-permute-start | bytes 983048 | tf_op jit(solution)/shard_map/ppermute | solution.py:26
  119.2 17.1 %collective-permute-start.14 = (bf16[640,256]{1,0:T(8,128)(2,1)}, bf16[640,256]{1,0:T(8,128)(2,1)S(1)}, u32[]{:S(2)}, u32[]{:S(2)}) collective-permute-start(bf16[640,256]{1,0:T(8,128)(2,1)} %gate_up.1.a0), channel_id=1, source_target_pairs={{0,2},{1,3},{2,0},{3,1},{4,6},{5,7},{6,4},{7,5},{8,10},{9,11},{10,... | collective-permute-start | bytes 983048 | tf_op jit(solution)/shard_map/ppermute | solution.py:26
  122.1 14.1 %collective-permute-start.15 = (bf16[640,256]{1,0:T(8,128)(2,1)}, bf16[640,256]{1,0:T(8,128)(2,1)S(1)}, u32[]{:S(2)}, u32[]{:S(2)}) collective-permute-start(bf16[640,256]{1,0:T(8,128)(2,1)} %gate_up.1.a0), channel_id=1, source_target_pairs={{0,3},{1,0},{2,1},{3,2},{4,7},{5,4},{6,5},{7,6},{8,11},{9,8},{10,9... | collective-permute-start | bytes 983048 | tf_op jit(solution)/shard_map/ppermute | solution.py:26
  139.9 36.3 %copy-start.28 = (f32[32,128]{1,0:T(8,128)S(1)}, f32[32,128]{1,0:T(8,128)}, u32[]{:S(2)}) copy-start(f32[32,128]{1,0:T(8,128)} %copy-done.27) | copy-start | bytes 49156
  142.7 32.3 %all-to-all-start.2 = ((bf16[32,20,512]{2,1,0:T(8,128)(2,1)}), bf16[32,20,512]{2,1,0:T(8,128)(2,1)S(1)}, u32[]{:S(2)}, u32[]{:S(2)}) async-start(bf16[32,20,512]{2,1,0:T(8,128)(2,1)} %down.1), calls=%async_computation.2 | async-start | bytes 1572864 | tf_op jit(solution)/shard_map/all_to_all | solution.py:290
  152.4 46.4 %copy-start.29 = (s32[32,3]{0,1:T(4,128)S(1)}, s32[32,3]{0,1:T(4,128)}, u32[]{:S(2)}) copy-start(s32[32,3]{0,1:T(4,128)} %param.16) | copy-start | bytes 1156
  152.4 65.1 %copy-start.36 = (s32[1,16]{1,0:T(1,128)S(1)}, s32[1,16]{1,0:T(1,128)}, u32[]{:S(2)}) copy-start(s32[1,16]{1,0:T(1,128)} %param.29) | copy-start | bytes 196
  152.4 68.9 %copy-start.34 = (s32[1,1024]{1,0:T(1,128)S(1)}, s32[1,1024]{1,0:T(1,128)}, u32[]{:S(2)}) copy-start(s32[1,1024]{1,0:T(1,128)} %param.28) | copy-start | bytes 12292
  153.5 3.5 %collective-permute-start.3 = (f32[128,128]{0,1:T(8,128)S(1)}, f32[128,128]{0,1:T(8,128)S(1)}, u32[]{:S(2)}, u32[]{:S(2)}) collective-permute-start(f32[128,128]{0,1:T(8,128)S(1)} %pad_maximum_fusion.1), channel_id=1, source_target_pairs={{0,3},{1,0},{2,1},{3,2},{4,7},{5,4},{6,5},{7,6},{8,11},{9,8},{10,9... | collective-permute-start | bytes 196616 | tf_op jit(solution)/shard_map/ppermute | solution.py:26
  155.4 4.9 %collective-permute-start.2 = (f32[128,128]{0,1:T(8,128)S(1)}, f32[128,128]{0,1:T(8,128)S(1)}, u32[]{:S(2)}, u32[]{:S(2)}) collective-permute-start(f32[128,128]{0,1:T(8,128)S(1)} %pad_maximum_fusion.1), channel_id=1, source_target_pairs={{0,2},{1,3},{2,0},{3,1},{4,6},{5,7},{6,4},{7,5},{8,10},{9,11},{10,... | collective-permute-start | bytes 196616 | tf_op jit(solution)/shard_map/ppermute | solution.py:26
  155.4 5.7 %collective-permute-start.1 = (f32[128,128]{0,1:T(8,128)S(1)}, f32[128,128]{0,1:T(8,128)S(1)}, u32[]{:S(2)}, u32[]{:S(2)}) collective-permute-start(f32[128,128]{0,1:T(8,128)S(1)} %pad_maximum_fusion.1), channel_id=1, source_target_pairs={{0,1},{1,2},{2,3},{3,0},{4,5},{5,6},{6,7},{7,4},{8,9},{9,10},{10,1... | collective-permute-start | bytes 196616 | tf_op jit(solution)/shard_map/ppermute | solution.py:26
  176.7 5.4 %copy-start.19 = (bf16[128,512]{1,0:T(8,128)(2,1)}, bf16[128,512]{1,0:T(8,128)(2,1)S(1)}, u32[]{:S(2)}) copy-start(bf16[128,512]{1,0:T(8,128)(2,1)S(1)} %fusion.1.moe_ref) | copy-start | bytes 393220
  176.7 5.4 %collective-permute-start.16 = (bf16[128,512]{1,0:T(8,128)(2,1)S(1)}, bf16[128,512]{1,0:T(8,128)(2,1)S(1)}, u32[]{:S(2)}, u32[]{:S(2)}) collective-permute-start(bf16[128,512]{1,0:T(8,128)(2,1)S(1)} %fusion.1.moe_ref), channel_id=1, source_target_pairs={{0,4},{4,0},{1,5},{5,1},{2,6},{6,2},{3,7},{7,3},{8,12},{12,8},{9,1... | collective-permute-start | bytes 393224 | tf_op jit(solution)/shard_map/ppermute | solution.py:30
  184.7 4.6 %collective-permute-start.20 = (f32[136,128]{1,0:T(8,128)}, f32[136,128]{1,0:T(8,128)S(1)}, u32[]{:S(2)}, u32[]{:S(2)}) collective-permute-start(f32[136,128]{1,0:T(8,128)} %get-tuple-element.15.p0), channel_id=1, source_target_pairs={{0,1},{1,2},{2,3},{3,0},{4,5},{5,6},{6,7},{7,4},{8,9},{9,10},{10,1... | collective-permute-start | bytes 208904 | tf_op jit(solution)/shard_map/ppermute | solution.py:26
  184.7 5.6 %collective-permute-start.21 = (f32[136,128]{1,0:T(8,128)}, f32[136,128]{1,0:T(8,128)S(1)}, u32[]{:S(2)}, u32[]{:S(2)}) collective-permute-start(f32[136,128]{1,0:T(8,128)} %get-tuple-element.15.p0), channel_id=1, source_target_pairs={{0,2},{1,3},{2,0},{3,1},{4,6},{5,7},{6,4},{7,5},{8,10},{9,11},{10,... | collective-permute-start | bytes 208904 | tf_op jit(solution)/shard_map/ppermute | solution.py:26
  187.6 3.4 %collective-permute-start.22 = (f32[136,128]{1,0:T(8,128)}, f32[136,128]{1,0:T(8,128)S(1)}, u32[]{:S(2)}, u32[]{:S(2)}) collective-permute-start(f32[136,128]{1,0:T(8,128)} %get-tuple-element.15.p0), channel_id=1, source_target_pairs={{0,3},{1,0},{2,1},{3,2},{4,7},{5,4},{6,5},{7,6},{8,11},{9,8},{10,9... | collective-permute-start | bytes 208904 | tf_op jit(solution)/shard_map/ppermute | solution.py:26
  193.6 19.1 %all-to-all-start.3 = ((bf16[16,128,128]{2,1,0:T(8,128)(2,1)}), bf16[16,128,128]{2,1,0:T(8,128)(2,1)S(1)}, u32[]{:S(2)}, u32[]{:S(2)}) async-start(bf16[16,128,128]{2,1,0:T(8,128)(2,1)} %vectors.1), calls=%async_computation.3 | async-start | bytes 1048576 | tf_op jit(solution)/shard_map/all_to_all | solution.py:317
  212.8 17.3 %copy-start.16 = (bf16[16,128,128]{2,1,0:T(8,128)(2,1)}, bf16[16,128,128]{2,1,0:T(8,128)(2,1)S(1)}, u32[]{:S(2)}) copy-start(bf16[16,128,128]{2,1,0:T(8,128)(2,1)S(1)} %all-to-all-done.3) | copy-start | bytes 1572868
  212.8 17.3 %collective-permute-start.23 = (bf16[2048,128]{1,0:T(8,128)(2,1)S(1)}, bf16[2048,128]{1,0:T(8,128)(2,1)S(1)}, u32[]{:S(2)}, u32[]{:S(2)}) collective-permute-start(bf16[2048,128]{1,0:T(8,128)(2,1)S(1)} %bitcast.37), channel_id=1, source_target_pairs={{0,8},{8,0},{1,9},{9,1},{2,10},{10,2},{3,11},{11,3},{4,12},{12,4},... | collective-permute-start | bytes 1572872 | tf_op jit(solution)/shard_map/ppermute | solution.py:318
  217.5 7.2 %collective-permute-start.17 = (bf16[128,512]{1,0:T(8,128)(2,1)}, bf16[128,512]{1,0:T(8,128)(2,1)S(1)}, u32[]{:S(2)}, u32[]{:S(2)}) collective-permute-start(bf16[128,512]{1,0:T(8,128)(2,1)} %get-tuple-element.14.p0), channel_id=1, source_target_pairs={{0,1},{1,2},{2,3},{3,0},{4,5},{5,6},{6,7},{7,4},{8,9},{9,10},{10,1... | collective-permute-start | bytes 393224 | tf_op jit(solution)/shard_map/ppermute | solution.py:26
  218.1 8.7 %collective-permute-start.18 = (bf16[128,512]{1,0:T(8,128)(2,1)}, bf16[128,512]{1,0:T(8,128)(2,1)S(1)}, u32[]{:S(2)}, u32[]{:S(2)}) collective-permute-start(bf16[128,512]{1,0:T(8,128)(2,1)} %get-tuple-element.14.p0), channel_id=1, source_target_pairs={{0,2},{1,3},{2,0},{3,1},{4,6},{5,7},{6,4},{7,5},{8,10},{9,11},{10,... | collective-permute-start | bytes 393224 | tf_op jit(solution)/shard_map/ppermute | solution.py:26
  220.1 7.4 %collective-permute-start.19 = (bf16[128,512]{1,0:T(8,128)(2,1)}, bf16[128,512]{1,0:T(8,128)(2,1)S(1)}, u32[]{:S(2)}, u32[]{:S(2)}) collective-permute-start(bf16[128,512]{1,0:T(8,128)(2,1)} %get-tuple-element.14.p0), channel_id=1, source_target_pairs={{0,3},{1,0},{2,1},{3,2},{4,7},{5,4},{6,5},{7,6},{8,11},{9,8},{10,9... | collective-permute-start | bytes 393224 | tf_op jit(solution)/shard_map/ppermute | solution.py:26
  224.7 2.7 %copy-start.21 = (bf16[128,512]{1,0:T(8,128)(2,1)}, bf16[128,512]{1,0:T(8,128)(2,1)S(1)}, u32[]{:S(2)}) copy-start(bf16[128,512]{1,0:T(8,128)(2,1)S(1)} %collective-permute-done.17.p1) | copy-start | bytes 393220
  (19 other events, 17.2 us)

commit v3 on v2

v3 whole, which is shorter than its diff:
```python
import math

import jax
import jax.numpy as jnp
from jax import lax
from jax.experimental import pallas as pl
from jax.experimental.pallas import tpu as pltpu
from jax.sharding import Mesh, PartitionSpec as P

HD = 128
TOPK = 8
TOK = 128
CAP = 20
EXPERTS = 64
WIDE = 32
GROUPS = ((0, 20),)
EPS = 1e-06
THETA = 50000.0
NEG = -1e30
W = ("z", "xl", "core")
N = ("xh", "y")
f32 = jnp.float32
bf16 = jnp.bfloat16


def y_shift(x, k):
    return lax.ppermute(x, "y", [(s, (s + k) % 4) for s in range(4)])


def x_swap(x):
    return lax.ppermute(x, "xh", [(0, 1), (1, 0)])


def attention_kernel(
    here_ref,
    lengths_ref,
    qk_ref,
    gain_ref,
    x_hbm,
    w_hbm,
    out_hbm,
    out0,
    out1,
    out2,
    out3,
    x_ref,
    w_ref,
    out_w_ref,
    sems,
):
    copies = [pltpu.make_async_copy(x_hbm, x_ref, sems.at[0])]
    copies += [
        pltpu.make_async_copy(w_hbm.at[part], w_ref.at[part], sems.at[1 + part]) for part in range(3)
    ]
    copies += [pltpu.make_async_copy(out_hbm, out_w_ref, sems.at[4])]
    for copy in copies:
        copy.start()
    wide = here_ref[2]
    one = lengths_ref[0, wide]
    two = one + lengths_ref[1, wide]

    def member_of(places):
        return (places >= one).astype(jnp.int32) + (places >= two).astype(jnp.int32)

    down_places = lax.broadcasted_iota(jnp.int32, (TOK, HD), 0)
    across_places = lax.broadcasted_iota(jnp.int32, (TOK, HD), 1)
    member = member_of(down_places)
    same = member == member_of(across_places)
    start = jnp.where(member == 0, 0, jnp.where(member == 1, one, two))
    half = lax.rem(across_places, HD // 2).astype(f32)
    freq = jnp.exp(half * (-math.log(THETA) / (HD // 2)))
    angle = (down_places - start).astype(f32) * freq
    cosine = jnp.cos(angle)
    sine = jnp.sin(angle)
    sine = jnp.where(across_places < HD // 2, -sine, sine)

    copies[0].wait()
    x = x_ref[...].astype(f32)
    scale = lax.rsqrt(jnp.mean(x * x, axis=1, keepdims=True) + EPS)
    normed = (x * scale * gain_ref[0:1, :]).astype(bf16)
    parts = []
    for part in range(3):
        copies[1 + part].wait()
        parts.append(jnp.dot(normed, w_ref[part], preferred_element_type=f32))
    query, keys, values = parts

    def turned(v, gain):
        v = v * lax.rsqrt(jnp.mean(v * v, axis=1, keepdims=True) + EPS) * gain
        return (v * cosine + pltpu.roll(v, HD // 2, 1) * sine).astype(bf16)

    mixed = []
    for head in range(2):
        at = slice(head * HD, (head + 1) * HD)
        q = turned(query[:, at], qk_ref[0:1, at])
        k = turned(keys[:, at], qk_ref[1:2, at])
        scores = lax.dot_general(q, k, (((1,), (1,)), ((), ())), preferred_element_type=f32)
        scores = jnp.where(same, scores * HD ** (-0.5), NEG)
        weights = jnp.exp(scores - jnp.max(scores, axis=1, keepdims=True))
        probs = (weights / jnp.sum(weights, axis=1, keepdims=True)).astype(bf16)
        mixed.append(
            jnp.dot(probs, values[:, at].astype(bf16), preferred_element_type=f32).astype(bf16)
        )
    mixed = jnp.concatenate(mixed, axis=1)
    copies[4].wait()
    j = here_ref[1]
    for k, out_ref in enumerate((out0, out1, out2, out3)):
        part = lax.rem(j + k, 4)
        columns = pl.ds(pl.multiple_of(part * 512, 512), 512)
        out_ref[...] = jnp.dot(mixed, out_w_ref[:, columns], preferred_element_type=f32).astype(bf16)


def dispatch_kernel(here_ref, x_ref, own_ref, par_ref, choose_ref, hidden_ref, *rows_refs):
    j = here_ref[1]
    mine = x_ref[:, pl.ds(pl.multiple_of(j * 512, 512), 512)].astype(f32)
    hidden = (mine + (own_ref[...].astype(f32) + par_ref[...].astype(f32))).astype(bf16)
    hidden_ref[...] = hidden
    rows = jnp.dot(choose_ref[...], hidden, preferred_element_type=f32)
    at = 0
    for rows_ref in rows_refs:
        size = rows_ref.shape[1]
        for s in range(WIDE):
            rows_ref[s] = rows[at : at + size].astype(bf16)
            at += size


def gate_up_kernel(
    here_ref, x0, x1, x2, x3, gain_ref, gate_hbm, up_hbm, gate_par, up_par, out_ref, w_ref, sems
):
    i, j = here_ref[0], here_ref[1]
    sources = (gate_hbm.at[i], up_hbm.at[i], gate_par, up_par)
    copies = [
        pltpu.make_async_copy(source, w_ref.at[n], sems.at[n]) for n, source in enumerate(sources)
    ]
    for copy in copies:
        copy.start()
    xs = (x0, x1, x2, x3)
    total = jnp.zeros((x0.shape[0], 1), f32)
    for x in xs:
        v = x[...].astype(f32)
        total = total + jnp.sum(v * v, axis=1, keepdims=True)
    scale = lax.rsqrt(total / 2048.0 + EPS)
    for copy in copies:
        copy.wait()
    own = jnp.zeros((x0.shape[0], 256), f32)
    par = jnp.zeros((x0.shape[0], 256), f32)
    for k, x in enumerate(xs):
        part = lax.rem(j - k + 4, 4)
        rows = pl.ds(pl.multiple_of(part * 512, 512), 512)
        normed = (x[...].astype(f32) * scale * gain_ref[1:2, rows]).astype(bf16)
        w_own = jnp.concatenate([w_ref[0, rows, :], w_ref[1, rows, :]], axis=1)
        w_par = jnp.concatenate([w_ref[2, rows, :], w_ref[3, rows, :]], axis=1)
        own = own + jnp.dot(normed, w_own, preferred_element_type=f32)
        par = par + jnp.dot(normed, w_par, preferred_element_type=f32)
    for at, both in ((0, own), (128, par)):
        gate, up = both[:, :128], both[:, 128:]
        out_ref[:, at : at + 128] = (gate / (1.0 + jnp.exp(-gate)) * up).astype(bf16)


def down_kernel(here_ref, a0, a1, a2, a3, w0, w1, w2, w3, par_ref, out_ref, w_ref, sems):
    i = here_ref[0]
    copies = []
    for k, w in enumerate((w0, w1, w2, w3)):
        copies.append(
            (
                pltpu.make_async_copy(w.at[i], w_ref.at[k, 0:128], sems.at[0, k]),
                pltpu.make_async_copy(par_ref.at[k], w_ref.at[k, 128:256], sems.at[1, k]),
            )
        )
    for pair in copies:
        for copy in pair:
            copy.start()
    total = jnp.zeros((a0.shape[0], 512), f32)
    for k, a in enumerate((a0, a1, a2, a3)):
        for copy in copies[k]:
            copy.wait()
        total = total + jnp.dot(a[...], w_ref[k], preferred_element_type=f32)
    size = out_ref.shape[1]
    for s in range(WIDE):
        out_ref[s] = total[s * size : (s + 1) * size].astype(bf16)


def embed_kernel(here_ref, hidden_ref, moe_ref, par_ref, gain_ref, w_ref, layer_ref, part_ref):
    mine = pl.ds(pl.multiple_of(here_ref[1] * 512, 512), 512)
    layer = hidden_ref[...].astype(f32) + (moe_ref[...].astype(f32) + par_ref[...].astype(f32))
    layer = layer.astype(bf16)
    layer_ref[...] = layer
    layer = layer.astype(f32)
    scaled = (layer * gain_ref[2:3, mine]).astype(bf16)
    part_ref[0:TOK, :] = jnp.dot(scaled, w_ref[mine, :], preferred_element_type=f32)
    square = jnp.broadcast_to(jnp.sum(layer * layer, axis=1, keepdims=True), (TOK, TOK))
    part_ref[TOK:, :] = jnp.transpose(square)[0:8]


def vector_kernel(p0, p1, p2, p3, out_ref):
    whole = p0[...] + p1[...] + p2[...] + p3[...]
    square = jnp.transpose(jnp.broadcast_to(whole[TOK : TOK + 1], (TOK, TOK)))
    embedded = whole[0:TOK] * lax.rsqrt(square / 2048.0 + EPS)
    norm = jnp.sum(embedded * embedded, axis=1, keepdims=True)
    vectors = (embedded * lax.rsqrt(norm + EPS)).astype(bf16)
    for copy in range(16):
        out_ref[copy] = vectors


def assemble_kernel(here_ref, p0, p1, p2, p3, out_ref):
    j = here_ref[1]
    for k, piece in enumerate((p0, p1, p2, p3)):
        part = lax.rem(j - k + 4, 4)
        out_ref[:, pl.ds(pl.multiple_of(part * 512, 512), 512)] = piece[...]


def score_kernel(info_ref, doc_ref, own_ref, other_ref, out_ref, query_ref, sems):
    def spot(d):
        return pl.multiple_of(jnp.minimum((info_ref[2, d] // 16) * 16, 2048 - 128), 16)

    def copy_of(ref, d):
        return pltpu.make_async_copy(ref.at[pl.ds(spot(d), 128), :], query_ref.at[d], sems.at[d])

    for d in range(16):

        @pl.when(info_ref[4, d] == 0)
        def _():
            copy_of(own_ref, d).start()

        @pl.when(info_ref[4, d] != 0)
        def _():
            copy_of(other_ref, d).start()

    lane = lax.broadcasted_iota(jnp.int32, (1, 16), 1)
    scores = jnp.zeros((1, 16), f32)
    rows = lax.broadcasted_iota(jnp.int32, (144, 128), 0)
    columns = lax.broadcasted_iota(jnp.int32, (1, 128), 1)
    for d in range(16):
        copy_of(own_ref, d).wait()
    for d in range(16):
        first, size = info_ref[0, d], info_ref[1, d]
        q_first, q_size = info_ref[2, d], info_ref[3, d]
        at = pl.multiple_of(jnp.minimum((first // 16) * 16, 1024 - 144), 16)
        sims = lax.dot_general(
            doc_ref[pl.ds(at, 144), :],
            query_ref[d],
            (((1,), (1,)), ((), ())),
            preferred_element_type=f32,
        )
        keep = (rows >= first - at) & (rows < first - at + size)
        best = jnp.max(jnp.where(keep, sims, NEG), axis=0, keepdims=True)
        q_start = q_first - spot(d)
        used = (columns >= q_start) & (columns < q_start + q_size)
        value = jnp.sum(jnp.where(used, best, 0.0), axis=1, keepdims=True) / q_size.astype(f32)
        scores = jnp.where(lane == d, value, scores)
    out_ref[...] = scores


def vmem():
    return pl.BlockSpec(memory_space=pltpu.VMEM)


def smem():
    return pl.BlockSpec(memory_space=pltpu.SMEM)


def hbm():
    return pl.BlockSpec(memory_space=pl.ANY)


def params():
    return pltpu.CompilerParams(vmem_limit_bytes=40 << 20)


def body(
    tokens,
    request_lengths,
    w_qkv,
    qk_gain,
    w_out,
    norm_gains,
    w_router,
    routes,
    w_gate,
    w_up,
    w_down,
    w_proj,
    doc_vectors,
    doc_segment,
    doc_request,
):
    i = lax.axis_index("xh")
    j = lax.axis_index("y")
    core = lax.axis_index("core")
    wide = lax.axis_index(W)
    here = jnp.stack([i, j, wide, core])

    def pick(array, which):
        return lax.dynamic_index_in_dim(array, which, 0, keepdims=False)

    def cut(array, part, axis):
        return lax.dynamic_slice_in_dim(array, lax.rem(part, 4) * 512, 512, axis)

    attn = pl.pallas_call(
        attention_kernel,
        out_shape=(jax.ShapeDtypeStruct((TOK, 512), bf16),) * 4,
        in_specs=[smem()] * 2 + [vmem()] * 2 + [hbm()] * 3,
        out_specs=(vmem(),) * 4,
        scratch_shapes=[
            pltpu.VMEM((TOK, 2048), bf16),
            pltpu.VMEM((3, 2048, 256), bf16),
            pltpu.VMEM((256, 2048), bf16),
            pltpu.SemaphoreType.DMA((5,)),
        ],
        compiler_params=params(),
        name="attention",
    )(
        here,
        request_lengths.T,
        qk_gain,
        norm_gains,
        tokens,
        w_qkv.transpose(1, 0, 2),
        w_out,
    )
    attn_parts = [y_shift(attn[k], k) for k in (1, 2, 3)]

    own_part, w_gate, w_up = lax.optimization_barrier((attn[0], w_gate, w_up))
    gate_par = x_swap(pick(w_gate, 1 - i))
    up_par = x_swap(pick(w_up, 1 - i))
    downs = [cut(w_down, j, 2)] + [y_shift(cut(w_down, j + k, 2), k) for k in (1, 2, 3)]
    down_par = x_swap(jnp.stack([pick(d, 1 - i) for d in downs]))

    experts_here = 2 * jnp.arange(WIDE, dtype=jnp.int32) + i
    hit = jnp.sum((routes.T[None, :, :] == experts_here[:, None, None]).astype(f32), axis=1)
    places = jnp.arange(TOK, dtype=jnp.int32)
    earlier = (places[:, None] < places[None, :]).astype(bf16)
    before = jnp.dot(hit.astype(bf16), earlier, preferred_element_type=f32)
    slot = jnp.arange(CAP, dtype=jnp.int32).astype(f32)
    chosen = (before[:, None, :] == slot[None, :, None]) & (hit[:, None, :] > 0)
    choose = jnp.concatenate(
        [chosen[:, a:b].astype(bf16).reshape(WIDE * (b - a), TOK) for a, b in GROUPS], axis=0
    )

    attn = (own_part.astype(f32) + sum(p.astype(f32) for p in attn_parts)).astype(bf16)
    attn, choose = lax.optimization_barrier((attn, choose))
    attn_par = x_swap(attn)
    attn_par, gate_par = lax.optimization_barrier((attn_par, gate_par))
    hidden, *rows = pl.pallas_call(
        dispatch_kernel,
        out_shape=(
            jax.ShapeDtypeStruct((TOK, 512), bf16),
            *(jax.ShapeDtypeStruct((WIDE, b - a, 512), bf16) for a, b in GROUPS),
        ),
        in_specs=[smem()] + [vmem()] * 4,
        out_specs=(vmem(),) * (1 + len(GROUPS)),
        compiler_params=params(),
        name="dispatch",
    )(here, tokens, attn, attn_par, choose)

    backs = []
    arrived = []
    for g, group in enumerate(rows):
        if arrived:
            group, arrived[-1] = lax.optimization_barrier((group, arrived[-1]))
        arrived.append(lax.all_to_all(group, W, 0, 0, tiled=True))
    for g, x in enumerate(arrived):
        size = x.shape[1]
        x = x.reshape(WIDE * size, 512)
        if g == 0:
            x, up_par = lax.optimization_barrier((x, up_par))
        act = pl.pallas_call(
            gate_up_kernel,
            out_shape=jax.ShapeDtypeStruct((WIDE * size, 256), bf16),
            in_specs=[smem()] + [vmem()] * 5 + [hbm()] * 4,
            out_specs=vmem(),
            scratch_shapes=[pltpu.VMEM((4, 2048, 128), bf16), pltpu.SemaphoreType.DMA((4,))],
            compiler_params=params(),
            name="gate_up",
        )(here, x, *(y_shift(x, k) for k in (1, 2, 3)), norm_gains, w_gate, w_up, gate_par, up_par)
        if g == 0:
            act, down_par = lax.optimization_barrier((act, down_par))
        out = pl.pallas_call(
            down_kernel,
            out_shape=jax.ShapeDtypeStruct((WIDE, size, 512), bf16),
            in_specs=[smem()] + [vmem()] * 4 + [hbm()] * 5,
            out_specs=vmem(),
            scratch_shapes=[pltpu.VMEM((4, 256, 512), bf16), pltpu.SemaphoreType.DMA((2, 4))],
            compiler_params=params(),
            name="down",
        )(here, act, *(y_shift(act, k) for k in (1, 2, 3)), *downs, down_par)
        backs.append(lax.all_to_all(out, W, 0, 0, tiled=True))

    hf = hidden.astype(f32)
    gain_mine = lax.dynamic_slice_in_dim(norm_gains[1], j * 512, 512, 0)
    router_mine = lax.dynamic_slice_in_dim(w_router, j * 512, 512, 0)
    part = jnp.dot((hf * gain_mine).astype(bf16), router_mine, preferred_element_type=f32)
    square = jnp.sum(hf * hf, axis=1, keepdims=True)
    part = jnp.concatenate([part, jnp.broadcast_to(square, (TOK, EXPERTS))], axis=1)
    whole = part
    for k in (1, 2, 3):
        whole = whole + y_shift(part, k)
    logits = whole[:, :EXPERTS] * lax.rsqrt(whole[:, EXPERTS : EXPERTS + 1] / 2048.0 + EPS)
    lifted = jax.nn.sigmoid(logits)
    onehot = jnp.sum(
        (routes[:, :, None] == jnp.arange(EXPERTS, dtype=jnp.int32)[None, None, :]).astype(f32),
        axis=1,
    )
    lifted = lifted * onehot
    gates = lifted / jnp.sum(lifted, axis=1, keepdims=True)
    gates = lax.dynamic_index_in_dim(gates.reshape(TOK, WIDE, 2), i, 2, keepdims=False).T

    moe = jnp.zeros((TOK, 512), f32)
    contract = (((0, 1), (0, 1)), ((), ()))
    for (a, b), back in zip(GROUPS, backs):
        mixing = jnp.where(chosen[:, a:b], gates[:, None, :], 0.0)
        mixing_hi = lax.reduce_precision(mixing, 8, 7)
        mixing_lo = (mixing - mixing_hi).astype(bf16)
        for matrix in (mixing_hi.astype(bf16), mixing_lo):
            moe = moe + lax.dot_general(matrix, back, contract, preferred_element_type=f32)
    moe = moe.astype(bf16)
    moe_par = x_swap(moe)
    layer, part = pl.pallas_call(
        embed_kernel,
        out_shape=(
            jax.ShapeDtypeStruct((TOK, 512), bf16),
            jax.ShapeDtypeStruct((TOK + 8, 128), f32),
        ),
        in_specs=[smem()] + [vmem()] * 5,
        out_specs=(vmem(), vmem()),
        name="embed",
    )(here, hidden, moe, moe_par, norm_gains, w_proj)
    parts = [part] + [y_shift(part, k) for k in (1, 2, 3)]

    vectors = pl.pallas_call(
        vector_kernel,
        out_shape=jax.ShapeDtypeStruct((16, TOK, 128), bf16),
        in_specs=[vmem()] * 4,
        out_specs=vmem(),
        name="vectors",
    )(*parts)
    vectors, layer = lax.optimization_barrier((vectors, layer))
    layers = [layer] + [y_shift(layer, k) for k in (1, 2, 3)]
    own = lax.all_to_all(vectors, ("z", "xl"), 0, 0, tiled=True).reshape(16 * TOK, 128)
    segment = doc_segment[0]
    requests = doc_request[0]
    docs = jnp.arange(16, dtype=jnp.int32)
    first = jnp.sum((segment[None, :] < docs[:, None]).astype(jnp.int32), axis=1)
    size = jnp.sum((segment[None, :] == docs[:, None]).astype(jnp.int32), axis=1)
    starts = jnp.cumsum(request_lengths, axis=1) - request_lengths
    starts = (starts + TOK * (jnp.arange(WIDE, dtype=jnp.int32) // 2)[:, None]).reshape(-1)
    match = requests[:, None] == jnp.arange(96, dtype=jnp.int32)[None, :]
    q_first = jnp.sum(jnp.where(match, starts[None, :], 0), axis=1)
    q_size = jnp.sum(jnp.where(match, request_lengths.reshape(-1)[None, :], 0), axis=1)
    away = lax.rem(requests // 3, 2) ^ core
    info = jnp.stack([first, size, q_first, q_size, away])
    own, info, *layers = lax.optimization_barrier((own, info, *layers))
    other = lax.ppermute(own, "core", [(0, 1), (1, 0)])
    layer_out = pl.pallas_call(
        assemble_kernel,
        out_shape=jax.ShapeDtypeStruct((TOK, 2048), bf16),
        in_specs=[smem()] + [vmem()] * 4,
        out_specs=vmem(),
        name="assemble",
    )(here, *layers)
    doc_scores = pl.pallas_call(
        score_kernel,
        out_shape=jax.ShapeDtypeStruct((1, 16), f32),
        in_specs=[smem(), vmem(), hbm(), hbm()],
        out_specs=vmem(),
        scratch_shapes=[pltpu.VMEM((16, 128, 128), bf16), pltpu.SemaphoreType.DMA((16,))],
        name="score",
    )(info, doc_vectors, own, other)
    return (layer_out, doc_scores)


def solution(mesh):
    split = Mesh(mesh.devices.reshape(8, 2, 2, 2, 4), ("z", "xl", "core", "xh", "y"))
    placed = (
        P(W, None),
        P(),
        P(None, None, N),
        P(None, N),
        P(N, None),
        P(),
        P(),
        P(W, None),
        P(W, None, N),
        P(W, None, N),
        P(W, N, None),
        P(),
        P(W + N, None),
        P(W + N, None),
        P(W + N, None),
    )
    return jax.shard_map(
        body,
        mesh=split,
        in_specs=placed,
        out_specs=(P(W, None), P(W + N, None)),
        check_vma=False,
    )
```

time: 235 us -> 217 us (0.923)
  waiting for transfers between devices: 110 us -> 88 us
  local copies, waits for them, and re-layouts: 29.5 us -> 33.6 us
  Pallas kernels: 18.7 us -> 21.5 us
  starting transfers between devices: 67.4 us -> 64.9 us
    all_to_all x3 -> x2, starting transfers between devices: 27.9 us -> 19.4 us  [the longest x1 11.6 us: body(): arrived.append(lax.all_to_all(group, W, 0, 0, tiled=True))]
    ppermute x18 -> x21, starting transfers between devices: 18.5 us -> 26.8 us  [y_shift(): return lax.ppermute(x, 'y', [(s, (s + k) % 4) for s in range(4)])]
    all_to_all x1, waiting for transfers between devices: 13.9 us -> 5.67 us  [body(): lax.all_to_all(vectors, ('z', 'xl'), 0, 0, tiled=True)]
    all_to_all x3 -> x2, waiting for transfers between devices: 26.6 us -> 20.2 us  [the longest x1 13.9 us: body(): backs.append(lax.all_to_all(out, W, 0, 0, tiled=True))]
    ppermute x5, waiting for transfers between devices: 14.1 us -> 8.18 us  [x_swap(): return lax.ppermute(x, 'xh', [(0, 1), (1, 0)])]
    eq x0 -> x4, local copies, waits for them, and re-layouts: none -> 4.68 us  [body(): chosen = (before[:, None, :] == slot[None, :, None]) & (hit[:, None, :] > 0)]
    unnamed x79 -> x85, local copies, waits for them, and re-layouts: 14.2 us -> 16.6 us
    pallas_call x3 -> x4, Pallas kernels: 10.3 us -> 12.2 us  [the longest x1 4.29 us: body(): pl.pallas_call(attention_kernel, out_shape=(jax.ShapeDtypeStruct((TOK, 51...]
  transfers between devices with their start and end apart: 28 -> 30, of which waited for: 23 -> 20; matrix products, arithmetic and copies ran while one was open for 7% -> 10% of each run, Pallas kernels for 3% -> 2%
where the time goes in v3:
time: 217 us; the launch traced here: 215 us
  waiting for transfers between devices  88 us (41%)
  starting transfers between devices  64.9 us (30%)
  local copies, waits for them, and re-layouts  33.6 us (15%)
  Pallas kernels  21.5 us (10%)
  other arithmetic  4.18 us (2%)
    ppermute x21, waiting for transfers between devices, y_shift(): return lax.ppermute(x, 'y', [(s, (s + k) % 4) for s in range(4)])  54 us
    ppermute x21, starting transfers between devices, y_shift(): return lax.ppermute(x, 'y', [(s, (s + k) % 4) for s in range(4)])  26.8 us
    unnamed x85, local copies, waits for them, and re-layouts  16.6 us
    all_to_all x1, waiting for transfers between devices, body(): backs.append(lax.all_to_all(out, W, 0, 0, tiled=True))  13.9 us
    all_to_all x1, starting transfers between devices, body(): arrived.append(lax.all_to_all(group, W, 0, 0, tiled=True))  11.6 us
    ppermute x5, starting transfers between devices, x_swap(): return lax.ppermute(x, 'xh', [(0, 1), (1, 0)])  9.12 us
    ppermute x5, waiting for transfers between devices, x_swap(): return lax.ppermute(x, 'xh', [(0, 1), (1, 0)])  8.18 us
    all_to_all x1, starting transfers between devices, body(): backs.append(lax.all_to_all(out, W, 0, 0, tiled=True))  7.75 us
  transfers between devices with their start and end apart: 30, of which 20 were waited for; matrix products, arithmetic and copies ran while one was open for 10% of the time, Pallas kernels for 2%

profile of v3, /device:TPU:1, one launch (start us, length us, event | category | flops | bytes accessed | tf_op | source)
XLA Modules:
  0.0 215.2 jit_solution(10936018731489599150)
XLA Ops:
  0.7 1.9 copy-done.1
  3.7 1.2 copy-done.7
  7.0 4.3 %attention.1 = (bf16[128,512]{1,0:T(8,128)(2,1)S(1)}, bf16[128,512]{1,0:T(8,128)(2,1)}, bf16[128,512]{1,0:T(8,128)(2,1)}, bf16[128,512]{1,0:T(8,128)(2,1)}) custom-call(s32[4]{0:T(128)S(1)} %pad_add_fusion.here_ref, s32[3,32]{1,0:T(4,128)S(1)} %bitcast.36, f32[2,256]{1,0:T(2,128)S(1)} %copy-done.25, f32[3,2048]{1,0:T(4,128)S(1)} %copy-done.18, ...), custom_call_target="tpu_custom_call" | custom-call | tf_op jit(solution)/shard_map/attention/pallas_call | solution.py:298
  12.0 3.6 %collective-permute-start.2 = (bf16[128,512]{1,0:T(8,128)(2,1)}, bf16[128,512]{1,0:T(8,128)(2,1)}, u32[]{:S(2)}, u32[]{:S(2)}) collective-permute-start(bf16[128,512]{1,0:T(8,128)(2,1)} %get-tuple-element.33), channel_id=1, source_target_pairs={{0,3},{1,0},{2,1},{3,2},{4,7},{5,4},{6,5},{7,6},{8,11},{9,8},{10,9... | collective-permute-start | bytes 393224 | tf_op jit(solution)/shard_map/ppermute | solution.py:27
  17.4 2.7 %collective-permute-start.4 = (bf16[2048,128]{1,0:T(8,128)(2,1)}, bf16[2048,128]{1,0:T(8,128)(2,1)S(1)}, u32[]{:S(2)}, u32[]{:S(2)}) collective-permute-start(bf16[2048,128]{1,0:T(8,128)(2,1)} %dynamic-slice_bitcast_fusion.1), channel_id=1, source_target_pairs={{0,4},{4,0},{1,5},{5,1},{2,6},{6,2},{3,7},{7,3},{8,12},{12,8},{9,1... | collective-permute-start | bytes 1572872 | tf_op jit(solution)/shard_map/ppermute | solution.py:31
  21.7 1.6 and.43
  23.3 1.5 eq.77
  24.8 1.8 eq.78
  28.0 1.2 and_convert_fusion.choose_ref
  30.6 5.1 %collective-permute-done.3.par_ref = bf16[128,512]{1,0:T(8,128)(2,1)S(1)} collective-permute-done((bf16[128,512]{1,0:T(8,128)(2,1)S(1)}, bf16[128,512]{1,0:T(8,128)(2,1)S(1)}, u32[]{:S(2)}, u32[]{:S(2)}) %collective-permute-start.3) | collective-permute-done | bytes 131104 | tf_op jit(solution)/shard_map/ppermute | solution.py:31
  37.5 11.6 %all-to-all-start = ((bf16[32,20,512]{2,1,0:T(8,128)(2,1)}), bf16[32,20,512]{2,1,0:T(8,128)(2,1)}, u32[]{:S(2)}, u32[]{:S(2)}) async-start(bf16[32,20,512]{2,1,0:T(8,128)(2,1)} %copy-done.9), calls=%async_computation | async-start | bytes 1572864 | tf_op jit(solution)/shard_map/all_to_all | solution.py:360
  50.0 1.7 collective-permute-start.8
  51.8 2.2 %constant_dynamic-slice_fusion = (bf16[2,128,512]{2,1,0:T(8,128)(2,1)}, bf16[2,128,512]{2,1,0:T(8,128)(2,1)}, bf16[2,128,512]{2,1,0:T(8,128)(2,1)}, bf16[2,128,512]{2,1,0:T(8,128)(2,1)}) fusion(bf16[2,128,2048]{2,1,0:T(8,128)(2,1)} %param.25, s32[]{:T(128)S(6)} %select_n.65, s32[]{:T(128)S(6)} %select_n.68, s32[]{:T(128)S(6)} %select_n.67, s32[]{:T(128)S(6)} %select_n.69), kind=kLoop, calls=%fused_computation.53 | loop fusion | bytes 2097168 | tf_op jit(solution)/shard_map/dynamic_slice | solution.py:296
  53.9 2.0 collective-permute-start.14
  55.9 1.4 collective-permute-start.13
  57.3 1.7 constant_dynamic-slice_fusion.7
  59.0 2.8 %collective-permute-done.14.w3 = bf16[2,128,512]{2,1,0:T(8,128)(2,1)S(1)} collective-permute-done((bf16[2,128,512]{2,1,0:T(8,128)(2,1)}, bf16[2,128,512]{2,1,0:T(8,128)(2,1)S(1)}, u32[]{:S(2)}, u32[]{:S(2)}) %collective-permute-start.14) | collective-permute-done | bytes 262176 | tf_op jit(solution)/shard_map/ppermute | solution.py:27
  62.6 2.2 %collective-permute-done.13.w2 = bf16[2,128,512]{2,1,0:T(8,128)(2,1)S(1)} collective-permute-done((bf16[2,128,512]{2,1,0:T(8,128)(2,1)}, bf16[2,128,512]{2,1,0:T(8,128)(2,1)S(1)}, u32[]{:S(2)}, u32[]{:S(2)}) %collective-permute-start.13) | collective-permute-done | bytes 262176 | tf_op jit(solution)/shard_map/ppermute | solution.py:27
  65.5 6.3 %all-to-all-done = bf16[32,20,512]{2,1,0:T(8,128)(2,1)} async-done(((bf16[32,20,512]{2,1,0:T(8,128)(2,1)}), bf16[32,20,512]{2,1,0:T(8,128)(2,1)}, u32[]{:S(2)}, u32[]{:S(2)}) %all-to-all-start) | async-done | bytes 655392 | tf_op jit(solution)/shard_map/all_to_all | solution.py:360
  71.8 1.2 reshape.57.x0
  73.1 1.7 collective-permute-start.9
  74.8 1.6 collective-permute-start.10
  79.3 2.0 collective-permute-start.15
  81.3 8.2 %collective-permute-done.9.x1 = bf16[640,512]{1,0:T(8,128)(2,1)S(1)} collective-permute-done((bf16[640,512]{1,0:T(8,128)(2,1)S(1)}, bf16[640,512]{1,0:T(8,128)(2,1)S(1)}, u32[]{:S(2)}, u32[]{:S(2)}) %collective-permute-start.9) | collective-permute-done | bytes 655392 | tf_op jit(solution)/shard_map/ppermute | solution.py:27
  89.5 14.5 %collective-permute-done.10.x2 = bf16[640,512]{1,0:T(8,128)(2,1)S(1)} collective-permute-done((bf16[640,512]{1,0:T(8,128)(2,1)S(1)}, bf16[640,512]{1,0:T(8,128)(2,1)S(1)}, u32[]{:S(2)}, u32[]{:S(2)}) %collective-permute-start.10) | collective-permute-done | bytes 655392 | tf_op jit(solution)/shard_map/ppermute | solution.py:27
  106.4 3.3 %gate_up.1.a0 = bf16[640,256]{1,0:T(8,128)(2,1)S(1)} custom-call(s32[4]{0:T(128)S(1)} %pad_add_fusion.here_ref, bf16[640,512]{1,0:T(8,128)(2,1)S(1)} %reshape.57.x0, bf16[640,512]{1,0:T(8,128)(2,1)S(1)} %collective-permute-done.9.x1, bf16[640,512]{1,0:T(8,128)(2,1)S(1)} %collective-permute-done.10.x2, bf16[640,512]{1,0:T(8,128)(2,1)S(1)} %collective-permute-done.11.x3, ...), custom_call_target="tpu_custom_call" | custom-call | tf_op jit(solution)/shard_map/gate_up/pallas_call | solution.py:366
  110.6 2.4 %collective-permute-start.16 = (bf16[640,256]{1,0:T(8,128)(2,1)S(1)}, bf16[640,256]{1,0:T(8,128)(2,1)S(1)}, u32[]{:S(2)}, u32[]{:S(2)}) collective-permute-start(bf16[640,256]{1,0:T(8,128)(2,1)S(1)} %gate_up.1.a0), channel_id=1, source_target_pairs={{0,1},{1,2},{2,3},{3,0},{4,5},{5,6},{6,7},{7,4},{8,9},{9,10},{10,1... | collective-permute-start | bytes 983048 | tf_op jit(solution)/shard_map/ppermute | solution.py:27
  113.0 2.1 collective-permute-start.17
  115.5 5.5 %collective-permute-done.16.a1 = bf16[640,256]{1,0:T(8,128)(2,1)S(1)} collective-permute-done((bf16[640,256]{1,0:T(8,128)(2,1)S(1)}, bf16[640,256]{1,0:T(8,128)(2,1)S(1)}, u32[]{:S(2)}, u32[]{:S(2)}) %collective-permute-start.16) | collective-permute-done | bytes 327712 | tf_op jit(solution)/shard_map/ppermute | solution.py:27
  120.9 8.6 %collective-permute-done.17.a2 = bf16[640,256]{1,0:T(8,128)(2,1)S(1)} collective-permute-done((bf16[640,256]{1,0:T(8,128)(2,1)S(1)}, bf16[640,256]{1,0:T(8,128)(2,1)S(1)}, u32[]{:S(2)}, u32[]{:S(2)}) %collective-permute-start.17) | collective-permute-done | bytes 327712 | tf_op jit(solution)/shard_map/ppermute | solution.py:27
  133.4 3.7 %down.1 = bf16[32,20,512]{2,1,0:T(8,128)(2,1)} custom-call(s32[4]{0:T(128)S(1)} %pad_add_fusion.here_ref, bf16[640,256]{1,0:T(8,128)(2,1)S(1)} %gate_up.1.a0, bf16[640,256]{1,0:T(8,128)(2,1)S(1)} %collective-permute-done.16.a1, bf16[640,256]{1,0:T(8,128)(2,1)S(1)} %collective-permute-done.17.a2, bf16[640,256]{1,0:T(8,128)(2,1)S(1)} %collective-permute-done.18.a3, ...), custom_call_target="tpu_custom_call" | custom-call | tf_op jit(solution)/shard_map/down/pallas_call | solution.py:377
  137.1 7.7 %all-to-all-start.1 = ((bf16[32,20,512]{2,1,0:T(8,128)(2,1)}), bf16[32,20,512]{2,1,0:T(8,128)(2,1)S(1)}, u32[]{:S(2)}, u32[]{:S(2)}) async-start(bf16[32,20,512]{2,1,0:T(8,128)(2,1)} %down.1), calls=%async_computation.1 | async-start | bytes 1572864 | tf_op jit(solution)/shard_map/all_to_all | solution.py:386
  145.2 1.9 collective-permute-start.7
  148.8 3.2 %collective-permute-done.6 = f32[128,128]{0,1:T(8,128)S(1)} collective-permute-done((f32[128,128]{0,1:T(8,128)S(1)}, f32[128,128]{0,1:T(8,128)S(1)}, u32[]{:S(2)}, u32[]{:S(2)}) %collective-permute-start.6) | collective-permute-done | bytes 65568 | tf_op jit(solution)/shard_map/ppermute | solution.py:27
  151.9 1.5 collective-permute-done.5
  153.6 13.9 %all-to-all-done.1 = bf16[32,20,512]{2,1,0:T(8,128)(2,1)S(1)} async-done(((bf16[32,20,512]{2,1,0:T(8,128)(2,1)}), bf16[32,20,512]{2,1,0:T(8,128)(2,1)S(1)}, u32[]{:S(2)}, u32[]{:S(2)}) %all-to-all-start.1) | async-done | bytes 655392 | tf_op jit(solution)/shard_map/all_to_all | solution.py:386
  168.3 2.3 %collective-permute-start.19 = (bf16[128,512]{1,0:T(8,128)(2,1)S(1)}, bf16[128,512]{1,0:T(8,128)(2,1)S(1)}, u32[]{:S(2)}, u32[]{:S(2)}) collective-permute-start(bf16[128,512]{1,0:T(8,128)(2,1)S(1)} %fusion.1.moe_ref), channel_id=1, source_target_pairs={{0,4},{4,0},{1,5},{5,1},{2,6},{6,2},{3,7},{7,3},{8,12},{12,8},{9,1... | collective-permute-start | bytes 393224 | tf_op jit(solution)/shard_map/ppermute | solution.py:31
  170.6 3.1 %collective-permute-done.19.par_ref = bf16[128,512]{1,0:T(8,128)(2,1)S(1)} collective-permute-done((bf16[128,512]{1,0:T(8,128)(2,1)S(1)}, bf16[128,512]{1,0:T(8,128)(2,1)S(1)}, u32[]{:S(2)}, u32[]{:S(2)}) %collective-permute-start.19) | collective-permute-done | bytes 131104 | tf_op jit(solution)/shard_map/ppermute | solution.py:31
  174.3 2.1 embed.1
  177.2 2.2 %collective-permute-start.21 = (f32[136,128]{1,0:T(8,128)}, f32[136,128]{1,0:T(8,128)S(1)}, u32[]{:S(2)}, u32[]{:S(2)}) collective-permute-start(f32[136,128]{1,0:T(8,128)} %get-tuple-element.46.p0), channel_id=1, source_target_pairs={{0,2},{1,3},{2,0},{3,1},{4,6},{5,7},{6,4},{7,5},{8,10},{9,11},{10,... | collective-permute-start | bytes 208904 | tf_op jit(solution)/shard_map/ppermute | solution.py:27
  183.4 2.0 vectors.1
  185.4 5.2 %all-to-all-start.2 = ((bf16[16,128,128]{2,1,0:T(8,128)(2,1)}), bf16[16,128,128]{2,1,0:T(8,128)(2,1)S(1)}, u32[]{:S(2)}, u32[]{:S(2)}) async-start(bf16[16,128,128]{2,1,0:T(8,128)(2,1)} %vectors.1), calls=%async_computation.2 | async-start | bytes 1048576 | tf_op jit(solution)/shard_map/all_to_all | solution.py:438
  191.4 2.4 %collective-permute-start.24 = (bf16[128,512]{1,0:T(8,128)(2,1)}, bf16[128,512]{1,0:T(8,128)(2,1)S(1)}, u32[]{:S(2)}, u32[]{:S(2)}) collective-permute-start(bf16[128,512]{1,0:T(8,128)(2,1)} %get-tuple-element.50.p0), channel_id=1, source_target_pairs={{0,2},{1,3},{2,0},{3,1},{4,6},{5,7},{6,4},{7,5},{8,10},{9,11},{10,... | collective-permute-start | bytes 393224 | tf_op jit(solution)/shard_map/ppermute | solution.py:27
  195.7 2.3 %collective-permute-done.23.p1 = bf16[128,512]{1,0:T(8,128)(2,1)S(1)} collective-permute-done((bf16[128,512]{1,0:T(8,128)(2,1)}, bf16[128,512]{1,0:T(8,128)(2,1)S(1)}, u32[]{:S(2)}, u32[]{:S(2)}) %collective-permute-start.23) | collective-permute-done | bytes 131104 | tf_op jit(solution)/shard_map/ppermute | solution.py:27
  198.9 5.7 %all-to-all-done.2 = bf16[16,128,128]{2,1,0:T(8,128)(2,1)S(1)} async-done(((bf16[16,128,128]{2,1,0:T(8,128)(2,1)}), bf16[16,128,128]{2,1,0:T(8,128)(2,1)S(1)}, u32[]{:S(2)}, u32[]{:S(2)}) %all-to-all-start.2) | async-done | bytes 524320 | tf_op jit(solution)/shard_map/all_to_all | solution.py:438
  204.5 4.4 %collective-permute-start.26 = (bf16[2048,128]{1,0:T(8,128)(2,1)S(1)}, bf16[2048,128]{1,0:T(8,128)(2,1)S(1)}, u32[]{:S(2)}, u32[]{:S(2)}) collective-permute-start(bf16[2048,128]{1,0:T(8,128)(2,1)S(1)} %bitcast.37), channel_id=1, source_target_pairs={{0,8},{8,0},{1,9},{9,1},{2,10},{10,2},{3,11},{11,3},{4,12},{12,4},... | collective-permute-start | bytes 1572872 | tf_op jit(solution)/shard_map/ppermute | solution.py:452
  209.0 1.9 assemble.1
  211.7 3.3 %score.1 = f32[1,16]{1,0:T(1,128)} custom-call(s32[5,16]{1,0:T(8,128)} %stack.48.info_ref, bf16[1024,128]{1,0:T(8,128)(2,1)} %doc_ref.1, bf16[2048,128]{1,0:T(8,128)(2,1)} %bitcast.38, bf16[2048,128]{1,0:T(8,128)(2,1)} %copy-done.27), custom_call_target="tpu_custom_call" | custom-call | tf_op jit(solution)/shard_map/score/pallas_call | solution.py:460
  (152 shorter events, 37.2 us)
Async XLA Ops:
  0.6 144.2 %copy-start = (bf16[2048,64]{0,1:T(8,128)(2,1)S(1)}, bf16[2048,64]{0,1:T(8,128)(2,1)}, u32[]{:S(2)}) copy-start(bf16[2048,64]{0,1:T(8,128)(2,1)} %param.21) | copy-start | bytes 786436
  0.6 19.5 %copy-start.37 = (s32[128,8]{0,1:T(8,128)S(1)}, s32[128,8]{0,1:T(8,128)}, u32[]{:S(2)}) copy-start(s32[128,8]{0,1:T(8,128)} %param.22) | copy-start | bytes 12292
  0.7 128.8 %copy-start.24 = (s32[4]{0:T(128)}, s32[4]{0:T(128)S(1)}, u32[]{:S(2)}) copy-start(s32[4]{0:T(128)S(1)} %pad_add_fusion.here_ref) | copy-start | bytes 52
  7.0 9.6 %copy-start.2 = (bf16[2,2048,128]{2,1,0:T(8,128)(2,1)S(1)}, bf16[2,2048,128]{2,1,0:T(8,128)(2,1)}, u32[]{:S(2)}) copy-start(bf16[2,2048,128]{2,1,0:T(8,128)(2,1)} %gate_hbm) | copy-start | bytes 3145732
  7.0 28.7 %copy-start.5 = (bf16[128,2048]{1,0:T(8,128)(2,1)S(1)}, bf16[128,2048]{1,0:T(8,128)(2,1)}, u32[]{:S(2)}) copy-start(bf16[128,2048]{1,0:T(8,128)(2,1)} %x_ref.1) | copy-start | bytes 1572868
  12.0 17.2 %copy-start.21 = (bf16[128,512]{1,0:T(8,128)(2,1)S(1)}, bf16[128,512]{1,0:T(8,128)(2,1)}, u32[]{:S(2)}) copy-start(bf16[128,512]{1,0:T(8,128)(2,1)} %copy-done.20) | copy-start | bytes 393220
  12.0 17.2 %collective-permute-start.2 = (bf16[128,512]{1,0:T(8,128)(2,1)}, bf16[128,512]{1,0:T(8,128)(2,1)}, u32[]{:S(2)}, u32[]{:S(2)}) collective-permute-start(bf16[128,512]{1,0:T(8,128)(2,1)} %get-tuple-element.33), channel_id=1, source_target_pairs={{0,3},{1,0},{2,1},{3,2},{4,7},{5,4},{6,5},{7,6},{8,11},{9,8},{10,9... | collective-permute-start | bytes 393224 | tf_op jit(solution)/shard_map/ppermute | solution.py:27
  15.6 13.6 %collective-permute-start.1 = (bf16[128,512]{1,0:T(8,128)(2,1)}, bf16[128,512]{1,0:T(8,128)(2,1)}, u32[]{:S(2)}, u32[]{:S(2)}) collective-permute-start(bf16[128,512]{1,0:T(8,128)(2,1)} %get-tuple-element.32), channel_id=1, source_target_pairs={{0,2},{1,3},{2,0},{3,1},{4,6},{5,7},{6,4},{7,5},{8,10},{9,11},{10,... | collective-permute-start | bytes 393224 | tf_op jit(solution)/shard_map/ppermute | solution.py:27
  15.9 13.3 %collective-permute-start = (bf16[128,512]{1,0:T(8,128)(2,1)}, bf16[128,512]{1,0:T(8,128)(2,1)}, u32[]{:S(2)}, u32[]{:S(2)}) collective-permute-start(bf16[128,512]{1,0:T(8,128)(2,1)} %get-tuple-element.31), channel_id=1, source_target_pairs={{0,1},{1,2},{2,3},{3,0},{4,5},{5,6},{6,7},{7,4},{8,9},{9,10},{10,1... | collective-permute-start | bytes 393224 | tf_op jit(solution)/shard_map/ppermute | solution.py:27
  16.6 32.6 %copy-start.3 = (bf16[2,2048,128]{2,1,0:T(8,128)(2,1)S(1)}, bf16[2,2048,128]{2,1,0:T(8,128)(2,1)}, u32[]{:S(2)}) copy-start(bf16[2,2048,128]{2,1,0:T(8,128)(2,1)} %up_hbm) | copy-start | bytes 3145732
  17.4 18.3 %collective-permute-start.4 = (bf16[2048,128]{1,0:T(8,128)(2,1)}, bf16[2048,128]{1,0:T(8,128)(2,1)S(1)}, u32[]{:S(2)}, u32[]{:S(2)}) collective-permute-start(bf16[2048,128]{1,0:T(8,128)(2,1)} %dynamic-slice_bitcast_fusion.1), channel_id=1, source_target_pairs={{0,4},{4,0},{1,5},{5,1},{2,6},{6,2},{3,7},{7,3},{8,12},{12,8},{9,1... | collective-permute-start | bytes 1572872 | tf_op jit(solution)/shard_map/ppermute | solution.py:31
  30.3 5.4 %collective-permute-start.3 = (bf16[128,512]{1,0:T(8,128)(2,1)S(1)}, bf16[128,512]{1,0:T(8,128)(2,1)S(1)}, u32[]{:S(2)}, u32[]{:S(2)}) collective-permute-start(bf16[128,512]{1,0:T(8,128)(2,1)S(1)} %add_convert_fusion.own_ref), channel_id=1, source_target_pairs={{0,4},{4,0},{1,5},{5,1},{2,6},{6,2},{3,7},{7,3},{8,12},{12,8},{9,1... | collective-permute-start | bytes 393224 | tf_op jit(solution)/shard_map/ppermute | solution.py:31
  35.7 26.8 %copy-start.14 = (bf16[2048,128]{1,0:T(8,128)(2,1)}, bf16[2048,128]{1,0:T(8,128)(2,1)S(1)}, u32[]{:S(2)}) copy-start(bf16[2048,128]{1,0:T(8,128)(2,1)S(1)} %collective-permute-done.4.gate_par) | copy-start | bytes 1572868
  37.5 107.6 %copy-start.6 = (bf16[128,512]{1,0:T(8,128)(2,1)}, bf16[128,512]{1,0:T(8,128)(2,1)S(1)}, u32[]{:S(2)}) copy-start(bf16[128,512]{1,0:T(8,128)(2,1)S(1)} %get-tuple-element.38.hidden_ref) | copy-start | bytes 393220
  37.5 34.3 %all-to-all-start = ((bf16[32,20,512]{2,1,0:T(8,128)(2,1)}), bf16[32,20,512]{2,1,0:T(8,128)(2,1)}, u32[]{:S(2)}, u32[]{:S(2)}) async-start(bf16[32,20,512]{2,1,0:T(8,128)(2,1)} %copy-done.9), calls=%async_computation | async-start | bytes 1572864 | tf_op jit(solution)/shard_map/all_to_all | solution.py:360
  50.0 23.1 %collective-permute-start.8 = (bf16[2048,128]{1,0:T(8,128)(2,1)}, bf16[2048,128]{1,0:T(8,128)(2,1)}, u32[]{:S(2)}, u32[]{:S(2)}) collective-permute-start(bf16[2048,128]{1,0:T(8,128)(2,1)} %dynamic-slice_bitcast_fusion), channel_id=1, source_target_pairs={{0,4},{4,0},{1,5},{5,1},{2,6},{6,2},{3,7},{7,3},{8,12},{12,8},{9,1... | collective-permute-start | bytes 1572872 | tf_op jit(solution)/shard_map/ppermute | solution.py:31
  53.9 7.9 %collective-permute-start.14 = (bf16[2,128,512]{2,1,0:T(8,128)(2,1)}, bf16[2,128,512]{2,1,0:T(8,128)(2,1)S(1)}, u32[]{:S(2)}, u32[]{:S(2)}) collective-permute-start(bf16[2,128,512]{2,1,0:T(8,128)(2,1)} %get-tuple-element.63), channel_id=1, source_target_pairs={{0,3},{1,0},{2,1},{3,2},{4,7},{5,4},{6,5},{7,6},{8,11},{9,8},{10,9... | collective-permute-start | bytes 786440 | tf_op jit(solution)/shard_map/ppermute | solution.py:27
  55.9 8.8 %collective-permute-start.13 = (bf16[2,128,512]{2,1,0:T(8,128)(2,1)}, bf16[2,128,512]{2,1,0:T(8,128)(2,1)S(1)}, u32[]{:S(2)}, u32[]{:S(2)}) collective-permute-start(bf16[2,128,512]{2,1,0:T(8,128)(2,1)} %get-tuple-element.61), channel_id=1, source_target_pairs={{0,2},{1,3},{2,0},{3,1},{4,6},{5,7},{6,4},{7,5},{8,10},{9,11},{10,... | collective-permute-start | bytes 786440 | tf_op jit(solution)/shard_map/ppermute | solution.py:27
  57.3 19.9 %collective-permute-start.12 = (bf16[2,128,512]{2,1,0:T(8,128)(2,1)}, bf16[2,128,512]{2,1,0:T(8,128)(2,1)}, u32[]{:S(2)}, u32[]{:S(2)}) collective-permute-start(bf16[2,128,512]{2,1,0:T(8,128)(2,1)} %get-tuple-element.62), channel_id=1, source_target_pairs={{0,1},{1,2},{2,3},{3,0},{4,5},{5,6},{6,7},{7,4},{8,9},{9,10},{10,1... | collective-permute-start | bytes 786440 | tf_op jit(solution)/shard_map/ppermute | solution.py:27
  61.9 42.2 %copy-start.10 = (bf16[2,128,512]{2,1,0:T(8,128)(2,1)}, bf16[2,128,512]{2,1,0:T(8,128)(2,1)S(1)}, u32[]{:S(2)}) copy-start(bf16[2,128,512]{2,1,0:T(8,128)(2,1)S(1)} %collective-permute-done.14.w3) | copy-start | bytes 786436
  73.1 16.4 %collective-permute-start.9 = (bf16[640,512]{1,0:T(8,128)(2,1)S(1)}, bf16[640,512]{1,0:T(8,128)(2,1)S(1)}, u32[]{:S(2)}, u32[]{:S(2)}) collective-permute-start(bf16[640,512]{1,0:T(8,128)(2,1)S(1)} %reshape.57.x0), channel_id=1, source_target_pairs={{0,1},{1,2},{2,3},{3,0},{4,5},{5,6},{6,7},{7,4},{8,9},{9,10},{10,1... | collective-permute-start | bytes 1966088 | tf_op jit(solution)/shard_map/ppermute | solution.py:27
  74.8 29.2 %collective-permute-start.10 = (bf16[640,512]{1,0:T(8,128)(2,1)S(1)}, bf16[640,512]{1,0:T(8,128)(2,1)S(1)}, u32[]{:S(2)}, u32[]{:S(2)}) collective-permute-start(bf16[640,512]{1,0:T(8,128)(2,1)S(1)} %reshape.57.x0), channel_id=1, source_target_pairs={{0,2},{1,3},{2,0},{3,1},{4,6},{5,7},{6,4},{7,5},{8,10},{9,11},{10,... | collective-permute-start | bytes 1966088 | tf_op jit(solution)/shard_map/ppermute | solution.py:27
  76.3 28.3 %collective-permute-start.11 = (bf16[640,512]{1,0:T(8,128)(2,1)S(1)}, bf16[640,512]{1,0:T(8,128)(2,1)S(1)}, u32[]{:S(2)}, u32[]{:S(2)}) collective-permute-start(bf16[640,512]{1,0:T(8,128)(2,1)S(1)} %reshape.57.x0), channel_id=1, source_target_pairs={{0,3},{1,0},{2,1},{3,2},{4,7},{5,4},{6,5},{7,6},{8,11},{9,8},{10,9... | collective-permute-start | bytes 1966088 | tf_op jit(solution)/shard_map/ppermute | solution.py:27
  79.3 30.5 %collective-permute-start.15 = (bf16[4,128,512]{2,1,0:T(8,128)(2,1)S(1)}, bf16[4,128,512]{2,1,0:T(8,128)(2,1)S(1)}, u32[]{:S(2)}, u32[]{:S(2)}) collective-permute-start(bf16[4,128,512]{2,1,0:T(8,128)(2,1)S(1)} %pad_maximum_fusion), channel_id=1, source_target_pairs={{0,4},{4,0},{1,5},{5,1},{2,6},{6,2},{3,7},{7,3},{8,12},{12,8},{9,1... | collective-permute-start | bytes 1572872 | tf_op jit(solution)/shard_map/ppermute | solution.py:31
  110.6 10.4 %collective-permute-start.16 = (bf16[640,256]{1,0:T(8,128)(2,1)S(1)}, bf16[640,256]{1,0:T(8,128)(2,1)S(1)}, u32[]{:S(2)}, u32[]{:S(2)}) collective-permute-start(bf16[640,256]{1,0:T(8,128)(2,1)S(1)} %gate_up.1.a0), channel_id=1, source_target_pairs={{0,1},{1,2},{2,3},{3,0},{4,5},{5,6},{6,7},{7,4},{8,9},{9,10},{10,1... | collective-permute-start | bytes 983048 | tf_op jit(solution)/shard_map/ppermute | solution.py:27
  113.0 16.5 %collective-permute-start.17 = (bf16[640,256]{1,0:T(8,128)(2,1)S(1)}, bf16[640,256]{1,0:T(8,128)(2,1)S(1)}, u32[]{:S(2)}, u32[]{:S(2)}) collective-permute-start(bf16[640,256]{1,0:T(8,128)(2,1)S(1)} %gate_up.1.a0), channel_id=1, source_target_pairs={{0,2},{1,3},{2,0},{3,1},{4,6},{5,7},{6,4},{7,5},{8,10},{9,11},{10,... | collective-permute-start | bytes 983048 | tf_op jit(solution)/shard_map/ppermute | solution.py:27
  115.2 14.3 %collective-permute-start.18 = (bf16[640,256]{1,0:T(8,128)(2,1)S(1)}, bf16[640,256]{1,0:T(8,128)(2,1)S(1)}, u32[]{:S(2)}, u32[]{:S(2)}) collective-permute-start(bf16[640,256]{1,0:T(8,128)(2,1)S(1)} %gate_up.1.a0), channel_id=1, source_target_pairs={{0,3},{1,0},{2,1},{3,2},{4,7},{5,4},{6,5},{7,6},{8,11},{9,8},{10,9... | collective-permute-start | bytes 983048 | tf_op jit(solution)/shard_map/ppermute | solution.py:27
  133.4 34.1 %copy-start.29 = (f32[32,128]{1,0:T(8,128)S(1)}, f32[32,128]{1,0:T(8,128)}, u32[]{:S(2)}) copy-start(f32[32,128]{1,0:T(8,128)} %fusion.20) | copy-start | bytes 49156
  133.4 34.1 %copy-start.40 = (f32[20]{0:T(128)S(1)}, f32[20]{0:T(128)}, u32[]{:S(2)}) copy-start(f32[20]{0:T(128)} %copy-done.39) | copy-start | bytes 244
  137.1 30.4 %all-to-all-start.1 = ((bf16[32,20,512]{2,1,0:T(8,128)(2,1)}), bf16[32,20,512]{2,1,0:T(8,128)(2,1)S(1)}, u32[]{:S(2)}, u32[]{:S(2)}) async-start(bf16[32,20,512]{2,1,0:T(8,128)(2,1)} %down.1), calls=%async_computation.1 | async-start | bytes 1572864 | tf_op jit(solution)/shard_map/all_to_all | solution.py:386
  144.9 45.7 %copy-start.23 = (s32[32,3]{0,1:T(4,128)S(1)}, s32[32,3]{0,1:T(4,128)}, u32[]{:S(2)}) copy-start(s32[32,3]{0,1:T(4,128)} %param.16) | copy-start | bytes 1156
  144.9 46.1 %copy-start.41 = (s32[1,16]{1,0:T(1,128)S(1)}, s32[1,16]{1,0:T(1,128)}, u32[]{:S(2)}) copy-start(s32[1,16]{1,0:T(1,128)} %param.29) | copy-start | bytes 196
  144.9 50.1 %copy-start.38 = (s32[1,1024]{1,0:T(1,128)S(1)}, s32[1,1024]{1,0:T(1,128)}, u32[]{:S(2)}) copy-start(s32[1,1024]{1,0:T(1,128)} %param.28) | copy-start | bytes 12292
  145.2 3.5 %collective-permute-start.7 = (f32[128,128]{0,1:T(8,128)S(1)}, f32[128,128]{0,1:T(8,128)S(1)}, u32[]{:S(2)}, u32[]{:S(2)}) collective-permute-start(f32[128,128]{0,1:T(8,128)S(1)} %pad_maximum_fusion.1), channel_id=1, source_target_pairs={{0,3},{1,0},{2,1},{3,2},{4,7},{5,4},{6,5},{7,6},{8,11},{9,8},{10,9... | collective-permute-start | bytes 196616 | tf_op jit(solution)/shard_map/ppermute | solution.py:27
  147.1 4.8 %collective-permute-start.6 = (f32[128,128]{0,1:T(8,128)S(1)}, f32[128,128]{0,1:T(8,128)S(1)}, u32[]{:S(2)}, u32[]{:S(2)}) collective-permute-start(f32[128,128]{0,1:T(8,128)S(1)} %pad_maximum_fusion.1), channel_id=1, source_target_pairs={{0,2},{1,3},{2,0},{3,1},{4,6},{5,7},{6,4},{7,5},{8,10},{9,11},{10,... | collective-permute-start | bytes 196616 | tf_op jit(solution)/shard_map/ppermute | solution.py:27
  147.8 5.6 %collective-permute-start.5 = (f32[128,128]{0,1:T(8,128)S(1)}, f32[128,128]{0,1:T(8,128)S(1)}, u32[]{:S(2)}, u32[]{:S(2)}) collective-permute-start(f32[128,128]{0,1:T(8,128)S(1)} %pad_maximum_fusion.1), channel_id=1, source_target_pairs={{0,1},{1,2},{2,3},{3,0},{4,5},{5,6},{6,7},{7,4},{8,9},{9,10},{10,1... | collective-permute-start | bytes 196616 | tf_op jit(solution)/shard_map/ppermute | solution.py:27
  168.3 5.4 %collective-permute-start.19 = (bf16[128,512]{1,0:T(8,128)(2,1)S(1)}, bf16[128,512]{1,0:T(8,128)(2,1)S(1)}, u32[]{:S(2)}, u32[]{:S(2)}) collective-permute-start(bf16[128,512]{1,0:T(8,128)(2,1)S(1)} %fusion.1.moe_ref), channel_id=1, source_target_pairs={{0,4},{4,0},{1,5},{5,1},{2,6},{6,2},{3,7},{7,3},{8,12},{12,8},{9,1... | collective-permute-start | bytes 393224 | tf_op jit(solution)/shard_map/ppermute | solution.py:31
  176.4 4.6 %collective-permute-start.20 = (f32[136,128]{1,0:T(8,128)}, f32[136,128]{1,0:T(8,128)S(1)}, u32[]{:S(2)}, u32[]{:S(2)}) collective-permute-start(f32[136,128]{1,0:T(8,128)} %get-tuple-element.46.p0), channel_id=1, source_target_pairs={{0,1},{1,2},{2,3},{3,0},{4,5},{5,6},{6,7},{7,4},{8,9},{9,10},{10,1... | collective-permute-start | bytes 208904 | tf_op jit(solution)/shard_map/ppermute | solution.py:27
  177.2 4.9 %collective-permute-start.21 = (f32[136,128]{1,0:T(8,128)}, f32[136,128]{1,0:T(8,128)S(1)}, u32[]{:S(2)}, u32[]{:S(2)}) collective-permute-start(f32[136,128]{1,0:T(8,128)} %get-tuple-element.46.p0), channel_id=1, source_target_pairs={{0,2},{1,3},{2,0},{3,1},{4,6},{5,7},{6,4},{7,5},{8,10},{9,11},{10,... | collective-permute-start | bytes 208904 | tf_op jit(solution)/shard_map/ppermute | solution.py:27
  179.4 3.4 %collective-permute-start.22 = (f32[136,128]{1,0:T(8,128)}, f32[136,128]{1,0:T(8,128)S(1)}, u32[]{:S(2)}, u32[]{:S(2)}) collective-permute-start(f32[136,128]{1,0:T(8,128)} %get-tuple-element.46.p0), channel_id=1, source_target_pairs={{0,3},{1,0},{2,1},{3,2},{4,7},{5,4},{6,5},{7,6},{8,11},{9,8},{10,9... | collective-permute-start | bytes 208904 | tf_op jit(solution)/shard_map/ppermute | solution.py:27
  185.4 19.1 %all-to-all-start.2 = ((bf16[16,128,128]{2,1,0:T(8,128)(2,1)}), bf16[16,128,128]{2,1,0:T(8,128)(2,1)S(1)}, u32[]{:S(2)}, u32[]{:S(2)}) async-start(bf16[16,128,128]{2,1,0:T(8,128)(2,1)} %vectors.1), calls=%async_computation.2 | async-start | bytes 1048576 | tf_op jit(solution)/shard_map/all_to_all | solution.py:438
  191.1 6.9 %collective-permute-start.23 = (bf16[128,512]{1,0:T(8,128)(2,1)}, bf16[128,512]{1,0:T(8,128)(2,1)S(1)}, u32[]{:S(2)}, u32[]{:S(2)}) collective-permute-start(bf16[128,512]{1,0:T(8,128)(2,1)} %get-tuple-element.50.p0), channel_id=1, source_target_pairs={{0,1},{1,2},{2,3},{3,0},{4,5},{5,6},{6,7},{7,4},{8,9},{9,10},{10,1... | collective-permute-start | bytes 393224 | tf_op jit(solution)/shard_map/ppermute | solution.py:27
  191.4 6.6 %collective-permute-start.24 = (bf16[128,512]{1,0:T(8,128)(2,1)}, bf16[128,512]{1,0:T(8,128)(2,1)S(1)}, u32[]{:S(2)}, u32[]{:S(2)}) collective-permute-start(bf16[128,512]{1,0:T(8,128)(2,1)} %get-tuple-element.50.p0), channel_id=1, source_target_pairs={{0,2},{1,3},{2,0},{3,1},{4,6},{5,7},{6,4},{7,5},{8,10},{9,11},{10,... | collective-permute-start | bytes 393224 | tf_op jit(solution)/shard_map/ppermute | solution.py:27
  193.8 5.1 %collective-permute-start.25 = (bf16[128,512]{1,0:T(8,128)(2,1)}, bf16[128,512]{1,0:T(8,128)(2,1)S(1)}, u32[]{:S(2)}, u32[]{:S(2)}) collective-permute-start(bf16[128,512]{1,0:T(8,128)(2,1)} %get-tuple-element.50.p0), channel_id=1, source_target_pairs={{0,3},{1,0},{2,1},{3,2},{4,7},{5,4},{6,5},{7,6},{8,11},{9,8},{10,9... | collective-permute-start | bytes 393224 | tf_op jit(solution)/shard_map/ppermute | solution.py:27
  198.0 10.9 %copy-start.31 = (bf16[128,512]{1,0:T(8,128)(2,1)}, bf16[128,512]{1,0:T(8,128)(2,1)S(1)}, u32[]{:S(2)}) copy-start(bf16[128,512]{1,0:T(8,128)(2,1)S(1)} %collective-permute-done.23.p1) | copy-start | bytes 393220
  198.0 10.9 %copy-start.32 = (bf16[128,512]{1,0:T(8,128)(2,1)}, bf16[128,512]{1,0:T(8,128)(2,1)S(1)}, u32[]{:S(2)}) copy-start(bf16[128,512]{1,0:T(8,128)(2,1)S(1)} %collective-permute-done.24.p2) | copy-start | bytes 393220
  198.9 10.1 %copy-start.33 = (bf16[128,512]{1,0:T(8,128)(2,1)}, bf16[128,512]{1,0:T(8,128)(2,1)S(1)}, u32[]{:S(2)}) copy-start(bf16[128,512]{1,0:T(8,128)(2,1)S(1)} %collective-permute-done.25.p3) | copy-start | bytes 393220
  204.5 6.4 %collective-permute-start.26 = (bf16[2048,128]{1,0:T(8,128)(2,1)S(1)}, bf16[2048,128]{1,0:T(8,128)(2,1)S(1)}, u32[]{:S(2)}, u32[]{:S(2)}) collective-permute-start(bf16[2048,128]{1,0:T(8,128)(2,1)S(1)} %bitcast.37), channel_id=1, source_target_pairs={{0,8},{8,0},{1,9},{9,1},{2,10},{10,2},{3,11},{11,3},{4,12},{12,4},... | collective-permute-start | bytes 1572872 | tf_op jit(solution)/shard_map/ppermute | solution.py:452
  (24 other events, 36.9 us)

commit v4 on v3

--- a/solution.py
+++ b/solution.py
@@ -13,7 +13,7 @@
 CAP = 20
 EXPERTS = 64
 WIDE = 32
-GROUPS = ((0, 20),)
+GROUPS = ((0, 8), (8, 20))
 EPS = 1e-06
 THETA = 50000.0
 NEG = -1e30
@@ -109,18 +109,39 @@
         out_ref[...] = jnp.dot(mixed, out_w_ref[:, columns], preferred_element_type=f32).astype(bf16)
 
 
-def dispatch_kernel(here_ref, x_ref, own_ref, par_ref, choose_ref, hidden_ref, *rows_refs):
+def choose_kernel(here_ref, routes_ref, *out_refs):
+    expert = 2 * lax.broadcasted_iota(jnp.int32, (WIDE, TOK), 0) + here_ref[0]
+    hit = jnp.zeros((WIDE, TOK), f32)
+    for k in range(TOPK):
+        hit = hit + (routes_ref[k : k + 1, :] == expert).astype(f32)
+    sooner = lax.broadcasted_iota(jnp.int32, (TOK, TOK), 0)
+    earlier = (sooner < lax.broadcasted_iota(jnp.int32, (TOK, TOK), 1)).astype(f32).astype(bf16)
+    before = jnp.dot(hit.astype(bf16), earlier, preferred_element_type=f32)
+    place = jnp.where(hit > 0, before, -1.0).astype(bf16)
+    for (a, b), out_ref in zip(GROUPS, out_refs):
+        size = b - a
+        owner = size * lax.broadcasted_iota(jnp.int32, (WIDE * size, WIDE), 1)
+        offset = lax.broadcasted_iota(jnp.int32, (WIDE * size, WIDE), 0) - owner
+        inside = (offset >= 0) & (offset < size)
+        spread = jnp.dot(
+            inside.astype(f32).astype(bf16), place, preferred_element_type=f32
+        )
+        slot = jnp.sum(jnp.where(inside, offset + a, 0).astype(f32), axis=1, keepdims=True)
+        out_ref[...] = (spread == slot).astype(f32).astype(bf16)
+
+
+def dispatch_kernel(here_ref, x_ref, own_ref, par_ref, *refs):
+    chooses = refs[: len(GROUPS)]
+    hidden_ref = refs[len(GROUPS)]
     j = here_ref[1]
     mine = x_ref[:, pl.ds(pl.multiple_of(j * 512, 512), 512)].astype(f32)
     hidden = (mine + (own_ref[...].astype(f32) + par_ref[...].astype(f32))).astype(bf16)
     hidden_ref[...] = hidden
-    rows = jnp.dot(choose_ref[...], hidden, preferred_element_type=f32)
-    at = 0
-    for rows_ref in rows_refs:
+    for choose_ref, rows_ref in zip(chooses, refs[len(GROUPS) + 1 :]):
+        rows = jnp.dot(choose_ref[...], hidden, preferred_element_type=f32)
         size = rows_ref.shape[1]
         for s in range(WIDE):
-            rows_ref[s] = rows[at : at + size].astype(bf16)
-            at += size
+            rows_ref[s] = rows[s * size : (s + 1) * size].astype(bf16)
 
 
 def gate_up_kernel(
@@ -259,7 +280,7 @@
 
 
 def hbm():
-    return pl.BlockSpec(memory_space=pl.ANY)
+    return pl.BlockSpec(memory_space=pltpu.HBM)
 
 
 def params():
@@ -332,12 +353,17 @@
     before = jnp.dot(hit.astype(bf16), earlier, preferred_element_type=f32)
     slot = jnp.arange(CAP, dtype=jnp.int32).astype(f32)
     chosen = (before[:, None, :] == slot[None, :, None]) & (hit[:, None, :] > 0)
-    choose = jnp.concatenate(
-        [chosen[:, a:b].astype(bf16).reshape(WIDE * (b - a), TOK) for a, b in GROUPS], axis=0
-    )
+    chooses = pl.pallas_call(
+        choose_kernel,
+        out_shape=tuple(jax.ShapeDtypeStruct((WIDE * (b - a), TOK), bf16) for a, b in GROUPS),
+        in_specs=[smem(), vmem()],
+        out_specs=(vmem(),) * len(GROUPS),
+        compiler_params=params(),
+        name="choose",
+    )(here, routes.T)
 
     attn = (own_part.astype(f32) + sum(p.astype(f32) for p in attn_parts)).astype(bf16)
-    attn, choose = lax.optimization_barrier((attn, choose))
+    attn, *chooses = lax.optimization_barrier((attn, *chooses))
     attn_par = x_swap(attn)
     attn_par, gate_par = lax.optimization_barrier((attn_par, gate_par))
     hidden, *rows = pl.pallas_call(
@@ -346,11 +372,11 @@
             jax.ShapeDtypeStruct((TOK, 512), bf16),
             *(jax.ShapeDtypeStruct((WIDE, b - a, 512), bf16) for a, b in GROUPS),
         ),
-        in_specs=[smem()] + [vmem()] * 4,
+        in_specs=[smem()] + [vmem()] * (3 + len(GROUPS)),
         out_specs=(vmem(),) * (1 + len(GROUPS)),
         compiler_params=params(),
         name="dispatch",
-    )(here, tokens, attn, attn_par, choose)
+    )(here, tokens, attn, attn_par, *chooses)
 
     backs = []
     arrived = []

time: 217 us -> 229 us (1.055)
  starting transfers between devices: 64.9 us -> 84.2 us
  waiting for transfers between devices: 88 us -> 74.3 us
  local copies, waits for them, and re-layouts: 33.6 us -> 26.6 us
  Pallas kernels: 21.5 us -> 28.4 us
  matrix products: 1.67 us -> 5.52 us
  other arithmetic: 4.18 us -> 6.53 us
    ppermute x21 -> x27, waiting for transfers between devices: 54 us -> 35.7 us  [y_shift(): return lax.ppermute(x, 'y', [(s, (s + k) % 4) for s in range(4)])]
    all_to_all x1 -> x2, starting transfers between devices: 7.75 us -> 19 us  [body(): backs.append(lax.all_to_all(out, W, 0, 0, tiled=True))]
    ppermute x5, waiting for transfers between devices: 8.18 us -> 15.3 us  [x_swap(): return lax.ppermute(x, 'xh', [(0, 1), (1, 0)])]
    all_to_all x1 -> x2, starting transfers between devices: 11.6 us -> 17.4 us  [body(): arrived.append(lax.all_to_all(group, W, 0, 0, tiled=True))]
    eq x4 -> x0, local copies, waits for them, and re-layouts: 4.68 us -> none  [body(): chosen = (before[:, None, :] == slot[None, :, None]) & (hit[:, None, :] > 0)]
    pallas_call x1 -> x2, Pallas kernels: 3.32 us -> 6.91 us  [body(): pl.pallas_call(gate_up_kernel, out_shape=jax.ShapeDtypeStruct((WIDE * siz...]
    pallas_call x1 -> x2, Pallas kernels: 3.68 us -> 6.18 us  [body(): pl.pallas_call(down_kernel, out_shape=jax.ShapeDtypeStruct((WIDE, size, 5...]
    dot_general x2 -> x4, matrix products: 0.76 us -> 3.23 us  [body(): lax.dot_general(matrix, back, contract, preferred_element_type=f32)]
  transfers between devices with their start and end apart: 30 -> 38, of which waited for: 20 -> 18; matrix products, arithmetic and copies ran while one was open for 10% -> 9% of each run, Pallas kernels for 2% -> 7%
where the time goes in v4:
time: 229 us; the launch traced here: 227 us
  starting transfers between devices  84.2 us (37%)
  waiting for transfers between devices  74.3 us (32%)
  Pallas kernels  28.4 us (12%)
  local copies, waits for them, and re-layouts  26.6 us (12%)
  other arithmetic  6.53 us (3%)
  matrix products  5.52 us (2%)
    ppermute x27, waiting for transfers between devices, y_shift(): return lax.ppermute(x, 'y', [(s, (s + k) % 4) for s in range(4)])  35.7 us
    ppermute x27, starting transfers between devices, y_shift(): return lax.ppermute(x, 'y', [(s, (s + k) % 4) for s in range(4)])  27.5 us
    all_to_all x2, starting transfers between devices, body(): backs.append(lax.all_to_all(out, W, 0, 0, tiled=True))  19 us
    all_to_all x2, starting transfers between devices, body(): arrived.append(lax.all_to_all(group, W, 0, 0, tiled=True))  17.4 us
    all_to_all x2, waiting for transfers between devices, body(): backs.append(lax.all_to_all(out, W, 0, 0, tiled=True))  15.4 us
    ppermute x5, waiting for transfers between devices, x_swap(): return lax.ppermute(x, 'xh', [(0, 1), (1, 0)])  15.3 us
    unnamed x71, local copies, waits for them, and re-layouts  15.1 us
    ppermute x5, starting transfers between devices, x_swap(): return lax.ppermute(x, 'xh', [(0, 1), (1, 0)])  10.8 us
  transfers between devices with their start and end apart: 38, of which 18 were waited for; matrix products, arithmetic and copies ran while one was open for 9% of the time, Pallas kernels for 7%

profile of v4, /device:TPU:1, one launch (start us, length us, event | category | flops | bytes accessed | tf_op | source)
XLA Modules:
  0.0 226.9 jit_solution(5557019425968790530)
XLA Ops:
  0.8 2.0 copy-done.3
  7.2 4.3 %attention.1 = (bf16[128,512]{1,0:T(8,128)(2,1)S(1)}, bf16[128,512]{1,0:T(8,128)(2,1)S(1)}, bf16[128,512]{1,0:T(8,128)(2,1)}, bf16[128,512]{1,0:T(8,128)(2,1)}) custom-call(s32[4]{0:T(128)S(1)} %pad_add_fusion.here_ref, s32[3,32]{1,0:T(4,128)S(1)} %bitcast.45, f32[2,256]{1,0:T(2,128)S(1)} %copy-done.19, f32[3,2048]{1,0:T(4,128)S(1)} %copy-done.10, ...), custom_call_target="tpu_custom_call" | custom-call | tf_op jit(solution)/shard_map/attention/pallas_call | solution.py:319
  11.5 2.2 collective-permute-start
  13.7 2.6 %collective-permute-start.1 = (bf16[128,512]{1,0:T(8,128)(2,1)}, bf16[128,512]{1,0:T(8,128)(2,1)}, u32[]{:S(2)}, u32[]{:S(2)}) collective-permute-start(bf16[128,512]{1,0:T(8,128)(2,1)} %get-tuple-element.38), channel_id=1, source_target_pairs={{0,2},{1,3},{2,0},{3,1},{4,6},{5,7},{6,4},{7,5},{8,10},{9,11},{10,... | collective-permute-start | bytes 393224 | tf_op jit(solution)/shard_map/ppermute | solution.py:27
  18.2 2.7 %collective-permute-start.8 = (bf16[2048,128]{1,0:T(8,128)(2,1)}, bf16[2048,128]{1,0:T(8,128)(2,1)S(1)}, u32[]{:S(2)}, u32[]{:S(2)}) collective-permute-start(bf16[2048,128]{1,0:T(8,128)(2,1)} %dynamic-slice_bitcast_fusion), channel_id=1, source_target_pairs={{0,4},{4,0},{1,5},{5,1},{2,6},{6,2},{3,7},{7,3},{8,12},{12,8},{9,1... | collective-permute-start | bytes 1572872 | tf_op jit(solution)/shard_map/ppermute | solution.py:31
  22.0 2.2 constant_dynamic-slice_fusion.2
  25.7 2.2 collective-permute-start.13
  29.0 2.8 %collective-permute-start.3 = (bf16[128,512]{1,0:T(8,128)(2,1)S(1)}, bf16[128,512]{1,0:T(8,128)(2,1)S(1)}, u32[]{:S(2)}, u32[]{:S(2)}) collective-permute-start(bf16[128,512]{1,0:T(8,128)(2,1)S(1)} %add_convert_fusion.own_ref), channel_id=1, source_target_pairs={{0,4},{4,0},{1,5},{5,1},{2,6},{6,2},{3,7},{7,3},{8,12},{12,8},{9,1... | collective-permute-start | bytes 393224 | tf_op jit(solution)/shard_map/ppermute | solution.py:31
  31.8 1.7 constant_dynamic-slice_fusion.7
  33.5 12.5 %collective-permute-done.3.par_ref = bf16[128,512]{1,0:T(8,128)(2,1)S(1)} collective-permute-done((bf16[128,512]{1,0:T(8,128)(2,1)S(1)}, bf16[128,512]{1,0:T(8,128)(2,1)S(1)}, u32[]{:S(2)}, u32[]{:S(2)}) %collective-permute-start.3) | collective-permute-done | bytes 131104 | tf_op jit(solution)/shard_map/ppermute | solution.py:31
  49.8 12.2 %all-to-all-start = ((bf16[32,8,512]{2,1,0:T(8,128)(2,1)}), bf16[32,8,512]{2,1,0:T(8,128)(2,1)}, u32[]{:S(2)}, u32[]{:S(2)}) async-start(bf16[32,8,512]{2,1,0:T(8,128)(2,1)} %copy-done.14), calls=%async_computation | async-start | bytes 524288 | tf_op jit(solution)/shard_map/all_to_all | solution.py:386
  64.6 1.8 pad_maximum_fusion
  66.4 2.5 %collective-permute-start.15 = (bf16[4,128,512]{2,1,0:T(8,128)(2,1)}, bf16[4,128,512]{2,1,0:T(8,128)(2,1)}, u32[]{:S(2)}, u32[]{:S(2)}) collective-permute-start(bf16[4,128,512]{2,1,0:T(8,128)(2,1)} %pad_maximum_fusion), channel_id=1, source_target_pairs={{0,4},{4,0},{1,5},{5,1},{2,6},{6,2},{3,7},{7,3},{8,12},{12,8},{9,1... | collective-permute-start | bytes 1572872 | tf_op jit(solution)/shard_map/ppermute | solution.py:31
  68.9 4.7 %all-to-all-done = bf16[32,8,512]{2,1,0:T(8,128)(2,1)} async-done(((bf16[32,8,512]{2,1,0:T(8,128)(2,1)}), bf16[32,8,512]{2,1,0:T(8,128)(2,1)}, u32[]{:S(2)}, u32[]{:S(2)}) %all-to-all-start) | async-done | bytes 262176 | tf_op jit(solution)/shard_map/all_to_all | solution.py:386
  73.5 5.2 %all-to-all-start.2 = ((bf16[32,12,512]{2,1,0:T(8,128)(2,1)}), bf16[32,12,512]{2,1,0:T(8,128)(2,1)}, u32[]{:S(2)}, u32[]{:S(2)}) async-start(bf16[32,12,512]{2,1,0:T(8,128)(2,1)} %copy-done.13), calls=%async_computation.2 | async-start | bytes 1048576 | tf_op jit(solution)/shard_map/all_to_all | solution.py:386
  79.5 2.3 %collective-permute-start.11 = (bf16[256,512]{1,0:T(8,128)(2,1)}, bf16[256,512]{1,0:T(8,128)(2,1)S(1)}, u32[]{:S(2)}, u32[]{:S(2)}) collective-permute-start(bf16[256,512]{1,0:T(8,128)(2,1)} %bitcast.13.x0), channel_id=1, source_target_pairs={{0,3},{1,0},{2,1},{3,2},{4,7},{5,4},{6,5},{7,6},{8,11},{9,8},{10,9... | collective-permute-start | bytes 786440 | tf_op jit(solution)/shard_map/ppermute | solution.py:27
  83.3 4.6 %collective-permute-done.11.x3 = bf16[256,512]{1,0:T(8,128)(2,1)S(1)} collective-permute-done((bf16[256,512]{1,0:T(8,128)(2,1)}, bf16[256,512]{1,0:T(8,128)(2,1)S(1)}, u32[]{:S(2)}, u32[]{:S(2)}) %collective-permute-start.11) | collective-permute-done | bytes 262176 | tf_op jit(solution)/shard_map/ppermute | solution.py:27
  87.9 2.9 %collective-permute-done.10.x2 = bf16[256,512]{1,0:T(8,128)(2,1)S(1)} collective-permute-done((bf16[256,512]{1,0:T(8,128)(2,1)}, bf16[256,512]{1,0:T(8,128)(2,1)S(1)}, u32[]{:S(2)}, u32[]{:S(2)}) %collective-permute-start.10) | collective-permute-done | bytes 262176 | tf_op jit(solution)/shard_map/ppermute | solution.py:27
  90.8 6.0 %collective-permute-done.9.x1 = bf16[256,512]{1,0:T(8,128)(2,1)S(1)} collective-permute-done((bf16[256,512]{1,0:T(8,128)(2,1)}, bf16[256,512]{1,0:T(8,128)(2,1)S(1)}, u32[]{:S(2)}, u32[]{:S(2)}) %collective-permute-start.9) | collective-permute-done | bytes 262176 | tf_op jit(solution)/shard_map/ppermute | solution.py:27
  97.5 3.5 %gate_up.2.a0 = bf16[256,256]{1,0:T(8,128)(2,1)} custom-call(s32[4]{0:T(128)S(1)} %pad_add_fusion.here_ref, bf16[256,512]{1,0:T(8,128)(2,1)} %bitcast.13.x0, bf16[256,512]{1,0:T(8,128)(2,1)S(1)} %collective-permute-done.9.x1, bf16[256,512]{1,0:T(8,128)(2,1)S(1)} %collective-permute-done.10.x2, bf16[256,512]{1,0:T(8,128)(2,1)S(1)} %collective-permute-done.11.x3, ...), custom_call_target="tpu_custom_call" | custom-call | tf_op jit(solution)/shard_map/gate_up/pallas_call | solution.py:392
  104.8 1.9 reshape.57.x0
  106.7 2.3 %collective-permute-start.21 = (bf16[384,512]{1,0:T(8,128)(2,1)}, bf16[384,512]{1,0:T(8,128)(2,1)}, u32[]{:S(2)}, u32[]{:S(2)}) collective-permute-start(bf16[384,512]{1,0:T(8,128)(2,1)} %reshape.57.x0), channel_id=1, source_target_pairs={{0,3},{1,0},{2,1},{3,2},{4,7},{5,4},{6,5},{7,6},{8,11},{9,8},{10,9... | collective-permute-start | bytes 1179656 | tf_op jit(solution)/shard_map/ppermute | solution.py:27
  112.5 2.9 %down.2 = bf16[32,8,512]{2,1,0:T(8,128)(2,1)S(1)} custom-call(s32[4]{0:T(128)S(1)} %pad_add_fusion.here_ref, bf16[256,256]{1,0:T(8,128)(2,1)} %gate_up.2.a0, bf16[256,256]{1,0:T(8,128)(2,1)} %collective-permute-done.16.a1, bf16[256,256]{1,0:T(8,128)(2,1)} %collective-permute-done.17.a2, bf16[256,256]{1,0:T(8,128)(2,1)} %collective-permute-done.18.a3, ...), custom_call_target="tpu_custom_call" | custom-call | tf_op jit(solution)/shard_map/down/pallas_call | solution.py:403
  116.1 10.5 %all-to-all-start.1 = ((bf16[32,8,512]{2,1,0:T(8,128)(2,1)}), bf16[32,8,512]{2,1,0:T(8,128)(2,1)}, u32[]{:S(2)}, u32[]{:S(2)}) async-start(bf16[32,8,512]{2,1,0:T(8,128)(2,1)} %copy-done.8), calls=%async_computation.1 | async-start | bytes 524288 | tf_op jit(solution)/shard_map/all_to_all | solution.py:412
  128.2 2.1 collective-permute-start.7
  132.5 3.4 %gate_up.3.a0 = bf16[384,256]{1,0:T(8,128)(2,1)S(1)} custom-call(s32[4]{0:T(128)S(1)} %pad_add_fusion.here_ref, bf16[384,512]{1,0:T(8,128)(2,1)S(1)} %copy-done.6, bf16[384,512]{1,0:T(8,128)(2,1)} %collective-permute-done.19.x1, bf16[384,512]{1,0:T(8,128)(2,1)} %collective-permute-done.20.x2, bf16[384,512]{1,0:T(8,128)(2,1)} %collective-permute-done.21.x3, ...), custom_call_target="tpu_custom_call" | custom-call | tf_op jit(solution)/shard_map/gate_up/pallas_call | solution.py:392
  135.9 2.3 %collective-permute-start.24 = (bf16[384,256]{1,0:T(8,128)(2,1)S(1)}, bf16[384,256]{1,0:T(8,128)(2,1)S(1)}, u32[]{:S(2)}, u32[]{:S(2)}) collective-permute-start(bf16[384,256]{1,0:T(8,128)(2,1)S(1)} %gate_up.3.a0), channel_id=1, source_target_pairs={{0,3},{1,0},{2,1},{3,2},{4,7},{5,4},{6,5},{7,6},{8,11},{9,8},{10,9... | collective-permute-start | bytes 589832 | tf_op jit(solution)/shard_map/ppermute | solution.py:27
  139.0 3.0 %collective-permute-done.24.a3 = bf16[384,256]{1,0:T(8,128)(2,1)S(1)} collective-permute-done((bf16[384,256]{1,0:T(8,128)(2,1)S(1)}, bf16[384,256]{1,0:T(8,128)(2,1)S(1)}, u32[]{:S(2)}, u32[]{:S(2)}) %collective-permute-start.24) | collective-permute-done | bytes 196640 | tf_op jit(solution)/shard_map/ppermute | solution.py:27
  142.0 2.9 %collective-permute-done.23.a2 = bf16[384,256]{1,0:T(8,128)(2,1)S(1)} collective-permute-done((bf16[384,256]{1,0:T(8,128)(2,1)S(1)}, bf16[384,256]{1,0:T(8,128)(2,1)S(1)}, u32[]{:S(2)}, u32[]{:S(2)}) %collective-permute-start.23) | collective-permute-done | bytes 196640 | tf_op jit(solution)/shard_map/ppermute | solution.py:27
  144.8 5.9 %collective-permute-done.22.a1 = bf16[384,256]{1,0:T(8,128)(2,1)S(1)} collective-permute-done((bf16[384,256]{1,0:T(8,128)(2,1)S(1)}, bf16[384,256]{1,0:T(8,128)(2,1)S(1)}, u32[]{:S(2)}, u32[]{:S(2)}) %collective-permute-start.22) | collective-permute-done | bytes 196640 | tf_op jit(solution)/shard_map/ppermute | solution.py:27
  150.7 3.3 %down.3 = bf16[32,12,512]{2,1,0:T(8,128)(2,1)} custom-call(s32[4]{0:T(128)S(1)} %pad_add_fusion.here_ref, bf16[384,256]{1,0:T(8,128)(2,1)S(1)} %gate_up.3.a0, bf16[384,256]{1,0:T(8,128)(2,1)S(1)} %collective-permute-done.22.a1, bf16[384,256]{1,0:T(8,128)(2,1)S(1)} %collective-permute-done.23.a2, bf16[384,256]{1,0:T(8,128)(2,1)S(1)} %collective-permute-done.24.a3, ...), custom_call_target="tpu_custom_call" | custom-call | tf_op jit(solution)/shard_map/down/pallas_call | solution.py:403
  154.0 8.4 %all-to-all-start.3 = ((bf16[32,12,512]{2,1,0:T(8,128)(2,1)}), bf16[32,12,512]{2,1,0:T(8,128)(2,1)S(1)}, u32[]{:S(2)}, u32[]{:S(2)}) async-start(bf16[32,12,512]{2,1,0:T(8,128)(2,1)} %down.3), calls=%async_computation.3 | async-start | bytes 1048576 | tf_op jit(solution)/shard_map/all_to_all | solution.py:412
  163.8 15.4 %all-to-all-done.3 = bf16[32,12,512]{2,1,0:T(8,128)(2,1)S(1)} async-done(((bf16[32,12,512]{2,1,0:T(8,128)(2,1)}), bf16[32,12,512]{2,1,0:T(8,128)(2,1)S(1)}, u32[]{:S(2)}, u32[]{:S(2)}) %all-to-all-start.3) | async-done | bytes 393248 | tf_op jit(solution)/shard_map/all_to_all | solution.py:412
  181.3 2.5 %collective-permute-start.25 = (bf16[128,512]{1,0:T(8,128)(2,1)S(1)}, bf16[128,512]{1,0:T(8,128)(2,1)S(1)}, u32[]{:S(2)}, u32[]{:S(2)}) collective-permute-start(bf16[128,512]{1,0:T(8,128)(2,1)S(1)} %fusion.3.moe_ref), channel_id=1, source_target_pairs={{0,4},{4,0},{1,5},{5,1},{2,6},{6,2},{3,7},{7,3},{8,12},{12,8},{9,1... | collective-permute-start | bytes 393224 | tf_op jit(solution)/shard_map/ppermute | solution.py:31
  183.8 2.9 %collective-permute-done.25.par_ref = bf16[128,512]{1,0:T(8,128)(2,1)S(1)} collective-permute-done((bf16[128,512]{1,0:T(8,128)(2,1)S(1)}, bf16[128,512]{1,0:T(8,128)(2,1)S(1)}, u32[]{:S(2)}, u32[]{:S(2)}) %collective-permute-start.25) | collective-permute-done | bytes 131104 | tf_op jit(solution)/shard_map/ppermute | solution.py:31
  187.3 2.1 embed.1
  190.9 1.9 collective-permute-done.28.p3
  192.8 1.9 collective-permute-done.27.p2
  196.1 2.0 vectors.1
  198.1 4.4 %all-to-all-start.4 = ((bf16[16,128,128]{2,1,0:T(8,128)(2,1)}), bf16[16,128,128]{2,1,0:T(8,128)(2,1)S(1)}, u32[]{:S(2)}, u32[]{:S(2)}) async-start(bf16[16,128,128]{2,1,0:T(8,128)(2,1)} %vectors.1), calls=%async_computation.4 | async-start | bytes 1048576 | tf_op jit(solution)/shard_map/all_to_all | solution.py:464
  203.0 2.3 collective-permute-start.31
  206.9 2.1 collective-permute-done.31.p3
  208.9 2.0 collective-permute-done.30.p2
  210.9 1.4 collective-permute-done.29.p1
  212.3 3.3 %all-to-all-done.4 = bf16[16,128,128]{2,1,0:T(8,128)(2,1)S(1)} async-done(((bf16[16,128,128]{2,1,0:T(8,128)(2,1)}), bf16[16,128,128]{2,1,0:T(8,128)(2,1)S(1)}, u32[]{:S(2)}, u32[]{:S(2)}) %all-to-all-start.4) | async-done | bytes 524320 | tf_op jit(solution)/shard_map/all_to_all | solution.py:464
  215.6 5.1 %collective-permute-start.32 = (bf16[2048,128]{1,0:T(8,128)(2,1)S(1)}, bf16[2048,128]{1,0:T(8,128)(2,1)S(1)}, u32[]{:S(2)}, u32[]{:S(2)}) collective-permute-start(bf16[2048,128]{1,0:T(8,128)(2,1)S(1)} %bitcast.46), channel_id=1, source_target_pairs={{0,8},{8,0},{1,9},{9,1},{2,10},{10,2},{3,11},{11,3},{4,12},{12,4},... | collective-permute-start | bytes 1572872 | tf_op jit(solution)/shard_map/ppermute | solution.py:478
  220.7 1.9 assemble.1
  223.5 3.2 %score.1 = f32[1,16]{1,0:T(1,128)} custom-call(s32[5,16]{1,0:T(8,128)} %stack.48.info_ref, bf16[1024,128]{1,0:T(8,128)(2,1)} %doc_ref.1, bf16[2048,128]{1,0:T(8,128)(2,1)} %bitcast.47, bf16[2048,128]{1,0:T(8,128)(2,1)} %copy-done.21), custom_call_target="tpu_custom_call" | custom-call | tf_op jit(solution)/shard_map/score/pallas_call | solution.py:486
  (153 shorter events, 41.6 us)
Async XLA Ops:
  0.6 110.4 %copy-start = (bf16[2048,64]{0,1:T(8,128)(2,1)S(1)}, bf16[2048,64]{0,1:T(8,128)(2,1)}, u32[]{:S(2)}) copy-start(bf16[2048,64]{0,1:T(8,128)(2,1)} %param.21) | copy-start | bytes 786436
  0.6 16.7 %copy-start.2 = (bf16[2,2048,128]{2,1,0:T(8,128)(2,1)S(1)}, bf16[2,2048,128]{2,1,0:T(8,128)(2,1)}, u32[]{:S(2)}) copy-start(bf16[2,2048,128]{2,1,0:T(8,128)(2,1)} %up_hbm.1) | copy-start | bytes 3145732
  0.7 20.3 %copy-start.1 = (bf16[2,2048,128]{2,1,0:T(8,128)(2,1)S(1)}, bf16[2,2048,128]{2,1,0:T(8,128)(2,1)}, u32[]{:S(2)}) copy-start(bf16[2,2048,128]{2,1,0:T(8,128)(2,1)} %gate_hbm.1) | copy-start | bytes 3145732
  0.8 150.0 %copy-start.15 = (s32[4]{0:T(128)}, s32[4]{0:T(128)S(1)}, u32[]{:S(2)}) copy-start(s32[4]{0:T(128)S(1)} %pad_add_fusion.here_ref) | copy-start | bytes 52
  11.5 12.7 %copy-start.16 = (s32[128,8]{0,1:T(8,128)S(1)}, s32[128,8]{0,1:T(8,128)}, u32[]{:S(2)}) copy-start(s32[128,8]{0,1:T(8,128)} %param.22) | copy-start | bytes 12292
  11.5 13.6 %collective-permute-start = (bf16[128,512]{1,0:T(8,128)(2,1)S(1)}, bf16[128,512]{1,0:T(8,128)(2,1)S(1)}, u32[]{:S(2)}, u32[]{:S(2)}) collective-permute-start(bf16[128,512]{1,0:T(8,128)(2,1)S(1)} %get-tuple-element.37), channel_id=1, source_target_pairs={{0,1},{1,2},{2,3},{3,0},{4,5},{5,6},{6,7},{7,4},{8,9},{9,10},{10,1... | collective-permute-start | bytes 393224 | tf_op jit(solution)/shard_map/ppermute | solution.py:27
  13.7 12.0 %collective-permute-start.1 = (bf16[128,512]{1,0:T(8,128)(2,1)}, bf16[128,512]{1,0:T(8,128)(2,1)}, u32[]{:S(2)}, u32[]{:S(2)}) collective-permute-start(bf16[128,512]{1,0:T(8,128)(2,1)} %get-tuple-element.38), channel_id=1, source_target_pairs={{0,2},{1,3},{2,0},{3,1},{4,6},{5,7},{6,4},{7,5},{8,10},{9,11},{10,... | collective-permute-start | bytes 393224 | tf_op jit(solution)/shard_map/ppermute | solution.py:27
  16.3 11.6 %collective-permute-start.2 = (bf16[128,512]{1,0:T(8,128)(2,1)}, bf16[128,512]{1,0:T(8,128)(2,1)}, u32[]{:S(2)}, u32[]{:S(2)}) collective-permute-start(bf16[128,512]{1,0:T(8,128)(2,1)} %get-tuple-element.39), channel_id=1, source_target_pairs={{0,3},{1,0},{2,1},{3,2},{4,7},{5,4},{6,5},{7,6},{8,11},{9,8},{10,9... | collective-permute-start | bytes 393224 | tf_op jit(solution)/shard_map/ppermute | solution.py:27
  18.2 61.3 %collective-permute-start.8 = (bf16[2048,128]{1,0:T(8,128)(2,1)}, bf16[2048,128]{1,0:T(8,128)(2,1)S(1)}, u32[]{:S(2)}, u32[]{:S(2)}) collective-permute-start(bf16[2048,128]{1,0:T(8,128)(2,1)} %dynamic-slice_bitcast_fusion), channel_id=1, source_target_pairs={{0,4},{4,0},{1,5},{5,1},{2,6},{6,2},{3,7},{7,3},{8,12},{12,8},{9,1... | collective-permute-start | bytes 1572872 | tf_op jit(solution)/shard_map/ppermute | solution.py:31
  21.8 24.6 %collective-permute-start.4 = (bf16[2048,128]{1,0:T(8,128)(2,1)}, bf16[2048,128]{1,0:T(8,128)(2,1)}, u32[]{:S(2)}, u32[]{:S(2)}) collective-permute-start(bf16[2048,128]{1,0:T(8,128)(2,1)} %dynamic-slice_bitcast_fusion.1), channel_id=1, source_target_pairs={{0,4},{4,0},{1,5},{5,1},{2,6},{6,2},{3,7},{7,3},{8,12},{12,8},{9,1... | collective-permute-start | bytes 1572872 | tf_op jit(solution)/shard_map/ppermute | solution.py:31
  25.7 37.0 %collective-permute-start.14 = (bf16[2,128,512]{2,1,0:T(8,128)(2,1)}, bf16[2,128,512]{2,1,0:T(8,128)(2,1)S(1)}, u32[]{:S(2)}, u32[]{:S(2)}) collective-permute-start(bf16[2,128,512]{2,1,0:T(8,128)(2,1)} %get-tuple-element.72), channel_id=1, source_target_pairs={{0,3},{1,0},{2,1},{3,2},{4,7},{5,4},{6,5},{7,6},{8,11},{9,8},{10,9... | collective-permute-start | bytes 786440 | tf_op jit(solution)/shard_map/ppermute | solution.py:27
  25.7 37.1 %collective-permute-start.13 = (bf16[2,128,512]{2,1,0:T(8,128)(2,1)}, bf16[2,128,512]{2,1,0:T(8,128)(2,1)}, u32[]{:S(2)}, u32[]{:S(2)}) collective-permute-start(bf16[2,128,512]{2,1,0:T(8,128)(2,1)} %get-tuple-element.73), channel_id=1, source_target_pairs={{0,2},{1,3},{2,0},{3,1},{4,6},{5,7},{6,4},{7,5},{8,10},{9,11},{10,... | collective-permute-start | bytes 786440 | tf_op jit(solution)/shard_map/ppermute | solution.py:27
  29.0 17.0 %collective-permute-start.3 = (bf16[128,512]{1,0:T(8,128)(2,1)S(1)}, bf16[128,512]{1,0:T(8,128)(2,1)S(1)}, u32[]{:S(2)}, u32[]{:S(2)}) collective-permute-start(bf16[128,512]{1,0:T(8,128)(2,1)S(1)} %add_convert_fusion.own_ref), channel_id=1, source_target_pairs={{0,4},{4,0},{1,5},{5,1},{2,6},{6,2},{3,7},{7,3},{8,12},{12,8},{9,1... | collective-permute-start | bytes 393224 | tf_op jit(solution)/shard_map/ppermute | solution.py:31
  46.0 17.7 %collective-permute-start.12 = (bf16[2,128,512]{2,1,0:T(8,128)(2,1)}, bf16[2,128,512]{2,1,0:T(8,128)(2,1)}, u32[]{:S(2)}, u32[]{:S(2)}) collective-permute-start(bf16[2,128,512]{2,1,0:T(8,128)(2,1)} %get-tuple-element.74), channel_id=1, source_target_pairs={{0,1},{1,2},{2,3},{3,0},{4,5},{5,6},{6,7},{7,4},{8,9},{9,10},{10,1... | collective-permute-start | bytes 786440 | tf_op jit(solution)/shard_map/ppermute | solution.py:27
  49.8 76.8 %copy-start.7 = (bf16[128,512]{1,0:T(8,128)(2,1)}, bf16[128,512]{1,0:T(8,128)(2,1)S(1)}, u32[]{:S(2)}) copy-start(bf16[128,512]{1,0:T(8,128)(2,1)S(1)} %get-tuple-element.47.hidden_ref) | copy-start | bytes 393220
  49.8 23.7 %all-to-all-start = ((bf16[32,8,512]{2,1,0:T(8,128)(2,1)}), bf16[32,8,512]{2,1,0:T(8,128)(2,1)}, u32[]{:S(2)}, u32[]{:S(2)}) async-start(bf16[32,8,512]{2,1,0:T(8,128)(2,1)} %copy-done.14), calls=%async_computation | async-start | bytes 524288 | tf_op jit(solution)/shard_map/all_to_all | solution.py:386
  66.4 34.6 %collective-permute-start.15 = (bf16[4,128,512]{2,1,0:T(8,128)(2,1)}, bf16[4,128,512]{2,1,0:T(8,128)(2,1)}, u32[]{:S(2)}, u32[]{:S(2)}) collective-permute-start(bf16[4,128,512]{2,1,0:T(8,128)(2,1)} %pad_maximum_fusion), channel_id=1, source_target_pairs={{0,4},{4,0},{1,5},{5,1},{2,6},{6,2},{3,7},{7,3},{8,12},{12,8},{9,1... | collective-permute-start | bytes 1572872 | tf_op jit(solution)/shard_map/ppermute | solution.py:31
  73.5 31.3 %all-to-all-start.2 = ((bf16[32,12,512]{2,1,0:T(8,128)(2,1)}), bf16[32,12,512]{2,1,0:T(8,128)(2,1)}, u32[]{:S(2)}, u32[]{:S(2)}) async-start(bf16[32,12,512]{2,1,0:T(8,128)(2,1)} %copy-done.13), calls=%async_computation.2 | async-start | bytes 1048576 | tf_op jit(solution)/shard_map/all_to_all | solution.py:386
  79.5 8.5 %collective-permute-start.11 = (bf16[256,512]{1,0:T(8,128)(2,1)}, bf16[256,512]{1,0:T(8,128)(2,1)S(1)}, u32[]{:S(2)}, u32[]{:S(2)}) collective-permute-start(bf16[256,512]{1,0:T(8,128)(2,1)} %bitcast.13.x0), channel_id=1, source_target_pairs={{0,3},{1,0},{2,1},{3,2},{4,7},{5,4},{6,5},{7,6},{8,11},{9,8},{10,9... | collective-permute-start | bytes 786440 | tf_op jit(solution)/shard_map/ppermute | solution.py:27
  81.8 9.0 %collective-permute-start.10 = (bf16[256,512]{1,0:T(8,128)(2,1)}, bf16[256,512]{1,0:T(8,128)(2,1)S(1)}, u32[]{:S(2)}, u32[]{:S(2)}) collective-permute-start(bf16[256,512]{1,0:T(8,128)(2,1)} %bitcast.13.x0), channel_id=1, source_target_pairs={{0,2},{1,3},{2,0},{3,1},{4,6},{5,7},{6,4},{7,5},{8,10},{9,11},{10,... | collective-permute-start | bytes 786440 | tf_op jit(solution)/shard_map/ppermute | solution.py:27
  81.8 15.0 %collective-permute-start.9 = (bf16[256,512]{1,0:T(8,128)(2,1)}, bf16[256,512]{1,0:T(8,128)(2,1)S(1)}, u32[]{:S(2)}, u32[]{:S(2)}) collective-permute-start(bf16[256,512]{1,0:T(8,128)(2,1)} %bitcast.13.x0), channel_id=1, source_target_pairs={{0,1},{1,2},{2,3},{3,0},{4,5},{5,6},{6,7},{7,4},{8,9},{9,10},{10,1... | collective-permute-start | bytes 786440 | tf_op jit(solution)/shard_map/ppermute | solution.py:27
  101.0 9.1 %collective-permute-start.18 = (bf16[256,256]{1,0:T(8,128)(2,1)}, bf16[256,256]{1,0:T(8,128)(2,1)}, u32[]{:S(2)}, u32[]{:S(2)}) collective-permute-start(bf16[256,256]{1,0:T(8,128)(2,1)} %gate_up.2.a0), channel_id=1, source_target_pairs={{0,3},{1,0},{2,1},{3,2},{4,7},{5,4},{6,5},{7,6},{8,11},{9,8},{10,9... | collective-permute-start | bytes 393224 | tf_op jit(solution)/shard_map/ppermute | solution.py:27
  103.3 9.2 %collective-permute-start.17 = (bf16[256,256]{1,0:T(8,128)(2,1)}, bf16[256,256]{1,0:T(8,128)(2,1)}, u32[]{:S(2)}, u32[]{:S(2)}) collective-permute-start(bf16[256,256]{1,0:T(8,128)(2,1)} %gate_up.2.a0), channel_id=1, source_target_pairs={{0,2},{1,3},{2,0},{3,1},{4,6},{5,7},{6,4},{7,5},{8,10},{9,11},{10,... | collective-permute-start | bytes 393224 | tf_op jit(solution)/shard_map/ppermute | solution.py:27
  104.0 8.5 %collective-permute-start.16 = (bf16[256,256]{1,0:T(8,128)(2,1)}, bf16[256,256]{1,0:T(8,128)(2,1)}, u32[]{:S(2)}, u32[]{:S(2)}) collective-permute-start(bf16[256,256]{1,0:T(8,128)(2,1)} %gate_up.2.a0), channel_id=1, source_target_pairs={{0,1},{1,2},{2,3},{3,0},{4,5},{5,6},{6,7},{7,4},{8,9},{9,10},{10,1... | collective-permute-start | bytes 393224 | tf_op jit(solution)/shard_map/ppermute | solution.py:27
  106.7 23.6 %collective-permute-start.21 = (bf16[384,512]{1,0:T(8,128)(2,1)}, bf16[384,512]{1,0:T(8,128)(2,1)}, u32[]{:S(2)}, u32[]{:S(2)}) collective-permute-start(bf16[384,512]{1,0:T(8,128)(2,1)} %reshape.57.x0), channel_id=1, source_target_pairs={{0,3},{1,0},{2,1},{3,2},{4,7},{5,4},{6,5},{7,6},{8,11},{9,8},{10,9... | collective-permute-start | bytes 1179656 | tf_op jit(solution)/shard_map/ppermute | solution.py:27
  109.0 21.3 %collective-permute-start.20 = (bf16[384,512]{1,0:T(8,128)(2,1)}, bf16[384,512]{1,0:T(8,128)(2,1)}, u32[]{:S(2)}, u32[]{:S(2)}) collective-permute-start(bf16[384,512]{1,0:T(8,128)(2,1)} %reshape.57.x0), channel_id=1, source_target_pairs={{0,2},{1,3},{2,0},{3,1},{4,6},{5,7},{6,4},{7,5},{8,10},{9,11},{10,... | collective-permute-start | bytes 1179656 | tf_op jit(solution)/shard_map/ppermute | solution.py:27
  110.2 20.6 %collective-permute-start.19 = (bf16[384,512]{1,0:T(8,128)(2,1)}, bf16[384,512]{1,0:T(8,128)(2,1)}, u32[]{:S(2)}, u32[]{:S(2)}) collective-permute-start(bf16[384,512]{1,0:T(8,128)(2,1)} %reshape.57.x0), channel_id=1, source_target_pairs={{0,1},{1,2},{2,3},{3,0},{4,5},{5,6},{6,7},{7,4},{8,9},{9,10},{10,1... | collective-permute-start | bytes 1179656 | tf_op jit(solution)/shard_map/ppermute | solution.py:27
  116.1 37.9 %all-to-all-start.1 = ((bf16[32,8,512]{2,1,0:T(8,128)(2,1)}), bf16[32,8,512]{2,1,0:T(8,128)(2,1)}, u32[]{:S(2)}, u32[]{:S(2)}) async-start(bf16[32,8,512]{2,1,0:T(8,128)(2,1)} %copy-done.8), calls=%async_computation.1 | async-start | bytes 524288 | tf_op jit(solution)/shard_map/all_to_all | solution.py:412
  127.5 11.0 %collective-permute-start.6 = (f32[128,128]{0,1:T(8,128)S(1)}, f32[128,128]{0,1:T(8,128)S(1)}, u32[]{:S(2)}, u32[]{:S(2)}) collective-permute-start(f32[128,128]{0,1:T(8,128)S(1)} %pad_maximum_fusion.1), channel_id=1, source_target_pairs={{0,2},{1,3},{2,0},{3,1},{4,6},{5,7},{6,4},{7,5},{8,10},{9,11},{10,... | collective-permute-start | bytes 196616 | tf_op jit(solution)/shard_map/ppermute | solution.py:27
  128.2 10.7 %collective-permute-start.7 = (f32[128,128]{0,1:T(8,128)S(1)}, f32[128,128]{0,1:T(8,128)S(1)}, u32[]{:S(2)}, u32[]{:S(2)}) collective-permute-start(f32[128,128]{0,1:T(8,128)S(1)} %pad_maximum_fusion.1), channel_id=1, source_target_pairs={{0,3},{1,0},{2,1},{3,2},{4,7},{5,4},{6,5},{7,6},{8,11},{9,8},{10,9... | collective-permute-start | bytes 196616 | tf_op jit(solution)/shard_map/ppermute | solution.py:27
  130.3 8.7 %collective-permute-start.5 = (f32[128,128]{0,1:T(8,128)S(1)}, f32[128,128]{0,1:T(8,128)S(1)}, u32[]{:S(2)}, u32[]{:S(2)}) collective-permute-start(f32[128,128]{0,1:T(8,128)S(1)} %pad_maximum_fusion.1), channel_id=1, source_target_pairs={{0,1},{1,2},{2,3},{3,0},{4,5},{5,6},{6,7},{7,4},{8,9},{9,10},{10,1... | collective-permute-start | bytes 196616 | tf_op jit(solution)/shard_map/ppermute | solution.py:27
  135.9 26.7 %copy-start.23 = (pred[32,20,128]{2,0,1:T(32,128)(4,1)S(1)}, pred[32,20,128]{2,0,1:T(32,128)(4,1)}, u32[]{:S(2)}) copy-start(pred[32,20,128]{2,0,1:T(32,128)(4,1)} %compare_and_fusion) | copy-start | bytes 245764
  135.9 6.0 %collective-permute-start.24 = (bf16[384,256]{1,0:T(8,128)(2,1)S(1)}, bf16[384,256]{1,0:T(8,128)(2,1)S(1)}, u32[]{:S(2)}, u32[]{:S(2)}) collective-permute-start(bf16[384,256]{1,0:T(8,128)(2,1)S(1)} %gate_up.3.a0), channel_id=1, source_target_pairs={{0,3},{1,0},{2,1},{3,2},{4,7},{5,4},{6,5},{7,6},{8,11},{9,8},{10,9... | collective-permute-start | bytes 589832 | tf_op jit(solution)/shard_map/ppermute | solution.py:27
  138.3 6.6 %collective-permute-start.23 = (bf16[384,256]{1,0:T(8,128)(2,1)S(1)}, bf16[384,256]{1,0:T(8,128)(2,1)S(1)}, u32[]{:S(2)}, u32[]{:S(2)}) collective-permute-start(bf16[384,256]{1,0:T(8,128)(2,1)S(1)} %gate_up.3.a0), channel_id=1, source_target_pairs={{0,2},{1,3},{2,0},{3,1},{4,6},{5,7},{6,4},{7,5},{8,10},{9,11},{10,... | collective-permute-start | bytes 589832 | tf_op jit(solution)/shard_map/ppermute | solution.py:27
  138.5 12.2 %collective-permute-start.22 = (bf16[384,256]{1,0:T(8,128)(2,1)S(1)}, bf16[384,256]{1,0:T(8,128)(2,1)S(1)}, u32[]{:S(2)}, u32[]{:S(2)}) collective-permute-start(bf16[384,256]{1,0:T(8,128)(2,1)S(1)} %gate_up.3.a0), channel_id=1, source_target_pairs={{0,1},{1,2},{2,3},{3,0},{4,5},{5,6},{6,7},{7,4},{8,9},{9,10},{10,1... | collective-permute-start | bytes 589832 | tf_op jit(solution)/shard_map/ppermute | solution.py:27
  154.0 25.2 %all-to-all-start.3 = ((bf16[32,12,512]{2,1,0:T(8,128)(2,1)}), bf16[32,12,512]{2,1,0:T(8,128)(2,1)S(1)}, u32[]{:S(2)}, u32[]{:S(2)}) async-start(bf16[32,12,512]{2,1,0:T(8,128)(2,1)} %down.3), calls=%async_computation.3 | async-start | bytes 1048576 | tf_op jit(solution)/shard_map/all_to_all | solution.py:412
  162.5 40.0 %copy-start.18 = (s32[32,3]{0,1:T(4,128)S(1)}, s32[32,3]{0,1:T(4,128)}, u32[]{:S(2)}) copy-start(s32[32,3]{0,1:T(4,128)} %param.16) | copy-start | bytes 1156
  162.6 40.4 %copy-start.34 = (s32[1,16]{1,0:T(1,128)S(1)}, s32[1,16]{1,0:T(1,128)}, u32[]{:S(2)}) copy-start(s32[1,16]{1,0:T(1,128)} %param.29) | copy-start | bytes 196
  162.6 43.6 %copy-start.33 = (s32[1,1024]{1,0:T(1,128)S(1)}, s32[1,1024]{1,0:T(1,128)}, u32[]{:S(2)}) copy-start(s32[1,1024]{1,0:T(1,128)} %param.28) | copy-start | bytes 12292
  181.3 5.4 %collective-permute-start.25 = (bf16[128,512]{1,0:T(8,128)(2,1)S(1)}, bf16[128,512]{1,0:T(8,128)(2,1)S(1)}, u32[]{:S(2)}, u32[]{:S(2)}) collective-permute-start(bf16[128,512]{1,0:T(8,128)(2,1)S(1)} %fusion.3.moe_ref), channel_id=1, source_target_pairs={{0,4},{4,0},{1,5},{5,1},{2,6},{6,2},{3,7},{7,3},{8,12},{12,8},{9,1... | collective-permute-start | bytes 393224 | tf_op jit(solution)/shard_map/ppermute | solution.py:31
  189.5 3.4 %collective-permute-start.28 = (f32[136,128]{1,0:T(8,128)}, f32[136,128]{1,0:T(8,128)S(1)}, u32[]{:S(2)}, u32[]{:S(2)}) collective-permute-start(f32[136,128]{1,0:T(8,128)} %get-tuple-element.58.p0), channel_id=1, source_target_pairs={{0,3},{1,0},{2,1},{3,2},{4,7},{5,4},{6,5},{7,6},{8,11},{9,8},{10,9... | collective-permute-start | bytes 208904 | tf_op jit(solution)/shard_map/ppermute | solution.py:27
  189.8 4.9 %collective-permute-start.27 = (f32[136,128]{1,0:T(8,128)}, f32[136,128]{1,0:T(8,128)S(1)}, u32[]{:S(2)}, u32[]{:S(2)}) collective-permute-start(f32[136,128]{1,0:T(8,128)} %get-tuple-element.58.p0), channel_id=1, source_target_pairs={{0,2},{1,3},{2,0},{3,1},{4,6},{5,7},{6,4},{7,5},{8,10},{9,11},{10,... | collective-permute-start | bytes 208904 | tf_op jit(solution)/shard_map/ppermute | solution.py:27
  190.0 5.4 %collective-permute-start.26 = (f32[136,128]{1,0:T(8,128)}, f32[136,128]{1,0:T(8,128)S(1)}, u32[]{:S(2)}, u32[]{:S(2)}) collective-permute-start(f32[136,128]{1,0:T(8,128)} %get-tuple-element.58.p0), channel_id=1, source_target_pairs={{0,1},{1,2},{2,3},{3,0},{4,5},{5,6},{6,7},{7,4},{8,9},{9,10},{10,1... | collective-permute-start | bytes 208904 | tf_op jit(solution)/shard_map/ppermute | solution.py:27
  198.1 17.6 %all-to-all-start.4 = ((bf16[16,128,128]{2,1,0:T(8,128)(2,1)}), bf16[16,128,128]{2,1,0:T(8,128)(2,1)S(1)}, u32[]{:S(2)}, u32[]{:S(2)}) async-start(bf16[16,128,128]{2,1,0:T(8,128)(2,1)} %vectors.1), calls=%async_computation.4 | async-start | bytes 1048576 | tf_op jit(solution)/shard_map/all_to_all | solution.py:464
  203.0 5.9 %collective-permute-start.31 = (bf16[128,512]{1,0:T(8,128)(2,1)}, bf16[128,512]{1,0:T(8,128)(2,1)S(1)}, u32[]{:S(2)}, u32[]{:S(2)}) collective-permute-start(bf16[128,512]{1,0:T(8,128)(2,1)} %get-tuple-element.62.p0), channel_id=1, source_target_pairs={{0,3},{1,0},{2,1},{3,2},{4,7},{5,4},{6,5},{7,6},{8,11},{9,8},{10,9... | collective-permute-start | bytes 393224 | tf_op jit(solution)/shard_map/ppermute | solution.py:27
  205.3 5.6 %collective-permute-start.30 = (bf16[128,512]{1,0:T(8,128)(2,1)}, bf16[128,512]{1,0:T(8,128)(2,1)S(1)}, u32[]{:S(2)}, u32[]{:S(2)}) collective-permute-start(bf16[128,512]{1,0:T(8,128)(2,1)} %get-tuple-element.62.p0), channel_id=1, source_target_pairs={{0,2},{1,3},{2,0},{3,1},{4,6},{5,7},{6,4},{7,5},{8,10},{9,11},{10,... | collective-permute-start | bytes 393224 | tf_op jit(solution)/shard_map/ppermute | solution.py:27
  205.8 6.5 %collective-permute-start.29 = (bf16[128,512]{1,0:T(8,128)(2,1)}, bf16[128,512]{1,0:T(8,128)(2,1)S(1)}, u32[]{:S(2)}, u32[]{:S(2)}) collective-permute-start(bf16[128,512]{1,0:T(8,128)(2,1)} %get-tuple-element.62.p0), channel_id=1, source_target_pairs={{0,1},{1,2},{2,3},{3,0},{4,5},{5,6},{6,7},{7,4},{8,9},{9,10},{10,1... | collective-permute-start | bytes 393224 | tf_op jit(solution)/shard_map/ppermute | solution.py:27
  215.6 7.0 %collective-permute-start.32 = (bf16[2048,128]{1,0:T(8,128)(2,1)S(1)}, bf16[2048,128]{1,0:T(8,128)(2,1)S(1)}, u32[]{:S(2)}, u32[]{:S(2)}) collective-permute-start(bf16[2048,128]{1,0:T(8,128)(2,1)S(1)} %bitcast.46), channel_id=1, source_target_pairs={{0,8},{8,0},{1,9},{9,1},{2,10},{10,2},{3,11},{11,3},{4,12},{12,4},... | collective-permute-start | bytes 1572872 | tf_op jit(solution)/shard_map/ppermute | solution.py:478
  (25 other events, 73.0 us)

commit v5 on v4

--- a/solution.py
+++ b/solution.py
@@ -13,7 +13,8 @@
 CAP = 20
 EXPERTS = 64
 WIDE = 32
-GROUPS = ((0, 8), (8, 20))
+GROUPS = ((0, 20),)
+SPLIT = ((0, 20),)
 EPS = 1e-06
 THETA = 50000.0
 NEG = -1e30
@@ -316,6 +317,9 @@
     def cut(array, part, axis):
         return lax.dynamic_slice_in_dim(array, lax.rem(part, 4) * 512, 512, axis)
 
+    gate_sent, tokens = lax.optimization_barrier((pick(w_gate, 1 - i), tokens))
+    gate_par = x_swap(gate_sent)
+
     attn = pl.pallas_call(
         attention_kernel,
         out_shape=(jax.ShapeDtypeStruct((TOK, 512), bf16),) * 4,
@@ -327,7 +331,7 @@
             pltpu.VMEM((256, 2048), bf16),
             pltpu.SemaphoreType.DMA((5,)),
         ],
-        compiler_params=params(),
+        compiler_params=pltpu.CompilerParams(vmem_limit_bytes=60 << 20),
         name="attention",
     )(
         here,
@@ -340,8 +344,6 @@
     )
     attn_parts = [y_shift(attn[k], k) for k in (1, 2, 3)]
 
-    own_part, w_gate, w_up = lax.optimization_barrier((attn[0], w_gate, w_up))
-    gate_par = x_swap(pick(w_gate, 1 - i))
     up_par = x_swap(pick(w_up, 1 - i))
     downs = [cut(w_down, j, 2)] + [y_shift(cut(w_down, j + k, 2), k) for k in (1, 2, 3)]
     down_par = x_swap(jnp.stack([pick(d, 1 - i) for d in downs]))
@@ -362,7 +364,7 @@
         name="choose",
     )(here, routes.T)
 
-    attn = (own_part.astype(f32) + sum(p.astype(f32) for p in attn_parts)).astype(bf16)
+    attn = (attn[0].astype(f32) + sum(p.astype(f32) for p in attn_parts)).astype(bf16)
     attn, *chooses = lax.optimization_barrier((attn, *chooses))
     attn_par = x_swap(attn)
     attn_par, gate_par = lax.optimization_barrier((attn_par, gate_par))
@@ -379,16 +381,11 @@
     )(here, tokens, attn, attn_par, *chooses)
 
     backs = []
-    arrived = []
-    for g, group in enumerate(rows):
-        if arrived:
-            group, arrived[-1] = lax.optimization_barrier((group, arrived[-1]))
-        arrived.append(lax.all_to_all(group, W, 0, 0, tiled=True))
-    for g, x in enumerate(arrived):
-        size = x.shape[1]
-        x = x.reshape(WIDE * size, 512)
-        if g == 0:
-            x, up_par = lax.optimization_barrier((x, up_par))
+    arrived = lax.all_to_all(rows[0], W, 0, 0, tiled=True)
+    arrived, up_par = lax.optimization_barrier((arrived, up_par))
+    for g, (a, b) in enumerate(SPLIT):
+        size = b - a
+        x = arrived[:, a:b].reshape(WIDE * size, 512)
         act = pl.pallas_call(
             gate_up_kernel,
             out_shape=jax.ShapeDtypeStruct((WIDE * size, 256), bf16),
@@ -432,7 +429,7 @@
 
     moe = jnp.zeros((TOK, 512), f32)
     contract = (((0, 1), (0, 1)), ((), ()))
-    for (a, b), back in zip(GROUPS, backs):
+    for (a, b), back in zip(SPLIT, backs):
         mixing = jnp.where(chosen[:, a:b], gates[:, None, :], 0.0)
         mixing_hi = lax.reduce_precision(mixing, 8, 7)
         mixing_lo = (mixing - mixing_hi).astype(bf16)

time: 229 us -> 206 us (0.90)
  waiting for transfers between devices: 74.3 us -> 102 us
  starting transfers between devices: 84.2 us -> 59.1 us
  local copies, waits for them, and re-layouts: 26.6 us -> 14.3 us
  Pallas kernels: 28.4 us -> 24 us
  matrix products: 5.52 us -> 1.24 us
  other arithmetic: 6.53 us -> 3.53 us
    ppermute x27 -> x21, waiting for transfers between devices: 35.7 us -> 70.3 us  [y_shift(): return lax.ppermute(x, 'y', [(s, (s + k) % 4) for s in range(4)])]
    unnamed x71 -> x55, local copies, waits for them, and re-layouts: 15.1 us -> 3.33 us
    all_to_all x2 -> x1, starting transfers between devices: 19 us -> 8.11 us  [body(): backs.append(lax.all_to_all(out, W, 0, 0, tiled=True))]
    all_to_all x2 -> x1, starting transfers between devices: 17.4 us -> 10.8 us  [body(): arrived = lax.all_to_all(rows[0], W, 0, 0, tiled=True)]
    ppermute x27 -> x21, starting transfers between devices: 27.5 us -> 21.7 us  [y_shift(): return lax.ppermute(x, 'y', [(s, (s + k) % 4) for s in range(4)])]
    all_to_all x2 -> x1, waiting for transfers between devices: 4.66 us -> 0.01 us  [body(): arrived = lax.all_to_all(rows[0], W, 0, 0, tiled=True)]
    ppermute x5, waiting for transfers between devices: 15.3 us -> 11.4 us  [x_swap(): return lax.ppermute(x, 'xh', [(0, 1), (1, 0)])]
    pallas_call x2 -> x1, Pallas kernels: 6.91 us -> 3.32 us  [body(): pl.pallas_call(gate_up_kernel, out_shape=jax.ShapeDtypeStruct((WIDE * siz...]
  transfers between devices with their start and end apart: 38 -> 30, of which waited for: 18 -> 23; matrix products, arithmetic and copies ran while one was open for 9% -> 6% of each run, Pallas kernels for 7% -> 5%
where the time goes in v5:
time: 206 us; the launch traced here: 205 us
  waiting for transfers between devices  102 us (50%)
  starting transfers between devices  59.1 us (29%)
  Pallas kernels  24 us (12%)
  local copies, waits for them, and re-layouts  14.3 us (7%)
  other arithmetic  3.53 us (2%)
    ppermute x21, waiting for transfers between devices, y_shift(): return lax.ppermute(x, 'y', [(s, (s + k) % 4) for s in range(4)])  70.3 us
    ppermute x21, starting transfers between devices, y_shift(): return lax.ppermute(x, 'y', [(s, (s + k) % 4) for s in range(4)])  21.7 us
    all_to_all x1, waiting for transfers between devices, body(): backs.append(lax.all_to_all(out, W, 0, 0, tiled=True))  14.3 us
    ppermute x5, waiting for transfers between devices, x_swap(): return lax.ppermute(x, 'xh', [(0, 1), (1, 0)])  11.4 us
    all_to_all x1, starting transfers between devices, body(): arrived = lax.all_to_all(rows[0], W, 0, 0, tiled=True)  10.8 us
    ppermute x5, starting transfers between devices, x_swap(): return lax.ppermute(x, 'xh', [(0, 1), (1, 0)])  8.96 us
    all_to_all x1, starting transfers between devices, body(): backs.append(lax.all_to_all(out, W, 0, 0, tiled=True))  8.11 us
    all_to_all x1, waiting for transfers between devices, body(): lax.all_to_all(vectors, ('z', 'xl'), 0, 0, tiled=True)  5.67 us
  transfers between devices with their start and end apart: 30, of which 23 were waited for; matrix products, arithmetic and copies ran while one was open for 6% of the time, Pallas kernels for 5%

profile of v5, /device:TPU:1, one launch (start us, length us, event | category | flops | bytes accessed | tf_op | source)
XLA Modules:
  0.0 205.2 jit_solution(1777288579193130957)
XLA Ops:
  0.7 1.1 dynamic-slice_bitcast_fusion.1
  1.8 3.7 %collective-permute-start.4 = (bf16[2048,128]{1,0:T(8,128)(2,1)S(1)}, bf16[2048,128]{1,0:T(8,128)(2,1)S(1)}, u32[]{:S(2)}, u32[]{:S(2)}) collective-permute-start(bf16[2048,128]{1,0:T(8,128)(2,1)S(1)} %dynamic-slice_bitcast_fusion.1), channel_id=1, source_target_pairs={{0,4},{4,0},{1,5},{5,1},{2,6},{6,2},{3,7},{7,3},{8,12},{12,8},{9,1... | collective-permute-start | bytes 1572872 | tf_op jit(solution)/shard_map/ppermute | solution.py:32
  6.1 5.1 %attention.1 = (bf16[128,512]{1,0:T(8,128)(2,1)}, bf16[128,512]{1,0:T(8,128)(2,1)}, bf16[128,512]{1,0:T(8,128)(2,1)}, bf16[128,512]{1,0:T(8,128)(2,1)}) custom-call(s32[4]{0:T(128)} %pad_add_fusion.here_ref, s32[3,32]{1,0:T(4,128)} %bitcast.39, f32[2,256]{1,0:T(2,128)} %qk_ref.1, f32[3,2048]{1,0:T(4,128)} %gain_ref.5, bf16[128,2048]{1,0:T(8,128)(2,1)} %x_ref, ...), custom_call_target="tpu_custom_call" | custom-call | tf_op jit(solution)/shard_map/attention/pallas_call | solution.py:323
  11.2 2.8 %collective-permute-start.2 = (bf16[128,512]{1,0:T(8,128)(2,1)}, bf16[128,512]{1,0:T(8,128)(2,1)S(1)}, u32[]{:S(2)}, u32[]{:S(2)}) collective-permute-start(bf16[128,512]{1,0:T(8,128)(2,1)} %get-tuple-element.32), channel_id=1, source_target_pairs={{0,3},{1,0},{2,1},{3,2},{4,7},{5,4},{6,5},{7,6},{8,11},{9,8},{10,9... | collective-permute-start | bytes 393224 | tf_op jit(solution)/shard_map/ppermute | solution.py:28
  16.0 3.2 %collective-permute-done.2 = bf16[128,512]{1,0:T(8,128)(2,1)S(1)} collective-permute-done((bf16[128,512]{1,0:T(8,128)(2,1)}, bf16[128,512]{1,0:T(8,128)(2,1)S(1)}, u32[]{:S(2)}, u32[]{:S(2)}) %collective-permute-start.2) | collective-permute-done | bytes 131104 | tf_op jit(solution)/shard_map/ppermute | solution.py:28
  19.7 3.8 %collective-permute-done = bf16[128,512]{1,0:T(8,128)(2,1)S(1)} collective-permute-done((bf16[128,512]{1,0:T(8,128)(2,1)}, bf16[128,512]{1,0:T(8,128)(2,1)S(1)}, u32[]{:S(2)}, u32[]{:S(2)}) %collective-permute-start) | collective-permute-done | bytes 131104 | tf_op jit(solution)/shard_map/ppermute | solution.py:28
  24.8 5.1 %collective-permute-done.3.par_ref = bf16[128,512]{1,0:T(8,128)(2,1)S(1)} collective-permute-done((bf16[128,512]{1,0:T(8,128)(2,1)S(1)}, bf16[128,512]{1,0:T(8,128)(2,1)S(1)}, u32[]{:S(2)}, u32[]{:S(2)}) %collective-permute-start.3) | collective-permute-done | bytes 131104 | tf_op jit(solution)/shard_map/ppermute | solution.py:32
  30.0 1.8 dispatch.1
  31.7 10.8 %all-to-all-start = ((bf16[32,20,512]{2,1,0:T(8,128)(2,1)}), bf16[32,20,512]{2,1,0:T(8,128)(2,1)}, u32[]{:S(2)}, u32[]{:S(2)}) async-start(bf16[32,20,512]{2,1,0:T(8,128)(2,1)} %get-tuple-element.38), calls=%async_computation | async-start | bytes 1572864 | tf_op jit(solution)/shard_map/all_to_all | solution.py:384
  42.6 2.2 %constant_dynamic-slice_fusion = (bf16[2,128,512]{2,1,0:T(8,128)(2,1)S(1)}, bf16[2,128,512]{2,1,0:T(8,128)(2,1)}, bf16[2,128,512]{2,1,0:T(8,128)(2,1)}, bf16[2,128,512]{2,1,0:T(8,128)(2,1)}) fusion(bf16[2,128,2048]{2,1,0:T(8,128)(2,1)} %param.25, s32[]{:T(128)S(6)} %select_n.65, s32[]{:T(128)S(6)} %select_n.68, s32[]{:T(128)S(6)} %select_n.67, s32[]{:T(128)S(6)} %select_n.69), kind=kLoop, calls=%fused_computation.54 | loop fusion | bytes 2097168 | tf_op jit(solution)/shard_map/dynamic_slice | solution.py:318
  45.9 1.7 collective-permute-start.8
  48.8 1.7 constant_dynamic-slice_fusion.7
  50.5 2.2 %collective-permute-done.14.w3 = bf16[2,128,512]{2,1,0:T(8,128)(2,1)S(1)} collective-permute-done((bf16[2,128,512]{2,1,0:T(8,128)(2,1)}, bf16[2,128,512]{2,1,0:T(8,128)(2,1)S(1)}, u32[]{:S(2)}, u32[]{:S(2)}) %collective-permute-start.14) | collective-permute-done | bytes 262176 | tf_op jit(solution)/shard_map/ppermute | solution.py:28
  53.4 3.1 %collective-permute-done.13.w2 = bf16[2,128,512]{2,1,0:T(8,128)(2,1)S(1)} collective-permute-done((bf16[2,128,512]{2,1,0:T(8,128)(2,1)}, bf16[2,128,512]{2,1,0:T(8,128)(2,1)S(1)}, u32[]{:S(2)}, u32[]{:S(2)}) %collective-permute-start.13) | collective-permute-done | bytes 262176 | tf_op jit(solution)/shard_map/ppermute | solution.py:28
  57.2 6.1 %collective-permute-done.12.w1 = bf16[2,128,512]{2,1,0:T(8,128)(2,1)} collective-permute-done((bf16[2,128,512]{2,1,0:T(8,128)(2,1)}, bf16[2,128,512]{2,1,0:T(8,128)(2,1)}, u32[]{:S(2)}, u32[]{:S(2)}) %collective-permute-start.12) | collective-permute-done | bytes 262176 | tf_op jit(solution)/shard_map/ppermute | solution.py:28
  63.3 1.6 constant_dynamic-slice_fusion.5
  64.9 2.8 %collective-permute-done.8.up_par = bf16[2048,128]{1,0:T(8,128)(2,1)} collective-permute-done((bf16[2048,128]{1,0:T(8,128)(2,1)}, bf16[2048,128]{1,0:T(8,128)(2,1)}, u32[]{:S(2)}, u32[]{:S(2)}) %collective-permute-start.8) | collective-permute-done | bytes 524320 | tf_op jit(solution)/shard_map/ppermute | solution.py:32
  67.7 1.3 reshape.53.x0
  69.1 1.5 collective-permute-start.10
  70.5 1.2 collective-permute-start.11
  71.7 1.2 pad_maximum_fusion
  72.9 1.3 collective-permute-start.15
  74.4 25.6 %collective-permute-done.9.x1 = bf16[640,512]{1,0:T(8,128)(2,1)S(1)} collective-permute-done((bf16[640,512]{1,0:T(8,128)(2,1)S(1)}, bf16[640,512]{1,0:T(8,128)(2,1)S(1)}, u32[]{:S(2)}, u32[]{:S(2)}) %collective-permute-start.9) | collective-permute-done | bytes 655392 | tf_op jit(solution)/shard_map/ppermute | solution.py:28
  101.4 3.3 %gate_up.1.a0 = bf16[640,256]{1,0:T(8,128)(2,1)S(1)} custom-call(s32[4]{0:T(128)S(1)} %copy-done.13, bf16[640,512]{1,0:T(8,128)(2,1)S(1)} %reshape.53.x0, bf16[640,512]{1,0:T(8,128)(2,1)S(1)} %collective-permute-done.9.x1, bf16[640,512]{1,0:T(8,128)(2,1)S(1)} %collective-permute-done.10.x2, bf16[640,512]{1,0:T(8,128)(2,1)S(1)} %collective-permute-done.11.x3, ...), custom_call_target="tpu_custom_call" | custom-call | tf_op jit(solution)/shard_map/gate_up/pallas_call | solution.py:389
  104.7 1.3 collective-permute-start.16
  106.0 2.9 %collective-permute-start.17 = (bf16[640,256]{1,0:T(8,128)(2,1)S(1)}, bf16[640,256]{1,0:T(8,128)(2,1)S(1)}, u32[]{:S(2)}, u32[]{:S(2)}) collective-permute-start(bf16[640,256]{1,0:T(8,128)(2,1)S(1)} %gate_up.1.a0), channel_id=1, source_target_pairs={{0,2},{1,3},{2,0},{3,1},{4,6},{5,7},{6,4},{7,5},{8,10},{9,11},{10,... | collective-permute-start | bytes 983048 | tf_op jit(solution)/shard_map/ppermute | solution.py:28
  109.1 5.0 %collective-permute-done.16.a1 = bf16[640,256]{1,0:T(8,128)(2,1)S(1)} collective-permute-done((bf16[640,256]{1,0:T(8,128)(2,1)S(1)}, bf16[640,256]{1,0:T(8,128)(2,1)S(1)}, u32[]{:S(2)}, u32[]{:S(2)}) %collective-permute-start.16) | collective-permute-done | bytes 327712 | tf_op jit(solution)/shard_map/ppermute | solution.py:28
  114.1 8.8 %collective-permute-done.17.a2 = bf16[640,256]{1,0:T(8,128)(2,1)S(1)} collective-permute-done((bf16[640,256]{1,0:T(8,128)(2,1)S(1)}, bf16[640,256]{1,0:T(8,128)(2,1)S(1)}, u32[]{:S(2)}, u32[]{:S(2)}) %collective-permute-start.17) | collective-permute-done | bytes 327712 | tf_op jit(solution)/shard_map/ppermute | solution.py:28
  122.9 3.7 %down.1 = bf16[32,20,512]{2,1,0:T(8,128)(2,1)} custom-call(s32[4]{0:T(128)S(1)} %copy-done.13, bf16[640,256]{1,0:T(8,128)(2,1)S(1)} %gate_up.1.a0, bf16[640,256]{1,0:T(8,128)(2,1)S(1)} %collective-permute-done.16.a1, bf16[640,256]{1,0:T(8,128)(2,1)S(1)} %collective-permute-done.17.a2, bf16[640,256]{1,0:T(8,128)(2,1)S(1)} %collective-permute-done.18.a3, ...), custom_call_target="tpu_custom_call" | custom-call | tf_op jit(solution)/shard_map/down/pallas_call | solution.py:400
  126.6 8.1 %all-to-all-start.1 = ((bf16[32,20,512]{2,1,0:T(8,128)(2,1)}), bf16[32,20,512]{2,1,0:T(8,128)(2,1)S(1)}, u32[]{:S(2)}, u32[]{:S(2)}) async-start(bf16[32,20,512]{2,1,0:T(8,128)(2,1)} %down.1), calls=%async_computation.1 | async-start | bytes 1572864 | tf_op jit(solution)/shard_map/all_to_all | solution.py:409
  135.1 2.0 collective-permute-start.7
  138.6 3.2 %collective-permute-done.6 = f32[128,128]{0,1:T(8,128)S(1)} collective-permute-done((f32[128,128]{0,1:T(8,128)S(1)}, f32[128,128]{0,1:T(8,128)S(1)}, u32[]{:S(2)}, u32[]{:S(2)}) %collective-permute-start.6) | collective-permute-done | bytes 65568 | tf_op jit(solution)/shard_map/ppermute | solution.py:28
  143.0 14.3 %all-to-all-done.1 = bf16[32,20,512]{2,1,0:T(8,128)(2,1)S(1)} async-done(((bf16[32,20,512]{2,1,0:T(8,128)(2,1)}), bf16[32,20,512]{2,1,0:T(8,128)(2,1)S(1)}, u32[]{:S(2)}, u32[]{:S(2)}) %all-to-all-start.1) | async-done | bytes 655392 | tf_op jit(solution)/shard_map/all_to_all | solution.py:409
  158.3 1.9 collective-permute-start.19
  160.2 3.5 %collective-permute-done.19.par_ref = bf16[128,512]{1,0:T(8,128)(2,1)S(1)} collective-permute-done((bf16[128,512]{1,0:T(8,128)(2,1)S(1)}, bf16[128,512]{1,0:T(8,128)(2,1)S(1)}, u32[]{:S(2)}, u32[]{:S(2)}) %collective-permute-start.19) | collective-permute-done | bytes 131104 | tf_op jit(solution)/shard_map/ppermute | solution.py:32
  164.3 2.1 %embed.1 = (bf16[128,512]{1,0:T(8,128)(2,1)}, f32[136,128]{1,0:T(8,128)}) custom-call(s32[4]{0:T(128)} %pad_add_fusion.here_ref, bf16[128,512]{1,0:T(8,128)(2,1)} %copy-done.4, bf16[128,512]{1,0:T(8,128)(2,1)} %copy-done.16, bf16[128,512]{1,0:T(8,128)(2,1)} %copy-done.17, f32[3,2048]{1,0:T(4,128)} %gain_ref.5, bf16[2048,128]{1,0:T(8,128)(2,1)} %w_ref.1), custom_call_target="tpu_custom_call" | custom-call | tf_op jit(solution)/shard_map/embed/pallas_call | solution.py:440
  166.6 2.9 %collective-permute-start.21 = (f32[136,128]{1,0:T(8,128)}, f32[136,128]{1,0:T(8,128)S(1)}, u32[]{:S(2)}, u32[]{:S(2)}) collective-permute-start(f32[136,128]{1,0:T(8,128)} %get-tuple-element.44.p0), channel_id=1, source_target_pairs={{0,2},{1,3},{2,0},{3,1},{4,6},{5,7},{6,4},{7,5},{8,10},{9,11},{10,... | collective-permute-start | bytes 208904 | tf_op jit(solution)/shard_map/ppermute | solution.py:28
  169.5 1.5 collective-permute-done.20.p1
  171.0 1.1 collective-permute-done.21.p2
  173.5 2.0 vectors.1
  175.5 5.1 %all-to-all-start.2 = ((bf16[16,128,128]{2,1,0:T(8,128)(2,1)}), bf16[16,128,128]{2,1,0:T(8,128)(2,1)S(1)}, u32[]{:S(2)}, u32[]{:S(2)}) async-start(bf16[16,128,128]{2,1,0:T(8,128)(2,1)} %vectors.1), calls=%async_computation.2 | async-start | bytes 1048576 | tf_op jit(solution)/shard_map/all_to_all | solution.py:461
  181.7 2.1 %collective-permute-start.24 = (bf16[128,512]{1,0:T(8,128)(2,1)}, bf16[128,512]{1,0:T(8,128)(2,1)S(1)}, u32[]{:S(2)}, u32[]{:S(2)}) collective-permute-start(bf16[128,512]{1,0:T(8,128)(2,1)} %get-tuple-element.48.p0), channel_id=1, source_target_pairs={{0,2},{1,3},{2,0},{3,1},{4,6},{5,7},{6,4},{7,5},{8,10},{9,11},{10,... | collective-permute-start | bytes 393224 | tf_op jit(solution)/shard_map/ppermute | solution.py:28
  183.8 1.1 collective-permute-start.25
  185.8 2.3 %collective-permute-done.23.p1 = bf16[128,512]{1,0:T(8,128)(2,1)S(1)} collective-permute-done((bf16[128,512]{1,0:T(8,128)(2,1)}, bf16[128,512]{1,0:T(8,128)(2,1)S(1)}, u32[]{:S(2)}, u32[]{:S(2)}) %collective-permute-start.23) | collective-permute-done | bytes 131104 | tf_op jit(solution)/shard_map/ppermute | solution.py:28
  189.0 5.7 %all-to-all-done.2 = bf16[16,128,128]{2,1,0:T(8,128)(2,1)S(1)} async-done(((bf16[16,128,128]{2,1,0:T(8,128)(2,1)}), bf16[16,128,128]{2,1,0:T(8,128)(2,1)S(1)}, u32[]{:S(2)}, u32[]{:S(2)}) %all-to-all-start.2) | async-done | bytes 524320 | tf_op jit(solution)/shard_map/all_to_all | solution.py:461
  194.6 4.4 %collective-permute-start.26 = (bf16[2048,128]{1,0:T(8,128)(2,1)S(1)}, bf16[2048,128]{1,0:T(8,128)(2,1)S(1)}, u32[]{:S(2)}, u32[]{:S(2)}) collective-permute-start(bf16[2048,128]{1,0:T(8,128)(2,1)S(1)} %bitcast.36), channel_id=1, source_target_pairs={{0,8},{8,0},{1,9},{9,1},{2,10},{10,2},{3,11},{11,3},{4,12},{12,4},... | collective-permute-start | bytes 1572872 | tf_op jit(solution)/shard_map/ppermute | solution.py:475
  199.0 1.9 assemble.1
  201.8 3.2 %score.1 = f32[1,16]{1,0:T(1,128)} custom-call(s32[5,16]{1,0:T(8,128)} %stack.48.info_ref, bf16[1024,128]{1,0:T(8,128)(2,1)} %doc_ref.1, bf16[2048,128]{1,0:T(8,128)(2,1)} %bitcast.37, bf16[2048,128]{1,0:T(8,128)(2,1)} %copy-done.15), custom_call_target="tpu_custom_call" | custom-call | tf_op jit(solution)/shard_map/score/pallas_call | solution.py:483
  (116 shorter events, 19.6 us)
Async XLA Ops:
  0.6 134.1 %copy-start = (bf16[2048,64]{0,1:T(8,128)(2,1)S(1)}, bf16[2048,64]{0,1:T(8,128)(2,1)}, u32[]{:S(2)}) copy-start(bf16[2048,64]{0,1:T(8,128)(2,1)} %param.21) | copy-start | bytes 786436
  0.6 14.5 %copy-start.12 = (s32[128,8]{0,1:T(8,128)S(1)}, s32[128,8]{0,1:T(8,128)}, u32[]{:S(2)}) copy-start(s32[128,8]{0,1:T(8,128)} %param.22) | copy-start | bytes 12292
  0.7 29.3 %copy-start.3 = (bf16[128,2048]{1,0:T(8,128)(2,1)S(1)}, bf16[128,2048]{1,0:T(8,128)(2,1)}, u32[]{:S(2)}) copy-start(bf16[128,2048]{1,0:T(8,128)(2,1)} %x_ref) | copy-start | bytes 1572868
  1.8 28.1 %collective-permute-start.4 = (bf16[2048,128]{1,0:T(8,128)(2,1)S(1)}, bf16[2048,128]{1,0:T(8,128)(2,1)S(1)}, u32[]{:S(2)}, u32[]{:S(2)}) collective-permute-start(bf16[2048,128]{1,0:T(8,128)(2,1)S(1)} %dynamic-slice_bitcast_fusion.1), channel_id=1, source_target_pairs={{0,4},{4,0},{1,5},{5,1},{2,6},{6,2},{3,7},{7,3},{8,12},{12,8},{9,1... | collective-permute-start | bytes 1572872 | tf_op jit(solution)/shard_map/ppermute | solution.py:32
  11.2 33.8 %copy-start.2 = (bf16[2,2048,128]{2,1,0:T(8,128)(2,1)S(1)}, bf16[2,2048,128]{2,1,0:T(8,128)(2,1)}, u32[]{:S(2)}) copy-start(bf16[2,2048,128]{2,1,0:T(8,128)(2,1)} %up_hbm.1) | copy-start | bytes 3145732
  11.2 8.0 %collective-permute-start.2 = (bf16[128,512]{1,0:T(8,128)(2,1)}, bf16[128,512]{1,0:T(8,128)(2,1)S(1)}, u32[]{:S(2)}, u32[]{:S(2)}) collective-permute-start(bf16[128,512]{1,0:T(8,128)(2,1)} %get-tuple-element.32), channel_id=1, source_target_pairs={{0,3},{1,0},{2,1},{3,2},{4,7},{5,4},{6,5},{7,6},{8,11},{9,8},{10,9... | collective-permute-start | bytes 393224 | tf_op jit(solution)/shard_map/ppermute | solution.py:28
  14.1 5.6 %collective-permute-start.1 = (bf16[128,512]{1,0:T(8,128)(2,1)}, bf16[128,512]{1,0:T(8,128)(2,1)S(1)}, u32[]{:S(2)}, u32[]{:S(2)}) collective-permute-start(bf16[128,512]{1,0:T(8,128)(2,1)} %get-tuple-element.31), channel_id=1, source_target_pairs={{0,2},{1,3},{2,0},{3,1},{4,6},{5,7},{6,4},{7,5},{8,10},{9,11},{10,... | collective-permute-start | bytes 393224 | tf_op jit(solution)/shard_map/ppermute | solution.py:28
  14.4 9.1 %collective-permute-start = (bf16[128,512]{1,0:T(8,128)(2,1)}, bf16[128,512]{1,0:T(8,128)(2,1)S(1)}, u32[]{:S(2)}, u32[]{:S(2)}) collective-permute-start(bf16[128,512]{1,0:T(8,128)(2,1)} %get-tuple-element.30), channel_id=1, source_target_pairs={{0,1},{1,2},{2,3},{3,0},{4,5},{5,6},{6,7},{7,4},{8,9},{9,10},{10,1... | collective-permute-start | bytes 393224 | tf_op jit(solution)/shard_map/ppermute | solution.py:28
  24.5 26.0 %copy-start.11 = (f32[3,2048]{1,0:T(4,128)S(1)}, f32[3,2048]{1,0:T(4,128)}, u32[]{:S(2)}) copy-start(f32[3,2048]{1,0:T(4,128)} %gain_ref.5) | copy-start | bytes 73732
  24.5 5.4 %collective-permute-start.3 = (bf16[128,512]{1,0:T(8,128)(2,1)S(1)}, bf16[128,512]{1,0:T(8,128)(2,1)S(1)}, u32[]{:S(2)}, u32[]{:S(2)}) collective-permute-start(bf16[128,512]{1,0:T(8,128)(2,1)S(1)} %add_convert_fusion.own_ref), channel_id=1, source_target_pairs={{0,4},{4,0},{1,5},{5,1},{2,6},{6,2},{3,7},{7,3},{8,12},{12,8},{9,1... | collective-permute-start | bytes 393224 | tf_op jit(solution)/shard_map/ppermute | solution.py:32
  30.0 12.6 %copy-start.9 = (bf16[2048,128]{1,0:T(8,128)(2,1)}, bf16[2048,128]{1,0:T(8,128)(2,1)S(1)}, u32[]{:S(2)}) copy-start(bf16[2048,128]{1,0:T(8,128)(2,1)S(1)} %collective-permute-done.4.gate_par) | copy-start | bytes 1572868
  31.7 103.2 %copy-start.4 = (bf16[128,512]{1,0:T(8,128)(2,1)}, bf16[128,512]{1,0:T(8,128)(2,1)S(1)}, u32[]{:S(2)}) copy-start(bf16[128,512]{1,0:T(8,128)(2,1)S(1)} %get-tuple-element.37.hidden_ref) | copy-start | bytes 393220
  31.7 36.0 %all-to-all-start = ((bf16[32,20,512]{2,1,0:T(8,128)(2,1)}), bf16[32,20,512]{2,1,0:T(8,128)(2,1)}, u32[]{:S(2)}, u32[]{:S(2)}) async-start(bf16[32,20,512]{2,1,0:T(8,128)(2,1)} %get-tuple-element.38), calls=%async_computation | async-start | bytes 1572864 | tf_op jit(solution)/shard_map/all_to_all | solution.py:384
  42.6 57.8 %copy-start.1 = (bf16[2,2048,128]{2,1,0:T(8,128)(2,1)S(1)}, bf16[2,2048,128]{2,1,0:T(8,128)(2,1)}, u32[]{:S(2)}) copy-start(bf16[2,2048,128]{2,1,0:T(8,128)(2,1)} %gate_hbm.1) | copy-start | bytes 3145732
  44.8 7.9 %collective-permute-start.14 = (bf16[2,128,512]{2,1,0:T(8,128)(2,1)}, bf16[2,128,512]{2,1,0:T(8,128)(2,1)S(1)}, u32[]{:S(2)}, u32[]{:S(2)}) collective-permute-start(bf16[2,128,512]{2,1,0:T(8,128)(2,1)} %get-tuple-element.61), channel_id=1, source_target_pairs={{0,3},{1,0},{2,1},{3,2},{4,7},{5,4},{6,5},{7,6},{8,11},{9,8},{10,9... | collective-permute-start | bytes 786440 | tf_op jit(solution)/shard_map/ppermute | solution.py:28
  45.9 21.8 %collective-permute-start.8 = (bf16[2048,128]{1,0:T(8,128)(2,1)}, bf16[2048,128]{1,0:T(8,128)(2,1)}, u32[]{:S(2)}, u32[]{:S(2)}) collective-permute-start(bf16[2048,128]{1,0:T(8,128)(2,1)} %dynamic-slice_bitcast_fusion), channel_id=1, source_target_pairs={{0,4},{4,0},{1,5},{5,1},{2,6},{6,2},{3,7},{7,3},{8,12},{12,8},{9,1... | collective-permute-start | bytes 1572872 | tf_op jit(solution)/shard_map/ppermute | solution.py:32
  47.6 8.8 %collective-permute-start.13 = (bf16[2,128,512]{2,1,0:T(8,128)(2,1)}, bf16[2,128,512]{2,1,0:T(8,128)(2,1)S(1)}, u32[]{:S(2)}, u32[]{:S(2)}) collective-permute-start(bf16[2,128,512]{2,1,0:T(8,128)(2,1)} %get-tuple-element.59), channel_id=1, source_target_pairs={{0,2},{1,3},{2,0},{3,1},{4,6},{5,7},{6,4},{7,5},{8,10},{9,11},{10,... | collective-permute-start | bytes 786440 | tf_op jit(solution)/shard_map/ppermute | solution.py:28
  48.0 15.3 %collective-permute-start.12 = (bf16[2,128,512]{2,1,0:T(8,128)(2,1)}, bf16[2,128,512]{2,1,0:T(8,128)(2,1)}, u32[]{:S(2)}, u32[]{:S(2)}) collective-permute-start(bf16[2,128,512]{2,1,0:T(8,128)(2,1)} %get-tuple-element.60), channel_id=1, source_target_pairs={{0,1},{1,2},{2,3},{3,0},{4,5},{5,6},{6,7},{7,4},{8,9},{9,10},{10,1... | collective-permute-start | bytes 786440 | tf_op jit(solution)/shard_map/ppermute | solution.py:28
  52.7 15.0 %copy-start.5 = (bf16[2,128,512]{2,1,0:T(8,128)(2,1)}, bf16[2,128,512]{2,1,0:T(8,128)(2,1)S(1)}, u32[]{:S(2)}) copy-start(bf16[2,128,512]{2,1,0:T(8,128)(2,1)S(1)} %collective-permute-done.14.w3) | copy-start | bytes 786436
  56.5 11.2 %copy-start.7 = (bf16[2,128,512]{2,1,0:T(8,128)(2,1)}, bf16[2,128,512]{2,1,0:T(8,128)(2,1)S(1)}, u32[]{:S(2)}) copy-start(bf16[2,128,512]{2,1,0:T(8,128)(2,1)S(1)} %collective-permute-done.13.w2) | copy-start | bytes 786436
  69.0 31.0 %collective-permute-start.9 = (bf16[640,512]{1,0:T(8,128)(2,1)S(1)}, bf16[640,512]{1,0:T(8,128)(2,1)S(1)}, u32[]{:S(2)}, u32[]{:S(2)}) collective-permute-start(bf16[640,512]{1,0:T(8,128)(2,1)S(1)} %reshape.53.x0), channel_id=1, source_target_pairs={{0,1},{1,2},{2,3},{3,0},{4,5},{5,6},{6,7},{7,4},{8,9},{9,10},{10,1... | collective-permute-start | bytes 1966088 | tf_op jit(solution)/shard_map/ppermute | solution.py:28
  69.1 30.9 %collective-permute-start.10 = (bf16[640,512]{1,0:T(8,128)(2,1)S(1)}, bf16[640,512]{1,0:T(8,128)(2,1)S(1)}, u32[]{:S(2)}, u32[]{:S(2)}) collective-permute-start(bf16[640,512]{1,0:T(8,128)(2,1)S(1)} %reshape.53.x0), channel_id=1, source_target_pairs={{0,2},{1,3},{2,0},{3,1},{4,6},{5,7},{6,4},{7,5},{8,10},{9,11},{10,... | collective-permute-start | bytes 1966088 | tf_op jit(solution)/shard_map/ppermute | solution.py:28
  70.5 29.8 %collective-permute-start.11 = (bf16[640,512]{1,0:T(8,128)(2,1)S(1)}, bf16[640,512]{1,0:T(8,128)(2,1)S(1)}, u32[]{:S(2)}, u32[]{:S(2)}) collective-permute-start(bf16[640,512]{1,0:T(8,128)(2,1)S(1)} %reshape.53.x0), channel_id=1, source_target_pairs={{0,3},{1,0},{2,1},{3,2},{4,7},{5,4},{6,5},{7,6},{8,11},{9,8},{10,9... | collective-permute-start | bytes 1966088 | tf_op jit(solution)/shard_map/ppermute | solution.py:28
  72.9 50.0 %copy-start.6 = (bf16[2,128,512]{2,1,0:T(8,128)(2,1)S(1)}, bf16[2,128,512]{2,1,0:T(8,128)(2,1)}, u32[]{:S(2)}) copy-start(bf16[2,128,512]{2,1,0:T(8,128)(2,1)} %copy-done.5) | copy-start | bytes 786436
  72.9 50.0 %copy-start.8 = (bf16[2,128,512]{2,1,0:T(8,128)(2,1)S(1)}, bf16[2,128,512]{2,1,0:T(8,128)(2,1)}, u32[]{:S(2)}) copy-start(bf16[2,128,512]{2,1,0:T(8,128)(2,1)} %copy-done.7) | copy-start | bytes 786436
  72.9 31.8 %collective-permute-start.15 = (bf16[4,128,512]{2,1,0:T(8,128)(2,1)S(1)}, bf16[4,128,512]{2,1,0:T(8,128)(2,1)S(1)}, u32[]{:S(2)}, u32[]{:S(2)}) collective-permute-start(bf16[4,128,512]{2,1,0:T(8,128)(2,1)S(1)} %pad_maximum_fusion), channel_id=1, source_target_pairs={{0,4},{4,0},{1,5},{5,1},{2,6},{6,2},{3,7},{7,3},{8,12},{12,8},{9,1... | collective-permute-start | bytes 1572872 | tf_op jit(solution)/shard_map/ppermute | solution.py:32
  104.7 9.3 %collective-permute-start.16 = (bf16[640,256]{1,0:T(8,128)(2,1)S(1)}, bf16[640,256]{1,0:T(8,128)(2,1)S(1)}, u32[]{:S(2)}, u32[]{:S(2)}) collective-permute-start(bf16[640,256]{1,0:T(8,128)(2,1)S(1)} %gate_up.1.a0), channel_id=1, source_target_pairs={{0,1},{1,2},{2,3},{3,0},{4,5},{5,6},{6,7},{7,4},{8,9},{9,10},{10,1... | collective-permute-start | bytes 983048 | tf_op jit(solution)/shard_map/ppermute | solution.py:28
  106.0 16.9 %collective-permute-start.17 = (bf16[640,256]{1,0:T(8,128)(2,1)S(1)}, bf16[640,256]{1,0:T(8,128)(2,1)S(1)}, u32[]{:S(2)}, u32[]{:S(2)}) collective-permute-start(bf16[640,256]{1,0:T(8,128)(2,1)S(1)} %gate_up.1.a0), channel_id=1, source_target_pairs={{0,2},{1,3},{2,0},{3,1},{4,6},{5,7},{6,4},{7,5},{8,10},{9,11},{10,... | collective-permute-start | bytes 983048 | tf_op jit(solution)/shard_map/ppermute | solution.py:28
  109.0 14.0 %collective-permute-start.18 = (bf16[640,256]{1,0:T(8,128)(2,1)S(1)}, bf16[640,256]{1,0:T(8,128)(2,1)S(1)}, u32[]{:S(2)}, u32[]{:S(2)}) collective-permute-start(bf16[640,256]{1,0:T(8,128)(2,1)S(1)} %gate_up.1.a0), channel_id=1, source_target_pairs={{0,3},{1,0},{2,1},{3,2},{4,7},{5,4},{6,5},{7,6},{8,11},{9,8},{10,9... | collective-permute-start | bytes 983048 | tf_op jit(solution)/shard_map/ppermute | solution.py:28
  126.6 30.7 %all-to-all-start.1 = ((bf16[32,20,512]{2,1,0:T(8,128)(2,1)}), bf16[32,20,512]{2,1,0:T(8,128)(2,1)S(1)}, u32[]{:S(2)}, u32[]{:S(2)}) async-start(bf16[32,20,512]{2,1,0:T(8,128)(2,1)} %down.1), calls=%async_computation.1 | async-start | bytes 1572864 | tf_op jit(solution)/shard_map/all_to_all | solution.py:409
  134.7 45.9 %copy-start.24 = (s32[32,3]{0,1:T(4,128)S(1)}, s32[32,3]{0,1:T(4,128)}, u32[]{:S(2)}) copy-start(s32[32,3]{0,1:T(4,128)} %param.16) | copy-start | bytes 1156
  134.7 46.4 %copy-start.26 = (s32[1,16]{1,0:T(1,128)S(1)}, s32[1,16]{1,0:T(1,128)}, u32[]{:S(2)}) copy-start(s32[1,16]{1,0:T(1,128)} %param.29) | copy-start | bytes 196
  134.8 50.3 %copy-start.25 = (s32[1,1024]{1,0:T(1,128)S(1)}, s32[1,1024]{1,0:T(1,128)}, u32[]{:S(2)}) copy-start(s32[1,1024]{1,0:T(1,128)} %param.28) | copy-start | bytes 12292
  135.1 3.5 %collective-permute-start.7 = (f32[128,128]{0,1:T(8,128)S(1)}, f32[128,128]{0,1:T(8,128)S(1)}, u32[]{:S(2)}, u32[]{:S(2)}) collective-permute-start(f32[128,128]{0,1:T(8,128)S(1)} %pad_maximum_fusion.1), channel_id=1, source_target_pairs={{0,3},{1,0},{2,1},{3,2},{4,7},{5,4},{6,5},{7,6},{8,11},{9,8},{10,9... | collective-permute-start | bytes 196616 | tf_op jit(solution)/shard_map/ppermute | solution.py:28
  137.0 4.7 %collective-permute-start.6 = (f32[128,128]{0,1:T(8,128)S(1)}, f32[128,128]{0,1:T(8,128)S(1)}, u32[]{:S(2)}, u32[]{:S(2)}) collective-permute-start(f32[128,128]{0,1:T(8,128)S(1)} %pad_maximum_fusion.1), channel_id=1, source_target_pairs={{0,2},{1,3},{2,0},{3,1},{4,6},{5,7},{6,4},{7,5},{8,10},{9,11},{10,... | collective-permute-start | bytes 196616 | tf_op jit(solution)/shard_map/ppermute | solution.py:28
  137.1 5.8 %collective-permute-start.5 = (f32[128,128]{0,1:T(8,128)S(1)}, f32[128,128]{0,1:T(8,128)S(1)}, u32[]{:S(2)}, u32[]{:S(2)}) collective-permute-start(f32[128,128]{0,1:T(8,128)S(1)} %pad_maximum_fusion.1), channel_id=1, source_target_pairs={{0,1},{1,2},{2,3},{3,0},{4,5},{5,6},{6,7},{7,4},{8,9},{9,10},{10,1... | collective-permute-start | bytes 196616 | tf_op jit(solution)/shard_map/ppermute | solution.py:28
  158.3 5.4 %collective-permute-start.19 = (bf16[128,512]{1,0:T(8,128)(2,1)S(1)}, bf16[128,512]{1,0:T(8,128)(2,1)S(1)}, u32[]{:S(2)}, u32[]{:S(2)}) collective-permute-start(bf16[128,512]{1,0:T(8,128)(2,1)S(1)} %fusion.1.moe_ref), channel_id=1, source_target_pairs={{0,4},{4,0},{1,5},{5,1},{2,6},{6,2},{3,7},{7,3},{8,12},{12,8},{9,1... | collective-permute-start | bytes 393224 | tf_op jit(solution)/shard_map/ppermute | solution.py:32
  166.4 4.6 %collective-permute-start.20 = (f32[136,128]{1,0:T(8,128)}, f32[136,128]{1,0:T(8,128)S(1)}, u32[]{:S(2)}, u32[]{:S(2)}) collective-permute-start(f32[136,128]{1,0:T(8,128)} %get-tuple-element.44.p0), channel_id=1, source_target_pairs={{0,1},{1,2},{2,3},{3,0},{4,5},{5,6},{6,7},{7,4},{8,9},{9,10},{10,1... | collective-permute-start | bytes 208904 | tf_op jit(solution)/shard_map/ppermute | solution.py:28
  166.6 5.6 %collective-permute-start.21 = (f32[136,128]{1,0:T(8,128)}, f32[136,128]{1,0:T(8,128)S(1)}, u32[]{:S(2)}, u32[]{:S(2)}) collective-permute-start(f32[136,128]{1,0:T(8,128)} %get-tuple-element.44.p0), channel_id=1, source_target_pairs={{0,2},{1,3},{2,0},{3,1},{4,6},{5,7},{6,4},{7,5},{8,10},{9,11},{10,... | collective-permute-start | bytes 208904 | tf_op jit(solution)/shard_map/ppermute | solution.py:28
  169.5 3.4 %collective-permute-start.22 = (f32[136,128]{1,0:T(8,128)}, f32[136,128]{1,0:T(8,128)S(1)}, u32[]{:S(2)}, u32[]{:S(2)}) collective-permute-start(f32[136,128]{1,0:T(8,128)} %get-tuple-element.44.p0), channel_id=1, source_target_pairs={{0,3},{1,0},{2,1},{3,2},{4,7},{5,4},{6,5},{7,6},{8,11},{9,8},{10,9... | collective-permute-start | bytes 208904 | tf_op jit(solution)/shard_map/ppermute | solution.py:28
  175.5 19.1 %all-to-all-start.2 = ((bf16[16,128,128]{2,1,0:T(8,128)(2,1)}), bf16[16,128,128]{2,1,0:T(8,128)(2,1)S(1)}, u32[]{:S(2)}, u32[]{:S(2)}) async-start(bf16[16,128,128]{2,1,0:T(8,128)(2,1)} %vectors.1), calls=%async_computation.2 | async-start | bytes 1048576 | tf_op jit(solution)/shard_map/all_to_all | solution.py:461
  181.2 6.9 %collective-permute-start.23 = (bf16[128,512]{1,0:T(8,128)(2,1)}, bf16[128,512]{1,0:T(8,128)(2,1)S(1)}, u32[]{:S(2)}, u32[]{:S(2)}) collective-permute-start(bf16[128,512]{1,0:T(8,128)(2,1)} %get-tuple-element.48.p0), channel_id=1, source_target_pairs={{0,1},{1,2},{2,3},{3,0},{4,5},{5,6},{6,7},{7,4},{8,9},{9,10},{10,1... | collective-permute-start | bytes 393224 | tf_op jit(solution)/shard_map/ppermute | solution.py:28
  181.7 6.4 %collective-permute-start.24 = (bf16[128,512]{1,0:T(8,128)(2,1)}, bf16[128,512]{1,0:T(8,128)(2,1)S(1)}, u32[]{:S(2)}, u32[]{:S(2)}) collective-permute-start(bf16[128,512]{1,0:T(8,128)(2,1)} %get-tuple-element.48.p0), channel_id=1, source_target_pairs={{0,2},{1,3},{2,0},{3,1},{4,6},{5,7},{6,4},{7,5},{8,10},{9,11},{10,... | collective-permute-start | bytes 393224 | tf_op jit(solution)/shard_map/ppermute | solution.py:28
  183.8 5.2 %collective-permute-start.25 = (bf16[128,512]{1,0:T(8,128)(2,1)}, bf16[128,512]{1,0:T(8,128)(2,1)S(1)}, u32[]{:S(2)}, u32[]{:S(2)}) collective-permute-start(bf16[128,512]{1,0:T(8,128)(2,1)} %get-tuple-element.48.p0), channel_id=1, source_target_pairs={{0,3},{1,0},{2,1},{3,2},{4,7},{5,4},{6,5},{7,6},{8,11},{9,8},{10,9... | collective-permute-start | bytes 393224 | tf_op jit(solution)/shard_map/ppermute | solution.py:28
  188.1 10.9 %copy-start.18 = (bf16[128,512]{1,0:T(8,128)(2,1)}, bf16[128,512]{1,0:T(8,128)(2,1)S(1)}, u32[]{:S(2)}) copy-start(bf16[128,512]{1,0:T(8,128)(2,1)S(1)} %collective-permute-done.23.p1) | copy-start | bytes 393220
  188.1 10.9 %copy-start.19 = (bf16[128,512]{1,0:T(8,128)(2,1)}, bf16[128,512]{1,0:T(8,128)(2,1)S(1)}, u32[]{:S(2)}) copy-start(bf16[128,512]{1,0:T(8,128)(2,1)S(1)} %collective-permute-done.24.p2) | copy-start | bytes 393220
  189.0 10.1 %copy-start.20 = (bf16[128,512]{1,0:T(8,128)(2,1)}, bf16[128,512]{1,0:T(8,128)(2,1)S(1)}, u32[]{:S(2)}) copy-start(bf16[128,512]{1,0:T(8,128)(2,1)S(1)} %collective-permute-done.25.p3) | copy-start | bytes 393220
  194.6 6.3 %collective-permute-start.26 = (bf16[2048,128]{1,0:T(8,128)(2,1)S(1)}, bf16[2048,128]{1,0:T(8,128)(2,1)S(1)}, u32[]{:S(2)}, u32[]{:S(2)}) collective-permute-start(bf16[2048,128]{1,0:T(8,128)(2,1)S(1)} %bitcast.36), channel_id=1, source_target_pairs={{0,8},{8,0},{1,9},{9,1},{2,10},{10,2},{3,11},{11,3},{4,12},{12,4},... | collective-permute-start | bytes 1572872 | tf_op jit(solution)/shard_map/ppermute | solution.py:475
  (9 other events, 26.4 us)

commit v6 on v5

--- a/solution.py
+++ b/solution.py
@@ -14,7 +14,7 @@
 EXPERTS = 64
 WIDE = 32
 GROUPS = ((0, 20),)
-SPLIT = ((0, 20),)
+HALF = WIDE * CAP // 2
 EPS = 1e-06
 THETA = 50000.0
 NEG = -1e30
@@ -178,10 +178,12 @@
         out_ref[:, at : at + 128] = (gate / (1.0 + jnp.exp(-gate)) * up).astype(bf16)
 
 
-def down_kernel(here_ref, a0, a1, a2, a3, w0, w1, w2, w3, par_ref, out_ref, w_ref, sems):
+def down_kernel(here_ref, *refs):
+    acts, weights, par_ref = refs[:8], refs[8:12], refs[12]
+    out_ref, w_ref, sems = refs[13:]
     i = here_ref[0]
     copies = []
-    for k, w in enumerate((w0, w1, w2, w3)):
+    for k, w in enumerate(weights):
         copies.append(
             (
                 pltpu.make_async_copy(w.at[i], w_ref.at[k, 0:128], sems.at[0, k]),
@@ -191,14 +193,17 @@
     for pair in copies:
         for copy in pair:
             copy.start()
-    total = jnp.zeros((a0.shape[0], 512), f32)
-    for k, a in enumerate((a0, a1, a2, a3)):
-        for copy in copies[k]:
-            copy.wait()
-        total = total + jnp.dot(a[...], w_ref[k], preferred_element_type=f32)
-    size = out_ref.shape[1]
-    for s in range(WIDE):
-        out_ref[s] = total[s * size : (s + 1) * size].astype(bf16)
+    for half in range(2):
+        total = jnp.zeros((HALF, 512), f32)
+        for k in range(4):
+            if half == 0:
+                for copy in copies[k]:
+                    copy.wait()
+            total = total + jnp.dot(
+                acts[4 * half + k][...], w_ref[k], preferred_element_type=f32
+            )
+        for s in range(WIDE // 2):
+            out_ref[half * (WIDE // 2) + s] = total[s * CAP : (s + 1) * CAP].astype(bf16)
 
 
 def embed_kernel(here_ref, hidden_ref, moe_ref, par_ref, gain_ref, w_ref, layer_ref, part_ref):
@@ -380,33 +385,38 @@
         name="dispatch",
     )(here, tokens, attn, attn_par, *chooses)
 
-    backs = []
     arrived = lax.all_to_all(rows[0], W, 0, 0, tiled=True)
-    arrived, up_par = lax.optimization_barrier((arrived, up_par))
-    for g, (a, b) in enumerate(SPLIT):
-        size = b - a
-        x = arrived[:, a:b].reshape(WIDE * size, 512)
-        act = pl.pallas_call(
+    first = arrived[: WIDE // 2].reshape(HALF, 512)
+    second = arrived[WIDE // 2 :].reshape(HALF, 512)
+    gathered = [first] + [y_shift(first, k) for k in (1, 2, 3)]
+    others = [second] + [y_shift(second, k) for k in (1, 2, 3)]
+    gathered, others[1], others[3] = lax.optimization_barrier((gathered, others[1], others[3]))
+
+    def gate_up(xs):
+        return pl.pallas_call(
             gate_up_kernel,
-            out_shape=jax.ShapeDtypeStruct((WIDE * size, 256), bf16),
+            out_shape=jax.ShapeDtypeStruct((HALF, 256), bf16),
             in_specs=[smem()] + [vmem()] * 5 + [hbm()] * 4,
             out_specs=vmem(),
             scratch_shapes=[pltpu.VMEM((4, 2048, 128), bf16), pltpu.SemaphoreType.DMA((4,))],
             compiler_params=params(),
             name="gate_up",
-        )(here, x, *(y_shift(x, k) for k in (1, 2, 3)), norm_gains, w_gate, w_up, gate_par, up_par)
-        if g == 0:
-            act, down_par = lax.optimization_barrier((act, down_par))
-        out = pl.pallas_call(
-            down_kernel,
-            out_shape=jax.ShapeDtypeStruct((WIDE, size, 512), bf16),
-            in_specs=[smem()] + [vmem()] * 4 + [hbm()] * 5,
-            out_specs=vmem(),
-            scratch_shapes=[pltpu.VMEM((4, 256, 512), bf16), pltpu.SemaphoreType.DMA((2, 4))],
-            compiler_params=params(),
-            name="down",
-        )(here, act, *(y_shift(act, k) for k in (1, 2, 3)), *downs, down_par)
-        backs.append(lax.all_to_all(out, W, 0, 0, tiled=True))
+        )(here, *xs, norm_gains, w_gate, w_up, gate_par, up_par)
+
+    act = gate_up(gathered)
+    acts = [act] + [y_shift(act, k) for k in (1, 2, 3)]
+    act = gate_up(others)
+    acts += [act] + [y_shift(act, k) for k in (1, 2, 3)]
+    out = pl.pallas_call(
+        down_kernel,
+        out_shape=jax.ShapeDtypeStruct((WIDE, CAP, 512), bf16),
+        in_specs=[smem()] + [vmem()] * 8 + [hbm()] * 5,
+        out_specs=vmem(),
+        scratch_shapes=[pltpu.VMEM((4, 256, 512), bf16), pltpu.SemaphoreType.DMA((2, 4))],
+        compiler_params=params(),
+        name="down",
+    )(here, *acts, *downs, down_par)
+    back = lax.all_to_all(out, W, 0, 0, tiled=True)
 
     hf = hidden.astype(f32)
     gain_mine = lax.dynamic_slice_in_dim(norm_gains[1], j * 512, 512, 0)
@@ -429,12 +439,11 @@
 
     moe = jnp.zeros((TOK, 512), f32)
     contract = (((0, 1), (0, 1)), ((), ()))
-    for (a, b), back in zip(SPLIT, backs):
-        mixing = jnp.where(chosen[:, a:b], gates[:, None, :], 0.0)
-        mixing_hi = lax.reduce_precision(mixing, 8, 7)
-        mixing_lo = (mixing - mixing_hi).astype(bf16)
-        for matrix in (mixing_hi.astype(bf16), mixing_lo):
-            moe = moe + lax.dot_general(matrix, back, contract, preferred_element_type=f32)
+    mixing = jnp.where(chosen, gates[:, None, :], 0.0)
+    mixing_hi = lax.reduce_precision(mixing, 8, 7)
+    mixing_lo = (mixing - mixing_hi).astype(bf16)
+    for matrix in (mixing_hi.astype(bf16), mixing_lo):
+        moe = moe + lax.dot_general(matrix, back, contract, preferred_element_type=f32)
     moe = moe.astype(bf16)
     moe_par = x_swap(moe)
     layer, part = pl.pallas_call(
@@ -483,7 +492,7 @@
     doc_scores = pl.pallas_call(
         score_kernel,
         out_shape=jax.ShapeDtypeStruct((1, 16), f32),
-        in_specs=[smem(), vmem(), hbm(), hbm()],
+        in_specs=[smem(), vmem()] + [pl.BlockSpec(memory_space=pl.ANY)] * 2,
         out_specs=vmem(),
         scratch_shapes=[pltpu.VMEM((16, 128, 128), bf16), pltpu.SemaphoreType.DMA((16,))],
         name="score",

time: 206 us -> 212 us (1.029)
  waiting for transfers between devices: 102 us -> 79.7 us
  starting transfers between devices: 59.1 us -> 72.7 us
  local copies, waits for them, and re-layouts: 14.3 us -> 22.7 us
  Pallas kernels: 24 us -> 27.9 us
    ppermute x21 -> x27, waiting for transfers between devices: 70.3 us -> 39 us  [y_shift(): return lax.ppermute(x, 'y', [(s, (s + k) % 4) for s in range(4)])]
    all_to_all x1, waiting for transfers between devices: 0.01 us -> 12.1 us  [body(): arrived = lax.all_to_all(rows[0], W, 0, 0, tiled=True)]
    ppermute x21 -> x27, starting transfers between devices: 21.7 us -> 30.6 us  [y_shift(): return lax.ppermute(x, 'y', [(s, (s + k) % 4) for s in range(4)])]
    all_to_all x1, starting transfers between devices: 8.11 us -> 13.4 us  [body(): back = lax.all_to_all(out, W, 0, 0, tiled=True)]
    pallas_call x2 -> x3, Pallas kernels: 7 us -> 10.8 us  [the longest x2 6.53 us: gate_up(): pl.pallas_call(gate_up_kernel, out_shape=jax.ShapeDtypeStruct((HALF, 256)...]
    unnamed x55 -> x63, local copies, waits for them, and re-layouts: 3.33 us -> 6.52 us
    reshape x1 -> x2, local copies, waits for them, and re-layouts: 1.25 us -> 3.59 us  [the longest x1 1.8 us: body(): first = arrived[:WIDE // 2].reshape(HALF, 512)]
    ppermute x5, waiting for transfers between devices: 11.4 us -> 9.29 us  [x_swap(): return lax.ppermute(x, 'xh', [(0, 1), (1, 0)])]
  transfers between devices with their start and end apart: 30 -> 36, of which waited for: 23 -> 23; matrix products, arithmetic and copies ran while one was open for 6% -> 10% of each run, Pallas kernels for 5% -> 7%
where the time goes in v6:
time: 212 us; the launch traced here: 211 us
  waiting for transfers between devices  79.7 us (38%)
  starting transfers between devices  72.7 us (34%)
  Pallas kernels  27.9 us (13%)
  local copies, waits for them, and re-layouts  22.7 us (11%)
  other arithmetic  4.79 us (2%)
    ppermute x27, waiting for transfers between devices, y_shift(): return lax.ppermute(x, 'y', [(s, (s + k) % 4) for s in range(4)])  39 us
    ppermute x27, starting transfers between devices, y_shift(): return lax.ppermute(x, 'y', [(s, (s + k) % 4) for s in range(4)])  30.6 us
    all_to_all x1, starting transfers between devices, body(): back = lax.all_to_all(out, W, 0, 0, tiled=True)  13.4 us
    all_to_all x1, waiting for transfers between devices, body(): back = lax.all_to_all(out, W, 0, 0, tiled=True)  13.3 us
    all_to_all x1, waiting for transfers between devices, body(): arrived = lax.all_to_all(rows[0], W, 0, 0, tiled=True)  12.1 us
    all_to_all x1, starting transfers between devices, body(): arrived = lax.all_to_all(rows[0], W, 0, 0, tiled=True)  10.8 us
    ppermute x5, waiting for transfers between devices, x_swap(): return lax.ppermute(x, 'xh', [(0, 1), (1, 0)])  9.29 us
    ppermute x5, starting transfers between devices, x_swap(): return lax.ppermute(x, 'xh', [(0, 1), (1, 0)])  8.57 us
  transfers between devices with their start and end apart: 36, of which 23 were waited for; matrix products, arithmetic and copies ran while one was open for 10% of the time, Pallas kernels for 7%

profile of v6, /device:TPU:1, one launch (start us, length us, event | category | flops | bytes accessed | tf_op | source)
XLA Modules:
  0.0 211.0 jit_solution(6317336031338901383)
XLA Ops:
  0.7 1.9 dynamic-slice_bitcast_fusion.1
  2.6 3.6 %collective-permute-start.4 = (bf16[2048,128]{1,0:T(8,128)(2,1)}, bf16[2048,128]{1,0:T(8,128)(2,1)S(1)}, u32[]{:S(2)}, u32[]{:S(2)}) collective-permute-start(bf16[2048,128]{1,0:T(8,128)(2,1)} %dynamic-slice_bitcast_fusion.1), channel_id=1, source_target_pairs={{0,4},{4,0},{1,5},{5,1},{2,6},{6,2},{3,7},{7,3},{8,12},{12,8},{9,1... | collective-permute-start | bytes 1572872 | tf_op jit(solution)/shard_map/ppermute | solution.py:32
  6.8 5.2 %attention.1 = (bf16[128,512]{1,0:T(8,128)(2,1)}, bf16[128,512]{1,0:T(8,128)(2,1)}, bf16[128,512]{1,0:T(8,128)(2,1)}, bf16[128,512]{1,0:T(8,128)(2,1)}) custom-call(s32[4]{0:T(128)} %pad_add_fusion.here_ref, s32[3,32]{1,0:T(4,128)} %bitcast.39, f32[2,256]{1,0:T(2,128)} %qk_ref.1, f32[3,2048]{1,0:T(4,128)} %gain_ref.7, bf16[128,2048]{1,0:T(8,128)(2,1)} %x_ref, ...), custom_call_target="tpu_custom_call" | custom-call | tf_op jit(solution)/shard_map/attention/pallas_call | solution.py:328
  12.0 2.8 %collective-permute-start.2 = (bf16[128,512]{1,0:T(8,128)(2,1)}, bf16[128,512]{1,0:T(8,128)(2,1)S(1)}, u32[]{:S(2)}, u32[]{:S(2)}) collective-permute-start(bf16[128,512]{1,0:T(8,128)(2,1)} %get-tuple-element.34), channel_id=1, source_target_pairs={{0,3},{1,0},{2,1},{3,2},{4,7},{5,4},{6,5},{7,6},{8,11},{9,8},{10,9... | collective-permute-start | bytes 393224 | tf_op jit(solution)/shard_map/ppermute | solution.py:28
  16.8 3.2 %collective-permute-done.2 = bf16[128,512]{1,0:T(8,128)(2,1)S(1)} collective-permute-done((bf16[128,512]{1,0:T(8,128)(2,1)}, bf16[128,512]{1,0:T(8,128)(2,1)S(1)}, u32[]{:S(2)}, u32[]{:S(2)}) %collective-permute-start.2) | collective-permute-done | bytes 131104 | tf_op jit(solution)/shard_map/ppermute | solution.py:28
  20.5 3.8 %collective-permute-done = bf16[128,512]{1,0:T(8,128)(2,1)S(1)} collective-permute-done((bf16[128,512]{1,0:T(8,128)(2,1)}, bf16[128,512]{1,0:T(8,128)(2,1)S(1)}, u32[]{:S(2)}, u32[]{:S(2)}) %collective-permute-start) | collective-permute-done | bytes 131104 | tf_op jit(solution)/shard_map/ppermute | solution.py:28
  25.6 5.1 %collective-permute-done.3.par_ref = bf16[128,512]{1,0:T(8,128)(2,1)S(1)} collective-permute-done((bf16[128,512]{1,0:T(8,128)(2,1)S(1)}, bf16[128,512]{1,0:T(8,128)(2,1)S(1)}, u32[]{:S(2)}, u32[]{:S(2)}) %collective-permute-start.3) | collective-permute-done | bytes 131104 | tf_op jit(solution)/shard_map/ppermute | solution.py:32
  30.7 1.8 dispatch.1
  32.5 10.8 %all-to-all-start = ((bf16[32,20,512]{2,1,0:T(8,128)(2,1)}), bf16[32,20,512]{2,1,0:T(8,128)(2,1)}, u32[]{:S(2)}, u32[]{:S(2)}) async-start(bf16[32,20,512]{2,1,0:T(8,128)(2,1)} %get-tuple-element.40), calls=%async_computation | async-start | bytes 1572864 | tf_op jit(solution)/shard_map/all_to_all | solution.py:388
  45.5 1.7 collective-permute-start.13
  48.8 1.7 constant_dynamic-slice_fusion.3
  50.4 1.9 collective-permute-done.23.refs_11_
  52.3 1.6 constant_dynamic-slice_fusion
  53.9 12.1 %all-to-all-done = bf16[32,20,512]{2,1,0:T(8,128)(2,1)} async-done(((bf16[32,20,512]{2,1,0:T(8,128)(2,1)}), bf16[32,20,512]{2,1,0:T(8,128)(2,1)}, u32[]{:S(2)}, u32[]{:S(2)}) %all-to-all-start) | async-done | bytes 655392 | tf_op jit(solution)/shard_map/all_to_all | solution.py:388
  66.0 2.1 fusion.39
  68.1 1.8 reshape.56.x0
  69.9 1.5 collective-permute-start.9
  74.5 1.9 pad_maximum_fusion
  76.4 1.7 collective-permute-start.24
  78.1 1.8 reshape.57.x0
  80.7 4.7 %collective-permute-done.9.x2 = bf16[320,512]{1,0:T(8,128)(2,1)} collective-permute-done((bf16[320,512]{1,0:T(8,128)(2,1)}, bf16[320,512]{1,0:T(8,128)(2,1)}, u32[]{:S(2)}, u32[]{:S(2)}) %collective-permute-start.9) | collective-permute-done | bytes 327712 | tf_op jit(solution)/shard_map/ppermute | solution.py:28
  85.5 2.1 %collective-permute-done.10.x3 = bf16[320,512]{1,0:T(8,128)(2,1)} collective-permute-done((bf16[320,512]{1,0:T(8,128)(2,1)}, bf16[320,512]{1,0:T(8,128)(2,1)}, u32[]{:S(2)}, u32[]{:S(2)}) %collective-permute-start.10) | collective-permute-done | bytes 327712 | tf_op jit(solution)/shard_map/ppermute | solution.py:28
  89.8 1.9 collective-permute-done.11.x1
  93.9 3.3 %gate_up.2.refs_0_ = bf16[320,256]{1,0:T(8,128)(2,1)} custom-call(s32[4]{0:T(128)S(1)} %copy-done.11, bf16[320,512]{1,0:T(8,128)(2,1)S(1)} %copy-done.4, bf16[320,512]{1,0:T(8,128)(2,1)} %collective-permute-done.8.x1, bf16[320,512]{1,0:T(8,128)(2,1)} %collective-permute-done.9.x2, bf16[320,512]{1,0:T(8,128)(2,1)} %collective-permute-done.10.x3, ...), custom_call_target="tpu_custom_call" | custom-call | tf_op jit(solution)/shard_map/gate_up/pallas_call | solution.py:396
  97.2 3.6 %collective-permute-start.14 = (bf16[320,256]{1,0:T(8,128)(2,1)}, bf16[320,256]{1,0:T(8,128)(2,1)S(1)}, u32[]{:S(2)}, u32[]{:S(2)}) collective-permute-start(bf16[320,256]{1,0:T(8,128)(2,1)} %gate_up.2.refs_0_), channel_id=1, source_target_pairs={{0,1},{1,2},{2,3},{3,0},{4,5},{5,6},{6,7},{7,4},{8,9},{9,10},{10,1... | collective-permute-start | bytes 491528 | tf_op jit(solution)/shard_map/ppermute | solution.py:28
  101.3 2.9 %collective-permute-start.15 = (bf16[320,256]{1,0:T(8,128)(2,1)}, bf16[320,256]{1,0:T(8,128)(2,1)}, u32[]{:S(2)}, u32[]{:S(2)}) collective-permute-start(bf16[320,256]{1,0:T(8,128)(2,1)} %gate_up.2.refs_0_), channel_id=1, source_target_pairs={{0,2},{1,3},{2,0},{3,1},{4,6},{5,7},{6,4},{7,5},{8,10},{9,11},{10,... | collective-permute-start | bytes 491528 | tf_op jit(solution)/shard_map/ppermute | solution.py:28
  104.2 2.1 collective-permute-start.16
  106.3 3.3 %gate_up.3.refs_4_ = bf16[320,256]{1,0:T(8,128)(2,1)} custom-call(s32[4]{0:T(128)S(1)} %copy-done.11, bf16[320,512]{1,0:T(8,128)(2,1)S(1)} %copy-done.5, bf16[320,512]{1,0:T(8,128)(2,1)} %collective-permute-done.11.x1, bf16[320,512]{1,0:T(8,128)(2,1)} %collective-permute-done.17.x2, bf16[320,512]{1,0:T(8,128)(2,1)} %collective-permute-done.12.x3, ...), custom_call_target="tpu_custom_call" | custom-call | tf_op jit(solution)/shard_map/gate_up/pallas_call | solution.py:396
  111.5 1.5 collective-permute-start.20
  113.0 7.2 %collective-permute-done.18.refs_5_ = bf16[320,256]{1,0:T(8,128)(2,1)S(1)} collective-permute-done((bf16[320,256]{1,0:T(8,128)(2,1)}, bf16[320,256]{1,0:T(8,128)(2,1)S(1)}, u32[]{:S(2)}, u32[]{:S(2)}) %collective-permute-start.18) | collective-permute-done | bytes 163872 | tf_op jit(solution)/shard_map/ppermute | solution.py:28
  122.1 4.3 %down.1 = bf16[32,20,512]{2,1,0:T(8,128)(2,1)} custom-call(s32[4]{0:T(128)S(1)} %copy-done.11, bf16[320,256]{1,0:T(8,128)(2,1)} %gate_up.2.refs_0_, bf16[320,256]{1,0:T(8,128)(2,1)S(1)} %copy-done.10, bf16[320,256]{1,0:T(8,128)(2,1)} %collective-permute-done.15.refs_2_, bf16[320,256]{1,0:T(8,128)(2,1)} %collective-permute-done.16.refs_3_, ...), custom_call_target="tpu_custom_call" | custom-call | tf_op jit(solution)/shard_map/down/pallas_call | solution.py:410
  126.4 13.4 %all-to-all-start.1 = ((bf16[32,20,512]{2,1,0:T(8,128)(2,1)}), bf16[32,20,512]{2,1,0:T(8,128)(2,1)S(1)}, u32[]{:S(2)}, u32[]{:S(2)}) async-start(bf16[32,20,512]{2,1,0:T(8,128)(2,1)} %down.1), calls=%async_computation.1 | async-start | bytes 1572864 | tf_op jit(solution)/shard_map/all_to_all | solution.py:419
  140.2 2.5 %collective-permute-start.7 = (f32[128,128]{0,1:T(8,128)S(1)}, f32[128,128]{0,1:T(8,128)S(1)}, u32[]{:S(2)}, u32[]{:S(2)}) collective-permute-start(f32[128,128]{0,1:T(8,128)S(1)} %pad_maximum_fusion.1), channel_id=1, source_target_pairs={{0,3},{1,0},{2,1},{3,2},{4,7},{5,4},{6,5},{7,6},{8,11},{9,8},{10,9... | collective-permute-start | bytes 196616 | tf_op jit(solution)/shard_map/ppermute | solution.py:28
  144.0 3.6 %collective-permute-done.6 = f32[128,128]{0,1:T(8,128)S(1)} collective-permute-done((f32[128,128]{0,1:T(8,128)S(1)}, f32[128,128]{0,1:T(8,128)S(1)}, u32[]{:S(2)}, u32[]{:S(2)}) %collective-permute-start.6) | collective-permute-done | bytes 65568 | tf_op jit(solution)/shard_map/ppermute | solution.py:28
  149.1 13.3 %all-to-all-done.1 = bf16[32,20,512]{2,1,0:T(8,128)(2,1)S(1)} async-done(((bf16[32,20,512]{2,1,0:T(8,128)(2,1)}), bf16[32,20,512]{2,1,0:T(8,128)(2,1)S(1)}, u32[]{:S(2)}, u32[]{:S(2)}) %all-to-all-start.1) | async-done | bytes 655392 | tf_op jit(solution)/shard_map/all_to_all | solution.py:419
  164.6 4.2 %collective-permute-done.25.par_ref = bf16[128,512]{1,0:T(8,128)(2,1)S(1)} collective-permute-done((bf16[128,512]{1,0:T(8,128)(2,1)S(1)}, bf16[128,512]{1,0:T(8,128)(2,1)S(1)}, u32[]{:S(2)}, u32[]{:S(2)}) %collective-permute-start.25) | collective-permute-done | bytes 131104 | tf_op jit(solution)/shard_map/ppermute | solution.py:32
  169.4 2.1 %embed.1 = (bf16[128,512]{1,0:T(8,128)(2,1)}, f32[136,128]{1,0:T(8,128)}) custom-call(s32[4]{0:T(128)} %pad_add_fusion.here_ref, bf16[128,512]{1,0:T(8,128)(2,1)} %copy-done.6, bf16[128,512]{1,0:T(8,128)(2,1)} %copy-done.18, bf16[128,512]{1,0:T(8,128)(2,1)} %copy-done.19, f32[3,2048]{1,0:T(4,128)} %gain_ref.7, bf16[2048,128]{1,0:T(8,128)(2,1)} %w_ref.1), custom_call_target="tpu_custom_call" | custom-call | tf_op jit(solution)/shard_map/embed/pallas_call | solution.py:449
  172.3 2.8 %collective-permute-start.27 = (f32[136,128]{1,0:T(8,128)}, f32[136,128]{1,0:T(8,128)S(1)}, u32[]{:S(2)}, u32[]{:S(2)}) collective-permute-start(f32[136,128]{1,0:T(8,128)} %get-tuple-element.48.p0), channel_id=1, source_target_pairs={{0,2},{1,3},{2,0},{3,1},{4,6},{5,7},{6,4},{7,5},{8,10},{9,11},{10,... | collective-permute-start | bytes 208904 | tf_op jit(solution)/shard_map/ppermute | solution.py:28
  176.1 1.6 collective-permute-done.27.p2
  179.4 2.0 vectors.1
  181.4 4.9 %all-to-all-start.2 = ((bf16[16,128,128]{2,1,0:T(8,128)(2,1)}), bf16[16,128,128]{2,1,0:T(8,128)(2,1)S(1)}, u32[]{:S(2)}, u32[]{:S(2)}) async-start(bf16[16,128,128]{2,1,0:T(8,128)(2,1)} %vectors.1), calls=%async_computation.2 | async-start | bytes 1048576 | tf_op jit(solution)/shard_map/all_to_all | solution.py:470
  186.9 1.7 collective-permute-start.30
  188.6 1.7 collective-permute-start.31
  191.2 2.3 %collective-permute-done.29.p1 = bf16[128,512]{1,0:T(8,128)(2,1)S(1)} collective-permute-done((bf16[128,512]{1,0:T(8,128)(2,1)}, bf16[128,512]{1,0:T(8,128)(2,1)S(1)}, u32[]{:S(2)}, u32[]{:S(2)}) %collective-permute-start.29) | collective-permute-done | bytes 131104 | tf_op jit(solution)/shard_map/ppermute | solution.py:28
  194.4 5.9 %all-to-all-done.2 = bf16[16,128,128]{2,1,0:T(8,128)(2,1)S(1)} async-done(((bf16[16,128,128]{2,1,0:T(8,128)(2,1)}), bf16[16,128,128]{2,1,0:T(8,128)(2,1)S(1)}, u32[]{:S(2)}, u32[]{:S(2)}) %all-to-all-start.2) | async-done | bytes 524320 | tf_op jit(solution)/shard_map/all_to_all | solution.py:470
  200.4 4.4 %collective-permute-start.32 = (bf16[2048,128]{1,0:T(8,128)(2,1)S(1)}, bf16[2048,128]{1,0:T(8,128)(2,1)S(1)}, u32[]{:S(2)}, u32[]{:S(2)}) collective-permute-start(bf16[2048,128]{1,0:T(8,128)(2,1)S(1)} %bitcast.36), channel_id=1, source_target_pairs={{0,8},{8,0},{1,9},{9,1},{2,10},{10,2},{3,11},{11,3},{4,12},{12,4},... | collective-permute-start | bytes 1572872 | tf_op jit(solution)/shard_map/ppermute | solution.py:484
  204.8 1.9 assemble.1
  207.6 3.2 %score.1 = f32[1,16]{1,0:T(1,128)} custom-call(s32[5,16]{1,0:T(8,128)} %stack.48.info_ref, bf16[1024,128]{1,0:T(8,128)(2,1)} %doc_ref.1, bf16[2048,128]{1,0:T(8,128)(2,1)} %bitcast.37, bf16[2048,128]{1,0:T(8,128)(2,1)} %copy-done.15), custom_call_target="tpu_custom_call" | custom-call | tf_op jit(solution)/shard_map/score/pallas_call | solution.py:492
  (139 shorter events, 33.4 us)
Async XLA Ops:
  0.6 139.2 %copy-start = (bf16[2048,64]{0,1:T(8,128)(2,1)S(1)}, bf16[2048,64]{0,1:T(8,128)(2,1)}, u32[]{:S(2)}) copy-start(bf16[2048,64]{0,1:T(8,128)(2,1)} %param.21) | copy-start | bytes 786436
  0.6 15.2 %copy-start.12 = (s32[128,8]{0,1:T(8,128)S(1)}, s32[128,8]{0,1:T(8,128)}, u32[]{:S(2)}) copy-start(s32[128,8]{0,1:T(8,128)} %param.22) | copy-start | bytes 12292
  0.7 30.1 %copy-start.3 = (bf16[128,2048]{1,0:T(8,128)(2,1)S(1)}, bf16[128,2048]{1,0:T(8,128)(2,1)}, u32[]{:S(2)}) copy-start(bf16[128,2048]{1,0:T(8,128)(2,1)} %x_ref) | copy-start | bytes 1572868
  2.6 28.1 %collective-permute-start.4 = (bf16[2048,128]{1,0:T(8,128)(2,1)}, bf16[2048,128]{1,0:T(8,128)(2,1)S(1)}, u32[]{:S(2)}, u32[]{:S(2)}) collective-permute-start(bf16[2048,128]{1,0:T(8,128)(2,1)} %dynamic-slice_bitcast_fusion.1), channel_id=1, source_target_pairs={{0,4},{4,0},{1,5},{5,1},{2,6},{6,2},{3,7},{7,3},{8,12},{12,8},{9,1... | collective-permute-start | bytes 1572872 | tf_op jit(solution)/shard_map/ppermute | solution.py:32
  6.8 36.5 %copy-start.14 = (bf16[2,128,2048]{2,1,0:T(8,128)(2,1)S(1)}, bf16[2,128,2048]{2,1,0:T(8,128)(2,1)}, u32[]{:S(2)}) copy-start(bf16[2,128,2048]{2,1,0:T(8,128)(2,1)} %param.25) | copy-start | bytes 3145732
  12.0 32.6 %copy-start.2 = (bf16[2,2048,128]{2,1,0:T(8,128)(2,1)S(1)}, bf16[2,2048,128]{2,1,0:T(8,128)(2,1)}, u32[]{:S(2)}) copy-start(bf16[2,2048,128]{2,1,0:T(8,128)(2,1)} %up_hbm.3) | copy-start | bytes 3145732
  12.0 8.0 %collective-permute-start.2 = (bf16[128,512]{1,0:T(8,128)(2,1)}, bf16[128,512]{1,0:T(8,128)(2,1)S(1)}, u32[]{:S(2)}, u32[]{:S(2)}) collective-permute-start(bf16[128,512]{1,0:T(8,128)(2,1)} %get-tuple-element.34), channel_id=1, source_target_pairs={{0,3},{1,0},{2,1},{3,2},{4,7},{5,4},{6,5},{7,6},{8,11},{9,8},{10,9... | collective-permute-start | bytes 393224 | tf_op jit(solution)/shard_map/ppermute | solution.py:28
  14.8 5.6 %collective-permute-start.1 = (bf16[128,512]{1,0:T(8,128)(2,1)}, bf16[128,512]{1,0:T(8,128)(2,1)S(1)}, u32[]{:S(2)}, u32[]{:S(2)}) collective-permute-start(bf16[128,512]{1,0:T(8,128)(2,1)} %get-tuple-element.33), channel_id=1, source_target_pairs={{0,2},{1,3},{2,0},{3,1},{4,6},{5,7},{6,4},{7,5},{8,10},{9,11},{10,... | collective-permute-start | bytes 393224 | tf_op jit(solution)/shard_map/ppermute | solution.py:28
  15.2 9.1 %collective-permute-start = (bf16[128,512]{1,0:T(8,128)(2,1)}, bf16[128,512]{1,0:T(8,128)(2,1)S(1)}, u32[]{:S(2)}, u32[]{:S(2)}) collective-permute-start(bf16[128,512]{1,0:T(8,128)(2,1)} %get-tuple-element.32), channel_id=1, source_target_pairs={{0,1},{1,2},{2,3},{3,0},{4,5},{5,6},{6,7},{7,4},{8,9},{9,10},{10,1... | collective-permute-start | bytes 393224 | tf_op jit(solution)/shard_map/ppermute | solution.py:28
  25.3 5.4 %collective-permute-start.3 = (bf16[128,512]{1,0:T(8,128)(2,1)S(1)}, bf16[128,512]{1,0:T(8,128)(2,1)S(1)}, u32[]{:S(2)}, u32[]{:S(2)}) collective-permute-start(bf16[128,512]{1,0:T(8,128)(2,1)S(1)} %add_convert_fusion.own_ref), channel_id=1, source_target_pairs={{0,4},{4,0},{1,5},{5,1},{2,6},{6,2},{3,7},{7,3},{8,12},{12,8},{9,1... | collective-permute-start | bytes 393224 | tf_op jit(solution)/shard_map/ppermute | solution.py:32
  32.5 107.5 %copy-start.6 = (bf16[128,512]{1,0:T(8,128)(2,1)}, bf16[128,512]{1,0:T(8,128)(2,1)S(1)}, u32[]{:S(2)}) copy-start(bf16[128,512]{1,0:T(8,128)(2,1)S(1)} %get-tuple-element.39.hidden_ref) | copy-start | bytes 393220
  32.5 33.5 %all-to-all-start = ((bf16[32,20,512]{2,1,0:T(8,128)(2,1)}), bf16[32,20,512]{2,1,0:T(8,128)(2,1)}, u32[]{:S(2)}, u32[]{:S(2)}) async-start(bf16[32,20,512]{2,1,0:T(8,128)(2,1)} %get-tuple-element.40), calls=%async_computation | async-start | bytes 1572864 | tf_op jit(solution)/shard_map/all_to_all | solution.py:388
  44.4 47.8 %copy-start.1 = (bf16[2,2048,128]{2,1,0:T(8,128)(2,1)S(1)}, bf16[2,2048,128]{2,1,0:T(8,128)(2,1)}, u32[]{:S(2)}) copy-start(bf16[2,2048,128]{2,1,0:T(8,128)(2,1)} %gate_hbm.3) | copy-start | bytes 3145732
  44.4 7.9 %collective-permute-start.23 = (bf16[2,128,512]{2,1,0:T(8,128)(2,1)}, bf16[2,128,512]{2,1,0:T(8,128)(2,1)}, u32[]{:S(2)}, u32[]{:S(2)}) collective-permute-start(bf16[2,128,512]{2,1,0:T(8,128)(2,1)} %get-tuple-element.62), channel_id=1, source_target_pairs={{0,3},{1,0},{2,1},{3,2},{4,7},{5,4},{6,5},{7,6},{8,11},{9,8},{10,9... | collective-permute-start | bytes 786440 | tf_op jit(solution)/shard_map/ppermute | solution.py:28
  45.5 46.6 %collective-permute-start.13 = (bf16[2048,128]{1,0:T(8,128)(2,1)}, bf16[2048,128]{1,0:T(8,128)(2,1)S(1)}, u32[]{:S(2)}, u32[]{:S(2)}) collective-permute-start(bf16[2048,128]{1,0:T(8,128)(2,1)} %dynamic-slice_bitcast_fusion), channel_id=1, source_target_pairs={{0,4},{4,0},{1,5},{5,1},{2,6},{6,2},{3,7},{7,3},{8,12},{12,8},{9,1... | collective-permute-start | bytes 1572872 | tf_op jit(solution)/shard_map/ppermute | solution.py:32
  47.2 26.4 %collective-permute-start.21 = (bf16[2,128,512]{2,1,0:T(8,128)(2,1)}, bf16[2,128,512]{2,1,0:T(8,128)(2,1)}, u32[]{:S(2)}, u32[]{:S(2)}) collective-permute-start(bf16[2,128,512]{2,1,0:T(8,128)(2,1)} %get-tuple-element.64), channel_id=1, source_target_pairs={{0,1},{1,2},{2,3},{3,0},{4,5},{5,6},{6,7},{7,4},{8,9},{9,10},{10,1... | collective-permute-start | bytes 786440 | tf_op jit(solution)/shard_map/ppermute | solution.py:28
  48.4 23.0 %collective-permute-start.22 = (bf16[2,128,512]{2,1,0:T(8,128)(2,1)}, bf16[2,128,512]{2,1,0:T(8,128)(2,1)}, u32[]{:S(2)}, u32[]{:S(2)}) collective-permute-start(bf16[2,128,512]{2,1,0:T(8,128)(2,1)} %get-tuple-element.63), channel_id=1, source_target_pairs={{0,2},{1,3},{2,0},{3,1},{4,6},{5,7},{6,4},{7,5},{8,10},{9,11},{10,... | collective-permute-start | bytes 786440 | tf_op jit(solution)/shard_map/ppermute | solution.py:28
  69.9 10.8 %collective-permute-start.8 = (bf16[320,512]{1,0:T(8,128)(2,1)}, bf16[320,512]{1,0:T(8,128)(2,1)}, u32[]{:S(2)}, u32[]{:S(2)}) collective-permute-start(bf16[320,512]{1,0:T(8,128)(2,1)} %reshape.56.x0), channel_id=1, source_target_pairs={{0,1},{1,2},{2,3},{3,0},{4,5},{5,6},{6,7},{7,4},{8,9},{9,10},{10,1... | collective-permute-start | bytes 983048 | tf_op jit(solution)/shard_map/ppermute | solution.py:28
  69.9 15.5 %collective-permute-start.9 = (bf16[320,512]{1,0:T(8,128)(2,1)}, bf16[320,512]{1,0:T(8,128)(2,1)}, u32[]{:S(2)}, u32[]{:S(2)}) collective-permute-start(bf16[320,512]{1,0:T(8,128)(2,1)} %reshape.56.x0), channel_id=1, source_target_pairs={{0,2},{1,3},{2,0},{3,1},{4,6},{5,7},{6,4},{7,5},{8,10},{9,11},{10,... | collective-permute-start | bytes 983048 | tf_op jit(solution)/shard_map/ppermute | solution.py:28
  72.3 15.4 %collective-permute-start.10 = (bf16[320,512]{1,0:T(8,128)(2,1)}, bf16[320,512]{1,0:T(8,128)(2,1)}, u32[]{:S(2)}, u32[]{:S(2)}) collective-permute-start(bf16[320,512]{1,0:T(8,128)(2,1)} %reshape.56.x0), channel_id=1, source_target_pairs={{0,3},{1,0},{2,1},{3,2},{4,7},{5,4},{6,5},{7,6},{8,11},{9,8},{10,9... | collective-permute-start | bytes 983048 | tf_op jit(solution)/shard_map/ppermute | solution.py:28
  76.4 33.3 %collective-permute-start.24 = (bf16[4,128,512]{2,1,0:T(8,128)(2,1)}, bf16[4,128,512]{2,1,0:T(8,128)(2,1)}, u32[]{:S(2)}, u32[]{:S(2)}) collective-permute-start(bf16[4,128,512]{2,1,0:T(8,128)(2,1)} %pad_maximum_fusion), channel_id=1, source_target_pairs={{0,4},{4,0},{1,5},{5,1},{2,6},{6,2},{3,7},{7,3},{8,12},{12,8},{9,1... | collective-permute-start | bytes 1572872 | tf_op jit(solution)/shard_map/ppermute | solution.py:32
  80.7 11.0 %collective-permute-start.11 = (bf16[320,512]{1,0:T(8,128)(2,1)}, bf16[320,512]{1,0:T(8,128)(2,1)}, u32[]{:S(2)}, u32[]{:S(2)}) collective-permute-start(bf16[320,512]{1,0:T(8,128)(2,1)} %reshape.57.x0), channel_id=1, source_target_pairs={{0,1},{1,2},{2,3},{3,0},{4,5},{5,6},{6,7},{7,4},{8,9},{9,10},{10,1... | collective-permute-start | bytes 983048 | tf_op jit(solution)/shard_map/ppermute | solution.py:28
  85.4 6.8 %collective-permute-start.12 = (bf16[320,512]{1,0:T(8,128)(2,1)}, bf16[320,512]{1,0:T(8,128)(2,1)}, u32[]{:S(2)}, u32[]{:S(2)}) collective-permute-start(bf16[320,512]{1,0:T(8,128)(2,1)} %reshape.57.x0), channel_id=1, source_target_pairs={{0,3},{1,0},{2,1},{3,2},{4,7},{5,4},{6,5},{7,6},{8,11},{9,8},{10,9... | collective-permute-start | bytes 983048 | tf_op jit(solution)/shard_map/ppermute | solution.py:28
  87.6 18.6 %collective-permute-start.17 = (bf16[320,512]{1,0:T(8,128)(2,1)}, bf16[320,512]{1,0:T(8,128)(2,1)}, u32[]{:S(2)}, u32[]{:S(2)}) collective-permute-start(bf16[320,512]{1,0:T(8,128)(2,1)} %reshape.57.x0), channel_id=1, source_target_pairs={{0,2},{1,3},{2,0},{3,1},{4,6},{5,7},{6,4},{7,5},{8,10},{9,11},{10,... | collective-permute-start | bytes 983048 | tf_op jit(solution)/shard_map/ppermute | solution.py:28
  97.2 13.7 %collective-permute-start.14 = (bf16[320,256]{1,0:T(8,128)(2,1)}, bf16[320,256]{1,0:T(8,128)(2,1)S(1)}, u32[]{:S(2)}, u32[]{:S(2)}) collective-permute-start(bf16[320,256]{1,0:T(8,128)(2,1)} %gate_up.2.refs_0_), channel_id=1, source_target_pairs={{0,1},{1,2},{2,3},{3,0},{4,5},{5,6},{6,7},{7,4},{8,9},{9,10},{10,1... | collective-permute-start | bytes 491528 | tf_op jit(solution)/shard_map/ppermute | solution.py:28
  101.3 11.7 %collective-permute-start.15 = (bf16[320,256]{1,0:T(8,128)(2,1)}, bf16[320,256]{1,0:T(8,128)(2,1)}, u32[]{:S(2)}, u32[]{:S(2)}) collective-permute-start(bf16[320,256]{1,0:T(8,128)(2,1)} %gate_up.2.refs_0_), channel_id=1, source_target_pairs={{0,2},{1,3},{2,0},{3,1},{4,6},{5,7},{6,4},{7,5},{8,10},{9,11},{10,... | collective-permute-start | bytes 491528 | tf_op jit(solution)/shard_map/ppermute | solution.py:28
  104.2 8.8 %collective-permute-start.16 = (bf16[320,256]{1,0:T(8,128)(2,1)}, bf16[320,256]{1,0:T(8,128)(2,1)}, u32[]{:S(2)}, u32[]{:S(2)}) collective-permute-start(bf16[320,256]{1,0:T(8,128)(2,1)} %gate_up.2.refs_0_), channel_id=1, source_target_pairs={{0,3},{1,0},{2,1},{3,2},{4,7},{5,4},{6,5},{7,6},{8,11},{9,8},{10,9... | collective-permute-start | bytes 491528 | tf_op jit(solution)/shard_map/ppermute | solution.py:28
  109.5 10.7 %collective-permute-start.18 = (bf16[320,256]{1,0:T(8,128)(2,1)}, bf16[320,256]{1,0:T(8,128)(2,1)S(1)}, u32[]{:S(2)}, u32[]{:S(2)}) collective-permute-start(bf16[320,256]{1,0:T(8,128)(2,1)} %gate_up.3.refs_4_), channel_id=1, source_target_pairs={{0,1},{1,2},{2,3},{3,0},{4,5},{5,6},{6,7},{7,4},{8,9},{9,10},{10,1... | collective-permute-start | bytes 491528 | tf_op jit(solution)/shard_map/ppermute | solution.py:28
  109.6 10.6 %collective-permute-start.19 = (bf16[320,256]{1,0:T(8,128)(2,1)}, bf16[320,256]{1,0:T(8,128)(2,1)S(1)}, u32[]{:S(2)}, u32[]{:S(2)}) collective-permute-start(bf16[320,256]{1,0:T(8,128)(2,1)} %gate_up.3.refs_4_), channel_id=1, source_target_pairs={{0,2},{1,3},{2,0},{3,1},{4,6},{5,7},{6,4},{7,5},{8,10},{9,11},{10,... | collective-permute-start | bytes 491528 | tf_op jit(solution)/shard_map/ppermute | solution.py:28
  111.5 8.8 %collective-permute-start.20 = (bf16[320,256]{1,0:T(8,128)(2,1)}, bf16[320,256]{1,0:T(8,128)(2,1)S(1)}, u32[]{:S(2)}, u32[]{:S(2)}) collective-permute-start(bf16[320,256]{1,0:T(8,128)(2,1)} %gate_up.3.refs_4_), channel_id=1, source_target_pairs={{0,3},{1,0},{2,1},{3,2},{4,7},{5,4},{6,5},{7,6},{8,11},{9,8},{10,9... | collective-permute-start | bytes 491528 | tf_op jit(solution)/shard_map/ppermute | solution.py:28
  122.1 40.3 %copy-start.27 = (f32[32,128]{1,0:T(8,128)S(1)}, f32[32,128]{1,0:T(8,128)}, u32[]{:S(2)}) copy-start(f32[32,128]{1,0:T(8,128)} %fusion.22) | copy-start | bytes 49156
  122.1 40.3 %copy-start.28 = (pred[32,128]{1,0:T(8,128)(4,1)S(1)}, pred[32,128]{1,0:T(8,128)(4,1)}, u32[]{:S(2)}) copy-start(pred[32,128]{1,0:T(8,128)(4,1)} %broadcast_compare_fusion) | copy-start | bytes 12292
  126.4 36.0 %all-to-all-start.1 = ((bf16[32,20,512]{2,1,0:T(8,128)(2,1)}), bf16[32,20,512]{2,1,0:T(8,128)(2,1)S(1)}, u32[]{:S(2)}, u32[]{:S(2)}) async-start(bf16[32,20,512]{2,1,0:T(8,128)(2,1)} %down.1), calls=%async_computation.1 | async-start | bytes 1572864 | tf_op jit(solution)/shard_map/all_to_all | solution.py:419
  139.8 46.6 %copy-start.26 = (s32[32,3]{0,1:T(4,128)S(1)}, s32[32,3]{0,1:T(4,128)}, u32[]{:S(2)}) copy-start(s32[32,3]{0,1:T(4,128)} %param.16) | copy-start | bytes 1156
  139.8 47.0 %copy-start.30 = (s32[1,16]{1,0:T(1,128)S(1)}, s32[1,16]{1,0:T(1,128)}, u32[]{:S(2)}) copy-start(s32[1,16]{1,0:T(1,128)} %param.29) | copy-start | bytes 196
  139.8 50.7 %copy-start.29 = (s32[1,1024]{1,0:T(1,128)S(1)}, s32[1,1024]{1,0:T(1,128)}, u32[]{:S(2)}) copy-start(s32[1,1024]{1,0:T(1,128)} %param.28) | copy-start | bytes 12292
  140.2 3.8 %collective-permute-start.7 = (f32[128,128]{0,1:T(8,128)S(1)}, f32[128,128]{0,1:T(8,128)S(1)}, u32[]{:S(2)}, u32[]{:S(2)}) collective-permute-start(f32[128,128]{0,1:T(8,128)S(1)} %pad_maximum_fusion.1), channel_id=1, source_target_pairs={{0,3},{1,0},{2,1},{3,2},{4,7},{5,4},{6,5},{7,6},{8,11},{9,8},{10,9... | collective-permute-start | bytes 196616 | tf_op jit(solution)/shard_map/ppermute | solution.py:28
  142.6 4.9 %collective-permute-start.6 = (f32[128,128]{0,1:T(8,128)S(1)}, f32[128,128]{0,1:T(8,128)S(1)}, u32[]{:S(2)}, u32[]{:S(2)}) collective-permute-start(f32[128,128]{0,1:T(8,128)S(1)} %pad_maximum_fusion.1), channel_id=1, source_target_pairs={{0,2},{1,3},{2,0},{3,1},{4,6},{5,7},{6,4},{7,5},{8,10},{9,11},{10,... | collective-permute-start | bytes 196616 | tf_op jit(solution)/shard_map/ppermute | solution.py:28
  142.8 6.2 %collective-permute-start.5 = (f32[128,128]{0,1:T(8,128)S(1)}, f32[128,128]{0,1:T(8,128)S(1)}, u32[]{:S(2)}, u32[]{:S(2)}) collective-permute-start(f32[128,128]{0,1:T(8,128)S(1)} %pad_maximum_fusion.1), channel_id=1, source_target_pairs={{0,1},{1,2},{2,3},{3,0},{4,5},{5,6},{6,7},{7,4},{8,9},{9,10},{10,1... | collective-permute-start | bytes 196616 | tf_op jit(solution)/shard_map/ppermute | solution.py:28
  163.4 5.4 %collective-permute-start.25 = (bf16[128,512]{1,0:T(8,128)(2,1)S(1)}, bf16[128,512]{1,0:T(8,128)(2,1)S(1)}, u32[]{:S(2)}, u32[]{:S(2)}) collective-permute-start(bf16[128,512]{1,0:T(8,128)(2,1)S(1)} %fusion.1.moe_ref), channel_id=1, source_target_pairs={{0,4},{4,0},{1,5},{5,1},{2,6},{6,2},{3,7},{7,3},{8,12},{12,8},{9,1... | collective-permute-start | bytes 393224 | tf_op jit(solution)/shard_map/ppermute | solution.py:32
  171.6 4.6 %collective-permute-start.26 = (f32[136,128]{1,0:T(8,128)}, f32[136,128]{1,0:T(8,128)S(1)}, u32[]{:S(2)}, u32[]{:S(2)}) collective-permute-start(f32[136,128]{1,0:T(8,128)} %get-tuple-element.48.p0), channel_id=1, source_target_pairs={{0,1},{1,2},{2,3},{3,0},{4,5},{5,6},{6,7},{7,4},{8,9},{9,10},{10,1... | collective-permute-start | bytes 208904 | tf_op jit(solution)/shard_map/ppermute | solution.py:28
  172.3 5.5 %collective-permute-start.27 = (f32[136,128]{1,0:T(8,128)}, f32[136,128]{1,0:T(8,128)S(1)}, u32[]{:S(2)}, u32[]{:S(2)}) collective-permute-start(f32[136,128]{1,0:T(8,128)} %get-tuple-element.48.p0), channel_id=1, source_target_pairs={{0,2},{1,3},{2,0},{3,1},{4,6},{5,7},{6,4},{7,5},{8,10},{9,11},{10,... | collective-permute-start | bytes 208904 | tf_op jit(solution)/shard_map/ppermute | solution.py:28
  175.1 3.7 %collective-permute-start.28 = (f32[136,128]{1,0:T(8,128)}, f32[136,128]{1,0:T(8,128)S(1)}, u32[]{:S(2)}, u32[]{:S(2)}) collective-permute-start(f32[136,128]{1,0:T(8,128)} %get-tuple-element.48.p0), channel_id=1, source_target_pairs={{0,3},{1,0},{2,1},{3,2},{4,7},{5,4},{6,5},{7,6},{8,11},{9,8},{10,9... | collective-permute-start | bytes 208904 | tf_op jit(solution)/shard_map/ppermute | solution.py:28
  181.4 19.0 %all-to-all-start.2 = ((bf16[16,128,128]{2,1,0:T(8,128)(2,1)}), bf16[16,128,128]{2,1,0:T(8,128)(2,1)S(1)}, u32[]{:S(2)}, u32[]{:S(2)}) async-start(bf16[16,128,128]{2,1,0:T(8,128)(2,1)} %vectors.1), calls=%async_computation.2 | async-start | bytes 1048576 | tf_op jit(solution)/shard_map/all_to_all | solution.py:470
  186.9 6.7 %collective-permute-start.29 = (bf16[128,512]{1,0:T(8,128)(2,1)}, bf16[128,512]{1,0:T(8,128)(2,1)S(1)}, u32[]{:S(2)}, u32[]{:S(2)}) collective-permute-start(bf16[128,512]{1,0:T(8,128)(2,1)} %get-tuple-element.52.p0), channel_id=1, source_target_pairs={{0,1},{1,2},{2,3},{3,0},{4,5},{5,6},{6,7},{7,4},{8,9},{9,10},{10,1... | collective-permute-start | bytes 393224 | tf_op jit(solution)/shard_map/ppermute | solution.py:28
  186.9 6.6 %collective-permute-start.30 = (bf16[128,512]{1,0:T(8,128)(2,1)}, bf16[128,512]{1,0:T(8,128)(2,1)S(1)}, u32[]{:S(2)}, u32[]{:S(2)}) collective-permute-start(bf16[128,512]{1,0:T(8,128)(2,1)} %get-tuple-element.52.p0), channel_id=1, source_target_pairs={{0,2},{1,3},{2,0},{3,1},{4,6},{5,7},{6,4},{7,5},{8,10},{9,11},{10,... | collective-permute-start | bytes 393224 | tf_op jit(solution)/shard_map/ppermute | solution.py:28
  188.6 5.8 %collective-permute-start.31 = (bf16[128,512]{1,0:T(8,128)(2,1)}, bf16[128,512]{1,0:T(8,128)(2,1)S(1)}, u32[]{:S(2)}, u32[]{:S(2)}) collective-permute-start(bf16[128,512]{1,0:T(8,128)(2,1)} %get-tuple-element.52.p0), channel_id=1, source_target_pairs={{0,3},{1,0},{2,1},{3,2},{4,7},{5,4},{6,5},{7,6},{8,11},{9,8},{10,9... | collective-permute-start | bytes 393224 | tf_op jit(solution)/shard_map/ppermute | solution.py:28
  200.4 6.4 %collective-permute-start.32 = (bf16[2048,128]{1,0:T(8,128)(2,1)S(1)}, bf16[2048,128]{1,0:T(8,128)(2,1)S(1)}, u32[]{:S(2)}, u32[]{:S(2)}) collective-permute-start(bf16[2048,128]{1,0:T(8,128)(2,1)S(1)} %bitcast.36), channel_id=1, source_target_pairs={{0,8},{8,0},{1,9},{9,1},{2,10},{10,2},{3,11},{11,3},{4,12},{12,4},... | collective-permute-start | bytes 1572872 | tf_op jit(solution)/shard_map/ppermute | solution.py:484
  (19 other events, 85.9 us)

commit v7 on v6

--- a/solution.py
+++ b/solution.py
@@ -13,7 +13,6 @@
 CAP = 20
 EXPERTS = 64
 WIDE = 32
-GROUPS = ((0, 20),)
 HALF = WIDE * CAP // 2
 EPS = 1e-06
 THETA = 50000.0
@@ -110,7 +109,7 @@
         out_ref[...] = jnp.dot(mixed, out_w_ref[:, columns], preferred_element_type=f32).astype(bf16)
 
 
-def choose_kernel(here_ref, routes_ref, *out_refs):
+def choose_kernel(here_ref, routes_ref, out_ref):
     expert = 2 * lax.broadcasted_iota(jnp.int32, (WIDE, TOK), 0) + here_ref[0]
     hit = jnp.zeros((WIDE, TOK), f32)
     for k in range(TOPK):
@@ -119,71 +118,80 @@
     earlier = (sooner < lax.broadcasted_iota(jnp.int32, (TOK, TOK), 1)).astype(f32).astype(bf16)
     before = jnp.dot(hit.astype(bf16), earlier, preferred_element_type=f32)
     place = jnp.where(hit > 0, before, -1.0).astype(bf16)
-    for (a, b), out_ref in zip(GROUPS, out_refs):
-        size = b - a
-        owner = size * lax.broadcasted_iota(jnp.int32, (WIDE * size, WIDE), 1)
-        offset = lax.broadcasted_iota(jnp.int32, (WIDE * size, WIDE), 0) - owner
-        inside = (offset >= 0) & (offset < size)
-        spread = jnp.dot(
-            inside.astype(f32).astype(bf16), place, preferred_element_type=f32
-        )
-        slot = jnp.sum(jnp.where(inside, offset + a, 0).astype(f32), axis=1, keepdims=True)
-        out_ref[...] = (spread == slot).astype(f32).astype(bf16)
-
-
-def dispatch_kernel(here_ref, x_ref, own_ref, par_ref, *refs):
-    chooses = refs[: len(GROUPS)]
-    hidden_ref = refs[len(GROUPS)]
+    owner = CAP * lax.broadcasted_iota(jnp.int32, (WIDE * CAP, WIDE), 1)
+    slot = lax.broadcasted_iota(jnp.int32, (WIDE * CAP, WIDE), 0) - owner
+    inside = (slot >= 0) & (slot < CAP)
+    spread = jnp.dot(inside.astype(f32).astype(bf16), place, preferred_element_type=f32)
+    slot = jnp.sum(jnp.where(inside, slot, 0).astype(f32), axis=1, keepdims=True)
+    out_ref[...] = (spread == slot).astype(f32).astype(bf16)
+
+
+def packed(rows):
+    return jnp.concatenate([rows[:, 0:256], rows[:, 256:512]], axis=0).astype(bf16)
+
+
+def dispatch_kernel(here_ref, x_ref, own_ref, par_ref, choose_ref, hidden_ref, rows_ref):
     j = here_ref[1]
     mine = x_ref[:, pl.ds(pl.multiple_of(j * 512, 512), 512)].astype(f32)
     hidden = (mine + (own_ref[...].astype(f32) + par_ref[...].astype(f32))).astype(bf16)
     hidden_ref[...] = hidden
-    for choose_ref, rows_ref in zip(chooses, refs[len(GROUPS) + 1 :]):
-        rows = jnp.dot(choose_ref[...], hidden, preferred_element_type=f32)
-        size = rows_ref.shape[1]
-        for s in range(WIDE):
-            rows_ref[s] = rows[s * size : (s + 1) * size].astype(bf16)
-
-
-def gate_up_kernel(
-    here_ref, x0, x1, x2, x3, gain_ref, gate_hbm, up_hbm, gate_par, up_par, out_ref, w_ref, sems
-):
+    rows = jnp.dot(choose_ref[...], hidden, preferred_element_type=f32)
+    for s in range(WIDE):
+        rows_ref[s] = packed(rows[s * CAP : (s + 1) * CAP])
+
+
+def unpack_kernel(in_ref, top_ref, bottom_ref, scratch):
+    for half, out_ref in enumerate((top_ref, bottom_ref)):
+        for s in range(WIDE // 2):
+            rows = in_ref[half * (WIDE // 2) + s].astype(f32)
+            at = slice(s * CAP, (s + 1) * CAP)
+            scratch[at, 0:256] = rows[0:CAP]
+            scratch[at, 256:512] = rows[CAP:]
+        out_ref[...] = scratch[...].astype(bf16)
+
+
+def gate_up_kernel(here_ref, *refs):
+    halves = refs[0:4], refs[4:8]
+    gain_hbm, gate_hbm, up_hbm, gate_par, up_par, out_ref, gain_ref, w_ref, sems = refs[8:]
     i, j = here_ref[0], here_ref[1]
     sources = (gate_hbm.at[i], up_hbm.at[i], gate_par, up_par)
     copies = [
         pltpu.make_async_copy(source, w_ref.at[n], sems.at[n]) for n, source in enumerate(sources)
     ]
+    copies.append(pltpu.make_async_copy(gain_hbm, gain_ref, sems.at[4]))
     for copy in copies:
         copy.start()
-    xs = (x0, x1, x2, x3)
-    total = jnp.zeros((x0.shape[0], 1), f32)
-    for x in xs:
-        v = x[...].astype(f32)
-        total = total + jnp.sum(v * v, axis=1, keepdims=True)
-    scale = lax.rsqrt(total / 2048.0 + EPS)
+    scales = []
+    for xs in halves:
+        total = jnp.zeros((HALF, 1), f32)
+        for x in xs:
+            v = x[...].astype(f32)
+            total = total + jnp.sum(v * v, axis=1, keepdims=True)
+        scales.append(lax.rsqrt(total / 2048.0 + EPS))
     for copy in copies:
         copy.wait()
-    own = jnp.zeros((x0.shape[0], 256), f32)
-    par = jnp.zeros((x0.shape[0], 256), f32)
-    for k, x in enumerate(xs):
-        part = lax.rem(j - k + 4, 4)
-        rows = pl.ds(pl.multiple_of(part * 512, 512), 512)
-        normed = (x[...].astype(f32) * scale * gain_ref[1:2, rows]).astype(bf16)
-        w_own = jnp.concatenate([w_ref[0, rows, :], w_ref[1, rows, :]], axis=1)
-        w_par = jnp.concatenate([w_ref[2, rows, :], w_ref[3, rows, :]], axis=1)
-        own = own + jnp.dot(normed, w_own, preferred_element_type=f32)
-        par = par + jnp.dot(normed, w_par, preferred_element_type=f32)
-    for at, both in ((0, own), (128, par)):
-        gate, up = both[:, :128], both[:, 128:]
-        out_ref[:, at : at + 128] = (gate / (1.0 + jnp.exp(-gate)) * up).astype(bf16)
-
-
-def down_kernel(here_ref, *refs):
-    acts, weights, par_ref = refs[:8], refs[8:12], refs[12]
-    out_ref, w_ref, sems = refs[13:]
+    for half, (xs, scale) in enumerate(zip(halves, scales)):
+        own = jnp.zeros((HALF, 256), f32)
+        par = jnp.zeros((HALF, 256), f32)
+        for k, x in enumerate(xs):
+            part = lax.rem(j + 4 + (0, -1, 1, 2)[k], 4)
+            rows = pl.ds(pl.multiple_of(part * 512, 512), 512)
+            normed = (x[...].astype(f32) * scale * gain_ref[1:2, rows]).astype(bf16)
+            w_own = jnp.concatenate([w_ref[0, rows, :], w_ref[1, rows, :]], axis=1)
+            w_par = jnp.concatenate([w_ref[2, rows, :], w_ref[3, rows, :]], axis=1)
+            own = own + jnp.dot(normed, w_own, preferred_element_type=f32)
+            par = par + jnp.dot(normed, w_par, preferred_element_type=f32)
+        for at, both in ((0, own), (128, par)):
+            gate, up = both[:, :128], both[:, 128:]
+            out_ref[half * HALF : (half + 1) * HALF, at : at + 128] = (
+                gate / (1.0 + jnp.exp(-gate)) * up
+            ).astype(bf16)
+
+
+def down_kernel(here_ref, a0, a1, a2, a3, w0, w1, w2, w3, par_ref, out_ref, w_ref, sems):
     i = here_ref[0]
     copies = []
-    for k, w in enumerate(weights):
+    for k, w in enumerate((w0, w1, w2, w3)):
         copies.append(
             (
                 pltpu.make_async_copy(w.at[i], w_ref.at[k, 0:128], sems.at[0, k]),
@@ -193,17 +201,14 @@
     for pair in copies:
         for copy in pair:
             copy.start()
-    for half in range(2):
-        total = jnp.zeros((HALF, 512), f32)
-        for k in range(4):
-            if half == 0:
-                for copy in copies[k]:
-                    copy.wait()
-            total = total + jnp.dot(
-                acts[4 * half + k][...], w_ref[k], preferred_element_type=f32
-            )
-        for s in range(WIDE // 2):
-            out_ref[half * (WIDE // 2) + s] = total[s * CAP : (s + 1) * CAP].astype(bf16)
+    total = jnp.zeros((a0.shape[0], 512), f32)
+    for k, a in enumerate((a0, a1, a2, a3)):
+        for copy in copies[k]:
+            copy.wait()
+        total = total + jnp.dot(a[...], w_ref[k], preferred_element_type=f32)
+    size = out_ref.shape[1]
+    for s in range(WIDE):
+        out_ref[s] = total[s * size : (s + 1) * size].astype(bf16)
 
 
 def embed_kernel(here_ref, hidden_ref, moe_ref, par_ref, gain_ref, w_ref, layer_ref, part_ref):
@@ -349,7 +354,6 @@
     )
     attn_parts = [y_shift(attn[k], k) for k in (1, 2, 3)]
 
-    up_par = x_swap(pick(w_up, 1 - i))
     downs = [cut(w_down, j, 2)] + [y_shift(cut(w_down, j + k, 2), k) for k in (1, 2, 3)]
     down_par = x_swap(jnp.stack([pick(d, 1 - i) for d in downs]))
 
@@ -360,62 +364,77 @@
     before = jnp.dot(hit.astype(bf16), earlier, preferred_element_type=f32)
     slot = jnp.arange(CAP, dtype=jnp.int32).astype(f32)
     chosen = (before[:, None, :] == slot[None, :, None]) & (hit[:, None, :] > 0)
-    chooses = pl.pallas_call(
+    choose = pl.pallas_call(
         choose_kernel,
-        out_shape=tuple(jax.ShapeDtypeStruct((WIDE * (b - a), TOK), bf16) for a, b in GROUPS),
+        out_shape=jax.ShapeDtypeStruct((WIDE * CAP, TOK), bf16),
         in_specs=[smem(), vmem()],
-        out_specs=(vmem(),) * len(GROUPS),
+        out_specs=vmem(),
         compiler_params=params(),
         name="choose",
     )(here, routes.T)
 
     attn = (attn[0].astype(f32) + sum(p.astype(f32) for p in attn_parts)).astype(bf16)
-    attn, *chooses = lax.optimization_barrier((attn, *chooses))
+    attn, choose = lax.optimization_barrier((attn, choose))
     attn_par = x_swap(attn)
     attn_par, gate_par = lax.optimization_barrier((attn_par, gate_par))
-    hidden, *rows = pl.pallas_call(
+    hidden, rows = pl.pallas_call(
         dispatch_kernel,
         out_shape=(
             jax.ShapeDtypeStruct((TOK, 512), bf16),
-            *(jax.ShapeDtypeStruct((WIDE, b - a, 512), bf16) for a, b in GROUPS),
+            jax.ShapeDtypeStruct((WIDE, 2 * CAP, 256), bf16),
         ),
-        in_specs=[smem()] + [vmem()] * (3 + len(GROUPS)),
-        out_specs=(vmem(),) * (1 + len(GROUPS)),
+        in_specs=[smem()] + [vmem()] * 4,
+        out_specs=(vmem(), vmem()),
         compiler_params=params(),
         name="dispatch",
-    )(here, tokens, attn, attn_par, *chooses)
-
-    arrived = lax.all_to_all(rows[0], W, 0, 0, tiled=True)
-    first = arrived[: WIDE // 2].reshape(HALF, 512)
-    second = arrived[WIDE // 2 :].reshape(HALF, 512)
-    gathered = [first] + [y_shift(first, k) for k in (1, 2, 3)]
-    others = [second] + [y_shift(second, k) for k in (1, 2, 3)]
-    gathered, others[1], others[3] = lax.optimization_barrier((gathered, others[1], others[3]))
-
-    def gate_up(xs):
-        return pl.pallas_call(
-            gate_up_kernel,
-            out_shape=jax.ShapeDtypeStruct((HALF, 256), bf16),
-            in_specs=[smem()] + [vmem()] * 5 + [hbm()] * 4,
-            out_specs=vmem(),
-            scratch_shapes=[pltpu.VMEM((4, 2048, 128), bf16), pltpu.SemaphoreType.DMA((4,))],
-            compiler_params=params(),
-            name="gate_up",
-        )(here, *xs, norm_gains, w_gate, w_up, gate_par, up_par)
-
-    act = gate_up(gathered)
-    acts = [act] + [y_shift(act, k) for k in (1, 2, 3)]
-    act = gate_up(others)
-    acts += [act] + [y_shift(act, k) for k in (1, 2, 3)]
+    )(here, tokens, attn, attn_par, choose)
+
+    arrived = lax.all_to_all(rows, W, 0, 0, tiled=True)
+    top, bottom = pl.pallas_call(
+        unpack_kernel,
+        out_shape=(jax.ShapeDtypeStruct((HALF, 512), bf16),) * 2,
+        in_specs=[vmem()],
+        out_specs=(vmem(), vmem()),
+        scratch_shapes=[pltpu.VMEM((HALF, 512), f32)],
+        compiler_params=params(),
+        name="unpack",
+    )(arrived)
+    top, bottom, up_sent = lax.optimization_barrier((top, bottom, pick(w_up, 1 - i)))
+    up_par = x_swap(up_sent)
+    top_back, bottom_ahead = y_shift(top, 1), y_shift(bottom, 3)
+    bottom_back, top_ahead = y_shift(bottom, 1), y_shift(top, 3)
+    top_far, bottom_far = y_shift(top_back, 1), y_shift(bottom_ahead, 3)
+    act = pl.pallas_call(
+        gate_up_kernel,
+        out_shape=jax.ShapeDtypeStruct((2 * HALF, 256), bf16),
+        in_specs=[smem()] + [vmem()] * 8 + [hbm()] * 5,
+        out_specs=vmem(),
+        scratch_shapes=[
+            pltpu.VMEM((3, 2048), f32),
+            pltpu.VMEM((4, 2048, 128), bf16),
+            pltpu.SemaphoreType.DMA((5,)),
+        ],
+        compiler_params=params(),
+        name="gate_up",
+    )(
+        here,
+        *(top, top_back, top_ahead, top_far),
+        *(bottom, bottom_back, bottom_ahead, bottom_far),
+        norm_gains,
+        w_gate,
+        w_up,
+        gate_par,
+        up_par,
+    )
     out = pl.pallas_call(
         down_kernel,
         out_shape=jax.ShapeDtypeStruct((WIDE, CAP, 512), bf16),
-        in_specs=[smem()] + [vmem()] * 8 + [hbm()] * 5,
+        in_specs=[smem()] + [vmem()] * 4 + [hbm()] * 5,
         out_specs=vmem(),
         scratch_shapes=[pltpu.VMEM((4, 256, 512), bf16), pltpu.SemaphoreType.DMA((2, 4))],
         compiler_params=params(),
         name="down",
-    )(here, *acts, *downs, down_par)
+    )(here, act, *(y_shift(act, k) for k in (1, 2, 3)), *downs, down_par)
     back = lax.all_to_all(out, W, 0, 0, tiled=True)
 
     hf = hidden.astype(f32)

time: 212 us -> 188 us (0.89)
  local copies, waits for them, and re-layouts: 22.7 us -> 12.9 us
  starting transfers between devices: 72.7 us -> 68.3 us
  Pallas kernels: 27.9 us -> 23.7 us
  waiting for transfers between devices: 79.7 us -> 76.4 us
    all_to_all x1, starting transfers between devices: 13.4 us -> 7.57 us  [body(): back = lax.all_to_all(out, W, 0, 0, tiled=True)]
    ppermute x27 -> x24, waiting for transfers between devices: 39 us -> 34.6 us  [y_shift(): return lax.ppermute(x, 'y', [(s, (s + k) % 4) for s in range(4)])]
    reshape x2 -> x0, local copies, waits for them, and re-layouts: 3.59 us -> none  [the longest x1 1.8 us: body(): first = arrived[:WIDE // 2].reshape(HALF, 512)]
    pallas_call x3, Pallas kernels: 7.41 us -> 3.93 us  [the longest x1 2.94 us: body(): pl.pallas_call(gate_up_kernel, out_shape=jax.ShapeDtypeStruct((2 * HALF,...]
    unnamed x63 -> x47, local copies, waits for them, and re-layouts: 6.52 us -> 3.3 us
    ppermute x27 -> x24, starting transfers between devices: 30.6 us -> 30.7 us  [y_shift(): return lax.ppermute(x, 'y', [(s, (s + k) % 4) for s in range(4)])]
  transfers between devices with their start and end apart: 36 -> 33, of which waited for: 23 -> 20; matrix products, arithmetic and copies ran while one was open for 10% -> 6% of each run, Pallas kernels for 7% -> 6%
where the time goes in v7:
time: 188 us; the launch traced here: 187 us
  waiting for transfers between devices  76.4 us (41%)
  starting transfers between devices  68.3 us (36%)
  Pallas kernels  23.7 us (13%)
  local copies, waits for them, and re-layouts  12.9 us (7%)
  other arithmetic  3.28 us (2%)
    ppermute x24, waiting for transfers between devices, y_shift(): return lax.ppermute(x, 'y', [(s, (s + k) % 4) for s in range(4)])  34.6 us
    ppermute x24, starting transfers between devices, y_shift(): return lax.ppermute(x, 'y', [(s, (s + k) % 4) for s in range(4)])  30.7 us
    all_to_all x1, waiting for transfers between devices, body(): back = lax.all_to_all(out, W, 0, 0, tiled=True)  15.2 us
    all_to_all x1, starting transfers between devices, body(): arrived = lax.all_to_all(rows, W, 0, 0, tiled=True)  11.6 us
    all_to_all x1, waiting for transfers between devices, body(): arrived = lax.all_to_all(rows, W, 0, 0, tiled=True)  11.5 us
    ppermute x5, starting transfers between devices, x_swap(): return lax.ppermute(x, 'xh', [(0, 1), (1, 0)])  9.12 us
    ppermute x5, waiting for transfers between devices, x_swap(): return lax.ppermute(x, 'xh', [(0, 1), (1, 0)])  8.92 us
    all_to_all x1, starting transfers between devices, body(): back = lax.all_to_all(out, W, 0, 0, tiled=True)  7.57 us
  transfers between devices with their start and end apart: 33, of which 20 were waited for; matrix products, arithmetic and copies ran while one was open for 6% of the time, Pallas kernels for 6%

profile of v7, /device:TPU:1, one launch (start us, length us, event | category | flops | bytes accessed | tf_op | source)
XLA Modules:
  0.0 187.0 jit_solution(3893261124070963897)
XLA Ops:
  0.7 1.1 dynamic-slice_bitcast_fusion.1
  1.8 3.7 %collective-permute-start.4 = (bf16[2048,128]{1,0:T(8,128)(2,1)S(1)}, bf16[2048,128]{1,0:T(8,128)(2,1)S(1)}, u32[]{:S(2)}, u32[]{:S(2)}) collective-permute-start(bf16[2048,128]{1,0:T(8,128)(2,1)S(1)} %dynamic-slice_bitcast_fusion.1), channel_id=1, source_target_pairs={{0,4},{4,0},{1,5},{5,1},{2,6},{6,2},{3,7},{7,3},{8,12},{12,8},{9,1... | collective-permute-start | bytes 1572872 | tf_op jit(solution)/shard_map/ppermute | solution.py:31
  6.1 5.1 %attention.1 = (bf16[128,512]{1,0:T(8,128)(2,1)}, bf16[128,512]{1,0:T(8,128)(2,1)}, bf16[128,512]{1,0:T(8,128)(2,1)}, bf16[128,512]{1,0:T(8,128)(2,1)}) custom-call(s32[4]{0:T(128)} %pad_add_fusion.here_ref, s32[3,32]{1,0:T(4,128)} %bitcast.39, f32[2,256]{1,0:T(2,128)} %qk_ref.1, f32[3,2048]{1,0:T(4,128)} %gain_ref.3, bf16[128,2048]{1,0:T(8,128)(2,1)} %x_ref, ...), custom_call_target="tpu_custom_call" | custom-call | tf_op jit(solution)/shard_map/attention/pallas_call | solution.py:333
  11.2 1.4 collective-permute-start
  12.6 2.6 %collective-permute-start.1 = (bf16[128,512]{1,0:T(8,128)(2,1)}, bf16[128,512]{1,0:T(8,128)(2,1)S(1)}, u32[]{:S(2)}, u32[]{:S(2)}) collective-permute-start(bf16[128,512]{1,0:T(8,128)(2,1)} %get-tuple-element.32), channel_id=1, source_target_pairs={{0,2},{1,3},{2,0},{3,1},{4,6},{5,7},{6,4},{7,5},{8,10},{9,11},{10,... | collective-permute-start | bytes 393224 | tf_op jit(solution)/shard_map/ppermute | solution.py:27
  15.2 1.1 collective-permute-start.2
  17.1 3.3 %collective-permute-done.1 = bf16[128,512]{1,0:T(8,128)(2,1)S(1)} collective-permute-done((bf16[128,512]{1,0:T(8,128)(2,1)}, bf16[128,512]{1,0:T(8,128)(2,1)S(1)}, u32[]{:S(2)}, u32[]{:S(2)}) %collective-permute-start.1) | collective-permute-done | bytes 131104 | tf_op jit(solution)/shard_map/ppermute | solution.py:27
  21.9 5.3 %collective-permute-done.3.par_ref = bf16[128,512]{1,0:T(8,128)(2,1)S(1)} collective-permute-done((bf16[128,512]{1,0:T(8,128)(2,1)S(1)}, bf16[128,512]{1,0:T(8,128)(2,1)S(1)}, u32[]{:S(2)}, u32[]{:S(2)}) %collective-permute-start.3) | collective-permute-done | bytes 131104 | tf_op jit(solution)/shard_map/ppermute | solution.py:31
  27.2 1.8 dispatch.1
  29.0 11.6 %all-to-all-start = ((bf16[32,40,256]{2,1,0:T(8,128)(2,1)}), bf16[32,40,256]{2,1,0:T(8,128)(2,1)S(1)}, u32[]{:S(2)}, u32[]{:S(2)}) async-start(bf16[32,40,256]{2,1,0:T(8,128)(2,1)} %get-tuple-element.39), calls=%async_computation | async-start | bytes 1310720 | tf_op jit(solution)/shard_map/all_to_all | solution.py:392
  40.6 2.2 %constant_dynamic-slice_fusion.4 = (bf16[2,128,512]{2,1,0:T(8,128)(2,1)}, bf16[2,128,512]{2,1,0:T(8,128)(2,1)}, bf16[2,128,512]{2,1,0:T(8,128)(2,1)}, bf16[2,128,512]{2,1,0:T(8,128)(2,1)S(1)}) fusion(bf16[2,128,2048]{2,1,0:T(8,128)(2,1)} %param.25, s32[]{:T(128)S(6)} %select_n.67, s32[]{:T(128)S(6)} %select_n.66, s32[]{:T(128)S(6)} %select_n.65, s32[]{:T(128)S(6)} %select_n.64), kind=kLoop, calls=%fused_computation.58 | loop fusion | bytes 2097168 | tf_op jit(solution)/shard_map/dynamic_slice | solution.py:328
  42.8 2.0 %collective-permute-start.20 = (bf16[2,128,512]{2,1,0:T(8,128)(2,1)}, bf16[2,128,512]{2,1,0:T(8,128)(2,1)}, u32[]{:S(2)}, u32[]{:S(2)}) collective-permute-start(bf16[2,128,512]{2,1,0:T(8,128)(2,1)} %get-tuple-element.60), channel_id=1, source_target_pairs={{0,3},{1,0},{2,1},{3,2},{4,7},{5,4},{6,5},{7,6},{8,11},{9,8},{10,9... | collective-permute-start | bytes 786440 | tf_op jit(solution)/shard_map/ppermute | solution.py:27
  46.0 1.7 constant_dynamic-slice_fusion.3
  48.7 11.5 %all-to-all-done.in_ref = bf16[32,40,256]{2,1,0:T(8,128)(2,1)S(1)} async-done(((bf16[32,40,256]{2,1,0:T(8,128)(2,1)}), bf16[32,40,256]{2,1,0:T(8,128)(2,1)S(1)}, u32[]{:S(2)}, u32[]{:S(2)}) %all-to-all-start) | async-done | bytes 655392 | tf_op jit(solution)/shard_map/all_to_all | solution.py:392
  60.3 1.0 collective-permute-start.8
  61.4 1.7 collective-permute-start.12
  64.1 1.8 collective-permute-start.14
  67.8 2.8 %collective-permute-start.9 = (bf16[320,512]{1,0:T(8,128)(2,1)S(1)}, bf16[320,512]{1,0:T(8,128)(2,1)S(1)}, u32[]{:S(2)}, u32[]{:S(2)}) collective-permute-start(bf16[320,512]{1,0:T(8,128)(2,1)S(1)} %get-tuple-element.42.refs_0_), channel_id=1, source_target_pairs={{0,3},{1,0},{2,1},{3,2},{4,7},{5,4},{6,5},{7,6},{8,11},{9,8},{10,9... | collective-permute-start | bytes 983048 | tf_op jit(solution)/shard_map/ppermute | solution.py:27
  70.6 2.7 %collective-permute-start.13 = (bf16[320,512]{1,0:T(8,128)(2,1)S(1)}, bf16[320,512]{1,0:T(8,128)(2,1)S(1)}, u32[]{:S(2)}, u32[]{:S(2)}) collective-permute-start(bf16[320,512]{1,0:T(8,128)(2,1)S(1)} %collective-permute-done.12.refs_6_), channel_id=1, source_target_pairs={{0,3},{1,0},{2,1},{3,2},{4,7},{5,4},{6,5},{7,6},{8,11},{9,8},{10,9... | collective-permute-start | bytes 983048 | tf_op jit(solution)/shard_map/ppermute | solution.py:27
  74.3 2.2 %collective-permute-done.11.refs_5_ = bf16[320,512]{1,0:T(8,128)(2,1)S(1)} collective-permute-done((bf16[320,512]{1,0:T(8,128)(2,1)S(1)}, bf16[320,512]{1,0:T(8,128)(2,1)S(1)}, u32[]{:S(2)}, u32[]{:S(2)}) %collective-permute-start.11) | collective-permute-done | bytes 327712 | tf_op jit(solution)/shard_map/ppermute | solution.py:27
  76.5 1.7 collective-permute-start.21
  78.3 5.3 %collective-permute-done.10.refs_3_ = bf16[320,512]{1,0:T(8,128)(2,1)S(1)} collective-permute-done((bf16[320,512]{1,0:T(8,128)(2,1)S(1)}, bf16[320,512]{1,0:T(8,128)(2,1)S(1)}, u32[]{:S(2)}, u32[]{:S(2)}) %collective-permute-start.10) | collective-permute-done | bytes 327712 | tf_op jit(solution)/shard_map/ppermute | solution.py:27
  83.5 1.0 copy-done.6
  84.6 2.9 %gate_up.1.a0 = bf16[640,256]{1,0:T(8,128)(2,1)S(1)} custom-call(s32[4]{0:T(128)S(1)} %copy-done.9, bf16[320,512]{1,0:T(8,128)(2,1)S(1)} %get-tuple-element.42.refs_0_, bf16[320,512]{1,0:T(8,128)(2,1)S(1)} %collective-permute-done.8.refs_1_, bf16[320,512]{1,0:T(8,128)(2,1)S(1)} %collective-permute-done.9.refs_2_, ...), custom_call_target="tpu_custom_call" | custom-call | tf_op jit(solution)/shard_map/gate_up/pallas_call | solution.py:407
  88.0 2.9 %collective-permute-start.16 = (bf16[640,256]{1,0:T(8,128)(2,1)S(1)}, bf16[640,256]{1,0:T(8,128)(2,1)S(1)}, u32[]{:S(2)}, u32[]{:S(2)}) collective-permute-start(bf16[640,256]{1,0:T(8,128)(2,1)S(1)} %gate_up.1.a0), channel_id=1, source_target_pairs={{0,2},{1,3},{2,0},{3,1},{4,6},{5,7},{6,4},{7,5},{8,10},{9,11},{10,... | collective-permute-start | bytes 983048 | tf_op jit(solution)/shard_map/ppermute | solution.py:27
  91.3 4.3 %collective-permute-done.15.a1 = bf16[640,256]{1,0:T(8,128)(2,1)S(1)} collective-permute-done((bf16[640,256]{1,0:T(8,128)(2,1)S(1)}, bf16[640,256]{1,0:T(8,128)(2,1)S(1)}, u32[]{:S(2)}, u32[]{:S(2)}) %collective-permute-start.15) | collective-permute-done | bytes 327712 | tf_op jit(solution)/shard_map/ppermute | solution.py:27
  95.5 6.4 %collective-permute-done.16.a2 = bf16[640,256]{1,0:T(8,128)(2,1)S(1)} collective-permute-done((bf16[640,256]{1,0:T(8,128)(2,1)S(1)}, bf16[640,256]{1,0:T(8,128)(2,1)S(1)}, u32[]{:S(2)}, u32[]{:S(2)}) %collective-permute-start.16) | collective-permute-done | bytes 327712 | tf_op jit(solution)/shard_map/ppermute | solution.py:27
  101.9 2.8 %collective-permute-done.17.a3 = bf16[640,256]{1,0:T(8,128)(2,1)S(1)} collective-permute-done((bf16[640,256]{1,0:T(8,128)(2,1)S(1)}, bf16[640,256]{1,0:T(8,128)(2,1)S(1)}, u32[]{:S(2)}, u32[]{:S(2)}) %collective-permute-start.17) | collective-permute-done | bytes 327712 | tf_op jit(solution)/shard_map/ppermute | solution.py:27
  104.7 3.7 %down.1 = bf16[32,20,512]{2,1,0:T(8,128)(2,1)} custom-call(s32[4]{0:T(128)S(1)} %copy-done.9, bf16[640,256]{1,0:T(8,128)(2,1)S(1)} %gate_up.1.a0, bf16[640,256]{1,0:T(8,128)(2,1)S(1)} %collective-permute-done.15.a1, bf16[640,256]{1,0:T(8,128)(2,1)S(1)} %collective-permute-done.16.a2, bf16[640,256]{1,0:T(8,128)(2,1)S(1)} %collective-permute-done.17.a3, ...), custom_call_target="tpu_custom_call" | custom-call | tf_op jit(solution)/shard_map/down/pallas_call | solution.py:429
  108.4 7.6 %all-to-all-start.1 = ((bf16[32,20,512]{2,1,0:T(8,128)(2,1)}), bf16[32,20,512]{2,1,0:T(8,128)(2,1)S(1)}, u32[]{:S(2)}, u32[]{:S(2)}) async-start(bf16[32,20,512]{2,1,0:T(8,128)(2,1)} %down.1), calls=%async_computation.1 | async-start | bytes 1572864 | tf_op jit(solution)/shard_map/all_to_all | solution.py:438
  117.1 2.5 %collective-permute-start.6 = (f32[128,128]{0,1:T(8,128)S(1)}, f32[128,128]{0,1:T(8,128)S(1)}, u32[]{:S(2)}, u32[]{:S(2)}) collective-permute-start(f32[128,128]{0,1:T(8,128)S(1)} %pad_maximum_fusion.1), channel_id=1, source_target_pairs={{0,2},{1,3},{2,0},{3,1},{4,6},{5,7},{6,4},{7,5},{8,10},{9,11},{10,... | collective-permute-start | bytes 196616 | tf_op jit(solution)/shard_map/ppermute | solution.py:27
  119.9 1.1 collective-permute-done.5
  121.1 2.0 %collective-permute-done.6 = f32[128,128]{0,1:T(8,128)S(1)} collective-permute-done((f32[128,128]{0,1:T(8,128)S(1)}, f32[128,128]{0,1:T(8,128)S(1)}, u32[]{:S(2)}, u32[]{:S(2)}) %collective-permute-start.6) | collective-permute-done | bytes 65568 | tf_op jit(solution)/shard_map/ppermute | solution.py:27
  123.4 15.2 %all-to-all-done.1 = bf16[32,20,512]{2,1,0:T(8,128)(2,1)S(1)} async-done(((bf16[32,20,512]{2,1,0:T(8,128)(2,1)}), bf16[32,20,512]{2,1,0:T(8,128)(2,1)S(1)}, u32[]{:S(2)}, u32[]{:S(2)}) %all-to-all-start.1) | async-done | bytes 655392 | tf_op jit(solution)/shard_map/all_to_all | solution.py:438
  139.5 1.8 collective-permute-start.22
  141.3 3.6 %collective-permute-done.22.par_ref = bf16[128,512]{1,0:T(8,128)(2,1)S(1)} collective-permute-done((bf16[128,512]{1,0:T(8,128)(2,1)S(1)}, bf16[128,512]{1,0:T(8,128)(2,1)S(1)}, u32[]{:S(2)}, u32[]{:S(2)}) %collective-permute-start.22) | collective-permute-done | bytes 131104 | tf_op jit(solution)/shard_map/ppermute | solution.py:31
  145.6 2.1 %embed.1 = (bf16[128,512]{1,0:T(8,128)(2,1)}, f32[136,128]{1,0:T(8,128)}) custom-call(s32[4]{0:T(128)} %pad_add_fusion.here_ref, bf16[128,512]{1,0:T(8,128)(2,1)} %copy-done.4, bf16[128,512]{1,0:T(8,128)(2,1)} %copy-done.12, bf16[128,512]{1,0:T(8,128)(2,1)} %copy-done.13, f32[3,2048]{1,0:T(4,128)} %gain_ref.3, bf16[2048,128]{1,0:T(8,128)(2,1)} %w_ref.1), custom_call_target="tpu_custom_call" | custom-call | tf_op jit(solution)/shard_map/embed/pallas_call | solution.py:468
  148.4 2.5 %collective-permute-start.24 = (f32[136,128]{1,0:T(8,128)}, f32[136,128]{1,0:T(8,128)S(1)}, u32[]{:S(2)}, u32[]{:S(2)}) collective-permute-start(f32[136,128]{1,0:T(8,128)} %get-tuple-element.46.p0), channel_id=1, source_target_pairs={{0,2},{1,3},{2,0},{3,1},{4,6},{5,7},{6,4},{7,5},{8,10},{9,11},{10,... | collective-permute-start | bytes 208904 | tf_op jit(solution)/shard_map/ppermute | solution.py:27
  152.3 1.3 collective-permute-done.24.p2
  155.2 2.0 %vectors.1 = bf16[16,128,128]{2,1,0:T(8,128)(2,1)} custom-call(f32[136,128]{1,0:T(8,128)} %get-tuple-element.46.p0, f32[136,128]{1,0:T(8,128)} %copy-done.17, f32[136,128]{1,0:T(8,128)} %copy-done.18, f32[136,128]{1,0:T(8,128)} %copy-done.19), custom_call_target="tpu_custom_call" | custom-call | tf_op jit(solution)/shard_map/vectors/pallas_call | solution.py:480
  157.2 5.0 %all-to-all-start.2 = ((bf16[16,128,128]{2,1,0:T(8,128)(2,1)}), bf16[16,128,128]{2,1,0:T(8,128)(2,1)S(1)}, u32[]{:S(2)}, u32[]{:S(2)}) async-start(bf16[16,128,128]{2,1,0:T(8,128)(2,1)} %vectors.1), calls=%async_computation.2 | async-start | bytes 1048576 | tf_op jit(solution)/shard_map/all_to_all | solution.py:489
  162.8 1.9 %collective-permute-start.27 = (bf16[128,512]{1,0:T(8,128)(2,1)}, bf16[128,512]{1,0:T(8,128)(2,1)S(1)}, u32[]{:S(2)}, u32[]{:S(2)}) collective-permute-start(bf16[128,512]{1,0:T(8,128)(2,1)} %get-tuple-element.50.p0), channel_id=1, source_target_pairs={{0,2},{1,3},{2,0},{3,1},{4,6},{5,7},{6,4},{7,5},{8,10},{9,11},{10,... | collective-permute-start | bytes 393224 | tf_op jit(solution)/shard_map/ppermute | solution.py:27
  164.8 1.3 collective-permute-start.28
  167.0 2.8 %collective-permute-done.26.p1 = bf16[128,512]{1,0:T(8,128)(2,1)S(1)} collective-permute-done((bf16[128,512]{1,0:T(8,128)(2,1)}, bf16[128,512]{1,0:T(8,128)(2,1)S(1)}, u32[]{:S(2)}, u32[]{:S(2)}) %collective-permute-start.26) | collective-permute-done | bytes 131104 | tf_op jit(solution)/shard_map/ppermute | solution.py:27
  170.3 6.2 %all-to-all-done.2 = bf16[16,128,128]{2,1,0:T(8,128)(2,1)S(1)} async-done(((bf16[16,128,128]{2,1,0:T(8,128)(2,1)}), bf16[16,128,128]{2,1,0:T(8,128)(2,1)S(1)}, u32[]{:S(2)}, u32[]{:S(2)}) %all-to-all-start.2) | async-done | bytes 524320 | tf_op jit(solution)/shard_map/all_to_all | solution.py:489
  176.5 4.3 %collective-permute-start.29 = (bf16[2048,128]{1,0:T(8,128)(2,1)S(1)}, bf16[2048,128]{1,0:T(8,128)(2,1)S(1)}, u32[]{:S(2)}, u32[]{:S(2)}) collective-permute-start(bf16[2048,128]{1,0:T(8,128)(2,1)S(1)} %bitcast.36), channel_id=1, source_target_pairs={{0,8},{8,0},{1,9},{9,1},{2,10},{10,2},{3,11},{11,3},{4,12},{12,4},... | collective-permute-start | bytes 1572872 | tf_op jit(solution)/shard_map/ppermute | solution.py:503
  180.9 1.9 %assemble.1 = bf16[128,2048]{1,0:T(8,128)(2,1)} custom-call(s32[4]{0:T(128)} %pad_add_fusion.here_ref, bf16[128,512]{1,0:T(8,128)(2,1)} %get-tuple-element.50.p0, bf16[128,512]{1,0:T(8,128)(2,1)} %copy-done.14, bf16[128,512]{1,0:T(8,128)(2,1)} %copy-done.15, bf16[128,512]{1,0:T(8,128)(2,1)} %copy-done.16), custom_call_target="tpu_custom_call" | custom-call | tf_op jit(solution)/shard_map/assemble/pallas_call | solution.py:504
  183.6 3.2 %score.1 = f32[1,16]{1,0:T(1,128)} custom-call(s32[5,16]{1,0:T(8,128)} %stack.48.info_ref, bf16[1024,128]{1,0:T(8,128)(2,1)} %doc_ref.1, bf16[2048,128]{1,0:T(8,128)(2,1)} %bitcast.37, bf16[2048,128]{1,0:T(8,128)(2,1)} %copy-done.11), custom_call_target="tpu_custom_call" | custom-call | tf_op jit(solution)/shard_map/score/pallas_call | solution.py:511
  (114 shorter events, 19.8 us)
Async XLA Ops:
  0.6 115.3 %copy-start = (bf16[2048,64]{0,1:T(8,128)(2,1)S(1)}, bf16[2048,64]{0,1:T(8,128)(2,1)}, u32[]{:S(2)}) copy-start(bf16[2048,64]{0,1:T(8,128)(2,1)} %param.21) | copy-start | bytes 786436
  0.6 15.6 %copy-start.8 = (s32[128,8]{0,1:T(8,128)S(1)}, s32[128,8]{0,1:T(8,128)}, u32[]{:S(2)}) copy-start(s32[128,8]{0,1:T(8,128)} %param.22) | copy-start | bytes 12292
  0.7 26.6 %copy-start.3 = (bf16[128,2048]{1,0:T(8,128)(2,1)S(1)}, bf16[128,2048]{1,0:T(8,128)(2,1)}, u32[]{:S(2)}) copy-start(bf16[128,2048]{1,0:T(8,128)(2,1)} %x_ref) | copy-start | bytes 1572868
  1.8 25.4 %collective-permute-start.4 = (bf16[2048,128]{1,0:T(8,128)(2,1)S(1)}, bf16[2048,128]{1,0:T(8,128)(2,1)S(1)}, u32[]{:S(2)}, u32[]{:S(2)}) collective-permute-start(bf16[2048,128]{1,0:T(8,128)(2,1)S(1)} %dynamic-slice_bitcast_fusion.1), channel_id=1, source_target_pairs={{0,4},{4,0},{1,5},{5,1},{2,6},{6,2},{3,7},{7,3},{8,12},{12,8},{9,1... | collective-permute-start | bytes 1572872 | tf_op jit(solution)/shard_map/ppermute | solution.py:31
  6.1 10.2 %copy-start.9 = (s32[4]{0:T(128)S(1)}, s32[4]{0:T(128)}, u32[]{:S(2)}) copy-start(s32[4]{0:T(128)} %pad_add_fusion.here_ref) | copy-start | bytes 52
  11.2 36.5 %copy-start.2 = (bf16[2,2048,128]{2,1,0:T(8,128)(2,1)S(1)}, bf16[2,2048,128]{2,1,0:T(8,128)(2,1)}, u32[]{:S(2)}) copy-start(bf16[2,2048,128]{2,1,0:T(8,128)(2,1)} %refs_10_.1) | copy-start | bytes 3145732
  11.2 6.0 %collective-permute-start = (bf16[128,512]{1,0:T(8,128)(2,1)}, bf16[128,512]{1,0:T(8,128)(2,1)S(1)}, u32[]{:S(2)}, u32[]{:S(2)}) collective-permute-start(bf16[128,512]{1,0:T(8,128)(2,1)} %get-tuple-element.31), channel_id=1, source_target_pairs={{0,1},{1,2},{2,3},{3,0},{4,5},{5,6},{6,7},{7,4},{8,9},{9,10},{10,1... | collective-permute-start | bytes 393224 | tf_op jit(solution)/shard_map/ppermute | solution.py:27
  12.6 7.9 %collective-permute-start.1 = (bf16[128,512]{1,0:T(8,128)(2,1)}, bf16[128,512]{1,0:T(8,128)(2,1)S(1)}, u32[]{:S(2)}, u32[]{:S(2)}) collective-permute-start(bf16[128,512]{1,0:T(8,128)(2,1)} %get-tuple-element.32), channel_id=1, source_target_pairs={{0,2},{1,3},{2,0},{3,1},{4,6},{5,7},{6,4},{7,5},{8,10},{9,11},{10,... | collective-permute-start | bytes 393224 | tf_op jit(solution)/shard_map/ppermute | solution.py:27
  15.2 5.6 %collective-permute-start.2 = (bf16[128,512]{1,0:T(8,128)(2,1)}, bf16[128,512]{1,0:T(8,128)(2,1)S(1)}, u32[]{:S(2)}, u32[]{:S(2)}) collective-permute-start(bf16[128,512]{1,0:T(8,128)(2,1)} %get-tuple-element.33), channel_id=1, source_target_pairs={{0,3},{1,0},{2,1},{3,2},{4,7},{5,4},{6,5},{7,6},{8,11},{9,8},{10,9... | collective-permute-start | bytes 393224 | tf_op jit(solution)/shard_map/ppermute | solution.py:27
  20.8 27.9 %copy-start.7 = (f32[3,2048]{1,0:T(4,128)S(1)}, f32[3,2048]{1,0:T(4,128)}, u32[]{:S(2)}) copy-start(f32[3,2048]{1,0:T(4,128)} %gain_ref.3) | copy-start | bytes 73732
  21.8 5.4 %collective-permute-start.3 = (bf16[128,512]{1,0:T(8,128)(2,1)S(1)}, bf16[128,512]{1,0:T(8,128)(2,1)S(1)}, u32[]{:S(2)}, u32[]{:S(2)}) collective-permute-start(bf16[128,512]{1,0:T(8,128)(2,1)S(1)} %add_convert_fusion.own_ref), channel_id=1, source_target_pairs={{0,4},{4,0},{1,5},{5,1},{2,6},{6,2},{3,7},{7,3},{8,12},{12,8},{9,1... | collective-permute-start | bytes 393224 | tf_op jit(solution)/shard_map/ppermute | solution.py:31
  29.0 87.2 %copy-start.4 = (bf16[128,512]{1,0:T(8,128)(2,1)}, bf16[128,512]{1,0:T(8,128)(2,1)S(1)}, u32[]{:S(2)}) copy-start(bf16[128,512]{1,0:T(8,128)(2,1)S(1)} %get-tuple-element.38.hidden_ref) | copy-start | bytes 393220
  29.0 31.2 %all-to-all-start = ((bf16[32,40,256]{2,1,0:T(8,128)(2,1)}), bf16[32,40,256]{2,1,0:T(8,128)(2,1)S(1)}, u32[]{:S(2)}, u32[]{:S(2)}) async-start(bf16[32,40,256]{2,1,0:T(8,128)(2,1)} %get-tuple-element.39), calls=%async_computation | async-start | bytes 1310720 | tf_op jit(solution)/shard_map/all_to_all | solution.py:392
  40.6 42.9 %copy-start.1 = (bf16[2,2048,128]{2,1,0:T(8,128)(2,1)S(1)}, bf16[2,2048,128]{2,1,0:T(8,128)(2,1)}, u32[]{:S(2)}) copy-start(bf16[2,2048,128]{2,1,0:T(8,128)(2,1)} %refs_9_.1) | copy-start | bytes 3145732
  42.8 20.3 %collective-permute-start.20 = (bf16[2,128,512]{2,1,0:T(8,128)(2,1)}, bf16[2,128,512]{2,1,0:T(8,128)(2,1)}, u32[]{:S(2)}, u32[]{:S(2)}) collective-permute-start(bf16[2,128,512]{2,1,0:T(8,128)(2,1)} %get-tuple-element.60), channel_id=1, source_target_pairs={{0,3},{1,0},{2,1},{3,2},{4,7},{5,4},{6,5},{7,6},{8,11},{9,8},{10,9... | collective-permute-start | bytes 786440 | tf_op jit(solution)/shard_map/ppermute | solution.py:27
  44.9 19.2 %collective-permute-start.19 = (bf16[2,128,512]{2,1,0:T(8,128)(2,1)}, bf16[2,128,512]{2,1,0:T(8,128)(2,1)}, u32[]{:S(2)}, u32[]{:S(2)}) collective-permute-start(bf16[2,128,512]{2,1,0:T(8,128)(2,1)} %get-tuple-element.61), channel_id=1, source_target_pairs={{0,2},{1,3},{2,0},{3,1},{4,6},{5,7},{6,4},{7,5},{8,10},{9,11},{10,... | collective-permute-start | bytes 786440 | tf_op jit(solution)/shard_map/ppermute | solution.py:27
  45.6 21.3 %collective-permute-start.18 = (bf16[2,128,512]{2,1,0:T(8,128)(2,1)}, bf16[2,128,512]{2,1,0:T(8,128)(2,1)}, u32[]{:S(2)}, u32[]{:S(2)}) collective-permute-start(bf16[2,128,512]{2,1,0:T(8,128)(2,1)} %get-tuple-element.62), channel_id=1, source_target_pairs={{0,1},{1,2},{2,3},{3,0},{4,5},{5,6},{6,7},{7,4},{8,9},{9,10},{10,1... | collective-permute-start | bytes 786440 | tf_op jit(solution)/shard_map/ppermute | solution.py:27
  60.3 10.3 %collective-permute-start.8 = (bf16[320,512]{1,0:T(8,128)(2,1)S(1)}, bf16[320,512]{1,0:T(8,128)(2,1)S(1)}, u32[]{:S(2)}, u32[]{:S(2)}) collective-permute-start(bf16[320,512]{1,0:T(8,128)(2,1)S(1)} %get-tuple-element.42.refs_0_), channel_id=1, source_target_pairs={{0,1},{1,2},{2,3},{3,0},{4,5},{5,6},{6,7},{7,4},{8,9},{9,10},{10,1... | collective-permute-start | bytes 983048 | tf_op jit(solution)/shard_map/ppermute | solution.py:27
  61.4 9.2 %collective-permute-start.12 = (bf16[320,512]{1,0:T(8,128)(2,1)S(1)}, bf16[320,512]{1,0:T(8,128)(2,1)S(1)}, u32[]{:S(2)}, u32[]{:S(2)}) collective-permute-start(bf16[320,512]{1,0:T(8,128)(2,1)S(1)} %get-tuple-element.43.refs_4_), channel_id=1, source_target_pairs={{0,3},{1,0},{2,1},{3,2},{4,7},{5,4},{6,5},{7,6},{8,11},{9,8},{10,9... | collective-permute-start | bytes 983048 | tf_op jit(solution)/shard_map/ppermute | solution.py:27
  64.0 12.5 %collective-permute-start.11 = (bf16[320,512]{1,0:T(8,128)(2,1)S(1)}, bf16[320,512]{1,0:T(8,128)(2,1)S(1)}, u32[]{:S(2)}, u32[]{:S(2)}) collective-permute-start(bf16[320,512]{1,0:T(8,128)(2,1)S(1)} %get-tuple-element.43.refs_4_), channel_id=1, source_target_pairs={{0,1},{1,2},{2,3},{3,0},{4,5},{5,6},{6,7},{7,4},{8,9},{9,10},{10,1... | collective-permute-start | bytes 983048 | tf_op jit(solution)/shard_map/ppermute | solution.py:27
  64.1 14.1 %collective-permute-start.14 = (bf16[2048,128]{1,0:T(8,128)(2,1)}, bf16[2048,128]{1,0:T(8,128)(2,1)S(1)}, u32[]{:S(2)}, u32[]{:S(2)}) collective-permute-start(bf16[2048,128]{1,0:T(8,128)(2,1)} %dynamic-slice_bitcast_fusion), channel_id=1, source_target_pairs={{0,4},{4,0},{1,5},{5,1},{2,6},{6,2},{3,7},{7,3},{8,12},{12,8},{9,1... | collective-permute-start | bytes 1572872 | tf_op jit(solution)/shard_map/ppermute | solution.py:31
  67.8 10.5 %collective-permute-start.9 = (bf16[320,512]{1,0:T(8,128)(2,1)S(1)}, bf16[320,512]{1,0:T(8,128)(2,1)S(1)}, u32[]{:S(2)}, u32[]{:S(2)}) collective-permute-start(bf16[320,512]{1,0:T(8,128)(2,1)S(1)} %get-tuple-element.42.refs_0_), channel_id=1, source_target_pairs={{0,3},{1,0},{2,1},{3,2},{4,7},{5,4},{6,5},{7,6},{8,11},{9,8},{10,9... | collective-permute-start | bytes 983048 | tf_op jit(solution)/shard_map/ppermute | solution.py:27
  70.6 12.9 %collective-permute-start.10 = (bf16[320,512]{1,0:T(8,128)(2,1)S(1)}, bf16[320,512]{1,0:T(8,128)(2,1)S(1)}, u32[]{:S(2)}, u32[]{:S(2)}) collective-permute-start(bf16[320,512]{1,0:T(8,128)(2,1)S(1)} %collective-permute-done.8.refs_1_), channel_id=1, source_target_pairs={{0,1},{1,2},{2,3},{3,0},{4,5},{5,6},{6,7},{7,4},{8,9},{9,10},{10,1... | collective-permute-start | bytes 983048 | tf_op jit(solution)/shard_map/ppermute | solution.py:27
  70.6 12.9 %collective-permute-start.13 = (bf16[320,512]{1,0:T(8,128)(2,1)S(1)}, bf16[320,512]{1,0:T(8,128)(2,1)S(1)}, u32[]{:S(2)}, u32[]{:S(2)}) collective-permute-start(bf16[320,512]{1,0:T(8,128)(2,1)S(1)} %collective-permute-done.12.refs_6_), channel_id=1, source_target_pairs={{0,3},{1,0},{2,1},{3,2},{4,7},{5,4},{6,5},{7,6},{8,11},{9,8},{10,9... | collective-permute-start | bytes 983048 | tf_op jit(solution)/shard_map/ppermute | solution.py:27
  76.5 14.8 %collective-permute-start.21 = (bf16[4,128,512]{2,1,0:T(8,128)(2,1)S(1)}, bf16[4,128,512]{2,1,0:T(8,128)(2,1)S(1)}, u32[]{:S(2)}, u32[]{:S(2)}) collective-permute-start(bf16[4,128,512]{2,1,0:T(8,128)(2,1)S(1)} %pad_maximum_fusion), channel_id=1, source_target_pairs={{0,4},{4,0},{1,5},{5,1},{2,6},{6,2},{3,7},{7,3},{8,12},{12,8},{9,1... | collective-permute-start | bytes 1572872 | tf_op jit(solution)/shard_map/ppermute | solution.py:31
  87.5 8.0 %collective-permute-start.15 = (bf16[640,256]{1,0:T(8,128)(2,1)S(1)}, bf16[640,256]{1,0:T(8,128)(2,1)S(1)}, u32[]{:S(2)}, u32[]{:S(2)}) collective-permute-start(bf16[640,256]{1,0:T(8,128)(2,1)S(1)} %gate_up.1.a0), channel_id=1, source_target_pairs={{0,1},{1,2},{2,3},{3,0},{4,5},{5,6},{6,7},{7,4},{8,9},{9,10},{10,1... | collective-permute-start | bytes 983048 | tf_op jit(solution)/shard_map/ppermute | solution.py:27
  88.0 14.0 %collective-permute-start.16 = (bf16[640,256]{1,0:T(8,128)(2,1)S(1)}, bf16[640,256]{1,0:T(8,128)(2,1)S(1)}, u32[]{:S(2)}, u32[]{:S(2)}) collective-permute-start(bf16[640,256]{1,0:T(8,128)(2,1)S(1)} %gate_up.1.a0), channel_id=1, source_target_pairs={{0,2},{1,3},{2,0},{3,1},{4,6},{5,7},{6,4},{7,5},{8,10},{9,11},{10,... | collective-permute-start | bytes 983048 | tf_op jit(solution)/shard_map/ppermute | solution.py:27
  90.8 13.8 %collective-permute-start.17 = (bf16[640,256]{1,0:T(8,128)(2,1)S(1)}, bf16[640,256]{1,0:T(8,128)(2,1)S(1)}, u32[]{:S(2)}, u32[]{:S(2)}) collective-permute-start(bf16[640,256]{1,0:T(8,128)(2,1)S(1)} %gate_up.1.a0), channel_id=1, source_target_pairs={{0,3},{1,0},{2,1},{3,2},{4,7},{5,4},{6,5},{7,6},{8,11},{9,8},{10,9... | collective-permute-start | bytes 983048 | tf_op jit(solution)/shard_map/ppermute | solution.py:27
  108.4 30.2 %all-to-all-start.1 = ((bf16[32,20,512]{2,1,0:T(8,128)(2,1)}), bf16[32,20,512]{2,1,0:T(8,128)(2,1)S(1)}, u32[]{:S(2)}, u32[]{:S(2)}) async-start(bf16[32,20,512]{2,1,0:T(8,128)(2,1)} %down.1), calls=%async_computation.1 | async-start | bytes 1572864 | tf_op jit(solution)/shard_map/all_to_all | solution.py:438
  115.9 46.3 %copy-start.20 = (s32[32,3]{0,1:T(4,128)S(1)}, s32[32,3]{0,1:T(4,128)}, u32[]{:S(2)}) copy-start(s32[32,3]{0,1:T(4,128)} %param.16) | copy-start | bytes 1156
  116.0 46.7 %copy-start.22 = (s32[1,16]{1,0:T(1,128)S(1)}, s32[1,16]{1,0:T(1,128)}, u32[]{:S(2)}) copy-start(s32[1,16]{1,0:T(1,128)} %param.29) | copy-start | bytes 196
  116.0 50.3 %copy-start.21 = (s32[1,1024]{1,0:T(1,128)S(1)}, s32[1,1024]{1,0:T(1,128)}, u32[]{:S(2)}) copy-start(s32[1,1024]{1,0:T(1,128)} %param.28) | copy-start | bytes 12292
  116.3 4.7 %collective-permute-start.5 = (f32[128,128]{0,1:T(8,128)S(1)}, f32[128,128]{0,1:T(8,128)S(1)}, u32[]{:S(2)}, u32[]{:S(2)}) collective-permute-start(f32[128,128]{0,1:T(8,128)S(1)} %pad_maximum_fusion.1), channel_id=1, source_target_pairs={{0,1},{1,2},{2,3},{3,0},{4,5},{5,6},{6,7},{7,4},{8,9},{9,10},{10,1... | collective-permute-start | bytes 196616 | tf_op jit(solution)/shard_map/ppermute | solution.py:27
  117.1 5.9 %collective-permute-start.6 = (f32[128,128]{0,1:T(8,128)S(1)}, f32[128,128]{0,1:T(8,128)S(1)}, u32[]{:S(2)}, u32[]{:S(2)}) collective-permute-start(f32[128,128]{0,1:T(8,128)S(1)} %pad_maximum_fusion.1), channel_id=1, source_target_pairs={{0,2},{1,3},{2,0},{3,1},{4,6},{5,7},{6,4},{7,5},{8,10},{9,11},{10,... | collective-permute-start | bytes 196616 | tf_op jit(solution)/shard_map/ppermute | solution.py:27
  119.6 3.6 %collective-permute-start.7 = (f32[128,128]{0,1:T(8,128)S(1)}, f32[128,128]{0,1:T(8,128)S(1)}, u32[]{:S(2)}, u32[]{:S(2)}) collective-permute-start(f32[128,128]{0,1:T(8,128)S(1)} %pad_maximum_fusion.1), channel_id=1, source_target_pairs={{0,3},{1,0},{2,1},{3,2},{4,7},{5,4},{6,5},{7,6},{8,11},{9,8},{10,9... | collective-permute-start | bytes 196616 | tf_op jit(solution)/shard_map/ppermute | solution.py:27
  139.5 5.4 %collective-permute-start.22 = (bf16[128,512]{1,0:T(8,128)(2,1)S(1)}, bf16[128,512]{1,0:T(8,128)(2,1)S(1)}, u32[]{:S(2)}, u32[]{:S(2)}) collective-permute-start(bf16[128,512]{1,0:T(8,128)(2,1)S(1)} %fusion.1.moe_ref), channel_id=1, source_target_pairs={{0,4},{4,0},{1,5},{5,1},{2,6},{6,2},{3,7},{7,3},{8,12},{12,8},{9,1... | collective-permute-start | bytes 393224 | tf_op jit(solution)/shard_map/ppermute | solution.py:31
  147.7 4.6 %collective-permute-start.23 = (f32[136,128]{1,0:T(8,128)}, f32[136,128]{1,0:T(8,128)S(1)}, u32[]{:S(2)}, u32[]{:S(2)}) collective-permute-start(f32[136,128]{1,0:T(8,128)} %get-tuple-element.46.p0), channel_id=1, source_target_pairs={{0,1},{1,2},{2,3},{3,0},{4,5},{5,6},{6,7},{7,4},{8,9},{9,10},{10,1... | collective-permute-start | bytes 208904 | tf_op jit(solution)/shard_map/ppermute | solution.py:27
  148.4 5.1 %collective-permute-start.24 = (f32[136,128]{1,0:T(8,128)}, f32[136,128]{1,0:T(8,128)S(1)}, u32[]{:S(2)}, u32[]{:S(2)}) collective-permute-start(f32[136,128]{1,0:T(8,128)} %get-tuple-element.46.p0), channel_id=1, source_target_pairs={{0,2},{1,3},{2,0},{3,1},{4,6},{5,7},{6,4},{7,5},{8,10},{9,11},{10,... | collective-permute-start | bytes 208904 | tf_op jit(solution)/shard_map/ppermute | solution.py:27
  150.9 3.7 %collective-permute-start.25 = (f32[136,128]{1,0:T(8,128)}, f32[136,128]{1,0:T(8,128)S(1)}, u32[]{:S(2)}, u32[]{:S(2)}) collective-permute-start(f32[136,128]{1,0:T(8,128)} %get-tuple-element.46.p0), channel_id=1, source_target_pairs={{0,3},{1,0},{2,1},{3,2},{4,7},{5,4},{6,5},{7,6},{8,11},{9,8},{10,9... | collective-permute-start | bytes 208904 | tf_op jit(solution)/shard_map/ppermute | solution.py:27
  157.2 19.3 %all-to-all-start.2 = ((bf16[16,128,128]{2,1,0:T(8,128)(2,1)}), bf16[16,128,128]{2,1,0:T(8,128)(2,1)S(1)}, u32[]{:S(2)}, u32[]{:S(2)}) async-start(bf16[16,128,128]{2,1,0:T(8,128)(2,1)} %vectors.1), calls=%async_computation.2 | async-start | bytes 1048576 | tf_op jit(solution)/shard_map/all_to_all | solution.py:489
  162.7 7.1 %collective-permute-start.26 = (bf16[128,512]{1,0:T(8,128)(2,1)}, bf16[128,512]{1,0:T(8,128)(2,1)S(1)}, u32[]{:S(2)}, u32[]{:S(2)}) collective-permute-start(bf16[128,512]{1,0:T(8,128)(2,1)} %get-tuple-element.50.p0), channel_id=1, source_target_pairs={{0,1},{1,2},{2,3},{3,0},{4,5},{5,6},{6,7},{7,4},{8,9},{9,10},{10,1... | collective-permute-start | bytes 393224 | tf_op jit(solution)/shard_map/ppermute | solution.py:27
  162.8 7.0 %collective-permute-start.27 = (bf16[128,512]{1,0:T(8,128)(2,1)}, bf16[128,512]{1,0:T(8,128)(2,1)S(1)}, u32[]{:S(2)}, u32[]{:S(2)}) collective-permute-start(bf16[128,512]{1,0:T(8,128)(2,1)} %get-tuple-element.50.p0), channel_id=1, source_target_pairs={{0,2},{1,3},{2,0},{3,1},{4,6},{5,7},{6,4},{7,5},{8,10},{9,11},{10,... | collective-permute-start | bytes 393224 | tf_op jit(solution)/shard_map/ppermute | solution.py:27
  164.8 5.6 %collective-permute-start.28 = (bf16[128,512]{1,0:T(8,128)(2,1)}, bf16[128,512]{1,0:T(8,128)(2,1)S(1)}, u32[]{:S(2)}, u32[]{:S(2)}) collective-permute-start(bf16[128,512]{1,0:T(8,128)(2,1)} %get-tuple-element.50.p0), channel_id=1, source_target_pairs={{0,3},{1,0},{2,1},{3,2},{4,7},{5,4},{6,5},{7,6},{8,11},{9,8},{10,9... | collective-permute-start | bytes 393224 | tf_op jit(solution)/shard_map/ppermute | solution.py:27
  169.8 11.0 %copy-start.14 = (bf16[128,512]{1,0:T(8,128)(2,1)}, bf16[128,512]{1,0:T(8,128)(2,1)S(1)}, u32[]{:S(2)}) copy-start(bf16[128,512]{1,0:T(8,128)(2,1)S(1)} %collective-permute-done.26.p1) | copy-start | bytes 393220
  169.8 11.0 %copy-start.15 = (bf16[128,512]{1,0:T(8,128)(2,1)}, bf16[128,512]{1,0:T(8,128)(2,1)S(1)}, u32[]{:S(2)}) copy-start(bf16[128,512]{1,0:T(8,128)(2,1)S(1)} %collective-permute-done.27.p2) | copy-start | bytes 393220
  170.3 10.5 %copy-start.16 = (bf16[128,512]{1,0:T(8,128)(2,1)}, bf16[128,512]{1,0:T(8,128)(2,1)S(1)}, u32[]{:S(2)}) copy-start(bf16[128,512]{1,0:T(8,128)(2,1)S(1)} %collective-permute-done.28.p3) | copy-start | bytes 393220
  176.5 6.3 %copy-start.10 = (bf16[16,128,128]{2,1,0:T(8,128)(2,1)}, bf16[16,128,128]{2,1,0:T(8,128)(2,1)S(1)}, u32[]{:S(2)}) copy-start(bf16[16,128,128]{2,1,0:T(8,128)(2,1)S(1)} %all-to-all-done.2) | copy-start | bytes 1572868
  176.5 6.2 %collective-permute-start.29 = (bf16[2048,128]{1,0:T(8,128)(2,1)S(1)}, bf16[2048,128]{1,0:T(8,128)(2,1)S(1)}, u32[]{:S(2)}, u32[]{:S(2)}) collective-permute-start(bf16[2048,128]{1,0:T(8,128)(2,1)S(1)} %bitcast.36), channel_id=1, source_target_pairs={{0,8},{8,0},{1,9},{9,1},{2,10},{10,2},{3,11},{11,3},{4,12},{12,4},... | collective-permute-start | bytes 1572872 | tf_op jit(solution)/shard_map/ppermute | solution.py:503
  (8 other events, 13.7 us)

commit v8 on v7

--- a/solution.py
+++ b/solution.py
@@ -19,6 +19,7 @@
 NEG = -1e30
 W = ("z", "xl", "core")
 N = ("xh", "y")
+E = W + ("xh",)
 f32 = jnp.float32
 bf16 = jnp.bfloat16
 
@@ -39,10 +40,7 @@
     x_hbm,
     w_hbm,
     out_hbm,
-    out0,
-    out1,
-    out2,
-    out3,
+    out_ref,
     x_ref,
     w_ref,
     out_w_ref,
@@ -102,24 +100,24 @@
         )
     mixed = jnp.concatenate(mixed, axis=1)
     copies[4].wait()
-    j = here_ref[1]
-    for k, out_ref in enumerate((out0, out1, out2, out3)):
-        part = lax.rem(j + k, 4)
-        columns = pl.ds(pl.multiple_of(part * 512, 512), 512)
-        out_ref[...] = jnp.dot(mixed, out_w_ref[:, columns], preferred_element_type=f32).astype(bf16)
-
-
-def choose_kernel(here_ref, routes_ref, out_ref):
-    expert = 2 * lax.broadcasted_iota(jnp.int32, (WIDE, TOK), 0) + here_ref[0]
-    hit = jnp.zeros((WIDE, TOK), f32)
+    for n in range(8):
+        at = 512 * (n % 4) + 256 * (n // 4)
+        out_ref[n] = jnp.dot(
+            mixed, out_w_ref[:, at : at + 256], preferred_element_type=f32
+        ).astype(bf16)
+
+
+def choose_kernel(routes_ref, out_ref):
+    expert = lax.broadcasted_iota(jnp.int32, (EXPERTS, TOK), 0)
+    hit = jnp.zeros((EXPERTS, TOK), f32)
     for k in range(TOPK):
         hit = hit + (routes_ref[k : k + 1, :] == expert).astype(f32)
     sooner = lax.broadcasted_iota(jnp.int32, (TOK, TOK), 0)
     earlier = (sooner < lax.broadcasted_iota(jnp.int32, (TOK, TOK), 1)).astype(f32).astype(bf16)
     before = jnp.dot(hit.astype(bf16), earlier, preferred_element_type=f32)
     place = jnp.where(hit > 0, before, -1.0).astype(bf16)
-    owner = CAP * lax.broadcasted_iota(jnp.int32, (WIDE * CAP, WIDE), 1)
-    slot = lax.broadcasted_iota(jnp.int32, (WIDE * CAP, WIDE), 0) - owner
+    owner = CAP * lax.broadcasted_iota(jnp.int32, (EXPERTS * CAP, EXPERTS), 1)
+    slot = lax.broadcasted_iota(jnp.int32, (EXPERTS * CAP, EXPERTS), 0) - owner
     inside = (slot >= 0) & (slot < CAP)
     spread = jnp.dot(inside.astype(f32).astype(bf16), place, preferred_element_type=f32)
     slot = jnp.sum(jnp.where(inside, slot, 0).astype(f32), axis=1, keepdims=True)
@@ -127,34 +125,40 @@
 
 
 def packed(rows):
-    return jnp.concatenate([rows[:, 0:256], rows[:, 256:512]], axis=0).astype(bf16)
-
-
-def dispatch_kernel(here_ref, x_ref, own_ref, par_ref, choose_ref, hidden_ref, rows_ref):
-    j = here_ref[1]
-    mine = x_ref[:, pl.ds(pl.multiple_of(j * 512, 512), 512)].astype(f32)
-    hidden = (mine + (own_ref[...].astype(f32) + par_ref[...].astype(f32))).astype(bf16)
+    return jnp.concatenate([rows[:, 0:128], rows[:, 128:256]], axis=0).astype(bf16)
+
+
+def mine_of(here_ref):
+    return pl.ds(pl.multiple_of(here_ref[1] * 512 + here_ref[0] * 256, 256), 256)
+
+
+def dispatch_kernel(here_ref, x_ref, parts_ref, choose_ref, hidden_ref, rows_ref):
+    total = x_ref[:, mine_of(here_ref)].astype(f32)
+    for n in range(8):
+        total = total + parts_ref[n].astype(f32)
+    hidden = total.astype(bf16)
     hidden_ref[...] = hidden
     rows = jnp.dot(choose_ref[...], hidden, preferred_element_type=f32)
-    for s in range(WIDE):
-        rows_ref[s] = packed(rows[s * CAP : (s + 1) * CAP])
+    for e in range(EXPERTS):
+        rows_ref[e] = packed(rows[e * CAP : (e + 1) * CAP])
 
 
 def unpack_kernel(in_ref, top_ref, bottom_ref, scratch):
     for half, out_ref in enumerate((top_ref, bottom_ref)):
         for s in range(WIDE // 2):
-            rows = in_ref[half * (WIDE // 2) + s].astype(f32)
             at = slice(s * CAP, (s + 1) * CAP)
-            scratch[at, 0:256] = rows[0:CAP]
-            scratch[at, 256:512] = rows[CAP:]
+            for h in range(2):
+                rows = in_ref[half * WIDE + 2 * s + h].astype(f32)
+                scratch[at, 256 * h : 256 * h + 128] = rows[0:CAP]
+                scratch[at, 256 * h + 128 : 256 * h + 256] = rows[CAP:]
         out_ref[...] = scratch[...].astype(bf16)
 
 
 def gate_up_kernel(here_ref, *refs):
     halves = refs[0:4], refs[4:8]
-    gain_hbm, gate_hbm, up_hbm, gate_par, up_par, out_ref, gain_ref, w_ref, sems = refs[8:]
+    gain_hbm, gate_hbm, up_hbm, both_par, out_ref, gain_ref, w_ref, sems = refs[8:]
     i, j = here_ref[0], here_ref[1]
-    sources = (gate_hbm.at[i], up_hbm.at[i], gate_par, up_par)
+    sources = (gate_hbm.at[i], up_hbm.at[i], both_par.at[0], both_par.at[1])
     copies = [
         pltpu.make_async_copy(source, w_ref.at[n], sems.at[n]) for n, source in enumerate(sources)
     ]
@@ -206,25 +210,65 @@
         for copy in copies[k]:
             copy.wait()
         total = total + jnp.dot(a[...], w_ref[k], preferred_element_type=f32)
-    size = out_ref.shape[1]
     for s in range(WIDE):
-        out_ref[s] = total[s * size : (s + 1) * size].astype(bf16)
-
-
-def embed_kernel(here_ref, hidden_ref, moe_ref, par_ref, gain_ref, w_ref, layer_ref, part_ref):
-    mine = pl.ds(pl.multiple_of(here_ref[1] * 512, 512), 512)
-    layer = hidden_ref[...].astype(f32) + (moe_ref[...].astype(f32) + par_ref[...].astype(f32))
-    layer = layer.astype(bf16)
+        rows = total[s * CAP : (s + 1) * CAP]
+        out_ref[2 * s] = packed(rows[:, 0:256])
+        out_ref[2 * s + 1] = packed(rows[:, 256:512])
+
+
+def mixing_kernel(whole_ref, routes_ref, high_ref, low_ref):
+    logits = whole_ref[:, 0:EXPERTS]
+    logits = logits * lax.rsqrt(whole_ref[:, EXPERTS : EXPERTS + 1] / 2048.0 + EPS)
+    expert = lax.broadcasted_iota(jnp.int32, (TOK, EXPERTS), 1)
+    hit = jnp.zeros((TOK, EXPERTS), f32)
+    for k in range(TOPK):
+        hit = hit + (routes_ref[:, k : k + 1] == expert).astype(f32)
+    lifted = jax.nn.sigmoid(logits) * hit
+    gates = lifted / jnp.sum(lifted, axis=1, keepdims=True)
+    sooner = lax.broadcasted_iota(jnp.int32, (TOK, TOK), 1)
+    earlier = (sooner < lax.broadcasted_iota(jnp.int32, (TOK, TOK), 0)).astype(f32).astype(bf16)
+    before = jnp.dot(earlier, hit.astype(bf16), preferred_element_type=f32)
+    place = jnp.where(hit > 0, before, -1.0).astype(bf16)
+    size = EXPERTS * 2 * CAP
+    owner = 2 * CAP * lax.broadcasted_iota(jnp.int32, (EXPERTS, size), 0)
+    offset = lax.broadcasted_iota(jnp.int32, (EXPERTS, size), 1) - owner
+    inside = ((offset >= 0) & (offset < 2 * CAP)).astype(f32).astype(bf16)
+    spread = jnp.dot(place, inside, preferred_element_type=f32)
+    spot = lax.rem(lax.broadcasted_iota(jnp.int32, (TOK, size), 1), 2 * CAP)
+    left = spread == spot.astype(f32)
+    right = spread == (spot - CAP).astype(f32)
+    high = gates.astype(bf16)
+    low = (gates - high.astype(f32)).astype(bf16)
+    for gate, ref in ((high, high_ref), (low, low_ref)):
+        value = jnp.dot(gate, inside, preferred_element_type=f32)
+        ref[0:TOK] = jnp.where(left & (spot < CAP), value, 0.0).astype(bf16)
+        ref[TOK:] = jnp.where(right & (spot >= CAP), value, 0.0).astype(bf16)
+
+
+def embed_kernel(
+    here_ref, hidden_ref, high_ref, low_ref, back_ref, gain_ref, w_ref, layer_ref, part_ref
+):
+    mine = mine_of(here_ref)
+    back = back_ref[...]
+    moe = jnp.dot(high_ref[...], back, preferred_element_type=f32)
+    moe = moe + jnp.dot(low_ref[...], back, preferred_element_type=f32)
+    moe = jnp.concatenate([moe[0:TOK], moe[TOK:]], axis=1)
+    layer = (hidden_ref[...].astype(f32) + moe).astype(bf16)
     layer_ref[...] = layer
     layer = layer.astype(f32)
     scaled = (layer * gain_ref[2:3, mine]).astype(bf16)
-    part_ref[0:TOK, :] = jnp.dot(scaled, w_ref[mine, :], preferred_element_type=f32)
+    part = jnp.dot(scaled, w_ref[mine, :], preferred_element_type=f32)
     square = jnp.broadcast_to(jnp.sum(layer * layer, axis=1, keepdims=True), (TOK, TOK))
-    part_ref[TOK:, :] = jnp.transpose(square)[0:8]
-
-
-def vector_kernel(p0, p1, p2, p3, out_ref):
-    whole = p0[...] + p1[...] + p2[...] + p3[...]
+    square = jnp.transpose(square)[0:8]
+    for copy in range(8):
+        part_ref[copy, 0:TOK, :] = part
+        part_ref[copy, TOK:, :] = square
+
+
+def vector_kernel(parts_ref, out_ref):
+    whole = parts_ref[0]
+    for n in range(1, 8):
+        whole = whole + parts_ref[n]
     square = jnp.transpose(jnp.broadcast_to(whole[TOK : TOK + 1], (TOK, TOK)))
     embedded = whole[0:TOK] * lax.rsqrt(square / 2048.0 + EPS)
     norm = jnp.sum(embedded * embedded, axis=1, keepdims=True)
@@ -327,14 +371,11 @@
     def cut(array, part, axis):
         return lax.dynamic_slice_in_dim(array, lax.rem(part, 4) * 512, 512, axis)
 
-    gate_sent, tokens = lax.optimization_barrier((pick(w_gate, 1 - i), tokens))
-    gate_par = x_swap(gate_sent)
-
     attn = pl.pallas_call(
         attention_kernel,
-        out_shape=(jax.ShapeDtypeStruct((TOK, 512), bf16),) * 4,
+        out_shape=jax.ShapeDtypeStruct((8, TOK, 256), bf16),
         in_specs=[smem()] * 2 + [vmem()] * 2 + [hbm()] * 3,
-        out_specs=(vmem(),) * 4,
+        out_specs=vmem(),
         scratch_shapes=[
             pltpu.VMEM((TOK, 2048), bf16),
             pltpu.VMEM((3, 2048, 256), bf16),
@@ -352,44 +393,30 @@
         w_qkv.transpose(1, 0, 2),
         w_out,
     )
-    attn_parts = [y_shift(attn[k], k) for k in (1, 2, 3)]
-
-    downs = [cut(w_down, j, 2)] + [y_shift(cut(w_down, j + k, 2), k) for k in (1, 2, 3)]
-    down_par = x_swap(jnp.stack([pick(d, 1 - i) for d in downs]))
-
-    experts_here = 2 * jnp.arange(WIDE, dtype=jnp.int32) + i
-    hit = jnp.sum((routes.T[None, :, :] == experts_here[:, None, None]).astype(f32), axis=1)
-    places = jnp.arange(TOK, dtype=jnp.int32)
-    earlier = (places[:, None] < places[None, :]).astype(bf16)
-    before = jnp.dot(hit.astype(bf16), earlier, preferred_element_type=f32)
-    slot = jnp.arange(CAP, dtype=jnp.int32).astype(f32)
-    chosen = (before[:, None, :] == slot[None, :, None]) & (hit[:, None, :] > 0)
+    attn = lax.all_to_all(attn, N, 0, 0, tiled=True)
+
     choose = pl.pallas_call(
         choose_kernel,
-        out_shape=jax.ShapeDtypeStruct((WIDE * CAP, TOK), bf16),
-        in_specs=[smem(), vmem()],
+        out_shape=jax.ShapeDtypeStruct((EXPERTS * CAP, TOK), bf16),
+        in_specs=[vmem()],
         out_specs=vmem(),
         compiler_params=params(),
         name="choose",
-    )(here, routes.T)
-
-    attn = (attn[0].astype(f32) + sum(p.astype(f32) for p in attn_parts)).astype(bf16)
-    attn, choose = lax.optimization_barrier((attn, choose))
-    attn_par = x_swap(attn)
-    attn_par, gate_par = lax.optimization_barrier((attn_par, gate_par))
+    )(routes.T)
+
     hidden, rows = pl.pallas_call(
         dispatch_kernel,
         out_shape=(
-            jax.ShapeDtypeStruct((TOK, 512), bf16),
-            jax.ShapeDtypeStruct((WIDE, 2 * CAP, 256), bf16),
+            jax.ShapeDtypeStruct((TOK, 256), bf16),
+            jax.ShapeDtypeStruct((EXPERTS, 2 * CAP, 128), bf16),
         ),
-        in_specs=[smem()] + [vmem()] * 4,
+        in_specs=[smem()] + [vmem()] * 3,
         out_specs=(vmem(), vmem()),
         compiler_params=params(),
         name="dispatch",
-    )(here, tokens, attn, attn_par, choose)
-
-    arrived = lax.all_to_all(rows, W, 0, 0, tiled=True)
+    )(here, tokens, attn, choose)
+    arrived = lax.all_to_all(rows, E, 0, 0, tiled=True)
+
     top, bottom = pl.pallas_call(
         unpack_kernel,
         out_shape=(jax.ShapeDtypeStruct((HALF, 512), bf16),) * 2,
@@ -399,15 +426,17 @@
         compiler_params=params(),
         name="unpack",
     )(arrived)
-    top, bottom, up_sent = lax.optimization_barrier((top, bottom, pick(w_up, 1 - i)))
-    up_par = x_swap(up_sent)
+    downs = [cut(w_down, j, 2)] + [y_shift(cut(w_down, j + k, 2), k) for k in (1, 2, 3)]
+    both_sent = jnp.stack([pick(w_gate, 1 - i), pick(w_up, 1 - i)])
+    top, bottom, both_sent, downs = lax.optimization_barrier((top, bottom, both_sent, downs))
+    both_par = x_swap(both_sent)
     top_back, bottom_ahead = y_shift(top, 1), y_shift(bottom, 3)
     bottom_back, top_ahead = y_shift(bottom, 1), y_shift(top, 3)
     top_far, bottom_far = y_shift(top_back, 1), y_shift(bottom_ahead, 3)
     act = pl.pallas_call(
         gate_up_kernel,
         out_shape=jax.ShapeDtypeStruct((2 * HALF, 256), bf16),
-        in_specs=[smem()] + [vmem()] * 8 + [hbm()] * 5,
+        in_specs=[smem()] + [vmem()] * 8 + [hbm()] * 4,
         out_specs=vmem(),
         scratch_shapes=[
             pltpu.VMEM((3, 2048), f32),
@@ -423,67 +452,65 @@
         norm_gains,
         w_gate,
         w_up,
-        gate_par,
-        up_par,
+        both_par,
     )
+    down_sent = jnp.stack([pick(d, 1 - i) for d in downs])
+    act, down_sent = lax.optimization_barrier((act, down_sent))
+    down_par = x_swap(down_sent)
     out = pl.pallas_call(
         down_kernel,
-        out_shape=jax.ShapeDtypeStruct((WIDE, CAP, 512), bf16),
+        out_shape=jax.ShapeDtypeStruct((EXPERTS, 2 * CAP, 128), bf16),
         in_specs=[smem()] + [vmem()] * 4 + [hbm()] * 5,
         out_specs=vmem(),
         scratch_shapes=[pltpu.VMEM((4, 256, 512), bf16), pltpu.SemaphoreType.DMA((2, 4))],
         compiler_params=params(),
         name="down",
     )(here, act, *(y_shift(act, k) for k in (1, 2, 3)), *downs, down_par)
-    back = lax.all_to_all(out, W, 0, 0, tiled=True)
+    back = lax.all_to_all(out, E, 0, 0, tiled=True)
 
     hf = hidden.astype(f32)
-    gain_mine = lax.dynamic_slice_in_dim(norm_gains[1], j * 512, 512, 0)
-    router_mine = lax.dynamic_slice_in_dim(w_router, j * 512, 512, 0)
+    first = j * 512 + i * 256
+    gain_mine = lax.dynamic_slice_in_dim(norm_gains[1], first, 256, 0)
+    router_mine = lax.dynamic_slice_in_dim(w_router, first, 256, 0)
     part = jnp.dot((hf * gain_mine).astype(bf16), router_mine, preferred_element_type=f32)
     square = jnp.sum(hf * hf, axis=1, keepdims=True)
     part = jnp.concatenate([part, jnp.broadcast_to(square, (TOK, EXPERTS))], axis=1)
     whole = part
     for k in (1, 2, 3):
         whole = whole + y_shift(part, k)
-    logits = whole[:, :EXPERTS] * lax.rsqrt(whole[:, EXPERTS : EXPERTS + 1] / 2048.0 + EPS)
-    lifted = jax.nn.sigmoid(logits)
-    onehot = jnp.sum(
-        (routes[:, :, None] == jnp.arange(EXPERTS, dtype=jnp.int32)[None, None, :]).astype(f32),
-        axis=1,
-    )
-    lifted = lifted * onehot
-    gates = lifted / jnp.sum(lifted, axis=1, keepdims=True)
-    gates = lax.dynamic_index_in_dim(gates.reshape(TOK, WIDE, 2), i, 2, keepdims=False).T
-
-    moe = jnp.zeros((TOK, 512), f32)
-    contract = (((0, 1), (0, 1)), ((), ()))
-    mixing = jnp.where(chosen, gates[:, None, :], 0.0)
-    mixing_hi = lax.reduce_precision(mixing, 8, 7)
-    mixing_lo = (mixing - mixing_hi).astype(bf16)
-    for matrix in (mixing_hi.astype(bf16), mixing_lo):
-        moe = moe + lax.dot_general(matrix, back, contract, preferred_element_type=f32)
-    moe = moe.astype(bf16)
-    moe_par = x_swap(moe)
+    whole = whole + x_swap(whole)
+    mixing = pl.pallas_call(
+        mixing_kernel,
+        out_shape=(jax.ShapeDtypeStruct((2 * TOK, EXPERTS * 2 * CAP), bf16),) * 2,
+        in_specs=[vmem()] * 2,
+        out_specs=(vmem(), vmem()),
+        compiler_params=params(),
+        name="mixing",
+    )(whole, routes)
+
     layer, part = pl.pallas_call(
         embed_kernel,
         out_shape=(
-            jax.ShapeDtypeStruct((TOK, 512), bf16),
-            jax.ShapeDtypeStruct((TOK + 8, 128), f32),
+            jax.ShapeDtypeStruct((TOK, 256), bf16),
+            jax.ShapeDtypeStruct((8, TOK + 8, 128), f32),
         ),
-        in_specs=[smem()] + [vmem()] * 5,
+        in_specs=[smem()] + [vmem()] * 6,
         out_specs=(vmem(), vmem()),
+        compiler_params=params(),
         name="embed",
-    )(here, hidden, moe, moe_par, norm_gains, w_proj)
-    parts = [part] + [y_shift(part, k) for k in (1, 2, 3)]
+    )(here, hidden, *mixing, back.reshape(-1, 128), norm_gains, w_proj)
+    parts = lax.all_to_all(part, N, 0, 0, tiled=True)
+    layer_par = x_swap(layer)
+    layer = jnp.where(i == 0, jnp.stack([layer, layer_par]), jnp.stack([layer_par, layer]))
+    layer = jnp.concatenate([layer[0], layer[1]], axis=1)
 
     vectors = pl.pallas_call(
         vector_kernel,
         out_shape=jax.ShapeDtypeStruct((16, TOK, 128), bf16),
-        in_specs=[vmem()] * 4,
+        in_specs=[vmem()],
         out_specs=vmem(),
         name="vectors",
-    )(*parts)
+    )(parts)
     vectors, layer = lax.optimization_barrier((vectors, layer))
     layers = [layer] + [y_shift(layer, k) for k in (1, 2, 3)]
     own = lax.all_to_all(vectors, ("z", "xl"), 0, 0, tiled=True).reshape(16 * TOK, 128)

time: 188 us -> 194 us (1.032)
  starting transfers between devices: 68.3 us -> 73.5 us
  waiting for transfers between devices: 76.4 us -> 78.8 us
    all_to_all x2 -> x4, starting transfers between devices: 19.2 us -> 35.3 us  [the longest x1 12.6 us: body(): arrived = lax.all_to_all(rows, E, 0, 0, tiled=True)]
    ppermute x24 -> x18, starting transfers between devices: 30.7 us -> 20 us  [y_shift(): return lax.ppermute(x, 'y', [(s, (s + k) % 4) for s in range(4)])]
    all_to_all x2 -> x4, waiting for transfers between devices: 26.7 us -> 34.9 us  [the longest x1 13.8 us: body(): arrived = lax.all_to_all(rows, E, 0, 0, tiled=True)]
    ppermute x5 -> x4, waiting for transfers between devices: 8.92 us -> 2.02 us  [x_swap(): return lax.ppermute(x, 'xh', [(0, 1), (1, 0)])]
    unnamed x47 -> x48, local copies, waits for them, and re-layouts: 3.3 us -> 6.01 us
    dynamic_slice x4, local copies, waits for them, and re-layouts: 4.41 us -> 1.99 us  [pick(): return lax.dynamic_index_in_dim(array, which, 0, keepdims=False)]
    squeeze x2 -> x1, local copies, waits for them, and re-layouts: 2.01 us -> 0.01 us  [body(): layer = jnp.concatenate([layer[0], layer[1]], axis=1)]
    ppermute x24 -> x18, waiting for transfers between devices: 34.6 us -> 36.5 us  [y_shift(): return lax.ppermute(x, 'y', [(s, (s + k) % 4) for s in range(4)])]
  transfers between devices with their start and end apart: 33 -> 28, of which waited for: 20 -> 17; matrix products, arithmetic and copies ran while one was open for 6% -> 5% of each run, Pallas kernels for 6% -> 2%
where the time goes in v8:
time: 194 us; the launch traced here: 193 us
  waiting for transfers between devices  78.8 us (41%)
  starting transfers between devices  73.5 us (38%)
  Pallas kernels  24.9 us (13%)
  local copies, waits for them, and re-layouts  11.3 us (6%)
  other arithmetic  3.35 us (2%)
    ppermute x18, waiting for transfers between devices, y_shift(): return lax.ppermute(x, 'y', [(s, (s + k) % 4) for s in range(4)])  36.5 us
    ppermute x18, starting transfers between devices, y_shift(): return lax.ppermute(x, 'y', [(s, (s + k) % 4) for s in range(4)])  20 us
    all_to_all x1, waiting for transfers between devices, body(): arrived = lax.all_to_all(rows, E, 0, 0, tiled=True)  13.8 us
    all_to_all x1, starting transfers between devices, body(): arrived = lax.all_to_all(rows, E, 0, 0, tiled=True)  12.6 us
    all_to_all x1, starting transfers between devices, body(): back = lax.all_to_all(out, E, 0, 0, tiled=True)  11.1 us
    all_to_all x1, waiting for transfers between devices, body(): attn = lax.all_to_all(attn, N, 0, 0, tiled=True)  8.55 us
    ppermute x4, starting transfers between devices, x_swap(): return lax.ppermute(x, 'xh', [(0, 1), (1, 0)])  8.23 us
    all_to_all x1, waiting for transfers between devices, body(): parts = lax.all_to_all(part, N, 0, 0, tiled=True)  7.92 us
  transfers between devices with their start and end apart: 28, of which 17 were waited for; matrix products, arithmetic and copies ran while one was open for 5% of the time, Pallas kernels for 2%

profile of v8, /device:TPU:1, one launch (start us, length us, event | category | flops | bytes accessed | tf_op | source)
XLA Modules:
  0.0 193.1 jit_solution(8997675086125244677)
XLA Ops:
  1.2 5.3 %attention.1 = bf16[8,128,256]{2,1,0:T(8,128)(2,1)} custom-call(s32[4]{0:T(128)} %pad_add_fusion.here_ref, s32[3,32]{1,0:T(4,128)} %bitcast.28, f32[2,256]{1,0:T(2,128)} %qk_ref.1, f32[3,2048]{1,0:T(4,128)} %gain_ref.3, bf16[128,2048]{1,0:T(8,128)(2,1)} %x_ref.1, bf16[3,2048,256]{2,1,0:T(8,128)(2,1)} %bitcast.24, bf16[256,2048]{1,0:T(8,128)(2,1)} %out_hbm.1), custom_call_target="tpu_custom_call" | custom-call | tf_op jit(solution)/shard_map/attention/pallas_call | solution.py:374
  6.5 7.6 %all-to-all-start = ((bf16[8,128,256]{2,1,0:T(8,128)(2,1)}), bf16[8,128,256]{2,1,0:T(8,128)(2,1)S(1)}, u32[]{:S(2)}, u32[]{:S(2)}) async-start(bf16[8,128,256]{2,1,0:T(8,128)(2,1)} %attention.1), calls=%async_computation | async-start | bytes 1048576 | tf_op jit(solution)/shard_map/all_to_all | solution.py:396
  14.6 8.6 %all-to-all-done.parts_ref = bf16[8,128,256]{2,1,0:T(8,128)(2,1)S(1)} async-done(((bf16[8,128,256]{2,1,0:T(8,128)(2,1)}), bf16[8,128,256]{2,1,0:T(8,128)(2,1)S(1)}, u32[]{:S(2)}, u32[]{:S(2)}) %all-to-all-start) | async-done | bytes 524320 | tf_op jit(solution)/shard_map/all_to_all | solution.py:396
  23.1 1.8 dispatch.1
  24.9 12.6 %all-to-all-start.1 = ((bf16[64,40,128]{2,1,0:T(8,128)(2,1)}), bf16[64,40,128]{2,1,0:T(8,128)(2,1)S(1)}, u32[]{:S(2)}, u32[]{:S(2)}) async-start(bf16[64,40,128]{2,1,0:T(8,128)(2,1)} %get-tuple-element.30), calls=%async_computation.1 | async-start | bytes 1310720 | tf_op jit(solution)/shard_map/all_to_all | solution.py:418
  37.5 2.2 %constant_dynamic-slice_fusion.4 = (bf16[2,128,512]{2,1,0:T(8,128)(2,1)}, bf16[2,128,512]{2,1,0:T(8,128)(2,1)}, bf16[2,128,512]{2,1,0:T(8,128)(2,1)S(1)}, bf16[2,128,512]{2,1,0:T(8,128)(2,1)}) fusion(bf16[2,128,2048]{2,1,0:T(8,128)(2,1)} %param.25, s32[]{:T(128)S(6)} %select_n.61, s32[]{:T(128)S(6)} %select_n.59, s32[]{:T(128)S(6)} %select_n.58, s32[]{:T(128)S(6)} %select_n.60), kind=kLoop, calls=%fused_computation.26 | loop fusion | bytes 2097168 | tf_op jit(solution)/shard_map/dynamic_slice | solution.py:372
  40.3 1.8 collective-permute-start.5
  42.8 1.1 pad_maximum_fusion
  43.9 13.8 %all-to-all-done.1.in_ref = bf16[64,40,128]{2,1,0:T(8,128)(2,1)S(1)} async-done(((bf16[64,40,128]{2,1,0:T(8,128)(2,1)}), bf16[64,40,128]{2,1,0:T(8,128)(2,1)S(1)}, u32[]{:S(2)}, u32[]{:S(2)}) %all-to-all-start.1) | async-done | bytes 655392 | tf_op jit(solution)/shard_map/all_to_all | solution.py:418
  57.9 2.0 %collective-permute-start.13 = (bf16[2,2048,128]{2,1,0:T(8,128)(2,1)}, bf16[2,2048,128]{2,1,0:T(8,128)(2,1)S(1)}, u32[]{:S(2)}, u32[]{:S(2)}) collective-permute-start(bf16[2,2048,128]{2,1,0:T(8,128)(2,1)} %pad_maximum_fusion), channel_id=1, source_target_pairs={{0,4},{4,0},{1,5},{5,1},{2,6},{6,2},{3,7},{7,3},{8,12},{12,8},{9,1... | collective-permute-start | bytes 3145736 | tf_op jit(solution)/shard_map/ppermute | solution.py:32
  60.0 1.2 collective-permute-start.11
  62.0 2.1 %collective-permute-start.8 = (bf16[320,512]{1,0:T(8,128)(2,1)S(1)}, bf16[320,512]{1,0:T(8,128)(2,1)S(1)}, u32[]{:S(2)}, u32[]{:S(2)}) collective-permute-start(bf16[320,512]{1,0:T(8,128)(2,1)S(1)} %get-tuple-element.33.refs_0_), channel_id=1, source_target_pairs={{0,3},{1,0},{2,1},{3,2},{4,7},{5,4},{6,5},{7,6},{8,11},{9,8},{10,9... | collective-permute-start | bytes 983048 | tf_op jit(solution)/shard_map/ppermute | solution.py:28
  64.1 3.4 %collective-permute-done.11.refs_6_ = bf16[320,512]{1,0:T(8,128)(2,1)S(1)} collective-permute-done((bf16[320,512]{1,0:T(8,128)(2,1)S(1)}, bf16[320,512]{1,0:T(8,128)(2,1)S(1)}, u32[]{:S(2)}, u32[]{:S(2)}) %collective-permute-start.11) | collective-permute-done | bytes 327712 | tf_op jit(solution)/shard_map/ppermute | solution.py:28
  67.5 2.4 %collective-permute-start.12 = (bf16[320,512]{1,0:T(8,128)(2,1)S(1)}, bf16[320,512]{1,0:T(8,128)(2,1)S(1)}, u32[]{:S(2)}, u32[]{:S(2)}) collective-permute-start(bf16[320,512]{1,0:T(8,128)(2,1)S(1)} %collective-permute-done.11.refs_6_), channel_id=1, source_target_pairs={{0,3},{1,0},{2,1},{3,2},{4,7},{5,4},{6,5},{7,6},{8,11},{9,8},{10,9... | collective-permute-start | bytes 983048 | tf_op jit(solution)/shard_map/ppermute | solution.py:28
  70.8 1.0 constant_dynamic-slice_fusion
  71.9 4.7 %collective-permute-done.10.refs_5_ = bf16[320,512]{1,0:T(8,128)(2,1)S(1)} collective-permute-done((bf16[320,512]{1,0:T(8,128)(2,1)S(1)}, bf16[320,512]{1,0:T(8,128)(2,1)S(1)}, u32[]{:S(2)}, u32[]{:S(2)}) %collective-permute-start.10) | collective-permute-done | bytes 327712 | tf_op jit(solution)/shard_map/ppermute | solution.py:28
  76.6 4.9 %collective-permute-done.12.refs_7_ = bf16[320,512]{1,0:T(8,128)(2,1)S(1)} collective-permute-done((bf16[320,512]{1,0:T(8,128)(2,1)S(1)}, bf16[320,512]{1,0:T(8,128)(2,1)S(1)}, u32[]{:S(2)}, u32[]{:S(2)}) %collective-permute-start.12) | collective-permute-done | bytes 327712 | tf_op jit(solution)/shard_map/ppermute | solution.py:28
  81.5 2.1 %collective-permute-done.9.refs_3_ = bf16[320,512]{1,0:T(8,128)(2,1)S(1)} collective-permute-done((bf16[320,512]{1,0:T(8,128)(2,1)S(1)}, bf16[320,512]{1,0:T(8,128)(2,1)S(1)}, u32[]{:S(2)}, u32[]{:S(2)}) %collective-permute-start.9) | collective-permute-done | bytes 327712 | tf_op jit(solution)/shard_map/ppermute | solution.py:28
  83.6 3.0 %gate_up.1.a0 = bf16[640,256]{1,0:T(8,128)(2,1)S(1)} custom-call(s32[4]{0:T(128)S(1)} %copy-done.11, bf16[320,512]{1,0:T(8,128)(2,1)S(1)} %get-tuple-element.33.refs_0_, bf16[320,512]{1,0:T(8,128)(2,1)S(1)} %collective-permute-done.7.refs_1_, bf16[320,512]{1,0:T(8,128)(2,1)S(1)} %collective-permute-done.8.refs_2_, ...), custom_call_target="tpu_custom_call" | custom-call | tf_op jit(solution)/shard_map/gate_up/pallas_call | solution.py:436
  86.6 1.4 collective-permute-start.17
  88.6 1.8 collective-permute-start.15
  91.0 4.5 %collective-permute-done.14.a1 = bf16[640,256]{1,0:T(8,128)(2,1)S(1)} collective-permute-done((bf16[640,256]{1,0:T(8,128)(2,1)S(1)}, bf16[640,256]{1,0:T(8,128)(2,1)S(1)}, u32[]{:S(2)}, u32[]{:S(2)}) %collective-permute-start.14) | collective-permute-done | bytes 327712 | tf_op jit(solution)/shard_map/ppermute | solution.py:28
  95.5 7.0 %collective-permute-done.15.a2 = bf16[640,256]{1,0:T(8,128)(2,1)S(1)} collective-permute-done((bf16[640,256]{1,0:T(8,128)(2,1)S(1)}, bf16[640,256]{1,0:T(8,128)(2,1)S(1)}, u32[]{:S(2)}, u32[]{:S(2)}) %collective-permute-start.15) | collective-permute-done | bytes 327712 | tf_op jit(solution)/shard_map/ppermute | solution.py:28
  102.5 2.9 %collective-permute-done.16.a3 = bf16[640,256]{1,0:T(8,128)(2,1)S(1)} collective-permute-done((bf16[640,256]{1,0:T(8,128)(2,1)S(1)}, bf16[640,256]{1,0:T(8,128)(2,1)S(1)}, u32[]{:S(2)}, u32[]{:S(2)}) %collective-permute-start.16) | collective-permute-done | bytes 327712 | tf_op jit(solution)/shard_map/ppermute | solution.py:28
  105.4 3.6 %down.1 = bf16[64,40,128]{2,1,0:T(8,128)(2,1)} custom-call(s32[4]{0:T(128)S(1)} %copy-done.11, bf16[640,256]{1,0:T(8,128)(2,1)S(1)} %gate_up.1.a0, bf16[640,256]{1,0:T(8,128)(2,1)S(1)} %collective-permute-done.14.a1, bf16[640,256]{1,0:T(8,128)(2,1)S(1)} %collective-permute-done.15.a2, bf16[640,256]{1,0:T(8,128)(2,1)S(1)} %collective-permute-done.16.a3, ...), custom_call_target="tpu_custom_call" | custom-call | tf_op jit(solution)/shard_map/down/pallas_call | solution.py:460
  109.0 11.1 %all-to-all-start.2 = ((bf16[64,40,128]{2,1,0:T(8,128)(2,1)}), bf16[64,40,128]{2,1,0:T(8,128)(2,1)S(1)}, u32[]{:S(2)}, u32[]{:S(2)}) async-start(bf16[64,40,128]{2,1,0:T(8,128)(2,1)} %down.1), calls=%async_computation.2 | async-start | bytes 1310720 | tf_op jit(solution)/shard_map/all_to_all | solution.py:469
  120.7 3.2 %collective-permute-start.1 = (f32[128,128]{1,0:T(8,128)S(1)}, f32[128,128]{1,0:T(8,128)S(1)}, u32[]{:S(2)}, u32[]{:S(2)}) collective-permute-start(f32[128,128]{1,0:T(8,128)S(1)} %pad_maximum_fusion.3), channel_id=1, source_target_pairs={{0,2},{1,3},{2,0},{3,1},{4,6},{5,7},{6,4},{7,5},{8,10},{9,11},{10,... | collective-permute-start | bytes 196616 | tf_op jit(solution)/shard_map/ppermute | solution.py:28
  123.9 1.4 collective-permute-done
  125.3 1.8 collective-permute-done.1
  127.9 2.9 %collective-permute-start.3 = (f32[128,128]{1,0:T(8,128)S(1)}, f32[128,128]{1,0:T(8,128)S(1)}, u32[]{:S(2)}, u32[]{:S(2)}) collective-permute-start(f32[128,128]{1,0:T(8,128)S(1)} %add_add_fusion), channel_id=1, source_target_pairs={{0,4},{4,0},{1,5},{5,1},{2,6},{6,2},{3,7},{7,3},{8,12},{12,8},{9,1... | collective-permute-start | bytes 196616 | tf_op jit(solution)/shard_map/ppermute | solution.py:32
  131.5 2.0 %collective-permute-done.3 = f32[128,128]{1,0:T(8,128)S(1)} collective-permute-done((f32[128,128]{1,0:T(8,128)S(1)}, f32[128,128]{1,0:T(8,128)S(1)}, u32[]{:S(2)}, u32[]{:S(2)}) %collective-permute-start.3) | collective-permute-done | bytes 65568 | tf_op jit(solution)/shard_map/ppermute | solution.py:32
  134.4 1.5 mixing.1
  135.8 4.6 %all-to-all-done.2 = bf16[64,40,128]{2,1,0:T(8,128)(2,1)S(1)} async-done(((bf16[64,40,128]{2,1,0:T(8,128)(2,1)}), bf16[64,40,128]{2,1,0:T(8,128)(2,1)S(1)}, u32[]{:S(2)}, u32[]{:S(2)}) %all-to-all-start.2) | async-done | bytes 655392 | tf_op jit(solution)/shard_map/all_to_all | solution.py:469
  141.2 1.0 copy-done.7
  143.0 2.0 %embed.1 = (bf16[128,256]{1,0:T(8,128)(2,1)}, f32[8,136,128]{2,1,0:T(8,128)S(1)}) custom-call(s32[4]{0:T(128)S(1)} %copy-done.11, bf16[128,256]{1,0:T(8,128)(2,1)S(1)} %copy-done.5, bf16[256,2560]{1,0:T(8,128)(2,1)S(1)} %get-tuple-element.28.high_ref, bf16[256,2560]{1,0:T(8,128)(2,1)S(1)} %get-tuple-element.29.low_ref, bf16[2560,128]{1,0:T(8,128)(2,1)S(1)} %bitcast.22, ...), custom_call_target="tpu_custom_call" | custom-call | tf_op jit(solution)/shard_map/embed/pallas_call | solution.py:491
  145.1 1.9 %collective-permute-start.18 = (bf16[128,256]{1,0:T(8,128)(2,1)}, bf16[128,256]{1,0:T(8,128)(2,1)S(1)}, u32[]{:S(2)}, u32[]{:S(2)}) collective-permute-start(bf16[128,256]{1,0:T(8,128)(2,1)} %get-tuple-element.43), channel_id=1, source_target_pairs={{0,4},{4,0},{1,5},{5,1},{2,6},{6,2},{3,7},{7,3},{8,12},{12,8},{9,1... | collective-permute-start | bytes 196616 | tf_op jit(solution)/shard_map/ppermute | solution.py:32
  147.0 4.1 %all-to-all-start.3 = ((f32[8,136,128]{2,1,0:T(8,128)}), f32[8,136,128]{2,1,0:T(8,128)S(1)}, u32[]{:S(2)}, u32[]{:S(2)}) async-start(f32[8,136,128]{2,1,0:T(8,128)} %copy-done.6), calls=%async_computation.3 | async-start | bytes 1114112 | tf_op jit(solution)/shard_map/all_to_all | solution.py:502
  151.1 0.9 maximum_select_fusion
  152.1 7.9 %all-to-all-done.3.parts_ref = f32[8,136,128]{2,1,0:T(8,128)S(1)} async-done(((f32[8,136,128]{2,1,0:T(8,128)}), f32[8,136,128]{2,1,0:T(8,128)S(1)}, u32[]{:S(2)}, u32[]{:S(2)}) %all-to-all-start.3) | async-done | bytes 557088 | tf_op jit(solution)/shard_map/all_to_all | solution.py:502
  160.9 2.1 %vectors.1 = bf16[16,128,128]{2,1,0:T(8,128)(2,1)} custom-call(f32[8,136,128]{2,1,0:T(8,128)} %copy-done.13), custom_call_target="tpu_custom_call" | custom-call | tf_op jit(solution)/shard_map/vectors/pallas_call | solution.py:507
  162.9 5.6 %all-to-all-start.4 = ((bf16[16,128,128]{2,1,0:T(8,128)(2,1)}), bf16[16,128,128]{2,1,0:T(8,128)(2,1)S(1)}, u32[]{:S(2)}, u32[]{:S(2)}) async-start(bf16[16,128,128]{2,1,0:T(8,128)(2,1)} %vectors.1), calls=%async_computation.4 | async-start | bytes 1048576 | tf_op jit(solution)/shard_map/all_to_all | solution.py:516
  169.6 2.4 %collective-permute-start.20 = (bf16[128,512]{1,0:T(8,128)(2,1)S(1)}, bf16[128,512]{1,0:T(8,128)(2,1)S(1)}, u32[]{:S(2)}, u32[]{:S(2)}) collective-permute-start(bf16[128,512]{1,0:T(8,128)(2,1)S(1)} %pad_maximum_fusion.2.p0), channel_id=1, source_target_pairs={{0,2},{1,3},{2,0},{3,1},{4,6},{5,7},{6,4},{7,5},{8,10},{9,11},{10,... | collective-permute-start | bytes 393224 | tf_op jit(solution)/shard_map/ppermute | solution.py:28
  172.0 1.2 collective-permute-start.21
  174.1 3.0 %collective-permute-done.20.p2 = bf16[128,512]{1,0:T(8,128)(2,1)S(1)} collective-permute-done((bf16[128,512]{1,0:T(8,128)(2,1)S(1)}, bf16[128,512]{1,0:T(8,128)(2,1)S(1)}, u32[]{:S(2)}, u32[]{:S(2)}) %collective-permute-start.20) | collective-permute-done | bytes 131104 | tf_op jit(solution)/shard_map/ppermute | solution.py:28
  177.1 5.4 %all-to-all-done.4 = bf16[16,128,128]{2,1,0:T(8,128)(2,1)S(1)} async-done(((bf16[16,128,128]{2,1,0:T(8,128)(2,1)}), bf16[16,128,128]{2,1,0:T(8,128)(2,1)S(1)}, u32[]{:S(2)}, u32[]{:S(2)}) %all-to-all-start.4) | async-done | bytes 524320 | tf_op jit(solution)/shard_map/all_to_all | solution.py:516
  182.5 4.4 %collective-permute-start.22 = (bf16[2048,128]{1,0:T(8,128)(2,1)S(1)}, bf16[2048,128]{1,0:T(8,128)(2,1)S(1)}, u32[]{:S(2)}, u32[]{:S(2)}) collective-permute-start(bf16[2048,128]{1,0:T(8,128)(2,1)S(1)} %bitcast.25), channel_id=1, source_target_pairs={{0,8},{8,0},{1,9},{9,1},{2,10},{10,2},{3,11},{11,3},{4,12},{12,4},... | collective-permute-start | bytes 1572872 | tf_op jit(solution)/shard_map/ppermute | solution.py:530
  186.9 1.9 %assemble.1 = bf16[128,2048]{1,0:T(8,128)(2,1)} custom-call(s32[4]{0:T(128)} %pad_add_fusion.here_ref, bf16[128,512]{1,0:T(8,128)(2,1)} %copy-done.16, bf16[128,512]{1,0:T(8,128)(2,1)} %copy-done.17, bf16[128,512]{1,0:T(8,128)(2,1)} %copy-done.18, bf16[128,512]{1,0:T(8,128)(2,1)} %copy-done.19), custom_call_target="tpu_custom_call" | custom-call | tf_op jit(solution)/shard_map/assemble/pallas_call | solution.py:531
  189.7 3.2 %score.1 = f32[1,16]{1,0:T(1,128)} custom-call(s32[5,16]{1,0:T(8,128)} %stack.72.info_ref, bf16[1024,128]{1,0:T(8,128)(2,1)} %doc_ref.1, bf16[2048,128]{1,0:T(8,128)(2,1)} %bitcast.26, bf16[2048,128]{1,0:T(8,128)(2,1)} %copy-done.15), custom_call_target="tpu_custom_call" | custom-call | tf_op jit(solution)/shard_map/score/pallas_call | solution.py:538
  (96 shorter events, 13.7 us)
Async XLA Ops:
  0.6 119.6 %copy-start = (bf16[2048,64]{0,1:T(8,128)(2,1)S(1)}, bf16[2048,64]{0,1:T(8,128)(2,1)}, u32[]{:S(2)}) copy-start(bf16[2048,64]{0,1:T(8,128)(2,1)} %param.21) | copy-start | bytes 786436
  1.2 12.9 %copy-start.12 = (s32[128,8]{0,1:T(8,128)S(1)}, s32[128,8]{0,1:T(8,128)}, u32[]{:S(2)}) copy-start(s32[128,8]{0,1:T(8,128)} %param.22) | copy-start | bytes 12292
  6.5 16.6 %copy-start.3 = (bf16[128,2048]{1,0:T(8,128)(2,1)S(1)}, bf16[128,2048]{1,0:T(8,128)(2,1)}, u32[]{:S(2)}) copy-start(bf16[128,2048]{1,0:T(8,128)(2,1)} %x_ref.1) | copy-start | bytes 1572868
  6.5 16.6 %copy-start.11 = (s32[4]{0:T(128)S(1)}, s32[4]{0:T(128)}, u32[]{:S(2)}) copy-start(s32[4]{0:T(128)} %pad_add_fusion.here_ref) | copy-start | bytes 52
  6.5 16.6 %all-to-all-start = ((bf16[8,128,256]{2,1,0:T(8,128)(2,1)}), bf16[8,128,256]{2,1,0:T(8,128)(2,1)S(1)}, u32[]{:S(2)}, u32[]{:S(2)}) async-start(bf16[8,128,256]{2,1,0:T(8,128)(2,1)} %attention.1), calls=%async_computation | async-start | bytes 1048576 | tf_op jit(solution)/shard_map/all_to_all | solution.py:396
  24.9 95.4 %copy-start.4 = (bf16[128,256]{1,0:T(8,128)(2,1)}, bf16[128,256]{1,0:T(8,128)(2,1)S(1)}, u32[]{:S(2)}) copy-start(bf16[128,256]{1,0:T(8,128)(2,1)S(1)} %get-tuple-element.27.hidden_ref) | copy-start | bytes 196612
  24.9 32.9 %all-to-all-start.1 = ((bf16[64,40,128]{2,1,0:T(8,128)(2,1)}), bf16[64,40,128]{2,1,0:T(8,128)(2,1)S(1)}, u32[]{:S(2)}, u32[]{:S(2)}) async-start(bf16[64,40,128]{2,1,0:T(8,128)(2,1)} %get-tuple-element.30), calls=%async_computation.1 | async-start | bytes 1310720 | tf_op jit(solution)/shard_map/all_to_all | solution.py:418
  37.5 5.3 %copy-start.2 = (bf16[2,2048,128]{2,1,0:T(8,128)(2,1)S(1)}, bf16[2,2048,128]{2,1,0:T(8,128)(2,1)}, u32[]{:S(2)}) copy-start(bf16[2,2048,128]{2,1,0:T(8,128)(2,1)} %refs_10_.1) | copy-start | bytes 3145732
  37.5 5.3 %copy-start.1 = (bf16[2,2048,128]{2,1,0:T(8,128)(2,1)S(1)}, bf16[2,2048,128]{2,1,0:T(8,128)(2,1)}, u32[]{:S(2)}) copy-start(bf16[2,2048,128]{2,1,0:T(8,128)(2,1)} %refs_9_.1) | copy-start | bytes 3145732
  39.8 18.1 %collective-permute-start.4 = (bf16[2,128,512]{2,1,0:T(8,128)(2,1)}, bf16[2,128,512]{2,1,0:T(8,128)(2,1)}, u32[]{:S(2)}, u32[]{:S(2)}) collective-permute-start(bf16[2,128,512]{2,1,0:T(8,128)(2,1)} %get-tuple-element.57), channel_id=1, source_target_pairs={{0,1},{1,2},{2,3},{3,0},{4,5},{5,6},{6,7},{7,4},{8,9},{9,10},{10,1... | collective-permute-start | bytes 786440 | tf_op jit(solution)/shard_map/ppermute | solution.py:28
  40.3 17.6 %collective-permute-start.5 = (bf16[2,128,512]{2,1,0:T(8,128)(2,1)}, bf16[2,128,512]{2,1,0:T(8,128)(2,1)}, u32[]{:S(2)}, u32[]{:S(2)}) collective-permute-start(bf16[2,128,512]{2,1,0:T(8,128)(2,1)} %get-tuple-element.59), channel_id=1, source_target_pairs={{0,2},{1,3},{2,0},{3,1},{4,6},{5,7},{6,4},{7,5},{8,10},{9,11},{10,... | collective-permute-start | bytes 786440 | tf_op jit(solution)/shard_map/ppermute | solution.py:28
  42.1 15.8 %collective-permute-start.6 = (bf16[2,128,512]{2,1,0:T(8,128)(2,1)}, bf16[2,128,512]{2,1,0:T(8,128)(2,1)}, u32[]{:S(2)}, u32[]{:S(2)}) collective-permute-start(bf16[2,128,512]{2,1,0:T(8,128)(2,1)} %get-tuple-element.56), channel_id=1, source_target_pairs={{0,3},{1,0},{2,1},{3,2},{4,7},{5,4},{6,5},{7,6},{8,11},{9,8},{10,9... | collective-permute-start | bytes 786440 | tf_op jit(solution)/shard_map/ppermute | solution.py:28
  43.9 39.7 %copy-start.8 = (f32[3,2048]{1,0:T(4,128)S(1)}, f32[3,2048]{1,0:T(4,128)}, u32[]{:S(2)}) copy-start(f32[3,2048]{1,0:T(4,128)} %gain_ref.3) | copy-start | bytes 73732
  57.9 25.7 %collective-permute-start.13 = (bf16[2,2048,128]{2,1,0:T(8,128)(2,1)}, bf16[2,2048,128]{2,1,0:T(8,128)(2,1)S(1)}, u32[]{:S(2)}, u32[]{:S(2)}) collective-permute-start(bf16[2,2048,128]{2,1,0:T(8,128)(2,1)} %pad_maximum_fusion), channel_id=1, source_target_pairs={{0,4},{4,0},{1,5},{5,1},{2,6},{6,2},{3,7},{7,3},{8,12},{12,8},{9,1... | collective-permute-start | bytes 3145736 | tf_op jit(solution)/shard_map/ppermute | solution.py:32
  60.0 7.5 %collective-permute-start.11 = (bf16[320,512]{1,0:T(8,128)(2,1)S(1)}, bf16[320,512]{1,0:T(8,128)(2,1)S(1)}, u32[]{:S(2)}, u32[]{:S(2)}) collective-permute-start(bf16[320,512]{1,0:T(8,128)(2,1)S(1)} %get-tuple-element.34.refs_4_), channel_id=1, source_target_pairs={{0,3},{1,0},{2,1},{3,2},{4,7},{5,4},{6,5},{7,6},{8,11},{9,8},{10,9... | collective-permute-start | bytes 983048 | tf_op jit(solution)/shard_map/ppermute | solution.py:28
  61.1 8.8 %collective-permute-start.7 = (bf16[320,512]{1,0:T(8,128)(2,1)S(1)}, bf16[320,512]{1,0:T(8,128)(2,1)S(1)}, u32[]{:S(2)}, u32[]{:S(2)}) collective-permute-start(bf16[320,512]{1,0:T(8,128)(2,1)S(1)} %get-tuple-element.33.refs_0_), channel_id=1, source_target_pairs={{0,1},{1,2},{2,3},{3,0},{4,5},{5,6},{6,7},{7,4},{8,9},{9,10},{10,1... | collective-permute-start | bytes 983048 | tf_op jit(solution)/shard_map/ppermute | solution.py:28
  61.4 15.2 %collective-permute-start.10 = (bf16[320,512]{1,0:T(8,128)(2,1)S(1)}, bf16[320,512]{1,0:T(8,128)(2,1)S(1)}, u32[]{:S(2)}, u32[]{:S(2)}) collective-permute-start(bf16[320,512]{1,0:T(8,128)(2,1)S(1)} %get-tuple-element.34.refs_4_), channel_id=1, source_target_pairs={{0,1},{1,2},{2,3},{3,0},{4,5},{5,6},{6,7},{7,4},{8,9},{9,10},{10,1... | collective-permute-start | bytes 983048 | tf_op jit(solution)/shard_map/ppermute | solution.py:28
  62.0 14.6 %collective-permute-start.8 = (bf16[320,512]{1,0:T(8,128)(2,1)S(1)}, bf16[320,512]{1,0:T(8,128)(2,1)S(1)}, u32[]{:S(2)}, u32[]{:S(2)}) collective-permute-start(bf16[320,512]{1,0:T(8,128)(2,1)S(1)} %get-tuple-element.33.refs_0_), channel_id=1, source_target_pairs={{0,3},{1,0},{2,1},{3,2},{4,7},{5,4},{6,5},{7,6},{8,11},{9,8},{10,9... | collective-permute-start | bytes 983048 | tf_op jit(solution)/shard_map/ppermute | solution.py:28
  67.5 14.0 %collective-permute-start.12 = (bf16[320,512]{1,0:T(8,128)(2,1)S(1)}, bf16[320,512]{1,0:T(8,128)(2,1)S(1)}, u32[]{:S(2)}, u32[]{:S(2)}) collective-permute-start(bf16[320,512]{1,0:T(8,128)(2,1)S(1)} %collective-permute-done.11.refs_6_), channel_id=1, source_target_pairs={{0,3},{1,0},{2,1},{3,2},{4,7},{5,4},{6,5},{7,6},{8,11},{9,8},{10,9... | collective-permute-start | bytes 983048 | tf_op jit(solution)/shard_map/ppermute | solution.py:28
  69.9 13.8 %collective-permute-start.9 = (bf16[320,512]{1,0:T(8,128)(2,1)S(1)}, bf16[320,512]{1,0:T(8,128)(2,1)S(1)}, u32[]{:S(2)}, u32[]{:S(2)}) collective-permute-start(bf16[320,512]{1,0:T(8,128)(2,1)S(1)} %collective-permute-done.7.refs_1_), channel_id=1, source_target_pairs={{0,1},{1,2},{2,3},{3,0},{4,5},{5,6},{6,7},{7,4},{8,9},{9,10},{10,1... | collective-permute-start | bytes 983048 | tf_op jit(solution)/shard_map/ppermute | solution.py:28
  86.6 18.8 %collective-permute-start.17 = (bf16[4,128,512]{2,1,0:T(8,128)(2,1)S(1)}, bf16[4,128,512]{2,1,0:T(8,128)(2,1)S(1)}, u32[]{:S(2)}, u32[]{:S(2)}) collective-permute-start(bf16[4,128,512]{2,1,0:T(8,128)(2,1)S(1)} %pad_maximum_fusion.1), channel_id=1, source_target_pairs={{0,4},{4,0},{1,5},{5,1},{2,6},{6,2},{3,7},{7,3},{8,12},{12,8},{9,1... | collective-permute-start | bytes 1572872 | tf_op jit(solution)/shard_map/ppermute | solution.py:32
  88.0 7.5 %collective-permute-start.14 = (bf16[640,256]{1,0:T(8,128)(2,1)S(1)}, bf16[640,256]{1,0:T(8,128)(2,1)S(1)}, u32[]{:S(2)}, u32[]{:S(2)}) collective-permute-start(bf16[640,256]{1,0:T(8,128)(2,1)S(1)} %gate_up.1.a0), channel_id=1, source_target_pairs={{0,1},{1,2},{2,3},{3,0},{4,5},{5,6},{6,7},{7,4},{8,9},{9,10},{10,1... | collective-permute-start | bytes 983048 | tf_op jit(solution)/shard_map/ppermute | solution.py:28
  88.6 14.0 %collective-permute-start.15 = (bf16[640,256]{1,0:T(8,128)(2,1)S(1)}, bf16[640,256]{1,0:T(8,128)(2,1)S(1)}, u32[]{:S(2)}, u32[]{:S(2)}) collective-permute-start(bf16[640,256]{1,0:T(8,128)(2,1)S(1)} %gate_up.1.a0), channel_id=1, source_target_pairs={{0,2},{1,3},{2,0},{3,1},{4,6},{5,7},{6,4},{7,5},{8,10},{9,11},{10,... | collective-permute-start | bytes 983048 | tf_op jit(solution)/shard_map/ppermute | solution.py:28
  90.4 15.1 %collective-permute-start.16 = (bf16[640,256]{1,0:T(8,128)(2,1)S(1)}, bf16[640,256]{1,0:T(8,128)(2,1)S(1)}, u32[]{:S(2)}, u32[]{:S(2)}) collective-permute-start(bf16[640,256]{1,0:T(8,128)(2,1)S(1)} %gate_up.1.a0), channel_id=1, source_target_pairs={{0,3},{1,0},{2,1},{3,2},{4,7},{5,4},{6,5},{7,6},{8,11},{9,8},{10,9... | collective-permute-start | bytes 983048 | tf_op jit(solution)/shard_map/ppermute | solution.py:28
  109.0 31.3 %all-to-all-start.2 = ((bf16[64,40,128]{2,1,0:T(8,128)(2,1)}), bf16[64,40,128]{2,1,0:T(8,128)(2,1)S(1)}, u32[]{:S(2)}, u32[]{:S(2)}) async-start(bf16[64,40,128]{2,1,0:T(8,128)(2,1)} %down.1), calls=%async_computation.2 | async-start | bytes 1310720 | tf_op jit(solution)/shard_map/all_to_all | solution.py:469
  120.6 4.7 %collective-permute-start = (f32[128,128]{1,0:T(8,128)S(1)}, f32[128,128]{1,0:T(8,128)S(1)}, u32[]{:S(2)}, u32[]{:S(2)}) collective-permute-start(f32[128,128]{1,0:T(8,128)S(1)} %pad_maximum_fusion.3), channel_id=1, source_target_pairs={{0,1},{1,2},{2,3},{3,0},{4,5},{5,6},{6,7},{7,4},{8,9},{9,10},{10,1... | collective-permute-start | bytes 196616 | tf_op jit(solution)/shard_map/ppermute | solution.py:28
  120.7 6.4 %collective-permute-start.1 = (f32[128,128]{1,0:T(8,128)S(1)}, f32[128,128]{1,0:T(8,128)S(1)}, u32[]{:S(2)}, u32[]{:S(2)}) collective-permute-start(f32[128,128]{1,0:T(8,128)S(1)} %pad_maximum_fusion.3), channel_id=1, source_target_pairs={{0,2},{1,3},{2,0},{3,1},{4,6},{5,7},{6,4},{7,5},{8,10},{9,11},{10,... | collective-permute-start | bytes 196616 | tf_op jit(solution)/shard_map/ppermute | solution.py:28
  123.9 3.9 %collective-permute-start.2 = (f32[128,128]{1,0:T(8,128)S(1)}, f32[128,128]{1,0:T(8,128)S(1)}, u32[]{:S(2)}, u32[]{:S(2)}) collective-permute-start(f32[128,128]{1,0:T(8,128)S(1)} %pad_maximum_fusion.3), channel_id=1, source_target_pairs={{0,3},{1,0},{2,1},{3,2},{4,7},{5,4},{6,5},{7,6},{8,11},{9,8},{10,9... | collective-permute-start | bytes 196616 | tf_op jit(solution)/shard_map/ppermute | solution.py:28
  127.9 5.6 %collective-permute-start.3 = (f32[128,128]{1,0:T(8,128)S(1)}, f32[128,128]{1,0:T(8,128)S(1)}, u32[]{:S(2)}, u32[]{:S(2)}) collective-permute-start(f32[128,128]{1,0:T(8,128)S(1)} %add_add_fusion), channel_id=1, source_target_pairs={{0,4},{4,0},{1,5},{5,1},{2,6},{6,2},{3,7},{7,3},{8,12},{12,8},{9,1... | collective-permute-start | bytes 196616 | tf_op jit(solution)/shard_map/ppermute | solution.py:32
  133.5 0.8 copy-start.10
  140.4 0.8 copy-start.5
  141.2 1.0 copy-start.7
  145.1 1.9 %copy-start.6 = (f32[8,136,128]{2,1,0:T(8,128)}, f32[8,136,128]{2,1,0:T(8,128)S(1)}, u32[]{:S(2)}) copy-start(f32[8,136,128]{2,1,0:T(8,128)S(1)} %get-tuple-element.42) | copy-start | bytes 1671172
  145.1 6.0 %collective-permute-start.18 = (bf16[128,256]{1,0:T(8,128)(2,1)}, bf16[128,256]{1,0:T(8,128)(2,1)S(1)}, u32[]{:S(2)}, u32[]{:S(2)}) collective-permute-start(bf16[128,256]{1,0:T(8,128)(2,1)} %get-tuple-element.43), channel_id=1, source_target_pairs={{0,4},{4,0},{1,5},{5,1},{2,6},{6,2},{3,7},{7,3},{8,12},{12,8},{9,1... | collective-permute-start | bytes 196616 | tf_op jit(solution)/shard_map/ppermute | solution.py:32
  147.0 13.0 %all-to-all-start.3 = ((f32[8,136,128]{2,1,0:T(8,128)}), f32[8,136,128]{2,1,0:T(8,128)S(1)}, u32[]{:S(2)}, u32[]{:S(2)}) async-start(f32[8,136,128]{2,1,0:T(8,128)} %copy-done.6), calls=%async_computation.3 | async-start | bytes 1114112 | tf_op jit(solution)/shard_map/all_to_all | solution.py:502
  152.0 16.4 %copy-start.20 = (s32[32,3]{0,1:T(4,128)S(1)}, s32[32,3]{0,1:T(4,128)}, u32[]{:S(2)}) copy-start(s32[32,3]{0,1:T(4,128)} %param.16) | copy-start | bytes 1156
  152.0 16.9 %copy-start.22 = (s32[1,16]{1,0:T(1,128)S(1)}, s32[1,16]{1,0:T(1,128)}, u32[]{:S(2)}) copy-start(s32[1,16]{1,0:T(1,128)} %param.29) | copy-start | bytes 196
  152.1 21.3 %copy-start.21 = (s32[1,1024]{1,0:T(1,128)S(1)}, s32[1,1024]{1,0:T(1,128)}, u32[]{:S(2)}) copy-start(s32[1,1024]{1,0:T(1,128)} %param.28) | copy-start | bytes 12292
  152.1 34.8 %copy-start.16 = (bf16[128,512]{1,0:T(8,128)(2,1)}, bf16[128,512]{1,0:T(8,128)(2,1)S(1)}, u32[]{:S(2)}) copy-start(bf16[128,512]{1,0:T(8,128)(2,1)S(1)} %pad_maximum_fusion.2.p0) | copy-start | bytes 393220
  162.9 19.6 %all-to-all-start.4 = ((bf16[16,128,128]{2,1,0:T(8,128)(2,1)}), bf16[16,128,128]{2,1,0:T(8,128)(2,1)S(1)}, u32[]{:S(2)}, u32[]{:S(2)}) async-start(bf16[16,128,128]{2,1,0:T(8,128)(2,1)} %vectors.1), calls=%async_computation.4 | async-start | bytes 1048576 | tf_op jit(solution)/shard_map/all_to_all | solution.py:516
  169.0 5.1 %collective-permute-start.19 = (bf16[128,512]{1,0:T(8,128)(2,1)S(1)}, bf16[128,512]{1,0:T(8,128)(2,1)S(1)}, u32[]{:S(2)}, u32[]{:S(2)}) collective-permute-start(bf16[128,512]{1,0:T(8,128)(2,1)S(1)} %pad_maximum_fusion.2.p0), channel_id=1, source_target_pairs={{0,1},{1,2},{2,3},{3,0},{4,5},{5,6},{6,7},{7,4},{8,9},{9,10},{10,1... | collective-permute-start | bytes 393224 | tf_op jit(solution)/shard_map/ppermute | solution.py:28
  169.6 7.5 %collective-permute-start.20 = (bf16[128,512]{1,0:T(8,128)(2,1)S(1)}, bf16[128,512]{1,0:T(8,128)(2,1)S(1)}, u32[]{:S(2)}, u32[]{:S(2)}) collective-permute-start(bf16[128,512]{1,0:T(8,128)(2,1)S(1)} %pad_maximum_fusion.2.p0), channel_id=1, source_target_pairs={{0,2},{1,3},{2,0},{3,1},{4,6},{5,7},{6,4},{7,5},{8,10},{9,11},{10,... | collective-permute-start | bytes 393224 | tf_op jit(solution)/shard_map/ppermute | solution.py:28
  172.0 5.1 %collective-permute-start.21 = (bf16[128,512]{1,0:T(8,128)(2,1)S(1)}, bf16[128,512]{1,0:T(8,128)(2,1)S(1)}, u32[]{:S(2)}, u32[]{:S(2)}) collective-permute-start(bf16[128,512]{1,0:T(8,128)(2,1)S(1)} %pad_maximum_fusion.2.p0), channel_id=1, source_target_pairs={{0,3},{1,0},{2,1},{3,2},{4,7},{5,4},{6,5},{7,6},{8,11},{9,8},{10,9... | collective-permute-start | bytes 393224 | tf_op jit(solution)/shard_map/ppermute | solution.py:28
  174.1 12.8 %copy-start.17 = (bf16[128,512]{1,0:T(8,128)(2,1)}, bf16[128,512]{1,0:T(8,128)(2,1)S(1)}, u32[]{:S(2)}) copy-start(bf16[128,512]{1,0:T(8,128)(2,1)S(1)} %collective-permute-done.19.p1) | copy-start | bytes 393220
  177.1 9.8 %copy-start.18 = (bf16[128,512]{1,0:T(8,128)(2,1)}, bf16[128,512]{1,0:T(8,128)(2,1)S(1)}, u32[]{:S(2)}) copy-start(bf16[128,512]{1,0:T(8,128)(2,1)S(1)} %collective-permute-done.20.p2) | copy-start | bytes 393220
  177.1 9.8 %copy-start.19 = (bf16[128,512]{1,0:T(8,128)(2,1)}, bf16[128,512]{1,0:T(8,128)(2,1)S(1)}, u32[]{:S(2)}) copy-start(bf16[128,512]{1,0:T(8,128)(2,1)S(1)} %collective-permute-done.21.p3) | copy-start | bytes 393220
  182.5 6.3 %copy-start.14 = (bf16[16,128,128]{2,1,0:T(8,128)(2,1)}, bf16[16,128,128]{2,1,0:T(8,128)(2,1)S(1)}, u32[]{:S(2)}) copy-start(bf16[16,128,128]{2,1,0:T(8,128)(2,1)S(1)} %all-to-all-done.4) | copy-start | bytes 1572868
  182.5 6.3 %collective-permute-start.22 = (bf16[2048,128]{1,0:T(8,128)(2,1)S(1)}, bf16[2048,128]{1,0:T(8,128)(2,1)S(1)}, u32[]{:S(2)}, u32[]{:S(2)}) collective-permute-start(bf16[2048,128]{1,0:T(8,128)(2,1)S(1)} %bitcast.25), channel_id=1, source_target_pairs={{0,8},{8,0},{1,9},{9,1},{2,10},{10,2},{3,11},{11,3},{4,12},{12,4},... | collective-permute-start | bytes 1572872 | tf_op jit(solution)/shard_map/ppermute | solution.py:530
  (3 other events, 2.4 us)

commit v9 on v7

--- a/solution.py
+++ b/solution.py
@@ -39,10 +39,12 @@
     x_hbm,
     w_hbm,
     out_hbm,
+    gate_hbm,
     out0,
     out1,
     out2,
     out3,
+    sent_hbm,
     x_ref,
     w_ref,
     out_w_ref,
@@ -53,6 +55,7 @@
         pltpu.make_async_copy(w_hbm.at[part], w_ref.at[part], sems.at[1 + part]) for part in range(3)
     ]
     copies += [pltpu.make_async_copy(out_hbm, out_w_ref, sems.at[4])]
+    copies += [pltpu.make_async_copy(gate_hbm.at[1 - here_ref[0]], sent_hbm, sems.at[5])]
     for copy in copies:
         copy.start()
     wide = here_ref[2]
@@ -107,6 +110,7 @@
         part = lax.rem(j + k, 4)
         columns = pl.ds(pl.multiple_of(part * 512, 512), 512)
         out_ref[...] = jnp.dot(mixed, out_w_ref[:, columns], preferred_element_type=f32).astype(bf16)
+    copies[5].wait()
 
 
 def choose_kernel(here_ref, routes_ref, out_ref):
@@ -171,16 +175,18 @@
     for copy in copies:
         copy.wait()
     for half, (xs, scale) in enumerate(zip(halves, scales)):
-        own = jnp.zeros((HALF, 256), f32)
-        par = jnp.zeros((HALF, 256), f32)
+        normed, weights = [], []
         for k, x in enumerate(xs):
             part = lax.rem(j + 4 + (0, -1, 1, 2)[k], 4)
             rows = pl.ds(pl.multiple_of(part * 512, 512), 512)
-            normed = (x[...].astype(f32) * scale * gain_ref[1:2, rows]).astype(bf16)
-            w_own = jnp.concatenate([w_ref[0, rows, :], w_ref[1, rows, :]], axis=1)
-            w_par = jnp.concatenate([w_ref[2, rows, :], w_ref[3, rows, :]], axis=1)
-            own = own + jnp.dot(normed, w_own, preferred_element_type=f32)
-            par = par + jnp.dot(normed, w_par, preferred_element_type=f32)
+            normed.append((x[...].astype(f32) * scale * gain_ref[1:2, rows]).astype(bf16))
+            weights.append(jnp.concatenate([w_ref[n, rows, :] for n in range(4)], axis=1))
+        both = jnp.dot(
+            jnp.concatenate(normed, axis=1),
+            jnp.concatenate(weights, axis=0),
+            preferred_element_type=f32,
+        )
+        own, par = both[:, 0:256], both[:, 256:512]
         for at, both in ((0, own), (128, par)):
             gate, up = both[:, :128], both[:, 128:]
             out_ref[half * HALF : (half + 1) * HALF, at : at + 128] = (
@@ -201,11 +207,14 @@
     for pair in copies:
         for copy in pair:
             copy.start()
-    total = jnp.zeros((a0.shape[0], 512), f32)
-    for k, a in enumerate((a0, a1, a2, a3)):
-        for copy in copies[k]:
+    for pair in copies:
+        for copy in pair:
             copy.wait()
-        total = total + jnp.dot(a[...], w_ref[k], preferred_element_type=f32)
+    total = jnp.dot(
+        jnp.concatenate([a0[...], a1[...], a2[...], a3[...]], axis=1),
+        jnp.concatenate([w_ref[k] for k in range(4)], axis=0),
+        preferred_element_type=f32,
+    )
     size = out_ref.shape[1]
     for s in range(WIDE):
         out_ref[s] = total[s * size : (s + 1) * size].astype(bf16)
@@ -327,19 +336,19 @@
     def cut(array, part, axis):
         return lax.dynamic_slice_in_dim(array, lax.rem(part, 4) * 512, 512, axis)
 
-    gate_sent, tokens = lax.optimization_barrier((pick(w_gate, 1 - i), tokens))
-    gate_par = x_swap(gate_sent)
-
-    attn = pl.pallas_call(
+    *attn, gate_sent = pl.pallas_call(
         attention_kernel,
-        out_shape=(jax.ShapeDtypeStruct((TOK, 512), bf16),) * 4,
-        in_specs=[smem()] * 2 + [vmem()] * 2 + [hbm()] * 3,
-        out_specs=(vmem(),) * 4,
+        out_shape=(
+            *(jax.ShapeDtypeStruct((TOK, 512), bf16),) * 4,
+            jax.ShapeDtypeStruct((2048, 128), bf16),
+        ),
+        in_specs=[smem()] * 2 + [vmem()] * 2 + [hbm()] * 4,
+        out_specs=(*(vmem(),) * 4, hbm()),
         scratch_shapes=[
             pltpu.VMEM((TOK, 2048), bf16),
             pltpu.VMEM((3, 2048, 256), bf16),
             pltpu.VMEM((256, 2048), bf16),
-            pltpu.SemaphoreType.DMA((5,)),
+            pltpu.SemaphoreType.DMA((6,)),
         ],
         compiler_params=pltpu.CompilerParams(vmem_limit_bytes=60 << 20),
         name="attention",
@@ -351,11 +360,13 @@
         tokens,
         w_qkv.transpose(1, 0, 2),
         w_out,
-    )
+        w_gate,
+    )
+    gate_par = x_swap(gate_sent)
     attn_parts = [y_shift(attn[k], k) for k in (1, 2, 3)]
 
     downs = [cut(w_down, j, 2)] + [y_shift(cut(w_down, j + k, 2), k) for k in (1, 2, 3)]
-    down_par = x_swap(jnp.stack([pick(d, 1 - i) for d in downs]))
+    down_sent = jnp.stack([pick(d, 1 - i) for d in downs])
 
     experts_here = 2 * jnp.arange(WIDE, dtype=jnp.int32) + i
     hit = jnp.sum((routes.T[None, :, :] == experts_here[:, None, None]).astype(f32), axis=1)
@@ -399,11 +410,15 @@
         compiler_params=params(),
         name="unpack",
     )(arrived)
-    top, bottom, up_sent = lax.optimization_barrier((top, bottom, pick(w_up, 1 - i)))
+    top, bottom, up_sent, down_sent = lax.optimization_barrier(
+        (top, bottom, pick(w_up, 1 - i), down_sent)
+    )
     up_par = x_swap(up_sent)
     top_back, bottom_ahead = y_shift(top, 1), y_shift(bottom, 3)
     bottom_back, top_ahead = y_shift(bottom, 1), y_shift(top, 3)
     top_far, bottom_far = y_shift(top_back, 1), y_shift(bottom_ahead, 3)
+    top_ahead, down_sent = lax.optimization_barrier((top_ahead, down_sent))
+    down_par = x_swap(down_sent)
     act = pl.pallas_call(
         gate_up_kernel,
         out_shape=jax.ShapeDtypeStruct((2 * HALF, 256), bf16),

time: 188 us -> 209 us (1.11)
  Pallas kernels: 23.7 us -> 39 us
  waiting for transfers between devices: 76.4 us -> 82.1 us
    ppermute x24, waiting for transfers between devices: 34.6 us -> 51.6 us  [y_shift(): return lax.ppermute(x, 'y', [(s, (s + k) % 4) for s in range(4)])]
    pallas_call x1, Pallas kernels: 5.08 us -> 18.7 us  [body(): pl.pallas_call(attention_kernel, out_shape=(*(jax.ShapeDtypeStruct((TOK,...]
    all_to_all x1, waiting for transfers between devices: 11.5 us -> 0.01 us  [body(): arrived = lax.all_to_all(rows, W, 0, 0, tiled=True)]
    all_to_all x1, starting transfers between devices: 7.57 us -> 9.72 us  [body(): back = lax.all_to_all(out, W, 0, 0, tiled=True)]
    unnamed x47 -> x51, local copies, waits for them, and re-layouts: 3.3 us -> 5.02 us
  transfers between devices with their start and end apart: 33 -> 33, of which waited for: 20 -> 22; matrix products, arithmetic and copies ran while one was open for 6% -> 5% of each run, Pallas kernels for 6% -> 3%
where the time goes in v9:
time: 209 us; the launch traced here: 208 us
  waiting for transfers between devices  82.1 us (39%)
  starting transfers between devices  68.4 us (33%)
  Pallas kernels  39 us (19%)
  local copies, waits for them, and re-layouts  12.8 us (6%)
  other arithmetic  3.2 us (2%)
    ppermute x24, waiting for transfers between devices, y_shift(): return lax.ppermute(x, 'y', [(s, (s + k) % 4) for s in range(4)])  51.6 us
    ppermute x24, starting transfers between devices, y_shift(): return lax.ppermute(x, 'y', [(s, (s + k) % 4) for s in range(4)])  28.7 us
    pallas_call x1, Pallas kernels, body(): pl.pallas_call(attention_kernel, out_shape=(*(jax.ShapeDtypeStruct((TOK,...  18.7 us
    all_to_all x1, waiting for transfers between devices, body(): back = lax.all_to_all(out, W, 0, 0, tiled=True)  15.2 us
    all_to_all x1, starting transfers between devices, body(): arrived = lax.all_to_all(rows, W, 0, 0, tiled=True)  11.6 us
    all_to_all x1, starting transfers between devices, body(): back = lax.all_to_all(out, W, 0, 0, tiled=True)  9.72 us
    ppermute x5, starting transfers between devices, x_swap(): return lax.ppermute(x, 'xh', [(0, 1), (1, 0)])  9.12 us
    ppermute x5, waiting for transfers between devices, x_swap(): return lax.ppermute(x, 'xh', [(0, 1), (1, 0)])  8.91 us
  transfers between devices with their start and end apart: 33, of which 22 were waited for; matrix products, arithmetic and copies ran while one was open for 5% of the time, Pallas kernels for 3%

profile of v9, /device:TPU:1, one launch (start us, length us, event | category | flops | bytes accessed | tf_op | source)
XLA Modules:
  0.0 207.8 jit_solution(16704342124115525128)
XLA Ops:
  1.3 18.7 %attention.1 = (bf16[128,512]{1,0:T(8,128)(2,1)}, bf16[128,512]{1,0:T(8,128)(2,1)}, bf16[128,512]{1,0:T(8,128)(2,1)}, bf16[128,512]{1,0:T(8,128)(2,1)}, bf16[2048,128]{1,0:T(8,128)(2,1)}) custom-call(s32[4]{0:T(128)} %pad_add_fusion.here_ref, s32[3,32]{1,0:T(4,128)} %bitcast.37, f32[2,256]{1,0:T(2,128)} %qk_ref.1, f32[3,2048]{1,0:T(4,128)} %gain_ref.3, ...), custom_call_target="tpu_custom_call" | custom-call | tf_op jit(solution)/shard_map/attention/pallas_call | solution.py:339
  20.0 3.7 %collective-permute-start.4 = (bf16[2048,128]{1,0:T(8,128)(2,1)}, bf16[2048,128]{1,0:T(8,128)(2,1)S(1)}, u32[]{:S(2)}, u32[]{:S(2)}) collective-permute-start(bf16[2048,128]{1,0:T(8,128)(2,1)} %get-tuple-element.36), channel_id=1, source_target_pairs={{0,4},{4,0},{1,5},{5,1},{2,6},{6,2},{3,7},{7,3},{8,12},{12,8},{9,1... | collective-permute-start | bytes 1572872 | tf_op jit(solution)/shard_map/ppermute | solution.py:31
  23.6 1.3 collective-permute-start
  24.9 2.6 %collective-permute-start.1 = (bf16[128,512]{1,0:T(8,128)(2,1)}, bf16[128,512]{1,0:T(8,128)(2,1)S(1)}, u32[]{:S(2)}, u32[]{:S(2)}) collective-permute-start(bf16[128,512]{1,0:T(8,128)(2,1)} %get-tuple-element.33), channel_id=1, source_target_pairs={{0,2},{1,3},{2,0},{3,1},{4,6},{5,7},{6,4},{7,5},{8,10},{9,11},{10,... | collective-permute-start | bytes 393224 | tf_op jit(solution)/shard_map/ppermute | solution.py:27
  27.5 1.1 collective-permute-start.2
  29.5 3.6 %collective-permute-done.1 = bf16[128,512]{1,0:T(8,128)(2,1)S(1)} collective-permute-done((bf16[128,512]{1,0:T(8,128)(2,1)}, bf16[128,512]{1,0:T(8,128)(2,1)S(1)}, u32[]{:S(2)}, u32[]{:S(2)}) %collective-permute-start.1) | collective-permute-done | bytes 131104 | tf_op jit(solution)/shard_map/ppermute | solution.py:27
  34.3 5.3 %collective-permute-done.3.par_ref = bf16[128,512]{1,0:T(8,128)(2,1)S(1)} collective-permute-done((bf16[128,512]{1,0:T(8,128)(2,1)S(1)}, bf16[128,512]{1,0:T(8,128)(2,1)S(1)}, u32[]{:S(2)}, u32[]{:S(2)}) %collective-permute-start.3) | collective-permute-done | bytes 131104 | tf_op jit(solution)/shard_map/ppermute | solution.py:31
  39.6 1.7 dispatch.1
  41.3 11.6 %all-to-all-start = ((bf16[32,40,256]{2,1,0:T(8,128)(2,1)}), bf16[32,40,256]{2,1,0:T(8,128)(2,1)S(1)}, u32[]{:S(2)}, u32[]{:S(2)}) async-start(bf16[32,40,256]{2,1,0:T(8,128)(2,1)} %get-tuple-element.40), calls=%async_computation | async-start | bytes 1310720 | tf_op jit(solution)/shard_map/all_to_all | solution.py:403
  53.0 2.2 %constant_dynamic-slice_fusion = (bf16[2,128,512]{2,1,0:T(8,128)(2,1)S(1)}, bf16[2,128,512]{2,1,0:T(8,128)(2,1)}, bf16[2,128,512]{2,1,0:T(8,128)(2,1)}, bf16[2,128,512]{2,1,0:T(8,128)(2,1)}) fusion(bf16[2,128,2048]{2,1,0:T(8,128)(2,1)} %param.25, s32[]{:T(128)S(6)} %select_n.64, s32[]{:T(128)S(6)} %select_n.67, s32[]{:T(128)S(6)} %select_n.66, s32[]{:T(128)S(6)} %select_n.68), kind=kLoop, calls=%fused_computation.53 | loop fusion | bytes 2097168 | tf_op jit(solution)/shard_map/dynamic_slice | solution.py:337
  55.2 2.0 collective-permute-start.10
  60.2 3.1 %collective-permute-done.10.w3 = bf16[2,128,512]{2,1,0:T(8,128)(2,1)} collective-permute-done((bf16[2,128,512]{2,1,0:T(8,128)(2,1)}, bf16[2,128,512]{2,1,0:T(8,128)(2,1)}, u32[]{:S(2)}, u32[]{:S(2)}) %collective-permute-start.10) | collective-permute-done | bytes 262176 | tf_op jit(solution)/shard_map/ppermute | solution.py:27
  64.3 2.2 %collective-permute-done.9.w2 = bf16[2,128,512]{2,1,0:T(8,128)(2,1)} collective-permute-done((bf16[2,128,512]{2,1,0:T(8,128)(2,1)}, bf16[2,128,512]{2,1,0:T(8,128)(2,1)}, u32[]{:S(2)}, u32[]{:S(2)}) %collective-permute-start.9) | collective-permute-done | bytes 262176 | tf_op jit(solution)/shard_map/ppermute | solution.py:27
  67.4 5.5 %collective-permute-done.8.w1 = bf16[2,128,512]{2,1,0:T(8,128)(2,1)} collective-permute-done((bf16[2,128,512]{2,1,0:T(8,128)(2,1)}, bf16[2,128,512]{2,1,0:T(8,128)(2,1)}, u32[]{:S(2)}, u32[]{:S(2)}) %collective-permute-start.8) | collective-permute-done | bytes 262176 | tf_op jit(solution)/shard_map/ppermute | solution.py:27
  75.6 2.7 %collective-permute-start.15 = (bf16[320,512]{1,0:T(8,128)(2,1)}, bf16[320,512]{1,0:T(8,128)(2,1)S(1)}, u32[]{:S(2)}, u32[]{:S(2)}) collective-permute-start(bf16[320,512]{1,0:T(8,128)(2,1)} %get-tuple-element.46.refs_4_), channel_id=1, source_target_pairs={{0,3},{1,0},{2,1},{3,2},{4,7},{5,4},{6,5},{7,6},{8,11},{9,8},{10,9... | collective-permute-start | bytes 983048 | tf_op jit(solution)/shard_map/ppermute | solution.py:27
  78.4 1.8 collective-permute-start.17
  80.4 1.6 collective-permute-start.14
  82.0 3.9 %collective-permute-done.11.refs_1_ = bf16[320,512]{1,0:T(8,128)(2,1)S(1)} collective-permute-done((bf16[320,512]{1,0:T(8,128)(2,1)}, bf16[320,512]{1,0:T(8,128)(2,1)S(1)}, u32[]{:S(2)}, u32[]{:S(2)}) %collective-permute-start.11) | collective-permute-done | bytes 327712 | tf_op jit(solution)/shard_map/ppermute | solution.py:27
  85.8 2.7 %collective-permute-start.16 = (bf16[320,512]{1,0:T(8,128)(2,1)S(1)}, bf16[320,512]{1,0:T(8,128)(2,1)S(1)}, u32[]{:S(2)}, u32[]{:S(2)}) collective-permute-start(bf16[320,512]{1,0:T(8,128)(2,1)S(1)} %collective-permute-done.15.refs_6_), channel_id=1, source_target_pairs={{0,3},{1,0},{2,1},{3,2},{4,7},{5,4},{6,5},{7,6},{8,11},{9,8},{10,9... | collective-permute-start | bytes 983048 | tf_op jit(solution)/shard_map/ppermute | solution.py:27
  89.3 2.6 %collective-permute-done.12.refs_2_ = bf16[320,512]{1,0:T(8,128)(2,1)S(1)} collective-permute-done((bf16[320,512]{1,0:T(8,128)(2,1)}, bf16[320,512]{1,0:T(8,128)(2,1)S(1)}, u32[]{:S(2)}, u32[]{:S(2)}) %collective-permute-start.12) | collective-permute-done | bytes 327712 | tf_op jit(solution)/shard_map/ppermute | solution.py:27
  91.9 1.7 collective-permute-start.21
  93.7 6.2 %collective-permute-done.13.refs_3_ = bf16[320,512]{1,0:T(8,128)(2,1)S(1)} collective-permute-done((bf16[320,512]{1,0:T(8,128)(2,1)S(1)}, bf16[320,512]{1,0:T(8,128)(2,1)S(1)}, u32[]{:S(2)}, u32[]{:S(2)}) %collective-permute-start.13) | collective-permute-done | bytes 327712 | tf_op jit(solution)/shard_map/ppermute | solution.py:27
  99.9 1.0 copy-done.6
  101.9 3.5 %gate_up.1.a0 = bf16[640,256]{1,0:T(8,128)(2,1)S(1)} custom-call(s32[4]{0:T(128)S(1)} %copy-done.11, bf16[320,512]{1,0:T(8,128)(2,1)} %get-tuple-element.43.refs_0_, bf16[320,512]{1,0:T(8,128)(2,1)S(1)} %collective-permute-done.11.refs_1_, bf16[320,512]{1,0:T(8,128)(2,1)S(1)} %collective-permute-done.12.refs_2_, ...), custom_call_target="tpu_custom_call" | custom-call | tf_op jit(solution)/shard_map/gate_up/pallas_call | solution.py:422
  105.5 3.5 %collective-permute-start.19 = (bf16[640,256]{1,0:T(8,128)(2,1)S(1)}, bf16[640,256]{1,0:T(8,128)(2,1)S(1)}, u32[]{:S(2)}, u32[]{:S(2)}) collective-permute-start(bf16[640,256]{1,0:T(8,128)(2,1)S(1)} %gate_up.1.a0), channel_id=1, source_target_pairs={{0,2},{1,3},{2,0},{3,1},{4,6},{5,7},{6,4},{7,5},{8,10},{9,11},{10,... | collective-permute-start | bytes 983048 | tf_op jit(solution)/shard_map/ppermute | solution.py:27
  109.1 5.4 %collective-permute-done.18.a1 = bf16[640,256]{1,0:T(8,128)(2,1)S(1)} collective-permute-done((bf16[640,256]{1,0:T(8,128)(2,1)S(1)}, bf16[640,256]{1,0:T(8,128)(2,1)S(1)}, u32[]{:S(2)}, u32[]{:S(2)}) %collective-permute-start.18) | collective-permute-done | bytes 327712 | tf_op jit(solution)/shard_map/ppermute | solution.py:27
  114.5 7.6 %collective-permute-done.19.a2 = bf16[640,256]{1,0:T(8,128)(2,1)S(1)} collective-permute-done((bf16[640,256]{1,0:T(8,128)(2,1)S(1)}, bf16[640,256]{1,0:T(8,128)(2,1)S(1)}, u32[]{:S(2)}, u32[]{:S(2)}) %collective-permute-start.19) | collective-permute-done | bytes 327712 | tf_op jit(solution)/shard_map/ppermute | solution.py:27
  122.9 4.0 %down.1 = bf16[32,20,512]{2,1,0:T(8,128)(2,1)} custom-call(s32[4]{0:T(128)S(1)} %copy-done.11, bf16[640,256]{1,0:T(8,128)(2,1)S(1)} %gate_up.1.a0, bf16[640,256]{1,0:T(8,128)(2,1)S(1)} %collective-permute-done.18.a1, bf16[640,256]{1,0:T(8,128)(2,1)S(1)} %collective-permute-done.19.a2, bf16[640,256]{1,0:T(8,128)(2,1)S(1)} %collective-permute-done.20.a3, ...), custom_call_target="tpu_custom_call" | custom-call | tf_op jit(solution)/shard_map/down/pallas_call | solution.py:444
  126.9 9.7 %all-to-all-start.1 = ((bf16[32,20,512]{2,1,0:T(8,128)(2,1)}), bf16[32,20,512]{2,1,0:T(8,128)(2,1)S(1)}, u32[]{:S(2)}, u32[]{:S(2)}) async-start(bf16[32,20,512]{2,1,0:T(8,128)(2,1)} %down.1), calls=%async_computation.1 | async-start | bytes 1572864 | tf_op jit(solution)/shard_map/all_to_all | solution.py:453
  137.1 3.3 %collective-permute-start.6 = (f32[128,128]{0,1:T(8,128)S(1)}, f32[128,128]{0,1:T(8,128)S(1)}, u32[]{:S(2)}, u32[]{:S(2)}) collective-permute-start(f32[128,128]{0,1:T(8,128)S(1)} %pad_maximum_fusion.1), channel_id=1, source_target_pairs={{0,2},{1,3},{2,0},{3,1},{4,6},{5,7},{6,4},{7,5},{8,10},{9,11},{10,... | collective-permute-start | bytes 196616 | tf_op jit(solution)/shard_map/ppermute | solution.py:27
  140.3 1.3 collective-permute-done.5
  141.7 2.1 collective-permute-done.6
  144.0 15.2 %all-to-all-done.1 = bf16[32,20,512]{2,1,0:T(8,128)(2,1)S(1)} async-done(((bf16[32,20,512]{2,1,0:T(8,128)(2,1)}), bf16[32,20,512]{2,1,0:T(8,128)(2,1)S(1)}, u32[]{:S(2)}, u32[]{:S(2)}) %all-to-all-start.1) | async-done | bytes 655392 | tf_op jit(solution)/shard_map/all_to_all | solution.py:453
  160.1 1.8 collective-permute-start.22
  162.0 3.6 %collective-permute-done.22.par_ref = bf16[128,512]{1,0:T(8,128)(2,1)S(1)} collective-permute-done((bf16[128,512]{1,0:T(8,128)(2,1)S(1)}, bf16[128,512]{1,0:T(8,128)(2,1)S(1)}, u32[]{:S(2)}, u32[]{:S(2)}) %collective-permute-start.22) | collective-permute-done | bytes 131104 | tf_op jit(solution)/shard_map/ppermute | solution.py:31
  166.2 2.1 %embed.1 = (bf16[128,512]{1,0:T(8,128)(2,1)}, f32[136,128]{1,0:T(8,128)}) custom-call(s32[4]{0:T(128)} %pad_add_fusion.here_ref, bf16[128,512]{1,0:T(8,128)(2,1)} %copy-done.4, bf16[128,512]{1,0:T(8,128)(2,1)} %copy-done.14, bf16[128,512]{1,0:T(8,128)(2,1)} %copy-done.15, f32[3,2048]{1,0:T(4,128)} %gain_ref.3, bf16[2048,128]{1,0:T(8,128)(2,1)} %w_ref.1), custom_call_target="tpu_custom_call" | custom-call | tf_op jit(solution)/shard_map/embed/pallas_call | solution.py:483
  168.3 3.3 %collective-permute-start.24 = (f32[136,128]{1,0:T(8,128)}, f32[136,128]{1,0:T(8,128)S(1)}, u32[]{:S(2)}, u32[]{:S(2)}) collective-permute-start(f32[136,128]{1,0:T(8,128)} %get-tuple-element.50.p0), channel_id=1, source_target_pairs={{0,2},{1,3},{2,0},{3,1},{4,6},{5,7},{6,4},{7,5},{8,10},{9,11},{10,... | collective-permute-start | bytes 208904 | tf_op jit(solution)/shard_map/ppermute | solution.py:27
  171.6 1.3 collective-permute-done.23.p1
  172.9 1.4 collective-permute-done.24.p2
  175.9 2.0 vectors.1
  177.9 5.1 %all-to-all-start.2 = ((bf16[16,128,128]{2,1,0:T(8,128)(2,1)}), bf16[16,128,128]{2,1,0:T(8,128)(2,1)S(1)}, u32[]{:S(2)}, u32[]{:S(2)}) async-start(bf16[16,128,128]{2,1,0:T(8,128)(2,1)} %vectors.1), calls=%async_computation.2 | async-start | bytes 1048576 | tf_op jit(solution)/shard_map/all_to_all | solution.py:504
  183.6 1.8 collective-permute-start.27
  185.4 1.4 collective-permute-start.28
  187.7 2.9 %collective-permute-done.26.p1 = bf16[128,512]{1,0:T(8,128)(2,1)S(1)} collective-permute-done((bf16[128,512]{1,0:T(8,128)(2,1)}, bf16[128,512]{1,0:T(8,128)(2,1)S(1)}, u32[]{:S(2)}, u32[]{:S(2)}) %collective-permute-start.26) | collective-permute-done | bytes 131104 | tf_op jit(solution)/shard_map/ppermute | solution.py:27
  191.1 6.5 %all-to-all-done.2 = bf16[16,128,128]{2,1,0:T(8,128)(2,1)S(1)} async-done(((bf16[16,128,128]{2,1,0:T(8,128)(2,1)}), bf16[16,128,128]{2,1,0:T(8,128)(2,1)S(1)}, u32[]{:S(2)}, u32[]{:S(2)}) %all-to-all-start.2) | async-done | bytes 524320 | tf_op jit(solution)/shard_map/all_to_all | solution.py:504
  197.6 4.1 %collective-permute-start.29 = (bf16[2048,128]{1,0:T(8,128)(2,1)S(1)}, bf16[2048,128]{1,0:T(8,128)(2,1)S(1)}, u32[]{:S(2)}, u32[]{:S(2)}) collective-permute-start(bf16[2048,128]{1,0:T(8,128)(2,1)S(1)} %bitcast.34), channel_id=1, source_target_pairs={{0,8},{8,0},{1,9},{9,1},{2,10},{10,2},{3,11},{11,3},{4,12},{12,4},... | collective-permute-start | bytes 1572872 | tf_op jit(solution)/shard_map/ppermute | solution.py:518
  201.6 1.9 assemble.1
  204.4 3.2 %score.1 = f32[1,16]{1,0:T(1,128)} custom-call(s32[5,16]{1,0:T(8,128)} %stack.48.info_ref, bf16[1024,128]{1,0:T(8,128)(2,1)} %doc_ref.1, bf16[2048,128]{1,0:T(8,128)(2,1)} %bitcast.35, bf16[2048,128]{1,0:T(8,128)(2,1)} %copy-done.13), custom_call_target="tpu_custom_call" | custom-call | tf_op jit(solution)/shard_map/score/pallas_call | solution.py:526
  (117 shorter events, 19.8 us)
Async XLA Ops:
  0.6 136.0 %copy-start = (bf16[2048,64]{0,1:T(8,128)(2,1)S(1)}, bf16[2048,64]{0,1:T(8,128)(2,1)}, u32[]{:S(2)}) copy-start(bf16[2048,64]{0,1:T(8,128)(2,1)} %param.21) | copy-start | bytes 786436
  0.6 28.0 %copy-start.10 = (s32[128,8]{0,1:T(8,128)S(1)}, s32[128,8]{0,1:T(8,128)}, u32[]{:S(2)}) copy-start(s32[128,8]{0,1:T(8,128)} %param.22) | copy-start | bytes 12292
  1.3 27.3 %copy-start.11 = (s32[4]{0:T(128)S(1)}, s32[4]{0:T(128)}, u32[]{:S(2)}) copy-start(s32[4]{0:T(128)} %pad_add_fusion.here_ref) | copy-start | bytes 52
  1.3 38.3 %copy-start.3 = (bf16[128,2048]{1,0:T(8,128)(2,1)S(1)}, bf16[128,2048]{1,0:T(8,128)(2,1)}, u32[]{:S(2)}) copy-start(bf16[128,2048]{1,0:T(8,128)(2,1)} %x_ref.1) | copy-start | bytes 1572868
  19.9 38.4 %copy-start.2 = (bf16[2,2048,128]{2,1,0:T(8,128)(2,1)S(1)}, bf16[2,2048,128]{2,1,0:T(8,128)(2,1)}, u32[]{:S(2)}) copy-start(bf16[2,2048,128]{2,1,0:T(8,128)(2,1)} %refs_10_.1) | copy-start | bytes 3145732
  20.0 19.6 %collective-permute-start.4 = (bf16[2048,128]{1,0:T(8,128)(2,1)}, bf16[2048,128]{1,0:T(8,128)(2,1)S(1)}, u32[]{:S(2)}, u32[]{:S(2)}) collective-permute-start(bf16[2048,128]{1,0:T(8,128)(2,1)} %get-tuple-element.36), channel_id=1, source_target_pairs={{0,4},{4,0},{1,5},{5,1},{2,6},{6,2},{3,7},{7,3},{8,12},{12,8},{9,1... | collective-permute-start | bytes 1572872 | tf_op jit(solution)/shard_map/ppermute | solution.py:31
  23.6 5.9 %collective-permute-start = (bf16[128,512]{1,0:T(8,128)(2,1)}, bf16[128,512]{1,0:T(8,128)(2,1)S(1)}, u32[]{:S(2)}, u32[]{:S(2)}) collective-permute-start(bf16[128,512]{1,0:T(8,128)(2,1)} %get-tuple-element.32), channel_id=1, source_target_pairs={{0,1},{1,2},{2,3},{3,0},{4,5},{5,6},{6,7},{7,4},{8,9},{9,10},{10,1... | collective-permute-start | bytes 393224 | tf_op jit(solution)/shard_map/ppermute | solution.py:27
  24.9 8.2 %collective-permute-start.1 = (bf16[128,512]{1,0:T(8,128)(2,1)}, bf16[128,512]{1,0:T(8,128)(2,1)S(1)}, u32[]{:S(2)}, u32[]{:S(2)}) collective-permute-start(bf16[128,512]{1,0:T(8,128)(2,1)} %get-tuple-element.33), channel_id=1, source_target_pairs={{0,2},{1,3},{2,0},{3,1},{4,6},{5,7},{6,4},{7,5},{8,10},{9,11},{10,... | collective-permute-start | bytes 393224 | tf_op jit(solution)/shard_map/ppermute | solution.py:27
  27.5 5.6 %collective-permute-start.2 = (bf16[128,512]{1,0:T(8,128)(2,1)}, bf16[128,512]{1,0:T(8,128)(2,1)S(1)}, u32[]{:S(2)}, u32[]{:S(2)}) collective-permute-start(bf16[128,512]{1,0:T(8,128)(2,1)} %get-tuple-element.34), channel_id=1, source_target_pairs={{0,3},{1,0},{2,1},{3,2},{4,7},{5,4},{6,5},{7,6},{8,11},{9,8},{10,9... | collective-permute-start | bytes 393224 | tf_op jit(solution)/shard_map/ppermute | solution.py:27
  34.2 5.4 %collective-permute-start.3 = (bf16[128,512]{1,0:T(8,128)(2,1)S(1)}, bf16[128,512]{1,0:T(8,128)(2,1)S(1)}, u32[]{:S(2)}, u32[]{:S(2)}) collective-permute-start(bf16[128,512]{1,0:T(8,128)(2,1)S(1)} %add_convert_fusion.own_ref), channel_id=1, source_target_pairs={{0,4},{4,0},{1,5},{5,1},{2,6},{6,2},{3,7},{7,3},{8,12},{12,8},{9,1... | collective-permute-start | bytes 393224 | tf_op jit(solution)/shard_map/ppermute | solution.py:31
  41.3 95.5 %copy-start.4 = (bf16[128,512]{1,0:T(8,128)(2,1)}, bf16[128,512]{1,0:T(8,128)(2,1)S(1)}, u32[]{:S(2)}) copy-start(bf16[128,512]{1,0:T(8,128)(2,1)S(1)} %get-tuple-element.39.hidden_ref) | copy-start | bytes 393220
  41.3 33.4 %all-to-all-start = ((bf16[32,40,256]{2,1,0:T(8,128)(2,1)}), bf16[32,40,256]{2,1,0:T(8,128)(2,1)S(1)}, u32[]{:S(2)}, u32[]{:S(2)}) async-start(bf16[32,40,256]{2,1,0:T(8,128)(2,1)} %get-tuple-element.40), calls=%async_computation | async-start | bytes 1310720 | tf_op jit(solution)/shard_map/all_to_all | solution.py:403
  53.0 25.3 %copy-start.7 = (f32[3,2048]{1,0:T(4,128)S(1)}, f32[3,2048]{1,0:T(4,128)}, u32[]{:S(2)}) copy-start(f32[3,2048]{1,0:T(4,128)} %gain_ref.3) | copy-start | bytes 73732
  53.0 46.9 %copy-start.1 = (bf16[2,2048,128]{2,1,0:T(8,128)(2,1)S(1)}, bf16[2,2048,128]{2,1,0:T(8,128)(2,1)}, u32[]{:S(2)}) copy-start(bf16[2,2048,128]{2,1,0:T(8,128)(2,1)} %refs_9_.1) | copy-start | bytes 3145732
  55.2 8.1 %collective-permute-start.10 = (bf16[2,128,512]{2,1,0:T(8,128)(2,1)}, bf16[2,128,512]{2,1,0:T(8,128)(2,1)}, u32[]{:S(2)}, u32[]{:S(2)}) collective-permute-start(bf16[2,128,512]{2,1,0:T(8,128)(2,1)} %get-tuple-element.67), channel_id=1, source_target_pairs={{0,3},{1,0},{2,1},{3,2},{4,7},{5,4},{6,5},{7,6},{8,11},{9,8},{10,9... | collective-permute-start | bytes 786440 | tf_op jit(solution)/shard_map/ppermute | solution.py:27
  57.2 9.2 %collective-permute-start.9 = (bf16[2,128,512]{2,1,0:T(8,128)(2,1)}, bf16[2,128,512]{2,1,0:T(8,128)(2,1)}, u32[]{:S(2)}, u32[]{:S(2)}) collective-permute-start(bf16[2,128,512]{2,1,0:T(8,128)(2,1)} %get-tuple-element.65), channel_id=1, source_target_pairs={{0,2},{1,3},{2,0},{3,1},{4,6},{5,7},{6,4},{7,5},{8,10},{9,11},{10,... | collective-permute-start | bytes 786440 | tf_op jit(solution)/shard_map/ppermute | solution.py:27
  57.9 15.0 %collective-permute-start.8 = (bf16[2,128,512]{2,1,0:T(8,128)(2,1)}, bf16[2,128,512]{2,1,0:T(8,128)(2,1)}, u32[]{:S(2)}, u32[]{:S(2)}) collective-permute-start(bf16[2,128,512]{2,1,0:T(8,128)(2,1)} %get-tuple-element.66), channel_id=1, source_target_pairs={{0,1},{1,2},{2,3},{3,0},{4,5},{5,6},{6,7},{7,4},{8,9},{9,10},{10,1... | collective-permute-start | bytes 786440 | tf_op jit(solution)/shard_map/ppermute | solution.py:27
  75.6 10.2 %collective-permute-start.11 = (bf16[320,512]{1,0:T(8,128)(2,1)}, bf16[320,512]{1,0:T(8,128)(2,1)S(1)}, u32[]{:S(2)}, u32[]{:S(2)}) collective-permute-start(bf16[320,512]{1,0:T(8,128)(2,1)} %get-tuple-element.43.refs_0_), channel_id=1, source_target_pairs={{0,1},{1,2},{2,3},{3,0},{4,5},{5,6},{6,7},{7,4},{8,9},{9,10},{10,1... | collective-permute-start | bytes 983048 | tf_op jit(solution)/shard_map/ppermute | solution.py:27
  75.6 10.2 %collective-permute-start.15 = (bf16[320,512]{1,0:T(8,128)(2,1)}, bf16[320,512]{1,0:T(8,128)(2,1)S(1)}, u32[]{:S(2)}, u32[]{:S(2)}) collective-permute-start(bf16[320,512]{1,0:T(8,128)(2,1)} %get-tuple-element.46.refs_4_), channel_id=1, source_target_pairs={{0,3},{1,0},{2,1},{3,2},{4,7},{5,4},{6,5},{7,6},{8,11},{9,8},{10,9... | collective-permute-start | bytes 983048 | tf_op jit(solution)/shard_map/ppermute | solution.py:27
  78.3 13.6 %collective-permute-start.12 = (bf16[320,512]{1,0:T(8,128)(2,1)}, bf16[320,512]{1,0:T(8,128)(2,1)S(1)}, u32[]{:S(2)}, u32[]{:S(2)}) collective-permute-start(bf16[320,512]{1,0:T(8,128)(2,1)} %get-tuple-element.43.refs_0_), channel_id=1, source_target_pairs={{0,3},{1,0},{2,1},{3,2},{4,7},{5,4},{6,5},{7,6},{8,11},{9,8},{10,9... | collective-permute-start | bytes 983048 | tf_op jit(solution)/shard_map/ppermute | solution.py:27
  78.4 15.2 %collective-permute-start.17 = (bf16[2048,128]{1,0:T(8,128)(2,1)}, bf16[2048,128]{1,0:T(8,128)(2,1)S(1)}, u32[]{:S(2)}, u32[]{:S(2)}) collective-permute-start(bf16[2048,128]{1,0:T(8,128)(2,1)} %dynamic-slice_bitcast_fusion), channel_id=1, source_target_pairs={{0,4},{4,0},{1,5},{5,1},{2,6},{6,2},{3,7},{7,3},{8,12},{12,8},{9,1... | collective-permute-start | bytes 1572872 | tf_op jit(solution)/shard_map/ppermute | solution.py:31
  80.4 13.3 %collective-permute-start.14 = (bf16[320,512]{1,0:T(8,128)(2,1)}, bf16[320,512]{1,0:T(8,128)(2,1)S(1)}, u32[]{:S(2)}, u32[]{:S(2)}) collective-permute-start(bf16[320,512]{1,0:T(8,128)(2,1)} %get-tuple-element.46.refs_4_), channel_id=1, source_target_pairs={{0,1},{1,2},{2,3},{3,0},{4,5},{5,6},{6,7},{7,4},{8,9},{9,10},{10,1... | collective-permute-start | bytes 983048 | tf_op jit(solution)/shard_map/ppermute | solution.py:27
  85.8 14.0 %collective-permute-start.13 = (bf16[320,512]{1,0:T(8,128)(2,1)S(1)}, bf16[320,512]{1,0:T(8,128)(2,1)S(1)}, u32[]{:S(2)}, u32[]{:S(2)}) collective-permute-start(bf16[320,512]{1,0:T(8,128)(2,1)S(1)} %collective-permute-done.11.refs_1_), channel_id=1, source_target_pairs={{0,1},{1,2},{2,3},{3,0},{4,5},{5,6},{6,7},{7,4},{8,9},{9,10},{10,1... | collective-permute-start | bytes 983048 | tf_op jit(solution)/shard_map/ppermute | solution.py:27
  85.8 14.0 %collective-permute-start.16 = (bf16[320,512]{1,0:T(8,128)(2,1)S(1)}, bf16[320,512]{1,0:T(8,128)(2,1)S(1)}, u32[]{:S(2)}, u32[]{:S(2)}) collective-permute-start(bf16[320,512]{1,0:T(8,128)(2,1)S(1)} %collective-permute-done.15.refs_6_), channel_id=1, source_target_pairs={{0,3},{1,0},{2,1},{3,2},{4,7},{5,4},{6,5},{7,6},{8,11},{9,8},{10,9... | collective-permute-start | bytes 983048 | tf_op jit(solution)/shard_map/ppermute | solution.py:27
  91.9 17.2 %collective-permute-start.21 = (bf16[4,128,512]{2,1,0:T(8,128)(2,1)}, bf16[4,128,512]{2,1,0:T(8,128)(2,1)S(1)}, u32[]{:S(2)}, u32[]{:S(2)}) collective-permute-start(bf16[4,128,512]{2,1,0:T(8,128)(2,1)} %pad_maximum_fusion), channel_id=1, source_target_pairs={{0,4},{4,0},{1,5},{5,1},{2,6},{6,2},{3,7},{7,3},{8,12},{12,8},{9,1... | collective-permute-start | bytes 1572872 | tf_op jit(solution)/shard_map/ppermute | solution.py:31
  105.4 9.1 %collective-permute-start.18 = (bf16[640,256]{1,0:T(8,128)(2,1)S(1)}, bf16[640,256]{1,0:T(8,128)(2,1)S(1)}, u32[]{:S(2)}, u32[]{:S(2)}) collective-permute-start(bf16[640,256]{1,0:T(8,128)(2,1)S(1)} %gate_up.1.a0), channel_id=1, source_target_pairs={{0,1},{1,2},{2,3},{3,0},{4,5},{5,6},{6,7},{7,4},{8,9},{9,10},{10,1... | collective-permute-start | bytes 983048 | tf_op jit(solution)/shard_map/ppermute | solution.py:27
  105.5 16.6 %collective-permute-start.19 = (bf16[640,256]{1,0:T(8,128)(2,1)S(1)}, bf16[640,256]{1,0:T(8,128)(2,1)S(1)}, u32[]{:S(2)}, u32[]{:S(2)}) collective-permute-start(bf16[640,256]{1,0:T(8,128)(2,1)S(1)} %gate_up.1.a0), channel_id=1, source_target_pairs={{0,2},{1,3},{2,0},{3,1},{4,6},{5,7},{6,4},{7,5},{8,10},{9,11},{10,... | collective-permute-start | bytes 983048 | tf_op jit(solution)/shard_map/ppermute | solution.py:27
  109.0 13.9 %collective-permute-start.20 = (bf16[640,256]{1,0:T(8,128)(2,1)S(1)}, bf16[640,256]{1,0:T(8,128)(2,1)S(1)}, u32[]{:S(2)}, u32[]{:S(2)}) collective-permute-start(bf16[640,256]{1,0:T(8,128)(2,1)S(1)} %gate_up.1.a0), channel_id=1, source_target_pairs={{0,3},{1,0},{2,1},{3,2},{4,7},{5,4},{6,5},{7,6},{8,11},{9,8},{10,9... | collective-permute-start | bytes 983048 | tf_op jit(solution)/shard_map/ppermute | solution.py:27
  126.9 32.3 %all-to-all-start.1 = ((bf16[32,20,512]{2,1,0:T(8,128)(2,1)}), bf16[32,20,512]{2,1,0:T(8,128)(2,1)S(1)}, u32[]{:S(2)}, u32[]{:S(2)}) async-start(bf16[32,20,512]{2,1,0:T(8,128)(2,1)} %down.1), calls=%async_computation.1 | async-start | bytes 1572864 | tf_op jit(solution)/shard_map/all_to_all | solution.py:453
  136.6 46.5 %copy-start.22 = (s32[32,3]{0,1:T(4,128)S(1)}, s32[32,3]{0,1:T(4,128)}, u32[]{:S(2)}) copy-start(s32[32,3]{0,1:T(4,128)} %param.16) | copy-start | bytes 1156
  136.6 46.9 %copy-start.24 = (s32[1,16]{1,0:T(1,128)S(1)}, s32[1,16]{1,0:T(1,128)}, u32[]{:S(2)}) copy-start(s32[1,16]{1,0:T(1,128)} %param.29) | copy-start | bytes 196
  136.6 50.4 %copy-start.23 = (s32[1,1024]{1,0:T(1,128)S(1)}, s32[1,1024]{1,0:T(1,128)}, u32[]{:S(2)}) copy-start(s32[1,1024]{1,0:T(1,128)} %param.28) | copy-start | bytes 12292
  137.0 4.7 %collective-permute-start.5 = (f32[128,128]{0,1:T(8,128)S(1)}, f32[128,128]{0,1:T(8,128)S(1)}, u32[]{:S(2)}, u32[]{:S(2)}) collective-permute-start(f32[128,128]{0,1:T(8,128)S(1)} %pad_maximum_fusion.1), channel_id=1, source_target_pairs={{0,1},{1,2},{2,3},{3,0},{4,5},{5,6},{6,7},{7,4},{8,9},{9,10},{10,1... | collective-permute-start | bytes 196616 | tf_op jit(solution)/shard_map/ppermute | solution.py:27
  137.1 6.7 %collective-permute-start.6 = (f32[128,128]{0,1:T(8,128)S(1)}, f32[128,128]{0,1:T(8,128)S(1)}, u32[]{:S(2)}, u32[]{:S(2)}) collective-permute-start(f32[128,128]{0,1:T(8,128)S(1)} %pad_maximum_fusion.1), channel_id=1, source_target_pairs={{0,2},{1,3},{2,0},{3,1},{4,6},{5,7},{6,4},{7,5},{8,10},{9,11},{10,... | collective-permute-start | bytes 196616 | tf_op jit(solution)/shard_map/ppermute | solution.py:27
  140.3 3.6 %collective-permute-start.7 = (f32[128,128]{0,1:T(8,128)S(1)}, f32[128,128]{0,1:T(8,128)S(1)}, u32[]{:S(2)}, u32[]{:S(2)}) collective-permute-start(f32[128,128]{0,1:T(8,128)S(1)} %pad_maximum_fusion.1), channel_id=1, source_target_pairs={{0,3},{1,0},{2,1},{3,2},{4,7},{5,4},{6,5},{7,6},{8,11},{9,8},{10,9... | collective-permute-start | bytes 196616 | tf_op jit(solution)/shard_map/ppermute | solution.py:27
  160.1 5.4 %collective-permute-start.22 = (bf16[128,512]{1,0:T(8,128)(2,1)S(1)}, bf16[128,512]{1,0:T(8,128)(2,1)S(1)}, u32[]{:S(2)}, u32[]{:S(2)}) collective-permute-start(bf16[128,512]{1,0:T(8,128)(2,1)S(1)} %fusion.1.moe_ref), channel_id=1, source_target_pairs={{0,4},{4,0},{1,5},{5,1},{2,6},{6,2},{3,7},{7,3},{8,12},{12,8},{9,1... | collective-permute-start | bytes 393224 | tf_op jit(solution)/shard_map/ppermute | solution.py:31
  168.3 4.6 %collective-permute-start.23 = (f32[136,128]{1,0:T(8,128)}, f32[136,128]{1,0:T(8,128)S(1)}, u32[]{:S(2)}, u32[]{:S(2)}) collective-permute-start(f32[136,128]{1,0:T(8,128)} %get-tuple-element.50.p0), channel_id=1, source_target_pairs={{0,1},{1,2},{2,3},{3,0},{4,5},{5,6},{6,7},{7,4},{8,9},{9,10},{10,1... | collective-permute-start | bytes 208904 | tf_op jit(solution)/shard_map/ppermute | solution.py:27
  168.3 5.9 %collective-permute-start.24 = (f32[136,128]{1,0:T(8,128)}, f32[136,128]{1,0:T(8,128)S(1)}, u32[]{:S(2)}, u32[]{:S(2)}) collective-permute-start(f32[136,128]{1,0:T(8,128)} %get-tuple-element.50.p0), channel_id=1, source_target_pairs={{0,2},{1,3},{2,0},{3,1},{4,6},{5,7},{6,4},{7,5},{8,10},{9,11},{10,... | collective-permute-start | bytes 208904 | tf_op jit(solution)/shard_map/ppermute | solution.py:27
  171.6 3.7 %collective-permute-start.25 = (f32[136,128]{1,0:T(8,128)}, f32[136,128]{1,0:T(8,128)S(1)}, u32[]{:S(2)}, u32[]{:S(2)}) collective-permute-start(f32[136,128]{1,0:T(8,128)} %get-tuple-element.50.p0), channel_id=1, source_target_pairs={{0,3},{1,0},{2,1},{3,2},{4,7},{5,4},{6,5},{7,6},{8,11},{9,8},{10,9... | collective-permute-start | bytes 208904 | tf_op jit(solution)/shard_map/ppermute | solution.py:27
  177.9 19.7 %all-to-all-start.2 = ((bf16[16,128,128]{2,1,0:T(8,128)(2,1)}), bf16[16,128,128]{2,1,0:T(8,128)(2,1)S(1)}, u32[]{:S(2)}, u32[]{:S(2)}) async-start(bf16[16,128,128]{2,1,0:T(8,128)(2,1)} %vectors.1), calls=%async_computation.2 | async-start | bytes 1048576 | tf_op jit(solution)/shard_map/all_to_all | solution.py:504
  183.5 7.1 %collective-permute-start.26 = (bf16[128,512]{1,0:T(8,128)(2,1)}, bf16[128,512]{1,0:T(8,128)(2,1)S(1)}, u32[]{:S(2)}, u32[]{:S(2)}) collective-permute-start(bf16[128,512]{1,0:T(8,128)(2,1)} %get-tuple-element.54.p0), channel_id=1, source_target_pairs={{0,1},{1,2},{2,3},{3,0},{4,5},{5,6},{6,7},{7,4},{8,9},{9,10},{10,1... | collective-permute-start | bytes 393224 | tf_op jit(solution)/shard_map/ppermute | solution.py:27
  183.6 7.1 %collective-permute-start.27 = (bf16[128,512]{1,0:T(8,128)(2,1)}, bf16[128,512]{1,0:T(8,128)(2,1)S(1)}, u32[]{:S(2)}, u32[]{:S(2)}) collective-permute-start(bf16[128,512]{1,0:T(8,128)(2,1)} %get-tuple-element.54.p0), channel_id=1, source_target_pairs={{0,2},{1,3},{2,0},{3,1},{4,6},{5,7},{6,4},{7,5},{8,10},{9,11},{10,... | collective-permute-start | bytes 393224 | tf_op jit(solution)/shard_map/ppermute | solution.py:27
  185.4 5.7 %collective-permute-start.28 = (bf16[128,512]{1,0:T(8,128)(2,1)}, bf16[128,512]{1,0:T(8,128)(2,1)S(1)}, u32[]{:S(2)}, u32[]{:S(2)}) collective-permute-start(bf16[128,512]{1,0:T(8,128)(2,1)} %get-tuple-element.54.p0), channel_id=1, source_target_pairs={{0,3},{1,0},{2,1},{3,2},{4,7},{5,4},{6,5},{7,6},{8,11},{9,8},{10,9... | collective-permute-start | bytes 393224 | tf_op jit(solution)/shard_map/ppermute | solution.py:27
  190.7 11.0 %copy-start.16 = (bf16[128,512]{1,0:T(8,128)(2,1)}, bf16[128,512]{1,0:T(8,128)(2,1)S(1)}, u32[]{:S(2)}) copy-start(bf16[128,512]{1,0:T(8,128)(2,1)S(1)} %collective-permute-done.26.p1) | copy-start | bytes 393220
  190.7 11.0 %copy-start.17 = (bf16[128,512]{1,0:T(8,128)(2,1)}, bf16[128,512]{1,0:T(8,128)(2,1)S(1)}, u32[]{:S(2)}) copy-start(bf16[128,512]{1,0:T(8,128)(2,1)S(1)} %collective-permute-done.27.p2) | copy-start | bytes 393220
  191.1 10.5 %copy-start.18 = (bf16[128,512]{1,0:T(8,128)(2,1)}, bf16[128,512]{1,0:T(8,128)(2,1)S(1)}, u32[]{:S(2)}) copy-start(bf16[128,512]{1,0:T(8,128)(2,1)S(1)} %collective-permute-done.28.p3) | copy-start | bytes 393220
  197.6 6.0 %copy-start.12 = (bf16[16,128,128]{2,1,0:T(8,128)(2,1)}, bf16[16,128,128]{2,1,0:T(8,128)(2,1)S(1)}, u32[]{:S(2)}) copy-start(bf16[16,128,128]{2,1,0:T(8,128)(2,1)S(1)} %all-to-all-done.2) | copy-start | bytes 1572868
  197.6 6.0 %collective-permute-start.29 = (bf16[2048,128]{1,0:T(8,128)(2,1)S(1)}, bf16[2048,128]{1,0:T(8,128)(2,1)S(1)}, u32[]{:S(2)}, u32[]{:S(2)}) collective-permute-start(bf16[2048,128]{1,0:T(8,128)(2,1)S(1)} %bitcast.34), channel_id=1, source_target_pairs={{0,8},{8,0},{1,9},{9,1},{2,10},{10,2},{3,11},{11,3},{4,12},{12,4},... | collective-permute-start | bytes 1572872 | tf_op jit(solution)/shard_map/ppermute | solution.py:518
  (10 other events, 15.4 us)

commit v10 on v7

--- a/solution.py
+++ b/solution.py
@@ -39,10 +39,12 @@
     x_hbm,
     w_hbm,
     out_hbm,
+    gate_hbm,
     out0,
     out1,
     out2,
     out3,
+    sent_ref,
     x_ref,
     w_ref,
     out_w_ref,
@@ -53,6 +55,7 @@
         pltpu.make_async_copy(w_hbm.at[part], w_ref.at[part], sems.at[1 + part]) for part in range(3)
     ]
     copies += [pltpu.make_async_copy(out_hbm, out_w_ref, sems.at[4])]
+    copies += [pltpu.make_async_copy(gate_hbm.at[1 - here_ref[0]], sent_ref, sems.at[5])]
     for copy in copies:
         copy.start()
     wide = here_ref[2]
@@ -107,6 +110,7 @@
         part = lax.rem(j + k, 4)
         columns = pl.ds(pl.multiple_of(part * 512, 512), 512)
         out_ref[...] = jnp.dot(mixed, out_w_ref[:, columns], preferred_element_type=f32).astype(bf16)
+    copies[5].wait()
 
 
 def choose_kernel(here_ref, routes_ref, out_ref):
@@ -294,8 +298,12 @@
     return pl.BlockSpec(memory_space=pltpu.HBM)
 
 
+def anywhere():
+    return pl.BlockSpec(memory_space=pl.ANY)
+
+
 def params():
-    return pltpu.CompilerParams(vmem_limit_bytes=40 << 20)
+    return pltpu.CompilerParams(vmem_limit_bytes=16 << 20)
 
 
 def body(
@@ -327,19 +335,19 @@
     def cut(array, part, axis):
         return lax.dynamic_slice_in_dim(array, lax.rem(part, 4) * 512, 512, axis)
 
-    gate_sent, tokens = lax.optimization_barrier((pick(w_gate, 1 - i), tokens))
-    gate_par = x_swap(gate_sent)
-
-    attn = pl.pallas_call(
+    *attn, gate_sent = pl.pallas_call(
         attention_kernel,
-        out_shape=(jax.ShapeDtypeStruct((TOK, 512), bf16),) * 4,
-        in_specs=[smem()] * 2 + [vmem()] * 2 + [hbm()] * 3,
-        out_specs=(vmem(),) * 4,
+        out_shape=(
+            *(jax.ShapeDtypeStruct((TOK, 512), bf16),) * 4,
+            jax.ShapeDtypeStruct((2048, 128), bf16),
+        ),
+        in_specs=[smem()] * 2 + [vmem()] * 2 + [hbm()] * 4,
+        out_specs=(vmem(),) * 5,
         scratch_shapes=[
             pltpu.VMEM((TOK, 2048), bf16),
             pltpu.VMEM((3, 2048, 256), bf16),
             pltpu.VMEM((256, 2048), bf16),
-            pltpu.SemaphoreType.DMA((5,)),
+            pltpu.SemaphoreType.DMA((6,)),
         ],
         compiler_params=pltpu.CompilerParams(vmem_limit_bytes=60 << 20),
         name="attention",
@@ -351,7 +359,9 @@
         tokens,
         w_qkv.transpose(1, 0, 2),
         w_out,
+        w_gate,
     )
+    gate_par = x_swap(gate_sent)
     attn_parts = [y_shift(attn[k], k) for k in (1, 2, 3)]
 
     downs = [cut(w_down, j, 2)] + [y_shift(cut(w_down, j + k, 2), k) for k in (1, 2, 3)]
@@ -407,7 +417,7 @@
     act = pl.pallas_call(
         gate_up_kernel,
         out_shape=jax.ShapeDtypeStruct((2 * HALF, 256), bf16),
-        in_specs=[smem()] + [vmem()] * 8 + [hbm()] * 5,
+        in_specs=[smem()] + [vmem()] * 8 + [anywhere()] * 5,
         out_specs=vmem(),
         scratch_shapes=[
             pltpu.VMEM((3, 2048), f32),
@@ -429,7 +439,7 @@
     out = pl.pallas_call(
         down_kernel,
         out_shape=jax.ShapeDtypeStruct((WIDE, CAP, 512), bf16),
-        in_specs=[smem()] + [vmem()] * 4 + [hbm()] * 5,
+        in_specs=[smem()] + [vmem()] * 4 + [anywhere()] * 5,
         out_specs=vmem(),
         scratch_shapes=[pltpu.VMEM((4, 256, 512), bf16), pltpu.SemaphoreType.DMA((2, 4))],
         compiler_params=params(),
@@ -473,6 +483,7 @@
         ),
         in_specs=[smem()] + [vmem()] * 5,
         out_specs=(vmem(), vmem()),
+        compiler_params=params(),
         name="embed",
     )(here, hidden, moe, moe_par, norm_gains, w_proj)
     parts = [part] + [y_shift(part, k) for k in (1, 2, 3)]
@@ -482,6 +493,7 @@
         out_shape=jax.ShapeDtypeStruct((16, TOK, 128), bf16),
         in_specs=[vmem()] * 4,
         out_specs=vmem(),
+        compiler_params=params(),
         name="vectors",
     )(*parts)
     vectors, layer = lax.optimization_barrier((vectors, layer))
@@ -506,14 +518,16 @@
         out_shape=jax.ShapeDtypeStruct((TOK, 2048), bf16),
         in_specs=[smem()] + [vmem()] * 4,
         out_specs=vmem(),
+        compiler_params=params(),
         name="assemble",
     )(here, *layers)
     doc_scores = pl.pallas_call(
         score_kernel,
         out_shape=jax.ShapeDtypeStruct((1, 16), f32),
-        in_specs=[smem(), vmem()] + [pl.BlockSpec(memory_space=pl.ANY)] * 2,
+        in_specs=[smem(), vmem()] + [anywhere()] * 2,
         out_specs=vmem(),
         scratch_shapes=[pltpu.VMEM((16, 128, 128), bf16), pltpu.SemaphoreType.DMA((16,))],
+        compiler_params=params(),
         name="score",
     )(info, doc_vectors, own, other)
     return (layer_out, doc_scores)

time: 188 us -> 182 us (0.968)
  local copies, waits for them, and re-layouts: 12.9 us -> 9 us
  Pallas kernels: 23.7 us -> 20.9 us
    unnamed x47 -> x29, local copies, waits for them, and re-layouts: 3.3 us -> 1.2 us
  transfers between devices with their start and end apart: 33 -> 33, of which waited for: 20 -> 20; matrix products, arithmetic and copies ran while one was open for 6% -> 6% of each run, Pallas kernels for 6% -> 3%
where the time goes in v10:
time: 182 us; the launch traced here: 181 us
  waiting for transfers between devices  77.6 us (43%)
  starting transfers between devices  68 us (37%)
  Pallas kernels  20.9 us (11%)
  local copies, waits for them, and re-layouts  9 us (5%)
  other arithmetic  3.37 us (2%)
    ppermute x24, waiting for transfers between devices, y_shift(): return lax.ppermute(x, 'y', [(s, (s + k) % 4) for s in range(4)])  35.4 us
    ppermute x24, starting transfers between devices, y_shift(): return lax.ppermute(x, 'y', [(s, (s + k) % 4) for s in range(4)])  30.3 us
    all_to_all x1, waiting for transfers between devices, body(): back = lax.all_to_all(out, W, 0, 0, tiled=True)  15.2 us
    all_to_all x1, starting transfers between devices, body(): arrived = lax.all_to_all(rows, W, 0, 0, tiled=True)  11.6 us
    all_to_all x1, waiting for transfers between devices, body(): arrived = lax.all_to_all(rows, W, 0, 0, tiled=True)  11.5 us
    ppermute x5, starting transfers between devices, x_swap(): return lax.ppermute(x, 'xh', [(0, 1), (1, 0)])  9.11 us
    ppermute x5, waiting for transfers between devices, x_swap(): return lax.ppermute(x, 'xh', [(0, 1), (1, 0)])  8.92 us
    all_to_all x1, starting transfers between devices, body(): back = lax.all_to_all(out, W, 0, 0, tiled=True)  7.69 us
  transfers between devices with their start and end apart: 33, of which 20 were waited for; matrix products, arithmetic and copies ran while one was open for 6% of the time, Pallas kernels for 3%

profile of v10, /device:TPU:1, one launch (start us, length us, event | category | flops | bytes accessed | tf_op | source)
XLA Modules:
  0.0 181.3 jit_solution(10805970428353398188)
XLA Ops:
  1.3 5.5 %attention.1 = (bf16[128,512]{1,0:T(8,128)(2,1)}, bf16[128,512]{1,0:T(8,128)(2,1)}, bf16[128,512]{1,0:T(8,128)(2,1)}, bf16[128,512]{1,0:T(8,128)(2,1)}, bf16[2048,128]{1,0:T(8,128)(2,1)}) custom-call(s32[4]{0:T(128)} %pad_add_fusion.here_ref, s32[3,32]{1,0:T(4,128)} %bitcast.37, f32[2,256]{1,0:T(2,128)} %qk_ref.1, f32[3,2048]{1,0:T(4,128)} %gain_ref.3, ...), custom_call_target="tpu_custom_call" | custom-call | tf_op jit(solution)/shard_map/attention/pallas_call | solution.py:338
  6.8 3.7 %collective-permute-start.4 = (bf16[2048,128]{1,0:T(8,128)(2,1)}, bf16[2048,128]{1,0:T(8,128)(2,1)S(1)}, u32[]{:S(2)}, u32[]{:S(2)}) collective-permute-start(bf16[2048,128]{1,0:T(8,128)(2,1)} %get-tuple-element.33), channel_id=1, source_target_pairs={{0,4},{4,0},{1,5},{5,1},{2,6},{6,2},{3,7},{7,3},{8,12},{12,8},{9,1... | collective-permute-start | bytes 1572872 | tf_op jit(solution)/shard_map/ppermute | solution.py:31
  10.5 1.3 collective-permute-start
  11.8 2.6 %collective-permute-start.1 = (bf16[128,512]{1,0:T(8,128)(2,1)}, bf16[128,512]{1,0:T(8,128)(2,1)S(1)}, u32[]{:S(2)}, u32[]{:S(2)}) collective-permute-start(bf16[128,512]{1,0:T(8,128)(2,1)} %get-tuple-element.30), channel_id=1, source_target_pairs={{0,2},{1,3},{2,0},{3,1},{4,6},{5,7},{6,4},{7,5},{8,10},{9,11},{10,... | collective-permute-start | bytes 393224 | tf_op jit(solution)/shard_map/ppermute | solution.py:27
  14.4 1.1 collective-permute-start.2
  16.3 3.6 %collective-permute-done.1 = bf16[128,512]{1,0:T(8,128)(2,1)S(1)} collective-permute-done((bf16[128,512]{1,0:T(8,128)(2,1)}, bf16[128,512]{1,0:T(8,128)(2,1)S(1)}, u32[]{:S(2)}, u32[]{:S(2)}) %collective-permute-start.1) | collective-permute-done | bytes 131104 | tf_op jit(solution)/shard_map/ppermute | solution.py:27
  20.0 1.0 add_convert_fusion.own_ref
  21.1 5.3 %collective-permute-done.3.par_ref = bf16[128,512]{1,0:T(8,128)(2,1)S(1)} collective-permute-done((bf16[128,512]{1,0:T(8,128)(2,1)S(1)}, bf16[128,512]{1,0:T(8,128)(2,1)S(1)}, u32[]{:S(2)}, u32[]{:S(2)}) %collective-permute-start.3) | collective-permute-done | bytes 131104 | tf_op jit(solution)/shard_map/ppermute | solution.py:31
  26.4 1.7 dispatch.1
  28.2 11.6 %all-to-all-start = ((bf16[32,40,256]{2,1,0:T(8,128)(2,1)}), bf16[32,40,256]{2,1,0:T(8,128)(2,1)S(1)}, u32[]{:S(2)}, u32[]{:S(2)}) async-start(bf16[32,40,256]{2,1,0:T(8,128)(2,1)} %get-tuple-element.37), calls=%async_computation | async-start | bytes 1310720 | tf_op jit(solution)/shard_map/all_to_all | solution.py:402
  39.9 2.2 %constant_dynamic-slice_fusion.4 = (bf16[2,128,512]{2,1,0:T(8,128)(2,1)}, bf16[2,128,512]{2,1,0:T(8,128)(2,1)}, bf16[2,128,512]{2,1,0:T(8,128)(2,1)}, bf16[2,128,512]{2,1,0:T(8,128)(2,1)S(1)}) fusion(bf16[2,128,2048]{2,1,0:T(8,128)(2,1)} %param.25, s32[]{:T(128)S(6)} %select_n.66, s32[]{:T(128)S(6)} %select_n.65, s32[]{:T(128)S(6)} %select_n.64, s32[]{:T(128)S(6)} %select_n.63), kind=kLoop, calls=%fused_computation.57 | loop fusion | bytes 2097168 | tf_op jit(solution)/shard_map/dynamic_slice | solution.py:336
  42.1 2.0 %collective-permute-start.20 = (bf16[2,128,512]{2,1,0:T(8,128)(2,1)}, bf16[2,128,512]{2,1,0:T(8,128)(2,1)}, u32[]{:S(2)}, u32[]{:S(2)}) collective-permute-start(bf16[2,128,512]{2,1,0:T(8,128)(2,1)} %get-tuple-element.58), channel_id=1, source_target_pairs={{0,3},{1,0},{2,1},{3,2},{4,7},{5,4},{6,5},{7,6},{8,11},{9,8},{10,9... | collective-permute-start | bytes 786440 | tf_op jit(solution)/shard_map/ppermute | solution.py:27
  45.2 1.7 constant_dynamic-slice_fusion.3
  47.9 11.5 %all-to-all-done.in_ref = bf16[32,40,256]{2,1,0:T(8,128)(2,1)S(1)} async-done(((bf16[32,40,256]{2,1,0:T(8,128)(2,1)}), bf16[32,40,256]{2,1,0:T(8,128)(2,1)S(1)}, u32[]{:S(2)}, u32[]{:S(2)}) %all-to-all-start) | async-done | bytes 655392 | tf_op jit(solution)/shard_map/all_to_all | solution.py:402
  60.5 1.8 collective-permute-start.12
  63.3 1.8 %collective-permute-start.14 = (bf16[2048,128]{1,0:T(8,128)(2,1)}, bf16[2048,128]{1,0:T(8,128)(2,1)S(1)}, u32[]{:S(2)}, u32[]{:S(2)}) collective-permute-start(bf16[2048,128]{1,0:T(8,128)(2,1)} %dynamic-slice_bitcast_fusion), channel_id=1, source_target_pairs={{0,4},{4,0},{1,5},{5,1},{2,6},{6,2},{3,7},{7,3},{8,12},{12,8},{9,1... | collective-permute-start | bytes 1572872 | tf_op jit(solution)/shard_map/ppermute | solution.py:31
  67.0 2.8 %collective-permute-start.9 = (bf16[320,512]{1,0:T(8,128)(2,1)S(1)}, bf16[320,512]{1,0:T(8,128)(2,1)S(1)}, u32[]{:S(2)}, u32[]{:S(2)}) collective-permute-start(bf16[320,512]{1,0:T(8,128)(2,1)S(1)} %get-tuple-element.40.refs_0_), channel_id=1, source_target_pairs={{0,3},{1,0},{2,1},{3,2},{4,7},{5,4},{6,5},{7,6},{8,11},{9,8},{10,9... | collective-permute-start | bytes 983048 | tf_op jit(solution)/shard_map/ppermute | solution.py:27
  69.8 2.7 %collective-permute-start.13 = (bf16[320,512]{1,0:T(8,128)(2,1)S(1)}, bf16[320,512]{1,0:T(8,128)(2,1)S(1)}, u32[]{:S(2)}, u32[]{:S(2)}) collective-permute-start(bf16[320,512]{1,0:T(8,128)(2,1)S(1)} %collective-permute-done.12.refs_6_), channel_id=1, source_target_pairs={{0,3},{1,0},{2,1},{3,2},{4,7},{5,4},{6,5},{7,6},{8,11},{9,8},{10,9... | collective-permute-start | bytes 983048 | tf_op jit(solution)/shard_map/ppermute | solution.py:27
  72.5 1.0 pad_maximum_fusion
  73.5 2.2 %collective-permute-done.11.refs_5_ = bf16[320,512]{1,0:T(8,128)(2,1)S(1)} collective-permute-done((bf16[320,512]{1,0:T(8,128)(2,1)S(1)}, bf16[320,512]{1,0:T(8,128)(2,1)S(1)}, u32[]{:S(2)}, u32[]{:S(2)}) %collective-permute-start.11) | collective-permute-done | bytes 327712 | tf_op jit(solution)/shard_map/ppermute | solution.py:27
  75.7 1.7 collective-permute-start.21
  77.5 5.3 %collective-permute-done.10.refs_3_ = bf16[320,512]{1,0:T(8,128)(2,1)S(1)} collective-permute-done((bf16[320,512]{1,0:T(8,128)(2,1)S(1)}, bf16[320,512]{1,0:T(8,128)(2,1)S(1)}, u32[]{:S(2)}, u32[]{:S(2)}) %collective-permute-start.10) | collective-permute-done | bytes 327712 | tf_op jit(solution)/shard_map/ppermute | solution.py:27
  82.8 1.0 copy-done.5
  83.8 3.0 %gate_up.1.a0 = bf16[640,256]{1,0:T(8,128)(2,1)S(1)} custom-call(s32[4]{0:T(128)S(1)} %copy-done.10, bf16[320,512]{1,0:T(8,128)(2,1)S(1)} %get-tuple-element.40.refs_0_, bf16[320,512]{1,0:T(8,128)(2,1)S(1)} %collective-permute-done.8.refs_1_, bf16[320,512]{1,0:T(8,128)(2,1)S(1)} %collective-permute-done.9.refs_2_, ...), custom_call_target="tpu_custom_call" | custom-call | tf_op jit(solution)/shard_map/gate_up/pallas_call | solution.py:417
  87.2 2.9 %collective-permute-start.16 = (bf16[640,256]{1,0:T(8,128)(2,1)S(1)}, bf16[640,256]{1,0:T(8,128)(2,1)S(1)}, u32[]{:S(2)}, u32[]{:S(2)}) collective-permute-start(bf16[640,256]{1,0:T(8,128)(2,1)S(1)} %gate_up.1.a0), channel_id=1, source_target_pairs={{0,2},{1,3},{2,0},{3,1},{4,6},{5,7},{6,4},{7,5},{8,10},{9,11},{10,... | collective-permute-start | bytes 983048 | tf_op jit(solution)/shard_map/ppermute | solution.py:27
  90.5 4.3 %collective-permute-done.15.a1 = bf16[640,256]{1,0:T(8,128)(2,1)S(1)} collective-permute-done((bf16[640,256]{1,0:T(8,128)(2,1)S(1)}, bf16[640,256]{1,0:T(8,128)(2,1)S(1)}, u32[]{:S(2)}, u32[]{:S(2)}) %collective-permute-start.15) | collective-permute-done | bytes 327712 | tf_op jit(solution)/shard_map/ppermute | solution.py:27
  94.8 6.4 %collective-permute-done.16.a2 = bf16[640,256]{1,0:T(8,128)(2,1)S(1)} collective-permute-done((bf16[640,256]{1,0:T(8,128)(2,1)S(1)}, bf16[640,256]{1,0:T(8,128)(2,1)S(1)}, u32[]{:S(2)}, u32[]{:S(2)}) %collective-permute-start.16) | collective-permute-done | bytes 327712 | tf_op jit(solution)/shard_map/ppermute | solution.py:27
  101.1 2.8 %collective-permute-done.17.a3 = bf16[640,256]{1,0:T(8,128)(2,1)S(1)} collective-permute-done((bf16[640,256]{1,0:T(8,128)(2,1)S(1)}, bf16[640,256]{1,0:T(8,128)(2,1)S(1)}, u32[]{:S(2)}, u32[]{:S(2)}) %collective-permute-start.17) | collective-permute-done | bytes 327712 | tf_op jit(solution)/shard_map/ppermute | solution.py:27
  103.9 3.7 %down.1 = bf16[32,20,512]{2,1,0:T(8,128)(2,1)} custom-call(s32[4]{0:T(128)S(1)} %copy-done.10, bf16[640,256]{1,0:T(8,128)(2,1)S(1)} %gate_up.1.a0, bf16[640,256]{1,0:T(8,128)(2,1)S(1)} %collective-permute-done.15.a1, bf16[640,256]{1,0:T(8,128)(2,1)S(1)} %collective-permute-done.16.a2, bf16[640,256]{1,0:T(8,128)(2,1)S(1)} %collective-permute-done.17.a3, ...), custom_call_target="tpu_custom_call" | custom-call | tf_op jit(solution)/shard_map/down/pallas_call | solution.py:439
  107.6 7.7 %all-to-all-start.1 = ((bf16[32,20,512]{2,1,0:T(8,128)(2,1)}), bf16[32,20,512]{2,1,0:T(8,128)(2,1)S(1)}, u32[]{:S(2)}, u32[]{:S(2)}) async-start(bf16[32,20,512]{2,1,0:T(8,128)(2,1)} %down.1), calls=%async_computation.1 | async-start | bytes 1572864 | tf_op jit(solution)/shard_map/all_to_all | solution.py:448
  116.5 2.5 %collective-permute-start.6 = (f32[128,128]{0,1:T(8,128)S(1)}, f32[128,128]{0,1:T(8,128)S(1)}, u32[]{:S(2)}, u32[]{:S(2)}) collective-permute-start(f32[128,128]{0,1:T(8,128)S(1)} %pad_maximum_fusion.1), channel_id=1, source_target_pairs={{0,2},{1,3},{2,0},{3,1},{4,6},{5,7},{6,4},{7,5},{8,10},{9,11},{10,... | collective-permute-start | bytes 196616 | tf_op jit(solution)/shard_map/ppermute | solution.py:27
  119.3 1.1 collective-permute-done.5
  120.4 2.0 %collective-permute-done.6 = f32[128,128]{0,1:T(8,128)S(1)} collective-permute-done((f32[128,128]{0,1:T(8,128)S(1)}, f32[128,128]{0,1:T(8,128)S(1)}, u32[]{:S(2)}, u32[]{:S(2)}) %collective-permute-start.6) | collective-permute-done | bytes 65568 | tf_op jit(solution)/shard_map/ppermute | solution.py:27
  122.8 15.2 %all-to-all-done.1 = bf16[32,20,512]{2,1,0:T(8,128)(2,1)S(1)} async-done(((bf16[32,20,512]{2,1,0:T(8,128)(2,1)}), bf16[32,20,512]{2,1,0:T(8,128)(2,1)S(1)}, u32[]{:S(2)}, u32[]{:S(2)}) %all-to-all-start.1) | async-done | bytes 655392 | tf_op jit(solution)/shard_map/all_to_all | solution.py:448
  138.9 1.8 collective-permute-start.22
  140.7 3.6 %collective-permute-done.22.par_ref = bf16[128,512]{1,0:T(8,128)(2,1)S(1)} collective-permute-done((bf16[128,512]{1,0:T(8,128)(2,1)S(1)}, bf16[128,512]{1,0:T(8,128)(2,1)S(1)}, u32[]{:S(2)}, u32[]{:S(2)}) %collective-permute-start.22) | collective-permute-done | bytes 131104 | tf_op jit(solution)/shard_map/ppermute | solution.py:31
  145.1 1.0 collective-permute-start.23
  146.1 2.5 %collective-permute-start.24 = (f32[136,128]{1,0:T(8,128)S(1)}, f32[136,128]{1,0:T(8,128)S(1)}, u32[]{:S(2)}, u32[]{:S(2)}) collective-permute-start(f32[136,128]{1,0:T(8,128)S(1)} %get-tuple-element.44.p0), channel_id=1, source_target_pairs={{0,2},{1,3},{2,0},{3,1},{4,6},{5,7},{6,4},{7,5},{8,10},{9,11},{10,... | collective-permute-start | bytes 208904 | tf_op jit(solution)/shard_map/ppermute | solution.py:27
  149.7 1.3 collective-permute-done.24.p2
  151.0 1.0 collective-permute-done.25.p3
  152.0 1.0 vectors.1
  153.1 5.0 %all-to-all-start.2 = ((bf16[16,128,128]{2,1,0:T(8,128)(2,1)}), bf16[16,128,128]{2,1,0:T(8,128)(2,1)S(1)}, u32[]{:S(2)}, u32[]{:S(2)}) async-start(bf16[16,128,128]{2,1,0:T(8,128)(2,1)} %vectors.1), calls=%async_computation.2 | async-start | bytes 1048576 | tf_op jit(solution)/shard_map/all_to_all | solution.py:501
  158.7 1.9 %collective-permute-start.27 = (bf16[128,512]{1,0:T(8,128)(2,1)S(1)}, bf16[128,512]{1,0:T(8,128)(2,1)S(1)}, u32[]{:S(2)}, u32[]{:S(2)}) collective-permute-start(bf16[128,512]{1,0:T(8,128)(2,1)S(1)} %get-tuple-element.48.p0), channel_id=1, source_target_pairs={{0,2},{1,3},{2,0},{3,1},{4,6},{5,7},{6,4},{7,5},{8,10},{9,11},{10,... | collective-permute-start | bytes 393224 | tf_op jit(solution)/shard_map/ppermute | solution.py:27
  161.7 3.8 %collective-permute-done.26.p1 = bf16[128,512]{1,0:T(8,128)(2,1)S(1)} collective-permute-done((bf16[128,512]{1,0:T(8,128)(2,1)S(1)}, bf16[128,512]{1,0:T(8,128)(2,1)S(1)}, u32[]{:S(2)}, u32[]{:S(2)}) %collective-permute-start.26) | collective-permute-done | bytes 131104 | tf_op jit(solution)/shard_map/ppermute | solution.py:27
  166.0 6.4 %all-to-all-done.2 = bf16[16,128,128]{2,1,0:T(8,128)(2,1)S(1)} async-done(((bf16[16,128,128]{2,1,0:T(8,128)(2,1)}), bf16[16,128,128]{2,1,0:T(8,128)(2,1)S(1)}, u32[]{:S(2)}, u32[]{:S(2)}) %all-to-all-start.2) | async-done | bytes 524320 | tf_op jit(solution)/shard_map/all_to_all | solution.py:501
  172.4 4.3 %collective-permute-start.29 = (bf16[2048,128]{1,0:T(8,128)(2,1)S(1)}, bf16[2048,128]{1,0:T(8,128)(2,1)S(1)}, u32[]{:S(2)}, u32[]{:S(2)}) collective-permute-start(bf16[2048,128]{1,0:T(8,128)(2,1)S(1)} %bitcast.31), channel_id=1, source_target_pairs={{0,8},{8,0},{1,9},{9,1},{2,10},{10,2},{3,11},{11,3},{4,12},{12,4},... | collective-permute-start | bytes 1572872 | tf_op jit(solution)/shard_map/ppermute | solution.py:515
  176.7 1.4 assemble.1
  178.2 2.9 %score.1 = f32[1,16]{1,0:T(1,128)} custom-call(s32[5,16]{1,0:T(8,128)S(1)} %stack.48.info_ref, bf16[1024,128]{1,0:T(8,128)(2,1)S(1)} %copy-done.8, bf16[2048,128]{1,0:T(8,128)(2,1)S(1)} %bitcast.32, bf16[2048,128]{1,0:T(8,128)(2,1)S(1)} %collective-permute-done.29.other_ref), custom_call_target="tpu_custom_call" | custom-call | tf_op jit(solution)/shard_map/score/pallas_call | solution.py:524
  (95 shorter events, 15.6 us)
Async XLA Ops:
  0.6 114.7 %copy-start = (bf16[2048,64]{0,1:T(8,128)(2,1)S(1)}, bf16[2048,64]{0,1:T(8,128)(2,1)}, u32[]{:S(2)}) copy-start(bf16[2048,64]{0,1:T(8,128)(2,1)} %param.21) | copy-start | bytes 786436
  0.6 14.8 %copy-start.9 = (s32[128,8]{0,1:T(8,128)S(1)}, s32[128,8]{0,1:T(8,128)}, u32[]{:S(2)}) copy-start(s32[128,8]{0,1:T(8,128)} %param.22) | copy-start | bytes 12292
  1.3 14.1 %copy-start.10 = (s32[4]{0:T(128)S(1)}, s32[4]{0:T(128)}, u32[]{:S(2)}) copy-start(s32[4]{0:T(128)} %pad_add_fusion.here_ref) | copy-start | bytes 52
  1.3 25.1 %copy-start.3 = (bf16[128,2048]{1,0:T(8,128)(2,1)S(1)}, bf16[128,2048]{1,0:T(8,128)(2,1)}, u32[]{:S(2)}) copy-start(bf16[128,2048]{1,0:T(8,128)(2,1)} %x_ref.1) | copy-start | bytes 1572868
  6.8 40.1 %copy-start.2 = (bf16[2,2048,128]{2,1,0:T(8,128)(2,1)S(1)}, bf16[2,2048,128]{2,1,0:T(8,128)(2,1)}, u32[]{:S(2)}) copy-start(bf16[2,2048,128]{2,1,0:T(8,128)(2,1)} %refs_10_.1) | copy-start | bytes 3145732
  6.8 19.6 %collective-permute-start.4 = (bf16[2048,128]{1,0:T(8,128)(2,1)}, bf16[2048,128]{1,0:T(8,128)(2,1)S(1)}, u32[]{:S(2)}, u32[]{:S(2)}) collective-permute-start(bf16[2048,128]{1,0:T(8,128)(2,1)} %get-tuple-element.33), channel_id=1, source_target_pairs={{0,4},{4,0},{1,5},{5,1},{2,6},{6,2},{3,7},{7,3},{8,12},{12,8},{9,1... | collective-permute-start | bytes 1572872 | tf_op jit(solution)/shard_map/ppermute | solution.py:31
  10.5 5.9 %collective-permute-start = (bf16[128,512]{1,0:T(8,128)(2,1)}, bf16[128,512]{1,0:T(8,128)(2,1)S(1)}, u32[]{:S(2)}, u32[]{:S(2)}) collective-permute-start(bf16[128,512]{1,0:T(8,128)(2,1)} %get-tuple-element.29), channel_id=1, source_target_pairs={{0,1},{1,2},{2,3},{3,0},{4,5},{5,6},{6,7},{7,4},{8,9},{9,10},{10,1... | collective-permute-start | bytes 393224 | tf_op jit(solution)/shard_map/ppermute | solution.py:27
  11.8 8.2 %collective-permute-start.1 = (bf16[128,512]{1,0:T(8,128)(2,1)}, bf16[128,512]{1,0:T(8,128)(2,1)S(1)}, u32[]{:S(2)}, u32[]{:S(2)}) collective-permute-start(bf16[128,512]{1,0:T(8,128)(2,1)} %get-tuple-element.30), channel_id=1, source_target_pairs={{0,2},{1,3},{2,0},{3,1},{4,6},{5,7},{6,4},{7,5},{8,10},{9,11},{10,... | collective-permute-start | bytes 393224 | tf_op jit(solution)/shard_map/ppermute | solution.py:27
  14.4 5.6 %collective-permute-start.2 = (bf16[128,512]{1,0:T(8,128)(2,1)}, bf16[128,512]{1,0:T(8,128)(2,1)S(1)}, u32[]{:S(2)}, u32[]{:S(2)}) collective-permute-start(bf16[128,512]{1,0:T(8,128)(2,1)} %get-tuple-element.31), channel_id=1, source_target_pairs={{0,3},{1,0},{2,1},{3,2},{4,7},{5,4},{6,5},{7,6},{8,11},{9,8},{10,9... | collective-permute-start | bytes 393224 | tf_op jit(solution)/shard_map/ppermute | solution.py:27
  20.0 27.9 %copy-start.7 = (f32[3,2048]{1,0:T(4,128)S(1)}, f32[3,2048]{1,0:T(4,128)}, u32[]{:S(2)}) copy-start(f32[3,2048]{1,0:T(4,128)} %gain_ref.3) | copy-start | bytes 73732
  21.0 5.4 %collective-permute-start.3 = (bf16[128,512]{1,0:T(8,128)(2,1)S(1)}, bf16[128,512]{1,0:T(8,128)(2,1)S(1)}, u32[]{:S(2)}, u32[]{:S(2)}) collective-permute-start(bf16[128,512]{1,0:T(8,128)(2,1)S(1)} %add_convert_fusion.own_ref), channel_id=1, source_target_pairs={{0,4},{4,0},{1,5},{5,1},{2,6},{6,2},{3,7},{7,3},{8,12},{12,8},{9,1... | collective-permute-start | bytes 393224 | tf_op jit(solution)/shard_map/ppermute | solution.py:31
  26.4 1.7 copy-start.4
  28.2 31.2 %all-to-all-start = ((bf16[32,40,256]{2,1,0:T(8,128)(2,1)}), bf16[32,40,256]{2,1,0:T(8,128)(2,1)S(1)}, u32[]{:S(2)}, u32[]{:S(2)}) async-start(bf16[32,40,256]{2,1,0:T(8,128)(2,1)} %get-tuple-element.37), calls=%async_computation | async-start | bytes 1310720 | tf_op jit(solution)/shard_map/all_to_all | solution.py:402
  39.8 42.9 %copy-start.1 = (bf16[2,2048,128]{2,1,0:T(8,128)(2,1)S(1)}, bf16[2,2048,128]{2,1,0:T(8,128)(2,1)}, u32[]{:S(2)}) copy-start(bf16[2,2048,128]{2,1,0:T(8,128)(2,1)} %refs_9_.1) | copy-start | bytes 3145732
  42.1 20.3 %collective-permute-start.20 = (bf16[2,128,512]{2,1,0:T(8,128)(2,1)}, bf16[2,128,512]{2,1,0:T(8,128)(2,1)}, u32[]{:S(2)}, u32[]{:S(2)}) collective-permute-start(bf16[2,128,512]{2,1,0:T(8,128)(2,1)} %get-tuple-element.58), channel_id=1, source_target_pairs={{0,3},{1,0},{2,1},{3,2},{4,7},{5,4},{6,5},{7,6},{8,11},{9,8},{10,9... | collective-permute-start | bytes 786440 | tf_op jit(solution)/shard_map/ppermute | solution.py:27
  44.1 19.3 %collective-permute-start.19 = (bf16[2,128,512]{2,1,0:T(8,128)(2,1)}, bf16[2,128,512]{2,1,0:T(8,128)(2,1)}, u32[]{:S(2)}, u32[]{:S(2)}) collective-permute-start(bf16[2,128,512]{2,1,0:T(8,128)(2,1)} %get-tuple-element.59), channel_id=1, source_target_pairs={{0,2},{1,3},{2,0},{3,1},{4,6},{5,7},{6,4},{7,5},{8,10},{9,11},{10,... | collective-permute-start | bytes 786440 | tf_op jit(solution)/shard_map/ppermute | solution.py:27
  44.7 21.4 %collective-permute-start.18 = (bf16[2,128,512]{2,1,0:T(8,128)(2,1)}, bf16[2,128,512]{2,1,0:T(8,128)(2,1)}, u32[]{:S(2)}, u32[]{:S(2)}) collective-permute-start(bf16[2,128,512]{2,1,0:T(8,128)(2,1)} %get-tuple-element.60), channel_id=1, source_target_pairs={{0,1},{1,2},{2,3},{3,0},{4,5},{5,6},{6,7},{7,4},{8,9},{9,10},{10,1... | collective-permute-start | bytes 786440 | tf_op jit(solution)/shard_map/ppermute | solution.py:27
  59.6 10.3 %collective-permute-start.8 = (bf16[320,512]{1,0:T(8,128)(2,1)S(1)}, bf16[320,512]{1,0:T(8,128)(2,1)S(1)}, u32[]{:S(2)}, u32[]{:S(2)}) collective-permute-start(bf16[320,512]{1,0:T(8,128)(2,1)S(1)} %get-tuple-element.40.refs_0_), channel_id=1, source_target_pairs={{0,1},{1,2},{2,3},{3,0},{4,5},{5,6},{6,7},{7,4},{8,9},{9,10},{10,1... | collective-permute-start | bytes 983048 | tf_op jit(solution)/shard_map/ppermute | solution.py:27
  60.5 9.3 %collective-permute-start.12 = (bf16[320,512]{1,0:T(8,128)(2,1)S(1)}, bf16[320,512]{1,0:T(8,128)(2,1)S(1)}, u32[]{:S(2)}, u32[]{:S(2)}) collective-permute-start(bf16[320,512]{1,0:T(8,128)(2,1)S(1)} %get-tuple-element.41.refs_4_), channel_id=1, source_target_pairs={{0,3},{1,0},{2,1},{3,2},{4,7},{5,4},{6,5},{7,6},{8,11},{9,8},{10,9... | collective-permute-start | bytes 983048 | tf_op jit(solution)/shard_map/ppermute | solution.py:27
  63.2 12.5 %collective-permute-start.11 = (bf16[320,512]{1,0:T(8,128)(2,1)S(1)}, bf16[320,512]{1,0:T(8,128)(2,1)S(1)}, u32[]{:S(2)}, u32[]{:S(2)}) collective-permute-start(bf16[320,512]{1,0:T(8,128)(2,1)S(1)} %get-tuple-element.41.refs_4_), channel_id=1, source_target_pairs={{0,1},{1,2},{2,3},{3,0},{4,5},{5,6},{6,7},{7,4},{8,9},{9,10},{10,1... | collective-permute-start | bytes 983048 | tf_op jit(solution)/shard_map/ppermute | solution.py:27
  63.3 14.1 %collective-permute-start.14 = (bf16[2048,128]{1,0:T(8,128)(2,1)}, bf16[2048,128]{1,0:T(8,128)(2,1)S(1)}, u32[]{:S(2)}, u32[]{:S(2)}) collective-permute-start(bf16[2048,128]{1,0:T(8,128)(2,1)} %dynamic-slice_bitcast_fusion), channel_id=1, source_target_pairs={{0,4},{4,0},{1,5},{5,1},{2,6},{6,2},{3,7},{7,3},{8,12},{12,8},{9,1... | collective-permute-start | bytes 1572872 | tf_op jit(solution)/shard_map/ppermute | solution.py:31
  67.0 10.5 %collective-permute-start.9 = (bf16[320,512]{1,0:T(8,128)(2,1)S(1)}, bf16[320,512]{1,0:T(8,128)(2,1)S(1)}, u32[]{:S(2)}, u32[]{:S(2)}) collective-permute-start(bf16[320,512]{1,0:T(8,128)(2,1)S(1)} %get-tuple-element.40.refs_0_), channel_id=1, source_target_pairs={{0,3},{1,0},{2,1},{3,2},{4,7},{5,4},{6,5},{7,6},{8,11},{9,8},{10,9... | collective-permute-start | bytes 983048 | tf_op jit(solution)/shard_map/ppermute | solution.py:27
  69.8 12.9 %collective-permute-start.10 = (bf16[320,512]{1,0:T(8,128)(2,1)S(1)}, bf16[320,512]{1,0:T(8,128)(2,1)S(1)}, u32[]{:S(2)}, u32[]{:S(2)}) collective-permute-start(bf16[320,512]{1,0:T(8,128)(2,1)S(1)} %collective-permute-done.8.refs_1_), channel_id=1, source_target_pairs={{0,1},{1,2},{2,3},{3,0},{4,5},{5,6},{6,7},{7,4},{8,9},{9,10},{10,1... | collective-permute-start | bytes 983048 | tf_op jit(solution)/shard_map/ppermute | solution.py:27
  69.8 12.9 %collective-permute-start.13 = (bf16[320,512]{1,0:T(8,128)(2,1)S(1)}, bf16[320,512]{1,0:T(8,128)(2,1)S(1)}, u32[]{:S(2)}, u32[]{:S(2)}) collective-permute-start(bf16[320,512]{1,0:T(8,128)(2,1)S(1)} %collective-permute-done.12.refs_6_), channel_id=1, source_target_pairs={{0,3},{1,0},{2,1},{3,2},{4,7},{5,4},{6,5},{7,6},{8,11},{9,8},{10,9... | collective-permute-start | bytes 983048 | tf_op jit(solution)/shard_map/ppermute | solution.py:27
  75.7 14.8 %collective-permute-start.21 = (bf16[4,128,512]{2,1,0:T(8,128)(2,1)S(1)}, bf16[4,128,512]{2,1,0:T(8,128)(2,1)S(1)}, u32[]{:S(2)}, u32[]{:S(2)}) collective-permute-start(bf16[4,128,512]{2,1,0:T(8,128)(2,1)S(1)} %pad_maximum_fusion), channel_id=1, source_target_pairs={{0,4},{4,0},{1,5},{5,1},{2,6},{6,2},{3,7},{7,3},{8,12},{12,8},{9,1... | collective-permute-start | bytes 1572872 | tf_op jit(solution)/shard_map/ppermute | solution.py:31
  82.7 1.0 copy-start.5
  86.8 8.0 %collective-permute-start.15 = (bf16[640,256]{1,0:T(8,128)(2,1)S(1)}, bf16[640,256]{1,0:T(8,128)(2,1)S(1)}, u32[]{:S(2)}, u32[]{:S(2)}) collective-permute-start(bf16[640,256]{1,0:T(8,128)(2,1)S(1)} %gate_up.1.a0), channel_id=1, source_target_pairs={{0,1},{1,2},{2,3},{3,0},{4,5},{5,6},{6,7},{7,4},{8,9},{9,10},{10,1... | collective-permute-start | bytes 983048 | tf_op jit(solution)/shard_map/ppermute | solution.py:27
  87.2 13.9 %collective-permute-start.16 = (bf16[640,256]{1,0:T(8,128)(2,1)S(1)}, bf16[640,256]{1,0:T(8,128)(2,1)S(1)}, u32[]{:S(2)}, u32[]{:S(2)}) collective-permute-start(bf16[640,256]{1,0:T(8,128)(2,1)S(1)} %gate_up.1.a0), channel_id=1, source_target_pairs={{0,2},{1,3},{2,0},{3,1},{4,6},{5,7},{6,4},{7,5},{8,10},{9,11},{10,... | collective-permute-start | bytes 983048 | tf_op jit(solution)/shard_map/ppermute | solution.py:27
  90.1 13.9 %collective-permute-start.17 = (bf16[640,256]{1,0:T(8,128)(2,1)S(1)}, bf16[640,256]{1,0:T(8,128)(2,1)S(1)}, u32[]{:S(2)}, u32[]{:S(2)}) collective-permute-start(bf16[640,256]{1,0:T(8,128)(2,1)S(1)} %gate_up.1.a0), channel_id=1, source_target_pairs={{0,3},{1,0},{2,1},{3,2},{4,7},{5,4},{6,5},{7,6},{8,11},{9,8},{10,9... | collective-permute-start | bytes 983048 | tf_op jit(solution)/shard_map/ppermute | solution.py:27
  107.6 36.7 %copy-start.6 = (bf16[2048,128]{1,0:T(8,128)(2,1)S(1)}, bf16[2048,128]{1,0:T(8,128)(2,1)}, u32[]{:S(2)}) copy-start(bf16[2048,128]{1,0:T(8,128)(2,1)} %w_ref.1) | copy-start | bytes 1572868
  107.6 30.3 %all-to-all-start.1 = ((bf16[32,20,512]{2,1,0:T(8,128)(2,1)}), bf16[32,20,512]{2,1,0:T(8,128)(2,1)S(1)}, u32[]{:S(2)}, u32[]{:S(2)}) async-start(bf16[32,20,512]{2,1,0:T(8,128)(2,1)} %down.1), calls=%async_computation.1 | async-start | bytes 1572864 | tf_op jit(solution)/shard_map/all_to_all | solution.py:448
  115.3 42.8 %copy-start.11 = (s32[32,3]{0,1:T(4,128)S(1)}, s32[32,3]{0,1:T(4,128)}, u32[]{:S(2)}) copy-start(s32[32,3]{0,1:T(4,128)} %param.16) | copy-start | bytes 1156
  115.3 43.2 %copy-start.13 = (s32[1,16]{1,0:T(1,128)S(1)}, s32[1,16]{1,0:T(1,128)}, u32[]{:S(2)}) copy-start(s32[1,16]{1,0:T(1,128)} %param.29) | copy-start | bytes 196
  115.4 46.2 %copy-start.12 = (s32[1,1024]{1,0:T(1,128)S(1)}, s32[1,1024]{1,0:T(1,128)}, u32[]{:S(2)}) copy-start(s32[1,1024]{1,0:T(1,128)} %param.28) | copy-start | bytes 12292
  115.7 4.7 %collective-permute-start.5 = (f32[128,128]{0,1:T(8,128)S(1)}, f32[128,128]{0,1:T(8,128)S(1)}, u32[]{:S(2)}, u32[]{:S(2)}) collective-permute-start(f32[128,128]{0,1:T(8,128)S(1)} %pad_maximum_fusion.1), channel_id=1, source_target_pairs={{0,1},{1,2},{2,3},{3,0},{4,5},{5,6},{6,7},{7,4},{8,9},{9,10},{10,1... | collective-permute-start | bytes 196616 | tf_op jit(solution)/shard_map/ppermute | solution.py:27
  116.5 5.9 %collective-permute-start.6 = (f32[128,128]{0,1:T(8,128)S(1)}, f32[128,128]{0,1:T(8,128)S(1)}, u32[]{:S(2)}, u32[]{:S(2)}) collective-permute-start(f32[128,128]{0,1:T(8,128)S(1)} %pad_maximum_fusion.1), channel_id=1, source_target_pairs={{0,2},{1,3},{2,0},{3,1},{4,6},{5,7},{6,4},{7,5},{8,10},{9,11},{10,... | collective-permute-start | bytes 196616 | tf_op jit(solution)/shard_map/ppermute | solution.py:27
  119.0 3.6 %collective-permute-start.7 = (f32[128,128]{0,1:T(8,128)S(1)}, f32[128,128]{0,1:T(8,128)S(1)}, u32[]{:S(2)}, u32[]{:S(2)}) collective-permute-start(f32[128,128]{0,1:T(8,128)S(1)} %pad_maximum_fusion.1), channel_id=1, source_target_pairs={{0,3},{1,0},{2,1},{3,2},{4,7},{5,4},{6,5},{7,6},{8,11},{9,8},{10,9... | collective-permute-start | bytes 196616 | tf_op jit(solution)/shard_map/ppermute | solution.py:27
  137.9 40.3 %copy-start.8 = (bf16[1024,128]{1,0:T(8,128)(2,1)S(1)}, bf16[1024,128]{1,0:T(8,128)(2,1)}, u32[]{:S(2)}) copy-start(bf16[1024,128]{1,0:T(8,128)(2,1)} %doc_ref.1) | copy-start | bytes 786436
  138.9 5.4 %collective-permute-start.22 = (bf16[128,512]{1,0:T(8,128)(2,1)S(1)}, bf16[128,512]{1,0:T(8,128)(2,1)S(1)}, u32[]{:S(2)}, u32[]{:S(2)}) collective-permute-start(bf16[128,512]{1,0:T(8,128)(2,1)S(1)} %fusion.1.moe_ref), channel_id=1, source_target_pairs={{0,4},{4,0},{1,5},{5,1},{2,6},{6,2},{3,7},{7,3},{8,12},{12,8},{9,1... | collective-permute-start | bytes 393224 | tf_op jit(solution)/shard_map/ppermute | solution.py:31
  145.1 4.7 %collective-permute-start.23 = (f32[136,128]{1,0:T(8,128)S(1)}, f32[136,128]{1,0:T(8,128)S(1)}, u32[]{:S(2)}, u32[]{:S(2)}) collective-permute-start(f32[136,128]{1,0:T(8,128)S(1)} %get-tuple-element.44.p0), channel_id=1, source_target_pairs={{0,1},{1,2},{2,3},{3,0},{4,5},{5,6},{6,7},{7,4},{8,9},{9,10},{10,1... | collective-permute-start | bytes 208904 | tf_op jit(solution)/shard_map/ppermute | solution.py:27
  146.1 4.9 %collective-permute-start.24 = (f32[136,128]{1,0:T(8,128)S(1)}, f32[136,128]{1,0:T(8,128)S(1)}, u32[]{:S(2)}, u32[]{:S(2)}) collective-permute-start(f32[136,128]{1,0:T(8,128)S(1)} %get-tuple-element.44.p0), channel_id=1, source_target_pairs={{0,2},{1,3},{2,0},{3,1},{4,6},{5,7},{6,4},{7,5},{8,10},{9,11},{10,... | collective-permute-start | bytes 208904 | tf_op jit(solution)/shard_map/ppermute | solution.py:27
  148.6 3.5 %collective-permute-start.25 = (f32[136,128]{1,0:T(8,128)S(1)}, f32[136,128]{1,0:T(8,128)S(1)}, u32[]{:S(2)}, u32[]{:S(2)}) collective-permute-start(f32[136,128]{1,0:T(8,128)S(1)} %get-tuple-element.44.p0), channel_id=1, source_target_pairs={{0,3},{1,0},{2,1},{3,2},{4,7},{5,4},{6,5},{7,6},{8,11},{9,8},{10,9... | collective-permute-start | bytes 208904 | tf_op jit(solution)/shard_map/ppermute | solution.py:27
  153.1 19.3 %all-to-all-start.2 = ((bf16[16,128,128]{2,1,0:T(8,128)(2,1)}), bf16[16,128,128]{2,1,0:T(8,128)(2,1)S(1)}, u32[]{:S(2)}, u32[]{:S(2)}) async-start(bf16[16,128,128]{2,1,0:T(8,128)(2,1)} %vectors.1), calls=%async_computation.2 | async-start | bytes 1048576 | tf_op jit(solution)/shard_map/all_to_all | solution.py:501
  158.6 6.9 %collective-permute-start.26 = (bf16[128,512]{1,0:T(8,128)(2,1)S(1)}, bf16[128,512]{1,0:T(8,128)(2,1)S(1)}, u32[]{:S(2)}, u32[]{:S(2)}) collective-permute-start(bf16[128,512]{1,0:T(8,128)(2,1)S(1)} %get-tuple-element.48.p0), channel_id=1, source_target_pairs={{0,1},{1,2},{2,3},{3,0},{4,5},{5,6},{6,7},{7,4},{8,9},{9,10},{10,1... | collective-permute-start | bytes 393224 | tf_op jit(solution)/shard_map/ppermute | solution.py:27
  158.7 6.8 %collective-permute-start.27 = (bf16[128,512]{1,0:T(8,128)(2,1)S(1)}, bf16[128,512]{1,0:T(8,128)(2,1)S(1)}, u32[]{:S(2)}, u32[]{:S(2)}) collective-permute-start(bf16[128,512]{1,0:T(8,128)(2,1)S(1)} %get-tuple-element.48.p0), channel_id=1, source_target_pairs={{0,2},{1,3},{2,0},{3,1},{4,6},{5,7},{6,4},{7,5},{8,10},{9,11},{10,... | collective-permute-start | bytes 393224 | tf_op jit(solution)/shard_map/ppermute | solution.py:27
  160.6 5.4 %collective-permute-start.28 = (bf16[128,512]{1,0:T(8,128)(2,1)S(1)}, bf16[128,512]{1,0:T(8,128)(2,1)S(1)}, u32[]{:S(2)}, u32[]{:S(2)}) collective-permute-start(bf16[128,512]{1,0:T(8,128)(2,1)S(1)} %get-tuple-element.48.p0), channel_id=1, source_target_pairs={{0,3},{1,0},{2,1},{3,2},{4,7},{5,4},{6,5},{7,6},{8,11},{9,8},{10,9... | collective-permute-start | bytes 393224 | tf_op jit(solution)/shard_map/ppermute | solution.py:27
  172.4 5.8 %collective-permute-start.29 = (bf16[2048,128]{1,0:T(8,128)(2,1)S(1)}, bf16[2048,128]{1,0:T(8,128)(2,1)S(1)}, u32[]{:S(2)}, u32[]{:S(2)}) collective-permute-start(bf16[2048,128]{1,0:T(8,128)(2,1)S(1)} %bitcast.31), channel_id=1, source_target_pairs={{0,8},{8,0},{1,9},{9,1},{2,10},{10,2},{3,11},{11,3},{4,12},{12,4},... | collective-permute-start | bytes 1572872 | tf_op jit(solution)/shard_map/ppermute | solution.py:515

commit v11 on v10

--- a/solution.py
+++ b/solution.py
@@ -32,7 +32,9 @@
 
 
 def attention_kernel(
-    here_ref,
+    i_ref,
+    j_ref,
+    wide_ref,
     lengths_ref,
     qk_ref,
     gain_ref,
@@ -55,10 +57,10 @@
         pltpu.make_async_copy(w_hbm.at[part], w_ref.at[part], sems.at[1 + part]) for part in range(3)
     ]
     copies += [pltpu.make_async_copy(out_hbm, out_w_ref, sems.at[4])]
-    copies += [pltpu.make_async_copy(gate_hbm.at[1 - here_ref[0]], sent_ref, sems.at[5])]
+    copies += [pltpu.make_async_copy(gate_hbm.at[1 - i_ref[0]], sent_ref, sems.at[5])]
     for copy in copies:
         copy.start()
-    wide = here_ref[2]
+    wide = wide_ref[0]
     one = lengths_ref[0, wide]
     two = one + lengths_ref[1, wide]
 
@@ -105,7 +107,7 @@
         )
     mixed = jnp.concatenate(mixed, axis=1)
     copies[4].wait()
-    j = here_ref[1]
+    j = j_ref[0]
     for k, out_ref in enumerate((out0, out1, out2, out3)):
         part = lax.rem(j + k, 4)
         columns = pl.ds(pl.multiple_of(part * 512, 512), 512)
@@ -210,14 +212,14 @@
         for copy in copies[k]:
             copy.wait()
         total = total + jnp.dot(a[...], w_ref[k], preferred_element_type=f32)
-    size = out_ref.shape[1]
     for s in range(WIDE):
-        out_ref[s] = total[s * size : (s + 1) * size].astype(bf16)
+        out_ref[s] = packed(total[s * CAP : (s + 1) * CAP])
 
 
 def embed_kernel(here_ref, hidden_ref, moe_ref, par_ref, gain_ref, w_ref, layer_ref, part_ref):
     mine = pl.ds(pl.multiple_of(here_ref[1] * 512, 512), 512)
-    layer = hidden_ref[...].astype(f32) + (moe_ref[...].astype(f32) + par_ref[...].astype(f32))
+    moe = moe_ref[...].astype(f32) + par_ref[...].astype(f32)
+    layer = hidden_ref[...].astype(f32) + jnp.concatenate([moe[0:TOK], moe[TOK:]], axis=1)
     layer = layer.astype(bf16)
     layer_ref[...] = layer
     layer = layer.astype(f32)
@@ -341,7 +343,7 @@
             *(jax.ShapeDtypeStruct((TOK, 512), bf16),) * 4,
             jax.ShapeDtypeStruct((2048, 128), bf16),
         ),
-        in_specs=[smem()] * 2 + [vmem()] * 2 + [hbm()] * 4,
+        in_specs=[smem()] * 4 + [vmem()] * 2 + [hbm()] * 4,
         out_specs=(vmem(),) * 5,
         scratch_shapes=[
             pltpu.VMEM((TOK, 2048), bf16),
@@ -352,7 +354,9 @@
         compiler_params=pltpu.CompilerParams(vmem_limit_bytes=60 << 20),
         name="attention",
     )(
-        here,
+        i.reshape(1),
+        j.reshape(1),
+        wide.reshape(1),
         request_lengths.T,
         qk_gain,
         norm_gains,
@@ -438,7 +442,7 @@
     )
     out = pl.pallas_call(
         down_kernel,
-        out_shape=jax.ShapeDtypeStruct((WIDE, CAP, 512), bf16),
+        out_shape=jax.ShapeDtypeStruct((WIDE, 2 * CAP, 256), bf16),
         in_specs=[smem()] + [vmem()] * 4 + [anywhere()] * 5,
         out_specs=vmem(),
         scratch_shapes=[pltpu.VMEM((4, 256, 512), bf16), pltpu.SemaphoreType.DMA((2, 4))],
@@ -466,12 +470,20 @@
     gates = lifted / jnp.sum(lifted, axis=1, keepdims=True)
     gates = lax.dynamic_index_in_dim(gates.reshape(TOK, WIDE, 2), i, 2, keepdims=False).T
 
-    moe = jnp.zeros((TOK, 512), f32)
+    moe = jnp.zeros((2 * TOK, 256), f32)
     contract = (((0, 1), (0, 1)), ((), ()))
     mixing = jnp.where(chosen, gates[:, None, :], 0.0)
+    blank = jnp.zeros_like(mixing)
+    mixing = jnp.concatenate(
+        [
+            jnp.concatenate([mixing, blank], axis=1),
+            jnp.concatenate([blank, mixing], axis=1),
+        ],
+        axis=2,
+    )
     mixing_hi = lax.reduce_precision(mixing, 8, 7)
     mixing_lo = (mixing - mixing_hi).astype(bf16)
-    for matrix in (mixing_hi.astype(bf16), mixing_lo):
+    for matrix in lax.optimization_barrier((mixing_hi.astype(bf16), mixing_lo)):
         moe = moe + lax.dot_general(matrix, back, contract, preferred_element_type=f32)
     moe = moe.astype(bf16)
     moe_par = x_swap(moe)

time: 182 us -> 180 us (0.989)
  starting transfers between devices: 68 us -> 65.7 us
    ppermute x24, waiting for transfers between devices: 35.4 us -> 31.2 us  [y_shift(): return lax.ppermute(x, 'y', [(s, (s + k) % 4) for s in range(4)])]
    all_to_all x1, waiting for transfers between devices: 15.2 us -> 19.1 us  [body(): back = lax.all_to_all(out, W, 0, 0, tiled=True)]
    all_to_all x1, waiting for transfers between devices: 11.5 us -> 13.6 us  [body(): arrived = lax.all_to_all(rows, W, 0, 0, tiled=True)]
  transfers between devices with their start and end apart: 33 -> 33, of which waited for: 20 -> 18; matrix products, arithmetic and copies ran while one was open for 6% -> 5% of each run, Pallas kernels for 3% -> 6%
where the time goes in v11:
time: 180 us
  waiting for transfers between devices  78.8 us (44%)
  starting transfers between devices  65.7 us (36%)
  Pallas kernels  22.2 us (12%)
  local copies, waits for them, and re-layouts  7.56 us (4%)
  other arithmetic  3.07 us (2%)
    ppermute x24, waiting for transfers between devices, y_shift(): return lax.ppermute(x, 'y', [(s, (s + k) % 4) for s in range(4)])  31.2 us
    ppermute x24, starting transfers between devices, y_shift(): return lax.ppermute(x, 'y', [(s, (s + k) % 4) for s in range(4)])  29 us
    all_to_all x1, waiting for transfers between devices, body(): back = lax.all_to_all(out, W, 0, 0, tiled=True)  19.1 us
    all_to_all x1, waiting for transfers between devices, body(): arrived = lax.all_to_all(rows, W, 0, 0, tiled=True)  13.6 us
    all_to_all x1, starting transfers between devices, body(): arrived = lax.all_to_all(rows, W, 0, 0, tiled=True)  11.6 us
    ppermute x5, waiting for transfers between devices, x_swap(): return lax.ppermute(x, 'xh', [(0, 1), (1, 0)])  8.91 us
    ppermute x5, starting transfers between devices, x_swap(): return lax.ppermute(x, 'xh', [(0, 1), (1, 0)])  8.61 us
    all_to_all x1, starting transfers between devices, body(): back = lax.all_to_all(out, W, 0, 0, tiled=True)  6.75 us
  transfers between devices with their start and end apart: 33, of which 18 were waited for; matrix products, arithmetic and copies ran while one was open for 5% of the time, Pallas kernels for 6%

profile of v11, /device:TPU:1, one launch (start us, length us, event | category | flops | bytes accessed | tf_op | source)
XLA Modules:
  0.0 179.8 jit_solution(3848358526312672341)
XLA Ops:
  0.7 5.5 %attention.1 = (bf16[128,512]{1,0:T(8,128)(2,1)}, bf16[128,512]{1,0:T(8,128)(2,1)}, bf16[128,512]{1,0:T(8,128)(2,1)}, bf16[128,512]{1,0:T(8,128)(2,1)}, bf16[2048,128]{1,0:T(8,128)(2,1)}) custom-call(s32[1]{0:T(128)} %bitcast.i_ref, s32[1]{0:T(128)} %bitcast.1.j_ref, s32[1]{0:T(128)} %bitcast.2.wide_ref, s32[3,32]{1,0:T(4,128)} %bitcast.42, ...), custom_call_target="tpu_custom_call" | custom-call | tf_op jit(solution)/shard_map/attention/pallas_call | solution.py:340
  6.2 3.7 %collective-permute-start.4 = (bf16[2048,128]{1,0:T(8,128)(2,1)}, bf16[2048,128]{1,0:T(8,128)(2,1)S(1)}, u32[]{:S(2)}, u32[]{:S(2)}) collective-permute-start(bf16[2048,128]{1,0:T(8,128)(2,1)} %get-tuple-element.35), channel_id=1, source_target_pairs={{0,4},{4,0},{1,5},{5,1},{2,6},{6,2},{3,7},{7,3},{8,12},{12,8},{9,1... | collective-permute-start | bytes 1572872 | tf_op jit(solution)/shard_map/ppermute | solution.py:31
  9.8 1.3 collective-permute-start
  11.1 2.6 %collective-permute-start.1 = (bf16[128,512]{1,0:T(8,128)(2,1)}, bf16[128,512]{1,0:T(8,128)(2,1)S(1)}, u32[]{:S(2)}, u32[]{:S(2)}) collective-permute-start(bf16[128,512]{1,0:T(8,128)(2,1)} %get-tuple-element.32), channel_id=1, source_target_pairs={{0,2},{1,3},{2,0},{3,1},{4,6},{5,7},{6,4},{7,5},{8,10},{9,11},{10,... | collective-permute-start | bytes 393224 | tf_op jit(solution)/shard_map/ppermute | solution.py:27
  13.7 1.1 collective-permute-start.2
  15.8 3.6 %collective-permute-done.1 = bf16[128,512]{1,0:T(8,128)(2,1)S(1)} collective-permute-done((bf16[128,512]{1,0:T(8,128)(2,1)}, bf16[128,512]{1,0:T(8,128)(2,1)S(1)}, u32[]{:S(2)}, u32[]{:S(2)}) %collective-permute-start.1) | collective-permute-done | bytes 131104 | tf_op jit(solution)/shard_map/ppermute | solution.py:27
  19.4 1.0 add_convert_fusion.own_ref
  20.5 5.3 %collective-permute-done.3.par_ref = bf16[128,512]{1,0:T(8,128)(2,1)S(1)} collective-permute-done((bf16[128,512]{1,0:T(8,128)(2,1)S(1)}, bf16[128,512]{1,0:T(8,128)(2,1)S(1)}, u32[]{:S(2)}, u32[]{:S(2)}) %collective-permute-start.3) | collective-permute-done | bytes 131104 | tf_op jit(solution)/shard_map/ppermute | solution.py:31
  26.6 1.7 dispatch.1
  28.3 11.6 %all-to-all-start = ((bf16[32,40,256]{2,1,0:T(8,128)(2,1)}), bf16[32,40,256]{2,1,0:T(8,128)(2,1)S(1)}, u32[]{:S(2)}, u32[]{:S(2)}) async-start(bf16[32,40,256]{2,1,0:T(8,128)(2,1)} %get-tuple-element.40), calls=%async_computation | async-start | bytes 1310720 | tf_op jit(solution)/shard_map/all_to_all | solution.py:406
  40.0 0.9 constant_dynamic-slice_fusion.4
  40.9 2.0 %collective-permute-start.20 = (bf16[2,128,512]{2,1,0:T(8,128)(2,1)}, bf16[2,128,512]{2,1,0:T(8,128)(2,1)}, u32[]{:S(2)}, u32[]{:S(2)}) collective-permute-start(bf16[2,128,512]{2,1,0:T(8,128)(2,1)} %get-tuple-element.62), channel_id=1, source_target_pairs={{0,3},{1,0},{2,1},{3,2},{4,7},{5,4},{6,5},{7,6},{8,11},{9,8},{10,9... | collective-permute-start | bytes 786440 | tf_op jit(solution)/shard_map/ppermute | solution.py:27
  46.0 13.6 %all-to-all-done.in_ref = bf16[32,40,256]{2,1,0:T(8,128)(2,1)S(1)} async-done(((bf16[32,40,256]{2,1,0:T(8,128)(2,1)}), bf16[32,40,256]{2,1,0:T(8,128)(2,1)S(1)}, u32[]{:S(2)}, u32[]{:S(2)}) %all-to-all-start) | async-done | bytes 655392 | tf_op jit(solution)/shard_map/all_to_all | solution.py:406
  61.3 1.8 %collective-permute-start.12 = (bf16[320,512]{1,0:T(8,128)(2,1)}, bf16[320,512]{1,0:T(8,128)(2,1)S(1)}, u32[]{:S(2)}, u32[]{:S(2)}) collective-permute-start(bf16[320,512]{1,0:T(8,128)(2,1)} %get-tuple-element.44.refs_4_), channel_id=1, source_target_pairs={{0,3},{1,0},{2,1},{3,2},{4,7},{5,4},{6,5},{7,6},{8,11},{9,8},{10,9... | collective-permute-start | bytes 983048 | tf_op jit(solution)/shard_map/ppermute | solution.py:27
  63.2 1.8 %collective-permute-start.14 = (bf16[2048,128]{1,0:T(8,128)(2,1)}, bf16[2048,128]{1,0:T(8,128)(2,1)S(1)}, u32[]{:S(2)}, u32[]{:S(2)}) collective-permute-start(bf16[2048,128]{1,0:T(8,128)(2,1)} %dynamic-slice_bitcast_fusion), channel_id=1, source_target_pairs={{0,4},{4,0},{1,5},{5,1},{2,6},{6,2},{3,7},{7,3},{8,12},{12,8},{9,1... | collective-permute-start | bytes 1572872 | tf_op jit(solution)/shard_map/ppermute | solution.py:31
  65.1 0.9 constant_dynamic-slice_fusion
  66.1 0.9 constant_dynamic-slice_fusion.1
  67.0 2.9 %collective-permute-start.9 = (bf16[320,512]{1,0:T(8,128)(2,1)}, bf16[320,512]{1,0:T(8,128)(2,1)S(1)}, u32[]{:S(2)}, u32[]{:S(2)}) collective-permute-start(bf16[320,512]{1,0:T(8,128)(2,1)} %get-tuple-element.43.refs_0_), channel_id=1, source_target_pairs={{0,3},{1,0},{2,1},{3,2},{4,7},{5,4},{6,5},{7,6},{8,11},{9,8},{10,9... | collective-permute-start | bytes 983048 | tf_op jit(solution)/shard_map/ppermute | solution.py:27
  69.9 2.7 %collective-permute-start.13 = (bf16[320,512]{1,0:T(8,128)(2,1)S(1)}, bf16[320,512]{1,0:T(8,128)(2,1)S(1)}, u32[]{:S(2)}, u32[]{:S(2)}) collective-permute-start(bf16[320,512]{1,0:T(8,128)(2,1)S(1)} %collective-permute-done.12.refs_6_), channel_id=1, source_target_pairs={{0,3},{1,0},{2,1},{3,2},{4,7},{5,4},{6,5},{7,6},{8,11},{9,8},{10,9... | collective-permute-start | bytes 983048 | tf_op jit(solution)/shard_map/ppermute | solution.py:27
  72.6 0.9 constant_dynamic-slice_fusion.2
  73.5 1.0 pad_maximum_fusion
  74.5 2.8 %collective-permute-done.11.refs_5_ = bf16[320,512]{1,0:T(8,128)(2,1)S(1)} collective-permute-done((bf16[320,512]{1,0:T(8,128)(2,1)}, bf16[320,512]{1,0:T(8,128)(2,1)S(1)}, u32[]{:S(2)}, u32[]{:S(2)}) %collective-permute-start.11) | collective-permute-done | bytes 327712 | tf_op jit(solution)/shard_map/ppermute | solution.py:27
  77.3 1.2 collective-permute-start.21
  78.5 5.8 %collective-permute-done.10.refs_3_ = bf16[320,512]{1,0:T(8,128)(2,1)S(1)} collective-permute-done((bf16[320,512]{1,0:T(8,128)(2,1)S(1)}, bf16[320,512]{1,0:T(8,128)(2,1)S(1)}, u32[]{:S(2)}, u32[]{:S(2)}) %collective-permute-start.10) | collective-permute-done | bytes 327712 | tf_op jit(solution)/shard_map/ppermute | solution.py:27
  84.3 1.0 copy-done.9
  85.3 3.5 %gate_up.1.a0 = bf16[640,256]{1,0:T(8,128)(2,1)S(1)} custom-call(s32[4]{0:T(128)S(1)} %pad_add_fusion.here_ref, bf16[320,512]{1,0:T(8,128)(2,1)} %get-tuple-element.43.refs_0_, bf16[320,512]{1,0:T(8,128)(2,1)S(1)} %collective-permute-done.8.refs_1_, bf16[320,512]{1,0:T(8,128)(2,1)S(1)} %collective-permute-done.9.refs_2_, ...), custom_call_target="tpu_custom_call" | custom-call | tf_op jit(solution)/shard_map/gate_up/pallas_call | solution.py:421
  89.6 2.0 %collective-permute-start.16 = (bf16[640,256]{1,0:T(8,128)(2,1)S(1)}, bf16[640,256]{1,0:T(8,128)(2,1)S(1)}, u32[]{:S(2)}, u32[]{:S(2)}) collective-permute-start(bf16[640,256]{1,0:T(8,128)(2,1)S(1)} %gate_up.1.a0), channel_id=1, source_target_pairs={{0,2},{1,3},{2,0},{3,1},{4,6},{5,7},{6,4},{7,5},{8,10},{9,11},{10,... | collective-permute-start | bytes 983048 | tf_op jit(solution)/shard_map/ppermute | solution.py:27
  91.6 1.3 collective-permute-start.17
  93.3 1.2 collective-permute-start.6
  94.5 4.6 %collective-permute-done.15.a1 = bf16[640,256]{1,0:T(8,128)(2,1)S(1)} collective-permute-done((bf16[640,256]{1,0:T(8,128)(2,1)S(1)}, bf16[640,256]{1,0:T(8,128)(2,1)S(1)}, u32[]{:S(2)}, u32[]{:S(2)}) %collective-permute-start.15) | collective-permute-done | bytes 327712 | tf_op jit(solution)/shard_map/ppermute | solution.py:27
  99.1 3.6 %collective-permute-done.16.a2 = bf16[640,256]{1,0:T(8,128)(2,1)S(1)} collective-permute-done((bf16[640,256]{1,0:T(8,128)(2,1)S(1)}, bf16[640,256]{1,0:T(8,128)(2,1)S(1)}, u32[]{:S(2)}, u32[]{:S(2)}) %collective-permute-start.16) | collective-permute-done | bytes 327712 | tf_op jit(solution)/shard_map/ppermute | solution.py:27
  102.7 4.6 %collective-permute-done.17.a3 = bf16[640,256]{1,0:T(8,128)(2,1)S(1)} collective-permute-done((bf16[640,256]{1,0:T(8,128)(2,1)S(1)}, bf16[640,256]{1,0:T(8,128)(2,1)S(1)}, u32[]{:S(2)}, u32[]{:S(2)}) %collective-permute-start.17) | collective-permute-done | bytes 327712 | tf_op jit(solution)/shard_map/ppermute | solution.py:27
  107.3 3.7 %down.1 = bf16[32,40,256]{2,1,0:T(8,128)(2,1)} custom-call(s32[4]{0:T(128)S(1)} %pad_add_fusion.here_ref, bf16[640,256]{1,0:T(8,128)(2,1)S(1)} %gate_up.1.a0, bf16[640,256]{1,0:T(8,128)(2,1)S(1)} %collective-permute-done.15.a1, bf16[640,256]{1,0:T(8,128)(2,1)S(1)} %collective-permute-done.16.a2, bf16[640,256]{1,0:T(8,128)(2,1)S(1)} %collective-permute-done.17.a3, ...), custom_call_target="tpu_custom_call" | custom-call | tf_op jit(solution)/shard_map/down/pallas_call | solution.py:443
  110.9 6.7 %all-to-all-start.1 = ((bf16[32,40,256]{2,1,0:T(8,128)(2,1)}), bf16[32,40,256]{2,1,0:T(8,128)(2,1)S(1)}, u32[]{:S(2)}, u32[]{:S(2)}) async-start(bf16[32,40,256]{2,1,0:T(8,128)(2,1)} %down.1), calls=%async_computation.1 | async-start | bytes 1310720 | tf_op jit(solution)/shard_map/all_to_all | solution.py:452
  118.2 19.1 %all-to-all-done.1 = bf16[32,40,256]{2,1,0:T(8,128)(2,1)S(1)} async-done(((bf16[32,40,256]{2,1,0:T(8,128)(2,1)}), bf16[32,40,256]{2,1,0:T(8,128)(2,1)S(1)}, u32[]{:S(2)}, u32[]{:S(2)}) %all-to-all-start.1) | async-done | bytes 655392 | tf_op jit(solution)/shard_map/all_to_all | solution.py:452
  138.1 1.8 %collective-permute-start.22 = (bf16[256,256]{1,0:T(8,128)(2,1)S(1)}, bf16[256,256]{1,0:T(8,128)(2,1)S(1)}, u32[]{:S(2)}, u32[]{:S(2)}) collective-permute-start(bf16[256,256]{1,0:T(8,128)(2,1)S(1)} %fusion.2.moe_ref), channel_id=1, source_target_pairs={{0,4},{4,0},{1,5},{5,1},{2,6},{6,2},{3,7},{7,3},{8,12},{12,8},{9,1... | collective-permute-start | bytes 393224 | tf_op jit(solution)/shard_map/ppermute | solution.py:31
  139.9 3.6 %collective-permute-done.22.par_ref = bf16[256,256]{1,0:T(8,128)(2,1)S(1)} collective-permute-done((bf16[256,256]{1,0:T(8,128)(2,1)S(1)}, bf16[256,256]{1,0:T(8,128)(2,1)S(1)}, u32[]{:S(2)}, u32[]{:S(2)}) %collective-permute-start.22) | collective-permute-done | bytes 131104 | tf_op jit(solution)/shard_map/ppermute | solution.py:31
  145.0 2.5 %collective-permute-start.24 = (f32[136,128]{1,0:T(8,128)S(1)}, f32[136,128]{1,0:T(8,128)S(1)}, u32[]{:S(2)}, u32[]{:S(2)}) collective-permute-start(f32[136,128]{1,0:T(8,128)S(1)} %get-tuple-element.48.p0), channel_id=1, source_target_pairs={{0,2},{1,3},{2,0},{3,1},{4,6},{5,7},{6,4},{7,5},{8,10},{9,11},{10,... | collective-permute-start | bytes 208904 | tf_op jit(solution)/shard_map/ppermute | solution.py:27
  149.0 1.0 collective-permute-done.24.p2
  150.7 1.0 vectors.1
  151.7 5.2 %all-to-all-start.2 = ((bf16[16,128,128]{2,1,0:T(8,128)(2,1)}), bf16[16,128,128]{2,1,0:T(8,128)(2,1)S(1)}, u32[]{:S(2)}, u32[]{:S(2)}) async-start(bf16[16,128,128]{2,1,0:T(8,128)(2,1)} %vectors.1), calls=%async_computation.2 | async-start | bytes 1048576 | tf_op jit(solution)/shard_map/all_to_all | solution.py:513
  157.5 2.5 %collective-permute-start.27 = (bf16[128,512]{1,0:T(8,128)(2,1)S(1)}, bf16[128,512]{1,0:T(8,128)(2,1)S(1)}, u32[]{:S(2)}, u32[]{:S(2)}) collective-permute-start(bf16[128,512]{1,0:T(8,128)(2,1)S(1)} %get-tuple-element.52.p0), channel_id=1, source_target_pairs={{0,2},{1,3},{2,0},{3,1},{4,6},{5,7},{6,4},{7,5},{8,10},{9,11},{10,... | collective-permute-start | bytes 393224 | tf_op jit(solution)/shard_map/ppermute | solution.py:27
  160.8 1.7 collective-permute-done.26.p1
  162.5 1.4 collective-permute-done.27.p2
  164.8 5.8 %all-to-all-done.2 = bf16[16,128,128]{2,1,0:T(8,128)(2,1)S(1)} async-done(((bf16[16,128,128]{2,1,0:T(8,128)(2,1)}), bf16[16,128,128]{2,1,0:T(8,128)(2,1)S(1)}, u32[]{:S(2)}, u32[]{:S(2)}) %all-to-all-start.2) | async-done | bytes 524320 | tf_op jit(solution)/shard_map/all_to_all | solution.py:513
  170.5 4.6 %collective-permute-start.29 = (bf16[2048,128]{1,0:T(8,128)(2,1)S(1)}, bf16[2048,128]{1,0:T(8,128)(2,1)S(1)}, u32[]{:S(2)}, u32[]{:S(2)}) collective-permute-start(bf16[2048,128]{1,0:T(8,128)(2,1)S(1)} %bitcast.35), channel_id=1, source_target_pairs={{0,8},{8,0},{1,9},{9,1},{2,10},{10,2},{3,11},{11,3},{4,12},{12,4},... | collective-permute-start | bytes 1572872 | tf_op jit(solution)/shard_map/ppermute | solution.py:527
  175.1 1.4 assemble.1
  176.7 2.9 %score.1 = f32[1,16]{1,0:T(1,128)} custom-call(s32[5,16]{1,0:T(8,128)S(1)} %stack.48.info_ref, bf16[1024,128]{1,0:T(8,128)(2,1)S(1)} %copy-done.10, bf16[2048,128]{1,0:T(8,128)(2,1)S(1)} %bitcast.36, bf16[2048,128]{1,0:T(8,128)(2,1)S(1)} %collective-permute-done.29.other_ref), custom_call_target="tpu_custom_call" | custom-call | tf_op jit(solution)/shard_map/score/pallas_call | solution.py:536
  (101 shorter events, 15.3 us)
Async XLA Ops:
  0.6 88.8 %copy-start = (bf16[2048,64]{0,1:T(8,128)(2,1)S(1)}, bf16[2048,64]{0,1:T(8,128)(2,1)}, u32[]{:S(2)}) copy-start(bf16[2048,64]{0,1:T(8,128)(2,1)} %param.21) | copy-start | bytes 786436
  0.7 14.2 %copy-start.11 = (s32[128,8]{0,1:T(8,128)S(1)}, s32[128,8]{0,1:T(8,128)}, u32[]{:S(2)}) copy-start(s32[128,8]{0,1:T(8,128)} %param.22) | copy-start | bytes 12292
  0.7 25.9 %copy-start.3 = (bf16[128,2048]{1,0:T(8,128)(2,1)S(1)}, bf16[128,2048]{1,0:T(8,128)(2,1)}, u32[]{:S(2)}) copy-start(bf16[128,2048]{1,0:T(8,128)(2,1)} %x_ref.1) | copy-start | bytes 1572868
  6.2 19.6 %collective-permute-start.4 = (bf16[2048,128]{1,0:T(8,128)(2,1)}, bf16[2048,128]{1,0:T(8,128)(2,1)S(1)}, u32[]{:S(2)}, u32[]{:S(2)}) collective-permute-start(bf16[2048,128]{1,0:T(8,128)(2,1)} %get-tuple-element.35), channel_id=1, source_target_pairs={{0,4},{4,0},{1,5},{5,1},{2,6},{6,2},{3,7},{7,3},{8,12},{12,8},{9,1... | collective-permute-start | bytes 1572872 | tf_op jit(solution)/shard_map/ppermute | solution.py:31
  9.8 5.9 %collective-permute-start = (bf16[128,512]{1,0:T(8,128)(2,1)}, bf16[128,512]{1,0:T(8,128)(2,1)S(1)}, u32[]{:S(2)}, u32[]{:S(2)}) collective-permute-start(bf16[128,512]{1,0:T(8,128)(2,1)} %get-tuple-element.31), channel_id=1, source_target_pairs={{0,1},{1,2},{2,3},{3,0},{4,5},{5,6},{6,7},{7,4},{8,9},{9,10},{10,1... | collective-permute-start | bytes 393224 | tf_op jit(solution)/shard_map/ppermute | solution.py:27
  11.1 8.2 %collective-permute-start.1 = (bf16[128,512]{1,0:T(8,128)(2,1)}, bf16[128,512]{1,0:T(8,128)(2,1)S(1)}, u32[]{:S(2)}, u32[]{:S(2)}) collective-permute-start(bf16[128,512]{1,0:T(8,128)(2,1)} %get-tuple-element.32), channel_id=1, source_target_pairs={{0,2},{1,3},{2,0},{3,1},{4,6},{5,7},{6,4},{7,5},{8,10},{9,11},{10,... | collective-permute-start | bytes 393224 | tf_op jit(solution)/shard_map/ppermute | solution.py:27
  13.7 5.6 %collective-permute-start.2 = (bf16[128,512]{1,0:T(8,128)(2,1)}, bf16[128,512]{1,0:T(8,128)(2,1)S(1)}, u32[]{:S(2)}, u32[]{:S(2)}) collective-permute-start(bf16[128,512]{1,0:T(8,128)(2,1)} %get-tuple-element.33), channel_id=1, source_target_pairs={{0,3},{1,0},{2,1},{3,2},{4,7},{5,4},{6,5},{7,6},{8,11},{9,8},{10,9... | collective-permute-start | bytes 393224 | tf_op jit(solution)/shard_map/ppermute | solution.py:27
  20.4 19.6 %copy-start.12 = (bf16[2,128,2048]{2,1,0:T(8,128)(2,1)S(1)}, bf16[2,128,2048]{2,1,0:T(8,128)(2,1)}, u32[]{:S(2)}) copy-start(bf16[2,128,2048]{2,1,0:T(8,128)(2,1)} %param.25) | copy-start | bytes 3145732
  20.4 5.4 %collective-permute-start.3 = (bf16[128,512]{1,0:T(8,128)(2,1)S(1)}, bf16[128,512]{1,0:T(8,128)(2,1)S(1)}, u32[]{:S(2)}, u32[]{:S(2)}) collective-permute-start(bf16[128,512]{1,0:T(8,128)(2,1)S(1)} %add_convert_fusion.own_ref), channel_id=1, source_target_pairs={{0,4},{4,0},{1,5},{5,1},{2,6},{6,2},{3,7},{7,3},{8,12},{12,8},{9,1... | collective-permute-start | bytes 393224 | tf_op jit(solution)/shard_map/ppermute | solution.py:31
  28.3 31.2 %all-to-all-start = ((bf16[32,40,256]{2,1,0:T(8,128)(2,1)}), bf16[32,40,256]{2,1,0:T(8,128)(2,1)S(1)}, u32[]{:S(2)}, u32[]{:S(2)}) async-start(bf16[32,40,256]{2,1,0:T(8,128)(2,1)} %get-tuple-element.40), calls=%async_computation | async-start | bytes 1310720 | tf_op jit(solution)/shard_map/all_to_all | solution.py:406
  40.0 4.4 %copy-start.2 = (bf16[2,2048,128]{2,1,0:T(8,128)(2,1)S(1)}, bf16[2,2048,128]{2,1,0:T(8,128)(2,1)}, u32[]{:S(2)}) copy-start(bf16[2,2048,128]{2,1,0:T(8,128)(2,1)} %refs_10_.1) | copy-start | bytes 3145732
  40.9 22.2 %copy-start.7 = (f32[3,2048]{1,0:T(4,128)S(1)}, f32[3,2048]{1,0:T(4,128)}, u32[]{:S(2)}) copy-start(f32[3,2048]{1,0:T(4,128)} %gain_ref.3) | copy-start | bytes 73732
  40.9 22.3 %collective-permute-start.20 = (bf16[2,128,512]{2,1,0:T(8,128)(2,1)}, bf16[2,128,512]{2,1,0:T(8,128)(2,1)}, u32[]{:S(2)}, u32[]{:S(2)}) collective-permute-start(bf16[2,128,512]{2,1,0:T(8,128)(2,1)} %get-tuple-element.62), channel_id=1, source_target_pairs={{0,3},{1,0},{2,1},{3,2},{4,7},{5,4},{6,5},{7,6},{8,11},{9,8},{10,9... | collective-permute-start | bytes 786440 | tf_op jit(solution)/shard_map/ppermute | solution.py:27
  43.0 23.0 %collective-permute-start.19 = (bf16[2,128,512]{2,1,0:T(8,128)(2,1)}, bf16[2,128,512]{2,1,0:T(8,128)(2,1)}, u32[]{:S(2)}, u32[]{:S(2)}) collective-permute-start(bf16[2,128,512]{2,1,0:T(8,128)(2,1)} %get-tuple-element.63), channel_id=1, source_target_pairs={{0,2},{1,3},{2,0},{3,1},{4,6},{5,7},{6,4},{7,5},{8,10},{9,11},{10,... | collective-permute-start | bytes 786440 | tf_op jit(solution)/shard_map/ppermute | solution.py:27
  43.6 23.4 %collective-permute-start.18 = (bf16[2,128,512]{2,1,0:T(8,128)(2,1)}, bf16[2,128,512]{2,1,0:T(8,128)(2,1)}, u32[]{:S(2)}, u32[]{:S(2)}) collective-permute-start(bf16[2,128,512]{2,1,0:T(8,128)(2,1)} %get-tuple-element.64), channel_id=1, source_target_pairs={{0,1},{1,2},{2,3},{3,0},{4,5},{5,6},{6,7},{7,4},{8,9},{9,10},{10,1... | collective-permute-start | bytes 786440 | tf_op jit(solution)/shard_map/ppermute | solution.py:27
  46.0 38.4 %copy-start.1 = (bf16[2,2048,128]{2,1,0:T(8,128)(2,1)S(1)}, bf16[2,2048,128]{2,1,0:T(8,128)(2,1)}, u32[]{:S(2)}) copy-start(bf16[2,2048,128]{2,1,0:T(8,128)(2,1)} %refs_9_.1) | copy-start | bytes 3145732
  60.5 9.4 %collective-permute-start.8 = (bf16[320,512]{1,0:T(8,128)(2,1)}, bf16[320,512]{1,0:T(8,128)(2,1)S(1)}, u32[]{:S(2)}, u32[]{:S(2)}) collective-permute-start(bf16[320,512]{1,0:T(8,128)(2,1)} %get-tuple-element.43.refs_0_), channel_id=1, source_target_pairs={{0,1},{1,2},{2,3},{3,0},{4,5},{5,6},{6,7},{7,4},{8,9},{9,10},{10,1... | collective-permute-start | bytes 983048 | tf_op jit(solution)/shard_map/ppermute | solution.py:27
  61.3 8.6 %collective-permute-start.12 = (bf16[320,512]{1,0:T(8,128)(2,1)}, bf16[320,512]{1,0:T(8,128)(2,1)S(1)}, u32[]{:S(2)}, u32[]{:S(2)}) collective-permute-start(bf16[320,512]{1,0:T(8,128)(2,1)} %get-tuple-element.44.refs_4_), channel_id=1, source_target_pairs={{0,3},{1,0},{2,1},{3,2},{4,7},{5,4},{6,5},{7,6},{8,11},{9,8},{10,9... | collective-permute-start | bytes 983048 | tf_op jit(solution)/shard_map/ppermute | solution.py:27
  63.2 21.1 %copy-start.5 = (bf16[2048,128]{1,0:T(8,128)(2,1)S(1)}, bf16[2048,128]{1,0:T(8,128)(2,1)}, u32[]{:S(2)}) copy-start(bf16[2048,128]{1,0:T(8,128)(2,1)} %copy-done.4) | copy-start | bytes 1572868
  63.2 15.3 %collective-permute-start.14 = (bf16[2048,128]{1,0:T(8,128)(2,1)}, bf16[2048,128]{1,0:T(8,128)(2,1)S(1)}, u32[]{:S(2)}, u32[]{:S(2)}) collective-permute-start(bf16[2048,128]{1,0:T(8,128)(2,1)} %dynamic-slice_bitcast_fusion), channel_id=1, source_target_pairs={{0,4},{4,0},{1,5},{5,1},{2,6},{6,2},{3,7},{7,3},{8,12},{12,8},{9,1... | collective-permute-start | bytes 1572872 | tf_op jit(solution)/shard_map/ppermute | solution.py:31
  66.0 11.3 %collective-permute-start.11 = (bf16[320,512]{1,0:T(8,128)(2,1)}, bf16[320,512]{1,0:T(8,128)(2,1)S(1)}, u32[]{:S(2)}, u32[]{:S(2)}) collective-permute-start(bf16[320,512]{1,0:T(8,128)(2,1)} %get-tuple-element.44.refs_4_), channel_id=1, source_target_pairs={{0,1},{1,2},{2,3},{3,0},{4,5},{5,6},{6,7},{7,4},{8,9},{9,10},{10,1... | collective-permute-start | bytes 983048 | tf_op jit(solution)/shard_map/ppermute | solution.py:27
  67.0 11.5 %collective-permute-start.9 = (bf16[320,512]{1,0:T(8,128)(2,1)}, bf16[320,512]{1,0:T(8,128)(2,1)S(1)}, u32[]{:S(2)}, u32[]{:S(2)}) collective-permute-start(bf16[320,512]{1,0:T(8,128)(2,1)} %get-tuple-element.43.refs_0_), channel_id=1, source_target_pairs={{0,3},{1,0},{2,1},{3,2},{4,7},{5,4},{6,5},{7,6},{8,11},{9,8},{10,9... | collective-permute-start | bytes 983048 | tf_op jit(solution)/shard_map/ppermute | solution.py:27
  69.9 14.4 %collective-permute-start.10 = (bf16[320,512]{1,0:T(8,128)(2,1)S(1)}, bf16[320,512]{1,0:T(8,128)(2,1)S(1)}, u32[]{:S(2)}, u32[]{:S(2)}) collective-permute-start(bf16[320,512]{1,0:T(8,128)(2,1)S(1)} %collective-permute-done.8.refs_1_), channel_id=1, source_target_pairs={{0,1},{1,2},{2,3},{3,0},{4,5},{5,6},{6,7},{7,4},{8,9},{9,10},{10,1... | collective-permute-start | bytes 983048 | tf_op jit(solution)/shard_map/ppermute | solution.py:27
  69.9 14.4 %copy-start.8 = (bf16[320,512]{1,0:T(8,128)(2,1)}, bf16[320,512]{1,0:T(8,128)(2,1)S(1)}, u32[]{:S(2)}) copy-start(bf16[320,512]{1,0:T(8,128)(2,1)S(1)} %collective-permute-done.12.refs_6_) | copy-start | bytes 983044
  69.9 14.4 %collective-permute-start.13 = (bf16[320,512]{1,0:T(8,128)(2,1)S(1)}, bf16[320,512]{1,0:T(8,128)(2,1)S(1)}, u32[]{:S(2)}, u32[]{:S(2)}) collective-permute-start(bf16[320,512]{1,0:T(8,128)(2,1)S(1)} %collective-permute-done.12.refs_6_), channel_id=1, source_target_pairs={{0,3},{1,0},{2,1},{3,2},{4,7},{5,4},{6,5},{7,6},{8,11},{9,8},{10,9... | collective-permute-start | bytes 983048 | tf_op jit(solution)/shard_map/ppermute | solution.py:27
  77.3 16.0 %collective-permute-start.21 = (bf16[4,128,512]{2,1,0:T(8,128)(2,1)S(1)}, bf16[4,128,512]{2,1,0:T(8,128)(2,1)S(1)}, u32[]{:S(2)}, u32[]{:S(2)}) collective-permute-start(bf16[4,128,512]{2,1,0:T(8,128)(2,1)S(1)} %pad_maximum_fusion), channel_id=1, source_target_pairs={{0,4},{4,0},{1,5},{5,1},{2,6},{6,2},{3,7},{7,3},{8,12},{12,8},{9,1... | collective-permute-start | bytes 1572872 | tf_op jit(solution)/shard_map/ppermute | solution.py:31
  84.3 1.0 copy-start.9
  88.8 10.3 %collective-permute-start.15 = (bf16[640,256]{1,0:T(8,128)(2,1)S(1)}, bf16[640,256]{1,0:T(8,128)(2,1)S(1)}, u32[]{:S(2)}, u32[]{:S(2)}) collective-permute-start(bf16[640,256]{1,0:T(8,128)(2,1)S(1)} %gate_up.1.a0), channel_id=1, source_target_pairs={{0,1},{1,2},{2,3},{3,0},{4,5},{5,6},{6,7},{7,4},{8,9},{9,10},{10,1... | collective-permute-start | bytes 983048 | tf_op jit(solution)/shard_map/ppermute | solution.py:27
  89.6 13.0 %collective-permute-start.16 = (bf16[640,256]{1,0:T(8,128)(2,1)S(1)}, bf16[640,256]{1,0:T(8,128)(2,1)S(1)}, u32[]{:S(2)}, u32[]{:S(2)}) collective-permute-start(bf16[640,256]{1,0:T(8,128)(2,1)S(1)} %gate_up.1.a0), channel_id=1, source_target_pairs={{0,2},{1,3},{2,0},{3,1},{4,6},{5,7},{6,4},{7,5},{8,10},{9,11},{10,... | collective-permute-start | bytes 983048 | tf_op jit(solution)/shard_map/ppermute | solution.py:27
  91.6 15.7 %collective-permute-start.17 = (bf16[640,256]{1,0:T(8,128)(2,1)S(1)}, bf16[640,256]{1,0:T(8,128)(2,1)S(1)}, u32[]{:S(2)}, u32[]{:S(2)}) collective-permute-start(bf16[640,256]{1,0:T(8,128)(2,1)S(1)} %gate_up.1.a0), channel_id=1, source_target_pairs={{0,3},{1,0},{2,1},{3,2},{4,7},{5,4},{6,5},{7,6},{8,11},{9,8},{10,9... | collective-permute-start | bytes 983048 | tf_op jit(solution)/shard_map/ppermute | solution.py:27
  93.0 24.7 %collective-permute-start.5 = (f32[128,128]{0,1:T(8,128)S(1)}, f32[128,128]{0,1:T(8,128)S(1)}, u32[]{:S(2)}, u32[]{:S(2)}) collective-permute-start(f32[128,128]{0,1:T(8,128)S(1)} %pad_maximum_fusion.1), channel_id=1, source_target_pairs={{0,1},{1,2},{2,3},{3,0},{4,5},{5,6},{6,7},{7,4},{8,9},{9,10},{10,1... | collective-permute-start | bytes 196616 | tf_op jit(solution)/shard_map/ppermute | solution.py:27
  93.3 24.4 %collective-permute-start.6 = (f32[128,128]{0,1:T(8,128)S(1)}, f32[128,128]{0,1:T(8,128)S(1)}, u32[]{:S(2)}, u32[]{:S(2)}) collective-permute-start(f32[128,128]{0,1:T(8,128)S(1)} %pad_maximum_fusion.1), channel_id=1, source_target_pairs={{0,2},{1,3},{2,0},{3,1},{4,6},{5,7},{6,4},{7,5},{8,10},{9,11},{10,... | collective-permute-start | bytes 196616 | tf_op jit(solution)/shard_map/ppermute | solution.py:27
  99.1 18.6 %collective-permute-start.7 = (f32[128,128]{0,1:T(8,128)S(1)}, f32[128,128]{0,1:T(8,128)S(1)}, u32[]{:S(2)}, u32[]{:S(2)}) collective-permute-start(f32[128,128]{0,1:T(8,128)S(1)} %pad_maximum_fusion.1), channel_id=1, source_target_pairs={{0,3},{1,0},{2,1},{3,2},{4,7},{5,4},{6,5},{7,6},{8,11},{9,8},{10,9... | collective-permute-start | bytes 196616 | tf_op jit(solution)/shard_map/ppermute | solution.py:27
  110.9 26.4 %all-to-all-start.1 = ((bf16[32,40,256]{2,1,0:T(8,128)(2,1)}), bf16[32,40,256]{2,1,0:T(8,128)(2,1)S(1)}, u32[]{:S(2)}, u32[]{:S(2)}) async-start(bf16[32,40,256]{2,1,0:T(8,128)(2,1)} %down.1), calls=%async_computation.1 | async-start | bytes 1310720 | tf_op jit(solution)/shard_map/all_to_all | solution.py:452
  137.7 5.9 %copy-start.6 = (bf16[2048,128]{1,0:T(8,128)(2,1)S(1)}, bf16[2048,128]{1,0:T(8,128)(2,1)}, u32[]{:S(2)}) copy-start(bf16[2048,128]{1,0:T(8,128)(2,1)} %w_ref.1) | copy-start | bytes 1572868
  138.1 18.8 %copy-start.13 = (s32[32,3]{0,1:T(4,128)S(1)}, s32[32,3]{0,1:T(4,128)}, u32[]{:S(2)}) copy-start(s32[32,3]{0,1:T(4,128)} %param.16) | copy-start | bytes 1156
  138.1 19.2 %copy-start.15 = (s32[1,16]{1,0:T(1,128)S(1)}, s32[1,16]{1,0:T(1,128)}, u32[]{:S(2)}) copy-start(s32[1,16]{1,0:T(1,128)} %param.29) | copy-start | bytes 196
  138.1 22.5 %copy-start.14 = (s32[1,1024]{1,0:T(1,128)S(1)}, s32[1,1024]{1,0:T(1,128)}, u32[]{:S(2)}) copy-start(s32[1,1024]{1,0:T(1,128)} %param.28) | copy-start | bytes 12292
  138.1 5.4 %collective-permute-start.22 = (bf16[256,256]{1,0:T(8,128)(2,1)S(1)}, bf16[256,256]{1,0:T(8,128)(2,1)S(1)}, u32[]{:S(2)}, u32[]{:S(2)}) collective-permute-start(bf16[256,256]{1,0:T(8,128)(2,1)S(1)} %fusion.2.moe_ref), channel_id=1, source_target_pairs={{0,4},{4,0},{1,5},{5,1},{2,6},{6,2},{3,7},{7,3},{8,12},{12,8},{9,1... | collective-permute-start | bytes 393224 | tf_op jit(solution)/shard_map/ppermute | solution.py:31
  144.3 4.7 %collective-permute-start.23 = (f32[136,128]{1,0:T(8,128)S(1)}, f32[136,128]{1,0:T(8,128)S(1)}, u32[]{:S(2)}, u32[]{:S(2)}) collective-permute-start(f32[136,128]{1,0:T(8,128)S(1)} %get-tuple-element.48.p0), channel_id=1, source_target_pairs={{0,1},{1,2},{2,3},{3,0},{4,5},{5,6},{6,7},{7,4},{8,9},{9,10},{10,1... | collective-permute-start | bytes 208904 | tf_op jit(solution)/shard_map/ppermute | solution.py:27
  145.0 5.0 %collective-permute-start.24 = (f32[136,128]{1,0:T(8,128)S(1)}, f32[136,128]{1,0:T(8,128)S(1)}, u32[]{:S(2)}, u32[]{:S(2)}) collective-permute-start(f32[136,128]{1,0:T(8,128)S(1)} %get-tuple-element.48.p0), channel_id=1, source_target_pairs={{0,2},{1,3},{2,0},{3,1},{4,6},{5,7},{6,4},{7,5},{8,10},{9,11},{10,... | collective-permute-start | bytes 208904 | tf_op jit(solution)/shard_map/ppermute | solution.py:27
  147.5 3.2 %collective-permute-start.25 = (f32[136,128]{1,0:T(8,128)S(1)}, f32[136,128]{1,0:T(8,128)S(1)}, u32[]{:S(2)}, u32[]{:S(2)}) collective-permute-start(f32[136,128]{1,0:T(8,128)S(1)} %get-tuple-element.48.p0), channel_id=1, source_target_pairs={{0,3},{1,0},{2,1},{3,2},{4,7},{5,4},{6,5},{7,6},{8,11},{9,8},{10,9... | collective-permute-start | bytes 208904 | tf_op jit(solution)/shard_map/ppermute | solution.py:27
  151.7 25.0 %copy-start.10 = (bf16[1024,128]{1,0:T(8,128)(2,1)S(1)}, bf16[1024,128]{1,0:T(8,128)(2,1)}, u32[]{:S(2)}) copy-start(bf16[1024,128]{1,0:T(8,128)(2,1)} %doc_ref.1) | copy-start | bytes 786436
  151.7 18.8 %all-to-all-start.2 = ((bf16[16,128,128]{2,1,0:T(8,128)(2,1)}), bf16[16,128,128]{2,1,0:T(8,128)(2,1)S(1)}, u32[]{:S(2)}, u32[]{:S(2)}) async-start(bf16[16,128,128]{2,1,0:T(8,128)(2,1)} %vectors.1), calls=%async_computation.2 | async-start | bytes 1048576 | tf_op jit(solution)/shard_map/all_to_all | solution.py:513
  157.4 5.1 %collective-permute-start.26 = (bf16[128,512]{1,0:T(8,128)(2,1)S(1)}, bf16[128,512]{1,0:T(8,128)(2,1)S(1)}, u32[]{:S(2)}, u32[]{:S(2)}) collective-permute-start(bf16[128,512]{1,0:T(8,128)(2,1)S(1)} %get-tuple-element.52.p0), channel_id=1, source_target_pairs={{0,1},{1,2},{2,3},{3,0},{4,5},{5,6},{6,7},{7,4},{8,9},{9,10},{10,1... | collective-permute-start | bytes 393224 | tf_op jit(solution)/shard_map/ppermute | solution.py:27
  157.5 6.3 %collective-permute-start.27 = (bf16[128,512]{1,0:T(8,128)(2,1)S(1)}, bf16[128,512]{1,0:T(8,128)(2,1)S(1)}, u32[]{:S(2)}, u32[]{:S(2)}) collective-permute-start(bf16[128,512]{1,0:T(8,128)(2,1)S(1)} %get-tuple-element.52.p0), channel_id=1, source_target_pairs={{0,2},{1,3},{2,0},{3,1},{4,6},{5,7},{6,4},{7,5},{8,10},{9,11},{10,... | collective-permute-start | bytes 393224 | tf_op jit(solution)/shard_map/ppermute | solution.py:27
  160.1 4.7 %collective-permute-start.28 = (bf16[128,512]{1,0:T(8,128)(2,1)S(1)}, bf16[128,512]{1,0:T(8,128)(2,1)S(1)}, u32[]{:S(2)}, u32[]{:S(2)}) collective-permute-start(bf16[128,512]{1,0:T(8,128)(2,1)S(1)} %get-tuple-element.52.p0), channel_id=1, source_target_pairs={{0,3},{1,0},{2,1},{3,2},{4,7},{5,4},{6,5},{7,6},{8,11},{9,8},{10,9... | collective-permute-start | bytes 393224 | tf_op jit(solution)/shard_map/ppermute | solution.py:27
  170.5 6.1 %collective-permute-start.29 = (bf16[2048,128]{1,0:T(8,128)(2,1)S(1)}, bf16[2048,128]{1,0:T(8,128)(2,1)S(1)}, u32[]{:S(2)}, u32[]{:S(2)}) collective-permute-start(bf16[2048,128]{1,0:T(8,128)(2,1)S(1)} %bitcast.35), channel_id=1, source_target_pairs={{0,8},{8,0},{1,9},{9,1},{2,10},{10,2},{3,11},{11,3},{4,12},{12,4},... | collective-permute-start | bytes 1572872 | tf_op jit(solution)/shard_map/ppermute | solution.py:527
  (1 other events, 0.8 us)

commit v12 on v11

--- a/solution.py
+++ b/solution.py
@@ -224,13 +224,14 @@
     layer_ref[...] = layer
     layer = layer.astype(f32)
     scaled = (layer * gain_ref[2:3, mine]).astype(bf16)
-    part_ref[0:TOK, :] = jnp.dot(scaled, w_ref[mine, :], preferred_element_type=f32)
+    part = jnp.dot(scaled, w_ref[mine, :], preferred_element_type=f32)
+    part_ref[0:TOK, :] = part.astype(bf16)
     square = jnp.broadcast_to(jnp.sum(layer * layer, axis=1, keepdims=True), (TOK, TOK))
-    part_ref[TOK:, :] = jnp.transpose(square)[0:8]
+    part_ref[TOK:, :] = jnp.transpose(square)[0:16].astype(bf16)
 
 
 def vector_kernel(p0, p1, p2, p3, out_ref):
-    whole = p0[...] + p1[...] + p2[...] + p3[...]
+    whole = sum(p[...].astype(f32) for p in (p0, p1, p2, p3))
     square = jnp.transpose(jnp.broadcast_to(whole[TOK : TOK + 1], (TOK, TOK)))
     embedded = whole[0:TOK] * lax.rsqrt(square / 2048.0 + EPS)
     norm = jnp.sum(embedded * embedded, axis=1, keepdims=True)
@@ -449,14 +450,14 @@
         compiler_params=params(),
         name="down",
     )(here, act, *(y_shift(act, k) for k in (1, 2, 3)), *downs, down_par)
-    back = lax.all_to_all(out, W, 0, 0, tiled=True)
-
     hf = hidden.astype(f32)
     gain_mine = lax.dynamic_slice_in_dim(norm_gains[1], j * 512, 512, 0)
     router_mine = lax.dynamic_slice_in_dim(w_router, j * 512, 512, 0)
     part = jnp.dot((hf * gain_mine).astype(bf16), router_mine, preferred_element_type=f32)
     square = jnp.sum(hf * hf, axis=1, keepdims=True)
     part = jnp.concatenate([part, jnp.broadcast_to(square, (TOK, EXPERTS))], axis=1)
+    out, part = lax.optimization_barrier((out, part))
+    back = lax.all_to_all(out, W, 0, 0, tiled=True)
     whole = part
     for k in (1, 2, 3):
         whole = whole + y_shift(part, k)
@@ -491,7 +492,7 @@
         embed_kernel,
         out_shape=(
             jax.ShapeDtypeStruct((TOK, 512), bf16),
-            jax.ShapeDtypeStruct((TOK + 8, 128), f32),
+            jax.ShapeDtypeStruct((TOK + 16, 128), bf16),
         ),
         in_specs=[smem()] + [vmem()] * 5,
         out_specs=(vmem(), vmem()),

time: 180 us -> 180 us (level)
  starting transfers between devices: 65.7 us -> 67.6 us
    ppermute x24, starting transfers between devices: 29 us -> 31.8 us  [y_shift(): return lax.ppermute(x, 'y', [(s, (s + k) % 4) for s in range(4)])]
  transfers between devices with their start and end apart: 33 -> 33, of which waited for: 18 -> 19; matrix products, arithmetic and copies ran while one was open for 5% -> 5% of each run, Pallas kernels for 6% -> 3%
where the time goes in v12:
time: 180 us; the launch traced here: 179 us
  waiting for transfers between devices  79.6 us (44%)
  starting transfers between devices  67.6 us (38%)
  Pallas kernels  20.8 us (12%)
  local copies, waits for them, and re-layouts  5.81 us (3%)
  other arithmetic  3.06 us (2%)
    ppermute x24, starting transfers between devices, y_shift(): return lax.ppermute(x, 'y', [(s, (s + k) % 4) for s in range(4)])  31.8 us
    ppermute x24, waiting for transfers between devices, y_shift(): return lax.ppermute(x, 'y', [(s, (s + k) % 4) for s in range(4)])  31.4 us
    all_to_all x1, waiting for transfers between devices, body(): back = lax.all_to_all(out, W, 0, 0, tiled=True)  19.1 us
    all_to_all x1, waiting for transfers between devices, body(): arrived = lax.all_to_all(rows, W, 0, 0, tiled=True)  13.5 us
    all_to_all x1, starting transfers between devices, body(): arrived = lax.all_to_all(rows, W, 0, 0, tiled=True)  11.6 us
    ppermute x5, waiting for transfers between devices, x_swap(): return lax.ppermute(x, 'xh', [(0, 1), (1, 0)])  10.3 us
    ppermute x5, starting transfers between devices, x_swap(): return lax.ppermute(x, 'xh', [(0, 1), (1, 0)])  8.8 us
    all_to_all x1, starting transfers between devices, body(): back = lax.all_to_all(out, W, 0, 0, tiled=True)  6.52 us
  transfers between devices with their start and end apart: 33, of which 19 were waited for; matrix products, arithmetic and copies ran while one was open for 5% of the time, Pallas kernels for 3%

profile of v12, /device:TPU:1, one launch (start us, length us, event | category | flops | bytes accessed | tf_op | source)
XLA Modules:
  0.0 179.2 jit_solution(18058221287619060333)
XLA Ops:
  0.7 5.5 %attention.1 = (bf16[128,512]{1,0:T(8,128)(2,1)}, bf16[128,512]{1,0:T(8,128)(2,1)}, bf16[128,512]{1,0:T(8,128)(2,1)}, bf16[128,512]{1,0:T(8,128)(2,1)}, bf16[2048,128]{1,0:T(8,128)(2,1)}) custom-call(s32[1]{0:T(128)} %bitcast.i_ref, s32[1]{0:T(128)} %bitcast.1.j_ref, s32[1]{0:T(128)} %bitcast.2.wide_ref, s32[3,32]{1,0:T(4,128)} %bitcast.42, ...), custom_call_target="tpu_custom_call" | custom-call | tf_op jit(solution)/shard_map/attention/pallas_call | solution.py:341
  6.2 3.7 %collective-permute-start.4 = (bf16[2048,128]{1,0:T(8,128)(2,1)}, bf16[2048,128]{1,0:T(8,128)(2,1)S(1)}, u32[]{:S(2)}, u32[]{:S(2)}) collective-permute-start(bf16[2048,128]{1,0:T(8,128)(2,1)} %get-tuple-element.37), channel_id=1, source_target_pairs={{0,4},{4,0},{1,5},{5,1},{2,6},{6,2},{3,7},{7,3},{8,12},{12,8},{9,1... | collective-permute-start | bytes 1572872 | tf_op jit(solution)/shard_map/ppermute | solution.py:31
  9.8 1.3 collective-permute-start
  11.1 2.6 %collective-permute-start.1 = (bf16[128,512]{1,0:T(8,128)(2,1)}, bf16[128,512]{1,0:T(8,128)(2,1)S(1)}, u32[]{:S(2)}, u32[]{:S(2)}) collective-permute-start(bf16[128,512]{1,0:T(8,128)(2,1)} %get-tuple-element.34), channel_id=1, source_target_pairs={{0,2},{1,3},{2,0},{3,1},{4,6},{5,7},{6,4},{7,5},{8,10},{9,11},{10,... | collective-permute-start | bytes 393224 | tf_op jit(solution)/shard_map/ppermute | solution.py:27
  13.7 1.1 collective-permute-start.2
  15.8 3.6 %collective-permute-done.1 = bf16[128,512]{1,0:T(8,128)(2,1)S(1)} collective-permute-done((bf16[128,512]{1,0:T(8,128)(2,1)}, bf16[128,512]{1,0:T(8,128)(2,1)S(1)}, u32[]{:S(2)}, u32[]{:S(2)}) %collective-permute-start.1) | collective-permute-done | bytes 131104 | tf_op jit(solution)/shard_map/ppermute | solution.py:27
  19.4 1.0 add_convert_fusion.own_ref
  20.5 5.3 %collective-permute-done.3.par_ref = bf16[128,512]{1,0:T(8,128)(2,1)S(1)} collective-permute-done((bf16[128,512]{1,0:T(8,128)(2,1)S(1)}, bf16[128,512]{1,0:T(8,128)(2,1)S(1)}, u32[]{:S(2)}, u32[]{:S(2)}) %collective-permute-start.3) | collective-permute-done | bytes 131104 | tf_op jit(solution)/shard_map/ppermute | solution.py:31
  25.8 1.7 dispatch.1
  27.5 11.6 %all-to-all-start = ((bf16[32,40,256]{2,1,0:T(8,128)(2,1)}), bf16[32,40,256]{2,1,0:T(8,128)(2,1)S(1)}, u32[]{:S(2)}, u32[]{:S(2)}) async-start(bf16[32,40,256]{2,1,0:T(8,128)(2,1)} %get-tuple-element.41), calls=%async_computation | async-start | bytes 1310720 | tf_op jit(solution)/shard_map/all_to_all | solution.py:407
  39.2 0.9 constant_dynamic-slice_fusion.6
  40.1 2.0 %collective-permute-start.17 = (bf16[2,128,512]{2,1,0:T(8,128)(2,1)}, bf16[2,128,512]{2,1,0:T(8,128)(2,1)}, u32[]{:S(2)}, u32[]{:S(2)}) collective-permute-start(bf16[2,128,512]{2,1,0:T(8,128)(2,1)} %get-tuple-element.66), channel_id=1, source_target_pairs={{0,3},{1,0},{2,1},{3,2},{4,7},{5,4},{6,5},{7,6},{8,11},{9,8},{10,9... | collective-permute-start | bytes 786440 | tf_op jit(solution)/shard_map/ppermute | solution.py:27
  45.2 13.5 %all-to-all-done.in_ref = bf16[32,40,256]{2,1,0:T(8,128)(2,1)S(1)} async-done(((bf16[32,40,256]{2,1,0:T(8,128)(2,1)}), bf16[32,40,256]{2,1,0:T(8,128)(2,1)S(1)}, u32[]{:S(2)}, u32[]{:S(2)}) %all-to-all-start) | async-done | bytes 655392 | tf_op jit(solution)/shard_map/all_to_all | solution.py:407
  58.9 2.1 %collective-permute-start.9 = (bf16[320,512]{1,0:T(8,128)(2,1)S(1)}, bf16[320,512]{1,0:T(8,128)(2,1)S(1)}, u32[]{:S(2)}, u32[]{:S(2)}) collective-permute-start(bf16[320,512]{1,0:T(8,128)(2,1)S(1)} %get-tuple-element.45.refs_4_), channel_id=1, source_target_pairs={{0,3},{1,0},{2,1},{3,2},{4,7},{5,4},{6,5},{7,6},{8,11},{9,8},{10,9... | collective-permute-start | bytes 983048 | tf_op jit(solution)/shard_map/ppermute | solution.py:27
  61.0 0.9 constant_dynamic-slice_fusion.2
  61.9 2.8 %collective-permute-start.6 = (bf16[320,512]{1,0:T(8,128)(2,1)S(1)}, bf16[320,512]{1,0:T(8,128)(2,1)S(1)}, u32[]{:S(2)}, u32[]{:S(2)}) collective-permute-start(bf16[320,512]{1,0:T(8,128)(2,1)S(1)} %get-tuple-element.44.refs_0_), channel_id=1, source_target_pairs={{0,3},{1,0},{2,1},{3,2},{4,7},{5,4},{6,5},{7,6},{8,11},{9,8},{10,9... | collective-permute-start | bytes 983048 | tf_op jit(solution)/shard_map/ppermute | solution.py:27
  64.6 1.7 collective-permute-start.11
  66.4 0.9 constant_dynamic-slice_fusion.3
  67.3 0.9 constant_dynamic-slice_fusion.4
  68.5 2.7 %collective-permute-start.10 = (bf16[320,512]{1,0:T(8,128)(2,1)S(1)}, bf16[320,512]{1,0:T(8,128)(2,1)S(1)}, u32[]{:S(2)}, u32[]{:S(2)}) collective-permute-start(bf16[320,512]{1,0:T(8,128)(2,1)S(1)} %collective-permute-done.9.refs_6_), channel_id=1, source_target_pairs={{0,3},{1,0},{2,1},{3,2},{4,7},{5,4},{6,5},{7,6},{8,11},{9,8},{10,9... | collective-permute-start | bytes 983048 | tf_op jit(solution)/shard_map/ppermute | solution.py:27
  71.2 1.0 pad_maximum_fusion
  72.2 1.7 collective-permute-done.6.refs_2_
  73.8 1.7 collective-permute-start.18
  76.4 1.2 collective-permute-done.11.refs_12_
  77.6 3.3 %collective-permute-done.10.refs_7_ = bf16[320,512]{1,0:T(8,128)(2,1)S(1)} collective-permute-done((bf16[320,512]{1,0:T(8,128)(2,1)S(1)}, bf16[320,512]{1,0:T(8,128)(2,1)S(1)}, u32[]{:S(2)}, u32[]{:S(2)}) %collective-permute-start.10) | collective-permute-done | bytes 327712 | tf_op jit(solution)/shard_map/ppermute | solution.py:27
  80.9 2.6 %collective-permute-done.7.refs_3_ = bf16[320,512]{1,0:T(8,128)(2,1)S(1)} collective-permute-done((bf16[320,512]{1,0:T(8,128)(2,1)S(1)}, bf16[320,512]{1,0:T(8,128)(2,1)S(1)}, u32[]{:S(2)}, u32[]{:S(2)}) %collective-permute-start.7) | collective-permute-done | bytes 327712 | tf_op jit(solution)/shard_map/ppermute | solution.py:27
  83.5 2.9 %gate_up.1.a0 = bf16[640,256]{1,0:T(8,128)(2,1)S(1)} custom-call(s32[4]{0:T(128)S(1)} %pad_add_fusion.here_ref, bf16[320,512]{1,0:T(8,128)(2,1)S(1)} %get-tuple-element.44.refs_0_, bf16[320,512]{1,0:T(8,128)(2,1)S(1)} %collective-permute-done.5.refs_1_, bf16[320,512]{1,0:T(8,128)(2,1)S(1)} %collective-permute-done.6.refs_2_, ...), custom_call_target="tpu_custom_call" | custom-call | tf_op jit(solution)/shard_map/gate_up/pallas_call | solution.py:422
  86.5 1.8 %collective-permute-start.13 = (bf16[640,256]{1,0:T(8,128)(2,1)S(1)}, bf16[640,256]{1,0:T(8,128)(2,1)S(1)}, u32[]{:S(2)}, u32[]{:S(2)}) collective-permute-start(bf16[640,256]{1,0:T(8,128)(2,1)S(1)} %gate_up.1.a0), channel_id=1, source_target_pairs={{0,2},{1,3},{2,0},{3,1},{4,6},{5,7},{6,4},{7,5},{8,10},{9,11},{10,... | collective-permute-start | bytes 983048 | tf_op jit(solution)/shard_map/ppermute | solution.py:27
  89.4 4.4 %collective-permute-done.12.a1 = bf16[640,256]{1,0:T(8,128)(2,1)S(1)} collective-permute-done((bf16[640,256]{1,0:T(8,128)(2,1)S(1)}, bf16[640,256]{1,0:T(8,128)(2,1)S(1)}, u32[]{:S(2)}, u32[]{:S(2)}) %collective-permute-start.12) | collective-permute-done | bytes 327712 | tf_op jit(solution)/shard_map/ppermute | solution.py:27
  93.8 7.1 %collective-permute-done.13.a2 = bf16[640,256]{1,0:T(8,128)(2,1)S(1)} collective-permute-done((bf16[640,256]{1,0:T(8,128)(2,1)S(1)}, bf16[640,256]{1,0:T(8,128)(2,1)S(1)}, u32[]{:S(2)}, u32[]{:S(2)}) %collective-permute-start.13) | collective-permute-done | bytes 327712 | tf_op jit(solution)/shard_map/ppermute | solution.py:27
  100.8 2.2 %collective-permute-done.14.a3 = bf16[640,256]{1,0:T(8,128)(2,1)S(1)} collective-permute-done((bf16[640,256]{1,0:T(8,128)(2,1)S(1)}, bf16[640,256]{1,0:T(8,128)(2,1)S(1)}, u32[]{:S(2)}, u32[]{:S(2)}) %collective-permute-start.14) | collective-permute-done | bytes 327712 | tf_op jit(solution)/shard_map/ppermute | solution.py:27
  103.0 3.6 %down.1 = bf16[32,40,256]{2,1,0:T(8,128)(2,1)} custom-call(s32[4]{0:T(128)S(1)} %pad_add_fusion.here_ref, bf16[640,256]{1,0:T(8,128)(2,1)S(1)} %gate_up.1.a0, bf16[640,256]{1,0:T(8,128)(2,1)S(1)} %collective-permute-done.12.a1, bf16[640,256]{1,0:T(8,128)(2,1)S(1)} %collective-permute-done.13.a2, bf16[640,256]{1,0:T(8,128)(2,1)S(1)} %collective-permute-done.14.a3, ...), custom_call_target="tpu_custom_call" | custom-call | tf_op jit(solution)/shard_map/down/pallas_call | solution.py:444
  107.3 4.0 %collective-permute-start.20 = (f32[128,128]{0,1:T(8,128)S(1)}, f32[128,128]{0,1:T(8,128)S(1)}, u32[]{:S(2)}, u32[]{:S(2)}) collective-permute-start(f32[128,128]{0,1:T(8,128)S(1)} %pad_maximum_fusion.1), channel_id=1, source_target_pairs={{0,2},{1,3},{2,0},{3,1},{4,6},{5,7},{6,4},{7,5},{8,10},{9,11},{10,... | collective-permute-start | bytes 196616 | tf_op jit(solution)/shard_map/ppermute | solution.py:27
  111.3 6.5 %all-to-all-start.1 = ((bf16[32,40,256]{2,1,0:T(8,128)(2,1)}), bf16[32,40,256]{2,1,0:T(8,128)(2,1)S(1)}, u32[]{:S(2)}, u32[]{:S(2)}) async-start(bf16[32,40,256]{2,1,0:T(8,128)(2,1)} %down.1), calls=%async_computation.1 | async-start | bytes 1310720 | tf_op jit(solution)/shard_map/all_to_all | solution.py:460
  118.3 19.1 %all-to-all-done.1 = bf16[32,40,256]{2,1,0:T(8,128)(2,1)S(1)} async-done(((bf16[32,40,256]{2,1,0:T(8,128)(2,1)}), bf16[32,40,256]{2,1,0:T(8,128)(2,1)S(1)}, u32[]{:S(2)}, u32[]{:S(2)}) %all-to-all-start.1) | async-done | bytes 655392 | tf_op jit(solution)/shard_map/all_to_all | solution.py:460
  138.3 1.6 collective-permute-start.22
  139.9 3.8 %collective-permute-done.22.par_ref = bf16[256,256]{1,0:T(8,128)(2,1)S(1)} collective-permute-done((bf16[256,256]{1,0:T(8,128)(2,1)S(1)}, bf16[256,256]{1,0:T(8,128)(2,1)S(1)}, u32[]{:S(2)}, u32[]{:S(2)}) %collective-permute-start.22) | collective-permute-done | bytes 131104 | tf_op jit(solution)/shard_map/ppermute | solution.py:31
  144.5 2.0 %collective-permute-start.23 = (bf16[144,128]{1,0:T(8,128)(2,1)S(1)}, bf16[144,128]{1,0:T(8,128)(2,1)S(1)}, u32[]{:S(2)}, u32[]{:S(2)}) collective-permute-start(bf16[144,128]{1,0:T(8,128)(2,1)S(1)} %get-tuple-element.52.p0), channel_id=1, source_target_pairs={{0,1},{1,2},{2,3},{3,0},{4,5},{5,6},{6,7},{7,4},{8,9},{9,10},{10,1... | collective-permute-start | bytes 110600 | tf_op jit(solution)/shard_map/ppermute | solution.py:27
  147.0 2.1 %collective-permute-start.25 = (bf16[144,128]{1,0:T(8,128)(2,1)S(1)}, bf16[144,128]{1,0:T(8,128)(2,1)S(1)}, u32[]{:S(2)}, u32[]{:S(2)}) collective-permute-start(bf16[144,128]{1,0:T(8,128)(2,1)S(1)} %get-tuple-element.52.p0), channel_id=1, source_target_pairs={{0,3},{1,0},{2,1},{3,2},{4,7},{5,4},{6,5},{7,6},{8,11},{9,8},{10,9... | collective-permute-start | bytes 110600 | tf_op jit(solution)/shard_map/ppermute | solution.py:27
  149.0 2.2 %collective-permute-done.24.p2 = bf16[144,128]{1,0:T(8,128)(2,1)S(1)} collective-permute-done((bf16[144,128]{1,0:T(8,128)(2,1)S(1)}, bf16[144,128]{1,0:T(8,128)(2,1)S(1)}, u32[]{:S(2)}, u32[]{:S(2)}) %collective-permute-start.24) | collective-permute-done | bytes 36896 | tf_op jit(solution)/shard_map/ppermute | solution.py:27
  151.2 1.0 vectors.1
  152.2 4.1 %all-to-all-start.2 = ((bf16[16,128,128]{2,1,0:T(8,128)(2,1)}), bf16[16,128,128]{2,1,0:T(8,128)(2,1)S(1)}, u32[]{:S(2)}, u32[]{:S(2)}) async-start(bf16[16,128,128]{2,1,0:T(8,128)(2,1)} %vectors.1), calls=%async_computation.2 | async-start | bytes 1048576 | tf_op jit(solution)/shard_map/all_to_all | solution.py:514
  157.3 3.3 %collective-permute-start.27 = (bf16[128,512]{1,0:T(8,128)(2,1)S(1)}, bf16[128,512]{1,0:T(8,128)(2,1)S(1)}, u32[]{:S(2)}, u32[]{:S(2)}) collective-permute-start(bf16[128,512]{1,0:T(8,128)(2,1)S(1)} %get-tuple-element.56.p0), channel_id=1, source_target_pairs={{0,2},{1,3},{2,0},{3,1},{4,6},{5,7},{6,4},{7,5},{8,10},{9,11},{10,... | collective-permute-start | bytes 393224 | tf_op jit(solution)/shard_map/ppermute | solution.py:27
  161.9 2.4 %collective-permute-done.27.p2 = bf16[128,512]{1,0:T(8,128)(2,1)S(1)} collective-permute-done((bf16[128,512]{1,0:T(8,128)(2,1)S(1)}, bf16[128,512]{1,0:T(8,128)(2,1)S(1)}, u32[]{:S(2)}, u32[]{:S(2)}) %collective-permute-start.27) | collective-permute-done | bytes 131104 | tf_op jit(solution)/shard_map/ppermute | solution.py:27
  164.7 5.1 %all-to-all-done.2 = bf16[16,128,128]{2,1,0:T(8,128)(2,1)S(1)} async-done(((bf16[16,128,128]{2,1,0:T(8,128)(2,1)}), bf16[16,128,128]{2,1,0:T(8,128)(2,1)S(1)}, u32[]{:S(2)}, u32[]{:S(2)}) %all-to-all-start.2) | async-done | bytes 524320 | tf_op jit(solution)/shard_map/all_to_all | solution.py:514
  169.8 4.7 %collective-permute-start.29 = (bf16[2048,128]{1,0:T(8,128)(2,1)S(1)}, bf16[2048,128]{1,0:T(8,128)(2,1)S(1)}, u32[]{:S(2)}, u32[]{:S(2)}) collective-permute-start(bf16[2048,128]{1,0:T(8,128)(2,1)S(1)} %bitcast.35), channel_id=1, source_target_pairs={{0,8},{8,0},{1,9},{9,1},{2,10},{10,2},{3,11},{11,3},{4,12},{12,4},... | collective-permute-start | bytes 1572872 | tf_op jit(solution)/shard_map/ppermute | solution.py:528
  174.6 1.4 assemble.1
  176.1 2.9 %score.1 = f32[1,16]{1,0:T(1,128)} custom-call(s32[5,16]{1,0:T(8,128)S(1)} %stack.48.info_ref, bf16[1024,128]{1,0:T(8,128)(2,1)S(1)} %copy-done.8, bf16[2048,128]{1,0:T(8,128)(2,1)S(1)} %bitcast.36, bf16[2048,128]{1,0:T(8,128)(2,1)S(1)} %collective-permute-done.29.other_ref), custom_call_target="tpu_custom_call" | custom-call | tf_op jit(solution)/shard_map/score/pallas_call | solution.py:537
  (97 shorter events, 12.4 us)
Async XLA Ops:
  0.6 88.5 %copy-start = (bf16[2048,64]{0,1:T(8,128)(2,1)S(1)}, bf16[2048,64]{0,1:T(8,128)(2,1)}, u32[]{:S(2)}) copy-start(bf16[2048,64]{0,1:T(8,128)(2,1)} %param.21) | copy-start | bytes 786436
  0.7 14.2 %copy-start.9 = (s32[128,8]{0,1:T(8,128)S(1)}, s32[128,8]{0,1:T(8,128)}, u32[]{:S(2)}) copy-start(s32[128,8]{0,1:T(8,128)} %param.22) | copy-start | bytes 12292
  0.7 25.1 %copy-start.3 = (bf16[128,2048]{1,0:T(8,128)(2,1)S(1)}, bf16[128,2048]{1,0:T(8,128)(2,1)}, u32[]{:S(2)}) copy-start(bf16[128,2048]{1,0:T(8,128)(2,1)} %x_ref.1) | copy-start | bytes 1572868
  6.2 19.6 %collective-permute-start.4 = (bf16[2048,128]{1,0:T(8,128)(2,1)}, bf16[2048,128]{1,0:T(8,128)(2,1)S(1)}, u32[]{:S(2)}, u32[]{:S(2)}) collective-permute-start(bf16[2048,128]{1,0:T(8,128)(2,1)} %get-tuple-element.37), channel_id=1, source_target_pairs={{0,4},{4,0},{1,5},{5,1},{2,6},{6,2},{3,7},{7,3},{8,12},{12,8},{9,1... | collective-permute-start | bytes 1572872 | tf_op jit(solution)/shard_map/ppermute | solution.py:31
  9.8 5.9 %collective-permute-start = (bf16[128,512]{1,0:T(8,128)(2,1)}, bf16[128,512]{1,0:T(8,128)(2,1)S(1)}, u32[]{:S(2)}, u32[]{:S(2)}) collective-permute-start(bf16[128,512]{1,0:T(8,128)(2,1)} %get-tuple-element.33), channel_id=1, source_target_pairs={{0,1},{1,2},{2,3},{3,0},{4,5},{5,6},{6,7},{7,4},{8,9},{9,10},{10,1... | collective-permute-start | bytes 393224 | tf_op jit(solution)/shard_map/ppermute | solution.py:27
  11.1 8.2 %collective-permute-start.1 = (bf16[128,512]{1,0:T(8,128)(2,1)}, bf16[128,512]{1,0:T(8,128)(2,1)S(1)}, u32[]{:S(2)}, u32[]{:S(2)}) collective-permute-start(bf16[128,512]{1,0:T(8,128)(2,1)} %get-tuple-element.34), channel_id=1, source_target_pairs={{0,2},{1,3},{2,0},{3,1},{4,6},{5,7},{6,4},{7,5},{8,10},{9,11},{10,... | collective-permute-start | bytes 393224 | tf_op jit(solution)/shard_map/ppermute | solution.py:27
  13.7 5.6 %collective-permute-start.2 = (bf16[128,512]{1,0:T(8,128)(2,1)}, bf16[128,512]{1,0:T(8,128)(2,1)S(1)}, u32[]{:S(2)}, u32[]{:S(2)}) collective-permute-start(bf16[128,512]{1,0:T(8,128)(2,1)} %get-tuple-element.35), channel_id=1, source_target_pairs={{0,3},{1,0},{2,1},{3,2},{4,7},{5,4},{6,5},{7,6},{8,11},{9,8},{10,9... | collective-permute-start | bytes 393224 | tf_op jit(solution)/shard_map/ppermute | solution.py:27
  20.3 18.8 %copy-start.10 = (bf16[2,128,2048]{2,1,0:T(8,128)(2,1)S(1)}, bf16[2,128,2048]{2,1,0:T(8,128)(2,1)}, u32[]{:S(2)}) copy-start(bf16[2,128,2048]{2,1,0:T(8,128)(2,1)} %param.25) | copy-start | bytes 3145732
  20.4 5.4 %collective-permute-start.3 = (bf16[128,512]{1,0:T(8,128)(2,1)S(1)}, bf16[128,512]{1,0:T(8,128)(2,1)S(1)}, u32[]{:S(2)}, u32[]{:S(2)}) collective-permute-start(bf16[128,512]{1,0:T(8,128)(2,1)S(1)} %add_convert_fusion.own_ref), channel_id=1, source_target_pairs={{0,4},{4,0},{1,5},{5,1},{2,6},{6,2},{3,7},{7,3},{8,12},{12,8},{9,1... | collective-permute-start | bytes 393224 | tf_op jit(solution)/shard_map/ppermute | solution.py:31
  25.8 1.7 copy-start.4
  27.5 31.2 %all-to-all-start = ((bf16[32,40,256]{2,1,0:T(8,128)(2,1)}), bf16[32,40,256]{2,1,0:T(8,128)(2,1)S(1)}, u32[]{:S(2)}, u32[]{:S(2)}) async-start(bf16[32,40,256]{2,1,0:T(8,128)(2,1)} %get-tuple-element.41), calls=%async_computation | async-start | bytes 1310720 | tf_op jit(solution)/shard_map/all_to_all | solution.py:407
  39.1 4.4 %copy-start.2 = (bf16[2,2048,128]{2,1,0:T(8,128)(2,1)S(1)}, bf16[2,2048,128]{2,1,0:T(8,128)(2,1)}, u32[]{:S(2)}) copy-start(bf16[2,2048,128]{2,1,0:T(8,128)(2,1)} %refs_10_.1) | copy-start | bytes 3145732
  39.2 6.0 %copy-start.7 = (f32[3,2048]{1,0:T(4,128)S(1)}, f32[3,2048]{1,0:T(4,128)}, u32[]{:S(2)}) copy-start(f32[3,2048]{1,0:T(4,128)} %gain_ref.3) | copy-start | bytes 73732
  40.1 20.9 %collective-permute-start.17 = (bf16[2,128,512]{2,1,0:T(8,128)(2,1)}, bf16[2,128,512]{2,1,0:T(8,128)(2,1)}, u32[]{:S(2)}, u32[]{:S(2)}) collective-permute-start(bf16[2,128,512]{2,1,0:T(8,128)(2,1)} %get-tuple-element.66), channel_id=1, source_target_pairs={{0,3},{1,0},{2,1},{3,2},{4,7},{5,4},{6,5},{7,6},{8,11},{9,8},{10,9... | collective-permute-start | bytes 786440 | tf_op jit(solution)/shard_map/ppermute | solution.py:27
  42.1 22.5 %collective-permute-start.16 = (bf16[2,128,512]{2,1,0:T(8,128)(2,1)}, bf16[2,128,512]{2,1,0:T(8,128)(2,1)}, u32[]{:S(2)}, u32[]{:S(2)}) collective-permute-start(bf16[2,128,512]{2,1,0:T(8,128)(2,1)} %get-tuple-element.67), channel_id=1, source_target_pairs={{0,2},{1,3},{2,0},{3,1},{4,6},{5,7},{6,4},{7,5},{8,10},{9,11},{10,... | collective-permute-start | bytes 786440 | tf_op jit(solution)/shard_map/ppermute | solution.py:27
  42.7 24.6 %collective-permute-start.15 = (bf16[2,128,512]{2,1,0:T(8,128)(2,1)}, bf16[2,128,512]{2,1,0:T(8,128)(2,1)}, u32[]{:S(2)}, u32[]{:S(2)}) collective-permute-start(bf16[2,128,512]{2,1,0:T(8,128)(2,1)} %get-tuple-element.68), channel_id=1, source_target_pairs={{0,1},{1,2},{2,3},{3,0},{4,5},{5,6},{6,7},{7,4},{8,9},{9,10},{10,1... | collective-permute-start | bytes 786440 | tf_op jit(solution)/shard_map/ppermute | solution.py:27
  45.2 38.3 %copy-start.1 = (bf16[2,2048,128]{2,1,0:T(8,128)(2,1)S(1)}, bf16[2,2048,128]{2,1,0:T(8,128)(2,1)}, u32[]{:S(2)}) copy-start(bf16[2,2048,128]{2,1,0:T(8,128)(2,1)} %refs_9_.1) | copy-start | bytes 3145732
  58.8 24.7 %copy-start.5 = (bf16[2048,128]{1,0:T(8,128)(2,1)S(1)}, bf16[2048,128]{1,0:T(8,128)(2,1)}, u32[]{:S(2)}) copy-start(bf16[2048,128]{1,0:T(8,128)(2,1)} %copy-done.4) | copy-start | bytes 1572868
  58.9 9.6 %collective-permute-start.9 = (bf16[320,512]{1,0:T(8,128)(2,1)S(1)}, bf16[320,512]{1,0:T(8,128)(2,1)S(1)}, u32[]{:S(2)}, u32[]{:S(2)}) collective-permute-start(bf16[320,512]{1,0:T(8,128)(2,1)S(1)} %get-tuple-element.45.refs_4_), channel_id=1, source_target_pairs={{0,3},{1,0},{2,1},{3,2},{4,7},{5,4},{6,5},{7,6},{8,11},{9,8},{10,9... | collective-permute-start | bytes 983048 | tf_op jit(solution)/shard_map/ppermute | solution.py:27
  61.0 10.2 %collective-permute-start.5 = (bf16[320,512]{1,0:T(8,128)(2,1)S(1)}, bf16[320,512]{1,0:T(8,128)(2,1)S(1)}, u32[]{:S(2)}, u32[]{:S(2)}) collective-permute-start(bf16[320,512]{1,0:T(8,128)(2,1)S(1)} %get-tuple-element.44.refs_0_), channel_id=1, source_target_pairs={{0,1},{1,2},{2,3},{3,0},{4,5},{5,6},{6,7},{7,4},{8,9},{9,10},{10,1... | collective-permute-start | bytes 983048 | tf_op jit(solution)/shard_map/ppermute | solution.py:27
  61.9 11.9 %collective-permute-start.6 = (bf16[320,512]{1,0:T(8,128)(2,1)S(1)}, bf16[320,512]{1,0:T(8,128)(2,1)S(1)}, u32[]{:S(2)}, u32[]{:S(2)}) collective-permute-start(bf16[320,512]{1,0:T(8,128)(2,1)S(1)} %get-tuple-element.44.refs_0_), channel_id=1, source_target_pairs={{0,3},{1,0},{2,1},{3,2},{4,7},{5,4},{6,5},{7,6},{8,11},{9,8},{10,9... | collective-permute-start | bytes 983048 | tf_op jit(solution)/shard_map/ppermute | solution.py:27
  64.6 12.9 %collective-permute-start.11 = (bf16[2048,128]{1,0:T(8,128)(2,1)}, bf16[2048,128]{1,0:T(8,128)(2,1)S(1)}, u32[]{:S(2)}, u32[]{:S(2)}) collective-permute-start(bf16[2048,128]{1,0:T(8,128)(2,1)} %dynamic-slice_bitcast_fusion), channel_id=1, source_target_pairs={{0,4},{4,0},{1,5},{5,1},{2,6},{6,2},{3,7},{7,3},{8,12},{12,8},{9,1... | collective-permute-start | bytes 1572872 | tf_op jit(solution)/shard_map/ppermute | solution.py:31
  68.2 8.2 %collective-permute-start.8 = (bf16[320,512]{1,0:T(8,128)(2,1)S(1)}, bf16[320,512]{1,0:T(8,128)(2,1)S(1)}, u32[]{:S(2)}, u32[]{:S(2)}) collective-permute-start(bf16[320,512]{1,0:T(8,128)(2,1)S(1)} %get-tuple-element.45.refs_4_), channel_id=1, source_target_pairs={{0,1},{1,2},{2,3},{3,0},{4,5},{5,6},{6,7},{7,4},{8,9},{9,10},{10,1... | collective-permute-start | bytes 983048 | tf_op jit(solution)/shard_map/ppermute | solution.py:27
  68.5 12.3 %collective-permute-start.10 = (bf16[320,512]{1,0:T(8,128)(2,1)S(1)}, bf16[320,512]{1,0:T(8,128)(2,1)S(1)}, u32[]{:S(2)}, u32[]{:S(2)}) collective-permute-start(bf16[320,512]{1,0:T(8,128)(2,1)S(1)} %collective-permute-done.9.refs_6_), channel_id=1, source_target_pairs={{0,3},{1,0},{2,1},{3,2},{4,7},{5,4},{6,5},{7,6},{8,11},{9,8},{10,9... | collective-permute-start | bytes 983048 | tf_op jit(solution)/shard_map/ppermute | solution.py:27
  71.2 12.3 %collective-permute-start.7 = (bf16[320,512]{1,0:T(8,128)(2,1)S(1)}, bf16[320,512]{1,0:T(8,128)(2,1)S(1)}, u32[]{:S(2)}, u32[]{:S(2)}) collective-permute-start(bf16[320,512]{1,0:T(8,128)(2,1)S(1)} %collective-permute-done.5.refs_1_), channel_id=1, source_target_pairs={{0,1},{1,2},{2,3},{3,0},{4,5},{5,6},{6,7},{7,4},{8,9},{9,10},{10,1... | collective-permute-start | bytes 983048 | tf_op jit(solution)/shard_map/ppermute | solution.py:27
  73.8 15.5 %collective-permute-start.18 = (bf16[4,128,512]{2,1,0:T(8,128)(2,1)S(1)}, bf16[4,128,512]{2,1,0:T(8,128)(2,1)S(1)}, u32[]{:S(2)}, u32[]{:S(2)}) collective-permute-start(bf16[4,128,512]{2,1,0:T(8,128)(2,1)S(1)} %pad_maximum_fusion), channel_id=1, source_target_pairs={{0,4},{4,0},{1,5},{5,1},{2,6},{6,2},{3,7},{7,3},{8,12},{12,8},{9,1... | collective-permute-start | bytes 1572872 | tf_op jit(solution)/shard_map/ppermute | solution.py:31
  86.4 7.4 %collective-permute-start.12 = (bf16[640,256]{1,0:T(8,128)(2,1)S(1)}, bf16[640,256]{1,0:T(8,128)(2,1)S(1)}, u32[]{:S(2)}, u32[]{:S(2)}) collective-permute-start(bf16[640,256]{1,0:T(8,128)(2,1)S(1)} %gate_up.1.a0), channel_id=1, source_target_pairs={{0,1},{1,2},{2,3},{3,0},{4,5},{5,6},{6,7},{7,4},{8,9},{9,10},{10,1... | collective-permute-start | bytes 983048 | tf_op jit(solution)/shard_map/ppermute | solution.py:27
  86.5 14.3 %collective-permute-start.13 = (bf16[640,256]{1,0:T(8,128)(2,1)S(1)}, bf16[640,256]{1,0:T(8,128)(2,1)S(1)}, u32[]{:S(2)}, u32[]{:S(2)}) collective-permute-start(bf16[640,256]{1,0:T(8,128)(2,1)S(1)} %gate_up.1.a0), channel_id=1, source_target_pairs={{0,2},{1,3},{2,0},{3,1},{4,6},{5,7},{6,4},{7,5},{8,10},{9,11},{10,... | collective-permute-start | bytes 983048 | tf_op jit(solution)/shard_map/ppermute | solution.py:27
  88.3 14.7 %collective-permute-start.14 = (bf16[640,256]{1,0:T(8,128)(2,1)S(1)}, bf16[640,256]{1,0:T(8,128)(2,1)S(1)}, u32[]{:S(2)}, u32[]{:S(2)}) collective-permute-start(bf16[640,256]{1,0:T(8,128)(2,1)S(1)} %gate_up.1.a0), channel_id=1, source_target_pairs={{0,3},{1,0},{2,1},{3,2},{4,7},{5,4},{6,5},{7,6},{8,11},{9,8},{10,9... | collective-permute-start | bytes 983048 | tf_op jit(solution)/shard_map/ppermute | solution.py:27
  106.7 11.2 %collective-permute-start.19 = (f32[128,128]{0,1:T(8,128)S(1)}, f32[128,128]{0,1:T(8,128)S(1)}, u32[]{:S(2)}, u32[]{:S(2)}) collective-permute-start(f32[128,128]{0,1:T(8,128)S(1)} %pad_maximum_fusion.1), channel_id=1, source_target_pairs={{0,1},{1,2},{2,3},{3,0},{4,5},{5,6},{6,7},{7,4},{8,9},{9,10},{10,1... | collective-permute-start | bytes 196616 | tf_op jit(solution)/shard_map/ppermute | solution.py:27
  107.3 10.6 %collective-permute-start.20 = (f32[128,128]{0,1:T(8,128)S(1)}, f32[128,128]{0,1:T(8,128)S(1)}, u32[]{:S(2)}, u32[]{:S(2)}) collective-permute-start(f32[128,128]{0,1:T(8,128)S(1)} %pad_maximum_fusion.1), channel_id=1, source_target_pairs={{0,2},{1,3},{2,0},{3,1},{4,6},{5,7},{6,4},{7,5},{8,10},{9,11},{10,... | collective-permute-start | bytes 196616 | tf_op jit(solution)/shard_map/ppermute | solution.py:27
  111.3 6.6 %collective-permute-start.21 = (f32[128,128]{0,1:T(8,128)S(1)}, f32[128,128]{0,1:T(8,128)S(1)}, u32[]{:S(2)}, u32[]{:S(2)}) collective-permute-start(f32[128,128]{0,1:T(8,128)S(1)} %pad_maximum_fusion.1), channel_id=1, source_target_pairs={{0,3},{1,0},{2,1},{3,2},{4,7},{5,4},{6,5},{7,6},{8,11},{9,8},{10,9... | collective-permute-start | bytes 196616 | tf_op jit(solution)/shard_map/ppermute | solution.py:27
  111.3 26.1 %all-to-all-start.1 = ((bf16[32,40,256]{2,1,0:T(8,128)(2,1)}), bf16[32,40,256]{2,1,0:T(8,128)(2,1)S(1)}, u32[]{:S(2)}, u32[]{:S(2)}) async-start(bf16[32,40,256]{2,1,0:T(8,128)(2,1)} %down.1), calls=%async_computation.1 | async-start | bytes 1310720 | tf_op jit(solution)/shard_map/all_to_all | solution.py:460
  137.9 5.9 %copy-start.6 = (bf16[2048,128]{1,0:T(8,128)(2,1)S(1)}, bf16[2048,128]{1,0:T(8,128)(2,1)}, u32[]{:S(2)}) copy-start(bf16[2048,128]{1,0:T(8,128)(2,1)} %w_ref.1) | copy-start | bytes 1572868
  138.3 18.1 %copy-start.11 = (s32[32,3]{0,1:T(4,128)S(1)}, s32[32,3]{0,1:T(4,128)}, u32[]{:S(2)}) copy-start(s32[32,3]{0,1:T(4,128)} %param.16) | copy-start | bytes 1156
  138.3 18.5 %copy-start.13 = (s32[1,16]{1,0:T(1,128)S(1)}, s32[1,16]{1,0:T(1,128)}, u32[]{:S(2)}) copy-start(s32[1,16]{1,0:T(1,128)} %param.29) | copy-start | bytes 196
  138.3 22.6 %copy-start.12 = (s32[1,1024]{1,0:T(1,128)S(1)}, s32[1,1024]{1,0:T(1,128)}, u32[]{:S(2)}) copy-start(s32[1,1024]{1,0:T(1,128)} %param.28) | copy-start | bytes 12292
  138.3 5.4 %collective-permute-start.22 = (bf16[256,256]{1,0:T(8,128)(2,1)S(1)}, bf16[256,256]{1,0:T(8,128)(2,1)S(1)}, u32[]{:S(2)}, u32[]{:S(2)}) collective-permute-start(bf16[256,256]{1,0:T(8,128)(2,1)S(1)} %fusion.2.moe_ref), channel_id=1, source_target_pairs={{0,4},{4,0},{1,5},{5,1},{2,6},{6,2},{3,7},{7,3},{8,12},{12,8},{9,1... | collective-permute-start | bytes 393224 | tf_op jit(solution)/shard_map/ppermute | solution.py:31
  144.5 31.6 %copy-start.8 = (bf16[1024,128]{1,0:T(8,128)(2,1)S(1)}, bf16[1024,128]{1,0:T(8,128)(2,1)}, u32[]{:S(2)}) copy-start(bf16[1024,128]{1,0:T(8,128)(2,1)} %doc_ref.1) | copy-start | bytes 786436
  144.5 4.5 %collective-permute-start.23 = (bf16[144,128]{1,0:T(8,128)(2,1)S(1)}, bf16[144,128]{1,0:T(8,128)(2,1)S(1)}, u32[]{:S(2)}, u32[]{:S(2)}) collective-permute-start(bf16[144,128]{1,0:T(8,128)(2,1)S(1)} %get-tuple-element.52.p0), channel_id=1, source_target_pairs={{0,1},{1,2},{2,3},{3,0},{4,5},{5,6},{6,7},{7,4},{8,9},{9,10},{10,1... | collective-permute-start | bytes 110600 | tf_op jit(solution)/shard_map/ppermute | solution.py:27
  146.5 4.7 %collective-permute-start.24 = (bf16[144,128]{1,0:T(8,128)(2,1)S(1)}, bf16[144,128]{1,0:T(8,128)(2,1)S(1)}, u32[]{:S(2)}, u32[]{:S(2)}) collective-permute-start(bf16[144,128]{1,0:T(8,128)(2,1)S(1)} %get-tuple-element.52.p0), channel_id=1, source_target_pairs={{0,2},{1,3},{2,0},{3,1},{4,6},{5,7},{6,4},{7,5},{8,10},{9,11},{10,... | collective-permute-start | bytes 110600 | tf_op jit(solution)/shard_map/ppermute | solution.py:27
  147.0 4.2 %collective-permute-start.25 = (bf16[144,128]{1,0:T(8,128)(2,1)S(1)}, bf16[144,128]{1,0:T(8,128)(2,1)S(1)}, u32[]{:S(2)}, u32[]{:S(2)}) collective-permute-start(bf16[144,128]{1,0:T(8,128)(2,1)S(1)} %get-tuple-element.52.p0), channel_id=1, source_target_pairs={{0,3},{1,0},{2,1},{3,2},{4,7},{5,4},{6,5},{7,6},{8,11},{9,8},{10,9... | collective-permute-start | bytes 110600 | tf_op jit(solution)/shard_map/ppermute | solution.py:27
  152.2 17.6 %all-to-all-start.2 = ((bf16[16,128,128]{2,1,0:T(8,128)(2,1)}), bf16[16,128,128]{2,1,0:T(8,128)(2,1)S(1)}, u32[]{:S(2)}, u32[]{:S(2)}) async-start(bf16[16,128,128]{2,1,0:T(8,128)(2,1)} %vectors.1), calls=%async_computation.2 | async-start | bytes 1048576 | tf_op jit(solution)/shard_map/all_to_all | solution.py:514
  156.8 5.1 %collective-permute-start.26 = (bf16[128,512]{1,0:T(8,128)(2,1)S(1)}, bf16[128,512]{1,0:T(8,128)(2,1)S(1)}, u32[]{:S(2)}, u32[]{:S(2)}) collective-permute-start(bf16[128,512]{1,0:T(8,128)(2,1)S(1)} %get-tuple-element.56.p0), channel_id=1, source_target_pairs={{0,1},{1,2},{2,3},{3,0},{4,5},{5,6},{6,7},{7,4},{8,9},{9,10},{10,1... | collective-permute-start | bytes 393224 | tf_op jit(solution)/shard_map/ppermute | solution.py:27
  157.3 7.1 %collective-permute-start.27 = (bf16[128,512]{1,0:T(8,128)(2,1)S(1)}, bf16[128,512]{1,0:T(8,128)(2,1)S(1)}, u32[]{:S(2)}, u32[]{:S(2)}) collective-permute-start(bf16[128,512]{1,0:T(8,128)(2,1)S(1)} %get-tuple-element.56.p0), channel_id=1, source_target_pairs={{0,2},{1,3},{2,0},{3,1},{4,6},{5,7},{6,4},{7,5},{8,10},{9,11},{10,... | collective-permute-start | bytes 393224 | tf_op jit(solution)/shard_map/ppermute | solution.py:27
  160.6 4.1 %collective-permute-start.28 = (bf16[128,512]{1,0:T(8,128)(2,1)S(1)}, bf16[128,512]{1,0:T(8,128)(2,1)S(1)}, u32[]{:S(2)}, u32[]{:S(2)}) collective-permute-start(bf16[128,512]{1,0:T(8,128)(2,1)S(1)} %get-tuple-element.56.p0), channel_id=1, source_target_pairs={{0,3},{1,0},{2,1},{3,2},{4,7},{5,4},{6,5},{7,6},{8,11},{9,8},{10,9... | collective-permute-start | bytes 393224 | tf_op jit(solution)/shard_map/ppermute | solution.py:27
  169.8 6.3 %collective-permute-start.29 = (bf16[2048,128]{1,0:T(8,128)(2,1)S(1)}, bf16[2048,128]{1,0:T(8,128)(2,1)S(1)}, u32[]{:S(2)}, u32[]{:S(2)}) collective-permute-start(bf16[2048,128]{1,0:T(8,128)(2,1)S(1)} %bitcast.35), channel_id=1, source_target_pairs={{0,8},{8,0},{1,9},{9,1},{2,10},{10,2},{3,11},{11,3},{4,12},{12,4},... | collective-permute-start | bytes 1572872 | tf_op jit(solution)/shard_map/ppermute | solution.py:528

commit v13 on v12

--- a/solution.py
+++ b/solution.py
@@ -404,6 +404,16 @@
         name="dispatch",
     )(here, tokens, attn, attn_par, choose)
 
+    hf = hidden.astype(f32)
+    gain_mine = lax.dynamic_slice_in_dim(norm_gains[1], j * 512, 512, 0)
+    router_mine = lax.dynamic_slice_in_dim(w_router, j * 512, 512, 0)
+    part = jnp.dot((hf * gain_mine).astype(bf16), router_mine, preferred_element_type=f32)
+    square = jnp.sum(hf * hf, axis=1, keepdims=True)
+    part = jnp.concatenate([part, jnp.broadcast_to(square, (TOK, EXPERTS))], axis=1)
+    whole = part
+    for k in (1, 2, 3):
+        whole = whole + y_shift(part, k)
+
     arrived = lax.all_to_all(rows, W, 0, 0, tiled=True)
     top, bottom = pl.pallas_call(
         unpack_kernel,
@@ -414,7 +424,9 @@
         compiler_params=params(),
         name="unpack",
     )(arrived)
-    top, bottom, up_sent = lax.optimization_barrier((top, bottom, pick(w_up, 1 - i)))
+    top, bottom, up_sent, whole = lax.optimization_barrier(
+        (top, bottom, pick(w_up, 1 - i), whole)
+    )
     up_par = x_swap(up_sent)
     top_back, bottom_ahead = y_shift(top, 1), y_shift(bottom, 3)
     bottom_back, top_ahead = y_shift(bottom, 1), y_shift(top, 3)
@@ -450,17 +462,8 @@
         compiler_params=params(),
         name="down",
     )(here, act, *(y_shift(act, k) for k in (1, 2, 3)), *downs, down_par)
-    hf = hidden.astype(f32)
-    gain_mine = lax.dynamic_slice_in_dim(norm_gains[1], j * 512, 512, 0)
-    router_mine = lax.dynamic_slice_in_dim(w_router, j * 512, 512, 0)
-    part = jnp.dot((hf * gain_mine).astype(bf16), router_mine, preferred_element_type=f32)
-    square = jnp.sum(hf * hf, axis=1, keepdims=True)
-    part = jnp.concatenate([part, jnp.broadcast_to(square, (TOK, EXPERTS))], axis=1)
-    out, part = lax.optimization_barrier((out, part))
     back = lax.all_to_all(out, W, 0, 0, tiled=True)
-    whole = part
-    for k in (1, 2, 3):
-        whole = whole + y_shift(part, k)
+
     logits = whole[:, :EXPERTS] * lax.rsqrt(whole[:, EXPERTS : EXPERTS + 1] / 2048.0 + EPS)
     lifted = jax.nn.sigmoid(logits)
     onehot = jnp.sum(

time: 180 us -> 176 us (0.978)
  waiting for transfers between devices: 79.6 us -> 74.2 us
    ppermute x5, waiting for transfers between devices: 10.3 us -> 5.5 us  [x_swap(): return lax.ppermute(x, 'xh', [(0, 1), (1, 0)])]
    all_to_all x1, waiting for transfers between devices: 13.5 us -> 9.76 us  [body(): arrived = lax.all_to_all(rows, W, 0, 0, tiled=True)]
    ppermute x24, waiting for transfers between devices: 31.4 us -> 33.8 us  [y_shift(): return lax.ppermute(x, 'y', [(s, (s + k) % 4) for s in range(4)])]
  transfers between devices with their start and end apart: 33 -> 33, of which waited for: 19 -> 20; matrix products, arithmetic and copies ran while one was open for 5% -> 6% of each run, Pallas kernels for 3% -> 4%
where the time goes in v13:
time: 176 us; the launch traced here: 175 us
  waiting for transfers between devices  74.2 us (42%)
  starting transfers between devices  67.9 us (39%)
  Pallas kernels  20 us (11%)
  local copies, waits for them, and re-layouts  7.55 us (4%)
  other arithmetic  3.11 us (2%)
    ppermute x24, waiting for transfers between devices, y_shift(): return lax.ppermute(x, 'y', [(s, (s + k) % 4) for s in range(4)])  33.8 us
    ppermute x24, starting transfers between devices, y_shift(): return lax.ppermute(x, 'y', [(s, (s + k) % 4) for s in range(4)])  30.8 us
    all_to_all x1, waiting for transfers between devices, body(): back = lax.all_to_all(out, W, 0, 0, tiled=True)  19.2 us
    all_to_all x1, starting transfers between devices, body(): arrived = lax.all_to_all(rows, W, 0, 0, tiled=True)  11.6 us
    all_to_all x1, waiting for transfers between devices, body(): arrived = lax.all_to_all(rows, W, 0, 0, tiled=True)  9.76 us
    ppermute x5, starting transfers between devices, x_swap(): return lax.ppermute(x, 'xh', [(0, 1), (1, 0)])  9.13 us
    all_to_all x1, starting transfers between devices, body(): back = lax.all_to_all(out, W, 0, 0, tiled=True)  6.74 us
    all_to_all x1, waiting for transfers between devices, body(): lax.all_to_all(vectors, ('z', 'xl'), 0, 0, tiled=True)  5.81 us
  transfers between devices with their start and end apart: 33, of which 20 were waited for; matrix products, arithmetic and copies ran while one was open for 6% of the time, Pallas kernels for 4%

profile of v13, /device:TPU:1, one launch (start us, length us, event | category | flops | bytes accessed | tf_op | source)
XLA Modules:
  0.0 175.1 jit_solution(10719892559611325638)
XLA Ops:
  0.7 5.5 %attention.1 = (bf16[128,512]{1,0:T(8,128)(2,1)}, bf16[128,512]{1,0:T(8,128)(2,1)}, bf16[128,512]{1,0:T(8,128)(2,1)}, bf16[128,512]{1,0:T(8,128)(2,1)}, bf16[2048,128]{1,0:T(8,128)(2,1)}) custom-call(s32[1]{0:T(128)} %bitcast.i_ref, s32[1]{0:T(128)} %bitcast.1.j_ref, s32[1]{0:T(128)} %bitcast.2.wide_ref, s32[3,32]{1,0:T(4,128)} %bitcast.42, ...), custom_call_target="tpu_custom_call" | custom-call | tf_op jit(solution)/shard_map/attention/pallas_call | solution.py:341
  6.2 3.7 %collective-permute-start.4 = (bf16[2048,128]{1,0:T(8,128)(2,1)}, bf16[2048,128]{1,0:T(8,128)(2,1)S(1)}, u32[]{:S(2)}, u32[]{:S(2)}) collective-permute-start(bf16[2048,128]{1,0:T(8,128)(2,1)} %get-tuple-element.36), channel_id=1, source_target_pairs={{0,4},{4,0},{1,5},{5,1},{2,6},{6,2},{3,7},{7,3},{8,12},{12,8},{9,1... | collective-permute-start | bytes 1572872 | tf_op jit(solution)/shard_map/ppermute | solution.py:31
  9.8 1.3 collective-permute-start
  11.1 2.6 %collective-permute-start.1 = (bf16[128,512]{1,0:T(8,128)(2,1)}, bf16[128,512]{1,0:T(8,128)(2,1)S(1)}, u32[]{:S(2)}, u32[]{:S(2)}) collective-permute-start(bf16[128,512]{1,0:T(8,128)(2,1)} %get-tuple-element.33), channel_id=1, source_target_pairs={{0,2},{1,3},{2,0},{3,1},{4,6},{5,7},{6,4},{7,5},{8,10},{9,11},{10,... | collective-permute-start | bytes 393224 | tf_op jit(solution)/shard_map/ppermute | solution.py:27
  13.8 1.1 collective-permute-start.2
  15.8 3.5 %collective-permute-done.1 = bf16[128,512]{1,0:T(8,128)(2,1)S(1)} collective-permute-done((bf16[128,512]{1,0:T(8,128)(2,1)}, bf16[128,512]{1,0:T(8,128)(2,1)S(1)}, u32[]{:S(2)}, u32[]{:S(2)}) %collective-permute-start.1) | collective-permute-done | bytes 131104 | tf_op jit(solution)/shard_map/ppermute | solution.py:27
  19.4 1.0 add_convert_fusion.own_ref
  21.5 2.4 %collective-permute-start.20 = (bf16[2,128,512]{2,1,0:T(8,128)(2,1)}, bf16[2,128,512]{2,1,0:T(8,128)(2,1)}, u32[]{:S(2)}, u32[]{:S(2)}) collective-permute-start(bf16[2,128,512]{2,1,0:T(8,128)(2,1)} %get-tuple-element.64), channel_id=1, source_target_pairs={{0,3},{1,0},{2,1},{3,2},{4,7},{5,4},{6,5},{7,6},{8,11},{9,8},{10,9... | collective-permute-start | bytes 786440 | tf_op jit(solution)/shard_map/ppermute | solution.py:27
  23.9 1.9 %collective-permute-done.3.par_ref = bf16[128,512]{1,0:T(8,128)(2,1)S(1)} collective-permute-done((bf16[128,512]{1,0:T(8,128)(2,1)S(1)}, bf16[128,512]{1,0:T(8,128)(2,1)S(1)}, u32[]{:S(2)}, u32[]{:S(2)}) %collective-permute-start.3) | collective-permute-done | bytes 131104 | tf_op jit(solution)/shard_map/ppermute | solution.py:31
  27.6 11.6 %all-to-all-start = ((bf16[32,40,256]{2,1,0:T(8,128)(2,1)}), bf16[32,40,256]{2,1,0:T(8,128)(2,1)S(1)}, u32[]{:S(2)}, u32[]{:S(2)}) async-start(bf16[32,40,256]{2,1,0:T(8,128)(2,1)} %copy-done.4), calls=%async_computation | async-start | bytes 1310720 | tf_op jit(solution)/shard_map/all_to_all | solution.py:417
  39.3 1.7 constant_dynamic-slice_fusion.3
  42.1 0.9 collective-permute-start.5
  43.0 2.3 %collective-permute-start.6 = (f32[128,128]{0,1:T(8,128)S(1)}, f32[128,128]{0,1:T(8,128)S(1)}, u32[]{:S(2)}, u32[]{:S(2)}) collective-permute-start(f32[128,128]{0,1:T(8,128)S(1)} %pad_maximum_fusion.1), channel_id=1, source_target_pairs={{0,2},{1,3},{2,0},{3,1},{4,6},{5,7},{6,4},{7,5},{8,10},{9,11},{10,... | collective-permute-start | bytes 196616 | tf_op jit(solution)/shard_map/ppermute | solution.py:27
  45.4 1.2 collective-permute-start.7
  47.0 1.8 %collective-permute-done.6 = f32[128,128]{0,1:T(8,128)S(1)} collective-permute-done((f32[128,128]{0,1:T(8,128)S(1)}, f32[128,128]{0,1:T(8,128)S(1)}, u32[]{:S(2)}, u32[]{:S(2)}) %collective-permute-start.6) | collective-permute-done | bytes 65568 | tf_op jit(solution)/shard_map/ppermute | solution.py:27
  49.1 9.8 %all-to-all-done.in_ref = bf16[32,40,256]{2,1,0:T(8,128)(2,1)S(1)} async-done(((bf16[32,40,256]{2,1,0:T(8,128)(2,1)}), bf16[32,40,256]{2,1,0:T(8,128)(2,1)S(1)}, u32[]{:S(2)}, u32[]{:S(2)}) %all-to-all-start) | async-done | bytes 655392 | tf_op jit(solution)/shard_map/all_to_all | solution.py:417
  59.0 0.9 collective-permute-start.8
  59.9 1.8 %collective-permute-start.12 = (bf16[320,512]{1,0:T(8,128)(2,1)S(1)}, bf16[320,512]{1,0:T(8,128)(2,1)S(1)}, u32[]{:S(2)}, u32[]{:S(2)}) collective-permute-start(bf16[320,512]{1,0:T(8,128)(2,1)S(1)} %get-tuple-element.46.refs_4_), channel_id=1, source_target_pairs={{0,3},{1,0},{2,1},{3,2},{4,7},{5,4},{6,5},{7,6},{8,11},{9,8},{10,9... | collective-permute-start | bytes 983048 | tf_op jit(solution)/shard_map/ppermute | solution.py:27
  62.8 1.8 %collective-permute-start.14 = (bf16[2048,128]{1,0:T(8,128)(2,1)}, bf16[2048,128]{1,0:T(8,128)(2,1)S(1)}, u32[]{:S(2)}, u32[]{:S(2)}) collective-permute-start(bf16[2048,128]{1,0:T(8,128)(2,1)} %dynamic-slice_bitcast_fusion), channel_id=1, source_target_pairs={{0,4},{4,0},{1,5},{5,1},{2,6},{6,2},{3,7},{7,3},{8,12},{12,8},{9,1... | collective-permute-start | bytes 1572872 | tf_op jit(solution)/shard_map/ppermute | solution.py:31
  66.4 2.6 %collective-permute-start.9 = (bf16[320,512]{1,0:T(8,128)(2,1)S(1)}, bf16[320,512]{1,0:T(8,128)(2,1)S(1)}, u32[]{:S(2)}, u32[]{:S(2)}) collective-permute-start(bf16[320,512]{1,0:T(8,128)(2,1)S(1)} %get-tuple-element.45.refs_0_), channel_id=1, source_target_pairs={{0,3},{1,0},{2,1},{3,2},{4,7},{5,4},{6,5},{7,6},{8,11},{9,8},{10,9... | collective-permute-start | bytes 983048 | tf_op jit(solution)/shard_map/ppermute | solution.py:27
  69.1 2.7 %collective-permute-start.13 = (bf16[320,512]{1,0:T(8,128)(2,1)S(1)}, bf16[320,512]{1,0:T(8,128)(2,1)S(1)}, u32[]{:S(2)}, u32[]{:S(2)}) collective-permute-start(bf16[320,512]{1,0:T(8,128)(2,1)S(1)} %collective-permute-done.12.refs_6_), channel_id=1, source_target_pairs={{0,3},{1,0},{2,1},{3,2},{4,7},{5,4},{6,5},{7,6},{8,11},{9,8},{10,9... | collective-permute-start | bytes 983048 | tf_op jit(solution)/shard_map/ppermute | solution.py:27
  71.8 1.0 pad_maximum_fusion
  72.7 2.4 %collective-permute-done.11.refs_5_ = bf16[320,512]{1,0:T(8,128)(2,1)S(1)} collective-permute-done((bf16[320,512]{1,0:T(8,128)(2,1)S(1)}, bf16[320,512]{1,0:T(8,128)(2,1)S(1)}, u32[]{:S(2)}, u32[]{:S(2)}) %collective-permute-start.11) | collective-permute-done | bytes 327712 | tf_op jit(solution)/shard_map/ppermute | solution.py:27
  75.1 1.7 collective-permute-start.21
  77.0 5.1 %collective-permute-done.10.refs_3_ = bf16[320,512]{1,0:T(8,128)(2,1)S(1)} collective-permute-done((bf16[320,512]{1,0:T(8,128)(2,1)S(1)}, bf16[320,512]{1,0:T(8,128)(2,1)S(1)}, u32[]{:S(2)}, u32[]{:S(2)}) %collective-permute-start.10) | collective-permute-done | bytes 327712 | tf_op jit(solution)/shard_map/ppermute | solution.py:27
  82.2 2.9 %gate_up.1.a0 = bf16[640,256]{1,0:T(8,128)(2,1)S(1)} custom-call(s32[4]{0:T(128)S(1)} %pad_add_fusion.here_ref, bf16[320,512]{1,0:T(8,128)(2,1)S(1)} %get-tuple-element.45.refs_0_, bf16[320,512]{1,0:T(8,128)(2,1)S(1)} %collective-permute-done.8.refs_1_, bf16[320,512]{1,0:T(8,128)(2,1)S(1)} %collective-permute-done.9.refs_2_, ...), custom_call_target="tpu_custom_call" | custom-call | tf_op jit(solution)/shard_map/gate_up/pallas_call | solution.py:434
  85.7 2.5 %collective-permute-start.16 = (bf16[640,256]{1,0:T(8,128)(2,1)S(1)}, bf16[640,256]{1,0:T(8,128)(2,1)S(1)}, u32[]{:S(2)}, u32[]{:S(2)}) collective-permute-start(bf16[640,256]{1,0:T(8,128)(2,1)S(1)} %gate_up.1.a0), channel_id=1, source_target_pairs={{0,2},{1,3},{2,0},{3,1},{4,6},{5,7},{6,4},{7,5},{8,10},{9,11},{10,... | collective-permute-start | bytes 983048 | tf_op jit(solution)/shard_map/ppermute | solution.py:27
  89.0 5.0 %collective-permute-done.15.a1 = bf16[640,256]{1,0:T(8,128)(2,1)S(1)} collective-permute-done((bf16[640,256]{1,0:T(8,128)(2,1)S(1)}, bf16[640,256]{1,0:T(8,128)(2,1)S(1)}, u32[]{:S(2)}, u32[]{:S(2)}) %collective-permute-start.15) | collective-permute-done | bytes 327712 | tf_op jit(solution)/shard_map/ppermute | solution.py:27
  94.0 5.3 %collective-permute-done.16.a2 = bf16[640,256]{1,0:T(8,128)(2,1)S(1)} collective-permute-done((bf16[640,256]{1,0:T(8,128)(2,1)S(1)}, bf16[640,256]{1,0:T(8,128)(2,1)S(1)}, u32[]{:S(2)}, u32[]{:S(2)}) %collective-permute-start.16) | collective-permute-done | bytes 327712 | tf_op jit(solution)/shard_map/ppermute | solution.py:27
  99.3 3.1 %collective-permute-done.17.a3 = bf16[640,256]{1,0:T(8,128)(2,1)S(1)} collective-permute-done((bf16[640,256]{1,0:T(8,128)(2,1)S(1)}, bf16[640,256]{1,0:T(8,128)(2,1)S(1)}, u32[]{:S(2)}, u32[]{:S(2)}) %collective-permute-start.17) | collective-permute-done | bytes 327712 | tf_op jit(solution)/shard_map/ppermute | solution.py:27
  102.4 3.6 %down.1 = bf16[32,40,256]{2,1,0:T(8,128)(2,1)} custom-call(s32[4]{0:T(128)S(1)} %pad_add_fusion.here_ref, bf16[640,256]{1,0:T(8,128)(2,1)S(1)} %gate_up.1.a0, bf16[640,256]{1,0:T(8,128)(2,1)S(1)} %collective-permute-done.15.a1, bf16[640,256]{1,0:T(8,128)(2,1)S(1)} %collective-permute-done.16.a2, bf16[640,256]{1,0:T(8,128)(2,1)S(1)} %collective-permute-done.17.a3, ...), custom_call_target="tpu_custom_call" | custom-call | tf_op jit(solution)/shard_map/down/pallas_call | solution.py:456
  106.1 6.7 %all-to-all-start.1 = ((bf16[32,40,256]{2,1,0:T(8,128)(2,1)}), bf16[32,40,256]{2,1,0:T(8,128)(2,1)S(1)}, u32[]{:S(2)}, u32[]{:S(2)}) async-start(bf16[32,40,256]{2,1,0:T(8,128)(2,1)} %down.1), calls=%async_computation.1 | async-start | bytes 1310720 | tf_op jit(solution)/shard_map/all_to_all | solution.py:465
  113.3 19.2 %all-to-all-done.1 = bf16[32,40,256]{2,1,0:T(8,128)(2,1)S(1)} async-done(((bf16[32,40,256]{2,1,0:T(8,128)(2,1)}), bf16[32,40,256]{2,1,0:T(8,128)(2,1)S(1)}, u32[]{:S(2)}, u32[]{:S(2)}) %all-to-all-start.1) | async-done | bytes 655392 | tf_op jit(solution)/shard_map/all_to_all | solution.py:465
  133.3 1.8 %collective-permute-start.22 = (bf16[256,256]{1,0:T(8,128)(2,1)S(1)}, bf16[256,256]{1,0:T(8,128)(2,1)S(1)}, u32[]{:S(2)}, u32[]{:S(2)}) collective-permute-start(bf16[256,256]{1,0:T(8,128)(2,1)S(1)} %fusion.2.moe_ref), channel_id=1, source_target_pairs={{0,4},{4,0},{1,5},{5,1},{2,6},{6,2},{3,7},{7,3},{8,12},{12,8},{9,1... | collective-permute-start | bytes 393224 | tf_op jit(solution)/shard_map/ppermute | solution.py:31
  135.1 3.6 %collective-permute-done.22.par_ref = bf16[256,256]{1,0:T(8,128)(2,1)S(1)} collective-permute-done((bf16[256,256]{1,0:T(8,128)(2,1)S(1)}, bf16[256,256]{1,0:T(8,128)(2,1)S(1)}, u32[]{:S(2)}, u32[]{:S(2)}) %collective-permute-start.22) | collective-permute-done | bytes 131104 | tf_op jit(solution)/shard_map/ppermute | solution.py:31
  139.5 1.1 collective-permute-start.23
  140.6 2.7 %collective-permute-start.24 = (bf16[144,128]{1,0:T(8,128)(2,1)S(1)}, bf16[144,128]{1,0:T(8,128)(2,1)S(1)}, u32[]{:S(2)}, u32[]{:S(2)}) collective-permute-start(bf16[144,128]{1,0:T(8,128)(2,1)S(1)} %get-tuple-element.50.p0), channel_id=1, source_target_pairs={{0,2},{1,3},{2,0},{3,1},{4,6},{5,7},{6,4},{7,5},{8,10},{9,11},{10,... | collective-permute-start | bytes 110600 | tf_op jit(solution)/shard_map/ppermute | solution.py:27
  143.8 1.3 collective-permute-done.24.p2
  145.0 1.1 collective-permute-done.25.p3
  146.1 1.0 vectors.1
  147.1 5.1 %all-to-all-start.2 = ((bf16[16,128,128]{2,1,0:T(8,128)(2,1)}), bf16[16,128,128]{2,1,0:T(8,128)(2,1)S(1)}, u32[]{:S(2)}, u32[]{:S(2)}) async-start(bf16[16,128,128]{2,1,0:T(8,128)(2,1)} %vectors.1), calls=%async_computation.2 | async-start | bytes 1048576 | tf_op jit(solution)/shard_map/all_to_all | solution.py:517
  152.8 1.8 %collective-permute-start.27 = (bf16[128,512]{1,0:T(8,128)(2,1)S(1)}, bf16[128,512]{1,0:T(8,128)(2,1)S(1)}, u32[]{:S(2)}, u32[]{:S(2)}) collective-permute-start(bf16[128,512]{1,0:T(8,128)(2,1)S(1)} %get-tuple-element.54.p0), channel_id=1, source_target_pairs={{0,2},{1,3},{2,0},{3,1},{4,6},{5,7},{6,4},{7,5},{8,10},{9,11},{10,... | collective-permute-start | bytes 393224 | tf_op jit(solution)/shard_map/ppermute | solution.py:27
  154.6 1.2 collective-permute-start.28
  156.1 3.1 %collective-permute-done.26.p1 = bf16[128,512]{1,0:T(8,128)(2,1)S(1)} collective-permute-done((bf16[128,512]{1,0:T(8,128)(2,1)S(1)}, bf16[128,512]{1,0:T(8,128)(2,1)S(1)}, u32[]{:S(2)}, u32[]{:S(2)}) %collective-permute-start.26) | collective-permute-done | bytes 131104 | tf_op jit(solution)/shard_map/ppermute | solution.py:27
  160.1 5.8 %all-to-all-done.2 = bf16[16,128,128]{2,1,0:T(8,128)(2,1)S(1)} async-done(((bf16[16,128,128]{2,1,0:T(8,128)(2,1)}), bf16[16,128,128]{2,1,0:T(8,128)(2,1)S(1)}, u32[]{:S(2)}, u32[]{:S(2)}) %all-to-all-start.2) | async-done | bytes 524320 | tf_op jit(solution)/shard_map/all_to_all | solution.py:517
  166.0 4.5 %collective-permute-start.29 = (bf16[2048,128]{1,0:T(8,128)(2,1)S(1)}, bf16[2048,128]{1,0:T(8,128)(2,1)S(1)}, u32[]{:S(2)}, u32[]{:S(2)}) collective-permute-start(bf16[2048,128]{1,0:T(8,128)(2,1)S(1)} %bitcast.35), channel_id=1, source_target_pairs={{0,8},{8,0},{1,9},{9,1},{2,10},{10,2},{3,11},{11,3},{4,12},{12,4},... | collective-permute-start | bytes 1572872 | tf_op jit(solution)/shard_map/ppermute | solution.py:531
  170.5 1.4 assemble.1
  172.0 2.9 %score.1 = f32[1,16]{1,0:T(1,128)} custom-call(s32[5,16]{1,0:T(8,128)S(1)} %stack.48.info_ref, bf16[1024,128]{1,0:T(8,128)(2,1)S(1)} %copy-done.9, bf16[2048,128]{1,0:T(8,128)(2,1)S(1)} %bitcast.36, bf16[2048,128]{1,0:T(8,128)(2,1)S(1)} %collective-permute-done.29.other_ref), custom_call_target="tpu_custom_call" | custom-call | tf_op jit(solution)/shard_map/score/pallas_call | solution.py:540
  (99 shorter events, 14.5 us)
Async XLA Ops:
  0.6 41.3 %copy-start = (bf16[2048,64]{0,1:T(8,128)(2,1)S(1)}, bf16[2048,64]{0,1:T(8,128)(2,1)}, u32[]{:S(2)}) copy-start(bf16[2048,64]{0,1:T(8,128)(2,1)} %param.21) | copy-start | bytes 786436
  0.7 14.2 %copy-start.10 = (s32[128,8]{0,1:T(8,128)S(1)}, s32[128,8]{0,1:T(8,128)}, u32[]{:S(2)}) copy-start(s32[128,8]{0,1:T(8,128)} %param.22) | copy-start | bytes 12292
  0.7 19.9 %copy-start.11 = (bf16[2,128,2048]{2,1,0:T(8,128)(2,1)S(1)}, bf16[2,128,2048]{2,1,0:T(8,128)(2,1)}, u32[]{:S(2)}) copy-start(bf16[2,128,2048]{2,1,0:T(8,128)(2,1)} %param.25) | copy-start | bytes 3145732
  6.2 19.7 %collective-permute-start.4 = (bf16[2048,128]{1,0:T(8,128)(2,1)}, bf16[2048,128]{1,0:T(8,128)(2,1)S(1)}, u32[]{:S(2)}, u32[]{:S(2)}) collective-permute-start(bf16[2048,128]{1,0:T(8,128)(2,1)} %get-tuple-element.36), channel_id=1, source_target_pairs={{0,4},{4,0},{1,5},{5,1},{2,6},{6,2},{3,7},{7,3},{8,12},{12,8},{9,1... | collective-permute-start | bytes 1572872 | tf_op jit(solution)/shard_map/ppermute | solution.py:31
  9.8 6.0 %collective-permute-start = (bf16[128,512]{1,0:T(8,128)(2,1)}, bf16[128,512]{1,0:T(8,128)(2,1)S(1)}, u32[]{:S(2)}, u32[]{:S(2)}) collective-permute-start(bf16[128,512]{1,0:T(8,128)(2,1)} %get-tuple-element.32), channel_id=1, source_target_pairs={{0,1},{1,2},{2,3},{3,0},{4,5},{5,6},{6,7},{7,4},{8,9},{9,10},{10,1... | collective-permute-start | bytes 393224 | tf_op jit(solution)/shard_map/ppermute | solution.py:27
  11.1 8.2 %collective-permute-start.1 = (bf16[128,512]{1,0:T(8,128)(2,1)}, bf16[128,512]{1,0:T(8,128)(2,1)S(1)}, u32[]{:S(2)}, u32[]{:S(2)}) collective-permute-start(bf16[128,512]{1,0:T(8,128)(2,1)} %get-tuple-element.33), channel_id=1, source_target_pairs={{0,2},{1,3},{2,0},{3,1},{4,6},{5,7},{6,4},{7,5},{8,10},{9,11},{10,... | collective-permute-start | bytes 393224 | tf_op jit(solution)/shard_map/ppermute | solution.py:27
  13.8 5.6 %collective-permute-start.2 = (bf16[128,512]{1,0:T(8,128)(2,1)}, bf16[128,512]{1,0:T(8,128)(2,1)S(1)}, u32[]{:S(2)}, u32[]{:S(2)}) collective-permute-start(bf16[128,512]{1,0:T(8,128)(2,1)} %get-tuple-element.34), channel_id=1, source_target_pairs={{0,3},{1,0},{2,1},{3,2},{4,7},{5,4},{6,5},{7,6},{8,11},{9,8},{10,9... | collective-permute-start | bytes 393224 | tf_op jit(solution)/shard_map/ppermute | solution.py:27
  19.4 4.5 %copy-start.8 = (f32[3,2048]{1,0:T(4,128)S(1)}, f32[3,2048]{1,0:T(4,128)}, u32[]{:S(2)}) copy-start(f32[3,2048]{1,0:T(4,128)} %gain_ref.3) | copy-start | bytes 73732
  19.4 6.5 %copy-start.3 = (bf16[128,2048]{1,0:T(8,128)(2,1)S(1)}, bf16[128,2048]{1,0:T(8,128)(2,1)}, u32[]{:S(2)}) copy-start(bf16[128,2048]{1,0:T(8,128)(2,1)} %x_ref.1) | copy-start | bytes 1572868
  20.4 5.4 %collective-permute-start.3 = (bf16[128,512]{1,0:T(8,128)(2,1)S(1)}, bf16[128,512]{1,0:T(8,128)(2,1)S(1)}, u32[]{:S(2)}, u32[]{:S(2)}) collective-permute-start(bf16[128,512]{1,0:T(8,128)(2,1)S(1)} %add_convert_fusion.own_ref), channel_id=1, source_target_pairs={{0,4},{4,0},{1,5},{5,1},{2,6},{6,2},{3,7},{7,3},{8,12},{12,8},{9,1... | collective-permute-start | bytes 393224 | tf_op jit(solution)/shard_map/ppermute | solution.py:31
  21.5 19.5 %copy-start.2 = (bf16[2,2048,128]{2,1,0:T(8,128)(2,1)S(1)}, bf16[2,2048,128]{2,1,0:T(8,128)(2,1)}, u32[]{:S(2)}) copy-start(bf16[2,2048,128]{2,1,0:T(8,128)(2,1)} %refs_10_.1) | copy-start | bytes 3145732
  21.5 40.3 %collective-permute-start.20 = (bf16[2,128,512]{2,1,0:T(8,128)(2,1)}, bf16[2,128,512]{2,1,0:T(8,128)(2,1)}, u32[]{:S(2)}, u32[]{:S(2)}) collective-permute-start(bf16[2,128,512]{2,1,0:T(8,128)(2,1)} %get-tuple-element.64), channel_id=1, source_target_pairs={{0,3},{1,0},{2,1},{3,2},{4,7},{5,4},{6,5},{7,6},{8,11},{9,8},{10,9... | collective-permute-start | bytes 786440 | tf_op jit(solution)/shard_map/ppermute | solution.py:27
  23.9 38.9 %collective-permute-start.19 = (bf16[2,128,512]{2,1,0:T(8,128)(2,1)}, bf16[2,128,512]{2,1,0:T(8,128)(2,1)}, u32[]{:S(2)}, u32[]{:S(2)}) collective-permute-start(bf16[2,128,512]{2,1,0:T(8,128)(2,1)} %get-tuple-element.65), channel_id=1, source_target_pairs={{0,2},{1,3},{2,0},{3,1},{4,6},{5,7},{6,4},{7,5},{8,10},{9,11},{10,... | collective-permute-start | bytes 786440 | tf_op jit(solution)/shard_map/ppermute | solution.py:27
  25.9 1.8 %copy-start.5 = (bf16[2048,128]{1,0:T(8,128)(2,1)}, bf16[2048,128]{1,0:T(8,128)(2,1)S(1)}, u32[]{:S(2)}) copy-start(bf16[2048,128]{1,0:T(8,128)(2,1)S(1)} %collective-permute-done.4.refs_11_) | copy-start | bytes 1572868
  26.8 0.8 copy-start.4
  27.6 31.2 %all-to-all-start = ((bf16[32,40,256]{2,1,0:T(8,128)(2,1)}), bf16[32,40,256]{2,1,0:T(8,128)(2,1)S(1)}, u32[]{:S(2)}, u32[]{:S(2)}) async-start(bf16[32,40,256]{2,1,0:T(8,128)(2,1)} %copy-done.4), calls=%async_computation | async-start | bytes 1310720 | tf_op jit(solution)/shard_map/all_to_all | solution.py:417
  42.1 4.7 %collective-permute-start.5 = (f32[128,128]{0,1:T(8,128)S(1)}, f32[128,128]{0,1:T(8,128)S(1)}, u32[]{:S(2)}, u32[]{:S(2)}) collective-permute-start(f32[128,128]{0,1:T(8,128)S(1)} %pad_maximum_fusion.1), channel_id=1, source_target_pairs={{0,1},{1,2},{2,3},{3,0},{4,5},{5,6},{6,7},{7,4},{8,9},{9,10},{10,1... | collective-permute-start | bytes 196616 | tf_op jit(solution)/shard_map/ppermute | solution.py:27
  43.0 5.7 %collective-permute-start.6 = (f32[128,128]{0,1:T(8,128)S(1)}, f32[128,128]{0,1:T(8,128)S(1)}, u32[]{:S(2)}, u32[]{:S(2)}) collective-permute-start(f32[128,128]{0,1:T(8,128)S(1)} %pad_maximum_fusion.1), channel_id=1, source_target_pairs={{0,2},{1,3},{2,0},{3,1},{4,6},{5,7},{6,4},{7,5},{8,10},{9,11},{10,... | collective-permute-start | bytes 196616 | tf_op jit(solution)/shard_map/ppermute | solution.py:27
  45.4 3.7 %collective-permute-start.7 = (f32[128,128]{0,1:T(8,128)S(1)}, f32[128,128]{0,1:T(8,128)S(1)}, u32[]{:S(2)}, u32[]{:S(2)}) collective-permute-start(f32[128,128]{0,1:T(8,128)S(1)} %pad_maximum_fusion.1), channel_id=1, source_target_pairs={{0,3},{1,0},{2,1},{3,2},{4,7},{5,4},{6,5},{7,6},{8,11},{9,8},{10,9... | collective-permute-start | bytes 196616 | tf_op jit(solution)/shard_map/ppermute | solution.py:27
  46.9 18.6 %collective-permute-start.18 = (bf16[2,128,512]{2,1,0:T(8,128)(2,1)}, bf16[2,128,512]{2,1,0:T(8,128)(2,1)}, u32[]{:S(2)}, u32[]{:S(2)}) collective-permute-start(bf16[2,128,512]{2,1,0:T(8,128)(2,1)} %get-tuple-element.66), channel_id=1, source_target_pairs={{0,1},{1,2},{2,3},{3,0},{4,5},{5,6},{6,7},{7,4},{8,9},{9,10},{10,1... | collective-permute-start | bytes 786440 | tf_op jit(solution)/shard_map/ppermute | solution.py:27
  49.1 33.1 %copy-start.1 = (bf16[2,2048,128]{2,1,0:T(8,128)(2,1)S(1)}, bf16[2,2048,128]{2,1,0:T(8,128)(2,1)}, u32[]{:S(2)}) copy-start(bf16[2,2048,128]{2,1,0:T(8,128)(2,1)} %refs_9_.1) | copy-start | bytes 3145732
  58.9 23.3 %copy-start.6 = (bf16[2048,128]{1,0:T(8,128)(2,1)S(1)}, bf16[2048,128]{1,0:T(8,128)(2,1)}, u32[]{:S(2)}) copy-start(bf16[2048,128]{1,0:T(8,128)(2,1)} %copy-done.5) | copy-start | bytes 1572868
  59.0 10.1 %collective-permute-start.8 = (bf16[320,512]{1,0:T(8,128)(2,1)S(1)}, bf16[320,512]{1,0:T(8,128)(2,1)S(1)}, u32[]{:S(2)}, u32[]{:S(2)}) collective-permute-start(bf16[320,512]{1,0:T(8,128)(2,1)S(1)} %get-tuple-element.45.refs_0_), channel_id=1, source_target_pairs={{0,1},{1,2},{2,3},{3,0},{4,5},{5,6},{6,7},{7,4},{8,9},{9,10},{10,1... | collective-permute-start | bytes 983048 | tf_op jit(solution)/shard_map/ppermute | solution.py:27
  59.9 9.2 %collective-permute-start.12 = (bf16[320,512]{1,0:T(8,128)(2,1)S(1)}, bf16[320,512]{1,0:T(8,128)(2,1)S(1)}, u32[]{:S(2)}, u32[]{:S(2)}) collective-permute-start(bf16[320,512]{1,0:T(8,128)(2,1)S(1)} %get-tuple-element.46.refs_4_), channel_id=1, source_target_pairs={{0,3},{1,0},{2,1},{3,2},{4,7},{5,4},{6,5},{7,6},{8,11},{9,8},{10,9... | collective-permute-start | bytes 983048 | tf_op jit(solution)/shard_map/ppermute | solution.py:27
  62.7 12.5 %collective-permute-start.11 = (bf16[320,512]{1,0:T(8,128)(2,1)S(1)}, bf16[320,512]{1,0:T(8,128)(2,1)S(1)}, u32[]{:S(2)}, u32[]{:S(2)}) collective-permute-start(bf16[320,512]{1,0:T(8,128)(2,1)S(1)} %get-tuple-element.46.refs_4_), channel_id=1, source_target_pairs={{0,1},{1,2},{2,3},{3,0},{4,5},{5,6},{6,7},{7,4},{8,9},{9,10},{10,1... | collective-permute-start | bytes 983048 | tf_op jit(solution)/shard_map/ppermute | solution.py:27
  62.8 14.3 %collective-permute-start.14 = (bf16[2048,128]{1,0:T(8,128)(2,1)}, bf16[2048,128]{1,0:T(8,128)(2,1)S(1)}, u32[]{:S(2)}, u32[]{:S(2)}) collective-permute-start(bf16[2048,128]{1,0:T(8,128)(2,1)} %dynamic-slice_bitcast_fusion), channel_id=1, source_target_pairs={{0,4},{4,0},{1,5},{5,1},{2,6},{6,2},{3,7},{7,3},{8,12},{12,8},{9,1... | collective-permute-start | bytes 1572872 | tf_op jit(solution)/shard_map/ppermute | solution.py:31
  66.4 10.6 %collective-permute-start.9 = (bf16[320,512]{1,0:T(8,128)(2,1)S(1)}, bf16[320,512]{1,0:T(8,128)(2,1)S(1)}, u32[]{:S(2)}, u32[]{:S(2)}) collective-permute-start(bf16[320,512]{1,0:T(8,128)(2,1)S(1)} %get-tuple-element.45.refs_0_), channel_id=1, source_target_pairs={{0,3},{1,0},{2,1},{3,2},{4,7},{5,4},{6,5},{7,6},{8,11},{9,8},{10,9... | collective-permute-start | bytes 983048 | tf_op jit(solution)/shard_map/ppermute | solution.py:27
  69.1 13.1 %collective-permute-start.10 = (bf16[320,512]{1,0:T(8,128)(2,1)S(1)}, bf16[320,512]{1,0:T(8,128)(2,1)S(1)}, u32[]{:S(2)}, u32[]{:S(2)}) collective-permute-start(bf16[320,512]{1,0:T(8,128)(2,1)S(1)} %collective-permute-done.8.refs_1_), channel_id=1, source_target_pairs={{0,1},{1,2},{2,3},{3,0},{4,5},{5,6},{6,7},{7,4},{8,9},{9,10},{10,1... | collective-permute-start | bytes 983048 | tf_op jit(solution)/shard_map/ppermute | solution.py:27
  69.1 13.1 %collective-permute-start.13 = (bf16[320,512]{1,0:T(8,128)(2,1)S(1)}, bf16[320,512]{1,0:T(8,128)(2,1)S(1)}, u32[]{:S(2)}, u32[]{:S(2)}) collective-permute-start(bf16[320,512]{1,0:T(8,128)(2,1)S(1)} %collective-permute-done.12.refs_6_), channel_id=1, source_target_pairs={{0,3},{1,0},{2,1},{3,2},{4,7},{5,4},{6,5},{7,6},{8,11},{9,8},{10,9... | collective-permute-start | bytes 983048 | tf_op jit(solution)/shard_map/ppermute | solution.py:27
  75.1 13.9 %collective-permute-start.21 = (bf16[4,128,512]{2,1,0:T(8,128)(2,1)S(1)}, bf16[4,128,512]{2,1,0:T(8,128)(2,1)S(1)}, u32[]{:S(2)}, u32[]{:S(2)}) collective-permute-start(bf16[4,128,512]{2,1,0:T(8,128)(2,1)S(1)} %pad_maximum_fusion), channel_id=1, source_target_pairs={{0,4},{4,0},{1,5},{5,1},{2,6},{6,2},{3,7},{7,3},{8,12},{12,8},{9,1... | collective-permute-start | bytes 1572872 | tf_op jit(solution)/shard_map/ppermute | solution.py:31
  85.1 8.9 %collective-permute-start.15 = (bf16[640,256]{1,0:T(8,128)(2,1)S(1)}, bf16[640,256]{1,0:T(8,128)(2,1)S(1)}, u32[]{:S(2)}, u32[]{:S(2)}) collective-permute-start(bf16[640,256]{1,0:T(8,128)(2,1)S(1)} %gate_up.1.a0), channel_id=1, source_target_pairs={{0,1},{1,2},{2,3},{3,0},{4,5},{5,6},{6,7},{7,4},{8,9},{9,10},{10,1... | collective-permute-start | bytes 983048 | tf_op jit(solution)/shard_map/ppermute | solution.py:27
  85.7 13.6 %collective-permute-start.16 = (bf16[640,256]{1,0:T(8,128)(2,1)S(1)}, bf16[640,256]{1,0:T(8,128)(2,1)S(1)}, u32[]{:S(2)}, u32[]{:S(2)}) collective-permute-start(bf16[640,256]{1,0:T(8,128)(2,1)S(1)} %gate_up.1.a0), channel_id=1, source_target_pairs={{0,2},{1,3},{2,0},{3,1},{4,6},{5,7},{6,4},{7,5},{8,10},{9,11},{10,... | collective-permute-start | bytes 983048 | tf_op jit(solution)/shard_map/ppermute | solution.py:27
  88.2 14.2 %collective-permute-start.17 = (bf16[640,256]{1,0:T(8,128)(2,1)S(1)}, bf16[640,256]{1,0:T(8,128)(2,1)S(1)}, u32[]{:S(2)}, u32[]{:S(2)}) collective-permute-start(bf16[640,256]{1,0:T(8,128)(2,1)S(1)} %gate_up.1.a0), channel_id=1, source_target_pairs={{0,3},{1,0},{2,1},{3,2},{4,7},{5,4},{6,5},{7,6},{8,11},{9,8},{10,9... | collective-permute-start | bytes 983048 | tf_op jit(solution)/shard_map/ppermute | solution.py:27
  106.1 26.4 %all-to-all-start.1 = ((bf16[32,40,256]{2,1,0:T(8,128)(2,1)}), bf16[32,40,256]{2,1,0:T(8,128)(2,1)S(1)}, u32[]{:S(2)}, u32[]{:S(2)}) async-start(bf16[32,40,256]{2,1,0:T(8,128)(2,1)} %down.1), calls=%async_computation.1 | async-start | bytes 1310720 | tf_op jit(solution)/shard_map/all_to_all | solution.py:465
  132.8 5.9 %copy-start.7 = (bf16[2048,128]{1,0:T(8,128)(2,1)S(1)}, bf16[2048,128]{1,0:T(8,128)(2,1)}, u32[]{:S(2)}) copy-start(bf16[2048,128]{1,0:T(8,128)(2,1)} %w_ref.1) | copy-start | bytes 1572868
  133.2 19.0 %copy-start.12 = (s32[32,3]{0,1:T(4,128)S(1)}, s32[32,3]{0,1:T(4,128)}, u32[]{:S(2)}) copy-start(s32[32,3]{0,1:T(4,128)} %param.16) | copy-start | bytes 1156
  133.2 19.4 %copy-start.14 = (s32[1,16]{1,0:T(1,128)S(1)}, s32[1,16]{1,0:T(1,128)}, u32[]{:S(2)}) copy-start(s32[1,16]{1,0:T(1,128)} %param.29) | copy-start | bytes 196
  133.3 22.7 %copy-start.13 = (s32[1,1024]{1,0:T(1,128)S(1)}, s32[1,1024]{1,0:T(1,128)}, u32[]{:S(2)}) copy-start(s32[1,1024]{1,0:T(1,128)} %param.28) | copy-start | bytes 12292
  133.3 5.4 %collective-permute-start.22 = (bf16[256,256]{1,0:T(8,128)(2,1)S(1)}, bf16[256,256]{1,0:T(8,128)(2,1)S(1)}, u32[]{:S(2)}, u32[]{:S(2)}) collective-permute-start(bf16[256,256]{1,0:T(8,128)(2,1)S(1)} %fusion.2.moe_ref), channel_id=1, source_target_pairs={{0,4},{4,0},{1,5},{5,1},{2,6},{6,2},{3,7},{7,3},{8,12},{12,8},{9,1... | collective-permute-start | bytes 393224 | tf_op jit(solution)/shard_map/ppermute | solution.py:31
  139.4 32.6 %copy-start.9 = (bf16[1024,128]{1,0:T(8,128)(2,1)S(1)}, bf16[1024,128]{1,0:T(8,128)(2,1)}, u32[]{:S(2)}) copy-start(bf16[1024,128]{1,0:T(8,128)(2,1)} %doc_ref.1) | copy-start | bytes 786436
  139.5 4.3 %collective-permute-start.23 = (bf16[144,128]{1,0:T(8,128)(2,1)S(1)}, bf16[144,128]{1,0:T(8,128)(2,1)S(1)}, u32[]{:S(2)}, u32[]{:S(2)}) collective-permute-start(bf16[144,128]{1,0:T(8,128)(2,1)S(1)} %get-tuple-element.50.p0), channel_id=1, source_target_pairs={{0,1},{1,2},{2,3},{3,0},{4,5},{5,6},{6,7},{7,4},{8,9},{9,10},{10,1... | collective-permute-start | bytes 110600 | tf_op jit(solution)/shard_map/ppermute | solution.py:27
  140.6 4.4 %collective-permute-start.24 = (bf16[144,128]{1,0:T(8,128)(2,1)S(1)}, bf16[144,128]{1,0:T(8,128)(2,1)S(1)}, u32[]{:S(2)}, u32[]{:S(2)}) collective-permute-start(bf16[144,128]{1,0:T(8,128)(2,1)S(1)} %get-tuple-element.50.p0), channel_id=1, source_target_pairs={{0,2},{1,3},{2,0},{3,1},{4,6},{5,7},{6,4},{7,5},{8,10},{9,11},{10,... | collective-permute-start | bytes 110600 | tf_op jit(solution)/shard_map/ppermute | solution.py:27
  143.3 2.8 %collective-permute-start.25 = (bf16[144,128]{1,0:T(8,128)(2,1)S(1)}, bf16[144,128]{1,0:T(8,128)(2,1)S(1)}, u32[]{:S(2)}, u32[]{:S(2)}) collective-permute-start(bf16[144,128]{1,0:T(8,128)(2,1)S(1)} %get-tuple-element.50.p0), channel_id=1, source_target_pairs={{0,3},{1,0},{2,1},{3,2},{4,7},{5,4},{6,5},{7,6},{8,11},{9,8},{10,9... | collective-permute-start | bytes 110600 | tf_op jit(solution)/shard_map/ppermute | solution.py:27
  147.1 18.8 %all-to-all-start.2 = ((bf16[16,128,128]{2,1,0:T(8,128)(2,1)}), bf16[16,128,128]{2,1,0:T(8,128)(2,1)S(1)}, u32[]{:S(2)}, u32[]{:S(2)}) async-start(bf16[16,128,128]{2,1,0:T(8,128)(2,1)} %vectors.1), calls=%async_computation.2 | async-start | bytes 1048576 | tf_op jit(solution)/shard_map/all_to_all | solution.py:517
  152.7 6.5 %collective-permute-start.26 = (bf16[128,512]{1,0:T(8,128)(2,1)S(1)}, bf16[128,512]{1,0:T(8,128)(2,1)S(1)}, u32[]{:S(2)}, u32[]{:S(2)}) collective-permute-start(bf16[128,512]{1,0:T(8,128)(2,1)S(1)} %get-tuple-element.54.p0), channel_id=1, source_target_pairs={{0,1},{1,2},{2,3},{3,0},{4,5},{5,6},{6,7},{7,4},{8,9},{9,10},{10,1... | collective-permute-start | bytes 393224 | tf_op jit(solution)/shard_map/ppermute | solution.py:27
  152.8 6.4 %collective-permute-start.27 = (bf16[128,512]{1,0:T(8,128)(2,1)S(1)}, bf16[128,512]{1,0:T(8,128)(2,1)S(1)}, u32[]{:S(2)}, u32[]{:S(2)}) collective-permute-start(bf16[128,512]{1,0:T(8,128)(2,1)S(1)} %get-tuple-element.54.p0), channel_id=1, source_target_pairs={{0,2},{1,3},{2,0},{3,1},{4,6},{5,7},{6,4},{7,5},{8,10},{9,11},{10,... | collective-permute-start | bytes 393224 | tf_op jit(solution)/shard_map/ppermute | solution.py:27
  154.6 5.6 %collective-permute-start.28 = (bf16[128,512]{1,0:T(8,128)(2,1)S(1)}, bf16[128,512]{1,0:T(8,128)(2,1)S(1)}, u32[]{:S(2)}, u32[]{:S(2)}) collective-permute-start(bf16[128,512]{1,0:T(8,128)(2,1)S(1)} %get-tuple-element.54.p0), channel_id=1, source_target_pairs={{0,3},{1,0},{2,1},{3,2},{4,7},{5,4},{6,5},{7,6},{8,11},{9,8},{10,9... | collective-permute-start | bytes 393224 | tf_op jit(solution)/shard_map/ppermute | solution.py:27
  166.0 6.1 %collective-permute-start.29 = (bf16[2048,128]{1,0:T(8,128)(2,1)S(1)}, bf16[2048,128]{1,0:T(8,128)(2,1)S(1)}, u32[]{:S(2)}, u32[]{:S(2)}) collective-permute-start(bf16[2048,128]{1,0:T(8,128)(2,1)S(1)} %bitcast.35), channel_id=1, source_target_pairs={{0,8},{8,0},{1,9},{9,1},{2,10},{10,2},{3,11},{11,3},{4,12},{12,4},... | collective-permute-start | bytes 1572872 | tf_op jit(solution)/shard_map/ppermute | solution.py:531

commit v14 on v13

--- a/solution.py
+++ b/solution.py
@@ -158,15 +158,8 @@
 
 def gate_up_kernel(here_ref, *refs):
     halves = refs[0:4], refs[4:8]
-    gain_hbm, gate_hbm, up_hbm, gate_par, up_par, out_ref, gain_ref, w_ref, sems = refs[8:]
+    gain_ref, gate_ref, up_ref, gate_par, up_par, out_ref = refs[8:]
     i, j = here_ref[0], here_ref[1]
-    sources = (gate_hbm.at[i], up_hbm.at[i], gate_par, up_par)
-    copies = [
-        pltpu.make_async_copy(source, w_ref.at[n], sems.at[n]) for n, source in enumerate(sources)
-    ]
-    copies.append(pltpu.make_async_copy(gain_hbm, gain_ref, sems.at[4]))
-    for copy in copies:
-        copy.start()
     scales = []
     for xs in halves:
         total = jnp.zeros((HALF, 1), f32)
@@ -174,8 +167,6 @@
             v = x[...].astype(f32)
             total = total + jnp.sum(v * v, axis=1, keepdims=True)
         scales.append(lax.rsqrt(total / 2048.0 + EPS))
-    for copy in copies:
-        copy.wait()
     for half, (xs, scale) in enumerate(zip(halves, scales)):
         own = jnp.zeros((HALF, 256), f32)
         par = jnp.zeros((HALF, 256), f32)
@@ -183,8 +174,8 @@
             part = lax.rem(j + 4 + (0, -1, 1, 2)[k], 4)
             rows = pl.ds(pl.multiple_of(part * 512, 512), 512)
             normed = (x[...].astype(f32) * scale * gain_ref[1:2, rows]).astype(bf16)
-            w_own = jnp.concatenate([w_ref[0, rows, :], w_ref[1, rows, :]], axis=1)
-            w_par = jnp.concatenate([w_ref[2, rows, :], w_ref[3, rows, :]], axis=1)
+            w_own = jnp.concatenate([gate_ref[i, rows, :], up_ref[i, rows, :]], axis=1)
+            w_par = jnp.concatenate([gate_par[rows, :], up_par[rows, :]], axis=1)
             own = own + jnp.dot(normed, w_own, preferred_element_type=f32)
             par = par + jnp.dot(normed, w_par, preferred_element_type=f32)
         for at, both in ((0, own), (128, par)):
@@ -194,24 +185,12 @@
             ).astype(bf16)
 
 
-def down_kernel(here_ref, a0, a1, a2, a3, w0, w1, w2, w3, par_ref, out_ref, w_ref, sems):
+def down_kernel(here_ref, a0, a1, a2, a3, w0, w1, w2, w3, par_ref, out_ref):
     i = here_ref[0]
-    copies = []
-    for k, w in enumerate((w0, w1, w2, w3)):
-        copies.append(
-            (
-                pltpu.make_async_copy(w.at[i], w_ref.at[k, 0:128], sems.at[0, k]),
-                pltpu.make_async_copy(par_ref.at[k], w_ref.at[k, 128:256], sems.at[1, k]),
-            )
-        )
-    for pair in copies:
-        for copy in pair:
-            copy.start()
     total = jnp.zeros((a0.shape[0], 512), f32)
-    for k, a in enumerate((a0, a1, a2, a3)):
-        for copy in copies[k]:
-            copy.wait()
-        total = total + jnp.dot(a[...], w_ref[k], preferred_element_type=f32)
+    for k, (a, w) in enumerate(((a0, w0), (a1, w1), (a2, w2), (a3, w3))):
+        weight = jnp.concatenate([w[i], par_ref[k]], axis=0)
+        total = total + jnp.dot(a[...], weight, preferred_element_type=f32)
     for s in range(WIDE):
         out_ref[s] = packed(total[s * CAP : (s + 1) * CAP])
 
@@ -434,13 +413,8 @@
     act = pl.pallas_call(
         gate_up_kernel,
         out_shape=jax.ShapeDtypeStruct((2 * HALF, 256), bf16),
-        in_specs=[smem()] + [vmem()] * 8 + [anywhere()] * 5,
+        in_specs=[smem()] + [vmem()] * 13,
         out_specs=vmem(),
-        scratch_shapes=[
-            pltpu.VMEM((3, 2048), f32),
-            pltpu.VMEM((4, 2048, 128), bf16),
-            pltpu.SemaphoreType.DMA((5,)),
-        ],
         compiler_params=params(),
         name="gate_up",
     )(
@@ -456,9 +430,8 @@
     out = pl.pallas_call(
         down_kernel,
         out_shape=jax.ShapeDtypeStruct((WIDE, 2 * CAP, 256), bf16),
-        in_specs=[smem()] + [vmem()] * 4 + [anywhere()] * 5,
+        in_specs=[smem()] + [vmem()] * 9,
         out_specs=vmem(),
-        scratch_shapes=[pltpu.VMEM((4, 256, 512), bf16), pltpu.SemaphoreType.DMA((2, 4))],
         compiler_params=params(),
         name="down",
     )(here, act, *(y_shift(act, k) for k in (1, 2, 3)), *downs, down_par)

time: 176 us -> 174 us (0.989)
  transfers between devices with their start and end apart: 33 -> 33, of which waited for: 20 -> 20; matrix products, arithmetic and copies ran while one was open for 6% -> 6% of each run, Pallas kernels for 4% -> 3%
where the time goes in v14:
time: 174 us
  waiting for transfers between devices  74.2 us (43%)
  starting transfers between devices  67.6 us (39%)
  Pallas kernels  18.7 us (11%)
  local copies, waits for them, and re-layouts  7.55 us (4%)
  other arithmetic  3.11 us (2%)
    ppermute x24, waiting for transfers between devices, y_shift(): return lax.ppermute(x, 'y', [(s, (s + k) % 4) for s in range(4)])  33.8 us
    ppermute x24, starting transfers between devices, y_shift(): return lax.ppermute(x, 'y', [(s, (s + k) % 4) for s in range(4)])  30.6 us
    all_to_all x1, waiting for transfers between devices, body(): back = lax.all_to_all(out, W, 0, 0, tiled=True)  19.2 us
    all_to_all x1, starting transfers between devices, body(): arrived = lax.all_to_all(rows, W, 0, 0, tiled=True)  11.6 us
    all_to_all x1, waiting for transfers between devices, body(): arrived = lax.all_to_all(rows, W, 0, 0, tiled=True)  9.76 us
    ppermute x5, starting transfers between devices, x_swap(): return lax.ppermute(x, 'xh', [(0, 1), (1, 0)])  9.11 us
    all_to_all x1, starting transfers between devices, body(): back = lax.all_to_all(out, W, 0, 0, tiled=True)  6.7 us
    all_to_all x1, waiting for transfers between devices, body(): lax.all_to_all(vectors, ('z', 'xl'), 0, 0, tiled=True)  5.83 us
  transfers between devices with their start and end apart: 33, of which 20 were waited for; matrix products, arithmetic and copies ran while one was open for 6% of the time, Pallas kernels for 3%

profile of v14, /device:TPU:1, one launch (start us, length us, event | category | flops | bytes accessed | tf_op | source)
XLA Modules:
  0.0 173.5 jit_solution(16804531159526281654)
XLA Ops:
  0.7 5.5 %attention.1 = (bf16[128,512]{1,0:T(8,128)(2,1)}, bf16[128,512]{1,0:T(8,128)(2,1)}, bf16[128,512]{1,0:T(8,128)(2,1)}, bf16[128,512]{1,0:T(8,128)(2,1)}, bf16[2048,128]{1,0:T(8,128)(2,1)}) custom-call(s32[1]{0:T(128)} %bitcast.i_ref, s32[1]{0:T(128)} %bitcast.1.j_ref, s32[1]{0:T(128)} %bitcast.2.wide_ref, s32[3,32]{1,0:T(4,128)} %bitcast.42, ...), custom_call_target="tpu_custom_call" | custom-call | tf_op jit(solution)/shard_map/attention/pallas_call | solution.py:320
  6.2 3.7 %collective-permute-start.4 = (bf16[2048,128]{1,0:T(8,128)(2,1)}, bf16[2048,128]{1,0:T(8,128)(2,1)S(1)}, u32[]{:S(2)}, u32[]{:S(2)}) collective-permute-start(bf16[2048,128]{1,0:T(8,128)(2,1)} %get-tuple-element.36), channel_id=1, source_target_pairs={{0,4},{4,0},{1,5},{5,1},{2,6},{6,2},{3,7},{7,3},{8,12},{12,8},{9,1... | collective-permute-start | bytes 1572872 | tf_op jit(solution)/shard_map/ppermute | solution.py:31
  9.8 1.3 collective-permute-start
  11.1 2.6 %collective-permute-start.1 = (bf16[128,512]{1,0:T(8,128)(2,1)}, bf16[128,512]{1,0:T(8,128)(2,1)S(1)}, u32[]{:S(2)}, u32[]{:S(2)}) collective-permute-start(bf16[128,512]{1,0:T(8,128)(2,1)} %get-tuple-element.33), channel_id=1, source_target_pairs={{0,2},{1,3},{2,0},{3,1},{4,6},{5,7},{6,4},{7,5},{8,10},{9,11},{10,... | collective-permute-start | bytes 393224 | tf_op jit(solution)/shard_map/ppermute | solution.py:27
  13.8 1.1 collective-permute-start.2
  15.8 3.5 %collective-permute-done.1 = bf16[128,512]{1,0:T(8,128)(2,1)S(1)} collective-permute-done((bf16[128,512]{1,0:T(8,128)(2,1)}, bf16[128,512]{1,0:T(8,128)(2,1)S(1)}, u32[]{:S(2)}, u32[]{:S(2)}) %collective-permute-start.1) | collective-permute-done | bytes 131104 | tf_op jit(solution)/shard_map/ppermute | solution.py:27
  19.4 1.0 add_convert_fusion.own_ref
  21.5 2.4 %collective-permute-start.20 = (bf16[2,128,512]{2,1,0:T(8,128)(2,1)}, bf16[2,128,512]{2,1,0:T(8,128)(2,1)}, u32[]{:S(2)}, u32[]{:S(2)}) collective-permute-start(bf16[2,128,512]{2,1,0:T(8,128)(2,1)} %get-tuple-element.64), channel_id=1, source_target_pairs={{0,3},{1,0},{2,1},{3,2},{4,7},{5,4},{6,5},{7,6},{8,11},{9,8},{10,9... | collective-permute-start | bytes 786440 | tf_op jit(solution)/shard_map/ppermute | solution.py:27
  23.9 1.9 %collective-permute-done.3.par_ref = bf16[128,512]{1,0:T(8,128)(2,1)S(1)} collective-permute-done((bf16[128,512]{1,0:T(8,128)(2,1)S(1)}, bf16[128,512]{1,0:T(8,128)(2,1)S(1)}, u32[]{:S(2)}, u32[]{:S(2)}) %collective-permute-start.3) | collective-permute-done | bytes 131104 | tf_op jit(solution)/shard_map/ppermute | solution.py:31
  27.6 11.6 %all-to-all-start = ((bf16[32,40,256]{2,1,0:T(8,128)(2,1)}), bf16[32,40,256]{2,1,0:T(8,128)(2,1)S(1)}, u32[]{:S(2)}, u32[]{:S(2)}) async-start(bf16[32,40,256]{2,1,0:T(8,128)(2,1)} %copy-done.4), calls=%async_computation | async-start | bytes 1310720 | tf_op jit(solution)/shard_map/all_to_all | solution.py:396
  39.3 1.7 constant_dynamic-slice_fusion.3
  42.1 0.9 collective-permute-start.5
  43.0 2.3 %collective-permute-start.6 = (f32[128,128]{0,1:T(8,128)S(1)}, f32[128,128]{0,1:T(8,128)S(1)}, u32[]{:S(2)}, u32[]{:S(2)}) collective-permute-start(f32[128,128]{0,1:T(8,128)S(1)} %pad_maximum_fusion.1), channel_id=1, source_target_pairs={{0,2},{1,3},{2,0},{3,1},{4,6},{5,7},{6,4},{7,5},{8,10},{9,11},{10,... | collective-permute-start | bytes 196616 | tf_op jit(solution)/shard_map/ppermute | solution.py:27
  45.4 1.2 collective-permute-start.7
  47.0 1.8 %collective-permute-done.6 = f32[128,128]{0,1:T(8,128)S(1)} collective-permute-done((f32[128,128]{0,1:T(8,128)S(1)}, f32[128,128]{0,1:T(8,128)S(1)}, u32[]{:S(2)}, u32[]{:S(2)}) %collective-permute-start.6) | collective-permute-done | bytes 65568 | tf_op jit(solution)/shard_map/ppermute | solution.py:27
  49.1 9.8 %all-to-all-done.in_ref = bf16[32,40,256]{2,1,0:T(8,128)(2,1)S(1)} async-done(((bf16[32,40,256]{2,1,0:T(8,128)(2,1)}), bf16[32,40,256]{2,1,0:T(8,128)(2,1)S(1)}, u32[]{:S(2)}, u32[]{:S(2)}) %all-to-all-start) | async-done | bytes 655392 | tf_op jit(solution)/shard_map/all_to_all | solution.py:396
  59.0 0.9 collective-permute-start.8
  59.9 1.8 %collective-permute-start.12 = (bf16[320,512]{1,0:T(8,128)(2,1)S(1)}, bf16[320,512]{1,0:T(8,128)(2,1)S(1)}, u32[]{:S(2)}, u32[]{:S(2)}) collective-permute-start(bf16[320,512]{1,0:T(8,128)(2,1)S(1)} %get-tuple-element.46.refs_4_), channel_id=1, source_target_pairs={{0,3},{1,0},{2,1},{3,2},{4,7},{5,4},{6,5},{7,6},{8,11},{9,8},{10,9... | collective-permute-start | bytes 983048 | tf_op jit(solution)/shard_map/ppermute | solution.py:27
  62.8 1.8 %collective-permute-start.14 = (bf16[2048,128]{1,0:T(8,128)(2,1)}, bf16[2048,128]{1,0:T(8,128)(2,1)S(1)}, u32[]{:S(2)}, u32[]{:S(2)}) collective-permute-start(bf16[2048,128]{1,0:T(8,128)(2,1)} %dynamic-slice_bitcast_fusion), channel_id=1, source_target_pairs={{0,4},{4,0},{1,5},{5,1},{2,6},{6,2},{3,7},{7,3},{8,12},{12,8},{9,1... | collective-permute-start | bytes 1572872 | tf_op jit(solution)/shard_map/ppermute | solution.py:31
  66.4 2.6 %collective-permute-start.9 = (bf16[320,512]{1,0:T(8,128)(2,1)S(1)}, bf16[320,512]{1,0:T(8,128)(2,1)S(1)}, u32[]{:S(2)}, u32[]{:S(2)}) collective-permute-start(bf16[320,512]{1,0:T(8,128)(2,1)S(1)} %get-tuple-element.45.refs_0_), channel_id=1, source_target_pairs={{0,3},{1,0},{2,1},{3,2},{4,7},{5,4},{6,5},{7,6},{8,11},{9,8},{10,9... | collective-permute-start | bytes 983048 | tf_op jit(solution)/shard_map/ppermute | solution.py:27
  69.1 2.7 %collective-permute-start.13 = (bf16[320,512]{1,0:T(8,128)(2,1)S(1)}, bf16[320,512]{1,0:T(8,128)(2,1)S(1)}, u32[]{:S(2)}, u32[]{:S(2)}) collective-permute-start(bf16[320,512]{1,0:T(8,128)(2,1)S(1)} %collective-permute-done.12.refs_6_), channel_id=1, source_target_pairs={{0,3},{1,0},{2,1},{3,2},{4,7},{5,4},{6,5},{7,6},{8,11},{9,8},{10,9... | collective-permute-start | bytes 983048 | tf_op jit(solution)/shard_map/ppermute | solution.py:27
  71.8 1.0 pad_maximum_fusion
  72.7 2.4 %collective-permute-done.11.refs_5_ = bf16[320,512]{1,0:T(8,128)(2,1)S(1)} collective-permute-done((bf16[320,512]{1,0:T(8,128)(2,1)S(1)}, bf16[320,512]{1,0:T(8,128)(2,1)S(1)}, u32[]{:S(2)}, u32[]{:S(2)}) %collective-permute-start.11) | collective-permute-done | bytes 327712 | tf_op jit(solution)/shard_map/ppermute | solution.py:27
  75.1 1.7 collective-permute-start.21
  77.0 5.1 %collective-permute-done.10.refs_3_ = bf16[320,512]{1,0:T(8,128)(2,1)S(1)} collective-permute-done((bf16[320,512]{1,0:T(8,128)(2,1)S(1)}, bf16[320,512]{1,0:T(8,128)(2,1)S(1)}, u32[]{:S(2)}, u32[]{:S(2)}) %collective-permute-start.10) | collective-permute-done | bytes 327712 | tf_op jit(solution)/shard_map/ppermute | solution.py:27
  82.2 2.4 %gate_up.1.a0 = bf16[640,256]{1,0:T(8,128)(2,1)S(1)} custom-call(s32[4]{0:T(128)S(1)} %pad_add_fusion.here_ref, bf16[320,512]{1,0:T(8,128)(2,1)S(1)} %get-tuple-element.45.refs_0_, bf16[320,512]{1,0:T(8,128)(2,1)S(1)} %collective-permute-done.8.refs_1_, bf16[320,512]{1,0:T(8,128)(2,1)S(1)} %collective-permute-done.9.refs_2_, ...), custom_call_target="tpu_custom_call" | custom-call | tf_op jit(solution)/shard_map/gate_up/pallas_call | solution.py:413
  85.2 2.5 %collective-permute-start.16 = (bf16[640,256]{1,0:T(8,128)(2,1)S(1)}, bf16[640,256]{1,0:T(8,128)(2,1)S(1)}, u32[]{:S(2)}, u32[]{:S(2)}) collective-permute-start(bf16[640,256]{1,0:T(8,128)(2,1)S(1)} %gate_up.1.a0), channel_id=1, source_target_pairs={{0,2},{1,3},{2,0},{3,1},{4,6},{5,7},{6,4},{7,5},{8,10},{9,11},{10,... | collective-permute-start | bytes 983048 | tf_op jit(solution)/shard_map/ppermute | solution.py:27
  88.6 5.0 %collective-permute-done.15.a1 = bf16[640,256]{1,0:T(8,128)(2,1)S(1)} collective-permute-done((bf16[640,256]{1,0:T(8,128)(2,1)S(1)}, bf16[640,256]{1,0:T(8,128)(2,1)S(1)}, u32[]{:S(2)}, u32[]{:S(2)}) %collective-permute-start.15) | collective-permute-done | bytes 327712 | tf_op jit(solution)/shard_map/ppermute | solution.py:27
  93.6 5.3 %collective-permute-done.16.a2 = bf16[640,256]{1,0:T(8,128)(2,1)S(1)} collective-permute-done((bf16[640,256]{1,0:T(8,128)(2,1)S(1)}, bf16[640,256]{1,0:T(8,128)(2,1)S(1)}, u32[]{:S(2)}, u32[]{:S(2)}) %collective-permute-start.16) | collective-permute-done | bytes 327712 | tf_op jit(solution)/shard_map/ppermute | solution.py:27
  98.8 3.1 %collective-permute-done.17.a3 = bf16[640,256]{1,0:T(8,128)(2,1)S(1)} collective-permute-done((bf16[640,256]{1,0:T(8,128)(2,1)S(1)}, bf16[640,256]{1,0:T(8,128)(2,1)S(1)}, u32[]{:S(2)}, u32[]{:S(2)}) %collective-permute-start.17) | collective-permute-done | bytes 327712 | tf_op jit(solution)/shard_map/ppermute | solution.py:27
  102.0 2.8 %down.1 = bf16[32,40,256]{2,1,0:T(8,128)(2,1)} custom-call(s32[4]{0:T(128)S(1)} %pad_add_fusion.here_ref, bf16[640,256]{1,0:T(8,128)(2,1)S(1)} %gate_up.1.a0, bf16[640,256]{1,0:T(8,128)(2,1)S(1)} %collective-permute-done.15.a1, bf16[640,256]{1,0:T(8,128)(2,1)S(1)} %collective-permute-done.16.a2, bf16[640,256]{1,0:T(8,128)(2,1)S(1)} %collective-permute-done.17.a3, ...), custom_call_target="tpu_custom_call" | custom-call | tf_op jit(solution)/shard_map/down/pallas_call | solution.py:430
  104.8 6.7 %all-to-all-start.1 = ((bf16[32,40,256]{2,1,0:T(8,128)(2,1)}), bf16[32,40,256]{2,1,0:T(8,128)(2,1)S(1)}, u32[]{:S(2)}, u32[]{:S(2)}) async-start(bf16[32,40,256]{2,1,0:T(8,128)(2,1)} %down.1), calls=%async_computation.1 | async-start | bytes 1310720 | tf_op jit(solution)/shard_map/all_to_all | solution.py:438
  111.9 19.2 %all-to-all-done.1 = bf16[32,40,256]{2,1,0:T(8,128)(2,1)S(1)} async-done(((bf16[32,40,256]{2,1,0:T(8,128)(2,1)}), bf16[32,40,256]{2,1,0:T(8,128)(2,1)S(1)}, u32[]{:S(2)}, u32[]{:S(2)}) %all-to-all-start.1) | async-done | bytes 655392 | tf_op jit(solution)/shard_map/all_to_all | solution.py:438
  131.9 1.8 %collective-permute-start.22 = (bf16[256,256]{1,0:T(8,128)(2,1)S(1)}, bf16[256,256]{1,0:T(8,128)(2,1)S(1)}, u32[]{:S(2)}, u32[]{:S(2)}) collective-permute-start(bf16[256,256]{1,0:T(8,128)(2,1)S(1)} %fusion.2.moe_ref), channel_id=1, source_target_pairs={{0,4},{4,0},{1,5},{5,1},{2,6},{6,2},{3,7},{7,3},{8,12},{12,8},{9,1... | collective-permute-start | bytes 393224 | tf_op jit(solution)/shard_map/ppermute | solution.py:31
  133.7 3.6 %collective-permute-done.22.par_ref = bf16[256,256]{1,0:T(8,128)(2,1)S(1)} collective-permute-done((bf16[256,256]{1,0:T(8,128)(2,1)S(1)}, bf16[256,256]{1,0:T(8,128)(2,1)S(1)}, u32[]{:S(2)}, u32[]{:S(2)}) %collective-permute-start.22) | collective-permute-done | bytes 131104 | tf_op jit(solution)/shard_map/ppermute | solution.py:31
  138.1 0.9 collective-permute-start.23
  139.1 2.7 %collective-permute-start.24 = (bf16[144,128]{1,0:T(8,128)(2,1)S(1)}, bf16[144,128]{1,0:T(8,128)(2,1)S(1)}, u32[]{:S(2)}, u32[]{:S(2)}) collective-permute-start(bf16[144,128]{1,0:T(8,128)(2,1)S(1)} %get-tuple-element.50.p0), channel_id=1, source_target_pairs={{0,2},{1,3},{2,0},{3,1},{4,6},{5,7},{6,4},{7,5},{8,10},{9,11},{10,... | collective-permute-start | bytes 110600 | tf_op jit(solution)/shard_map/ppermute | solution.py:27
  142.2 1.3 collective-permute-done.24.p2
  143.5 1.1 collective-permute-done.25.p3
  144.5 1.0 vectors.1
  145.5 5.1 %all-to-all-start.2 = ((bf16[16,128,128]{2,1,0:T(8,128)(2,1)}), bf16[16,128,128]{2,1,0:T(8,128)(2,1)S(1)}, u32[]{:S(2)}, u32[]{:S(2)}) async-start(bf16[16,128,128]{2,1,0:T(8,128)(2,1)} %vectors.1), calls=%async_computation.2 | async-start | bytes 1048576 | tf_op jit(solution)/shard_map/all_to_all | solution.py:490
  151.2 1.8 %collective-permute-start.27 = (bf16[128,512]{1,0:T(8,128)(2,1)S(1)}, bf16[128,512]{1,0:T(8,128)(2,1)S(1)}, u32[]{:S(2)}, u32[]{:S(2)}) collective-permute-start(bf16[128,512]{1,0:T(8,128)(2,1)S(1)} %get-tuple-element.54.p0), channel_id=1, source_target_pairs={{0,2},{1,3},{2,0},{3,1},{4,6},{5,7},{6,4},{7,5},{8,10},{9,11},{10,... | collective-permute-start | bytes 393224 | tf_op jit(solution)/shard_map/ppermute | solution.py:27
  153.0 1.1 collective-permute-start.28
  154.5 3.1 %collective-permute-done.26.p1 = bf16[128,512]{1,0:T(8,128)(2,1)S(1)} collective-permute-done((bf16[128,512]{1,0:T(8,128)(2,1)S(1)}, bf16[128,512]{1,0:T(8,128)(2,1)S(1)}, u32[]{:S(2)}, u32[]{:S(2)}) %collective-permute-start.26) | collective-permute-done | bytes 131104 | tf_op jit(solution)/shard_map/ppermute | solution.py:27
  158.6 5.8 %all-to-all-done.2 = bf16[16,128,128]{2,1,0:T(8,128)(2,1)S(1)} async-done(((bf16[16,128,128]{2,1,0:T(8,128)(2,1)}), bf16[16,128,128]{2,1,0:T(8,128)(2,1)S(1)}, u32[]{:S(2)}, u32[]{:S(2)}) %all-to-all-start.2) | async-done | bytes 524320 | tf_op jit(solution)/shard_map/all_to_all | solution.py:490
  164.4 4.5 %collective-permute-start.29 = (bf16[2048,128]{1,0:T(8,128)(2,1)S(1)}, bf16[2048,128]{1,0:T(8,128)(2,1)S(1)}, u32[]{:S(2)}, u32[]{:S(2)}) collective-permute-start(bf16[2048,128]{1,0:T(8,128)(2,1)S(1)} %bitcast.35), channel_id=1, source_target_pairs={{0,8},{8,0},{1,9},{9,1},{2,10},{10,2},{3,11},{11,3},{4,12},{12,4},... | collective-permute-start | bytes 1572872 | tf_op jit(solution)/shard_map/ppermute | solution.py:504
  168.9 1.4 assemble.1
  170.4 2.9 %score.1 = f32[1,16]{1,0:T(1,128)} custom-call(s32[5,16]{1,0:T(8,128)S(1)} %stack.48.info_ref, bf16[1024,128]{1,0:T(8,128)(2,1)S(1)} %copy-done.9, bf16[2048,128]{1,0:T(8,128)(2,1)S(1)} %bitcast.36, bf16[2048,128]{1,0:T(8,128)(2,1)S(1)} %collective-permute-done.29.other_ref), custom_call_target="tpu_custom_call" | custom-call | tf_op jit(solution)/shard_map/score/pallas_call | solution.py:513
  (99 shorter events, 14.5 us)
Async XLA Ops:
  0.6 41.3 %copy-start = (bf16[2048,64]{0,1:T(8,128)(2,1)S(1)}, bf16[2048,64]{0,1:T(8,128)(2,1)}, u32[]{:S(2)}) copy-start(bf16[2048,64]{0,1:T(8,128)(2,1)} %param.21) | copy-start | bytes 786436
  0.7 14.2 %copy-start.10 = (s32[128,8]{0,1:T(8,128)S(1)}, s32[128,8]{0,1:T(8,128)}, u32[]{:S(2)}) copy-start(s32[128,8]{0,1:T(8,128)} %param.22) | copy-start | bytes 12292
  0.7 19.9 %copy-start.11 = (bf16[2,128,2048]{2,1,0:T(8,128)(2,1)S(1)}, bf16[2,128,2048]{2,1,0:T(8,128)(2,1)}, u32[]{:S(2)}) copy-start(bf16[2,128,2048]{2,1,0:T(8,128)(2,1)} %param.25) | copy-start | bytes 3145732
  6.2 19.7 %collective-permute-start.4 = (bf16[2048,128]{1,0:T(8,128)(2,1)}, bf16[2048,128]{1,0:T(8,128)(2,1)S(1)}, u32[]{:S(2)}, u32[]{:S(2)}) collective-permute-start(bf16[2048,128]{1,0:T(8,128)(2,1)} %get-tuple-element.36), channel_id=1, source_target_pairs={{0,4},{4,0},{1,5},{5,1},{2,6},{6,2},{3,7},{7,3},{8,12},{12,8},{9,1... | collective-permute-start | bytes 1572872 | tf_op jit(solution)/shard_map/ppermute | solution.py:31
  9.8 6.0 %collective-permute-start = (bf16[128,512]{1,0:T(8,128)(2,1)}, bf16[128,512]{1,0:T(8,128)(2,1)S(1)}, u32[]{:S(2)}, u32[]{:S(2)}) collective-permute-start(bf16[128,512]{1,0:T(8,128)(2,1)} %get-tuple-element.32), channel_id=1, source_target_pairs={{0,1},{1,2},{2,3},{3,0},{4,5},{5,6},{6,7},{7,4},{8,9},{9,10},{10,1... | collective-permute-start | bytes 393224 | tf_op jit(solution)/shard_map/ppermute | solution.py:27
  11.1 8.2 %collective-permute-start.1 = (bf16[128,512]{1,0:T(8,128)(2,1)}, bf16[128,512]{1,0:T(8,128)(2,1)S(1)}, u32[]{:S(2)}, u32[]{:S(2)}) collective-permute-start(bf16[128,512]{1,0:T(8,128)(2,1)} %get-tuple-element.33), channel_id=1, source_target_pairs={{0,2},{1,3},{2,0},{3,1},{4,6},{5,7},{6,4},{7,5},{8,10},{9,11},{10,... | collective-permute-start | bytes 393224 | tf_op jit(solution)/shard_map/ppermute | solution.py:27
  13.8 5.6 %collective-permute-start.2 = (bf16[128,512]{1,0:T(8,128)(2,1)}, bf16[128,512]{1,0:T(8,128)(2,1)S(1)}, u32[]{:S(2)}, u32[]{:S(2)}) collective-permute-start(bf16[128,512]{1,0:T(8,128)(2,1)} %get-tuple-element.34), channel_id=1, source_target_pairs={{0,3},{1,0},{2,1},{3,2},{4,7},{5,4},{6,5},{7,6},{8,11},{9,8},{10,9... | collective-permute-start | bytes 393224 | tf_op jit(solution)/shard_map/ppermute | solution.py:27
  19.4 4.5 %copy-start.8 = (f32[3,2048]{1,0:T(4,128)S(1)}, f32[3,2048]{1,0:T(4,128)}, u32[]{:S(2)}) copy-start(f32[3,2048]{1,0:T(4,128)} %gain_ref.3) | copy-start | bytes 73732
  19.4 6.5 %copy-start.3 = (bf16[128,2048]{1,0:T(8,128)(2,1)S(1)}, bf16[128,2048]{1,0:T(8,128)(2,1)}, u32[]{:S(2)}) copy-start(bf16[128,2048]{1,0:T(8,128)(2,1)} %x_ref.1) | copy-start | bytes 1572868
  20.4 5.4 %collective-permute-start.3 = (bf16[128,512]{1,0:T(8,128)(2,1)S(1)}, bf16[128,512]{1,0:T(8,128)(2,1)S(1)}, u32[]{:S(2)}, u32[]{:S(2)}) collective-permute-start(bf16[128,512]{1,0:T(8,128)(2,1)S(1)} %add_convert_fusion.own_ref), channel_id=1, source_target_pairs={{0,4},{4,0},{1,5},{5,1},{2,6},{6,2},{3,7},{7,3},{8,12},{12,8},{9,1... | collective-permute-start | bytes 393224 | tf_op jit(solution)/shard_map/ppermute | solution.py:31
  21.5 19.5 %copy-start.2 = (bf16[2,2048,128]{2,1,0:T(8,128)(2,1)S(1)}, bf16[2,2048,128]{2,1,0:T(8,128)(2,1)}, u32[]{:S(2)}) copy-start(bf16[2,2048,128]{2,1,0:T(8,128)(2,1)} %refs_10_.1) | copy-start | bytes 3145732
  21.5 40.3 %collective-permute-start.20 = (bf16[2,128,512]{2,1,0:T(8,128)(2,1)}, bf16[2,128,512]{2,1,0:T(8,128)(2,1)}, u32[]{:S(2)}, u32[]{:S(2)}) collective-permute-start(bf16[2,128,512]{2,1,0:T(8,128)(2,1)} %get-tuple-element.64), channel_id=1, source_target_pairs={{0,3},{1,0},{2,1},{3,2},{4,7},{5,4},{6,5},{7,6},{8,11},{9,8},{10,9... | collective-permute-start | bytes 786440 | tf_op jit(solution)/shard_map/ppermute | solution.py:27
  23.9 38.9 %collective-permute-start.19 = (bf16[2,128,512]{2,1,0:T(8,128)(2,1)}, bf16[2,128,512]{2,1,0:T(8,128)(2,1)}, u32[]{:S(2)}, u32[]{:S(2)}) collective-permute-start(bf16[2,128,512]{2,1,0:T(8,128)(2,1)} %get-tuple-element.65), channel_id=1, source_target_pairs={{0,2},{1,3},{2,0},{3,1},{4,6},{5,7},{6,4},{7,5},{8,10},{9,11},{10,... | collective-permute-start | bytes 786440 | tf_op jit(solution)/shard_map/ppermute | solution.py:27
  25.9 1.8 %copy-start.5 = (bf16[2048,128]{1,0:T(8,128)(2,1)}, bf16[2048,128]{1,0:T(8,128)(2,1)S(1)}, u32[]{:S(2)}) copy-start(bf16[2048,128]{1,0:T(8,128)(2,1)S(1)} %collective-permute-done.4.refs_11_) | copy-start | bytes 1572868
  26.8 0.8 copy-start.4
  27.6 31.2 %all-to-all-start = ((bf16[32,40,256]{2,1,0:T(8,128)(2,1)}), bf16[32,40,256]{2,1,0:T(8,128)(2,1)S(1)}, u32[]{:S(2)}, u32[]{:S(2)}) async-start(bf16[32,40,256]{2,1,0:T(8,128)(2,1)} %copy-done.4), calls=%async_computation | async-start | bytes 1310720 | tf_op jit(solution)/shard_map/all_to_all | solution.py:396
  42.1 4.7 %collective-permute-start.5 = (f32[128,128]{0,1:T(8,128)S(1)}, f32[128,128]{0,1:T(8,128)S(1)}, u32[]{:S(2)}, u32[]{:S(2)}) collective-permute-start(f32[128,128]{0,1:T(8,128)S(1)} %pad_maximum_fusion.1), channel_id=1, source_target_pairs={{0,1},{1,2},{2,3},{3,0},{4,5},{5,6},{6,7},{7,4},{8,9},{9,10},{10,1... | collective-permute-start | bytes 196616 | tf_op jit(solution)/shard_map/ppermute | solution.py:27
  43.0 5.7 %collective-permute-start.6 = (f32[128,128]{0,1:T(8,128)S(1)}, f32[128,128]{0,1:T(8,128)S(1)}, u32[]{:S(2)}, u32[]{:S(2)}) collective-permute-start(f32[128,128]{0,1:T(8,128)S(1)} %pad_maximum_fusion.1), channel_id=1, source_target_pairs={{0,2},{1,3},{2,0},{3,1},{4,6},{5,7},{6,4},{7,5},{8,10},{9,11},{10,... | collective-permute-start | bytes 196616 | tf_op jit(solution)/shard_map/ppermute | solution.py:27
  45.4 3.7 %collective-permute-start.7 = (f32[128,128]{0,1:T(8,128)S(1)}, f32[128,128]{0,1:T(8,128)S(1)}, u32[]{:S(2)}, u32[]{:S(2)}) collective-permute-start(f32[128,128]{0,1:T(8,128)S(1)} %pad_maximum_fusion.1), channel_id=1, source_target_pairs={{0,3},{1,0},{2,1},{3,2},{4,7},{5,4},{6,5},{7,6},{8,11},{9,8},{10,9... | collective-permute-start | bytes 196616 | tf_op jit(solution)/shard_map/ppermute | solution.py:27
  46.9 18.6 %collective-permute-start.18 = (bf16[2,128,512]{2,1,0:T(8,128)(2,1)}, bf16[2,128,512]{2,1,0:T(8,128)(2,1)}, u32[]{:S(2)}, u32[]{:S(2)}) collective-permute-start(bf16[2,128,512]{2,1,0:T(8,128)(2,1)} %get-tuple-element.66), channel_id=1, source_target_pairs={{0,1},{1,2},{2,3},{3,0},{4,5},{5,6},{6,7},{7,4},{8,9},{9,10},{10,1... | collective-permute-start | bytes 786440 | tf_op jit(solution)/shard_map/ppermute | solution.py:27
  49.1 33.1 %copy-start.1 = (bf16[2,2048,128]{2,1,0:T(8,128)(2,1)S(1)}, bf16[2,2048,128]{2,1,0:T(8,128)(2,1)}, u32[]{:S(2)}) copy-start(bf16[2,2048,128]{2,1,0:T(8,128)(2,1)} %refs_9_.1) | copy-start | bytes 3145732
  58.9 23.3 %copy-start.6 = (bf16[2048,128]{1,0:T(8,128)(2,1)S(1)}, bf16[2048,128]{1,0:T(8,128)(2,1)}, u32[]{:S(2)}) copy-start(bf16[2048,128]{1,0:T(8,128)(2,1)} %copy-done.5) | copy-start | bytes 1572868
  59.0 10.1 %collective-permute-start.8 = (bf16[320,512]{1,0:T(8,128)(2,1)S(1)}, bf16[320,512]{1,0:T(8,128)(2,1)S(1)}, u32[]{:S(2)}, u32[]{:S(2)}) collective-permute-start(bf16[320,512]{1,0:T(8,128)(2,1)S(1)} %get-tuple-element.45.refs_0_), channel_id=1, source_target_pairs={{0,1},{1,2},{2,3},{3,0},{4,5},{5,6},{6,7},{7,4},{8,9},{9,10},{10,1... | collective-permute-start | bytes 983048 | tf_op jit(solution)/shard_map/ppermute | solution.py:27
  59.9 9.2 %collective-permute-start.12 = (bf16[320,512]{1,0:T(8,128)(2,1)S(1)}, bf16[320,512]{1,0:T(8,128)(2,1)S(1)}, u32[]{:S(2)}, u32[]{:S(2)}) collective-permute-start(bf16[320,512]{1,0:T(8,128)(2,1)S(1)} %get-tuple-element.46.refs_4_), channel_id=1, source_target_pairs={{0,3},{1,0},{2,1},{3,2},{4,7},{5,4},{6,5},{7,6},{8,11},{9,8},{10,9... | collective-permute-start | bytes 983048 | tf_op jit(solution)/shard_map/ppermute | solution.py:27
  62.7 12.5 %collective-permute-start.11 = (bf16[320,512]{1,0:T(8,128)(2,1)S(1)}, bf16[320,512]{1,0:T(8,128)(2,1)S(1)}, u32[]{:S(2)}, u32[]{:S(2)}) collective-permute-start(bf16[320,512]{1,0:T(8,128)(2,1)S(1)} %get-tuple-element.46.refs_4_), channel_id=1, source_target_pairs={{0,1},{1,2},{2,3},{3,0},{4,5},{5,6},{6,7},{7,4},{8,9},{9,10},{10,1... | collective-permute-start | bytes 983048 | tf_op jit(solution)/shard_map/ppermute | solution.py:27
  62.8 14.3 %collective-permute-start.14 = (bf16[2048,128]{1,0:T(8,128)(2,1)}, bf16[2048,128]{1,0:T(8,128)(2,1)S(1)}, u32[]{:S(2)}, u32[]{:S(2)}) collective-permute-start(bf16[2048,128]{1,0:T(8,128)(2,1)} %dynamic-slice_bitcast_fusion), channel_id=1, source_target_pairs={{0,4},{4,0},{1,5},{5,1},{2,6},{6,2},{3,7},{7,3},{8,12},{12,8},{9,1... | collective-permute-start | bytes 1572872 | tf_op jit(solution)/shard_map/ppermute | solution.py:31
  66.4 10.6 %collective-permute-start.9 = (bf16[320,512]{1,0:T(8,128)(2,1)S(1)}, bf16[320,512]{1,0:T(8,128)(2,1)S(1)}, u32[]{:S(2)}, u32[]{:S(2)}) collective-permute-start(bf16[320,512]{1,0:T(8,128)(2,1)S(1)} %get-tuple-element.45.refs_0_), channel_id=1, source_target_pairs={{0,3},{1,0},{2,1},{3,2},{4,7},{5,4},{6,5},{7,6},{8,11},{9,8},{10,9... | collective-permute-start | bytes 983048 | tf_op jit(solution)/shard_map/ppermute | solution.py:27
  69.1 13.1 %collective-permute-start.10 = (bf16[320,512]{1,0:T(8,128)(2,1)S(1)}, bf16[320,512]{1,0:T(8,128)(2,1)S(1)}, u32[]{:S(2)}, u32[]{:S(2)}) collective-permute-start(bf16[320,512]{1,0:T(8,128)(2,1)S(1)} %collective-permute-done.8.refs_1_), channel_id=1, source_target_pairs={{0,1},{1,2},{2,3},{3,0},{4,5},{5,6},{6,7},{7,4},{8,9},{9,10},{10,1... | collective-permute-start | bytes 983048 | tf_op jit(solution)/shard_map/ppermute | solution.py:27
  69.1 13.1 %collective-permute-start.13 = (bf16[320,512]{1,0:T(8,128)(2,1)S(1)}, bf16[320,512]{1,0:T(8,128)(2,1)S(1)}, u32[]{:S(2)}, u32[]{:S(2)}) collective-permute-start(bf16[320,512]{1,0:T(8,128)(2,1)S(1)} %collective-permute-done.12.refs_6_), channel_id=1, source_target_pairs={{0,3},{1,0},{2,1},{3,2},{4,7},{5,4},{6,5},{7,6},{8,11},{9,8},{10,9... | collective-permute-start | bytes 983048 | tf_op jit(solution)/shard_map/ppermute | solution.py:27
  75.1 13.4 %collective-permute-start.21 = (bf16[4,128,512]{2,1,0:T(8,128)(2,1)S(1)}, bf16[4,128,512]{2,1,0:T(8,128)(2,1)S(1)}, u32[]{:S(2)}, u32[]{:S(2)}) collective-permute-start(bf16[4,128,512]{2,1,0:T(8,128)(2,1)S(1)} %pad_maximum_fusion), channel_id=1, source_target_pairs={{0,4},{4,0},{1,5},{5,1},{2,6},{6,2},{3,7},{7,3},{8,12},{12,8},{9,1... | collective-permute-start | bytes 1572872 | tf_op jit(solution)/shard_map/ppermute | solution.py:31
  84.6 8.9 %collective-permute-start.15 = (bf16[640,256]{1,0:T(8,128)(2,1)S(1)}, bf16[640,256]{1,0:T(8,128)(2,1)S(1)}, u32[]{:S(2)}, u32[]{:S(2)}) collective-permute-start(bf16[640,256]{1,0:T(8,128)(2,1)S(1)} %gate_up.1.a0), channel_id=1, source_target_pairs={{0,1},{1,2},{2,3},{3,0},{4,5},{5,6},{6,7},{7,4},{8,9},{9,10},{10,1... | collective-permute-start | bytes 983048 | tf_op jit(solution)/shard_map/ppermute | solution.py:27
  85.2 13.6 %collective-permute-start.16 = (bf16[640,256]{1,0:T(8,128)(2,1)S(1)}, bf16[640,256]{1,0:T(8,128)(2,1)S(1)}, u32[]{:S(2)}, u32[]{:S(2)}) collective-permute-start(bf16[640,256]{1,0:T(8,128)(2,1)S(1)} %gate_up.1.a0), channel_id=1, source_target_pairs={{0,2},{1,3},{2,0},{3,1},{4,6},{5,7},{6,4},{7,5},{8,10},{9,11},{10,... | collective-permute-start | bytes 983048 | tf_op jit(solution)/shard_map/ppermute | solution.py:27
  87.7 14.2 %collective-permute-start.17 = (bf16[640,256]{1,0:T(8,128)(2,1)S(1)}, bf16[640,256]{1,0:T(8,128)(2,1)S(1)}, u32[]{:S(2)}, u32[]{:S(2)}) collective-permute-start(bf16[640,256]{1,0:T(8,128)(2,1)S(1)} %gate_up.1.a0), channel_id=1, source_target_pairs={{0,3},{1,0},{2,1},{3,2},{4,7},{5,4},{6,5},{7,6},{8,11},{9,8},{10,9... | collective-permute-start | bytes 983048 | tf_op jit(solution)/shard_map/ppermute | solution.py:27
  104.8 26.3 %all-to-all-start.1 = ((bf16[32,40,256]{2,1,0:T(8,128)(2,1)}), bf16[32,40,256]{2,1,0:T(8,128)(2,1)S(1)}, u32[]{:S(2)}, u32[]{:S(2)}) async-start(bf16[32,40,256]{2,1,0:T(8,128)(2,1)} %down.1), calls=%async_computation.1 | async-start | bytes 1310720 | tf_op jit(solution)/shard_map/all_to_all | solution.py:438
  131.5 5.9 %copy-start.7 = (bf16[2048,128]{1,0:T(8,128)(2,1)S(1)}, bf16[2048,128]{1,0:T(8,128)(2,1)}, u32[]{:S(2)}) copy-start(bf16[2048,128]{1,0:T(8,128)(2,1)} %w_ref.1) | copy-start | bytes 1572868
  131.9 18.8 %copy-start.12 = (s32[32,3]{0,1:T(4,128)S(1)}, s32[32,3]{0,1:T(4,128)}, u32[]{:S(2)}) copy-start(s32[32,3]{0,1:T(4,128)} %param.16) | copy-start | bytes 1156
  131.9 19.2 %copy-start.14 = (s32[1,16]{1,0:T(1,128)S(1)}, s32[1,16]{1,0:T(1,128)}, u32[]{:S(2)}) copy-start(s32[1,16]{1,0:T(1,128)} %param.29) | copy-start | bytes 196
  131.9 22.4 %copy-start.13 = (s32[1,1024]{1,0:T(1,128)S(1)}, s32[1,1024]{1,0:T(1,128)}, u32[]{:S(2)}) copy-start(s32[1,1024]{1,0:T(1,128)} %param.28) | copy-start | bytes 12292
  131.9 5.4 %collective-permute-start.22 = (bf16[256,256]{1,0:T(8,128)(2,1)S(1)}, bf16[256,256]{1,0:T(8,128)(2,1)S(1)}, u32[]{:S(2)}, u32[]{:S(2)}) collective-permute-start(bf16[256,256]{1,0:T(8,128)(2,1)S(1)} %fusion.2.moe_ref), channel_id=1, source_target_pairs={{0,4},{4,0},{1,5},{5,1},{2,6},{6,2},{3,7},{7,3},{8,12},{12,8},{9,1... | collective-permute-start | bytes 393224 | tf_op jit(solution)/shard_map/ppermute | solution.py:31
  138.1 32.4 %copy-start.9 = (bf16[1024,128]{1,0:T(8,128)(2,1)S(1)}, bf16[1024,128]{1,0:T(8,128)(2,1)}, u32[]{:S(2)}) copy-start(bf16[1024,128]{1,0:T(8,128)(2,1)} %doc_ref.1) | copy-start | bytes 786436
  138.1 4.1 %collective-permute-start.23 = (bf16[144,128]{1,0:T(8,128)(2,1)S(1)}, bf16[144,128]{1,0:T(8,128)(2,1)S(1)}, u32[]{:S(2)}, u32[]{:S(2)}) collective-permute-start(bf16[144,128]{1,0:T(8,128)(2,1)S(1)} %get-tuple-element.50.p0), channel_id=1, source_target_pairs={{0,1},{1,2},{2,3},{3,0},{4,5},{5,6},{6,7},{7,4},{8,9},{9,10},{10,1... | collective-permute-start | bytes 110600 | tf_op jit(solution)/shard_map/ppermute | solution.py:27
  139.1 4.4 %collective-permute-start.24 = (bf16[144,128]{1,0:T(8,128)(2,1)S(1)}, bf16[144,128]{1,0:T(8,128)(2,1)S(1)}, u32[]{:S(2)}, u32[]{:S(2)}) collective-permute-start(bf16[144,128]{1,0:T(8,128)(2,1)S(1)} %get-tuple-element.50.p0), channel_id=1, source_target_pairs={{0,2},{1,3},{2,0},{3,1},{4,6},{5,7},{6,4},{7,5},{8,10},{9,11},{10,... | collective-permute-start | bytes 110600 | tf_op jit(solution)/shard_map/ppermute | solution.py:27
  141.7 2.8 %collective-permute-start.25 = (bf16[144,128]{1,0:T(8,128)(2,1)S(1)}, bf16[144,128]{1,0:T(8,128)(2,1)S(1)}, u32[]{:S(2)}, u32[]{:S(2)}) collective-permute-start(bf16[144,128]{1,0:T(8,128)(2,1)S(1)} %get-tuple-element.50.p0), channel_id=1, source_target_pairs={{0,3},{1,0},{2,1},{3,2},{4,7},{5,4},{6,5},{7,6},{8,11},{9,8},{10,9... | collective-permute-start | bytes 110600 | tf_op jit(solution)/shard_map/ppermute | solution.py:27
  145.5 18.9 %all-to-all-start.2 = ((bf16[16,128,128]{2,1,0:T(8,128)(2,1)}), bf16[16,128,128]{2,1,0:T(8,128)(2,1)S(1)}, u32[]{:S(2)}, u32[]{:S(2)}) async-start(bf16[16,128,128]{2,1,0:T(8,128)(2,1)} %vectors.1), calls=%async_computation.2 | async-start | bytes 1048576 | tf_op jit(solution)/shard_map/all_to_all | solution.py:490
  151.1 6.5 %collective-permute-start.26 = (bf16[128,512]{1,0:T(8,128)(2,1)S(1)}, bf16[128,512]{1,0:T(8,128)(2,1)S(1)}, u32[]{:S(2)}, u32[]{:S(2)}) collective-permute-start(bf16[128,512]{1,0:T(8,128)(2,1)S(1)} %get-tuple-element.54.p0), channel_id=1, source_target_pairs={{0,1},{1,2},{2,3},{3,0},{4,5},{5,6},{6,7},{7,4},{8,9},{9,10},{10,1... | collective-permute-start | bytes 393224 | tf_op jit(solution)/shard_map/ppermute | solution.py:27
  151.2 6.4 %collective-permute-start.27 = (bf16[128,512]{1,0:T(8,128)(2,1)S(1)}, bf16[128,512]{1,0:T(8,128)(2,1)S(1)}, u32[]{:S(2)}, u32[]{:S(2)}) collective-permute-start(bf16[128,512]{1,0:T(8,128)(2,1)S(1)} %get-tuple-element.54.p0), channel_id=1, source_target_pairs={{0,2},{1,3},{2,0},{3,1},{4,6},{5,7},{6,4},{7,5},{8,10},{9,11},{10,... | collective-permute-start | bytes 393224 | tf_op jit(solution)/shard_map/ppermute | solution.py:27
  153.0 5.5 %collective-permute-start.28 = (bf16[128,512]{1,0:T(8,128)(2,1)S(1)}, bf16[128,512]{1,0:T(8,128)(2,1)S(1)}, u32[]{:S(2)}, u32[]{:S(2)}) collective-permute-start(bf16[128,512]{1,0:T(8,128)(2,1)S(1)} %get-tuple-element.54.p0), channel_id=1, source_target_pairs={{0,3},{1,0},{2,1},{3,2},{4,7},{5,4},{6,5},{7,6},{8,11},{9,8},{10,9... | collective-permute-start | bytes 393224 | tf_op jit(solution)/shard_map/ppermute | solution.py:27
  164.4 6.0 %collective-permute-start.29 = (bf16[2048,128]{1,0:T(8,128)(2,1)S(1)}, bf16[2048,128]{1,0:T(8,128)(2,1)S(1)}, u32[]{:S(2)}, u32[]{:S(2)}) collective-permute-start(bf16[2048,128]{1,0:T(8,128)(2,1)S(1)} %bitcast.35), channel_id=1, source_target_pairs={{0,8},{8,0},{1,9},{9,1},{2,10},{10,2},{3,11},{11,3},{4,12},{12,4},... | collective-permute-start | bytes 1572872 | tf_op jit(solution)/shard_map/ppermute | solution.py:504

commit v15 on v14

--- a/solution.py
+++ b/solution.py
@@ -226,36 +226,23 @@
         out_ref[:, pl.ds(pl.multiple_of(part * 512, 512), 512)] = piece[...]
 
 
-def score_kernel(info_ref, doc_ref, own_ref, other_ref, out_ref, query_ref, sems):
+def score_kernel(info_ref, doc_ref, own_ref, other_ref, out_ref):
     def spot(d):
         return pl.multiple_of(jnp.minimum((info_ref[2, d] // 16) * 16, 2048 - 128), 16)
-
-    def copy_of(ref, d):
-        return pltpu.make_async_copy(ref.at[pl.ds(spot(d), 128), :], query_ref.at[d], sems.at[d])
-
-    for d in range(16):
-
-        @pl.when(info_ref[4, d] == 0)
-        def _():
-            copy_of(own_ref, d).start()
-
-        @pl.when(info_ref[4, d] != 0)
-        def _():
-            copy_of(other_ref, d).start()
 
     lane = lax.broadcasted_iota(jnp.int32, (1, 16), 1)
     scores = jnp.zeros((1, 16), f32)
     rows = lax.broadcasted_iota(jnp.int32, (144, 128), 0)
     columns = lax.broadcasted_iota(jnp.int32, (1, 128), 1)
     for d in range(16):
-        copy_of(own_ref, d).wait()
-    for d in range(16):
         first, size = info_ref[0, d], info_ref[1, d]
         q_first, q_size = info_ref[2, d], info_ref[3, d]
         at = pl.multiple_of(jnp.minimum((first // 16) * 16, 1024 - 144), 16)
+        window = pl.ds(spot(d), 128)
+        query = jnp.where(info_ref[4, d] == 0, own_ref[window, :], other_ref[window, :])
         sims = lax.dot_general(
             doc_ref[pl.ds(at, 144), :],
-            query_ref[d],
+            query,
             (((1,), (1,)), ((), ())),
             preferred_element_type=f32,
         )
@@ -513,9 +500,8 @@
     doc_scores = pl.pallas_call(
         score_kernel,
         out_shape=jax.ShapeDtypeStruct((1, 16), f32),
-        in_specs=[smem(), vmem()] + [anywhere()] * 2,
+        in_specs=[smem()] + [vmem()] * 3,
         out_specs=vmem(),
-        scratch_shapes=[pltpu.VMEM((16, 128, 128), bf16), pltpu.SemaphoreType.DMA((16,))],
         compiler_params=params(),
         name="score",
     )(info, doc_vectors, own, other)

time: 174 us -> 173 us (level)
  no operation moved by 1% of the time
where the time goes in v15:
time: 173 us; the launch traced here: 172 us
  waiting for transfers between devices  74.2 us (43%)
  starting transfers between devices  67.6 us (39%)
  Pallas kernels  17.6 us (10%)
  local copies, waits for them, and re-layouts  7.55 us (4%)
  other arithmetic  3.11 us (2%)
    ppermute x24, waiting for transfers between devices, y_shift(): return lax.ppermute(x, 'y', [(s, (s + k) % 4) for s in range(4)])  33.8 us
    ppermute x24, starting transfers between devices, y_shift(): return lax.ppermute(x, 'y', [(s, (s + k) % 4) for s in range(4)])  30.6 us
    all_to_all x1, waiting for transfers between devices, body(): back = lax.all_to_all(out, W, 0, 0, tiled=True)  19.2 us
    all_to_all x1, starting transfers between devices, body(): arrived = lax.all_to_all(rows, W, 0, 0, tiled=True)  11.6 us
    all_to_all x1, waiting for transfers between devices, body(): arrived = lax.all_to_all(rows, W, 0, 0, tiled=True)  9.76 us
    ppermute x5, starting transfers between devices, x_swap(): return lax.ppermute(x, 'xh', [(0, 1), (1, 0)])  9.11 us
    all_to_all x1, starting transfers between devices, body(): back = lax.all_to_all(out, W, 0, 0, tiled=True)  6.7 us
    all_to_all x1, waiting for transfers between devices, body(): lax.all_to_all(vectors, ('z', 'xl'), 0, 0, tiled=True)  5.83 us
  transfers between devices with their start and end apart: 33, of which 20 were waited for; matrix products, arithmetic and copies ran while one was open for 6% of the time, Pallas kernels for 3%

profile of v15, /device:TPU:1, one launch (start us, length us, event | category | flops | bytes accessed | tf_op | source)
XLA Modules:
  0.0 172.2 jit_solution(2816014621208842599)
XLA Ops:
  0.7 5.5 %attention.1 = (bf16[128,512]{1,0:T(8,128)(2,1)}, bf16[128,512]{1,0:T(8,128)(2,1)}, bf16[128,512]{1,0:T(8,128)(2,1)}, bf16[128,512]{1,0:T(8,128)(2,1)}, bf16[2048,128]{1,0:T(8,128)(2,1)}) custom-call(s32[1]{0:T(128)} %bitcast.i_ref, s32[1]{0:T(128)} %bitcast.1.j_ref, s32[1]{0:T(128)} %bitcast.2.wide_ref, s32[3,32]{1,0:T(4,128)} %bitcast.42, ...), custom_call_target="tpu_custom_call" | custom-call | tf_op jit(solution)/shard_map/attention/pallas_call | solution.py:307
  6.2 3.7 %collective-permute-start.4 = (bf16[2048,128]{1,0:T(8,128)(2,1)}, bf16[2048,128]{1,0:T(8,128)(2,1)S(1)}, u32[]{:S(2)}, u32[]{:S(2)}) collective-permute-start(bf16[2048,128]{1,0:T(8,128)(2,1)} %get-tuple-element.36), channel_id=1, source_target_pairs={{0,4},{4,0},{1,5},{5,1},{2,6},{6,2},{3,7},{7,3},{8,12},{12,8},{9,1... | collective-permute-start | bytes 1572872 | tf_op jit(solution)/shard_map/ppermute | solution.py:31
  9.8 1.3 collective-permute-start
  11.1 2.6 %collective-permute-start.1 = (bf16[128,512]{1,0:T(8,128)(2,1)}, bf16[128,512]{1,0:T(8,128)(2,1)S(1)}, u32[]{:S(2)}, u32[]{:S(2)}) collective-permute-start(bf16[128,512]{1,0:T(8,128)(2,1)} %get-tuple-element.33), channel_id=1, source_target_pairs={{0,2},{1,3},{2,0},{3,1},{4,6},{5,7},{6,4},{7,5},{8,10},{9,11},{10,... | collective-permute-start | bytes 393224 | tf_op jit(solution)/shard_map/ppermute | solution.py:27
  13.8 1.1 collective-permute-start.2
  15.8 3.5 %collective-permute-done.1 = bf16[128,512]{1,0:T(8,128)(2,1)S(1)} collective-permute-done((bf16[128,512]{1,0:T(8,128)(2,1)}, bf16[128,512]{1,0:T(8,128)(2,1)S(1)}, u32[]{:S(2)}, u32[]{:S(2)}) %collective-permute-start.1) | collective-permute-done | bytes 131104 | tf_op jit(solution)/shard_map/ppermute | solution.py:27
  19.4 1.0 add_convert_fusion.own_ref
  21.5 2.4 %collective-permute-start.20 = (bf16[2,128,512]{2,1,0:T(8,128)(2,1)}, bf16[2,128,512]{2,1,0:T(8,128)(2,1)}, u32[]{:S(2)}, u32[]{:S(2)}) collective-permute-start(bf16[2,128,512]{2,1,0:T(8,128)(2,1)} %get-tuple-element.64), channel_id=1, source_target_pairs={{0,3},{1,0},{2,1},{3,2},{4,7},{5,4},{6,5},{7,6},{8,11},{9,8},{10,9... | collective-permute-start | bytes 786440 | tf_op jit(solution)/shard_map/ppermute | solution.py:27
  23.9 1.9 %collective-permute-done.3.par_ref = bf16[128,512]{1,0:T(8,128)(2,1)S(1)} collective-permute-done((bf16[128,512]{1,0:T(8,128)(2,1)S(1)}, bf16[128,512]{1,0:T(8,128)(2,1)S(1)}, u32[]{:S(2)}, u32[]{:S(2)}) %collective-permute-start.3) | collective-permute-done | bytes 131104 | tf_op jit(solution)/shard_map/ppermute | solution.py:31
  27.6 11.6 %all-to-all-start = ((bf16[32,40,256]{2,1,0:T(8,128)(2,1)}), bf16[32,40,256]{2,1,0:T(8,128)(2,1)S(1)}, u32[]{:S(2)}, u32[]{:S(2)}) async-start(bf16[32,40,256]{2,1,0:T(8,128)(2,1)} %copy-done.4), calls=%async_computation | async-start | bytes 1310720 | tf_op jit(solution)/shard_map/all_to_all | solution.py:383
  39.3 1.7 constant_dynamic-slice_fusion.3
  42.1 0.9 collective-permute-start.5
  43.0 2.3 %collective-permute-start.6 = (f32[128,128]{0,1:T(8,128)S(1)}, f32[128,128]{0,1:T(8,128)S(1)}, u32[]{:S(2)}, u32[]{:S(2)}) collective-permute-start(f32[128,128]{0,1:T(8,128)S(1)} %pad_maximum_fusion.1), channel_id=1, source_target_pairs={{0,2},{1,3},{2,0},{3,1},{4,6},{5,7},{6,4},{7,5},{8,10},{9,11},{10,... | collective-permute-start | bytes 196616 | tf_op jit(solution)/shard_map/ppermute | solution.py:27
  45.4 1.2 collective-permute-start.7
  47.0 1.8 %collective-permute-done.6 = f32[128,128]{0,1:T(8,128)S(1)} collective-permute-done((f32[128,128]{0,1:T(8,128)S(1)}, f32[128,128]{0,1:T(8,128)S(1)}, u32[]{:S(2)}, u32[]{:S(2)}) %collective-permute-start.6) | collective-permute-done | bytes 65568 | tf_op jit(solution)/shard_map/ppermute | solution.py:27
  49.1 9.8 %all-to-all-done.in_ref = bf16[32,40,256]{2,1,0:T(8,128)(2,1)S(1)} async-done(((bf16[32,40,256]{2,1,0:T(8,128)(2,1)}), bf16[32,40,256]{2,1,0:T(8,128)(2,1)S(1)}, u32[]{:S(2)}, u32[]{:S(2)}) %all-to-all-start) | async-done | bytes 655392 | tf_op jit(solution)/shard_map/all_to_all | solution.py:383
  59.0 0.9 collective-permute-start.8
  59.9 1.8 %collective-permute-start.12 = (bf16[320,512]{1,0:T(8,128)(2,1)S(1)}, bf16[320,512]{1,0:T(8,128)(2,1)S(1)}, u32[]{:S(2)}, u32[]{:S(2)}) collective-permute-start(bf16[320,512]{1,0:T(8,128)(2,1)S(1)} %get-tuple-element.46.refs_4_), channel_id=1, source_target_pairs={{0,3},{1,0},{2,1},{3,2},{4,7},{5,4},{6,5},{7,6},{8,11},{9,8},{10,9... | collective-permute-start | bytes 983048 | tf_op jit(solution)/shard_map/ppermute | solution.py:27
  62.8 1.8 %collective-permute-start.14 = (bf16[2048,128]{1,0:T(8,128)(2,1)}, bf16[2048,128]{1,0:T(8,128)(2,1)S(1)}, u32[]{:S(2)}, u32[]{:S(2)}) collective-permute-start(bf16[2048,128]{1,0:T(8,128)(2,1)} %dynamic-slice_bitcast_fusion), channel_id=1, source_target_pairs={{0,4},{4,0},{1,5},{5,1},{2,6},{6,2},{3,7},{7,3},{8,12},{12,8},{9,1... | collective-permute-start | bytes 1572872 | tf_op jit(solution)/shard_map/ppermute | solution.py:31
  66.4 2.6 %collective-permute-start.9 = (bf16[320,512]{1,0:T(8,128)(2,1)S(1)}, bf16[320,512]{1,0:T(8,128)(2,1)S(1)}, u32[]{:S(2)}, u32[]{:S(2)}) collective-permute-start(bf16[320,512]{1,0:T(8,128)(2,1)S(1)} %get-tuple-element.45.refs_0_), channel_id=1, source_target_pairs={{0,3},{1,0},{2,1},{3,2},{4,7},{5,4},{6,5},{7,6},{8,11},{9,8},{10,9... | collective-permute-start | bytes 983048 | tf_op jit(solution)/shard_map/ppermute | solution.py:27
  69.1 2.7 %collective-permute-start.13 = (bf16[320,512]{1,0:T(8,128)(2,1)S(1)}, bf16[320,512]{1,0:T(8,128)(2,1)S(1)}, u32[]{:S(2)}, u32[]{:S(2)}) collective-permute-start(bf16[320,512]{1,0:T(8,128)(2,1)S(1)} %collective-permute-done.12.refs_6_), channel_id=1, source_target_pairs={{0,3},{1,0},{2,1},{3,2},{4,7},{5,4},{6,5},{7,6},{8,11},{9,8},{10,9... | collective-permute-start | bytes 983048 | tf_op jit(solution)/shard_map/ppermute | solution.py:27
  71.8 1.0 pad_maximum_fusion
  72.7 2.4 %collective-permute-done.11.refs_5_ = bf16[320,512]{1,0:T(8,128)(2,1)S(1)} collective-permute-done((bf16[320,512]{1,0:T(8,128)(2,1)S(1)}, bf16[320,512]{1,0:T(8,128)(2,1)S(1)}, u32[]{:S(2)}, u32[]{:S(2)}) %collective-permute-start.11) | collective-permute-done | bytes 327712 | tf_op jit(solution)/shard_map/ppermute | solution.py:27
  75.1 1.7 %collective-permute-start.21 = (bf16[4,128,512]{2,1,0:T(8,128)(2,1)S(1)}, bf16[4,128,512]{2,1,0:T(8,128)(2,1)S(1)}, u32[]{:S(2)}, u32[]{:S(2)}) collective-permute-start(bf16[4,128,512]{2,1,0:T(8,128)(2,1)S(1)} %pad_maximum_fusion), channel_id=1, source_target_pairs={{0,4},{4,0},{1,5},{5,1},{2,6},{6,2},{3,7},{7,3},{8,12},{12,8},{9,1... | collective-permute-start | bytes 1572872 | tf_op jit(solution)/shard_map/ppermute | solution.py:31
  77.0 5.1 %collective-permute-done.10.refs_3_ = bf16[320,512]{1,0:T(8,128)(2,1)S(1)} collective-permute-done((bf16[320,512]{1,0:T(8,128)(2,1)S(1)}, bf16[320,512]{1,0:T(8,128)(2,1)S(1)}, u32[]{:S(2)}, u32[]{:S(2)}) %collective-permute-start.10) | collective-permute-done | bytes 327712 | tf_op jit(solution)/shard_map/ppermute | solution.py:27
  82.2 2.4 %gate_up.1.a0 = bf16[640,256]{1,0:T(8,128)(2,1)S(1)} custom-call(s32[4]{0:T(128)S(1)} %pad_add_fusion.here_ref, bf16[320,512]{1,0:T(8,128)(2,1)S(1)} %get-tuple-element.45.refs_0_, bf16[320,512]{1,0:T(8,128)(2,1)S(1)} %collective-permute-done.8.refs_1_, bf16[320,512]{1,0:T(8,128)(2,1)S(1)} %collective-permute-done.9.refs_2_, ...), custom_call_target="tpu_custom_call" | custom-call | tf_op jit(solution)/shard_map/gate_up/pallas_call | solution.py:400
  85.2 2.5 %collective-permute-start.16 = (bf16[640,256]{1,0:T(8,128)(2,1)S(1)}, bf16[640,256]{1,0:T(8,128)(2,1)S(1)}, u32[]{:S(2)}, u32[]{:S(2)}) collective-permute-start(bf16[640,256]{1,0:T(8,128)(2,1)S(1)} %gate_up.1.a0), channel_id=1, source_target_pairs={{0,2},{1,3},{2,0},{3,1},{4,6},{5,7},{6,4},{7,5},{8,10},{9,11},{10,... | collective-permute-start | bytes 983048 | tf_op jit(solution)/shard_map/ppermute | solution.py:27
  88.6 5.0 %collective-permute-done.15.a1 = bf16[640,256]{1,0:T(8,128)(2,1)S(1)} collective-permute-done((bf16[640,256]{1,0:T(8,128)(2,1)S(1)}, bf16[640,256]{1,0:T(8,128)(2,1)S(1)}, u32[]{:S(2)}, u32[]{:S(2)}) %collective-permute-start.15) | collective-permute-done | bytes 327712 | tf_op jit(solution)/shard_map/ppermute | solution.py:27
  93.6 5.3 %collective-permute-done.16.a2 = bf16[640,256]{1,0:T(8,128)(2,1)S(1)} collective-permute-done((bf16[640,256]{1,0:T(8,128)(2,1)S(1)}, bf16[640,256]{1,0:T(8,128)(2,1)S(1)}, u32[]{:S(2)}, u32[]{:S(2)}) %collective-permute-start.16) | collective-permute-done | bytes 327712 | tf_op jit(solution)/shard_map/ppermute | solution.py:27
  98.8 3.1 %collective-permute-done.17.a3 = bf16[640,256]{1,0:T(8,128)(2,1)S(1)} collective-permute-done((bf16[640,256]{1,0:T(8,128)(2,1)S(1)}, bf16[640,256]{1,0:T(8,128)(2,1)S(1)}, u32[]{:S(2)}, u32[]{:S(2)}) %collective-permute-start.17) | collective-permute-done | bytes 327712 | tf_op jit(solution)/shard_map/ppermute | solution.py:27
  102.0 2.8 %down.1 = bf16[32,40,256]{2,1,0:T(8,128)(2,1)} custom-call(s32[4]{0:T(128)S(1)} %pad_add_fusion.here_ref, bf16[640,256]{1,0:T(8,128)(2,1)S(1)} %gate_up.1.a0, bf16[640,256]{1,0:T(8,128)(2,1)S(1)} %collective-permute-done.15.a1, bf16[640,256]{1,0:T(8,128)(2,1)S(1)} %collective-permute-done.16.a2, bf16[640,256]{1,0:T(8,128)(2,1)S(1)} %collective-permute-done.17.a3, ...), custom_call_target="tpu_custom_call" | custom-call | tf_op jit(solution)/shard_map/down/pallas_call | solution.py:417
  104.8 6.7 %all-to-all-start.1 = ((bf16[32,40,256]{2,1,0:T(8,128)(2,1)}), bf16[32,40,256]{2,1,0:T(8,128)(2,1)S(1)}, u32[]{:S(2)}, u32[]{:S(2)}) async-start(bf16[32,40,256]{2,1,0:T(8,128)(2,1)} %down.1), calls=%async_computation.1 | async-start | bytes 1310720 | tf_op jit(solution)/shard_map/all_to_all | solution.py:425
  111.9 19.2 %all-to-all-done.1 = bf16[32,40,256]{2,1,0:T(8,128)(2,1)S(1)} async-done(((bf16[32,40,256]{2,1,0:T(8,128)(2,1)}), bf16[32,40,256]{2,1,0:T(8,128)(2,1)S(1)}, u32[]{:S(2)}, u32[]{:S(2)}) %all-to-all-start.1) | async-done | bytes 655392 | tf_op jit(solution)/shard_map/all_to_all | solution.py:425
  131.9 1.8 %collective-permute-start.22 = (bf16[256,256]{1,0:T(8,128)(2,1)S(1)}, bf16[256,256]{1,0:T(8,128)(2,1)S(1)}, u32[]{:S(2)}, u32[]{:S(2)}) collective-permute-start(bf16[256,256]{1,0:T(8,128)(2,1)S(1)} %fusion.2.moe_ref), channel_id=1, source_target_pairs={{0,4},{4,0},{1,5},{5,1},{2,6},{6,2},{3,7},{7,3},{8,12},{12,8},{9,1... | collective-permute-start | bytes 393224 | tf_op jit(solution)/shard_map/ppermute | solution.py:31
  133.7 3.6 %collective-permute-done.22.par_ref = bf16[256,256]{1,0:T(8,128)(2,1)S(1)} collective-permute-done((bf16[256,256]{1,0:T(8,128)(2,1)S(1)}, bf16[256,256]{1,0:T(8,128)(2,1)S(1)}, u32[]{:S(2)}, u32[]{:S(2)}) %collective-permute-start.22) | collective-permute-done | bytes 131104 | tf_op jit(solution)/shard_map/ppermute | solution.py:31
  138.1 0.9 collective-permute-start.23
  139.1 2.7 %collective-permute-start.24 = (bf16[144,128]{1,0:T(8,128)(2,1)S(1)}, bf16[144,128]{1,0:T(8,128)(2,1)S(1)}, u32[]{:S(2)}, u32[]{:S(2)}) collective-permute-start(bf16[144,128]{1,0:T(8,128)(2,1)S(1)} %get-tuple-element.50.p0), channel_id=1, source_target_pairs={{0,2},{1,3},{2,0},{3,1},{4,6},{5,7},{6,4},{7,5},{8,10},{9,11},{10,... | collective-permute-start | bytes 110600 | tf_op jit(solution)/shard_map/ppermute | solution.py:27
  142.2 1.3 collective-permute-done.24.p2
  143.5 1.1 collective-permute-done.25.p3
  144.5 1.0 vectors.1
  145.5 5.1 %all-to-all-start.2 = ((bf16[16,128,128]{2,1,0:T(8,128)(2,1)}), bf16[16,128,128]{2,1,0:T(8,128)(2,1)S(1)}, u32[]{:S(2)}, u32[]{:S(2)}) async-start(bf16[16,128,128]{2,1,0:T(8,128)(2,1)} %vectors.1), calls=%async_computation.2 | async-start | bytes 1048576 | tf_op jit(solution)/shard_map/all_to_all | solution.py:477
  151.2 1.8 %collective-permute-start.27 = (bf16[128,512]{1,0:T(8,128)(2,1)S(1)}, bf16[128,512]{1,0:T(8,128)(2,1)S(1)}, u32[]{:S(2)}, u32[]{:S(2)}) collective-permute-start(bf16[128,512]{1,0:T(8,128)(2,1)S(1)} %get-tuple-element.54.p0), channel_id=1, source_target_pairs={{0,2},{1,3},{2,0},{3,1},{4,6},{5,7},{6,4},{7,5},{8,10},{9,11},{10,... | collective-permute-start | bytes 393224 | tf_op jit(solution)/shard_map/ppermute | solution.py:27
  153.0 1.1 collective-permute-start.28
  154.5 3.1 %collective-permute-done.26.p1 = bf16[128,512]{1,0:T(8,128)(2,1)S(1)} collective-permute-done((bf16[128,512]{1,0:T(8,128)(2,1)S(1)}, bf16[128,512]{1,0:T(8,128)(2,1)S(1)}, u32[]{:S(2)}, u32[]{:S(2)}) %collective-permute-start.26) | collective-permute-done | bytes 131104 | tf_op jit(solution)/shard_map/ppermute | solution.py:27
  158.6 5.8 %all-to-all-done.2 = bf16[16,128,128]{2,1,0:T(8,128)(2,1)S(1)} async-done(((bf16[16,128,128]{2,1,0:T(8,128)(2,1)}), bf16[16,128,128]{2,1,0:T(8,128)(2,1)S(1)}, u32[]{:S(2)}, u32[]{:S(2)}) %all-to-all-start.2) | async-done | bytes 524320 | tf_op jit(solution)/shard_map/all_to_all | solution.py:477
  164.4 4.5 %collective-permute-start.29 = (bf16[2048,128]{1,0:T(8,128)(2,1)S(1)}, bf16[2048,128]{1,0:T(8,128)(2,1)S(1)}, u32[]{:S(2)}, u32[]{:S(2)}) collective-permute-start(bf16[2048,128]{1,0:T(8,128)(2,1)S(1)} %bitcast.35), channel_id=1, source_target_pairs={{0,8},{8,0},{1,9},{9,1},{2,10},{10,2},{3,11},{11,3},{4,12},{12,4},... | collective-permute-start | bytes 1572872 | tf_op jit(solution)/shard_map/ppermute | solution.py:491
  168.9 1.4 assemble.1
  170.4 1.8 %score.1 = f32[1,16]{1,0:T(1,128)} custom-call(s32[5,16]{1,0:T(8,128)S(1)} %stack.48.info_ref, bf16[1024,128]{1,0:T(8,128)(2,1)S(1)} %copy-done.9, bf16[2048,128]{1,0:T(8,128)(2,1)S(1)} %bitcast.36, bf16[2048,128]{1,0:T(8,128)(2,1)S(1)} %collective-permute-done.29.other_ref), custom_call_target="tpu_custom_call" | custom-call | tf_op jit(solution)/shard_map/score/pallas_call | solution.py:500
  (99 shorter events, 14.5 us)
Async XLA Ops:
  0.6 41.3 %copy-start = (bf16[2048,64]{0,1:T(8,128)(2,1)S(1)}, bf16[2048,64]{0,1:T(8,128)(2,1)}, u32[]{:S(2)}) copy-start(bf16[2048,64]{0,1:T(8,128)(2,1)} %param.21) | copy-start | bytes 786436
  0.7 14.2 %copy-start.10 = (s32[128,8]{0,1:T(8,128)S(1)}, s32[128,8]{0,1:T(8,128)}, u32[]{:S(2)}) copy-start(s32[128,8]{0,1:T(8,128)} %param.22) | copy-start | bytes 12292
  0.7 19.9 %copy-start.11 = (bf16[2,128,2048]{2,1,0:T(8,128)(2,1)S(1)}, bf16[2,128,2048]{2,1,0:T(8,128)(2,1)}, u32[]{:S(2)}) copy-start(bf16[2,128,2048]{2,1,0:T(8,128)(2,1)} %param.25) | copy-start | bytes 3145732
  6.2 19.7 %collective-permute-start.4 = (bf16[2048,128]{1,0:T(8,128)(2,1)}, bf16[2048,128]{1,0:T(8,128)(2,1)S(1)}, u32[]{:S(2)}, u32[]{:S(2)}) collective-permute-start(bf16[2048,128]{1,0:T(8,128)(2,1)} %get-tuple-element.36), channel_id=1, source_target_pairs={{0,4},{4,0},{1,5},{5,1},{2,6},{6,2},{3,7},{7,3},{8,12},{12,8},{9,1... | collective-permute-start | bytes 1572872 | tf_op jit(solution)/shard_map/ppermute | solution.py:31
  9.8 6.0 %collective-permute-start = (bf16[128,512]{1,0:T(8,128)(2,1)}, bf16[128,512]{1,0:T(8,128)(2,1)S(1)}, u32[]{:S(2)}, u32[]{:S(2)}) collective-permute-start(bf16[128,512]{1,0:T(8,128)(2,1)} %get-tuple-element.32), channel_id=1, source_target_pairs={{0,1},{1,2},{2,3},{3,0},{4,5},{5,6},{6,7},{7,4},{8,9},{9,10},{10,1... | collective-permute-start | bytes 393224 | tf_op jit(solution)/shard_map/ppermute | solution.py:27
  11.1 8.2 %collective-permute-start.1 = (bf16[128,512]{1,0:T(8,128)(2,1)}, bf16[128,512]{1,0:T(8,128)(2,1)S(1)}, u32[]{:S(2)}, u32[]{:S(2)}) collective-permute-start(bf16[128,512]{1,0:T(8,128)(2,1)} %get-tuple-element.33), channel_id=1, source_target_pairs={{0,2},{1,3},{2,0},{3,1},{4,6},{5,7},{6,4},{7,5},{8,10},{9,11},{10,... | collective-permute-start | bytes 393224 | tf_op jit(solution)/shard_map/ppermute | solution.py:27
  13.8 5.6 %collective-permute-start.2 = (bf16[128,512]{1,0:T(8,128)(2,1)}, bf16[128,512]{1,0:T(8,128)(2,1)S(1)}, u32[]{:S(2)}, u32[]{:S(2)}) collective-permute-start(bf16[128,512]{1,0:T(8,128)(2,1)} %get-tuple-element.34), channel_id=1, source_target_pairs={{0,3},{1,0},{2,1},{3,2},{4,7},{5,4},{6,5},{7,6},{8,11},{9,8},{10,9... | collective-permute-start | bytes 393224 | tf_op jit(solution)/shard_map/ppermute | solution.py:27
  19.4 4.5 %copy-start.8 = (f32[3,2048]{1,0:T(4,128)S(1)}, f32[3,2048]{1,0:T(4,128)}, u32[]{:S(2)}) copy-start(f32[3,2048]{1,0:T(4,128)} %gain_ref.3) | copy-start | bytes 73732
  19.4 6.5 %copy-start.3 = (bf16[128,2048]{1,0:T(8,128)(2,1)S(1)}, bf16[128,2048]{1,0:T(8,128)(2,1)}, u32[]{:S(2)}) copy-start(bf16[128,2048]{1,0:T(8,128)(2,1)} %x_ref.1) | copy-start | bytes 1572868
  20.4 5.4 %collective-permute-start.3 = (bf16[128,512]{1,0:T(8,128)(2,1)S(1)}, bf16[128,512]{1,0:T(8,128)(2,1)S(1)}, u32[]{:S(2)}, u32[]{:S(2)}) collective-permute-start(bf16[128,512]{1,0:T(8,128)(2,1)S(1)} %add_convert_fusion.own_ref), channel_id=1, source_target_pairs={{0,4},{4,0},{1,5},{5,1},{2,6},{6,2},{3,7},{7,3},{8,12},{12,8},{9,1... | collective-permute-start | bytes 393224 | tf_op jit(solution)/shard_map/ppermute | solution.py:31
  21.5 19.5 %copy-start.2 = (bf16[2,2048,128]{2,1,0:T(8,128)(2,1)S(1)}, bf16[2,2048,128]{2,1,0:T(8,128)(2,1)}, u32[]{:S(2)}) copy-start(bf16[2,2048,128]{2,1,0:T(8,128)(2,1)} %refs_10_.1) | copy-start | bytes 3145732
  21.5 40.3 %collective-permute-start.20 = (bf16[2,128,512]{2,1,0:T(8,128)(2,1)}, bf16[2,128,512]{2,1,0:T(8,128)(2,1)}, u32[]{:S(2)}, u32[]{:S(2)}) collective-permute-start(bf16[2,128,512]{2,1,0:T(8,128)(2,1)} %get-tuple-element.64), channel_id=1, source_target_pairs={{0,3},{1,0},{2,1},{3,2},{4,7},{5,4},{6,5},{7,6},{8,11},{9,8},{10,9... | collective-permute-start | bytes 786440 | tf_op jit(solution)/shard_map/ppermute | solution.py:27
  23.9 38.9 %collective-permute-start.19 = (bf16[2,128,512]{2,1,0:T(8,128)(2,1)}, bf16[2,128,512]{2,1,0:T(8,128)(2,1)}, u32[]{:S(2)}, u32[]{:S(2)}) collective-permute-start(bf16[2,128,512]{2,1,0:T(8,128)(2,1)} %get-tuple-element.65), channel_id=1, source_target_pairs={{0,2},{1,3},{2,0},{3,1},{4,6},{5,7},{6,4},{7,5},{8,10},{9,11},{10,... | collective-permute-start | bytes 786440 | tf_op jit(solution)/shard_map/ppermute | solution.py:27
  25.9 1.8 %copy-start.5 = (bf16[2048,128]{1,0:T(8,128)(2,1)}, bf16[2048,128]{1,0:T(8,128)(2,1)S(1)}, u32[]{:S(2)}) copy-start(bf16[2048,128]{1,0:T(8,128)(2,1)S(1)} %collective-permute-done.4.refs_11_) | copy-start | bytes 1572868
  26.8 0.8 copy-start.4
  27.6 31.2 %all-to-all-start = ((bf16[32,40,256]{2,1,0:T(8,128)(2,1)}), bf16[32,40,256]{2,1,0:T(8,128)(2,1)S(1)}, u32[]{:S(2)}, u32[]{:S(2)}) async-start(bf16[32,40,256]{2,1,0:T(8,128)(2,1)} %copy-done.4), calls=%async_computation | async-start | bytes 1310720 | tf_op jit(solution)/shard_map/all_to_all | solution.py:383
  42.1 4.7 %collective-permute-start.5 = (f32[128,128]{0,1:T(8,128)S(1)}, f32[128,128]{0,1:T(8,128)S(1)}, u32[]{:S(2)}, u32[]{:S(2)}) collective-permute-start(f32[128,128]{0,1:T(8,128)S(1)} %pad_maximum_fusion.1), channel_id=1, source_target_pairs={{0,1},{1,2},{2,3},{3,0},{4,5},{5,6},{6,7},{7,4},{8,9},{9,10},{10,1... | collective-permute-start | bytes 196616 | tf_op jit(solution)/shard_map/ppermute | solution.py:27
  43.0 5.7 %collective-permute-start.6 = (f32[128,128]{0,1:T(8,128)S(1)}, f32[128,128]{0,1:T(8,128)S(1)}, u32[]{:S(2)}, u32[]{:S(2)}) collective-permute-start(f32[128,128]{0,1:T(8,128)S(1)} %pad_maximum_fusion.1), channel_id=1, source_target_pairs={{0,2},{1,3},{2,0},{3,1},{4,6},{5,7},{6,4},{7,5},{8,10},{9,11},{10,... | collective-permute-start | bytes 196616 | tf_op jit(solution)/shard_map/ppermute | solution.py:27
  45.4 3.7 %collective-permute-start.7 = (f32[128,128]{0,1:T(8,128)S(1)}, f32[128,128]{0,1:T(8,128)S(1)}, u32[]{:S(2)}, u32[]{:S(2)}) collective-permute-start(f32[128,128]{0,1:T(8,128)S(1)} %pad_maximum_fusion.1), channel_id=1, source_target_pairs={{0,3},{1,0},{2,1},{3,2},{4,7},{5,4},{6,5},{7,6},{8,11},{9,8},{10,9... | collective-permute-start | bytes 196616 | tf_op jit(solution)/shard_map/ppermute | solution.py:27
  46.9 18.6 %collective-permute-start.18 = (bf16[2,128,512]{2,1,0:T(8,128)(2,1)}, bf16[2,128,512]{2,1,0:T(8,128)(2,1)}, u32[]{:S(2)}, u32[]{:S(2)}) collective-permute-start(bf16[2,128,512]{2,1,0:T(8,128)(2,1)} %get-tuple-element.66), channel_id=1, source_target_pairs={{0,1},{1,2},{2,3},{3,0},{4,5},{5,6},{6,7},{7,4},{8,9},{9,10},{10,1... | collective-permute-start | bytes 786440 | tf_op jit(solution)/shard_map/ppermute | solution.py:27
  49.1 33.1 %copy-start.1 = (bf16[2,2048,128]{2,1,0:T(8,128)(2,1)S(1)}, bf16[2,2048,128]{2,1,0:T(8,128)(2,1)}, u32[]{:S(2)}) copy-start(bf16[2,2048,128]{2,1,0:T(8,128)(2,1)} %refs_9_.1) | copy-start | bytes 3145732
  58.9 23.3 %copy-start.6 = (bf16[2048,128]{1,0:T(8,128)(2,1)S(1)}, bf16[2048,128]{1,0:T(8,128)(2,1)}, u32[]{:S(2)}) copy-start(bf16[2048,128]{1,0:T(8,128)(2,1)} %copy-done.5) | copy-start | bytes 1572868
  59.0 10.1 %collective-permute-start.8 = (bf16[320,512]{1,0:T(8,128)(2,1)S(1)}, bf16[320,512]{1,0:T(8,128)(2,1)S(1)}, u32[]{:S(2)}, u32[]{:S(2)}) collective-permute-start(bf16[320,512]{1,0:T(8,128)(2,1)S(1)} %get-tuple-element.45.refs_0_), channel_id=1, source_target_pairs={{0,1},{1,2},{2,3},{3,0},{4,5},{5,6},{6,7},{7,4},{8,9},{9,10},{10,1... | collective-permute-start | bytes 983048 | tf_op jit(solution)/shard_map/ppermute | solution.py:27
  59.9 9.2 %collective-permute-start.12 = (bf16[320,512]{1,0:T(8,128)(2,1)S(1)}, bf16[320,512]{1,0:T(8,128)(2,1)S(1)}, u32[]{:S(2)}, u32[]{:S(2)}) collective-permute-start(bf16[320,512]{1,0:T(8,128)(2,1)S(1)} %get-tuple-element.46.refs_4_), channel_id=1, source_target_pairs={{0,3},{1,0},{2,1},{3,2},{4,7},{5,4},{6,5},{7,6},{8,11},{9,8},{10,9... | collective-permute-start | bytes 983048 | tf_op jit(solution)/shard_map/ppermute | solution.py:27
  62.7 12.5 %collective-permute-start.11 = (bf16[320,512]{1,0:T(8,128)(2,1)S(1)}, bf16[320,512]{1,0:T(8,128)(2,1)S(1)}, u32[]{:S(2)}, u32[]{:S(2)}) collective-permute-start(bf16[320,512]{1,0:T(8,128)(2,1)S(1)} %get-tuple-element.46.refs_4_), channel_id=1, source_target_pairs={{0,1},{1,2},{2,3},{3,0},{4,5},{5,6},{6,7},{7,4},{8,9},{9,10},{10,1... | collective-permute-start | bytes 983048 | tf_op jit(solution)/shard_map/ppermute | solution.py:27
  62.8 14.3 %collective-permute-start.14 = (bf16[2048,128]{1,0:T(8,128)(2,1)}, bf16[2048,128]{1,0:T(8,128)(2,1)S(1)}, u32[]{:S(2)}, u32[]{:S(2)}) collective-permute-start(bf16[2048,128]{1,0:T(8,128)(2,1)} %dynamic-slice_bitcast_fusion), channel_id=1, source_target_pairs={{0,4},{4,0},{1,5},{5,1},{2,6},{6,2},{3,7},{7,3},{8,12},{12,8},{9,1... | collective-permute-start | bytes 1572872 | tf_op jit(solution)/shard_map/ppermute | solution.py:31
  66.4 10.6 %collective-permute-start.9 = (bf16[320,512]{1,0:T(8,128)(2,1)S(1)}, bf16[320,512]{1,0:T(8,128)(2,1)S(1)}, u32[]{:S(2)}, u32[]{:S(2)}) collective-permute-start(bf16[320,512]{1,0:T(8,128)(2,1)S(1)} %get-tuple-element.45.refs_0_), channel_id=1, source_target_pairs={{0,3},{1,0},{2,1},{3,2},{4,7},{5,4},{6,5},{7,6},{8,11},{9,8},{10,9... | collective-permute-start | bytes 983048 | tf_op jit(solution)/shard_map/ppermute | solution.py:27
  69.1 13.1 %collective-permute-start.10 = (bf16[320,512]{1,0:T(8,128)(2,1)S(1)}, bf16[320,512]{1,0:T(8,128)(2,1)S(1)}, u32[]{:S(2)}, u32[]{:S(2)}) collective-permute-start(bf16[320,512]{1,0:T(8,128)(2,1)S(1)} %collective-permute-done.8.refs_1_), channel_id=1, source_target_pairs={{0,1},{1,2},{2,3},{3,0},{4,5},{5,6},{6,7},{7,4},{8,9},{9,10},{10,1... | collective-permute-start | bytes 983048 | tf_op jit(solution)/shard_map/ppermute | solution.py:27
  69.1 13.1 %collective-permute-start.13 = (bf16[320,512]{1,0:T(8,128)(2,1)S(1)}, bf16[320,512]{1,0:T(8,128)(2,1)S(1)}, u32[]{:S(2)}, u32[]{:S(2)}) collective-permute-start(bf16[320,512]{1,0:T(8,128)(2,1)S(1)} %collective-permute-done.12.refs_6_), channel_id=1, source_target_pairs={{0,3},{1,0},{2,1},{3,2},{4,7},{5,4},{6,5},{7,6},{8,11},{9,8},{10,9... | collective-permute-start | bytes 983048 | tf_op jit(solution)/shard_map/ppermute | solution.py:27
  75.1 13.4 %collective-permute-start.21 = (bf16[4,128,512]{2,1,0:T(8,128)(2,1)S(1)}, bf16[4,128,512]{2,1,0:T(8,128)(2,1)S(1)}, u32[]{:S(2)}, u32[]{:S(2)}) collective-permute-start(bf16[4,128,512]{2,1,0:T(8,128)(2,1)S(1)} %pad_maximum_fusion), channel_id=1, source_target_pairs={{0,4},{4,0},{1,5},{5,1},{2,6},{6,2},{3,7},{7,3},{8,12},{12,8},{9,1... | collective-permute-start | bytes 1572872 | tf_op jit(solution)/shard_map/ppermute | solution.py:31
  84.6 8.9 %collective-permute-start.15 = (bf16[640,256]{1,0:T(8,128)(2,1)S(1)}, bf16[640,256]{1,0:T(8,128)(2,1)S(1)}, u32[]{:S(2)}, u32[]{:S(2)}) collective-permute-start(bf16[640,256]{1,0:T(8,128)(2,1)S(1)} %gate_up.1.a0), channel_id=1, source_target_pairs={{0,1},{1,2},{2,3},{3,0},{4,5},{5,6},{6,7},{7,4},{8,9},{9,10},{10,1... | collective-permute-start | bytes 983048 | tf_op jit(solution)/shard_map/ppermute | solution.py:27
  85.2 13.6 %collective-permute-start.16 = (bf16[640,256]{1,0:T(8,128)(2,1)S(1)}, bf16[640,256]{1,0:T(8,128)(2,1)S(1)}, u32[]{:S(2)}, u32[]{:S(2)}) collective-permute-start(bf16[640,256]{1,0:T(8,128)(2,1)S(1)} %gate_up.1.a0), channel_id=1, source_target_pairs={{0,2},{1,3},{2,0},{3,1},{4,6},{5,7},{6,4},{7,5},{8,10},{9,11},{10,... | collective-permute-start | bytes 983048 | tf_op jit(solution)/shard_map/ppermute | solution.py:27
  87.7 14.2 %collective-permute-start.17 = (bf16[640,256]{1,0:T(8,128)(2,1)S(1)}, bf16[640,256]{1,0:T(8,128)(2,1)S(1)}, u32[]{:S(2)}, u32[]{:S(2)}) collective-permute-start(bf16[640,256]{1,0:T(8,128)(2,1)S(1)} %gate_up.1.a0), channel_id=1, source_target_pairs={{0,3},{1,0},{2,1},{3,2},{4,7},{5,4},{6,5},{7,6},{8,11},{9,8},{10,9... | collective-permute-start | bytes 983048 | tf_op jit(solution)/shard_map/ppermute | solution.py:27
  104.8 26.3 %all-to-all-start.1 = ((bf16[32,40,256]{2,1,0:T(8,128)(2,1)}), bf16[32,40,256]{2,1,0:T(8,128)(2,1)S(1)}, u32[]{:S(2)}, u32[]{:S(2)}) async-start(bf16[32,40,256]{2,1,0:T(8,128)(2,1)} %down.1), calls=%async_computation.1 | async-start | bytes 1310720 | tf_op jit(solution)/shard_map/all_to_all | solution.py:425
  131.5 5.9 %copy-start.7 = (bf16[2048,128]{1,0:T(8,128)(2,1)S(1)}, bf16[2048,128]{1,0:T(8,128)(2,1)}, u32[]{:S(2)}) copy-start(bf16[2048,128]{1,0:T(8,128)(2,1)} %w_ref.1) | copy-start | bytes 1572868
  131.9 18.8 %copy-start.12 = (s32[32,3]{0,1:T(4,128)S(1)}, s32[32,3]{0,1:T(4,128)}, u32[]{:S(2)}) copy-start(s32[32,3]{0,1:T(4,128)} %param.16) | copy-start | bytes 1156
  131.9 19.2 %copy-start.14 = (s32[1,16]{1,0:T(1,128)S(1)}, s32[1,16]{1,0:T(1,128)}, u32[]{:S(2)}) copy-start(s32[1,16]{1,0:T(1,128)} %param.29) | copy-start | bytes 196
  131.9 22.4 %copy-start.13 = (s32[1,1024]{1,0:T(1,128)S(1)}, s32[1,1024]{1,0:T(1,128)}, u32[]{:S(2)}) copy-start(s32[1,1024]{1,0:T(1,128)} %param.28) | copy-start | bytes 12292
  131.9 5.4 %collective-permute-start.22 = (bf16[256,256]{1,0:T(8,128)(2,1)S(1)}, bf16[256,256]{1,0:T(8,128)(2,1)S(1)}, u32[]{:S(2)}, u32[]{:S(2)}) collective-permute-start(bf16[256,256]{1,0:T(8,128)(2,1)S(1)} %fusion.2.moe_ref), channel_id=1, source_target_pairs={{0,4},{4,0},{1,5},{5,1},{2,6},{6,2},{3,7},{7,3},{8,12},{12,8},{9,1... | collective-permute-start | bytes 393224 | tf_op jit(solution)/shard_map/ppermute | solution.py:31
  138.1 32.4 %copy-start.9 = (bf16[1024,128]{1,0:T(8,128)(2,1)S(1)}, bf16[1024,128]{1,0:T(8,128)(2,1)}, u32[]{:S(2)}) copy-start(bf16[1024,128]{1,0:T(8,128)(2,1)} %doc_ref.1) | copy-start | bytes 786436
  138.1 4.1 %collective-permute-start.23 = (bf16[144,128]{1,0:T(8,128)(2,1)S(1)}, bf16[144,128]{1,0:T(8,128)(2,1)S(1)}, u32[]{:S(2)}, u32[]{:S(2)}) collective-permute-start(bf16[144,128]{1,0:T(8,128)(2,1)S(1)} %get-tuple-element.50.p0), channel_id=1, source_target_pairs={{0,1},{1,2},{2,3},{3,0},{4,5},{5,6},{6,7},{7,4},{8,9},{9,10},{10,1... | collective-permute-start | bytes 110600 | tf_op jit(solution)/shard_map/ppermute | solution.py:27
  139.1 4.4 %collective-permute-start.24 = (bf16[144,128]{1,0:T(8,128)(2,1)S(1)}, bf16[144,128]{1,0:T(8,128)(2,1)S(1)}, u32[]{:S(2)}, u32[]{:S(2)}) collective-permute-start(bf16[144,128]{1,0:T(8,128)(2,1)S(1)} %get-tuple-element.50.p0), channel_id=1, source_target_pairs={{0,2},{1,3},{2,0},{3,1},{4,6},{5,7},{6,4},{7,5},{8,10},{9,11},{10,... | collective-permute-start | bytes 110600 | tf_op jit(solution)/shard_map/ppermute | solution.py:27
  141.7 2.8 %collective-permute-start.25 = (bf16[144,128]{1,0:T(8,128)(2,1)S(1)}, bf16[144,128]{1,0:T(8,128)(2,1)S(1)}, u32[]{:S(2)}, u32[]{:S(2)}) collective-permute-start(bf16[144,128]{1,0:T(8,128)(2,1)S(1)} %get-tuple-element.50.p0), channel_id=1, source_target_pairs={{0,3},{1,0},{2,1},{3,2},{4,7},{5,4},{6,5},{7,6},{8,11},{9,8},{10,9... | collective-permute-start | bytes 110600 | tf_op jit(solution)/shard_map/ppermute | solution.py:27
  145.5 18.9 %all-to-all-start.2 = ((bf16[16,128,128]{2,1,0:T(8,128)(2,1)}), bf16[16,128,128]{2,1,0:T(8,128)(2,1)S(1)}, u32[]{:S(2)}, u32[]{:S(2)}) async-start(bf16[16,128,128]{2,1,0:T(8,128)(2,1)} %vectors.1), calls=%async_computation.2 | async-start | bytes 1048576 | tf_op jit(solution)/shard_map/all_to_all | solution.py:477
  151.1 6.5 %collective-permute-start.26 = (bf16[128,512]{1,0:T(8,128)(2,1)S(1)}, bf16[128,512]{1,0:T(8,128)(2,1)S(1)}, u32[]{:S(2)}, u32[]{:S(2)}) collective-permute-start(bf16[128,512]{1,0:T(8,128)(2,1)S(1)} %get-tuple-element.54.p0), channel_id=1, source_target_pairs={{0,1},{1,2},{2,3},{3,0},{4,5},{5,6},{6,7},{7,4},{8,9},{9,10},{10,1... | collective-permute-start | bytes 393224 | tf_op jit(solution)/shard_map/ppermute | solution.py:27
  151.2 6.4 %collective-permute-start.27 = (bf16[128,512]{1,0:T(8,128)(2,1)S(1)}, bf16[128,512]{1,0:T(8,128)(2,1)S(1)}, u32[]{:S(2)}, u32[]{:S(2)}) collective-permute-start(bf16[128,512]{1,0:T(8,128)(2,1)S(1)} %get-tuple-element.54.p0), channel_id=1, source_target_pairs={{0,2},{1,3},{2,0},{3,1},{4,6},{5,7},{6,4},{7,5},{8,10},{9,11},{10,... | collective-permute-start | bytes 393224 | tf_op jit(solution)/shard_map/ppermute | solution.py:27
  153.0 5.5 %collective-permute-start.28 = (bf16[128,512]{1,0:T(8,128)(2,1)S(1)}, bf16[128,512]{1,0:T(8,128)(2,1)S(1)}, u32[]{:S(2)}, u32[]{:S(2)}) collective-permute-start(bf16[128,512]{1,0:T(8,128)(2,1)S(1)} %get-tuple-element.54.p0), channel_id=1, source_target_pairs={{0,3},{1,0},{2,1},{3,2},{4,7},{5,4},{6,5},{7,6},{8,11},{9,8},{10,9... | collective-permute-start | bytes 393224 | tf_op jit(solution)/shard_map/ppermute | solution.py:27
  164.4 6.0 %collective-permute-start.29 = (bf16[2048,128]{1,0:T(8,128)(2,1)S(1)}, bf16[2048,128]{1,0:T(8,128)(2,1)S(1)}, u32[]{:S(2)}, u32[]{:S(2)}) collective-permute-start(bf16[2048,128]{1,0:T(8,128)(2,1)S(1)} %bitcast.35), channel_id=1, source_target_pairs={{0,8},{8,0},{1,9},{9,1},{2,10},{10,2},{3,11},{11,3},{4,12},{12,4},... | collective-permute-start | bytes 1572872 | tf_op jit(solution)/shard_map/ppermute | solution.py:491
